TPU v7x, 32 devices: a whole 2x2x4 slice. The times are simulated.
32 devices in a mesh: eta: 2 (over x), phi: 4 (over z), replica: 4 (over y, core).
Axes of the slice: x: 2, y: 2, z: 4, core: 2. Of those that a mesh axis runs over, the one named last changes fastest.
Arguments:
- tokens: bfloat16 [4, 64, 128, 768], P('replica', 'eta', 'phi'), may hold values from -6 to 6
- send_pos: int32 [4, 2, 4, 8, 35], P('replica', 'eta', 'phi'), may hold values from 0 to 1024, as said below
- enc_src: int32 [4, 2, 4, 256], P('replica', 'eta', 'phi'), may hold values from 0 to 279, as said below
- window_id: int32 [4, 2, 4, 256], P('replica', 'eta', 'phi'), may hold values from 0 to 3
- enc_cot: bfloat16 [4, 2, 4, 256, 768], P('replica', 'eta', 'phi'), may hold values from -0.0625 to 0.0625
- w_qkv: bfloat16 [768, 2304], replicated, may hold values from -0.21875 to 0.21875
- head_scale: float32 [12], replicated, may hold values from 2 to 12
- w_out: bfloat16 [768, 768], replicated, may hold values from -0.21875 to 0.21875
- w_dec_in: bfloat16 [768, 384], replicated, may hold values from -0.21875 to 0.21875
- mask_token: bfloat16 [384], replicated, may hold values from -4 to 4
- conv_kernel: float32 [7, 7, 384], replicated, may hold values from -0.875 to 0.875
- w_up: bfloat16 [384, 768], replicated, may hold values from -0.3125 to 0.3125
- w_down: bfloat16 [768, 384], replicated, may hold values from -0.21875 to 0.21875
- w_head: bfloat16 [384, 128], replicated, may hold values from -0.3125 to 0.3125
Outputs:
- weight_grads: float32 [3072, 768], P(('eta', 'phi'))
- reconstruction: float32 [4, 64, 128, 128], P('replica', 'eta', 'phi')
Inputs may be any that keep to these rules, and one draw needn't show every extreme that they name: send_pos[e,a,b,d,k] is the cell of the k-th visible token that tile (a,b) sends to encoder shard d; 1024 marks an empty slot and empty slots follow the live ones. The visible cells of a tile are whole aligned 2 x 2 blocks, each sent exactly once; every encoder shard receives exactly 256 live slots; some tile fills all 35 slots to some shard. enc_src[e,a,b,r] = s * 35 + k names a live slot (send_pos of tile s towards this shard, slot k); each live slot arriving at the shard appears exactly once.
All inputs are finite; a program needn't handle non-finite values.
Results may differ from a plain program's by a relative error of at most 0.0095.
Values may be sent and summed in bfloat16 or wider, within the bound.
No kernel may reach another device: no remote copies, remote signals or barrier semaphores. Data moves between devices by JAX's collectives and lax.ppermute only.
A program may use at most 128 MiB of HBM per device.

v0:
```python
import jax
import jax.numpy as jnp
from jax import lax
from jax.sharding import PartitionSpec as P

norm_eps = 1e-05
length_eps = 1e-06
highest = lax.Precision.HIGHEST


def extended(block, sides, width):
    for axis, dim in sides:
        count = lax.axis_size(axis)
        forward = [(i, i + 1) for i in range(count - 1)]
        forward.append((count - 1, 0))
        backward = [(target, source) for source, target in forward]
        low = lax.ppermute(
            lax.slice_in_dim(block, block.shape[dim] - width, None, axis=dim), axis, forward
        )
        high = lax.ppermute(lax.slice_in_dim(block, 0, width, axis=dim), axis, backward)
        block = jnp.concatenate([low, block, high], axis=dim)
    return block


def plain_norm(values):
    centre = jnp.mean(values, axis=-1, keepdims=True)
    centred = values - centre
    spread = jnp.mean(centred * centred, axis=-1, keepdims=True)
    return centred * lax.rsqrt(spread + norm_eps)


def encoder_pass(enc_in, window, cotangent, w_qkv, head_scale, w_out):
    row_count, feature_width = enc_in.shape
    head_count = head_scale.shape[0]
    head_size = feature_width // head_count
    normed = plain_norm(enc_in.astype(jnp.float32)).astype(jnp.bfloat16)
    qkv = jnp.dot(normed, w_qkv, preferred_element_type=jnp.float32).reshape(
        row_count, 3, head_count, head_size
    )
    query = qkv[:, 0]
    keyed = qkv[:, 1]
    value_low = qkv[:, 2].astype(jnp.bfloat16)
    query_len = jnp.sqrt(jnp.sum(query * query, axis=-1, keepdims=True) + length_eps)
    key_len = jnp.sqrt(jnp.sum(keyed * keyed, axis=-1, keepdims=True) + length_eps)
    query_unit = query / query_len
    key_unit = keyed / key_len
    same_window = window[:, None] == window[None, :]
    scores = (
        jnp.einsum("qhd,khd->hqk", query_unit, key_unit, precision=highest)
        * head_scale[:, None, None]
    )
    raised = jnp.where(same_window[None], jnp.exp(scores), jnp.zeros((), jnp.float32))
    softmax_weights = raised / jnp.sum(raised, axis=-1, keepdims=True)
    softmax_low = softmax_weights.astype(jnp.bfloat16)
    attended = jnp.einsum(
        "hqk,khd->qhd", softmax_low, value_low, preferred_element_type=jnp.float32
    )
    attended = attended.reshape(row_count, feature_width).astype(jnp.bfloat16)
    enc_out = (
        enc_in.astype(jnp.float32) + jnp.dot(attended, w_out, preferred_element_type=jnp.float32)
    ).astype(jnp.bfloat16)
    grad_attended = lax.dot_general(
        cotangent, w_out, (((1,), (1,)), ((), ())), preferred_element_type=jnp.float32
    )
    grad_attended = grad_attended.astype(jnp.bfloat16).reshape(row_count, head_count, head_size)
    grad_soft = jnp.einsum(
        "qhd,khd->hqk", grad_attended, value_low, preferred_element_type=jnp.float32
    )
    grad_value = jnp.einsum(
        "hqk,qhd->khd", softmax_low, grad_attended, preferred_element_type=jnp.float32
    )
    grad_scores = softmax_weights * (
        grad_soft - jnp.sum(softmax_weights * grad_soft, axis=-1, keepdims=True)
    )
    grad_scores = grad_scores * head_scale[:, None, None]
    grad_qunit = jnp.einsum("hqk,khd->qhd", grad_scores, key_unit, precision=highest)
    grad_kunit = jnp.einsum("hqk,qhd->khd", grad_scores, query_unit, precision=highest)
    grad_query = (
        grad_qunit - query_unit * jnp.sum(query_unit * grad_qunit, axis=-1, keepdims=True)
    ) / query_len
    grad_key = (
        grad_kunit - key_unit * jnp.sum(key_unit * grad_kunit, axis=-1, keepdims=True)
    ) / key_len
    grad_qkv = (
        jnp.stack([grad_query, grad_key, grad_value], axis=1)
        .reshape(row_count, 3 * feature_width)
        .astype(jnp.bfloat16)
    )
    contract_rows = (((0,), (0,)), ((), ()))
    term = jnp.concatenate(
        [
            lax.dot_general(grad_qkv, normed, contract_rows, preferred_element_type=jnp.float32),
            lax.dot_general(cotangent, attended, contract_rows, preferred_element_type=jnp.float32),
        ],
        axis=0,
    )
    return (enc_out, term)


def body(
    tokens,
    send_pos,
    enc_src,
    window_id,
    enc_cot,
    w_qkv,
    head_scale,
    w_out,
    w_dec_in,
    mask_token,
    conv_kernel,
    w_up,
    w_down,
    w_head,
):
    eta_cells = tokens.shape[1]
    phi_cells = tokens.shape[2]
    feature_width = tokens.shape[3]
    dec_width = w_dec_in.shape[1]
    tile_len = eta_cells * phi_cells
    eta_count = lax.axis_size("eta")
    phi_count = lax.axis_size("phi")
    group_size = eta_count * phi_count
    slot_count = send_pos.shape[-1]
    flat_tile = tokens.reshape(tile_len, feature_width)
    slot_cells = send_pos.reshape(group_size * slot_count)
    outgoing = jnp.take(flat_tile, jnp.minimum(slot_cells, tile_len - 1), axis=0)
    outgoing = outgoing.reshape(group_size, slot_count, feature_width)
    arrived = lax.all_to_all(outgoing, ("eta", "phi"), split_axis=0, concat_axis=0, tiled=True)
    arrived = arrived.reshape(group_size * slot_count, feature_width)
    sources = enc_src.reshape(-1)
    enc_in = jnp.take(arrived, sources, axis=0)
    enc_out, term = encoder_pass(
        enc_in, window_id.reshape(-1), enc_cot.reshape(-1, feature_width), w_qkv, head_scale, w_out
    )
    grad_share = lax.psum_scatter(term, ("eta", "phi", "replica"), scatter_dimension=0, tiled=True)
    grad_total = lax.all_gather(
        grad_share.astype(jnp.bfloat16), "replica", axis=0, tiled=True
    ).astype(grad_share.dtype)
    outbound = (
        jnp.zeros((group_size * slot_count, feature_width), jnp.bfloat16).at[sources].set(enc_out)
    )
    returned = lax.all_to_all(
        outbound.reshape(group_size, slot_count, feature_width),
        ("eta", "phi"),
        split_axis=0,
        concat_axis=0,
        tiled=True,
    )
    returned = returned.reshape(group_size * slot_count, feature_width)
    dec_slots = jnp.dot(returned, w_dec_in, preferred_element_type=jnp.float32).astype(jnp.bfloat16)
    filled = (
        jnp.zeros((tile_len, dec_width), jnp.bfloat16).at[slot_cells].set(dec_slots, mode="drop")
    )
    seen_cells = jnp.zeros((tile_len,), jnp.bool_).at[slot_cells].set(True, mode="drop")
    dec_grid = jnp.where(seen_cells[:, None], filled, mask_token).reshape(
        eta_cells, phi_cells, dec_width
    )
    kernel_span = conv_kernel.shape[0]
    rim_width = kernel_span // 2
    padded = extended(dec_grid, (("eta", 0), ("phi", 1)), rim_width)
    eta_place = lax.axis_index("eta")
    rim_line = lax.broadcasted_iota(jnp.int32, (eta_cells + 2 * rim_width, 1, 1), 0)
    keep_rim = jnp.logical_and(
        jnp.logical_or(rim_line >= rim_width, eta_place > 0),
        jnp.logical_or(rim_line < eta_cells + rim_width, eta_place < eta_count - 1),
    )
    padded = jnp.where(keep_rim, padded, jnp.zeros((), padded.dtype))
    mixed_cells = jnp.zeros((eta_cells, phi_cells, dec_width), jnp.float32)
    for row_shift in range(kernel_span):
        for col_shift in range(kernel_span):
            window_cells = padded[
                row_shift : row_shift + eta_cells, col_shift : col_shift + phi_cells
            ].astype(jnp.float32)
            mixed_cells = mixed_cells + conv_kernel[row_shift, col_shift] * window_cells
    dec_normed = plain_norm(mixed_cells).astype(jnp.bfloat16).reshape(tile_len, dec_width)
    hidden = jax.nn.gelu(
        jnp.dot(dec_normed, w_up, preferred_element_type=jnp.float32), approximate=False
    ).astype(jnp.bfloat16)
    decoded = (
        dec_grid.reshape(tile_len, dec_width).astype(jnp.float32)
        + jnp.dot(hidden, w_down, preferred_element_type=jnp.float32)
    ).astype(jnp.bfloat16)
    reconstruction = jnp.dot(decoded, w_head, preferred_element_type=jnp.float32).reshape(
        1, eta_cells, phi_cells, -1
    )
    return (grad_total, reconstruction)


def solution(mesh):
    in_specs = (
        P("replica", "eta", "phi", None),
        P("replica", "eta", "phi", None, None),
        P("replica", "eta", "phi", None),
        P("replica", "eta", "phi", None),
        P("replica", "eta", "phi", None, None),
        P(),
        P(),
        P(),
        P(),
        P(),
        P(),
        P(),
        P(),
        P(),
    )
    out_specs = (P(("eta", "phi"), None), P("replica", "eta", "phi", None))
    return jax.shard_map(body, mesh=mesh, in_specs=in_specs, out_specs=out_specs, check_vma=False)
```

profile of v0, /device:TPU:0, one launch (start us, length us, event | category | flops | bytes accessed | tf_op | source)
XLA Modules:
  0.0 229.6 jit_solution(4999208129221974570)
XLA Ops:
  7.2 0.8 compare_and_fusion
  8.0 0.9 reshape.238
  9.6 4.6 %gather_fusion = bf16[280,768]{1,0:T(8,128)(2,1)} fusion(bf16[1024,768]{1,0:T(8,128)(2,1)} %bitcast.105, s32[1024]{0:T(1024)S(1)} %pad_clamp_fusion.1), kind=kCustom, calls=%fused_computation | custom fusion | bytes 861280 | tf_op jit(solution)/shard_map/jit(_take)/gather | solution.py:127
  14.1 1.9 gather.11
  16.1 1.9 broadcast_select_fusion.1
  18.0 7.3 %all-to-all-start = ((bf16[8,35,768]{2,1,0:T(8,128)(2,1)}), bf16[8,35,768]{2,1,0:T(8,128)(2,1)}, u32[]{:S(2)}, u32[]{:S(2)}) async-start(bf16[8,35,768]{2,1,0:T(8,128)(2,1)} %broadcast_select_fusion.1), calls=%async_computation | async-start | bytes 983040 | tf_op jit(solution)/shard_map/all_to_all | solution.py:129
  25.3 2.6 %convolution_convert_fusion.2 = bf16[256,768]{1,0:T(8,128)(2,1)} fusion(bf16[768,768]{1,0:T(8,128)(2,1)} %param.21, bf16[1,1,1,256,768]{4,3,2,1,0:T(8,128)(2,1)} %param.18), kind=kOutput, calls=%fused_computation.52 | convolution fusion | flops 302186496 | bytes 1966080 | tf_op jit(solution)/shard_map/dot_general | solution.py:62
  28.0 1.9 copy.32
  31.3 8.7 %all-to-all-done = bf16[8,35,768]{2,1,0:T(8,128)(2,1)} async-done(((bf16[8,35,768]{2,1,0:T(8,128)(2,1)}), bf16[8,35,768]{2,1,0:T(8,128)(2,1)}, u32[]{:S(2)}, u32[]{:S(2)}) %all-to-all-start) | async-done | bytes 430112 | tf_op jit(solution)/shard_map/all_to_all | solution.py:129
  40.0 1.9 reshape.239
  42.0 3.2 %gather_fusion.1 = bf16[256,768]{1,0:T(8,128)(2,1)} fusion(bf16[280,768]{1,0:T(8,128)(2,1)} %reshape.239, s32[1024]{0:T(1024)S(1)} %pad_clamp_fusion), kind=kCustom, calls=%fused_computation.1 | custom fusion | bytes 787456 | tf_op jit(solution)/shard_map/jit(_take)/gather | solution.py:132
  45.2 1.2 convert_reduce_fusion
  46.4 1.3 fusion.29
  47.7 2.6 %fusion.53 = f32[256,2304]{0,1:T(8,128)S(1)} fusion(bf16[768,2304]{1,0:T(8,128)(2,1)S(1)} %copy-done, f32[256]{0:T(256)S(1)} %add_rsqrt_fusion.1, f32[256]{0:T(256)S(1)} %broadcast_multiply_fusion.1, bf16[256,768]{1,0:T(8,128)(2,1)} %gather_fusion.1, pred[256]{0:T(512)(128)(4,1)S(1)} %compare_and_fusion.1), kind=kOutput, calls=%fused_computation.163 | convolution fusion | flops 906952704 | bytes 6293760 | tf_op jit(solution)/shard_map/dot_general | solution.py:37
  51.2 3.4 %fusion.13 = (f32[12,256]{1,0:T(8,128)S(1)}, f32[12,256,256]{1,2,0:T(8,128)S(1)}) fusion(f32[12]{0:T(128)S(1)} %copy-done.44, pred[256,256]{0,1:T(8,128)(4,1)S(1)} %copy-done.6, f32[256,3,12,64]{0,3,2,1:T(8,128)S(1)} %bitcast.107, f32[256,12]{0,1:T(8,128)S(1)} %get-tuple-element.66, f32[256,12]{0,1:T(8,128)S(1)} %get-tuple-element.65), kind=kOutput, calls=%fused_computation.31 | convolution fusion | flops 606729216 | bytes 4829696 | tf_op jit(solution)/shard_map/qhd,khd->hqk/dot_general | solution.py:49
  54.6 0.9 convolution_convert_fusion
  55.6 0.9 fusion.24
  56.4 1.2 multiply_reduce_fusion
  57.6 4.1 %convolution_bitcast_fusion.1 = f32[256,12,64]{0,2,1:T(8,128)S(1)} fusion(f32[12,256,256]{1,2,0:T(8,128)S(1)} %get-tuple-element.64, f32[12,256]{1,0:T(8,128)S(1)} %get-tuple-element.63, f32[12]{0:T(128)S(1)} %copy-done.44, f32[256,3,12,64]{0,3,2,1:T(8,128)S(1)} %bitcast.110, f32[256,12]{0,1:T(8,128)S(1)} %get-tuple-element.65, ...), kind=kOutput, calls=%fused_computation.44 | convolution fusion | flops 608894976 | bytes 7979520 | tf_op jit(solution)/shard_map/hqk,qhd->khd/dot_general | solution.py:77
  61.7 3.1 %convolution_bitcast_fusion.2 = f32[256,12,64]{0,2,1:T(8,128)S(1)} fusion(f32[12,256,256]{1,2,0:T(8,128)S(1)} %get-tuple-element.64, f32[12,256]{1,0:T(8,128)S(1)} %get-tuple-element.63, f32[12]{0:T(128)S(1)} %copy-done.44, f32[256,3,12,64]{0,3,2,1:T(8,128)S(1)} %bitcast.111, f32[256,12]{0,1:T(8,128)S(1)} %get-tuple-element.66, ...), kind=kOutput, calls=%fused_computation.45 | convolution fusion | flops 608894976 | bytes 7979520 | tf_op jit(solution)/shard_map/hqk,khd->qhd/dot_general | solution.py:76
  64.8 1.9 convolution_bitcast_fusion
  67.4 0.8 copy-done.1
  68.3 4.1 %fusion.51 = f32[2304,768]{1,0:T(8,128)} fusion(bf16[256,2304]{0,1:T(8,128)(2,1)S(1)} %bitcast.104, f32[256]{0:T(256)S(1)} %add_rsqrt_fusion.1, f32[256]{0:T(256)S(1)} %broadcast_multiply_fusion.1, bf16[256,768]{1,0:T(8,128)(2,1)S(1)} %copy-done.1, pred[256]{0:T(512)(128)(4,1)S(1)} %compare_and_fusion.1), kind=kOutput, calls=%fused_computation.162 | convolution fusion | flops 906952704 | bytes 8653056 | tf_op jit(solution)/shard_map/dot_general | solution.py:92
  72.4 8.0 %pad_maximum_fusion = f32[3072,768]{1,0:T(8,128)} fusion(f32[768,768]{1,0:T(8,128)} %convolution_bitcast_fusion, f32[2304,768]{1,0:T(8,128)} %fusion.51), kind=kLoop, calls=%fused_computation.7 | loop fusion | flops 2359296 | bytes 18874368 | tf_op jit(solution)/shard_map/concatenate | solution.py:90
  80.3 2.7 %fusion.21 = bf16[256,768]{1,0:T(8,128)(2,1)} fusion(bf16[256,768]{0,1:T(8,128)(2,1)} %bitcast.116, bf16[768,768]{1,0:T(8,128)(2,1)} %param.21, bf16[256,768]{1,0:T(8,128)(2,1)} %gather_fusion.1, pred[256]{0:T(512)(128)(4,1)S(1)} %compare_and_fusion.1), kind=kOutput, calls=%fused_computation.47 | convolution fusion | flops 302776320 | bytes 2359552 | tf_op jit(solution)/shard_map/dot_general | solution.py:60
  83.1 2.8 %scatter_custom_fusion.1 = bf16[280,768]{1,0:T(8,128)(2,1)} fusion(s32[256]{0:T(256)S(1)} %bitcast.123, bf16[256,768]{1,0:T(8,128)(2,1)} %fusion.21, bf16[]{:T(256)} %constant.20.clone.1), kind=kCustom, calls=%fused_computation.86 | custom fusion | bytes 430592 | tf_op jit(solution)/shard_map/scatter | solution.py:141
  85.9 1.9 reshape.244
  87.8 4.1 %all-to-all-start.1 = ((bf16[8,35,768]{2,1,0:T(8,128)(2,1)}), bf16[8,35,768]{2,1,0:T(8,128)(2,1)}, u32[]{:S(2)}, u32[]{:S(2)}) async-start(bf16[8,35,768]{2,1,0:T(8,128)(2,1)} %reshape.244), calls=%async_computation.2 | async-start | bytes 983040 | tf_op jit(solution)/shard_map/all_to_all | solution.py:143
  92.0 2.3 scatter_custom_fusion
  94.3 1.9 slice_reduce_fusion.48
  96.2 1.9 slice_reduce_fusion.47
  98.1 7.4 %all-to-all-done.1 = bf16[8,35,768]{2,1,0:T(8,128)(2,1)} async-done(((bf16[8,35,768]{2,1,0:T(8,128)(2,1)}), bf16[8,35,768]{2,1,0:T(8,128)(2,1)}, u32[]{:S(2)}, u32[]{:S(2)}) %all-to-all-start.1) | async-done | bytes 430112 | tf_op jit(solution)/shard_map/all_to_all | solution.py:143
  105.5 2.0 reshape.245
  107.5 2.3 %convolution_convert_fusion.3 = bf16[280,384]{1,0:T(8,128)(2,1)} fusion(bf16[280,768]{1,0:T(8,128)(2,1)} %reshape.245, bf16[768,384]{1,0:T(8,128)(2,1)} %param.22), kind=kOutput, calls=%fused_computation.56 | convolution fusion | flops 165258240 | bytes 1234944 | tf_op jit(solution)/shard_map/dot_general | solution.py:151
  109.8 2.9 %scatter_custom_fusion.2 = bf16[1024,384]{1,0:T(8,128)(2,1)} fusion(s32[280]{0:T(512)} %get-tuple-element.53, bf16[280,384]{1,0:T(8,128)(2,1)} %convolution_convert_fusion.3, bf16[]{:T(256)} %constant.20.clone.1), kind=kCustom, calls=%fused_computation.83 | custom fusion | bytes 786944 | tf_op jit(solution)/shard_map/scatter | solution.py:153
  112.8 1.4 broadcast_select_fusion
  114.8 1.5 collective-permute-start
  116.3 1.0 slice_reduce_fusion.46
  117.2 1.4 collective-permute-done.1
  119.9 3.8 %collective-permute-start.3 = (bf16[38,3,384]{2,1,0:T(4,128)(2,1)S(1)}, bf16[38,3,384]{2,1,0:T(4,128)(2,1)S(1)}, u32[]{:S(2)}, u32[]{:S(2)}) collective-permute-start(bf16[38,3,384]{2,1,0:T(4,128)(2,1)S(1)} %get-tuple-element.58), channel_id=1, source_target_pairs={{4,0},{8,4},{12,8},{0,12},{5,1},{9,5},{13,9},{1,13},{6,2},{10,6},{... | collective-permute-start | bytes 262664 | tf_op jit(solution)/shard_map/ppermute | solution.py:20
  123.7 2.8 %collective-permute-done.2 = bf16[38,3,384]{2,1,0:T(4,128)(2,1)S(1)} collective-permute-done((bf16[38,3,384]{2,1,0:T(4,128)(2,1)S(1)}, bf16[38,3,384]{2,1,0:T(4,128)(2,1)S(1)}, u32[]{:S(2)}, u32[]{:S(2)}) %collective-permute-start.2) | collective-permute-done | bytes 87584 | tf_op jit(solution)/shard_map/ppermute | solution.py:17
  127.3 11.6 %fusion.66 = (f32[32,32]{1,0:T(8,128)S(1)}, f32[32,32,384]{2,1,0:T(8,128)S(1)}) fusion(bf16[38,38,384]{2,1,0:T(8,128)(2,1)S(1)} %maximum_select_fusion, f32[384]{0:T(512)S(1)} %get-tuple-element.51, f32[384]{0:T(512)S(1)} %get-tuple-element.52, f32[384]{0:T(512)S(1)} %get-tuple-element.5, f32[384]{0:T(512)S(1)} %get-tuple-element.6, ...), kind=kLoop, calls=%fused_computation.165 | loop fusion | flops 57801728 | bytes 40187392 | tf_op jit(solution)/shard_map/reduce_sum | solution.py:26
  140.4 8.7 %fusion.4 = bf16[1024,768]{1,0:T(8,128)(2,1)} fusion(bf16[1024,384]{1,0:T(8,128)(2,1)S(1)} %bitcast.114, bf16[384,768]{1,0:T(8,128)(2,1)S(1)} %copy-done.43), kind=kOutput, calls=%fused_computation.11 | convolution fusion | flops 655097856 | bytes 2949120 | tf_op jit(solution)/shard_map/dot_general | solution.py:178
  149.1 3.8 %fusion.20 = f32[1024,128]{1,0:T(8,128)} fusion(bf16[384,128]{1,0:T(8,128)(2,1)} %param.27, bf16[1024,384]{1,0:T(8,128)(2,1)} %copy-done.2, bf16[1024,768]{1,0:T(8,128)(2,1)} %fusion.4, bf16[768,384]{1,0:T(8,128)(2,1)} %param.26), kind=kOutput, calls=%fused_computation.46 | convolution fusion | flops 705822720 | bytes 3571712 | tf_op jit(solution)/shard_map/dot_general | solution.py:184
  152.9 60.6 %reduce-scatter.2.cloned.1.call-done = f32[96,768]{1,0:T(8,128)} async-done(((f32[3072,768]{1,0:T(8,128)}), f32[96,768]{1,0:T(8,128)}) %reduce-scatter.2.cloned.1.call-update) | async-done | bytes 294928 | tf_op jit(solution)/shard_map/reduce_scatter | solution.py:136
  213.5 1.0 convert_element_type.212
  214.4 7.2 %all_gather.3 = bf16[384,768]{1,0:T(8,128)(2,1)S(1)} all-gather(bf16[96,768]{1,0:T(8,128)(2,1)S(1)} %convert_element_type.212), channel_id=1, replica_groups=mesh['eta'=2,'phi'=4,'replica'=4] {'replica'}, dimensions={0}, use_global_device_ids=true | all-gather | bytes 737280 | tf_op jit(solution)/shard_map/all_gather | solution.py:137
  221.7 1.1 convert_element_type.213
  (117 shorter events, 7.3 us)
Async XLA Ops:
  7.2 40.5 %copy-start = (bf16[768,2304]{1,0:T(8,128)(2,1)S(1)}, bf16[768,2304]{1,0:T(8,128)(2,1)}, u32[]{:S(2)}) copy-start(bf16[768,2304]{1,0:T(8,128)(2,1)} %param.19) | copy-start | bytes 10616836
  18.0 22.0 %all-to-all-start = ((bf16[8,35,768]{2,1,0:T(8,128)(2,1)}), bf16[8,35,768]{2,1,0:T(8,128)(2,1)}, u32[]{:S(2)}, u32[]{:S(2)}) async-start(bf16[8,35,768]{2,1,0:T(8,128)(2,1)} %broadcast_select_fusion.1), calls=%async_computation | async-start | bytes 983040 | tf_op jit(solution)/shard_map/all_to_all | solution.py:129
  25.3 4.6 %copy-start.42 = (s32[1,1,1,256]{3,2,1,0:T(1,128)S(1)}, s32[1,1,1,256]{3,2,1,0:T(1,128)}, u32[]{:S(2)}) copy-start(s32[1,1,1,256]{3,2,1,0:T(1,128)} %param.16) | copy-start | bytes 3076
  25.3 5.3 %copy-start.41 = (s32[1,1,1,256]{3,2,1,0:T(1,128)S(1)}, s32[1,1,1,256]{3,2,1,0:T(1,128)}, u32[]{:S(2)}) copy-start(s32[1,1,1,256]{3,2,1,0:T(1,128)} %param.17) | copy-start | bytes 3076
  25.3 188.2 %reduce-scatter.2.cloned.1.call-start = ((), (), s32[]{:S(2)}) async-start(), calls=%async_computation.3 | async-start | bytes 9732096 | tf_op jit(solution)/shard_map/reduce_scatter | solution.py:136
  55.4 9.4 %copy-start.4 = (bf16[12,64,256]{2,1,0:T(8,128)(2,1)}, bf16[12,64,256]{2,1,0:T(8,128)(2,1)S(1)}, u32[]{:S(2)}) copy-start(bf16[12,64,256]{2,1,0:T(8,128)(2,1)S(1)} %convolution_convert_fusion) | copy-start | bytes 1179652
  61.7 3.1 %copy-start.3 = (bf16[1,1,1,256,768]{4,3,2,1,0:T(8,128)(2,1)S(1)}, bf16[1,1,1,256,768]{4,3,2,1,0:T(8,128)(2,1)}, u32[]{:S(2)}) copy-start(bf16[1,1,1,256,768]{4,3,2,1,0:T(8,128)(2,1)} %param.18) | copy-start | bytes 1179652
  87.8 17.7 %all-to-all-start.1 = ((bf16[8,35,768]{2,1,0:T(8,128)(2,1)}), bf16[8,35,768]{2,1,0:T(8,128)(2,1)}, u32[]{:S(2)}, u32[]{:S(2)}) async-start(bf16[8,35,768]{2,1,0:T(8,128)(2,1)} %reshape.244), calls=%async_computation.2 | async-start | bytes 983040 | tf_op jit(solution)/shard_map/all_to_all | solution.py:143
  114.2 12.8 %copy-start.2 = (bf16[1024,384]{1,0:T(8,128)(2,1)}, bf16[1024,384]{1,0:T(8,128)(2,1)S(1)}, u32[]{:S(2)}) copy-start(bf16[1024,384]{1,0:T(8,128)(2,1)S(1)} %broadcast_select_fusion) | copy-start | bytes 2359300
  114.2 4.4 %collective-permute-start.1 = (bf16[3,32,384]{2,1,0:T(8,128)(2,1)S(1)}, bf16[3,32,384]{2,1,0:T(8,128)(2,1)S(1)}, u32[]{:S(2)}, u32[]{:S(2)}) collective-permute-start(bf16[3,32,384]{2,1,0:T(8,128)(2,1)S(1)} %bitcast.120), channel_id=1, source_target_pairs={{16,0},{0,16},{17,1},{1,17},{18,2},{2,18},{19,3},{3,19},{20,4},{4,... | collective-permute-start | bytes 221192 | tf_op jit(solution)/shard_map/ppermute | solution.py:20
  114.8 4.6 %collective-permute-start = (bf16[3,32,384]{2,1,0:T(8,128)(2,1)S(1)}, bf16[3,32,384]{2,1,0:T(8,128)(2,1)S(1)}, u32[]{:S(2)}, u32[]{:S(2)}) collective-permute-start(bf16[3,32,384]{2,1,0:T(8,128)(2,1)S(1)} %bitcast.119), channel_id=1, source_target_pairs={{0,16},{16,0},{1,17},{17,1},{2,18},{18,2},{3,19},{19,3},{4,20},{20... | collective-permute-start | bytes 221192 | tf_op jit(solution)/shard_map/ppermute | solution.py:17
  119.4 7.6 %copy-start.7 = (f32[384]{0:T(512)S(1)}, f32[384]{0:T(512)}, u32[]{:S(2)}) copy-start(f32[384]{0:T(512)} %get-tuple-element.8) | copy-start | bytes 4612
  119.4 7.6 %copy-start.8 = (f32[384]{0:T(512)S(1)}, f32[384]{0:T(512)}, u32[]{:S(2)}) copy-start(f32[384]{0:T(512)} %get-tuple-element.9) | copy-start | bytes 4612
  119.4 7.6 %copy-start.9 = (f32[384]{0:T(512)S(1)}, f32[384]{0:T(512)}, u32[]{:S(2)}) copy-start(f32[384]{0:T(512)} %get-tuple-element.10) | copy-start | bytes 4612
  119.4 7.6 %copy-start.10 = (f32[384]{0:T(512)S(1)}, f32[384]{0:T(512)}, u32[]{:S(2)}) copy-start(f32[384]{0:T(512)} %get-tuple-element.11) | copy-start | bytes 4612
  119.4 7.6 %copy-start.11 = (f32[384]{0:T(512)S(1)}, f32[384]{0:T(512)}, u32[]{:S(2)}) copy-start(f32[384]{0:T(512)} %get-tuple-element.12) | copy-start | bytes 4612
  119.4 7.6 %copy-start.12 = (f32[384]{0:T(512)S(1)}, f32[384]{0:T(512)}, u32[]{:S(2)}) copy-start(f32[384]{0:T(512)} %get-tuple-element.13) | copy-start | bytes 4612
  119.4 7.6 %copy-start.13 = (f32[384]{0:T(512)S(1)}, f32[384]{0:T(512)}, u32[]{:S(2)}) copy-start(f32[384]{0:T(512)} %get-tuple-element.14) | copy-start | bytes 4612
  119.4 7.6 %copy-start.14 = (f32[384]{0:T(512)S(1)}, f32[384]{0:T(512)}, u32[]{:S(2)}) copy-start(f32[384]{0:T(512)} %get-tuple-element.15) | copy-start | bytes 4612
  119.5 7.6 %copy-start.15 = (f32[384]{0:T(512)S(1)}, f32[384]{0:T(512)}, u32[]{:S(2)}) copy-start(f32[384]{0:T(512)} %get-tuple-element.16) | copy-start | bytes 4612
  119.5 7.6 %copy-start.16 = (f32[384]{0:T(512)S(1)}, f32[384]{0:T(512)}, u32[]{:S(2)}) copy-start(f32[384]{0:T(512)} %get-tuple-element.17) | copy-start | bytes 4612
  119.5 7.6 %copy-start.17 = (f32[384]{0:T(512)S(1)}, f32[384]{0:T(512)}, u32[]{:S(2)}) copy-start(f32[384]{0:T(512)} %get-tuple-element.18) | copy-start | bytes 4612
  119.5 7.6 %copy-start.18 = (f32[384]{0:T(512)S(1)}, f32[384]{0:T(512)}, u32[]{:S(2)}) copy-start(f32[384]{0:T(512)} %get-tuple-element.19) | copy-start | bytes 4612
  119.5 7.6 %copy-start.19 = (f32[384]{0:T(512)S(1)}, f32[384]{0:T(512)}, u32[]{:S(2)}) copy-start(f32[384]{0:T(512)} %get-tuple-element.20) | copy-start | bytes 4612
  119.5 7.6 %copy-start.20 = (f32[384]{0:T(512)S(1)}, f32[384]{0:T(512)}, u32[]{:S(2)}) copy-start(f32[384]{0:T(512)} %get-tuple-element.21) | copy-start | bytes 4612
  119.5 7.6 %copy-start.21 = (f32[384]{0:T(512)S(1)}, f32[384]{0:T(512)}, u32[]{:S(2)}) copy-start(f32[384]{0:T(512)} %get-tuple-element.22) | copy-start | bytes 4612
  119.5 7.6 %copy-start.22 = (f32[384]{0:T(512)S(1)}, f32[384]{0:T(512)}, u32[]{:S(2)}) copy-start(f32[384]{0:T(512)} %get-tuple-element.23) | copy-start | bytes 4612
  119.5 7.6 %copy-start.23 = (f32[384]{0:T(512)S(1)}, f32[384]{0:T(512)}, u32[]{:S(2)}) copy-start(f32[384]{0:T(512)} %get-tuple-element.24) | copy-start | bytes 4612
  119.5 7.6 %copy-start.24 = (f32[384]{0:T(512)S(1)}, f32[384]{0:T(512)}, u32[]{:S(2)}) copy-start(f32[384]{0:T(512)} %get-tuple-element.25) | copy-start | bytes 4612
  119.6 7.6 %copy-start.25 = (f32[384]{0:T(512)S(1)}, f32[384]{0:T(512)}, u32[]{:S(2)}) copy-start(f32[384]{0:T(512)} %get-tuple-element.26) | copy-start | bytes 4612
  119.6 7.6 %copy-start.26 = (f32[384]{0:T(512)S(1)}, f32[384]{0:T(512)}, u32[]{:S(2)}) copy-start(f32[384]{0:T(512)} %get-tuple-element.27) | copy-start | bytes 4612
  119.6 7.6 %copy-start.27 = (f32[384]{0:T(512)S(1)}, f32[384]{0:T(512)}, u32[]{:S(2)}) copy-start(f32[384]{0:T(512)} %get-tuple-element.28) | copy-start | bytes 4612
  119.6 7.6 %copy-start.28 = (f32[384]{0:T(512)S(1)}, f32[384]{0:T(512)}, u32[]{:S(2)}) copy-start(f32[384]{0:T(512)} %get-tuple-element.29) | copy-start | bytes 4612
  119.6 7.6 %copy-start.29 = (f32[384]{0:T(512)S(1)}, f32[384]{0:T(512)}, u32[]{:S(2)}) copy-start(f32[384]{0:T(512)} %get-tuple-element.30) | copy-start | bytes 4612
  119.6 7.6 %copy-start.30 = (f32[384]{0:T(512)S(1)}, f32[384]{0:T(512)}, u32[]{:S(2)}) copy-start(f32[384]{0:T(512)} %get-tuple-element.31) | copy-start | bytes 4612
  119.6 7.6 %copy-start.31 = (f32[384]{0:T(512)S(1)}, f32[384]{0:T(512)}, u32[]{:S(2)}) copy-start(f32[384]{0:T(512)} %get-tuple-element.32) | copy-start | bytes 4612
  119.6 7.6 %copy-start.32 = (f32[384]{0:T(512)S(1)}, f32[384]{0:T(512)}, u32[]{:S(2)}) copy-start(f32[384]{0:T(512)} %get-tuple-element.33) | copy-start | bytes 4612
  119.6 7.6 %copy-start.33 = (f32[384]{0:T(512)S(1)}, f32[384]{0:T(512)}, u32[]{:S(2)}) copy-start(f32[384]{0:T(512)} %get-tuple-element.34) | copy-start | bytes 4612
  119.6 7.6 %copy-start.34 = (f32[384]{0:T(512)S(1)}, f32[384]{0:T(512)}, u32[]{:S(2)}) copy-start(f32[384]{0:T(512)} %get-tuple-element.35) | copy-start | bytes 4612
  119.7 7.6 %copy-start.35 = (f32[384]{0:T(512)S(1)}, f32[384]{0:T(512)}, u32[]{:S(2)}) copy-start(f32[384]{0:T(512)} %get-tuple-element.36) | copy-start | bytes 4612
  119.7 7.6 %copy-start.36 = (f32[384]{0:T(512)S(1)}, f32[384]{0:T(512)}, u32[]{:S(2)}) copy-start(f32[384]{0:T(512)} %get-tuple-element.37) | copy-start | bytes 4612
  119.7 7.6 %copy-start.37 = (f32[384]{0:T(512)S(1)}, f32[384]{0:T(512)}, u32[]{:S(2)}) copy-start(f32[384]{0:T(512)} %get-tuple-element.38) | copy-start | bytes 4612
  119.7 7.6 %copy-start.38 = (f32[384]{0:T(512)S(1)}, f32[384]{0:T(512)}, u32[]{:S(2)}) copy-start(f32[384]{0:T(512)} %get-tuple-element.39) | copy-start | bytes 4612
  119.7 7.6 %copy-start.39 = (f32[384]{0:T(512)S(1)}, f32[384]{0:T(512)}, u32[]{:S(2)}) copy-start(f32[384]{0:T(512)} %get-tuple-element.40) | copy-start | bytes 4612
  119.7 7.6 %copy-start.40 = (f32[384]{0:T(512)S(1)}, f32[384]{0:T(512)}, u32[]{:S(2)}) copy-start(f32[384]{0:T(512)} %get-tuple-element.41) | copy-start | bytes 4612
  119.8 6.7 %collective-permute-start.2 = (bf16[38,3,384]{2,1,0:T(4,128)(2,1)S(1)}, bf16[38,3,384]{2,1,0:T(4,128)(2,1)S(1)}, u32[]{:S(2)}, u32[]{:S(2)}) collective-permute-start(bf16[38,3,384]{2,1,0:T(4,128)(2,1)S(1)} %get-tuple-element.57), channel_id=1, source_target_pairs={{0,4},{4,8},{8,12},{12,0},{1,5},{5,9},{9,13},{13,1},{2,6},{6,10},{... | collective-permute-start | bytes 262664 | tf_op jit(solution)/shard_map/ppermute | solution.py:17
  119.9 6.6 %collective-permute-start.3 = (bf16[38,3,384]{2,1,0:T(4,128)(2,1)S(1)}, bf16[38,3,384]{2,1,0:T(4,128)(2,1)S(1)}, u32[]{:S(2)}, u32[]{:S(2)}) collective-permute-start(bf16[38,3,384]{2,1,0:T(4,128)(2,1)S(1)} %get-tuple-element.58), channel_id=1, source_target_pairs={{4,0},{8,4},{12,8},{0,12},{5,1},{9,5},{13,9},{1,13},{6,2},{10,6},{... | collective-permute-start | bytes 262664 | tf_op jit(solution)/shard_map/ppermute | solution.py:20
  139.3 1.1 copy-start.43
  (4 other events, 3.7 us)
Sparse Core Ops, SparseCore 0:
  80.5 132.9 reduce-scatter.1
where the time goes:
time: 231 us; the launch traced here: 230 us
  waiting for transfers between devices  81.7 us (35%)
  matrix products  42.4 us (18%)
  local copies, waits for them, and re-layouts  33.7 us (15%)
  other arithmetic  32.4 us (14%)
  starting transfers between devices  17.4 us (8%)
  between operations  14.8 us (6%)
  blocking collectives  7.22 us (3%)
    reduce_scatter x1, waiting for transfers between devices, body(): lax.psum_scatter(term, ('eta', 'phi', 'replica'), scatter_dimension=0, ti...  60.6 us
    reduce_sum x2, other arithmetic, plain_norm(): centre = jnp.mean(values, axis=-1, keepdims=True)  12.8 us
    dot_general x1, matrix products, body(): jnp.dot(dec_normed, w_up, preferred_element_type=jnp.float32)  8.74 us
    all_to_all x1, waiting for transfers between devices, body(): lax.all_to_all(outgoing, ('eta', 'phi'), split_axis=0, concat_axis=0, til...  8.72 us
    concatenate x1, other arithmetic, encoder_pass(): jnp.concatenate([lax.dot_general(grad_qkv, normed, contract_rows, preferr...  7.96 us
    all_to_all x1, waiting for transfers between devices, body(): lax.all_to_all(outbound.reshape(group_size, slot_count, feature_width), (...  7.45 us
    all_to_all x1, starting transfers between devices, body(): lax.all_to_all(outgoing, ('eta', 'phi'), split_axis=0, concat_axis=0, til...  7.25 us
    all_gather x1, blocking collectives, body(): lax.all_gather(grad_share.astype(jnp.bfloat16), 'replica', axis=0, tiled=...  7.22 us
  transfers between devices with their start and end apart: 7, of which 6 were waited for; matrix products, arithmetic and copies ran while one was open for 24% of the time, Pallas kernels for 0%

commit v1 on v0

v1 whole, which is shorter than its diff:
```python
import functools

import jax
import jax.numpy as jnp
from jax import lax
from jax.experimental import pallas as pl
from jax.experimental.pallas import tpu as pltpu
from jax.sharding import PartitionSpec as P

norm_eps = 1e-05
length_eps = 1e-06
f32 = jnp.float32
bf16 = jnp.bfloat16
MIB = 1024 * 1024

NN = (((1,), (0,)), ((), ()))
NT = (((1,), (1,)), ((), ()))
TN = (((0,), (0,)), ((), ()))


def mm(a, b, dims=NN):
    return lax.dot_general(a, b, dims, preferred_element_type=f32)


def vmem():
    return pl.BlockSpec(memory_space=pltpu.VMEM)


def smem():
    return pl.BlockSpec(memory_space=pltpu.SMEM)


def call(kernel, name, outs, in_specs, scratch=(), flops=0, nbytes=0, limit=48):
    single = not isinstance(outs, (list, tuple))
    out_list = [outs] if single else list(outs)
    specs = [vmem() for _ in out_list]
    return pl.pallas_call(
        kernel,
        out_shape=out_list[0] if single else tuple(out_list),
        in_specs=in_specs,
        out_specs=specs[0] if single else tuple(specs),
        scratch_shapes=list(scratch),
        compiler_params=pltpu.CompilerParams(vmem_limit_bytes=limit * MIB),
        cost_estimate=pl.CostEstimate(flops=flops, bytes_accessed=nbytes, transcendentals=0),
        name=name,
    )


def sds(shape, dtype):
    return jax.ShapeDtypeStruct(shape, dtype)


def column_of(row):
    return jnp.transpose(jnp.broadcast_to(row, (8, row.shape[1])))[:, 0:1]


def slot_column(pos_ref, wide_ref, padded):
    group, cap = pos_ref.shape
    wide_ref[...] = jnp.full(wide_ref.shape, -1.0, f32)
    wide_ref[:, 0:cap] = pos_ref[...].astype(f32)
    turned = jnp.transpose(wide_ref[...])
    return jnp.concatenate([turned[0:padded, d : d + 1] for d in range(group)], axis=0)


def pick_kernel(padded, pos_ref, tok_ref, out_ref, wide_ref):
    slots = slot_column(pos_ref, wide_ref, padded)
    cells = lax.broadcasted_iota(jnp.int32, (slots.shape[0], tok_ref.shape[0]), 1).astype(f32)
    chosen = (slots == cells).astype(f32).astype(bf16)
    out_ref[...] = mm(chosen, tok_ref[...]).astype(bf16)


def prep_kernel(cot_ref, wout_ref, wqkv_ref, ga_ref, cot_t_ref, wqkv_t_ref):
    ga_ref[...] = mm(wout_ref[...], cot_ref[...], NT).astype(bf16)
    cot_t_ref[...] = jnp.transpose(cot_ref[...])
    wqkv_t_ref[...] = jnp.transpose(wqkv_ref[...])


def forward_kernel(
    cap, padded, src_ref, win_ref, scale_ref, arr_ref, wqkv_t_ref, wout_ref, wdec_ref,
    out_ref, e_ref, p_ref, u_ref, len_ref, v_ref, att_ref,
):
    rows, width = e_ref.shape[1], e_ref.shape[2]
    heads = p_ref.shape[0]
    size = width // heads
    slots = arr_ref.shape[0]
    src = src_ref[...].astype(f32)
    slot_row = src + (padded - cap) * jnp.floor((src + 0.5) * (1.0 / cap))
    slot_col = column_of(slot_row)
    lanes = lax.broadcasted_iota(jnp.int32, (rows, slots), 1).astype(f32)
    pick = (slot_col == lanes).astype(f32).astype(bf16)
    enc_in = mm(pick, arr_ref[...])
    centred = enc_in - jnp.mean(enc_in, axis=-1, keepdims=True)
    spread = jnp.mean(centred * centred, axis=-1, keepdims=True)
    normed = (centred * lax.rsqrt(spread + norm_eps)).astype(bf16)
    e_ref[0] = normed
    u_ref[0:width] = mm(wqkv_t_ref[0:width], normed, NT)
    u_ref[width : 2 * width] = mm(wqkv_t_ref[width : 2 * width], normed, NT)
    v_ref[...] = mm(wqkv_t_ref[2 * width : 3 * width], normed, NT).astype(bf16)
    win = win_ref[...].astype(f32)
    same = column_of(win) == win
    for h in range(heads):
        lo, hi = h * size, (h + 1) * size
        q = u_ref[lo:hi]
        k = u_ref[width + lo : width + hi]
        q_inv = lax.rsqrt(jnp.sum(q * q, axis=0, keepdims=True) + length_eps)
        k_inv = lax.rsqrt(jnp.sum(k * k, axis=0, keepdims=True) + length_eps)
        q = q * q_inv
        k = k * k_inv
        u_ref[lo:hi] = q
        u_ref[width + lo : width + hi] = k
        len_ref[h : h + 1] = q_inv
        len_ref[heads + h : heads + h + 1] = k_inv
        scores = mm(k.astype(bf16), q.astype(bf16), TN)
        raised = jnp.where(same, jnp.exp(scores * scale_ref[h]), 0.0)
        weights = (raised * (1.0 / jnp.sum(raised, axis=0, keepdims=True))).astype(bf16)
        p_ref[h] = weights
        att_ref[lo:hi] = mm(v_ref[lo:hi], weights).astype(bf16)
    attended = jnp.transpose(att_ref[...])
    e_ref[1] = attended
    enc_out = (enc_in + mm(attended, wout_ref[...])).astype(bf16)
    dec = mm(enc_out, wdec_ref[...]).astype(bf16)
    places = lax.broadcasted_iota(jnp.int32, (slots, rows), 0).astype(f32)
    put = (places == slot_row).astype(f32).astype(bf16)
    out_ref[...] = mm(put, dec).astype(bf16)


def backward_kernel(
    split, me_ref, scale_ref, p_ref, u_ref, len_ref, v_ref, ga_ref, cot_t_ref, out_ref
):
    heads = p_ref.shape[0]
    width = v_ref.shape[0]
    size = width // heads
    unit = 32
    if split is not None:
        me = me_ref[0]
        per_shard, per_part = split[0] // unit, split[1] // unit

    def emit(start, block):
        for j in range(block.shape[0] // unit):
            u = (start + j * unit) // unit
            piece = block[j * unit : (j + 1) * unit]
            if split is None:
                out_ref[u * unit : (u + 1) * unit] = piece
            else:
                shard, rest = divmod(u, per_shard)
                part, place = divmod(rest, per_part)
                out_ref[me ^ part, shard, place * unit : (place + 1) * unit] = piece

    for h in range(heads):
        lo, hi = h * size, (h + 1) * size
        ga = ga_ref[lo:hi]
        low = p_ref[h]
        weights = low.astype(f32)
        grad_soft = mm(v_ref[lo:hi], ga, TN)
        part = weights * grad_soft
        total = jnp.sum(part, axis=0, keepdims=True)
        grad_scores = ((part - weights * total) * scale_ref[h]).astype(bf16)
        q = u_ref[lo:hi]
        k = u_ref[width + lo : width + hi]
        grad_v = mm(ga, low, NT)
        grad_q = mm(k.astype(bf16), grad_scores)
        grad_k = mm(q.astype(bf16), grad_scores, NT)
        grad_q = (grad_q - q * jnp.sum(q * grad_q, axis=0, keepdims=True)) * len_ref[h : h + 1]
        grad_k = (grad_k - k * jnp.sum(k * grad_k, axis=0, keepdims=True)) * len_ref[
            heads + h : heads + h + 1
        ]
        emit(lo, grad_q.astype(bf16))
        emit(width + lo, grad_k.astype(bf16))
        emit(2 * width + lo, grad_v.astype(bf16))
    emit(3 * width, cot_t_ref[...])


def term_kernel(
    qkv_shards, place_ref, l0, l1, l2, l3, e01, e2, e3, keep_ref, send_ref
):
    shards, part, rows = l0.shape
    half = shards // 2
    width = keep_ref.shape[-1]
    lhs = (l0, l1, l2, l3)

    def rhs(k, which):
        return (e01[0, which], e01[1, which], e2[which], e3[which])[k]

    def block(lo, hi, which):
        acc = None
        for k in range(4):
            left = lhs[k][lo:hi].reshape((hi - lo) * part, rows)
            step = mm(left, rhs(k, which))
            acc = step if acc is None else acc + step
        return acc.reshape(hi - lo, part, width)

    spans = []
    for lo, hi in ((0, half), (half, shards)):
        cut = min(max(qkv_shards, lo), hi)
        pieces = []
        if cut > lo:
            pieces.append((0, block(lo, cut, 0)))
        if hi > cut:
            pieces.append((cut - lo, block(cut, hi, 1)))
        spans.append(pieces)
    for mine in range(2):

        @pl.when(place_ref[0] == mine)
        def _():
            for at, value in spans[mine]:
                keep_ref[at : at + value.shape[0]] = value
            for at, value in spans[1 - mine]:
                send_ref[at : at + value.shape[0]] = value.astype(bf16)


def line_kernel(place_ref, keep_ref, got_ref, own_ref, send_ref):
    count = keep_ref.shape[0]
    me = place_ref[0]
    for k in range(count):
        at = lax.rem(me + k, count)
        value = keep_ref[at] + got_ref[at].astype(f32)
        if k == 0:
            own_ref[...] = value
        else:
            send_ref[k - 1] = value.astype(bf16)


def close_kernel(own_ref, *refs):
    total = own_ref[...]
    for ref in refs[:-1]:
        total = total + ref[...].astype(f32)
    refs[-1][...] = total.astype(bf16)


def spread_kernel(me_ref, first_ref, second_ref, out_ref):
    me = me_ref[0]
    out_ref[me] = first_ref[0].astype(f32)
    out_ref[me ^ 2] = first_ref[1].astype(f32)
    out_ref[me ^ 1] = second_ref[0].astype(f32)
    out_ref[me ^ 3] = second_ref[1].astype(f32)


def flip(value, axis, bit):
    return lax.ppermute(value, axis, [(i, i ^ bit) for i in range(lax.axis_size(axis))])


def turn(value, axis, k):
    count = lax.axis_size(axis)
    return lax.ppermute(value, axis, [(i, (i + k) % count) for i in range(count)])


def extended(block, sides, width):
    for axis, dim in sides:
        low = turn(lax.slice_in_dim(block, block.shape[dim] - width, None, axis=dim), axis, 1)
        high = turn(lax.slice_in_dim(block, 0, width, axis=dim), axis, -1)
        block = jnp.concatenate([low, block, high], axis=dim)
    return block


def plain_norm(values):
    centre = jnp.mean(values, axis=-1, keepdims=True)
    centred = values - centre
    spread = jnp.mean(centred * centred, axis=-1, keepdims=True)
    return centred * lax.rsqrt(spread + norm_eps)


def summed_slow(left, both, width):
    qkv_rows = left.shape[0] - width
    term = jnp.concatenate([mm(left[:qkv_rows], both[0]), mm(left[qkv_rows:], both[1])], axis=0)
    share = lax.psum_scatter(term, ("eta", "phi", "replica"), scatter_dimension=0, tiled=True)
    return lax.all_gather(share.astype(bf16), "replica", axis=0, tiled=True).astype(f32)


def summed_fast(left, both, width, phi_count):
    shards, part, rows = left.shape[1:]
    pair = jnp.stack([both, flip(both, "replica", 2)])
    e01 = pair
    other = flip(pair, "replica", 1)
    got = [flip(left[k], "replica", k) for k in (1, 2, 3)]
    place = lax.axis_index("eta").astype(jnp.int32).reshape(1)
    keep, send = call(
        functools.partial(term_kernel, shards * 3 // 4),
        "terms",
        [sds((shards // 2, part, width), f32), sds((shards // 2, part, width), bf16)],
        [smem()] + [vmem()] * 7,
        flops=2 * shards * part * width * rows * 4,
        nbytes=8 * MIB,
    )(place, left[0], got[1], got[0], got[2], e01, other[0], other[1])
    arrived = turn(send, "eta", 1)
    line = lax.axis_index("phi").astype(jnp.int32).reshape(1)
    own, outgoing = call(
        line_kernel,
        "line",
        [sds((part, width), f32), sds((phi_count - 1, part, width), bf16)],
        [smem(), vmem(), vmem()],
        flops=shards * part * width,
        nbytes=3 * MIB,
    )(line, keep, arrived)
    pieces = [turn(outgoing[k - 1], "phi", k) for k in range(1, phi_count)]
    mine = call(
        close_kernel,
        "close",
        sds((part, width), bf16),
        [vmem()] * phi_count,
        flops=4 * part * width,
        nbytes=MIB,
    )(own, *pieces)
    first = jnp.stack([mine, flip(mine, "replica", 2)])
    second = flip(first, "replica", 1)
    me = lax.axis_index("replica").astype(jnp.int32).reshape(1)
    whole = call(
        spread_kernel,
        "spread",
        sds((4, part, width), f32),
        [smem(), vmem(), vmem()],
        flops=4 * part * width,
        nbytes=2 * MIB,
    )(me, first, second)
    return whole.reshape(4 * part, width)


def body(
    tokens, send_pos, enc_src, window_id, enc_cot, w_qkv, head_scale, w_out, w_dec_in,
    mask_token, conv_kernel, w_up, w_down, w_head,
):
    eta_cells, phi_cells, width = tokens.shape[1:]
    dec_width = w_dec_in.shape[1]
    tile_len = eta_cells * phi_cells
    eta_count = lax.axis_size("eta")
    phi_count = lax.axis_size("phi")
    replicas = lax.axis_size("replica")
    group = eta_count * phi_count
    cap = send_pos.shape[-1]
    padded = -(-cap // 8) * 8
    slots = group * padded
    rows = enc_cot.shape[-2]
    heads = head_scale.shape[0]
    out_rows = 4 * width
    shard_rows = out_rows // group
    part_rows = shard_rows // replicas
    fast = eta_count == 2 and replicas == 4 and part_rows % 32 == 0

    positions = send_pos.reshape(group, cap)
    outgoing = call(
        functools.partial(pick_kernel, padded),
        "pick",
        sds((slots, width), bf16),
        [vmem(), vmem()],
        scratch=[pltpu.VMEM((group, 128), f32)],
        flops=2 * slots * tile_len * width,
        nbytes=3 * MIB,
    )(positions, tokens.reshape(tile_len, width))
    arrived = lax.all_to_all(
        outgoing.reshape(group, padded, width), ("eta", "phi"), split_axis=0, concat_axis=0,
        tiled=True,
    ).reshape(slots, width)

    cotangent = enc_cot.reshape(rows, width)
    grad_att, cot_t, w_qkv_t = call(
        prep_kernel,
        "prep",
        [sds((width, rows), bf16), sds((width, rows), bf16), sds((3 * width, width), bf16)],
        [vmem()] * 3,
        flops=2 * rows * width * width,
        nbytes=10 * MIB,
    )(cotangent, w_out, w_qkv)

    outbound, both, weights, units, lengths, values = call(
        functools.partial(forward_kernel, cap, padded),
        "forward",
        [
            sds((slots, dec_width), bf16),
            sds((2, rows, width), bf16),
            sds((heads, rows, rows), bf16),
            sds((2 * width, rows), f32),
            sds((2 * heads, rows), f32),
            sds((width, rows), bf16),
        ],
        [vmem(), vmem(), smem(), vmem(), vmem(), vmem(), vmem()],
        scratch=[pltpu.VMEM((width, rows), bf16)],
        flops=2 * rows * width * width * 5,
        nbytes=10 * MIB,
    )(
        enc_src.reshape(1, rows), window_id.reshape(1, rows), head_scale, arrived, w_qkv_t,
        w_out, w_dec_in,
    )
    returned = lax.all_to_all(
        outbound.reshape(group, padded, dec_width), ("eta", "phi"), split_axis=0, concat_axis=0,
        tiled=True,
    )

    me = lax.axis_index("replica").astype(jnp.int32).reshape(1)
    left_shape = (replicas, group, part_rows, rows) if fast else (out_rows, rows)
    left = call(
        functools.partial(backward_kernel, (shard_rows, part_rows) if fast else None),
        "backward",
        sds(left_shape, bf16),
        [smem(), smem()] + [vmem()] * 6,
        flops=2 * rows * rows * width * 5,
        nbytes=10 * MIB,
    )(me, head_scale, weights, units, lengths, values, grad_att, cot_t)
    if fast:
        grad_total = summed_fast(left, both, width, phi_count)
    else:
        grad_total = summed_slow(left, both, width)

    dec_slots = returned[:, :cap].reshape(group * cap, dec_width)
    slot_cells = send_pos.reshape(group * cap)
    filled = jnp.zeros((tile_len, dec_width), bf16).at[slot_cells].set(dec_slots, mode="drop")
    seen_cells = jnp.zeros((tile_len,), jnp.bool_).at[slot_cells].set(True, mode="drop")
    dec_grid = jnp.where(seen_cells[:, None], filled, mask_token).reshape(
        eta_cells, phi_cells, dec_width
    )
    kernel_span = conv_kernel.shape[0]
    rim_width = kernel_span // 2
    full = extended(dec_grid, (("eta", 0), ("phi", 1)), rim_width)
    eta_place = lax.axis_index("eta")
    rim_line = lax.broadcasted_iota(jnp.int32, (eta_cells + 2 * rim_width, 1, 1), 0)
    keep_rim = jnp.logical_and(
        jnp.logical_or(rim_line >= rim_width, eta_place > 0),
        jnp.logical_or(rim_line < eta_cells + rim_width, eta_place < eta_count - 1),
    )
    full = jnp.where(keep_rim, full, jnp.zeros((), full.dtype))
    mixed_cells = jnp.zeros((eta_cells, phi_cells, dec_width), f32)
    for row_shift in range(kernel_span):
        for col_shift in range(kernel_span):
            window_cells = full[
                row_shift : row_shift + eta_cells, col_shift : col_shift + phi_cells
            ].astype(f32)
            mixed_cells = mixed_cells + conv_kernel[row_shift, col_shift] * window_cells
    dec_normed = plain_norm(mixed_cells).astype(bf16).reshape(tile_len, dec_width)
    hidden = jax.nn.gelu(mm(dec_normed, w_up), approximate=False).astype(bf16)
    decoded = (dec_grid.reshape(tile_len, dec_width).astype(f32) + mm(hidden, w_down)).astype(bf16)
    reconstruction = mm(decoded, w_head).reshape(1, eta_cells, phi_cells, -1)
    return (grad_total, reconstruction)


def solution(mesh):
    in_specs = (
        P("replica", "eta", "phi", None),
        P("replica", "eta", "phi", None, None),
        P("replica", "eta", "phi", None),
        P("replica", "eta", "phi", None),
        P("replica", "eta", "phi", None, None),
        P(), P(), P(), P(), P(), P(), P(), P(), P(),
    )
    out_specs = (P(("eta", "phi"), None), P("replica", "eta", "phi", None))
    return jax.shard_map(body, mesh=mesh, in_specs=in_specs, out_specs=out_specs, check_vma=False)
```

time: 231 us -> 141 us (0.61)
  waiting for transfers between devices: 81.7 us -> 34.8 us
  matrix products: 42.4 us -> 12.2 us
  Pallas kernels: 0 us -> 21.2 us
  other arithmetic: 32.4 us -> 16.7 us
  between operations: 14.8 us -> 1.6 us
  starting transfers between devices: 17.4 us -> 25.7 us
  blocking collectives: 7.22 us -> 0 us
  local copies, waits for them, and re-layouts: 33.7 us -> 26.8 us
    reduce_scatter x1 -> x0, waiting for transfers between devices: 60.6 us -> none  [body(): lax.psum_scatter(term, ('eta', 'phi', 'replica'), scatter_dimension=0, ti...]
    dot_general x14 -> x2, matrix products: 42.4 us -> 12.2 us  [mm(): return lax.dot_general(a, b, dims, preferred_element_type=f32)]
    pallas_call x0 -> x8, Pallas kernels: none -> 21.2 us  [the longest x1 8.2 us: body(): call(functools.partial(forward_kernel, cap, padded), 'forward', [sds((slo...]
    ppermute x4 -> x15, waiting for transfers between devices: 4.94 us -> 25.9 us  [the longest x8 25.9 us: turn(): lax.ppermute(value, axis, [(i, (i + k) % count) for i in range(count)])]
    unnamed x90 -> x132, local copies, waits for them, and re-layouts: 2.44 us -> 13.6 us
    gather x3 -> x0, local copies, waits for them, and re-layouts: 9.69 us -> none  [the longest x2 6.49 us: body(): jnp.take(flat_tile, jnp.minimum(slot_cells, tile_len - 1), axis=0)]
    ppermute x4 -> x15, starting transfers between devices: 5.96 us -> 15 us  [the longest x8 11.8 us: turn(): lax.ppermute(value, axis, [(i, (i + k) % count) for i in range(count)])]
    concatenate x1 -> x0, other arithmetic: 7.96 us -> none  [encoder_pass(): jnp.concatenate([lax.dot_general(grad_qkv, normed, contract_rows, preferr...]
  transfers between devices with their start and end apart: 7 -> 17, of which waited for: 6 -> 6; matrix products, arithmetic and copies ran while one was open for 24% -> 30% of each run, Pallas kernels for 0% -> 5%
where the time goes in v1:
time: 141 us; the launch traced here: 139 us
  waiting for transfers between devices  34.8 us (25%)
  local copies, waits for them, and re-layouts  26.8 us (19%)
  starting transfers between devices  25.7 us (18%)
  Pallas kernels  21.2 us (15%)
  other arithmetic  16.7 us (12%)
  matrix products  12.2 us (9%)
  between operations  1.6 us (1%)
    ppermute x8, waiting for transfers between devices, turn(): lax.ppermute(value, axis, [(i, (i + k) % count) for i in range(count)])  25.9 us
    unnamed x132, local copies, waits for them, and re-layouts  13.6 us
    reduce_sum x1, other arithmetic, plain_norm(): centre = jnp.mean(values, axis=-1, keepdims=True)  12.2 us
    dot_general x2, matrix products, mm(): return lax.dot_general(a, b, dims, preferred_element_type=f32)  12.2 us
    ppermute x8, starting transfers between devices, turn(): lax.ppermute(value, axis, [(i, (i + k) % count) for i in range(count)])  11.8 us
    all_to_all x1, waiting for transfers between devices, body(): lax.all_to_all(outgoing.reshape(group, padded, width), ('eta', 'phi'), sp...  8.92 us
    pallas_call x1, Pallas kernels, body(): call(functools.partial(forward_kernel, cap, padded), 'forward', [sds((slo...  8.2 us
    all_to_all x1, starting transfers between devices, body(): lax.all_to_all(outgoing.reshape(group, padded, width), ('eta', 'phi'), sp...  7.25 us
  transfers between devices with their start and end apart: 17, of which 6 were waited for; matrix products, arithmetic and copies ran while one was open for 30% of the time, Pallas kernels for 5%

profile of v1, /device:TPU:0, one launch (start us, length us, event | category | flops | bytes accessed | tf_op | source)
XLA Modules:
  0.0 139.0 jit_solution(14214965467590719763)
XLA Ops:
  0.7 1.5 %copy-done.3 = bf16[1,32,32,768]{3,2,1,0:T(8,128)(2,1)S(1)} copy-done((bf16[1,32,32,768]{3,2,1,0:T(8,128)(2,1)S(1)}, bf16[1,32,32,768]{3,2,1,0:T(8,128)(2,1)}, u32[]{:S(2)}) %copy-start.3) | copy-done | bytes 1572888
  2.2 0.7 copy-done.14
  2.9 1.7 %pick.1 = bf16[320,768]{1,0:T(8,128)(2,1)} custom-call(s32[8,35]{1,0:T(8,128)S(1)} %bitcast.53, bf16[1024,768]{1,0:T(8,128)(2,1)S(1)} %bitcast.48), custom_call_target="tpu_custom_call" | custom-call | flops 503316480 | bytes 3145728 | tf_op jit(solution)/shard_map/pick/pallas_call | solution.py:339
  4.5 7.3 %all-to-all-start = ((bf16[8,40,768]{2,1,0:T(8,128)(2,1)}), bf16[8,40,768]{2,1,0:T(8,128)(2,1)S(1)}, u32[]{:S(2)}, u32[]{:S(2)}) async-start(bf16[8,40,768]{2,1,0:T(8,128)(2,1)} %bitcast.7), calls=%async_computation | async-start | bytes 983040 | tf_op jit(solution)/shard_map/all_to_all | solution.py:348
  11.9 3.1 %prep.1 = (bf16[768,256]{1,0:T(8,128)(2,1)S(1)}, bf16[768,256]{1,0:T(8,128)(2,1)S(1)}, bf16[2304,768]{1,0:T(8,128)(2,1)S(1)}) custom-call(bf16[256,768]{1,0:T(8,128)(2,1)S(1)} %bitcast.51, bf16[768,768]{1,0:T(8,128)(2,1)S(1)} %copy-done.1, bf16[768,2304]{1,0:T(8,128)(2,1)} %wqkv_ref.1), custom_call_target="tpu_custom_call" | custom-call | flops 301989888 | bytes 10485760 | tf_op jit(solution)/shard_map/prep/pallas_call | solution.py:354
  15.1 1.7 %copy-done.2 = bf16[2304,768]{1,0:T(8,128)(2,1)} copy-done((bf16[2304,768]{1,0:T(8,128)(2,1)}, bf16[2304,768]{1,0:T(8,128)(2,1)S(1)}, u32[]{:S(2)}) %copy-start.2) | copy-done | bytes 3538968
  16.8 0.8 copy-done.9
  17.6 8.9 %all-to-all-done = bf16[8,40,768]{2,1,0:T(8,128)(2,1)S(1)} async-done(((bf16[8,40,768]{2,1,0:T(8,128)(2,1)}), bf16[8,40,768]{2,1,0:T(8,128)(2,1)S(1)}, u32[]{:S(2)}, u32[]{:S(2)}) %all-to-all-start) | async-done | bytes 491552 | tf_op jit(solution)/shard_map/all_to_all | solution.py:348
  26.5 1.1 copy-done.7
  27.6 8.2 %forward.1 = (bf16[320,384]{1,0:T(8,128)(2,1)S(1)}, bf16[2,256,768]{2,1,0:T(8,128)(2,1)S(1)}, bf16[12,256,256]{2,1,0:T(8,128)(2,1)S(1)}, f32[1536,256]{1,0:T(8,1...) custom-call(s32[1,256]{1,0:T(1,128)S(1)} %bitcast.54, s32[1,256]{1,0:T(1,128)S(1)} %bitcast.55, ...), custom_call_target="tpu_custom_call" | custom-call | flops 1509949440 | bytes 10485760 | tf_op jit(solution)/shard_map/forward/pallas_call | solution.py:363
  35.8 1.2 copy-done.4
  36.9 0.7 copy-done.11
  37.7 0.7 copy-done.13
  38.4 3.4 %all-to-all-start.1 = ((bf16[8,40,384]{2,1,0:T(8,128)(2,1)}), bf16[8,40,384]{2,1,0:T(8,128)(2,1)S(1)}, u32[]{:S(2)}, u32[]{:S(2)}) async-start(bf16[8,40,384]{2,1,0:T(8,128)(2,1)} %bitcast.52), calls=%async_computation.1 | async-start | bytes 491520 | tf_op jit(solution)/shard_map/all_to_all | solution.py:382
  41.8 2.1 %scatter_custom_fusion = pred[1024]{0:T(1024)(128)(4,1)} fusion(s32[280]{0:T(512)S(1)} %fusion.15, pred[280]{0:T(512)(128)(4,1)S(1)} %broadcast.68, pred[]{:T(512)} %constant.8.clone.1), kind=kCustom, calls=%fused_computation.48 | custom fusion | bytes 1025 | tf_op jit(solution)/shard_map/scatter | solution.py:405
  44.0 1.6 %slice_reduce_fusion.46 = (f32[384]{0:T(512)S(1)}, f32[384]{0:T(512)S(1)}, f32[384]{0:T(512)S(1)}, f32[384]{0:T(512)S(1)}, f32[384]{0:T(512)S(1)}, /*index=5*/f3...) fusion(f32[7,7,384]{2,1,0:T(8,128)} %param.24), kind=kLoop, calls=%fused_computation.97 | loop fusion | bytes 33792 | tf_op jit(solution)/shard_map/slice | solution.py:425
  45.5 1.9 %slice_reduce_fusion.48 = (f32[384]{0:T(512)}, f32[384]{0:T(512)}, f32[384]{0:T(512)}, f32[384]{0:T(512)}, f32[384]{0:T(512)}, /*index=5*/f32[384]{0:T(512)}, f3...) fusion(f32[7,7,384]{2,1,0:T(8,128)} %param.24), kind=kLoop, calls=%fused_computation.99 | loop fusion | bytes 58368 | tf_op jit(solution)/shard_map/slice | solution.py:425
  47.4 1.9 %slice_reduce_fusion.47 = (f32[384]{0:T(512)}, f32[384]{0:T(512)}, f32[384]{0:T(512)}, f32[384]{0:T(512)}, f32[384]{0:T(512)}, /*index=5*/f32[384]{0:T(512)}, f3...) fusion(f32[7,7,384]{2,1,0:T(8,128)} %param.24), kind=kLoop, calls=%fused_computation.98 | loop fusion | bytes 58368 | tf_op jit(solution)/shard_map/slice | solution.py:425
  49.4 1.5 %collective-permute-start.3 = (bf16[2,256,768]{2,1,0:T(8,128)(2,1)S(1)}, bf16[2,256,768]{2,1,0:T(8,128)(2,1)}, u32[]{:S(2)}, u32[]{:S(2)}) collective-permute-start(bf16[2,256,768]{2,1,0:T(8,128)(2,1)S(1)} %get-tuple-element.22), channel_id=1, source_target_pairs={{0,2},{1,3},{2,0},{3,1},{4,6},{5,7},{6,4},{7,5},{8,10},{9,11},{10,... | collective-permute-start | bytes 2359304 | tf_op jit(solution)/shard_map/ppermute | solution.py:239
  50.9 0.7 copy-done.22
  51.6 1.8 %reshape.143 = bf16[280,384]{1,0:T(8,128)(2,1)} reshape(bf16[8,35,384]{2,1,0:T(8,128)(2,1)} %bitcast.59) | data formatting | bytes 430080 | tf_op jit(solution)/shard_map/reshape | solution.py:402
  53.4 2.9 %scatter_custom_fusion.1 = bf16[1024,384]{1,0:T(8,128)(2,1)} fusion(s32[280]{0:T(512)} %copy-done.62, bf16[280,384]{1,0:T(8,128)(2,1)} %reshape.143, bf16[]{:T(256)} %constant.12.clone.1), kind=kCustom, calls=%fused_computation.35 | custom fusion | bytes 786944 | tf_op jit(solution)/shard_map/scatter | solution.py:404
  56.3 1.3 broadcast_select_fusion
  57.7 0.9 copy-done.18
  58.6 0.7 fusion.17
  59.2 1.9 %collective-permute-start.11 = (bf16[3,32,384]{2,1,0:T(8,128)(2,1)}, bf16[3,32,384]{2,1,0:T(8,128)(2,1)S(1)}, u32[]{:S(2)}, u32[]{:S(2)}) collective-permute-start(bf16[3,32,384]{2,1,0:T(8,128)(2,1)} %bitcast.25), channel_id=1, source_target_pairs={{0,16},{16,0},{1,17},{17,1},{2,18},{18,2},{3,19},{19,3},{4,20},{20... | collective-permute-start | bytes 221192 | tf_op jit(solution)/shard_map/ppermute | solution.py:244
  61.8 1.4 %copy-done.6 = f32[1536,256]{1,0:T(8,128)S(1)} copy-done((f32[1536,256]{1,0:T(8,128)S(1)}, f32[1536,256]{1,0:T(8,128)}, u32[]{:S(2)}) %copy-start.6) | copy-done | bytes 1572888
  63.2 1.0 copy-done.10
  64.2 1.0 copy-done.12
  65.2 4.0 %backward.1 = bf16[4,8,96,256]{3,2,1,0:T(8,128)(2,1)S(1)} custom-call(s32[1]{0:T(128)} %bitcast.me_ref, f32[12]{0:T(128)S(1)} %copy-done.15, bf16[12,256,256]{2,1,0:T(8,128)(2,1)S(1)} %copy-done.5, f32[1536,256]{1,0:T(8,128)S(1)} %copy-done.6, f32[24,256]{1,0:T(8,128)S(1)} %get-tuple-element.18.len_ref, bf16[768,256]{1,0:T(8,128)(2,1)S(1)} %copy-done.12, ...), custom_call_target="tpu_custom_call" | custom-call | flops 503316480 | bytes 10485760 | tf_op jit(solution)/shard_map/backward/pallas_call | solution.py:389
  69.4 2.0 %collective-permute-start.13 = (bf16[38,3,384]{2,1,0:T(4,128)(2,1)S(1)}, bf16[38,3,384]{2,1,0:T(4,128)(2,1)S(1)}, u32[]{:S(2)}, u32[]{:S(2)}) collective-permute-start(bf16[38,3,384]{2,1,0:T(4,128)(2,1)S(1)} %get-tuple-element.85), channel_id=1, source_target_pairs={{0,4},{4,8},{8,12},{12,0},{1,5},{5,9},{9,13},{13,1},{2,6},{6,10},{... | collective-permute-start | bytes 262664 | tf_op jit(solution)/shard_map/ppermute | solution.py:244
  71.3 1.9 %collective-permute-start.14 = (bf16[38,3,384]{2,1,0:T(4,128)(2,1)S(1)}, bf16[38,3,384]{2,1,0:T(4,128)(2,1)S(1)}, u32[]{:S(2)}, u32[]{:S(2)}) collective-permute-start(bf16[38,3,384]{2,1,0:T(4,128)(2,1)S(1)} %get-tuple-element.86), channel_id=1, source_target_pairs={{0,12},{4,0},{8,4},{12,8},{1,13},{5,1},{9,5},{13,9},{2,14},{6,2},{... | collective-permute-start | bytes 262664 | tf_op jit(solution)/shard_map/ppermute | solution.py:244
  73.3 0.9 collective-permute-start
  74.3 1.9 %collective-permute-done.13 = bf16[38,3,384]{2,1,0:T(4,128)(2,1)S(1)} collective-permute-done((bf16[38,3,384]{2,1,0:T(4,128)(2,1)S(1)}, bf16[38,3,384]{2,1,0:T(4,128)(2,1)S(1)}, u32[]{:S(2)}, u32[]{:S(2)}) %collective-permute-start.13) | collective-permute-done | bytes 87584 | tf_op jit(solution)/shard_map/ppermute | solution.py:244
  76.1 1.1 collective-permute-done.14
  78.2 1.3 pad_maximum_fusion.e01
  79.9 12.2 %fusion.16 = (f32[32,32]{1,0:T(8,128)S(1)}, f32[32,32,384]{2,1,0:T(8,128)S(1)}) fusion(bf16[38,38,384]{2,1,0:T(8,128)(2,1)S(1)} %maximum_select_fusion, f32[384]{0:T(512)S(1)} %copy-done.23, f32[384]{0:T(512)S(1)} %copy-done.24, f32[384]{0:T(512)S(1)} %copy-done.26, f32[384]{0:T(512)S(1)} %copy-done.27, f32[384]{0:T(512)S(1)} %copy-done.28, ...), kind=kLoop, calls=%fused_computation.100 | loop fusion | flops 57801728 | bytes 40187392 | tf_op jit(solution)/shard_map/reduce_sum | solution.py:256
  92.3 2.9 %terms.1 = (f32[4,96,768]{2,1,0:T(8,128)S(1)}, bf16[4,96,768]{2,1,0:T(8,128)(2,1)S(1)}) custom-call(s32[1]{0:T(128)} %bitcast.2.place_ref, bf16[8,96,256]{2,1,0:T(8,128)(2,1)S(1)} %get-tuple-element.84.l0, bf16[8,96,256]{2,1,0:T(8,128)(2,1)S(1)} %collective-permute-done.l1, bf16[8,96,256]{2,1,0:T(8,128)(2,1)S(1)} %collective-permute-done.1.l2, ...), custom_call_target="tpu_custom_call" | custom-call | flops 1207959552 | bytes 8388608 | tf_op jit(solution)/shard_map/terms/pallas_call | solution.py:276
  95.2 1.7 %collective-permute-start.5 = (bf16[4,96,768]{2,1,0:T(8,128)(2,1)S(1)}, bf16[4,96,768]{2,1,0:T(8,128)(2,1)S(1)}, u32[]{:S(2)}, u32[]{:S(2)}) collective-permute-start(bf16[4,96,768]{2,1,0:T(8,128)(2,1)S(1)} %get-tuple-element.24), channel_id=1, source_target_pairs={{0,16},{16,0},{1,17},{17,1},{2,18},{18,2},{3,19},{19,3},{4,20},{20... | collective-permute-start | bytes 1769480 | tf_op jit(solution)/shard_map/ppermute | solution.py:244
  97.3 13.7 %collective-permute-done.5.got_ref = bf16[4,96,768]{2,1,0:T(8,128)(2,1)S(1)} collective-permute-done((bf16[4,96,768]{2,1,0:T(8,128)(2,1)S(1)}, bf16[4,96,768]{2,1,0:T(8,128)(2,1)S(1)}, u32[]{:S(2)}, u32[]{:S(2)}) %collective-permute-start.5) | collective-permute-done | bytes 589856 | tf_op jit(solution)/shard_map/ppermute | solution.py:244
  111.1 0.8 collective-permute-start.6
  112.0 2.6 %collective-permute-start.7 = (bf16[96,768]{1,0:T(8,128)(2,1)S(1)}, bf16[96,768]{1,0:T(8,128)(2,1)S(1)}, u32[]{:S(2)}, u32[]{:S(2)}) collective-permute-start(bf16[96,768]{1,0:T(8,128)(2,1)S(1)} %get-tuple-element.90), channel_id=1, source_target_pairs={{0,8},{4,12},{8,0},{12,4},{1,9},{5,13},{9,1},{13,5},{2,10},{6,14},... | collective-permute-start | bytes 442376 | tf_op jit(solution)/shard_map/ppermute | solution.py:244
  114.5 0.8 collective-permute-start.8
  115.7 4.1 %collective-permute-done.6.refs_0_ = bf16[96,768]{1,0:T(8,128)(2,1)S(1)} collective-permute-done((bf16[96,768]{1,0:T(8,128)(2,1)S(1)}, bf16[96,768]{1,0:T(8,128)(2,1)S(1)}, u32[]{:S(2)}, u32[]{:S(2)}) %collective-permute-start.6) | collective-permute-done | bytes 147488 | tf_op jit(solution)/shard_map/ppermute | solution.py:244
  119.8 5.1 %collective-permute-done.7.refs_1_ = bf16[96,768]{1,0:T(8,128)(2,1)S(1)} collective-permute-done((bf16[96,768]{1,0:T(8,128)(2,1)S(1)}, bf16[96,768]{1,0:T(8,128)(2,1)S(1)}, u32[]{:S(2)}, u32[]{:S(2)}) %collective-permute-start.7) | collective-permute-done | bytes 147488 | tf_op jit(solution)/shard_map/ppermute | solution.py:244
  125.6 8.8 %fusion.2 = bf16[1024,768]{1,0:T(8,128)(2,1)} fusion(bf16[1024,384]{1,0:T(8,128)(2,1)S(1)} %bitcast.60, bf16[384,768]{1,0:T(8,128)(2,1)S(1)} %copy-done), kind=kOutput, calls=%fused_computation.5 | convolution fusion | flops 655097856 | bytes 2949120 | tf_op jit(solution)/shard_map/dot_general | solution.py:22
  134.5 3.4 %fusion.10 = f32[1024,128]{1,0:T(8,128)} fusion(bf16[384,128]{1,0:T(8,128)(2,1)S(1)} %copy-done.65, bf16[1024,384]{1,0:T(8,128)(2,1)S(1)} %copy-done.20, bf16[1024,768]{1,0:T(8,128)(2,1)} %fusion.2, bf16[768,384]{1,0:T(8,128)(2,1)S(1)} %copy-done.64), kind=kOutput, calls=%fused_computation.26 | convolution fusion | flops 705822720 | bytes 3571712 | tf_op jit(solution)/shard_map/dot_general | solution.py:22
  137.9 1.1 spread.1
  (152 shorter events, 3.5 us)
Async XLA Ops:
  0.6 125.0 %copy-start = (bf16[384,768]{1,0:T(8,128)(2,1)S(1)}, bf16[384,768]{1,0:T(8,128)(2,1)}, u32[]{:S(2)}) copy-start(bf16[384,768]{1,0:T(8,128)(2,1)} %param.25) | copy-start | bytes 1769476
  0.6 11.2 %copy-start.1 = (bf16[768,768]{1,0:T(8,128)(2,1)S(1)}, bf16[768,768]{1,0:T(8,128)(2,1)}, u32[]{:S(2)}) copy-start(bf16[768,768]{1,0:T(8,128)(2,1)} %wout_ref.3) | copy-start | bytes 3538948
  2.9 9.0 %copy-start.8 = (bf16[1,1,1,256,768]{4,3,2,1,0:T(8,128)(2,1)S(1)}, bf16[1,1,1,256,768]{4,3,2,1,0:T(8,128)(2,1)}, u32[]{:S(2)}) copy-start(bf16[1,1,1,256,768]{4,3,2,1,0:T(8,128)(2,1)} %param.18) | copy-start | bytes 1179652
  4.5 21.9 %all-to-all-start = ((bf16[8,40,768]{2,1,0:T(8,128)(2,1)}), bf16[8,40,768]{2,1,0:T(8,128)(2,1)S(1)}, u32[]{:S(2)}, u32[]{:S(2)}) async-start(bf16[8,40,768]{2,1,0:T(8,128)(2,1)} %bitcast.7), calls=%async_computation | async-start | bytes 983040 | tf_op jit(solution)/shard_map/all_to_all | solution.py:348
  11.9 14.6 %copy-start.15 = (f32[12]{0:T(128)S(1)}, f32[12]{0:T(128)}, u32[]{:S(2)}) copy-start(f32[12]{0:T(128)} %scale_ref.3) | copy-start | bytes 148
  11.9 14.6 %copy-start.16 = (s32[1,1,1,256]{3,2,1,0:T(1,128)S(1)}, s32[1,1,1,256]{3,2,1,0:T(1,128)}, u32[]{:S(2)}) copy-start(s32[1,1,1,256]{3,2,1,0:T(1,128)} %param.16) | copy-start | bytes 3076
  11.9 14.6 %copy-start.17 = (s32[1,1,1,256]{3,2,1,0:T(1,128)S(1)}, s32[1,1,1,256]{3,2,1,0:T(1,128)}, u32[]{:S(2)}) copy-start(s32[1,1,1,256]{3,2,1,0:T(1,128)} %param.17) | copy-start | bytes 3076
  38.4 12.5 %all-to-all-start.1 = ((bf16[8,40,384]{2,1,0:T(8,128)(2,1)}), bf16[8,40,384]{2,1,0:T(8,128)(2,1)S(1)}, u32[]{:S(2)}, u32[]{:S(2)}) async-start(bf16[8,40,384]{2,1,0:T(8,128)(2,1)} %bitcast.52), calls=%async_computation.1 | async-start | bytes 491520 | tf_op jit(solution)/shard_map/all_to_all | solution.py:382
  41.8 9.1 %copy-start.62 = (s32[280]{0:T(512)}, s32[280]{0:T(512)S(1)}, u32[]{:S(2)}) copy-start(s32[280]{0:T(512)S(1)} %fusion.15) | copy-start | bytes 3364
  49.4 28.4 %collective-permute-start.3 = (bf16[2,256,768]{2,1,0:T(8,128)(2,1)S(1)}, bf16[2,256,768]{2,1,0:T(8,128)(2,1)}, u32[]{:S(2)}, u32[]{:S(2)}) collective-permute-start(bf16[2,256,768]{2,1,0:T(8,128)(2,1)S(1)} %get-tuple-element.22), channel_id=1, source_target_pairs={{0,2},{1,3},{2,0},{3,1},{4,6},{5,7},{6,4},{7,5},{8,10},{9,11},{10,... | collective-permute-start | bytes 2359304 | tf_op jit(solution)/shard_map/ppermute | solution.py:239
  51.6 10.2 %copy-start.5 = (bf16[12,256,256]{2,1,0:T(8,128)(2,1)S(1)}, bf16[12,256,256]{2,1,0:T(8,128)(2,1)}, u32[]{:S(2)}) copy-start(bf16[12,256,256]{2,1,0:T(8,128)(2,1)} %copy-done.4) | copy-start | bytes 4718596
  59.2 10.0 %collective-permute-start.11 = (bf16[3,32,384]{2,1,0:T(8,128)(2,1)}, bf16[3,32,384]{2,1,0:T(8,128)(2,1)S(1)}, u32[]{:S(2)}, u32[]{:S(2)}) collective-permute-start(bf16[3,32,384]{2,1,0:T(8,128)(2,1)} %bitcast.25), channel_id=1, source_target_pairs={{0,16},{16,0},{1,17},{17,1},{2,18},{18,2},{3,19},{19,3},{4,20},{20... | collective-permute-start | bytes 221192 | tf_op jit(solution)/shard_map/ppermute | solution.py:244
  61.2 8.1 %collective-permute-start.12 = (bf16[3,32,384]{2,1,0:T(8,128)(2,1)}, bf16[3,32,384]{2,1,0:T(8,128)(2,1)S(1)}, u32[]{:S(2)}, u32[]{:S(2)}) collective-permute-start(bf16[3,32,384]{2,1,0:T(8,128)(2,1)} %bitcast.27), channel_id=1, source_target_pairs={{0,16},{16,0},{1,17},{17,1},{2,18},{18,2},{3,19},{19,3},{4,20},{20... | collective-permute-start | bytes 221192 | tf_op jit(solution)/shard_map/ppermute | solution.py:244
  65.2 4.0 %copy-start.19 = (bf16[1024,384]{1,0:T(8,128)(2,1)S(1)}, bf16[1024,384]{1,0:T(8,128)(2,1)}, u32[]{:S(2)}) copy-start(bf16[1024,384]{1,0:T(8,128)(2,1)} %copy-done.18) | copy-start | bytes 2359300
  69.4 6.8 %collective-permute-start.13 = (bf16[38,3,384]{2,1,0:T(4,128)(2,1)S(1)}, bf16[38,3,384]{2,1,0:T(4,128)(2,1)S(1)}, u32[]{:S(2)}, u32[]{:S(2)}) collective-permute-start(bf16[38,3,384]{2,1,0:T(4,128)(2,1)S(1)} %get-tuple-element.85), channel_id=1, source_target_pairs={{0,4},{4,8},{8,12},{12,0},{1,5},{5,9},{9,13},{13,1},{2,6},{6,10},{... | collective-permute-start | bytes 262664 | tf_op jit(solution)/shard_map/ppermute | solution.py:244
  71.3 5.9 %copy-start.63 = (pred[38]{0:T(512)(128)(4,1)S(1)}, pred[38]{0:T(512)(128)(4,1)}, u32[]{:S(2)}) copy-start(pred[38]{0:T(512)(128)(4,1)} %or_and_fusion) | copy-start | bytes 118
  71.3 5.9 %collective-permute-start.14 = (bf16[38,3,384]{2,1,0:T(4,128)(2,1)S(1)}, bf16[38,3,384]{2,1,0:T(4,128)(2,1)S(1)}, u32[]{:S(2)}, u32[]{:S(2)}) collective-permute-start(bf16[38,3,384]{2,1,0:T(4,128)(2,1)S(1)} %get-tuple-element.86), channel_id=1, source_target_pairs={{0,12},{4,0},{8,4},{12,8},{1,13},{5,1},{9,5},{13,9},{2,14},{6,2},{... | collective-permute-start | bytes 262664 | tf_op jit(solution)/shard_map/ppermute | solution.py:244
  73.3 18.9 %collective-permute-start = (bf16[8,96,256]{2,1,0:T(8,128)(2,1)S(1)}, bf16[8,96,256]{2,1,0:T(8,128)(2,1)S(1)}, u32[]{:S(2)}, u32[]{:S(2)}) collective-permute-start(bf16[8,96,256]{2,1,0:T(8,128)(2,1)S(1)} %get-tuple-element.83), channel_id=1, source_target_pairs={{0,2},{1,3},{2,0},{3,1},{4,6},{5,7},{6,4},{7,5},{8,10},{9,11},{10,... | collective-permute-start | bytes 1179656 | tf_op jit(solution)/shard_map/ppermute | solution.py:239
  74.3 18.0 %collective-permute-start.1 = (bf16[8,96,256]{2,1,0:T(8,128)(2,1)S(1)}, bf16[8,96,256]{2,1,0:T(8,128)(2,1)S(1)}, u32[]{:S(2)}, u32[]{:S(2)}) collective-permute-start(bf16[8,96,256]{2,1,0:T(8,128)(2,1)S(1)} %get-tuple-element.82), channel_id=1, source_target_pairs={{0,1},{1,0},{2,3},{3,2},{4,5},{5,4},{6,7},{7,6},{8,9},{9,8},{10,11... | collective-permute-start | bytes 1179656 | tf_op jit(solution)/shard_map/ppermute | solution.py:239
  76.1 16.2 %collective-permute-start.2 = (bf16[8,96,256]{2,1,0:T(8,128)(2,1)S(1)}, bf16[8,96,256]{2,1,0:T(8,128)(2,1)S(1)}, u32[]{:S(2)}, u32[]{:S(2)}) collective-permute-start(bf16[8,96,256]{2,1,0:T(8,128)(2,1)S(1)} %get-tuple-element.81), channel_id=1, source_target_pairs={{0,3},{1,2},{2,1},{3,0},{4,7},{5,6},{6,5},{7,4},{8,11},{9,10},{10,... | collective-permute-start | bytes 1179656 | tf_op jit(solution)/shard_map/ppermute | solution.py:239
  77.8 1.8 %copy-start.23 = (f32[384]{0:T(512)S(1)}, f32[384]{0:T(512)}, u32[]{:S(2)}) copy-start(f32[384]{0:T(512)} %get-tuple-element.75) | copy-start | bytes 4612
  77.8 1.8 %copy-start.24 = (f32[384]{0:T(512)S(1)}, f32[384]{0:T(512)}, u32[]{:S(2)}) copy-start(f32[384]{0:T(512)} %get-tuple-element.76) | copy-start | bytes 4612
  77.8 1.8 %copy-start.25 = (f32[384]{0:T(512)S(1)}, f32[384]{0:T(512)}, u32[]{:S(2)}) copy-start(f32[384]{0:T(512)} %get-tuple-element.28) | copy-start | bytes 4612
  77.8 1.8 %copy-start.26 = (f32[384]{0:T(512)S(1)}, f32[384]{0:T(512)}, u32[]{:S(2)}) copy-start(f32[384]{0:T(512)} %get-tuple-element.29) | copy-start | bytes 4612
  77.8 1.8 %copy-start.27 = (f32[384]{0:T(512)S(1)}, f32[384]{0:T(512)}, u32[]{:S(2)}) copy-start(f32[384]{0:T(512)} %get-tuple-element.30) | copy-start | bytes 4612
  77.8 1.8 %copy-start.28 = (f32[384]{0:T(512)S(1)}, f32[384]{0:T(512)}, u32[]{:S(2)}) copy-start(f32[384]{0:T(512)} %get-tuple-element.31) | copy-start | bytes 4612
  77.8 1.8 %copy-start.29 = (f32[384]{0:T(512)S(1)}, f32[384]{0:T(512)}, u32[]{:S(2)}) copy-start(f32[384]{0:T(512)} %get-tuple-element.32) | copy-start | bytes 4612
  77.8 1.8 %copy-start.30 = (f32[384]{0:T(512)S(1)}, f32[384]{0:T(512)}, u32[]{:S(2)}) copy-start(f32[384]{0:T(512)} %get-tuple-element.33) | copy-start | bytes 4612
  77.9 1.8 %copy-start.31 = (f32[384]{0:T(512)S(1)}, f32[384]{0:T(512)}, u32[]{:S(2)}) copy-start(f32[384]{0:T(512)} %get-tuple-element.34) | copy-start | bytes 4612
  77.9 1.8 %copy-start.32 = (f32[384]{0:T(512)S(1)}, f32[384]{0:T(512)}, u32[]{:S(2)}) copy-start(f32[384]{0:T(512)} %get-tuple-element.35) | copy-start | bytes 4612
  77.9 1.8 %copy-start.33 = (f32[384]{0:T(512)S(1)}, f32[384]{0:T(512)}, u32[]{:S(2)}) copy-start(f32[384]{0:T(512)} %get-tuple-element.36) | copy-start | bytes 4612
  77.9 1.8 %copy-start.34 = (f32[384]{0:T(512)S(1)}, f32[384]{0:T(512)}, u32[]{:S(2)}) copy-start(f32[384]{0:T(512)} %get-tuple-element.37) | copy-start | bytes 4612
  77.9 1.8 %copy-start.35 = (f32[384]{0:T(512)S(1)}, f32[384]{0:T(512)}, u32[]{:S(2)}) copy-start(f32[384]{0:T(512)} %get-tuple-element.38) | copy-start | bytes 4612
  77.9 1.8 %copy-start.36 = (f32[384]{0:T(512)S(1)}, f32[384]{0:T(512)}, u32[]{:S(2)}) copy-start(f32[384]{0:T(512)} %get-tuple-element.39) | copy-start | bytes 4612
  77.9 1.8 %copy-start.37 = (f32[384]{0:T(512)S(1)}, f32[384]{0:T(512)}, u32[]{:S(2)}) copy-start(f32[384]{0:T(512)} %get-tuple-element.40) | copy-start | bytes 4612
  77.9 1.8 %copy-start.38 = (f32[384]{0:T(512)S(1)}, f32[384]{0:T(512)}, u32[]{:S(2)}) copy-start(f32[384]{0:T(512)} %get-tuple-element.41) | copy-start | bytes 4612
  77.9 1.8 %copy-start.39 = (f32[384]{0:T(512)S(1)}, f32[384]{0:T(512)}, u32[]{:S(2)}) copy-start(f32[384]{0:T(512)} %get-tuple-element.42) | copy-start | bytes 4612
  79.4 12.7 %copy-start.21 = (bf16[2,2,256,768]{3,2,1,0:T(8,128)(2,1)}, bf16[2,2,256,768]{3,2,1,0:T(8,128)(2,1)S(1)}, u32[]{:S(2)}) copy-start(bf16[2,2,256,768]{3,2,1,0:T(8,128)(2,1)S(1)} %pad_maximum_fusion.e01) | copy-start | bytes 4718596
  79.5 12.7 %collective-permute-start.4 = (bf16[2,2,256,768]{3,2,1,0:T(8,128)(2,1)S(1)}, bf16[2,2,256,768]{3,2,1,0:T(8,128)(2,1)S(1)}, u32[]{:S(2)}, u32[]{:S(2)}) collective-permute-start(bf16[2,2,256,768]{3,2,1,0:T(8,128)(2,1)S(1)} %pad_maximum_fusion.e01), channel_id=1, source_target_pairs={{0,1},{1,0},{2,3},{3,2},{4,5},{5,4},{6,7},{7,6},{8,9},{9,8},{10,11... | collective-permute-start | bytes 4718600 | tf_op jit(solution)/shard_map/ppermute | solution.py:239
  95.2 15.8 %collective-permute-start.5 = (bf16[4,96,768]{2,1,0:T(8,128)(2,1)S(1)}, bf16[4,96,768]{2,1,0:T(8,128)(2,1)S(1)}, u32[]{:S(2)}, u32[]{:S(2)}) collective-permute-start(bf16[4,96,768]{2,1,0:T(8,128)(2,1)S(1)} %get-tuple-element.24), channel_id=1, source_target_pairs={{0,16},{16,0},{1,17},{17,1},{2,18},{18,2},{3,19},{19,3},{4,20},{20... | collective-permute-start | bytes 1769480 | tf_op jit(solution)/shard_map/ppermute | solution.py:244
  111.1 8.7 %collective-permute-start.6 = (bf16[96,768]{1,0:T(8,128)(2,1)S(1)}, bf16[96,768]{1,0:T(8,128)(2,1)S(1)}, u32[]{:S(2)}, u32[]{:S(2)}) collective-permute-start(bf16[96,768]{1,0:T(8,128)(2,1)S(1)} %get-tuple-element.91), channel_id=1, source_target_pairs={{0,4},{4,8},{8,12},{12,0},{1,5},{5,9},{9,13},{13,1},{2,6},{6,10},{... | collective-permute-start | bytes 442376 | tf_op jit(solution)/shard_map/ppermute | solution.py:244
  112.0 12.9 %collective-permute-start.7 = (bf16[96,768]{1,0:T(8,128)(2,1)S(1)}, bf16[96,768]{1,0:T(8,128)(2,1)S(1)}, u32[]{:S(2)}, u32[]{:S(2)}) collective-permute-start(bf16[96,768]{1,0:T(8,128)(2,1)S(1)} %get-tuple-element.90), channel_id=1, source_target_pairs={{0,8},{4,12},{8,0},{12,4},{1,9},{5,13},{9,1},{13,5},{2,10},{6,14},... | collective-permute-start | bytes 442376 | tf_op jit(solution)/shard_map/ppermute | solution.py:244
  114.5 10.4 %collective-permute-start.8 = (bf16[96,768]{1,0:T(8,128)(2,1)S(1)}, bf16[96,768]{1,0:T(8,128)(2,1)S(1)}, u32[]{:S(2)}, u32[]{:S(2)}) collective-permute-start(bf16[96,768]{1,0:T(8,128)(2,1)S(1)} %get-tuple-element.89), channel_id=1, source_target_pairs={{0,12},{4,0},{8,4},{12,8},{1,13},{5,1},{9,5},{13,9},{2,14},{6,2},{... | collective-permute-start | bytes 442376 | tf_op jit(solution)/shard_map/ppermute | solution.py:244
  125.0 9.4 %collective-permute-start.9 = (bf16[96,768]{1,0:T(8,128)(2,1)S(1)}, bf16[96,768]{1,0:T(8,128)(2,1)S(1)}, u32[]{:S(2)}, u32[]{:S(2)}) collective-permute-start(bf16[96,768]{1,0:T(8,128)(2,1)S(1)} %close.1), channel_id=1, source_target_pairs={{0,2},{1,3},{2,0},{3,1},{4,6},{5,7},{6,4},{7,5},{8,10},{9,11},{10,... | collective-permute-start | bytes 442376 | tf_op jit(solution)/shard_map/ppermute | solution.py:239
  125.6 8.9 %copy-start.20 = (bf16[1024,384]{1,0:T(8,128)(2,1)S(1)}, bf16[1024,384]{1,0:T(8,128)(2,1)}, u32[]{:S(2)}) copy-start(bf16[1024,384]{1,0:T(8,128)(2,1)} %copy-done.18) | copy-start | bytes 2359300
  125.6 8.9 %copy-start.64 = (bf16[768,384]{1,0:T(8,128)(2,1)S(1)}, bf16[768,384]{1,0:T(8,128)(2,1)}, u32[]{:S(2)}) copy-start(bf16[768,384]{1,0:T(8,128)(2,1)} %param.26) | copy-start | bytes 1769476
  125.6 8.9 %copy-start.65 = (bf16[384,128]{1,0:T(8,128)(2,1)S(1)}, bf16[384,128]{1,0:T(8,128)(2,1)}, u32[]{:S(2)}) copy-start(bf16[384,128]{1,0:T(8,128)(2,1)} %param.27) | copy-start | bytes 294916
  134.4 3.5 %collective-permute-start.10 = (bf16[2,96,768]{2,1,0:T(8,128)(2,1)S(1)}, bf16[2,96,768]{2,1,0:T(8,128)(2,1)S(1)}, u32[]{:S(2)}, u32[]{:S(2)}) collective-permute-start(bf16[2,96,768]{2,1,0:T(8,128)(2,1)S(1)} %pad_maximum_fusion.1.first_ref), channel_id=1, source_target_pairs={{0,1},{1,0},{2,3},{3,2},{4,5},{5,4},{6,7},{7,6},{8,9},{9,8},{10,11... | collective-permute-start | bytes 884744 | tf_op jit(solution)/shard_map/ppermute | solution.py:239
  (35 other events, 52.2 us)

commit v2 on v1

--- a/solution.py
+++ b/solution.py
@@ -2,6 +2,7 @@
 
 import jax
 import jax.numpy as jnp
+import numpy as np
 from jax import lax
 from jax.experimental import pallas as pl
 from jax.experimental.pallas import tpu as pltpu
@@ -30,7 +31,7 @@
     return pl.BlockSpec(memory_space=pltpu.SMEM)
 
 
-def call(kernel, name, outs, in_specs, scratch=(), flops=0, nbytes=0, limit=48):
+def call(kernel, name, outs, in_specs, scratch=(), flops=0, nbytes=0, limit=20):
     single = not isinstance(outs, (list, tuple))
     out_list = [outs] if single else list(outs)
     specs = [vmem() for _ in out_list]
@@ -235,6 +236,128 @@
     out_ref[me ^ 3] = second_ref[1].astype(f32)
 
 
+def fill_kernel(padded, place_ref, pos_ref, ids_ref, mask_ref, got_ref, *refs):
+    wide_ref = refs[-1]
+    slots = slot_column(pos_ref, wide_ref, padded)
+    ids = ids_ref[0:1] + place_ref[0].astype(f32) * ids_ref[1:2]
+    chosen = (slots == ids).astype(f32).astype(bf16)
+    got = got_ref[...]
+    values = mm(chosen, got, TN)
+    hits = mm(chosen, jnp.ones((got.shape[0], 128), bf16), TN)[:, 0:1]
+    values = jnp.where(hits > 0.5, values, mask_ref[...].astype(f32)).astype(bf16)
+    at = 0
+    for ref in refs[:-1]:
+        ref[...] = values[at : at + ref.shape[0]]
+        at += ref.shape[0]
+
+
+def conv_kernel_body(
+    shape, span, folded, place_ref, grid_ref, left_ref, right_ref, rims, taps_ref, out_ref,
+    full_ref, wide_ref, mixed_ref,
+):
+    lines, columns = shape
+    rim = span // 2
+    width = grid_ref.shape[-1]
+    lead = 8
+    full_ref[rim : rim + lines, lead : lead + columns] = (
+        grid_ref[...].astype(f32).reshape(lines, columns, width)
+    )
+    left = left_ref[...].astype(f32)
+    right = right_ref[...].astype(f32)
+    for x in range(lines):
+        full_ref[rim + x, lead - rim : lead] = left[rim * x : rim * (x + 1)]
+        full_ref[rim + x, lead + columns : lead + columns + rim] = right[rim * x : rim * (x + 1)]
+
+    def put(base, edge_ref, first_ref, last_ref):
+        edge = edge_ref[...].astype(f32)
+        first = first_ref[...].astype(f32)
+        last = last_ref[...].astype(f32)
+        for i in range(rim):
+            full_ref[base + i, lead : lead + columns] = edge[columns * i : columns * (i + 1)]
+            full_ref[base + i, lead - rim : lead] = first[rim * i : rim * (i + 1)]
+            full_ref[base + i, lead + columns : lead + columns + rim] = last[
+                rim * i : rim * (i + 1)
+            ]
+
+    if folded:
+        far = rim + lines
+        base = jnp.where(place_ref[0] == 0, far, 0)
+        for i in range(rim):
+            full_ref[far - base + i] = jnp.zeros(full_ref.shape[1:], f32)
+        put(base, *rims)
+    else:
+        put(0, *rims[:3])
+        put(rim + lines, *rims[3:])
+    for t in range(span * span):
+        wide_ref[t] = jnp.broadcast_to(taps_ref[t : t + 1], (8, width))
+    groups = columns // 8
+
+    for c in range(width // 128):
+        cut = slice(c * 128, (c + 1) * 128)
+
+        def step(x, accs, live, cut=cut):
+            accs = list(accs)
+            for v in range(span):
+                at = lead - rim + v
+                line = full_ref[x, at : at + columns, cut].reshape(groups, 8, 128)
+                for i in live:
+                    tap = wide_ref[(span - 1 - i) * span + v, :, cut]
+                    accs[i] = accs[i] + line * tap[None]
+            return accs
+
+        def store(row, acc, cut=cut):
+            at = row * columns
+            if not isinstance(row, int):
+                at = pl.multiple_of(at, columns)
+            mixed_ref[pl.ds(at, columns), cut] = acc.reshape(columns, 128)
+
+        zero = jnp.zeros((groups, 8, 128), f32)
+        accs = [zero] * span
+        for x in range(span - 1):
+            accs = step(x, accs, range(span - 1 - x, span))
+            accs = accs[1:] + [zero]
+
+        def middle(x, accs):
+            accs = step(x, accs, range(span))
+            store(x - (span - 1), accs[0])
+            return tuple(accs[1:] + [zero])
+
+        accs = list(lax.fori_loop(span - 1, lines, middle, tuple(accs)))
+        for x in range(lines, lines + span - 1):
+            accs = step(x, accs, range(0, lines + span - 1 - x))
+            store(x - (span - 1), accs[0])
+            accs = accs[1:] + [zero]
+
+    mixed = mixed_ref[...]
+    centred = mixed - jnp.mean(mixed, axis=-1, keepdims=True)
+    spread = jnp.mean(centred * centred, axis=-1, keepdims=True)
+    out_ref[...] = (centred * lax.rsqrt(spread + norm_eps)).astype(bf16)
+
+
+def mix_folded(shape, span, place, grid, left, right, a, b, c, taps, out, full, wide, mixed):
+    conv_kernel_body(
+        shape, span, True, place, grid, left, right, (a, b, c), taps, out, full, wide, mixed
+    )
+
+
+def mix_open(
+    shape, span, place, grid, left, right, a, b, c, d, e, g, taps, out, full, wide, mixed
+):
+    conv_kernel_body(
+        shape, span, False, place, grid, left, right, (a, b, c, d, e, g), taps, out, full, wide,
+        mixed,
+    )
+
+
+def feed_kernel(chunk, normed_ref, grid_ref, up_ref, down_ref, head_ref, out_ref):
+    for at in range(0, normed_ref.shape[0], chunk):
+        rows = slice(at, at + chunk)
+        wide = mm(normed_ref[rows], up_ref[...])
+        hidden = (0.5 * wide * (1.0 + lax.erf(wide * 0.7071067811865476))).astype(bf16)
+        decoded = (grid_ref[rows].astype(f32) + mm(hidden, down_ref[...])).astype(bf16)
+        out_ref[rows] = mm(decoded, head_ref[...])
+
+
 def flip(value, axis, bit):
     return lax.ppermute(value, axis, [(i, i ^ bit) for i in range(lax.axis_size(axis))])
 
@@ -242,21 +365,6 @@
 def turn(value, axis, k):
     count = lax.axis_size(axis)
     return lax.ppermute(value, axis, [(i, (i + k) % count) for i in range(count)])
-
-
-def extended(block, sides, width):
-    for axis, dim in sides:
-        low = turn(lax.slice_in_dim(block, block.shape[dim] - width, None, axis=dim), axis, 1)
-        high = turn(lax.slice_in_dim(block, 0, width, axis=dim), axis, -1)
-        block = jnp.concatenate([low, block, high], axis=dim)
-    return block
-
-
-def plain_norm(values):
-    centre = jnp.mean(values, axis=-1, keepdims=True)
-    centred = values - centre
-    spread = jnp.mean(centred * centred, axis=-1, keepdims=True)
-    return centred * lax.rsqrt(spread + norm_eps)
 
 
 def summed_slow(left, both, width):
@@ -394,39 +502,101 @@
         flops=2 * rows * rows * width * 5,
         nbytes=10 * MIB,
     )(me, head_scale, weights, units, lengths, values, grad_att, cot_t)
+    left, returned = lax.optimization_barrier((left, returned))
     if fast:
         grad_total = summed_fast(left, both, width, phi_count)
     else:
         grad_total = summed_slow(left, both, width)
 
-    dec_slots = returned[:, :cap].reshape(group * cap, dec_width)
-    slot_cells = send_pos.reshape(group * cap)
-    filled = jnp.zeros((tile_len, dec_width), bf16).at[slot_cells].set(dec_slots, mode="drop")
-    seen_cells = jnp.zeros((tile_len,), jnp.bool_).at[slot_cells].set(True, mode="drop")
-    dec_grid = jnp.where(seen_cells[:, None], filled, mask_token).reshape(
-        eta_cells, phi_cells, dec_width
-    )
-    kernel_span = conv_kernel.shape[0]
-    rim_width = kernel_span // 2
-    full = extended(dec_grid, (("eta", 0), ("phi", 1)), rim_width)
-    eta_place = lax.axis_index("eta")
-    rim_line = lax.broadcasted_iota(jnp.int32, (eta_cells + 2 * rim_width, 1, 1), 0)
-    keep_rim = jnp.logical_and(
-        jnp.logical_or(rim_line >= rim_width, eta_place > 0),
-        jnp.logical_or(rim_line < eta_cells + rim_width, eta_place < eta_count - 1),
-    )
-    full = jnp.where(keep_rim, full, jnp.zeros((), full.dtype))
-    mixed_cells = jnp.zeros((eta_cells, phi_cells, dec_width), f32)
-    for row_shift in range(kernel_span):
-        for col_shift in range(kernel_span):
-            window_cells = full[
-                row_shift : row_shift + eta_cells, col_shift : col_shift + phi_cells
-            ].astype(f32)
-            mixed_cells = mixed_cells + conv_kernel[row_shift, col_shift] * window_cells
-    dec_normed = plain_norm(mixed_cells).astype(bf16).reshape(tile_len, dec_width)
-    hidden = jax.nn.gelu(mm(dec_normed, w_up), approximate=False).astype(bf16)
-    decoded = (dec_grid.reshape(tile_len, dec_width).astype(f32) + mm(hidden, w_down)).astype(bf16)
-    reconstruction = mm(decoded, w_head).reshape(1, eta_cells, phi_cells, -1)
+    span = conv_kernel.shape[0]
+    rim = span // 2
+    folded = eta_count == 2
+    eta_place = lax.axis_index("eta").astype(jnp.int32).reshape(1)
+    lines = np.arange(eta_cells)[:, None]
+    columns = np.arange(phi_cells)[None, :]
+    cell = lines * phi_cells + columns
+    parts = [cell]
+    moves = [0]
+    if folded:
+        edge = cell[eta_cells - rim :]
+        parts += [cell[:, :rim], cell[:, -rim:], edge, edge[:, :rim], edge[:, -rim:]]
+        moves += [0, 0] + [-(eta_cells - rim) * phi_cells] * 3
+    sizes = [-(-p.size // 16) * 16 for p in parts]
+    ids = np.full((2, -(-sum(sizes) // 128) * 128), -7.0, np.float32)
+    ids[1] = 0
+    at = 0
+    for p, size, move in zip(parts, sizes, moves):
+        ids[0, at : at + p.size] = p.reshape(-1)
+        ids[1, at : at + p.size] = move
+        at += size
+    filled = call(
+        functools.partial(fill_kernel, padded),
+        "fill",
+        [sds((size, dec_width), bf16) for size in sizes],
+        [smem()] + [vmem()] * 4,
+        scratch=[pltpu.VMEM((group, 128), f32)],
+        flops=2 * slots * ids.shape[1] * (dec_width + 128),
+        nbytes=3 * MIB,
+    )(
+        eta_place, positions, jnp.asarray(ids), mask_token.reshape(1, dec_width),
+        returned.reshape(slots, dec_width),
+    )
+    dec_grid = filled[0]
+    plane = ("eta", "phi")
+
+    def shifted(value, by):
+        pairs = [
+            (e * phi_count + p, (1 - e) * phi_count + (p + by) % phi_count)
+            for e in range(2)
+            for p in range(phi_count)
+        ]
+        return lax.ppermute(value, plane, pairs)
+
+    if folded:
+        _, first, last, edge, edge_first, edge_last = filled
+        left = turn(last, "phi", 1)
+        right = turn(first, "phi", -1)
+        rims = (shifted(edge, 0), shifted(edge_last, 1), shifted(edge_first, -1))
+    else:
+        box = dec_grid.reshape(eta_cells, phi_cells, dec_width)
+        down = [(i, i + 1) for i in range(eta_count - 1)]
+        up = [(i + 1, i) for i in range(eta_count - 1)]
+        top = lax.ppermute(box[eta_cells - rim :], "eta", down)
+        bottom = lax.ppermute(box[:rim], "eta", up)
+        box = jnp.concatenate([top, box, bottom], axis=0)
+        low = turn(box[:, phi_cells - rim :], "phi", 1)
+        high = turn(box[:, :rim], "phi", -1)
+
+        def flat(value):
+            return value.reshape(-1, dec_width)
+
+        far = eta_cells + rim
+        left, right = flat(low[rim:far]), flat(high[rim:far])
+        rims = (
+            flat(top), flat(low[:rim]), flat(high[:rim]),
+            flat(bottom), flat(low[far:]), flat(high[far:]),
+        )
+    normed_cells = call(
+        functools.partial(mix_folded if folded else mix_open, (eta_cells, phi_cells), span),
+        "mix",
+        sds((tile_len, dec_width), bf16),
+        [smem()] + [vmem()] * (4 + len(rims)),
+        scratch=[
+            pltpu.VMEM((eta_cells + 2 * rim, phi_cells + 16, dec_width), f32),
+            pltpu.VMEM((span * span, 8, dec_width), f32),
+            pltpu.VMEM((tile_len, dec_width), f32),
+        ],
+        flops=400 * 2 * span * span * tile_len * dec_width,
+        nbytes=3 * MIB,
+    )(eta_place, dec_grid, left, right, *rims, conv_kernel.reshape(span * span, dec_width))
+    reconstruction = call(
+        functools.partial(feed_kernel, 256),
+        "feed",
+        sds((tile_len, w_head.shape[1]), f32),
+        [vmem()] * 5,
+        flops=2 * tile_len * dec_width * (2 * w_up.shape[1] + w_head.shape[1]),
+        nbytes=4 * MIB,
+    )(normed_cells, dec_grid, w_up, w_down, w_head).reshape(1, eta_cells, phi_cells, -1)
     return (grad_total, reconstruction)
 
 

time: 141 us -> 154 us (1.092)
  waiting for transfers between devices: 34.8 us -> 64.6 us
  other arithmetic: 16.7 us -> 0.17 us
  matrix products: 12.2 us -> 0 us
  Pallas kernels: 21.2 us -> 30.5 us
  starting transfers between devices: 25.7 us -> 34.9 us
  local copies, waits for them, and re-layouts: 26.8 us -> 21.6 us
    ppermute x7, waiting for transfers between devices: 0.02 us -> 30.4 us  [flip(): lax.ppermute(value, axis, [(i, i ^ bit) for i in range(lax.axis_size(axis...]
    pallas_call x0 -> x3, Pallas kernels: none -> 13.2 us  [the longest x1 7.45 us: body(): call(functools.partial(mix_folded if folded else mix_open, (eta_cells, ph...]
    reduce_sum x2 -> x0, other arithmetic: 12.6 us -> none  [the longest x1 12.2 us: plain_norm(): centre = jnp.mean(values, axis=-1, keepdims=True)]
    dot_general x2 -> x0, matrix products: 12.2 us -> none  [mm(): return lax.dot_general(a, b, dims, preferred_element_type=f32)]
    ppermute x0 -> x3, starting transfers between devices: none -> 6.25 us  [shifted(): return lax.ppermute(value, plane, pairs)]
    slice x4 -> x0, local copies, waits for them, and re-layouts: 6.06 us -> none  [the longest x3 5.38 us: body(): mixed_cells = mixed_cells + conv_kernel[row_shift, col_shift] * window_cells]
    unnamed x132 -> x64, local copies, waits for them, and re-layouts: 13.6 us -> 19.1 us
    scatter x2 -> x0, local copies, waits for them, and re-layouts: 5.07 us -> none  [the longest x1 2.92 us: body(): jnp.zeros((tile_len, dec_width), bf16).at[slot_cells]]
  transfers between devices with their start and end apart: 17 -> 18, of which waited for: 6 -> 9; matrix products, arithmetic and copies ran while one was open for 30% -> 2% of each run, Pallas kernels for 5% -> 12%
where the time goes in v2:
time: 154 us; the launch traced here: 153 us
  waiting for transfers between devices  64.6 us (42%)
  starting transfers between devices  34.9 us (23%)
  Pallas kernels  30.5 us (20%)
  local copies, waits for them, and re-layouts  21.6 us (14%)
    ppermute x7, waiting for transfers between devices, flip(): lax.ppermute(value, axis, [(i, i ^ bit) for i in range(lax.axis_size(axis...  30.4 us
    ppermute x6, waiting for transfers between devices, turn(): lax.ppermute(value, axis, [(i, (i + k) % count) for i in range(count)])  22.7 us
    unnamed x64, local copies, waits for them, and re-layouts  19.1 us
    ppermute x6, starting transfers between devices, turn(): lax.ppermute(value, axis, [(i, (i + k) % count) for i in range(count)])  11.8 us
    all_to_all x1, waiting for transfers between devices, body(): lax.all_to_all(outgoing.reshape(group, padded, width), ('eta', 'phi'), sp...  9.05 us
    pallas_call x1, Pallas kernels, body(): call(functools.partial(mix_folded if folded else mix_open, (eta_cells, ph...  7.45 us
    all_to_all x1, starting transfers between devices, body(): lax.all_to_all(outgoing.reshape(group, padded, width), ('eta', 'phi'), sp...  7.25 us
    pallas_call x1, Pallas kernels, body(): call(functools.partial(forward_kernel, cap, padded), 'forward', [sds((slo...  6.91 us
  transfers between devices with their start and end apart: 18, of which 9 were waited for; matrix products, arithmetic and copies ran while one was open for 2% of the time, Pallas kernels for 12%

profile of v2, /device:TPU:0, one launch (start us, length us, event | category | flops | bytes accessed | tf_op | source)
XLA Modules:
  0.0 152.7 jit_solution(11266013955244965881)
XLA Ops:
  0.6 1.5 copy-done.4
  2.8 1.7 %pick.1 = bf16[320,768]{1,0:T(8,128)(2,1)} custom-call(s32[8,35]{1,0:T(8,128)S(1)} %bitcast.41, bf16[1024,768]{1,0:T(8,128)(2,1)S(1)} %bitcast.37), custom_call_target="tpu_custom_call" | custom-call | flops 503316480 | bytes 3145728 | tf_op jit(solution)/shard_map/pick/pallas_call | solution.py:447
  4.5 7.3 %all-to-all-start = ((bf16[8,40,768]{2,1,0:T(8,128)(2,1)}), bf16[8,40,768]{2,1,0:T(8,128)(2,1)S(1)}, u32[]{:S(2)}, u32[]{:S(2)}) async-start(bf16[8,40,768]{2,1,0:T(8,128)(2,1)} %bitcast.7), calls=%async_computation | async-start | bytes 983040 | tf_op jit(solution)/shard_map/all_to_all | solution.py:456
  11.8 2.0 %copy-done.1 = bf16[768,2304]{1,0:T(8,128)(2,1)S(1)} copy-done((bf16[768,2304]{1,0:T(8,128)(2,1)S(1)}, bf16[768,2304]{1,0:T(8,128)(2,1)}, u32[]{:S(2)}) %copy-start.1) | copy-done | bytes 3538968
  13.8 1.1 prep.1
  14.9 1.7 %copy-done.2 = bf16[2304,768]{1,0:T(8,128)(2,1)} copy-done((bf16[2304,768]{1,0:T(8,128)(2,1)}, bf16[2304,768]{1,0:T(8,128)(2,1)S(1)}, u32[]{:S(2)}) %copy-start.2) | copy-done | bytes 3538968
  16.6 0.7 copy-done.11
  17.4 9.0 %all-to-all-done = bf16[8,40,768]{2,1,0:T(8,128)(2,1)S(1)} async-done(((bf16[8,40,768]{2,1,0:T(8,128)(2,1)}), bf16[8,40,768]{2,1,0:T(8,128)(2,1)S(1)}, u32[]{:S(2)}, u32[]{:S(2)}) %all-to-all-start) | async-done | bytes 491552 | tf_op jit(solution)/shard_map/all_to_all | solution.py:456
  26.5 2.0 %copy-done.3 = bf16[2304,768]{1,0:T(8,128)(2,1)S(1)} copy-done((bf16[2304,768]{1,0:T(8,128)(2,1)S(1)}, bf16[2304,768]{1,0:T(8,128)(2,1)}, u32[]{:S(2)}) %copy-start.3) | copy-done | bytes 3538968
  28.5 6.9 %forward.1 = (bf16[320,384]{1,0:T(8,128)(2,1)}, bf16[2,256,768]{2,1,0:T(8,128)(2,1)S(1)}, bf16[12,256,256]{2,1,0:T(8,128)(2,1)S(1)}, f32[1536,256]{1,0:T(8,128)S...) custom-call(s32[1,256]{1,0:T(1,128)S(1)} %bitcast.43, s32[1,256]{1,0:T(1,128)S(1)} %bitcast.44, ...), custom_call_target="tpu_custom_call" | custom-call | flops 1509949440 | bytes 10485760 | tf_op jit(solution)/shard_map/forward/pallas_call | solution.py:471
  35.4 0.7 copy-done.17
  36.7 1.5 collective-permute-start.3
  38.2 16.3 %collective-permute-done.3 = bf16[2,256,768]{2,1,0:T(8,128)(2,1)S(1)} collective-permute-done((bf16[2,256,768]{2,1,0:T(8,128)(2,1)S(1)}, bf16[2,256,768]{2,1,0:T(8,128)(2,1)S(1)}, u32[]{:S(2)}, u32[]{:S(2)}) %collective-permute-start.3) | collective-permute-done | bytes 786464 | tf_op jit(solution)/shard_map/ppermute | solution.py:362
  54.8 4.0 %all-to-all-start.1 = ((bf16[8,40,384]{2,1,0:T(8,128)(2,1)}), bf16[8,40,384]{2,1,0:T(8,128)(2,1)}, u32[]{:S(2)}, u32[]{:S(2)}) async-start(bf16[8,40,384]{2,1,0:T(8,128)(2,1)} %bitcast.10), calls=%async_computation.1 | async-start | bytes 491520 | tf_op jit(solution)/shard_map/all_to_all | solution.py:490
  58.9 1.4 copy-done.6
  60.3 1.4 copy-done.8
  61.7 1.0 copy-done.12
  62.7 1.0 copy-done.18
  64.4 4.0 %backward.1 = bf16[4,8,96,256]{3,2,1,0:T(8,128)(2,1)S(1)} custom-call(s32[1]{0:T(128)} %bitcast.me_ref, f32[12]{0:T(128)S(1)} %copy-done.23, bf16[12,256,256]{2,1,0:T(8,128)(2,1)S(1)} %copy-done.6, f32[1536,256]{1,0:T(8,128)S(1)} %copy-done.8, f32[24,256]{1,0:T(8,128)S(1)} %copy-done.20, bf16[768,256]{1,0:T(8,128)(2,1)S(1)} %copy-done.18, ...), custom_call_target="tpu_custom_call" | custom-call | flops 503316480 | bytes 10485760 | tf_op jit(solution)/shard_map/backward/pallas_call | solution.py:497
  68.4 0.8 all-to-all-done.1
  69.2 1.0 slice_bitcast_fusion.2
  70.2 1.5 collective-permute-start
  72.4 1.5 slice_bitcast_fusion
  73.8 8.6 %collective-permute-done.l1 = bf16[8,96,256]{2,1,0:T(8,128)(2,1)S(1)} collective-permute-done((bf16[8,96,256]{2,1,0:T(8,128)(2,1)}, bf16[8,96,256]{2,1,0:T(8,128)(2,1)S(1)}, u32[]{:S(2)}, u32[]{:S(2)}) %collective-permute-start) | collective-permute-done | bytes 393248 | tf_op jit(solution)/shard_map/ppermute | solution.py:362
  82.5 0.7 copy-done.13
  83.2 5.5 %collective-permute-done.2.l3 = bf16[8,96,256]{2,1,0:T(8,128)(2,1)S(1)} collective-permute-done((bf16[8,96,256]{2,1,0:T(8,128)(2,1)}, bf16[8,96,256]{2,1,0:T(8,128)(2,1)S(1)}, u32[]{:S(2)}, u32[]{:S(2)}) %collective-permute-start.2) | collective-permute-done | bytes 393248 | tf_op jit(solution)/shard_map/ppermute | solution.py:362
  88.7 0.7 copy-done.15
  89.5 1.0 copy-done.14
  90.5 1.0 copy-done.16
  91.5 2.3 %terms.1 = (f32[4,96,768]{2,1,0:T(8,128)S(1)}, bf16[4,96,768]{2,1,0:T(8,128)(2,1)}) custom-call(s32[1]{0:T(128)} %bitcast.2.place_ref.place, bf16[8,96,256]{2,1,0:T(8,128)(2,1)S(1)} %get-tuple-element.49.l0, bf16[8,96,256]{2,1,0:T(8,128)(2,1)S(1)} %collective-permute-done.l1, bf16[8,96,256]{2,1,0:T(8,128)(2,1)S(1)} %copy-done.14, ...), custom_call_target="tpu_custom_call" | custom-call | flops 1207959552 | bytes 8388608 | tf_op jit(solution)/shard_map/terms/pallas_call | solution.py:384
  93.8 1.8 %collective-permute-start.5 = (bf16[4,96,768]{2,1,0:T(8,128)(2,1)}, bf16[4,96,768]{2,1,0:T(8,128)(2,1)S(1)}, u32[]{:S(2)}, u32[]{:S(2)}) collective-permute-start(bf16[4,96,768]{2,1,0:T(8,128)(2,1)} %get-tuple-element.34), channel_id=1, source_target_pairs={{0,16},{16,0},{1,17},{17,1},{2,18},{18,2},{3,19},{19,3},{4,20},{20... | collective-permute-start | bytes 1769480 | tf_op jit(solution)/shard_map/ppermute | solution.py:367
  95.6 14.3 %collective-permute-done.5.got_ref = bf16[4,96,768]{2,1,0:T(8,128)(2,1)S(1)} collective-permute-done((bf16[4,96,768]{2,1,0:T(8,128)(2,1)}, bf16[4,96,768]{2,1,0:T(8,128)(2,1)S(1)}, u32[]{:S(2)}, u32[]{:S(2)}) %collective-permute-start.5) | collective-permute-done | bytes 589856 | tf_op jit(solution)/shard_map/ppermute | solution.py:367
  110.0 1.7 %collective-permute-start.6 = (bf16[96,768]{1,0:T(8,128)(2,1)S(1)}, bf16[96,768]{1,0:T(8,128)(2,1)S(1)}, u32[]{:S(2)}, u32[]{:S(2)}) collective-permute-start(bf16[96,768]{1,0:T(8,128)(2,1)S(1)} %get-tuple-element.52), channel_id=1, source_target_pairs={{0,4},{4,8},{8,12},{12,0},{1,5},{5,9},{9,13},{13,1},{2,6},{6,10},{... | collective-permute-start | bytes 442376 | tf_op jit(solution)/shard_map/ppermute | solution.py:367
  111.7 2.4 %collective-permute-start.7 = (bf16[96,768]{1,0:T(8,128)(2,1)S(1)}, bf16[96,768]{1,0:T(8,128)(2,1)S(1)}, u32[]{:S(2)}, u32[]{:S(2)}) collective-permute-start(bf16[96,768]{1,0:T(8,128)(2,1)S(1)} %get-tuple-element.51), channel_id=1, source_target_pairs={{0,8},{4,12},{8,0},{12,4},{1,9},{5,13},{9,1},{13,5},{2,10},{6,14},... | collective-permute-start | bytes 442376 | tf_op jit(solution)/shard_map/ppermute | solution.py:367
  114.1 1.5 collective-permute-start.8
  115.5 3.2 %collective-permute-done.6.refs_0_ = bf16[96,768]{1,0:T(8,128)(2,1)S(1)} collective-permute-done((bf16[96,768]{1,0:T(8,128)(2,1)S(1)}, bf16[96,768]{1,0:T(8,128)(2,1)S(1)}, u32[]{:S(2)}, u32[]{:S(2)}) %collective-permute-start.6) | collective-permute-done | bytes 147488 | tf_op jit(solution)/shard_map/ppermute | solution.py:367
  118.7 5.2 %collective-permute-done.7.refs_1_ = bf16[96,768]{1,0:T(8,128)(2,1)S(1)} collective-permute-done((bf16[96,768]{1,0:T(8,128)(2,1)S(1)}, bf16[96,768]{1,0:T(8,128)(2,1)S(1)}, u32[]{:S(2)}, u32[]{:S(2)}) %collective-permute-start.7) | collective-permute-done | bytes 147488 | tf_op jit(solution)/shard_map/ppermute | solution.py:367
  124.0 1.8 %collective-permute-start.9 = (bf16[96,768]{1,0:T(8,128)(2,1)S(1)}, bf16[96,768]{1,0:T(8,128)(2,1)S(1)}, u32[]{:S(2)}, u32[]{:S(2)}) collective-permute-start(bf16[96,768]{1,0:T(8,128)(2,1)S(1)} %close.1), channel_id=1, source_target_pairs={{0,2},{1,3},{2,0},{3,1},{4,6},{5,7},{6,4},{7,5},{8,10},{9,11},{10,... | collective-permute-start | bytes 442376 | tf_op jit(solution)/shard_map/ppermute | solution.py:362
  125.8 2.4 %fill.1 = (bf16[1024,384]{1,0:T(8,128)(2,1)S(1)}, bf16[96,384]{1,0:T(8,128)(2,1)S(1)}, bf16[96,384]{1,0:T(8,128)(2,1)S(1)}, bf16[96,384]{1,0:T(8,128)(2,1)S(1)},...) custom-call(s32[1]{0:T(128)} %bitcast.2.place_ref.place, s32[8,35]{1,0:T(8,128)S(1)} %bitcast.42, ...), custom_call_target="tpu_custom_call" | custom-call | flops 461373440 | bytes 3145728 | tf_op jit(solution)/shard_map/fill/pallas_call | solution.py:532
  128.3 3.7 %collective-permute-start.11 = (bf16[96,384]{1,0:T(8,128)(2,1)S(1)}, bf16[96,384]{1,0:T(8,128)(2,1)S(1)}, u32[]{:S(2)}, u32[]{:S(2)}) collective-permute-start(bf16[96,384]{1,0:T(8,128)(2,1)S(1)} %get-tuple-element.39), channel_id=1, source_target_pairs={{0,4},{4,8},{8,12},{12,0},{1,5},{5,9},{9,13},{13,1},{2,6},{6,10},{... | collective-permute-start | bytes 221192 | tf_op jit(solution)/shard_map/ppermute | solution.py:367
  131.9 0.9 collective-permute-start.12
  132.8 1.5 collective-permute-start.13
  134.3 1.1 collective-permute-start.14
  135.4 3.6 %collective-permute-start.15 = (bf16[16,384]{1,0:T(8,128)(2,1)S(1)}, bf16[16,384]{1,0:T(8,128)(2,1)S(1)}, u32[]{:S(2)}, u32[]{:S(2)}) collective-permute-start(bf16[16,384]{1,0:T(8,128)(2,1)S(1)} %get-tuple-element.43), channel_id=1, source_target_pairs={{0,28},{4,16},{8,20},{12,24},{16,12},{20,0},{24,4},{28,8},{1,29},{... | collective-permute-start | bytes 36872 | tf_op jit(solution)/shard_map/ppermute | solution.py:553
  139.1 1.6 %collective-permute-done.14.b = bf16[16,384]{1,0:T(8,128)(2,1)S(1)} collective-permute-done((bf16[16,384]{1,0:T(8,128)(2,1)S(1)}, bf16[16,384]{1,0:T(8,128)(2,1)S(1)}, u32[]{:S(2)}, u32[]{:S(2)}) %collective-permute-start.14) | collective-permute-done | bytes 12320 | tf_op jit(solution)/shard_map/ppermute | solution.py:553
  140.8 7.5 %mix.1.normed_ref = bf16[1024,384]{1,0:T(8,128)(2,1)S(1)} custom-call(s32[1]{0:T(128)} %bitcast.2.place_ref.place, bf16[1024,384]{1,0:T(8,128)(2,1)S(1)} %get-tuple-element.38.grid.grid_ref, bf16[96,384]{1,0:T(8,128)(2,1)S(1)} %collective-permute-done.11.left, bf16[96,384]{1,0:T(8,128)(2,1)S(1)} %collective-permute-done.12.right, ...), custom_call_target="tpu_custom_call" | custom-call | flops 15414067200 | bytes 3145728 | tf_op jit(solution)/shard_map/mix/pallas_call | solution.py:579
  148.3 3.4 %feed.1 = f32[1024,128]{1,0:T(8,128)} custom-call(bf16[1024,384]{1,0:T(8,128)(2,1)S(1)} %mix.1.normed_ref, bf16[1024,384]{1,0:T(8,128)(2,1)S(1)} %get-tuple-element.38.grid.grid_ref, bf16[384,768]{1,0:T(8,128)(2,1)S(1)} %copy-done.26, bf16[768,384]{1,0:T(8,128)(2,1)S(1)} %copy-done.27, bf16[384,128]{1,0:T(8,128)(2,1)S(1)} %copy-done.28), custom_call_target="tpu_custom_call" | custom-call | flops 1308622848 | bytes 4194304 | tf_op jit(solution)/shard_map/feed/pallas_call | solution.py:592
  151.6 1.1 spread.1
  (70 shorter events, 3.2 us)
Async XLA Ops:
  0.6 11.1 %copy-start = (bf16[768,768]{1,0:T(8,128)(2,1)S(1)}, bf16[768,768]{1,0:T(8,128)(2,1)}, u32[]{:S(2)}) copy-start(bf16[768,768]{1,0:T(8,128)(2,1)} %wout_ref.3) | copy-start | bytes 3538948
  0.6 1.5 copy-start.4
  2.8 8.9 %copy-start.10 = (bf16[1,1,1,256,768]{4,3,2,1,0:T(8,128)(2,1)S(1)}, bf16[1,1,1,256,768]{4,3,2,1,0:T(8,128)(2,1)}, u32[]{:S(2)}) copy-start(bf16[1,1,1,256,768]{4,3,2,1,0:T(8,128)(2,1)} %param.19) | copy-start | bytes 1179652
  4.5 21.9 %all-to-all-start = ((bf16[8,40,768]{2,1,0:T(8,128)(2,1)}), bf16[8,40,768]{2,1,0:T(8,128)(2,1)S(1)}, u32[]{:S(2)}, u32[]{:S(2)}) async-start(bf16[8,40,768]{2,1,0:T(8,128)(2,1)} %bitcast.7), calls=%async_computation | async-start | bytes 983040 | tf_op jit(solution)/shard_map/all_to_all | solution.py:456
  11.8 2.0 %copy-start.1 = (bf16[768,2304]{1,0:T(8,128)(2,1)S(1)}, bf16[768,2304]{1,0:T(8,128)(2,1)}, u32[]{:S(2)}) copy-start(bf16[768,2304]{1,0:T(8,128)(2,1)} %wqkv_ref.1) | copy-start | bytes 10616836
  13.8 12.7 %copy-start.9 = (bf16[768,384]{1,0:T(8,128)(2,1)S(1)}, bf16[768,384]{1,0:T(8,128)(2,1)}, u32[]{:S(2)}) copy-start(bf16[768,384]{1,0:T(8,128)(2,1)} %wdec_ref.1) | copy-start | bytes 1769476
  13.8 12.7 %copy-start.23 = (f32[12]{0:T(128)S(1)}, f32[12]{0:T(128)}, u32[]{:S(2)}) copy-start(f32[12]{0:T(128)} %scale_ref.3) | copy-start | bytes 148
  13.8 12.7 %copy-start.24 = (s32[1,1,1,256]{3,2,1,0:T(1,128)S(1)}, s32[1,1,1,256]{3,2,1,0:T(1,128)}, u32[]{:S(2)}) copy-start(s32[1,1,1,256]{3,2,1,0:T(1,128)} %param.17) | copy-start | bytes 3076
  13.8 12.7 %copy-start.25 = (s32[1,1,1,256]{3,2,1,0:T(1,128)S(1)}, s32[1,1,1,256]{3,2,1,0:T(1,128)}, u32[]{:S(2)}) copy-start(s32[1,1,1,256]{3,2,1,0:T(1,128)} %param.18) | copy-start | bytes 3076
  14.9 1.8 %copy-start.2 = (bf16[2304,768]{1,0:T(8,128)(2,1)}, bf16[2304,768]{1,0:T(8,128)(2,1)S(1)}, u32[]{:S(2)}) copy-start(bf16[2304,768]{1,0:T(8,128)(2,1)S(1)} %get-tuple-element.23.wqkv_t_ref) | copy-start | bytes 10616836
  16.6 0.7 copy-start.11
  26.5 2.0 %copy-start.3 = (bf16[2304,768]{1,0:T(8,128)(2,1)S(1)}, bf16[2304,768]{1,0:T(8,128)(2,1)}, u32[]{:S(2)}) copy-start(bf16[2304,768]{1,0:T(8,128)(2,1)} %copy-done.2) | copy-start | bytes 10616836
  35.4 0.7 copy-start.17
  36.7 18.0 %copy-start.5 = (bf16[12,256,256]{2,1,0:T(8,128)(2,1)}, bf16[12,256,256]{2,1,0:T(8,128)(2,1)S(1)}, u32[]{:S(2)}) copy-start(bf16[12,256,256]{2,1,0:T(8,128)(2,1)S(1)} %get-tuple-element.24.p_ref) | copy-start | bytes 4718596
  36.7 18.0 %copy-start.7 = (f32[1536,256]{1,0:T(8,128)}, f32[1536,256]{1,0:T(8,128)S(1)}, u32[]{:S(2)}) copy-start(f32[1536,256]{1,0:T(8,128)S(1)} %get-tuple-element.25.u_ref) | copy-start | bytes 4718596
  36.7 17.8 %collective-permute-start.3 = (bf16[2,256,768]{2,1,0:T(8,128)(2,1)S(1)}, bf16[2,256,768]{2,1,0:T(8,128)(2,1)S(1)}, u32[]{:S(2)}, u32[]{:S(2)}) collective-permute-start(bf16[2,256,768]{2,1,0:T(8,128)(2,1)S(1)} %get-tuple-element.32), channel_id=1, source_target_pairs={{0,2},{1,3},{2,0},{3,1},{4,6},{5,7},{6,4},{7,5},{8,10},{9,11},{10,... | collective-permute-start | bytes 2359304 | tf_op jit(solution)/shard_map/ppermute | solution.py:362
  54.7 17.7 %collective-permute-start.4 = (bf16[2,2,256,768]{3,2,1,0:T(8,128)(2,1)S(1)}, bf16[2,2,256,768]{3,2,1,0:T(8,128)(2,1)}, u32[]{:S(2)}, u32[]{:S(2)}) collective-permute-start(bf16[2,2,256,768]{3,2,1,0:T(8,128)(2,1)S(1)} %pad_maximum_fusion.e01), channel_id=1, source_target_pairs={{0,1},{1,0},{2,3},{3,2},{4,5},{5,4},{6,7},{7,6},{8,9},{9,8},{10,11... | collective-permute-start | bytes 4718600 | tf_op jit(solution)/shard_map/ppermute | solution.py:362
  54.8 14.4 %all-to-all-start.1 = ((bf16[8,40,384]{2,1,0:T(8,128)(2,1)}), bf16[8,40,384]{2,1,0:T(8,128)(2,1)}, u32[]{:S(2)}, u32[]{:S(2)}) async-start(bf16[8,40,384]{2,1,0:T(8,128)(2,1)} %bitcast.10), calls=%async_computation.1 | async-start | bytes 491520 | tf_op jit(solution)/shard_map/all_to_all | solution.py:490
  58.8 1.4 copy-start.6
  60.3 1.4 copy-start.8
  61.7 1.0 copy-start.12
  62.7 1.0 copy-start.18
  63.7 0.7 copy-start.20
  70.2 12.2 %collective-permute-start = (bf16[8,96,256]{2,1,0:T(8,128)(2,1)}, bf16[8,96,256]{2,1,0:T(8,128)(2,1)S(1)}, u32[]{:S(2)}, u32[]{:S(2)}) collective-permute-start(bf16[8,96,256]{2,1,0:T(8,128)(2,1)} %get-tuple-element.48), channel_id=1, source_target_pairs={{0,2},{1,3},{2,0},{3,1},{4,6},{5,7},{6,4},{7,5},{8,10},{9,11},{10,... | collective-permute-start | bytes 1179656 | tf_op jit(solution)/shard_map/ppermute | solution.py:362
  71.7 10.7 %collective-permute-start.1 = (bf16[8,96,256]{2,1,0:T(8,128)(2,1)}, bf16[8,96,256]{2,1,0:T(8,128)(2,1)S(1)}, u32[]{:S(2)}, u32[]{:S(2)}) collective-permute-start(bf16[8,96,256]{2,1,0:T(8,128)(2,1)} %get-tuple-element.47), channel_id=1, source_target_pairs={{0,1},{1,0},{2,3},{3,2},{4,5},{5,4},{6,7},{7,6},{8,9},{9,8},{10,11... | collective-permute-start | bytes 1179656 | tf_op jit(solution)/shard_map/ppermute | solution.py:362
  71.8 17.0 %collective-permute-start.2 = (bf16[8,96,256]{2,1,0:T(8,128)(2,1)}, bf16[8,96,256]{2,1,0:T(8,128)(2,1)S(1)}, u32[]{:S(2)}, u32[]{:S(2)}) collective-permute-start(bf16[8,96,256]{2,1,0:T(8,128)(2,1)} %get-tuple-element.46), channel_id=1, source_target_pairs={{0,3},{1,2},{2,1},{3,0},{4,7},{5,6},{6,5},{7,4},{8,11},{9,10},{10,... | collective-permute-start | bytes 1179656 | tf_op jit(solution)/shard_map/ppermute | solution.py:362
  82.5 0.7 copy-start.13
  88.7 0.7 copy-start.15
  89.5 1.0 copy-start.14
  90.5 1.0 copy-start.16
  93.8 16.1 %collective-permute-start.5 = (bf16[4,96,768]{2,1,0:T(8,128)(2,1)}, bf16[4,96,768]{2,1,0:T(8,128)(2,1)S(1)}, u32[]{:S(2)}, u32[]{:S(2)}) collective-permute-start(bf16[4,96,768]{2,1,0:T(8,128)(2,1)} %get-tuple-element.34), channel_id=1, source_target_pairs={{0,16},{16,0},{1,17},{17,1},{2,18},{18,2},{3,19},{19,3},{4,20},{20... | collective-permute-start | bytes 1769480 | tf_op jit(solution)/shard_map/ppermute | solution.py:367
  109.9 15.9 %copy-start.31 = (bf16[384]{0:T(512)(128)(2,1)S(1)}, bf16[384]{0:T(512)(128)(2,1)}, u32[]{:S(2)}) copy-start(bf16[384]{0:T(512)(128)(2,1)} %param.24) | copy-start | bytes 2308
  109.9 15.9 %copy-start.30 = (f32[7,7,384]{2,1,0:T(8,128)S(1)}, f32[7,7,384]{2,1,0:T(8,128)}, u32[]{:S(2)}) copy-start(f32[7,7,384]{2,1,0:T(8,128)} %param.25) | copy-start | bytes 225796
  109.9 15.9 %copy-start.22 = (s32[1,1,1,8,35]{4,3,2,1,0:T(8,128)S(1)}, s32[1,1,1,8,35]{4,3,2,1,0:T(8,128)}, u32[]{:S(2)}) copy-start(s32[1,1,1,8,35]{4,3,2,1,0:T(8,128)} %param.16) | copy-start | bytes 3364
  109.9 15.9 %copy-start.29 = (f32[2,1408]{1,0:T(2,128)S(1)}, f32[2,1408]{1,0:T(2,128)}, u32[]{:S(2)}) copy-start(f32[2,1408]{1,0:T(2,128)} %constant.15.clone.ids_ref) | copy-start | bytes 33796
  110.0 8.7 %collective-permute-start.6 = (bf16[96,768]{1,0:T(8,128)(2,1)S(1)}, bf16[96,768]{1,0:T(8,128)(2,1)S(1)}, u32[]{:S(2)}, u32[]{:S(2)}) collective-permute-start(bf16[96,768]{1,0:T(8,128)(2,1)S(1)} %get-tuple-element.52), channel_id=1, source_target_pairs={{0,4},{4,8},{8,12},{12,0},{1,5},{5,9},{9,13},{13,1},{2,6},{6,10},{... | collective-permute-start | bytes 442376 | tf_op jit(solution)/shard_map/ppermute | solution.py:367
  111.7 12.2 %collective-permute-start.7 = (bf16[96,768]{1,0:T(8,128)(2,1)S(1)}, bf16[96,768]{1,0:T(8,128)(2,1)S(1)}, u32[]{:S(2)}, u32[]{:S(2)}) collective-permute-start(bf16[96,768]{1,0:T(8,128)(2,1)S(1)} %get-tuple-element.51), channel_id=1, source_target_pairs={{0,8},{4,12},{8,0},{12,4},{1,9},{5,13},{9,1},{13,5},{2,10},{6,14},... | collective-permute-start | bytes 442376 | tf_op jit(solution)/shard_map/ppermute | solution.py:367
  114.1 9.8 %collective-permute-start.8 = (bf16[96,768]{1,0:T(8,128)(2,1)S(1)}, bf16[96,768]{1,0:T(8,128)(2,1)S(1)}, u32[]{:S(2)}, u32[]{:S(2)}) collective-permute-start(bf16[96,768]{1,0:T(8,128)(2,1)S(1)} %get-tuple-element.50), channel_id=1, source_target_pairs={{0,12},{4,0},{8,4},{12,8},{1,13},{5,1},{9,5},{13,9},{2,14},{6,2},{... | collective-permute-start | bytes 442376 | tf_op jit(solution)/shard_map/ppermute | solution.py:367
  124.0 11.5 %collective-permute-start.9 = (bf16[96,768]{1,0:T(8,128)(2,1)S(1)}, bf16[96,768]{1,0:T(8,128)(2,1)S(1)}, u32[]{:S(2)}, u32[]{:S(2)}) collective-permute-start(bf16[96,768]{1,0:T(8,128)(2,1)S(1)} %close.1), channel_id=1, source_target_pairs={{0,2},{1,3},{2,0},{3,1},{4,6},{5,7},{6,4},{7,5},{8,10},{9,11},{10,... | collective-permute-start | bytes 442376 | tf_op jit(solution)/shard_map/ppermute | solution.py:362
  128.3 12.5 %collective-permute-start.11 = (bf16[96,384]{1,0:T(8,128)(2,1)S(1)}, bf16[96,384]{1,0:T(8,128)(2,1)S(1)}, u32[]{:S(2)}, u32[]{:S(2)}) collective-permute-start(bf16[96,384]{1,0:T(8,128)(2,1)S(1)} %get-tuple-element.39), channel_id=1, source_target_pairs={{0,4},{4,8},{8,12},{12,0},{1,5},{5,9},{9,13},{13,1},{2,6},{6,10},{... | collective-permute-start | bytes 221192 | tf_op jit(solution)/shard_map/ppermute | solution.py:367
  131.9 8.8 %collective-permute-start.12 = (bf16[96,384]{1,0:T(8,128)(2,1)S(1)}, bf16[96,384]{1,0:T(8,128)(2,1)S(1)}, u32[]{:S(2)}, u32[]{:S(2)}) collective-permute-start(bf16[96,384]{1,0:T(8,128)(2,1)S(1)} %get-tuple-element.40), channel_id=1, source_target_pairs={{0,12},{4,0},{8,4},{12,8},{1,13},{5,1},{9,5},{13,9},{2,14},{6,2},{... | collective-permute-start | bytes 221192 | tf_op jit(solution)/shard_map/ppermute | solution.py:367
  132.8 7.9 %collective-permute-start.13 = (bf16[96,384]{1,0:T(8,128)(2,1)S(1)}, bf16[96,384]{1,0:T(8,128)(2,1)S(1)}, u32[]{:S(2)}, u32[]{:S(2)}) collective-permute-start(bf16[96,384]{1,0:T(8,128)(2,1)S(1)} %get-tuple-element.41), channel_id=1, source_target_pairs={{0,16},{4,20},{8,24},{12,28},{16,0},{20,4},{24,8},{28,12},{1,17},{... | collective-permute-start | bytes 221192 | tf_op jit(solution)/shard_map/ppermute | solution.py:553
  134.3 6.4 %collective-permute-start.14 = (bf16[16,384]{1,0:T(8,128)(2,1)S(1)}, bf16[16,384]{1,0:T(8,128)(2,1)S(1)}, u32[]{:S(2)}, u32[]{:S(2)}) collective-permute-start(bf16[16,384]{1,0:T(8,128)(2,1)S(1)} %get-tuple-element.42), channel_id=1, source_target_pairs={{0,20},{4,24},{8,28},{12,16},{16,4},{20,8},{24,12},{28,0},{1,21},{... | collective-permute-start | bytes 36872 | tf_op jit(solution)/shard_map/ppermute | solution.py:553
  135.4 5.3 %collective-permute-start.15 = (bf16[16,384]{1,0:T(8,128)(2,1)S(1)}, bf16[16,384]{1,0:T(8,128)(2,1)S(1)}, u32[]{:S(2)}, u32[]{:S(2)}) collective-permute-start(bf16[16,384]{1,0:T(8,128)(2,1)S(1)} %get-tuple-element.43), channel_id=1, source_target_pairs={{0,28},{4,16},{8,20},{12,24},{16,12},{20,0},{24,4},{28,8},{1,29},{... | collective-permute-start | bytes 36872 | tf_op jit(solution)/shard_map/ppermute | solution.py:553
  140.7 10.9 %collective-permute-start.10 = (bf16[2,96,768]{2,1,0:T(8,128)(2,1)S(1)}, bf16[2,96,768]{2,1,0:T(8,128)(2,1)S(1)}, u32[]{:S(2)}, u32[]{:S(2)}) collective-permute-start(bf16[2,96,768]{2,1,0:T(8,128)(2,1)S(1)} %pad_maximum_fusion.1.first_ref), channel_id=1, source_target_pairs={{0,1},{1,0},{2,3},{3,2},{4,5},{5,4},{6,7},{7,6},{8,9},{9,8},{10,11... | collective-permute-start | bytes 884744 | tf_op jit(solution)/shard_map/ppermute | solution.py:362
  140.7 7.5 %copy-start.26 = (bf16[384,768]{1,0:T(8,128)(2,1)S(1)}, bf16[384,768]{1,0:T(8,128)(2,1)}, u32[]{:S(2)}) copy-start(bf16[384,768]{1,0:T(8,128)(2,1)} %up_ref.1) | copy-start | bytes 1769476
  140.8 7.5 %copy-start.27 = (bf16[768,384]{1,0:T(8,128)(2,1)S(1)}, bf16[768,384]{1,0:T(8,128)(2,1)}, u32[]{:S(2)}) copy-start(bf16[768,384]{1,0:T(8,128)(2,1)} %down_ref.1) | copy-start | bytes 1769476
  140.8 7.5 %copy-start.28 = (bf16[384,128]{1,0:T(8,128)(2,1)S(1)}, bf16[384,128]{1,0:T(8,128)(2,1)}, u32[]{:S(2)}) copy-start(bf16[384,128]{1,0:T(8,128)(2,1)} %head_ref.1) | copy-start | bytes 294916
  (2 other events, 1.3 us)

commit v3 on v2

v3 whole, which is shorter than its diff:
```python
import functools

import jax
import jax.numpy as jnp
import numpy as np
from jax import lax
from jax.experimental import pallas as pl
from jax.experimental.pallas import tpu as pltpu
from jax.sharding import PartitionSpec as P

norm_eps = 1e-05
length_eps = 1e-06
f32 = jnp.float32
bf16 = jnp.bfloat16
MIB = 1024 * 1024

NN = (((1,), (0,)), ((), ()))
NT = (((1,), (1,)), ((), ()))
TN = (((0,), (0,)), ((), ()))


def mm(a, b, dims=NN):
    return lax.dot_general(a, b, dims, preferred_element_type=f32)


def vmem():
    return pl.BlockSpec(memory_space=pltpu.VMEM)


def smem():
    return pl.BlockSpec(memory_space=pltpu.SMEM)


def call(kernel, name, outs, in_specs, scratch=(), flops=0, nbytes=0, limit=20):
    single = not isinstance(outs, (list, tuple))
    out_list = [outs] if single else list(outs)
    specs = [vmem() for _ in out_list]
    return pl.pallas_call(
        kernel,
        out_shape=out_list[0] if single else tuple(out_list),
        in_specs=in_specs,
        out_specs=specs[0] if single else tuple(specs),
        scratch_shapes=list(scratch),
        compiler_params=pltpu.CompilerParams(vmem_limit_bytes=limit * MIB),
        cost_estimate=pl.CostEstimate(flops=flops, bytes_accessed=nbytes, transcendentals=0),
        name=name,
    )


def sds(shape, dtype):
    return jax.ShapeDtypeStruct(shape, dtype)


def column_of(row):
    return jnp.transpose(jnp.broadcast_to(row, (8, row.shape[1])))[:, 0:1]


def slot_column(pos_ref, wide_ref, padded):
    group, cap = pos_ref.shape
    wide_ref[...] = jnp.full(wide_ref.shape, -1.0, f32)
    wide_ref[:, 0:cap] = pos_ref[...].astype(f32)
    turned = jnp.transpose(wide_ref[...])
    return jnp.concatenate([turned[0:padded, d : d + 1] for d in range(group)], axis=0)


def pick_kernel(padded, pos_ref, tok_ref, out_ref, wide_ref):
    slots = slot_column(pos_ref, wide_ref, padded)
    cells = lax.broadcasted_iota(jnp.int32, (slots.shape[0], tok_ref.shape[0]), 1).astype(f32)
    chosen = (slots == cells).astype(f32).astype(bf16)
    out_ref[...] = mm(chosen, tok_ref[...]).astype(bf16)


def prep_kernel(split, cot_ref, wout_ref, wqkv_ref, ga_ref, wqkv_t_ref, *refs):
    ga_ref[...] = mm(wout_ref[...], cot_ref[...], NT).astype(bf16)
    emit(split, refs[-1], 0, jnp.transpose(cot_ref[...]))
    deal(split, refs[-1], refs[:-1])
    wqkv_t_ref[...] = jnp.transpose(wqkv_ref[...])


def project_kernel(
    cap, padded, src_ref, arr_ref, wqkv_t_ref, normed_ref, enc_ref, u_ref, len_ref, v_ref,
    place_ref,
):
    rows, width = normed_ref.shape
    heads = len_ref.shape[0] // 2
    size = width // heads
    slots = arr_ref.shape[0]
    src = src_ref[...].astype(f32)
    slot_row = src + (padded - cap) * jnp.floor((src + 0.5) * (1.0 / cap))
    place_ref[...] = slot_row
    slot_col = column_of(slot_row)
    lanes = lax.broadcasted_iota(jnp.int32, (rows, slots), 1).astype(f32)
    pick = (slot_col == lanes).astype(f32).astype(bf16)
    enc_in = mm(pick, arr_ref[...])
    enc_ref[...] = enc_in.astype(bf16)
    centred = enc_in - jnp.mean(enc_in, axis=-1, keepdims=True)
    spread = jnp.mean(centred * centred, axis=-1, keepdims=True)
    normed = (centred * lax.rsqrt(spread + norm_eps)).astype(bf16)
    normed_ref[...] = normed
    for t in range(2):
        raw = mm(wqkv_t_ref[t * width : (t + 1) * width], normed, NT)
        for h in range(heads):
            part = raw[h * size : (h + 1) * size]
            inv = lax.rsqrt(jnp.sum(part * part, axis=0, keepdims=True) + length_eps)
            at = t * width + h * size
            u_ref[at : at + size] = part * inv
            len_ref[t * heads + h : t * heads + h + 1] = inv
    v_ref[...] = mm(wqkv_t_ref[2 * width : 3 * width], normed, NT).astype(bf16)


def encode_kernel(
    split, win_ref, scale_ref, place_ref, enc_ref, u_ref, len_ref, v_ref, ga_ref, wout_ref,
    wdec_ref, out_ref, e_ref, *refs,
):
    left_refs = refs[:-3]
    p_ref, att_ref, left_ref = refs[-3:]
    rows, width = e_ref.shape
    heads = p_ref.shape[0]
    size = width // heads
    slots = out_ref.shape[0]
    win = win_ref[...].astype(f32)
    same = column_of(win) == win
    for h in range(heads):
        lo, hi = h * size, (h + 1) * size
        q = u_ref[lo:hi].astype(bf16)
        k = u_ref[width + lo : width + hi].astype(bf16)
        scores = mm(k, q, TN)
        raised = jnp.where(same, jnp.exp(scores * scale_ref[h]), 0.0)
        weights = (raised * (1.0 / jnp.sum(raised, axis=0, keepdims=True))).astype(bf16)
        p_ref[h] = weights
        att_ref[lo:hi] = mm(v_ref[lo:hi], weights).astype(bf16)
    attended = jnp.transpose(att_ref[...])
    e_ref[...] = attended
    enc_out = (enc_ref[...].astype(f32) + mm(attended, wout_ref[...])).astype(bf16)
    dec = mm(enc_out, wdec_ref[...]).astype(bf16)
    places = lax.broadcasted_iota(jnp.int32, (slots, rows), 0).astype(f32)
    put = (places == place_ref[...]).astype(f32).astype(bf16)
    out_ref[...] = mm(put, dec).astype(bf16)
    for h in range(heads):
        lo, hi = h * size, (h + 1) * size
        ga = ga_ref[lo:hi]
        low = p_ref[h]
        weights = low.astype(f32)
        grad_soft = mm(v_ref[lo:hi], ga, TN)
        part = weights * grad_soft
        total = jnp.sum(part, axis=0, keepdims=True)
        grad_scores = ((part - weights * total) * scale_ref[h]).astype(bf16)
        q = u_ref[lo:hi]
        k = u_ref[width + lo : width + hi]
        grad_v = mm(ga, low, NT)
        grad_q = mm(k.astype(bf16), grad_scores)
        grad_k = mm(q.astype(bf16), grad_scores, NT)
        grad_q = (grad_q - q * jnp.sum(q * grad_q, axis=0, keepdims=True)) * len_ref[h : h + 1]
        grad_k = (grad_k - k * jnp.sum(k * grad_k, axis=0, keepdims=True)) * len_ref[
            heads + h : heads + h + 1
        ]
        emit(split, left_ref, lo, grad_q.astype(bf16))
        emit(split, left_ref, width + lo, grad_k.astype(bf16))
        emit(split, left_ref, 2 * width + lo, grad_v.astype(bf16))
    deal(split, left_ref, left_refs)


def deal(split, left_ref, left_refs):
    if split is None:
        left_refs[0][...] = left_ref[...]
        return
    me = lax.axis_index("replica")
    for n, ref in enumerate(left_refs):
        ref[...] = left_ref[me ^ n]


def emit(split, out_ref, start, block):
    if split is None:
        out_ref[start : start + block.shape[0]] = block
        return
    unit = 32
    per_shard, per_part = split[0] // unit, split[1] // unit
    for j in range(block.shape[0] // unit):
        shard, rest = divmod(start // unit + j, per_shard)
        part, place = divmod(rest, per_part)
        out_ref[part, shard, place * unit : (place + 1) * unit] = block[
            j * unit : (j + 1) * unit
        ]


def term_kernel(columns, *refs):
    lefts, cots, normed, attended = refs[0:4], refs[4:8], refs[8:12], refs[12:16]
    keep_ref, send_ref = refs[16:]
    qkv, part, rows = lefts[0].shape
    shards = qkv + cots[0].shape[0]
    half = shards // 2
    cut = slice(*columns)
    width = columns[1] - columns[0]

    def block(left, lo, hi, right):
        acc = None
        for ref, e in zip(left, right):
            step = mm(ref[lo:hi].reshape((hi - lo) * part, rows), e[:, cut])
            acc = step if acc is None else acc + step
        return acc.reshape(hi - lo, part, width)

    first = [(0, block(lefts, 0, half, normed))]
    second = [
        (0, block(lefts, half, qkv, normed)),
        (qkv - half, block(cots, 0, shards - qkv, attended)),
    ]
    spans = (first, second)
    for mine in range(2):

        @pl.when(lax.axis_index("eta") == mine)
        def _():
            for at, value in spans[mine]:
                keep_ref[at : at + value.shape[0]] = value
            for at, value in spans[1 - mine]:
                send_ref[at : at + value.shape[0]] = value.astype(bf16)


def line_kernel(keep_ref, got_ref, own_ref, *send_refs):
    count = keep_ref.shape[0]
    me = lax.axis_index("phi")
    own_ref[...] = keep_ref[me] + got_ref[me].astype(f32)
    for k, ref in enumerate(send_refs):
        at = lax.rem(me + k + 1, count)
        ref[...] = (keep_ref[at] + got_ref[at].astype(f32)).astype(bf16)


def close_kernel(count, *refs):
    width = refs[0].shape[-1]
    for n in range((len(refs) - 1) // count):
        total = refs[n * count][...]
        for ref in refs[n * count + 1 : (n + 1) * count]:
            total = total + ref[...].astype(f32)
        refs[-1][:, n * width : (n + 1) * width] = total.astype(bf16)


def spread_kernel(own_ref, one_ref, two_ref, three_ref, out_ref):
    me = lax.axis_index("replica")
    for n, ref in enumerate((own_ref, one_ref, two_ref, three_ref)):
        out_ref[me ^ n] = ref[...].astype(f32)


def tie(values, *others):
    return lax.optimization_barrier((values, others))[0]


def fill_kernel(padded, pos_ref, ids_ref, mask_ref, got_ref, *refs):
    wide_ref = refs[-1]
    slots = slot_column(pos_ref, wide_ref, padded)
    ids = ids_ref[0:1] + lax.axis_index("eta").astype(f32) * ids_ref[1:2]
    chosen = (slots == ids).astype(f32).astype(bf16)
    got = got_ref[...]
    values = mm(chosen, got, TN)
    hits = mm(chosen, jnp.ones((got.shape[0], 128), bf16), TN)[:, 0:1]
    values = jnp.where(hits > 0.5, values, mask_ref[...].astype(f32)).astype(bf16)
    at = 0
    for ref in refs[:-1]:
        ref[...] = values[at : at + ref.shape[0]]
        at += ref.shape[0]


def conv_kernel_body(
    shape, span, folded, grid_ref, left_ref, right_ref, rims, taps_ref, out_ref,
    full_ref, wide_ref, mixed_ref,
):
    lines, columns = shape
    rim = span // 2
    width = grid_ref.shape[-1]
    lead = 8
    full_ref[rim : rim + lines, lead : lead + columns] = (
        grid_ref[...].astype(f32).reshape(lines, columns, width)
    )
    left = left_ref[...].astype(f32)
    right = right_ref[...].astype(f32)
    for x in range(lines):
        full_ref[rim + x, lead - rim : lead] = left[rim * x : rim * (x + 1)]
        full_ref[rim + x, lead + columns : lead + columns + rim] = right[rim * x : rim * (x + 1)]

    def put(base, edge_ref, first_ref, last_ref):
        edge = edge_ref[...].astype(f32)
        first = first_ref[...].astype(f32)
        last = last_ref[...].astype(f32)
        for i in range(rim):
            full_ref[base + i, lead : lead + columns] = edge[columns * i : columns * (i + 1)]
            full_ref[base + i, lead - rim : lead] = first[rim * i : rim * (i + 1)]
            full_ref[base + i, lead + columns : lead + columns + rim] = last[
                rim * i : rim * (i + 1)
            ]

    if folded:
        far = rim + lines
        base = jnp.where(lax.axis_index("eta") == 0, far, 0)
        for i in range(rim):
            full_ref[far - base + i] = jnp.zeros(full_ref.shape[1:], f32)
        put(base, *rims)
    else:
        put(0, *rims[:3])
        put(rim + lines, *rims[3:])
    for t in range(span * span):
        wide_ref[t] = jnp.broadcast_to(taps_ref[t // span, t % span : t % span + 1], (8, width))
    groups = columns // 8

    for c in range(width // 128):
        cut = slice(c * 128, (c + 1) * 128)

        def step(x, accs, live, cut=cut):
            accs = list(accs)
            for v in range(span):
                at = lead - rim + v
                line = full_ref[x, at : at + columns, cut].reshape(groups, 8, 128)
                for i in live:
                    tap = wide_ref[(span - 1 - i) * span + v, :, cut]
                    accs[i] = accs[i] + line * tap[None]
            return accs

        def store(row, acc, cut=cut):
            at = row * columns
            if not isinstance(row, int):
                at = pl.multiple_of(at, columns)
            mixed_ref[pl.ds(at, columns), cut] = acc.reshape(columns, 128)

        zero = jnp.zeros((groups, 8, 128), f32)
        accs = [zero] * span
        for x in range(span - 1):
            accs = step(x, accs, range(span - 1 - x, span))
            accs = accs[1:] + [zero]

        def middle(x, accs):
            accs = step(x, accs, range(span))
            store(x - (span - 1), accs[0])
            return tuple(accs[1:] + [zero])

        accs = list(lax.fori_loop(span - 1, lines, middle, tuple(accs)))
        for x in range(lines, lines + span - 1):
            accs = step(x, accs, range(0, lines + span - 1 - x))
            store(x - (span - 1), accs[0])
            accs = accs[1:] + [zero]

    mixed = mixed_ref[...]
    centred = mixed - jnp.mean(mixed, axis=-1, keepdims=True)
    spread = jnp.mean(centred * centred, axis=-1, keepdims=True)
    out_ref[...] = (centred * lax.rsqrt(spread + norm_eps)).astype(bf16)


def mix_folded(shape, span, grid, left, right, a, b, c, taps, out, full, wide, mixed):
    conv_kernel_body(
        shape, span, True, grid, left, right, (a, b, c), taps, out, full, wide, mixed
    )


def mix_open(
    shape, span, grid, left, right, a, b, c, d, e, g, taps, out, full, wide, mixed
):
    conv_kernel_body(
        shape, span, False, grid, left, right, (a, b, c, d, e, g), taps, out, full, wide,
        mixed,
    )


def feed_kernel(chunk, normed_ref, grid_ref, up_ref, down_ref, head_ref, out_ref):
    for at in range(0, normed_ref.shape[0], chunk):
        rows = slice(at, at + chunk)
        wide = mm(normed_ref[rows], up_ref[...])
        hidden = (0.5 * wide * (1.0 + lax.erf(wide * 0.7071067811865476))).astype(bf16)
        decoded = (grid_ref[rows].astype(f32) + mm(hidden, down_ref[...])).astype(bf16)
        out_ref[rows] = mm(decoded, head_ref[...])


def flip(value, axis, bit):
    return lax.ppermute(value, axis, [(i, i ^ bit) for i in range(lax.axis_size(axis))])


def turn(value, axis, k):
    count = lax.axis_size(axis)
    return lax.ppermute(value, axis, [(i, (i + k) % count) for i in range(count)])


def summed_slow(left, cot_t, normed, attended):
    term = jnp.concatenate([mm(left, normed), mm(cot_t, attended)], axis=0)
    share = lax.psum_scatter(term, ("eta", "phi", "replica"), scatter_dimension=0, tiled=True)
    return lax.all_gather(share.astype(bf16), "replica", axis=0, tiled=True).astype(f32)


def body(
    tokens, send_pos, enc_src, window_id, enc_cot, w_qkv, head_scale, w_out, w_dec_in,
    mask_token, conv_kernel, w_up, w_down, w_head,
):
    eta_cells, phi_cells, width = tokens.shape[1:]
    dec_width = w_dec_in.shape[1]
    tile_len = eta_cells * phi_cells
    eta_count = lax.axis_size("eta")
    phi_count = lax.axis_size("phi")
    replicas = lax.axis_size("replica")
    group = eta_count * phi_count
    cap = send_pos.shape[-1]
    padded = -(-cap // 8) * 8
    slots = group * padded
    rows = enc_cot.shape[-2]
    heads = head_scale.shape[0]
    out_rows = 4 * width
    shard_rows = out_rows // group
    part_rows = shard_rows // replicas
    fast = (
        eta_count == 2
        and replicas == 4
        and part_rows % 32 == 0
        and width % shard_rows == 0
        and 3 * width // shard_rows >= group // 2
    )

    positions = send_pos.reshape(group, cap)
    outgoing = call(
        functools.partial(pick_kernel, padded),
        "pick",
        sds((slots, width), bf16),
        [vmem(), vmem()],
        scratch=[pltpu.VMEM((group, 128), f32)],
        flops=2 * slots * tile_len * width,
        nbytes=3 * MIB,
        limit=8,
    )(positions, tokens.reshape(tile_len, width))
    arrived = lax.all_to_all(
        outgoing.reshape(group, padded, width), ("eta", "phi"), split_axis=0, concat_axis=0,
        tiled=True,
    ).reshape(slots, width)

    cotangent = enc_cot.reshape(rows, width)
    split = (shard_rows, part_rows) if fast else None
    pieces = replicas if fast else 1
    cot_part = (width // shard_rows, part_rows, rows) if fast else (width, rows)
    left_part = (3 * width // shard_rows, part_rows, rows) if fast else (3 * width, rows)
    cot_whole = (replicas,) + cot_part if fast else cot_part
    left_whole = (replicas,) + left_part if fast else left_part
    grad_att, w_qkv_t, *cots = call(
        functools.partial(prep_kernel, split),
        "prep",
        [sds((width, rows), bf16), sds((3 * width, width), bf16)]
        + [sds(cot_part, bf16)] * pieces,
        [vmem()] * 3,
        scratch=[pltpu.VMEM(cot_whole, bf16)],
        flops=2 * rows * width * width,
        nbytes=10 * MIB,
        limit=10,
    )(cotangent, w_out, w_qkv)
    if fast:
        cots = [cots[0]] + [flip(cots[k], "replica", k) for k in range(1, 4)]
        arrived = tie(arrived, cots)

    normed, enc_in, units, lengths, values, places = call(
        functools.partial(project_kernel, cap, padded),
        "project",
        [
            sds((rows, width), bf16),
            sds((rows, width), bf16),
            sds((2 * width, rows), f32),
            sds((2 * heads, rows), f32),
            sds((width, rows), bf16),
            sds((1, rows), f32),
        ],
        [vmem()] * 3,
        flops=2 * rows * width * width * 4,
        nbytes=8 * MIB,
        limit=10,
    )(enc_src.reshape(1, rows), arrived, w_qkv_t)
    if fast:
        normed_y = flip(normed, "replica", 2)

    outbound, attended, *lefts = call(
        functools.partial(encode_kernel, split),
        "encode",
        [sds((slots, dec_width), bf16), sds((rows, width), bf16)]
        + [sds(left_part, bf16)] * pieces,
        [vmem(), smem()] + [vmem()] * 8,
        scratch=[
            pltpu.VMEM((heads, rows, rows), bf16),
            pltpu.VMEM((width, rows), bf16),
            pltpu.VMEM(left_whole, bf16),
        ],
        flops=2 * rows * width * width * 10,
        nbytes=8 * MIB,
        limit=14,
    )(
        window_id.reshape(1, rows), head_scale, places, enc_in, units, lengths, values, grad_att,
        w_out, w_dec_in,
    )
    returned = lax.all_to_all(
        outbound.reshape(group, padded, dec_width), ("eta", "phi"), split_axis=0, concat_axis=0,
        tiled=True,
    )
    if fast:
        lefts = [lefts[0]] + [flip(lefts[k], "replica", k) for k in range(1, 4)]
        attended_y = flip(attended, "replica", 2)
        normed_y = tie(normed_y, attended)
        right = [normed, flip(normed, "replica", 1), normed_y, flip(normed_y, "replica", 1)]
        right += [
            attended, flip(attended, "replica", 1), attended_y, flip(attended_y, "replica", 1),
        ]
    else:
        grad_total = summed_slow(lefts[0], cots[0], normed, attended)

    span = conv_kernel.shape[0]
    rim = span // 2
    folded = eta_count == 2
    lines = np.arange(eta_cells)[:, None]
    columns = np.arange(phi_cells)[None, :]
    cell = lines * phi_cells + columns
    parts = [cell]
    moves = [0]
    if folded:
        edge = cell[eta_cells - rim :]
        parts += [cell[:, :rim], cell[:, -rim:], edge, edge[:, :rim], edge[:, -rim:]]
        moves += [0, 0] + [-(eta_cells - rim) * phi_cells] * 3
    sizes = [-(-p.size // 16) * 16 for p in parts]
    ids = np.full((2, -(-sum(sizes) // 128) * 128), -7.0, np.float32)
    ids[1] = 0
    at = 0
    for p, size, move in zip(parts, sizes, moves):
        ids[0, at : at + p.size] = p.reshape(-1)
        ids[1, at : at + p.size] = move
        at += size
    filled = call(
        functools.partial(fill_kernel, padded),
        "fill",
        [sds((size, dec_width), bf16) for size in sizes],
        [vmem()] * 4,
        scratch=[pltpu.VMEM((group, 128), f32)],
        flops=2 * slots * ids.shape[1] * (dec_width + 128),
        nbytes=3 * MIB,
        limit=12,
    )(
        positions, jnp.asarray(ids), mask_token.reshape(1, dec_width),
        returned.reshape(slots, dec_width),
    )
    dec_grid = filled[0]
    plane = ("eta", "phi")

    def shifted(value, by):
        pairs = [
            (e * phi_count + p, (1 - e) * phi_count + (p + by) % phi_count)
            for e in range(2)
            for p in range(phi_count)
        ]
        return lax.ppermute(value, plane, pairs)

    if folded:
        _, first, last, edge, edge_first, edge_last = filled
        left_halo = turn(last, "phi", 1)
        right_halo = turn(first, "phi", -1)
        rims = (shifted(edge, 0), shifted(edge_last, 1), shifted(edge_first, -1))
    else:
        box = dec_grid.reshape(eta_cells, phi_cells, dec_width)
        down = [(i, i + 1) for i in range(eta_count - 1)]
        up = [(i + 1, i) for i in range(eta_count - 1)]
        top = lax.ppermute(box[eta_cells - rim :], "eta", down)
        bottom = lax.ppermute(box[:rim], "eta", up)
        box = jnp.concatenate([top, box, bottom], axis=0)
        low = turn(box[:, phi_cells - rim :], "phi", 1)
        high = turn(box[:, :rim], "phi", -1)

        def flat(value):
            return value.reshape(-1, dec_width)

        far = eta_cells + rim
        left_halo, right_halo = flat(low[rim:far]), flat(high[rim:far])
        rims = (
            flat(top), flat(low[:rim]), flat(high[:rim]),
            flat(bottom), flat(low[far:]), flat(high[far:]),
        )
    if fast:
        lefts, cots, right = tie((lefts, cots, right), filled)
        chunk = width // 2
        half = group // 2
        kept, sent = [], []
        for c in range(2):
            keep, send = call(
                functools.partial(term_kernel, (c * chunk, (c + 1) * chunk)),
                "terms%d" % c,
                [sds((half, part_rows, chunk), f32), sds((half, part_rows, chunk), bf16)],
                [vmem()] * 16,
                flops=2 * out_rows * chunk * rows,
                nbytes=8 * MIB,
                limit=10,
            )(*lefts, *cots, *right)
            kept.append(keep)
            sent.append(turn(send, "eta", 1))
        left, right_halo, rims = tie((left_halo, right_halo, rims), kept)
    else:
        left = left_halo
    normed_cells = call(
        functools.partial(mix_folded if folded else mix_open, (eta_cells, phi_cells), span),
        "mix",
        sds((tile_len, dec_width), bf16),
        [vmem()] * (4 + len(rims)),
        scratch=[
            pltpu.VMEM((eta_cells + 2 * rim, phi_cells + 16, dec_width), f32),
            pltpu.VMEM((span * span, 8, dec_width), f32),
            pltpu.VMEM((tile_len, dec_width), f32),
        ],
        flops=200 * 2 * span * span * tile_len * dec_width,
        nbytes=3 * MIB,
        limit=16,
    )(dec_grid, left, right_halo, *rims, conv_kernel)
    if fast:
        summed = []
        for c in range(2):
            own, *outs = call(
                line_kernel,
                "line%d" % c,
                [sds((part_rows, chunk), f32)] + [sds((part_rows, chunk), bf16)] * (phi_count - 1),
                [vmem()] * 2,
                flops=half * part_rows * chunk,
                nbytes=2 * MIB,
                limit=4,
            )(kept[c], tie(sent[c], normed_cells))
            summed.append([own] + [turn(outs[k], "phi", k + 1) for k in range(phi_count - 1)])
            normed_cells = tie(normed_cells, own)
    reconstruction = call(
        functools.partial(feed_kernel, 256),
        "feed",
        sds((tile_len, w_head.shape[1]), f32),
        [vmem()] * 5,
        flops=2 * tile_len * dec_width * (2 * w_up.shape[1] + w_head.shape[1]),
        nbytes=4 * MIB,
        limit=12,
    )(normed_cells, dec_grid, w_up, w_down, w_head).reshape(1, eta_cells, phi_cells, -1)
    if fast:
        summed = tie(summed, reconstruction)
        mine = call(
            functools.partial(close_kernel, phi_count),
            "close",
            sds((part_rows, width), bf16),
            [vmem()] * (2 * phi_count),
            flops=4 * part_rows * width,
            nbytes=MIB,
            limit=4,
        )(*summed[0], *summed[1])
        mine_y = flip(mine, "replica", 2)
        grad_total = call(
            spread_kernel,
            "spread",
            sds((replicas, part_rows, width), f32),
            [vmem()] * 4,
            flops=4 * part_rows * width,
            nbytes=2 * MIB,
            limit=4,
        )(
            mine, flip(mine, "replica", 1), mine_y, flip(mine_y, "replica", 1),
        ).reshape(shard_rows, width)
    return (grad_total, reconstruction)


def solution(mesh):
    in_specs = (
        P("replica", "eta", "phi", None),
        P("replica", "eta", "phi", None, None),
        P("replica", "eta", "phi", None),
        P("replica", "eta", "phi", None),
        P("replica", "eta", "phi", None, None),
        P(), P(), P(), P(), P(), P(), P(), P(), P(),
    )
    out_specs = (P(("eta", "phi"), None), P("replica", "eta", "phi", None))
    return jax.shard_map(body, mesh=mesh, in_specs=in_specs, out_specs=out_specs, check_vma=False)
```

time: 154 us -> 114 us (0.74)
  waiting for transfers between devices: 64.6 us -> 30.9 us
  local copies, waits for them, and re-layouts: 21.6 us -> 9.38 us
  starting transfers between devices: 34.9 us -> 40.2 us
  Pallas kernels: 30.5 us -> 32.3 us
    ppermute x6 -> x10, waiting for transfers between devices: 22.7 us -> 5.05 us  [turn(): lax.ppermute(value, axis, [(i, (i + k) % count) for i in range(count)])]
    unnamed x64 -> x54, local copies, waits for them, and re-layouts: 19.1 us -> 9.38 us
    ppermute x7 -> x15, waiting for transfers between devices: 30.4 us -> 22.4 us  [flip(): lax.ppermute(value, axis, [(i, i ^ bit) for i in range(lax.axis_size(axis...]
    all_to_all x1, waiting for transfers between devices: 9.05 us -> 2.86 us  [body(): lax.all_to_all(outgoing.reshape(group, padded, width), ('eta', 'phi'), sp...]
    ppermute x7 -> x15, starting transfers between devices: 5.55 us -> 9.3 us  [flip(): lax.ppermute(value, axis, [(i, i ^ bit) for i in range(lax.axis_size(axis...]
    squeeze x3 -> x0, local copies, waits for them, and re-layouts: 2.53 us -> none  [the longest x1 1.47 us: summed_fast(): other[1]]
    pallas_call x7 -> x9, Pallas kernels: 15.6 us -> 17.4 us  [the longest x1 8.69 us: body(): call(functools.partial(encode_kernel, split), 'encode', [sds((slots, dec_...]
    ppermute x6 -> x10, starting transfers between devices: 11.8 us -> 13.6 us  [turn(): lax.ppermute(value, axis, [(i, (i + k) % count) for i in range(count)])]
  transfers between devices with their start and end apart: 18 -> 30, of which waited for: 9 -> 13; matrix products, arithmetic and copies ran while one was open for 2% -> 0% of each run, Pallas kernels for 12% -> 24%
where the time goes in v3:
time: 114 us
  starting transfers between devices  40.2 us (35%)
  Pallas kernels  32.3 us (28%)
  waiting for transfers between devices  30.9 us (27%)
  local copies, waits for them, and re-layouts  9.38 us (8%)
    ppermute x15, waiting for transfers between devices, flip(): lax.ppermute(value, axis, [(i, i ^ bit) for i in range(lax.axis_size(axis...  22.4 us
    ppermute x10, starting transfers between devices, turn(): lax.ppermute(value, axis, [(i, (i + k) % count) for i in range(count)])  13.6 us
    unnamed x54, local copies, waits for them, and re-layouts  9.38 us
    ppermute x15, starting transfers between devices, flip(): lax.ppermute(value, axis, [(i, i ^ bit) for i in range(lax.axis_size(axis...  9.3 us
    pallas_call x1, Pallas kernels, body(): call(functools.partial(encode_kernel, split), 'encode', [sds((slots, dec_...  8.69 us
    pallas_call x1, Pallas kernels, body(): call(functools.partial(mix_folded if folded else mix_open, (eta_cells, ph...  7.45 us
    all_to_all x1, starting transfers between devices, body(): lax.all_to_all(outgoing.reshape(group, padded, width), ('eta', 'phi'), sp...  7.25 us
    ppermute x3, starting transfers between devices, shifted(): return lax.ppermute(value, plane, pairs)  6.03 us
  transfers between devices with their start and end apart: 30, of which 13 were waited for; matrix products, arithmetic and copies ran while one was open for 0% of the time, Pallas kernels for 24%

profile of v3, /device:TPU:0, one launch (start us, length us, event | category | flops | bytes accessed | tf_op | source)
XLA Modules:
  0.0 113.7 jit_solution(10540463939320534916)
XLA Ops:
  0.6 1.4 %copy-done.1 = bf16[1,32,32,768]{3,2,1,0:T(8,128)(2,1)S(1)} copy-done((bf16[1,32,32,768]{3,2,1,0:T(8,128)(2,1)S(1)}, bf16[1,32,32,768]{3,2,1,0:T(8,128)(2,1)}, u32[]{:S(2)}) %copy-start.1) | copy-done | bytes 1572888
  2.0 0.7 copy-done.12
  2.7 1.7 %pick.1 = bf16[320,768]{1,0:T(8,128)(2,1)} custom-call(s32[8,35]{1,0:T(8,128)S(1)} %bitcast.14, bf16[1024,768]{1,0:T(8,128)(2,1)S(1)} %bitcast.11), custom_call_target="tpu_custom_call" | custom-call | flops 503316480 | bytes 3145728 | tf_op jit(solution)/shard_map/pick/pallas_call | solution.py:411
  4.4 7.3 %all-to-all-start = ((bf16[8,40,768]{2,1,0:T(8,128)(2,1)}), bf16[8,40,768]{2,1,0:T(8,128)(2,1)S(1)}, u32[]{:S(2)}, u32[]{:S(2)}) async-start(bf16[8,40,768]{2,1,0:T(8,128)(2,1)} %bitcast.4), calls=%async_computation | async-start | bytes 983040 | tf_op jit(solution)/shard_map/all_to_all | solution.py:421
  11.7 2.0 %copy-done = bf16[768,2304]{1,0:T(8,128)(2,1)S(1)} copy-done((bf16[768,2304]{1,0:T(8,128)(2,1)S(1)}, bf16[768,2304]{1,0:T(8,128)(2,1)}, u32[]{:S(2)}) %copy-start) | copy-done | bytes 3538968
  13.7 1.1 prep.1
  14.8 1.7 %copy-done.14 = bf16[2304,768]{1,0:T(8,128)(2,1)} copy-done((bf16[2304,768]{1,0:T(8,128)(2,1)}, bf16[2304,768]{1,0:T(8,128)(2,1)S(1)}, u32[]{:S(2)}) %copy-start.14) | copy-done | bytes 3538968
  16.6 1.5 %collective-permute-start.1 = (bf16[2,96,256]{2,1,0:T(8,128)(2,1)S(1)}, bf16[2,96,256]{2,1,0:T(8,128)(2,1)S(1)}, u32[]{:S(2)}, u32[]{:S(2)}) collective-permute-start(bf16[2,96,256]{2,1,0:T(8,128)(2,1)S(1)} %get-tuple-element.75), channel_id=1, source_target_pairs={{0,2},{1,3},{2,0},{3,1},{4,6},{5,7},{6,4},{7,5},{8,10},{9,11},{10,... | collective-permute-start | bytes 294920 | tf_op jit(solution)/shard_map/ppermute | solution.py:369
  18.4 3.7 %collective-permute-done.1.refs_6_ = bf16[2,96,256]{2,1,0:T(8,128)(2,1)S(1)} collective-permute-done((bf16[2,96,256]{2,1,0:T(8,128)(2,1)S(1)}, bf16[2,96,256]{2,1,0:T(8,128)(2,1)S(1)}, u32[]{:S(2)}, u32[]{:S(2)}) %collective-permute-start.1) | collective-permute-done | bytes 98336 | tf_op jit(solution)/shard_map/ppermute | solution.py:369
  22.1 1.3 %collective-permute-done.2.refs_7_ = bf16[2,96,256]{2,1,0:T(8,128)(2,1)S(1)} collective-permute-done((bf16[2,96,256]{2,1,0:T(8,128)(2,1)S(1)}, bf16[2,96,256]{2,1,0:T(8,128)(2,1)S(1)}, u32[]{:S(2)}, u32[]{:S(2)}) %collective-permute-start.2) | collective-permute-done | bytes 98336 | tf_op jit(solution)/shard_map/ppermute | solution.py:369
  23.5 2.9 %all-to-all-done = bf16[8,40,768]{2,1,0:T(8,128)(2,1)S(1)} async-done(((bf16[8,40,768]{2,1,0:T(8,128)(2,1)}), bf16[8,40,768]{2,1,0:T(8,128)(2,1)S(1)}, u32[]{:S(2)}, u32[]{:S(2)}) %all-to-all-start) | async-done | bytes 491552 | tf_op jit(solution)/shard_map/all_to_all | solution.py:421
  26.3 2.0 %copy-done.15 = bf16[2304,768]{1,0:T(8,128)(2,1)S(1)} copy-done((bf16[2304,768]{1,0:T(8,128)(2,1)S(1)}, bf16[2304,768]{1,0:T(8,128)(2,1)}, u32[]{:S(2)}) %copy-start.15) | copy-done | bytes 3538968
  28.4 2.0 %project.1 = (bf16[256,768]{1,0:T(8,128)(2,1)S(1)}, bf16[256,768]{1,0:T(8,128)(2,1)S(1)}, f32[1536,256]{1,0:T(8,128)S(1)}, f32[24,256]{1,0:T(8,128)S(1)}, bf16[7...) custom-call(s32[1,256]{1,0:T(1,128)S(1)} %bitcast.16, bf16[320,768]{1,0:T(8,128)(2,1)S(1)} %bitcast.12, ...), custom_call_target="tpu_custom_call" | custom-call | flops 1207959552 | bytes 8388608 | tf_op jit(solution)/shard_map/project/pallas_call | solution.py:448
  30.4 1.6 %collective-permute-start.7 = (bf16[256,768]{1,0:T(8,128)(2,1)S(1)}, bf16[256,768]{1,0:T(8,128)(2,1)S(1)}, u32[]{:S(2)}, u32[]{:S(2)}) collective-permute-start(bf16[256,768]{1,0:T(8,128)(2,1)S(1)} %get-tuple-element.107.refs_8_), channel_id=1, source_target_pairs={{0,2},{1,3},{2,0},{3,1},{4,6},{5,7},{6,4},{7,5},{8,10},{9,11},{10,... | collective-permute-start | bytes 1179656 | tf_op jit(solution)/shard_map/ppermute | solution.py:369
  32.0 8.7 %encode.1 = (bf16[320,384]{1,0:T(8,128)(2,1)}, bf16[256,768]{1,0:T(8,128)(2,1)S(1)}, bf16[6,96,256]{2,1,0:T(8,128)(2,1)S(1)}, bf16[6,96,256]{2,1,0:T(8,128)(2,1)...) custom-call(s32[1,256]{1,0:T(1,128)S(1)} %bitcast.17, f32[12]{0:T(128)S(1)} %copy-done.24, ...), custom_call_target="tpu_custom_call" | custom-call | flops 3019898880 | bytes 8388608 | tf_op jit(solution)/shard_map/encode/pallas_call | solution.py:467
  40.7 0.5 collective-permute-start.10
  41.2 1.5 %collective-permute-start.4 = (bf16[6,96,256]{2,1,0:T(8,128)(2,1)}, bf16[6,96,256]{2,1,0:T(8,128)(2,1)}, u32[]{:S(2)}, u32[]{:S(2)}) collective-permute-start(bf16[6,96,256]{2,1,0:T(8,128)(2,1)} %get-tuple-element.87), channel_id=1, source_target_pairs={{0,2},{1,3},{2,0},{3,1},{4,6},{5,7},{6,4},{7,5},{8,10},{9,11},{10,... | collective-permute-start | bytes 884744 | tf_op jit(solution)/shard_map/ppermute | solution.py:369
  42.8 4.0 %all-to-all-start.1 = ((bf16[8,40,384]{2,1,0:T(8,128)(2,1)}), bf16[8,40,384]{2,1,0:T(8,128)(2,1)}, u32[]{:S(2)}, u32[]{:S(2)}) async-start(bf16[8,40,384]{2,1,0:T(8,128)(2,1)} %bitcast.7), calls=%async_computation.1 | async-start | bytes 491520 | tf_op jit(solution)/shard_map/all_to_all | solution.py:485
  47.4 0.7 copy-done.2
  48.3 4.5 %collective-permute-done.10.refs_14_ = bf16[256,768]{1,0:T(8,128)(2,1)S(1)} collective-permute-done((bf16[256,768]{1,0:T(8,128)(2,1)S(1)}, bf16[256,768]{1,0:T(8,128)(2,1)S(1)}, u32[]{:S(2)}, u32[]{:S(2)}) %collective-permute-start.10) | collective-permute-done | bytes 393248 | tf_op jit(solution)/shard_map/ppermute | solution.py:369
  52.8 3.5 %collective-permute-done.4.refs_2_ = bf16[6,96,256]{2,1,0:T(8,128)(2,1)} collective-permute-done((bf16[6,96,256]{2,1,0:T(8,128)(2,1)}, bf16[6,96,256]{2,1,0:T(8,128)(2,1)}, u32[]{:S(2)}, u32[]{:S(2)}) %collective-permute-start.4) | collective-permute-done | bytes 294944 | tf_op jit(solution)/shard_map/ppermute | solution.py:369
  56.3 0.6 all-to-all-done.1
  56.9 0.8 copy-done.25
  57.7 2.4 %fill.1 = (bf16[1024,384]{1,0:T(8,128)(2,1)S(1)}, bf16[96,384]{1,0:T(8,128)(2,1)S(1)}, bf16[96,384]{1,0:T(8,128)(2,1)S(1)}, bf16[96,384]{1,0:T(8,128)(2,1)S(1)},...) custom-call(s32[8,35]{1,0:T(8,128)S(1)} %bitcast.15, f32[2,1408]{1,0:T(2,128)S(1)} %copy-done.25, ...), custom_call_target="tpu_custom_call" | custom-call | flops 461373440 | bytes 3145728 | tf_op jit(solution)/shard_map/fill/pallas_call | solution.py:520
  60.1 4.9 %collective-permute-done.5.refs_3_ = bf16[6,96,256]{2,1,0:T(8,128)(2,1)} collective-permute-done((bf16[6,96,256]{2,1,0:T(8,128)(2,1)}, bf16[6,96,256]{2,1,0:T(8,128)(2,1)}, u32[]{:S(2)}, u32[]{:S(2)}) %collective-permute-start.5) | collective-permute-done | bytes 294944 | tf_op jit(solution)/shard_map/ppermute | solution.py:369
  65.0 1.1 collective-permute-start.13
  66.1 2.7 %collective-permute-start.14 = (bf16[96,384]{1,0:T(8,128)(2,1)S(1)}, bf16[96,384]{1,0:T(8,128)(2,1)S(1)}, u32[]{:S(2)}, u32[]{:S(2)}) collective-permute-start(bf16[96,384]{1,0:T(8,128)(2,1)S(1)} %get-tuple-element.94), channel_id=1, source_target_pairs={{0,12},{4,0},{8,4},{12,8},{1,13},{5,1},{9,5},{13,9},{2,14},{6,2},{... | collective-permute-start | bytes 221192 | tf_op jit(solution)/shard_map/ppermute | solution.py:374
  68.8 1.3 %collective-permute-start.15 = (bf16[96,384]{1,0:T(8,128)(2,1)S(1)}, bf16[96,384]{1,0:T(8,128)(2,1)S(1)}, u32[]{:S(2)}, u32[]{:S(2)}) collective-permute-start(bf16[96,384]{1,0:T(8,128)(2,1)S(1)} %get-tuple-element.96), channel_id=1, source_target_pairs={{0,16},{4,20},{8,24},{12,28},{16,0},{20,4},{24,8},{28,12},{1,17},{... | collective-permute-start | bytes 221192 | tf_op jit(solution)/shard_map/ppermute | solution.py:542
  70.1 4.7 %collective-permute-start.17 = (bf16[16,384]{1,0:T(8,128)(2,1)S(1)}, bf16[16,384]{1,0:T(8,128)(2,1)S(1)}, u32[]{:S(2)}, u32[]{:S(2)}) collective-permute-start(bf16[16,384]{1,0:T(8,128)(2,1)S(1)} %get-tuple-element.97), channel_id=1, source_target_pairs={{0,28},{4,16},{8,20},{12,24},{16,12},{20,0},{24,4},{28,8},{1,29},{... | collective-permute-start | bytes 36872 | tf_op jit(solution)/shard_map/ppermute | solution.py:542
  74.9 2.1 %terms1.1 = (f32[4,96,384]{2,1,0:T(8,128)S(1)}, bf16[4,96,384]{2,1,0:T(8,128)(2,1)S(1)}) custom-call(bf16[6,96,256]{2,1,0:T(8,128)(2,1)S(1)} %get-tuple-element.99.refs_0_, bf16[6,96,256]{2,1,0:T(8,128)(2,1)S(1)} %copy-done.3, bf16[6,96,256]{2,1,0:T(8,128)(2,1)} %collective-permute-done.4.refs_2_, bf16[6,96,256]{2,1,0:T(8,128)(2,1)} %collective-permute-done.5.refs_3_, ...), custom_call_target="tpu_custom_call" | custom-call | flops 603979776 | bytes 8388608 | tf_op jit(solution)/shard_map/terms1/pallas_call | solution.py:574
  77.0 2.1 %terms0.1 = (f32[4,96,384]{2,1,0:T(8,128)S(1)}, bf16[4,96,384]{2,1,0:T(8,128)(2,1)S(1)}) custom-call(bf16[6,96,256]{2,1,0:T(8,128)(2,1)S(1)} %get-tuple-element.99.refs_0_, bf16[6,96,256]{2,1,0:T(8,128)(2,1)S(1)} %copy-done.3, bf16[6,96,256]{2,1,0:T(8,128)(2,1)} %collective-permute-done.4.refs_2_, bf16[6,96,256]{2,1,0:T(8,128)(2,1)} %collective-permute-done.5.refs_3_, ...), custom_call_target="tpu_custom_call" | custom-call | flops 603979776 | bytes 8388608 | tf_op jit(solution)/shard_map/terms0/pallas_call | solution.py:574
  79.2 0.8 collective-permute-start.12
  80.0 1.3 %collective-permute-start.21 = (bf16[4,96,384]{2,1,0:T(8,128)(2,1)S(1)}, bf16[4,96,384]{2,1,0:T(8,128)(2,1)S(1)}, u32[]{:S(2)}, u32[]{:S(2)}) collective-permute-start(bf16[4,96,384]{2,1,0:T(8,128)(2,1)S(1)} %get-tuple-element.128), channel_id=1, source_target_pairs={{0,16},{16,0},{1,17},{17,1},{2,18},{18,2},{3,19},{19,3},{4,20},{20... | collective-permute-start | bytes 884744 | tf_op jit(solution)/shard_map/ppermute | solution.py:374
  81.3 7.5 %mix.1.normed_ref = bf16[1024,384]{1,0:T(8,128)(2,1)S(1)} custom-call(bf16[1024,384]{1,0:T(8,128)(2,1)S(1)} %get-tuple-element.93.grid.grid_ref, bf16[96,384]{1,0:T(8,128)(2,1)S(1)} %collective-permute-done.13.left, bf16[96,384]{1,0:T(8,128)(2,1)S(1)} %collective-permute-done.14.right, bf16[96,384]{1,0:T(8,128)(2,1)S(1)} %collective-permute-done.15.a, ...), custom_call_target="tpu_custom_call" | custom-call | flops 7707033600 | bytes 3145728 | tf_op jit(solution)/shard_map/mix/pallas_call | solution.py:588
  88.8 0.3 collective-permute-done.12.got_ref
  89.2 3.1 %collective-permute-done.21.got_ref = bf16[4,96,384]{2,1,0:T(8,128)(2,1)S(1)} collective-permute-done((bf16[4,96,384]{2,1,0:T(8,128)(2,1)S(1)}, bf16[4,96,384]{2,1,0:T(8,128)(2,1)S(1)}, u32[]{:S(2)}, u32[]{:S(2)}) %collective-permute-start.21) | collective-permute-done | bytes 294944 | tf_op jit(solution)/shard_map/ppermute | solution.py:374
  92.4 1.2 %collective-permute-start.23 = (bf16[96,384]{1,0:T(8,128)(2,1)S(1)}, bf16[96,384]{1,0:T(8,128)(2,1)S(1)}, u32[]{:S(2)}, u32[]{:S(2)}) collective-permute-start(bf16[96,384]{1,0:T(8,128)(2,1)S(1)} %get-tuple-element.133), channel_id=1, source_target_pairs={{0,8},{4,12},{8,0},{12,4},{1,9},{5,13},{9,1},{13,5},{2,10},{6,14},... | collective-permute-start | bytes 221192 | tf_op jit(solution)/shard_map/ppermute | solution.py:374
  93.6 2.6 %collective-permute-start.24 = (bf16[96,384]{1,0:T(8,128)(2,1)S(1)}, bf16[96,384]{1,0:T(8,128)(2,1)S(1)}, u32[]{:S(2)}, u32[]{:S(2)}) collective-permute-start(bf16[96,384]{1,0:T(8,128)(2,1)S(1)} %get-tuple-element.134), channel_id=1, source_target_pairs={{0,12},{4,0},{8,4},{12,8},{1,13},{5,1},{9,5},{13,9},{2,14},{6,2},{... | collective-permute-start | bytes 221192 | tf_op jit(solution)/shard_map/ppermute | solution.py:374
  96.2 0.6 collective-permute-start.18
  96.8 1.5 %collective-permute-start.19 = (bf16[96,384]{1,0:T(8,128)(2,1)S(1)}, bf16[96,384]{1,0:T(8,128)(2,1)S(1)}, u32[]{:S(2)}, u32[]{:S(2)}) collective-permute-start(bf16[96,384]{1,0:T(8,128)(2,1)S(1)} %get-tuple-element.126), channel_id=1, source_target_pairs={{0,8},{4,12},{8,0},{12,4},{1,9},{5,13},{9,1},{13,5},{2,10},{6,14},... | collective-permute-start | bytes 221192 | tf_op jit(solution)/shard_map/ppermute | solution.py:374
  98.2 1.1 %collective-permute-done.22.refs_5_ = bf16[96,384]{1,0:T(8,128)(2,1)S(1)} collective-permute-done((bf16[96,384]{1,0:T(8,128)(2,1)S(1)}, bf16[96,384]{1,0:T(8,128)(2,1)S(1)}, u32[]{:S(2)}, u32[]{:S(2)}) %collective-permute-start.22) | collective-permute-done | bytes 73760 | tf_op jit(solution)/shard_map/ppermute | solution.py:374
  99.4 1.8 %collective-permute-start.20 = (bf16[96,384]{1,0:T(8,128)(2,1)S(1)}, bf16[96,384]{1,0:T(8,128)(2,1)S(1)}, u32[]{:S(2)}, u32[]{:S(2)}) collective-permute-start(bf16[96,384]{1,0:T(8,128)(2,1)S(1)} %get-tuple-element.127), channel_id=1, source_target_pairs={{0,12},{4,0},{8,4},{12,8},{1,13},{5,1},{9,5},{13,9},{2,14},{6,2},{... | collective-permute-start | bytes 221192 | tf_op jit(solution)/shard_map/ppermute | solution.py:374
  101.2 3.3 %feed.1 = f32[1024,128]{1,0:T(8,128)} custom-call(bf16[1024,384]{1,0:T(8,128)(2,1)S(1)} %mix.1.normed_ref, bf16[1024,384]{1,0:T(8,128)(2,1)S(1)} %get-tuple-element.93.grid.grid_ref, bf16[384,768]{1,0:T(8,128)(2,1)S(1)} %copy-done.17, bf16[768,384]{1,0:T(8,128)(2,1)S(1)} %copy-done.18, bf16[384,128]{1,0:T(8,128)(2,1)S(1)} %copy-done.20), custom_call_target="tpu_custom_call" | custom-call | flops 1308622848 | bytes 4194304 | tf_op jit(solution)/shard_map/feed/pallas_call | solution.py:616
  104.5 0.5 collective-permute-done.19.refs_2_
  105.1 3.0 %collective-permute-start.26 = (bf16[96,768]{1,0:T(8,128)(2,1)S(1)}, bf16[96,768]{1,0:T(8,128)(2,1)S(1)}, u32[]{:S(2)}, u32[]{:S(2)}) collective-permute-start(bf16[96,768]{1,0:T(8,128)(2,1)S(1)} %close.1.own_ref), channel_id=1, source_target_pairs={{0,2},{1,3},{2,0},{3,1},{4,6},{5,7},{6,4},{7,5},{8,10},{9,11},{10,... | collective-permute-start | bytes 442376 | tf_op jit(solution)/shard_map/ppermute | solution.py:369
  108.1 3.1 %collective-permute-done.26.two_ref = bf16[96,768]{1,0:T(8,128)(2,1)S(1)} collective-permute-done((bf16[96,768]{1,0:T(8,128)(2,1)S(1)}, bf16[96,768]{1,0:T(8,128)(2,1)S(1)}, u32[]{:S(2)}, u32[]{:S(2)}) %collective-permute-start.26) | collective-permute-done | bytes 147488 | tf_op jit(solution)/shard_map/ppermute | solution.py:369
  111.2 1.4 %collective-permute-done.27.three_ref = bf16[96,768]{1,0:T(8,128)(2,1)S(1)} collective-permute-done((bf16[96,768]{1,0:T(8,128)(2,1)S(1)}, bf16[96,768]{1,0:T(8,128)(2,1)S(1)}, u32[]{:S(2)}, u32[]{:S(2)}) %collective-permute-start.27) | collective-permute-done | bytes 147488 | tf_op jit(solution)/shard_map/ppermute | solution.py:369
  112.6 1.1 spread.1
  (80 shorter events, 1.6 us)
Async XLA Ops:
  2.7 8.9 %copy-start.4 = (bf16[768,768]{1,0:T(8,128)(2,1)S(1)}, bf16[768,768]{1,0:T(8,128)(2,1)}, u32[]{:S(2)}) copy-start(bf16[768,768]{1,0:T(8,128)(2,1)} %wout_ref.3) | copy-start | bytes 3538948
  2.7 8.9 %copy-start.5 = (bf16[1,1,1,256,768]{4,3,2,1,0:T(8,128)(2,1)S(1)}, bf16[1,1,1,256,768]{4,3,2,1,0:T(8,128)(2,1)}, u32[]{:S(2)}) copy-start(bf16[1,1,1,256,768]{4,3,2,1,0:T(8,128)(2,1)} %param.19) | copy-start | bytes 1179652
  4.4 21.9 %all-to-all-start = ((bf16[8,40,768]{2,1,0:T(8,128)(2,1)}), bf16[8,40,768]{2,1,0:T(8,128)(2,1)S(1)}, u32[]{:S(2)}, u32[]{:S(2)}) async-start(bf16[8,40,768]{2,1,0:T(8,128)(2,1)} %bitcast.4), calls=%async_computation | async-start | bytes 983040 | tf_op jit(solution)/shard_map/all_to_all | solution.py:421
  13.7 12.7 %copy-start.22 = (s32[1,1,1,256]{3,2,1,0:T(1,128)S(1)}, s32[1,1,1,256]{3,2,1,0:T(1,128)}, u32[]{:S(2)}) copy-start(s32[1,1,1,256]{3,2,1,0:T(1,128)} %param.17) | copy-start | bytes 3076
  16.5 1.9 %collective-permute-start = (bf16[2,96,256]{2,1,0:T(8,128)(2,1)S(1)}, bf16[2,96,256]{2,1,0:T(8,128)(2,1)S(1)}, u32[]{:S(2)}, u32[]{:S(2)}) collective-permute-start(bf16[2,96,256]{2,1,0:T(8,128)(2,1)S(1)} %get-tuple-element.74), channel_id=1, source_target_pairs={{0,1},{1,0},{2,3},{3,2},{4,5},{5,4},{6,7},{7,6},{8,9},{9,8},{10,11... | collective-permute-start | bytes 294920 | tf_op jit(solution)/shard_map/ppermute | solution.py:369
  16.6 5.6 %collective-permute-start.1 = (bf16[2,96,256]{2,1,0:T(8,128)(2,1)S(1)}, bf16[2,96,256]{2,1,0:T(8,128)(2,1)S(1)}, u32[]{:S(2)}, u32[]{:S(2)}) collective-permute-start(bf16[2,96,256]{2,1,0:T(8,128)(2,1)S(1)} %get-tuple-element.75), channel_id=1, source_target_pairs={{0,2},{1,3},{2,0},{3,1},{4,6},{5,7},{6,4},{7,5},{8,10},{9,11},{10,... | collective-permute-start | bytes 294920 | tf_op jit(solution)/shard_map/ppermute | solution.py:369
  18.1 5.4 %collective-permute-start.2 = (bf16[2,96,256]{2,1,0:T(8,128)(2,1)S(1)}, bf16[2,96,256]{2,1,0:T(8,128)(2,1)S(1)}, u32[]{:S(2)}, u32[]{:S(2)}) collective-permute-start(bf16[2,96,256]{2,1,0:T(8,128)(2,1)S(1)} %get-tuple-element.76), channel_id=1, source_target_pairs={{0,3},{1,2},{2,1},{3,0},{4,7},{5,6},{6,5},{7,4},{8,11},{9,10},{10,... | collective-permute-start | bytes 294920 | tf_op jit(solution)/shard_map/ppermute | solution.py:369
  18.4 12.0 %copy-start.6 = (bf16[2,96,256]{2,1,0:T(8,128)(2,1)}, bf16[2,96,256]{2,1,0:T(8,128)(2,1)S(1)}, u32[]{:S(2)}) copy-start(bf16[2,96,256]{2,1,0:T(8,128)(2,1)S(1)} %collective-permute-done.refs_5_) | copy-start | bytes 294916
  22.1 8.3 %copy-start.8 = (bf16[2,96,256]{2,1,0:T(8,128)(2,1)}, bf16[2,96,256]{2,1,0:T(8,128)(2,1)S(1)}, u32[]{:S(2)}) copy-start(bf16[2,96,256]{2,1,0:T(8,128)(2,1)S(1)} %collective-permute-done.1.refs_6_) | copy-start | bytes 294916
  23.5 6.9 %copy-start.10 = (bf16[2,96,256]{2,1,0:T(8,128)(2,1)}, bf16[2,96,256]{2,1,0:T(8,128)(2,1)S(1)}, u32[]{:S(2)}) copy-start(bf16[2,96,256]{2,1,0:T(8,128)(2,1)S(1)} %collective-permute-done.2.refs_7_) | copy-start | bytes 294916
  28.3 3.7 %copy-start.24 = (f32[12]{0:T(128)S(1)}, f32[12]{0:T(128)}, u32[]{:S(2)}) copy-start(f32[12]{0:T(128)} %scale_ref.1) | copy-start | bytes 148
  30.4 16.7 %collective-permute-start.7 = (bf16[256,768]{1,0:T(8,128)(2,1)S(1)}, bf16[256,768]{1,0:T(8,128)(2,1)S(1)}, u32[]{:S(2)}, u32[]{:S(2)}) collective-permute-start(bf16[256,768]{1,0:T(8,128)(2,1)S(1)} %get-tuple-element.107.refs_8_), channel_id=1, source_target_pairs={{0,2},{1,3},{2,0},{3,1},{4,6},{5,7},{6,4},{7,5},{8,10},{9,11},{10,... | collective-permute-start | bytes 1179656 | tf_op jit(solution)/shard_map/ppermute | solution.py:369
  32.0 24.3 %copy-start.26 = (bf16[384]{0:T(512)(128)(2,1)S(1)}, bf16[384]{0:T(512)(128)(2,1)}, u32[]{:S(2)}) copy-start(bf16[384]{0:T(512)(128)(2,1)} %param.24) | copy-start | bytes 2308
  32.0 24.9 %copy-start.13 = (s32[1,1,1,8,35]{4,3,2,1,0:T(8,128)S(1)}, s32[1,1,1,8,35]{4,3,2,1,0:T(8,128)}, u32[]{:S(2)}) copy-start(s32[1,1,1,8,35]{4,3,2,1,0:T(8,128)} %param.16) | copy-start | bytes 3364
  40.7 7.6 %copy-start.19 = (bf16[6,96,256]{2,1,0:T(8,128)(2,1)}, bf16[6,96,256]{2,1,0:T(8,128)(2,1)S(1)}, u32[]{:S(2)}) copy-start(bf16[6,96,256]{2,1,0:T(8,128)(2,1)S(1)} %get-tuple-element.88) | copy-start | bytes 884740
  40.7 12.1 %collective-permute-start.10 = (bf16[256,768]{1,0:T(8,128)(2,1)S(1)}, bf16[256,768]{1,0:T(8,128)(2,1)S(1)}, u32[]{:S(2)}, u32[]{:S(2)}) collective-permute-start(bf16[256,768]{1,0:T(8,128)(2,1)S(1)} %get-tuple-element.111.refs_12_), channel_id=1, source_target_pairs={{0,2},{1,3},{2,0},{3,1},{4,6},{5,7},{6,4},{7,5},{8,10},{9,11},{10,... | collective-permute-start | bytes 1179656 | tf_op jit(solution)/shard_map/ppermute | solution.py:369
  41.2 6.1 %collective-permute-start.3 = (bf16[6,96,256]{2,1,0:T(8,128)(2,1)}, bf16[6,96,256]{2,1,0:T(8,128)(2,1)S(1)}, u32[]{:S(2)}, u32[]{:S(2)}) collective-permute-start(bf16[6,96,256]{2,1,0:T(8,128)(2,1)} %get-tuple-element.86), channel_id=1, source_target_pairs={{0,1},{1,0},{2,3},{3,2},{4,5},{5,4},{6,7},{7,6},{8,9},{9,8},{10,11... | collective-permute-start | bytes 884744 | tf_op jit(solution)/shard_map/ppermute | solution.py:369
  41.2 15.0 %collective-permute-start.4 = (bf16[6,96,256]{2,1,0:T(8,128)(2,1)}, bf16[6,96,256]{2,1,0:T(8,128)(2,1)}, u32[]{:S(2)}, u32[]{:S(2)}) collective-permute-start(bf16[6,96,256]{2,1,0:T(8,128)(2,1)} %get-tuple-element.87), channel_id=1, source_target_pairs={{0,2},{1,3},{2,0},{3,1},{4,6},{5,7},{6,4},{7,5},{8,10},{9,11},{10,... | collective-permute-start | bytes 884744 | tf_op jit(solution)/shard_map/ppermute | solution.py:369
  42.8 14.1 %all-to-all-start.1 = ((bf16[8,40,384]{2,1,0:T(8,128)(2,1)}), bf16[8,40,384]{2,1,0:T(8,128)(2,1)}, u32[]{:S(2)}, u32[]{:S(2)}) async-start(bf16[8,40,384]{2,1,0:T(8,128)(2,1)} %bitcast.7), calls=%async_computation.1 | async-start | bytes 491520 | tf_op jit(solution)/shard_map/all_to_all | solution.py:485
  46.8 19.3 %collective-permute-start.9 = (bf16[256,768]{1,0:T(8,128)(2,1)S(1)}, bf16[256,768]{1,0:T(8,128)(2,1)S(1)}, u32[]{:S(2)}, u32[]{:S(2)}) collective-permute-start(bf16[256,768]{1,0:T(8,128)(2,1)S(1)} %get-tuple-element.111.refs_12_), channel_id=1, source_target_pairs={{0,1},{1,0},{2,3},{3,2},{4,5},{5,4},{6,7},{7,6},{8,9},{9,8},{10,11... | collective-permute-start | bytes 1179656 | tf_op jit(solution)/shard_map/ppermute | solution.py:369
  47.1 21.7 %collective-permute-start.6 = (bf16[256,768]{1,0:T(8,128)(2,1)S(1)}, bf16[256,768]{1,0:T(8,128)(2,1)S(1)}, u32[]{:S(2)}, u32[]{:S(2)}) collective-permute-start(bf16[256,768]{1,0:T(8,128)(2,1)S(1)} %get-tuple-element.107.refs_8_), channel_id=1, source_target_pairs={{0,1},{1,0},{2,3},{3,2},{4,5},{5,4},{6,7},{7,6},{8,9},{9,8},{10,11... | collective-permute-start | bytes 1179656 | tf_op jit(solution)/shard_map/ppermute | solution.py:369
  48.1 22.0 %collective-permute-start.8 = (bf16[256,768]{1,0:T(8,128)(2,1)S(1)}, bf16[256,768]{1,0:T(8,128)(2,1)S(1)}, u32[]{:S(2)}, u32[]{:S(2)}) collective-permute-start(bf16[256,768]{1,0:T(8,128)(2,1)S(1)} %collective-permute-done.7.refs_10_), channel_id=1, source_target_pairs={{0,1},{1,0},{2,3},{3,2},{4,5},{5,4},{6,7},{7,6},{8,9},{9,8},{10,11... | collective-permute-start | bytes 1179656 | tf_op jit(solution)/shard_map/ppermute | solution.py:369
  52.8 17.4 %collective-permute-start.11 = (bf16[256,768]{1,0:T(8,128)(2,1)S(1)}, bf16[256,768]{1,0:T(8,128)(2,1)S(1)}, u32[]{:S(2)}, u32[]{:S(2)}) collective-permute-start(bf16[256,768]{1,0:T(8,128)(2,1)S(1)} %collective-permute-done.10.refs_14_), channel_id=1, source_target_pairs={{0,1},{1,0},{2,3},{3,2},{4,5},{5,4},{6,7},{7,6},{8,9},{9,8},{10,11... | collective-permute-start | bytes 1179656 | tf_op jit(solution)/shard_map/ppermute | solution.py:369
  56.3 8.7 %collective-permute-start.5 = (bf16[6,96,256]{2,1,0:T(8,128)(2,1)}, bf16[6,96,256]{2,1,0:T(8,128)(2,1)}, u32[]{:S(2)}, u32[]{:S(2)}) collective-permute-start(bf16[6,96,256]{2,1,0:T(8,128)(2,1)} %copy-done.19), channel_id=1, source_target_pairs={{0,3},{1,2},{2,1},{3,0},{4,7},{5,6},{6,5},{7,4},{8,11},{9,10},{10,... | collective-permute-start | bytes 884744 | tf_op jit(solution)/shard_map/ppermute | solution.py:369
  56.9 18.0 %copy-start.3 = (bf16[6,96,256]{2,1,0:T(8,128)(2,1)S(1)}, bf16[6,96,256]{2,1,0:T(8,128)(2,1)}, u32[]{:S(2)}) copy-start(bf16[6,96,256]{2,1,0:T(8,128)(2,1)} %copy-done.2) | copy-start | bytes 884740
  56.9 18.0 %copy-start.7 = (bf16[2,96,256]{2,1,0:T(8,128)(2,1)S(1)}, bf16[2,96,256]{2,1,0:T(8,128)(2,1)}, u32[]{:S(2)}) copy-start(bf16[2,96,256]{2,1,0:T(8,128)(2,1)} %copy-done.6) | copy-start | bytes 294916
  56.9 18.0 %copy-start.9 = (bf16[2,96,256]{2,1,0:T(8,128)(2,1)S(1)}, bf16[2,96,256]{2,1,0:T(8,128)(2,1)}, u32[]{:S(2)}) copy-start(bf16[2,96,256]{2,1,0:T(8,128)(2,1)} %copy-done.8) | copy-start | bytes 294916
  56.9 18.0 %copy-start.11 = (bf16[2,96,256]{2,1,0:T(8,128)(2,1)S(1)}, bf16[2,96,256]{2,1,0:T(8,128)(2,1)}, u32[]{:S(2)}) copy-start(bf16[2,96,256]{2,1,0:T(8,128)(2,1)} %copy-done.10) | copy-start | bytes 294916
  65.0 14.2 %collective-permute-start.13 = (bf16[96,384]{1,0:T(8,128)(2,1)S(1)}, bf16[96,384]{1,0:T(8,128)(2,1)S(1)}, u32[]{:S(2)}, u32[]{:S(2)}) collective-permute-start(bf16[96,384]{1,0:T(8,128)(2,1)S(1)} %get-tuple-element.95), channel_id=1, source_target_pairs={{0,4},{4,8},{8,12},{12,0},{1,5},{5,9},{9,13},{13,1},{2,6},{6,10},{... | collective-permute-start | bytes 221192 | tf_op jit(solution)/shard_map/ppermute | solution.py:374
  66.1 13.0 %collective-permute-start.14 = (bf16[96,384]{1,0:T(8,128)(2,1)S(1)}, bf16[96,384]{1,0:T(8,128)(2,1)S(1)}, u32[]{:S(2)}, u32[]{:S(2)}) collective-permute-start(bf16[96,384]{1,0:T(8,128)(2,1)S(1)} %get-tuple-element.94), channel_id=1, source_target_pairs={{0,12},{4,0},{8,4},{12,8},{1,13},{5,1},{9,5},{13,9},{2,14},{6,2},{... | collective-permute-start | bytes 221192 | tf_op jit(solution)/shard_map/ppermute | solution.py:374
  68.8 10.4 %collective-permute-start.15 = (bf16[96,384]{1,0:T(8,128)(2,1)S(1)}, bf16[96,384]{1,0:T(8,128)(2,1)S(1)}, u32[]{:S(2)}, u32[]{:S(2)}) collective-permute-start(bf16[96,384]{1,0:T(8,128)(2,1)S(1)} %get-tuple-element.96), channel_id=1, source_target_pairs={{0,16},{4,20},{8,24},{12,28},{16,0},{20,4},{24,8},{28,12},{1,17},{... | collective-permute-start | bytes 221192 | tf_op jit(solution)/shard_map/ppermute | solution.py:542
  70.1 9.0 %collective-permute-start.16 = (bf16[16,384]{1,0:T(8,128)(2,1)S(1)}, bf16[16,384]{1,0:T(8,128)(2,1)S(1)}, u32[]{:S(2)}, u32[]{:S(2)}) collective-permute-start(bf16[16,384]{1,0:T(8,128)(2,1)S(1)} %get-tuple-element.98), channel_id=1, source_target_pairs={{0,20},{4,24},{8,28},{12,16},{16,4},{20,8},{24,12},{28,0},{1,21},{... | collective-permute-start | bytes 36872 | tf_op jit(solution)/shard_map/ppermute | solution.py:542
  70.1 9.0 %collective-permute-start.17 = (bf16[16,384]{1,0:T(8,128)(2,1)S(1)}, bf16[16,384]{1,0:T(8,128)(2,1)S(1)}, u32[]{:S(2)}, u32[]{:S(2)}) collective-permute-start(bf16[16,384]{1,0:T(8,128)(2,1)S(1)} %get-tuple-element.97), channel_id=1, source_target_pairs={{0,28},{4,16},{8,20},{12,24},{16,12},{20,0},{24,4},{28,8},{1,29},{... | collective-permute-start | bytes 36872 | tf_op jit(solution)/shard_map/ppermute | solution.py:542
  77.0 4.3 %copy-start.21 = (f32[7,7,384]{2,1,0:T(8,128)S(1)}, f32[7,7,384]{2,1,0:T(8,128)}, u32[]{:S(2)}) copy-start(f32[7,7,384]{2,1,0:T(8,128)} %taps.1) | copy-start | bytes 225796
  79.2 9.9 %collective-permute-start.12 = (bf16[4,96,384]{2,1,0:T(8,128)(2,1)S(1)}, bf16[4,96,384]{2,1,0:T(8,128)(2,1)S(1)}, u32[]{:S(2)}, u32[]{:S(2)}) collective-permute-start(bf16[4,96,384]{2,1,0:T(8,128)(2,1)S(1)} %get-tuple-element.116), channel_id=1, source_target_pairs={{0,16},{16,0},{1,17},{17,1},{2,18},{18,2},{3,19},{19,3},{4,20},{20... | collective-permute-start | bytes 884744 | tf_op jit(solution)/shard_map/ppermute | solution.py:374
  80.0 12.3 %collective-permute-start.21 = (bf16[4,96,384]{2,1,0:T(8,128)(2,1)S(1)}, bf16[4,96,384]{2,1,0:T(8,128)(2,1)S(1)}, u32[]{:S(2)}, u32[]{:S(2)}) collective-permute-start(bf16[4,96,384]{2,1,0:T(8,128)(2,1)S(1)} %get-tuple-element.128), channel_id=1, source_target_pairs={{0,16},{16,0},{1,17},{17,1},{2,18},{18,2},{3,19},{19,3},{4,20},{20... | collective-permute-start | bytes 884744 | tf_op jit(solution)/shard_map/ppermute | solution.py:374
  88.7 12.4 %copy-start.17 = (bf16[384,768]{1,0:T(8,128)(2,1)S(1)}, bf16[384,768]{1,0:T(8,128)(2,1)}, u32[]{:S(2)}) copy-start(bf16[384,768]{1,0:T(8,128)(2,1)} %up_ref.1) | copy-start | bytes 1769476
  88.7 12.4 %copy-start.18 = (bf16[768,384]{1,0:T(8,128)(2,1)S(1)}, bf16[768,384]{1,0:T(8,128)(2,1)}, u32[]{:S(2)}) copy-start(bf16[768,384]{1,0:T(8,128)(2,1)} %down_ref.1) | copy-start | bytes 1769476
  88.8 12.4 %copy-start.20 = (bf16[384,128]{1,0:T(8,128)(2,1)S(1)}, bf16[384,128]{1,0:T(8,128)(2,1)}, u32[]{:S(2)}) copy-start(bf16[384,128]{1,0:T(8,128)(2,1)} %head_ref.1) | copy-start | bytes 294916
  92.3 7.1 %collective-permute-start.22 = (bf16[96,384]{1,0:T(8,128)(2,1)S(1)}, bf16[96,384]{1,0:T(8,128)(2,1)S(1)}, u32[]{:S(2)}, u32[]{:S(2)}) collective-permute-start(bf16[96,384]{1,0:T(8,128)(2,1)S(1)} %get-tuple-element.132), channel_id=1, source_target_pairs={{0,4},{4,8},{8,12},{12,0},{1,5},{5,9},{9,13},{13,1},{2,6},{6,10},{... | collective-permute-start | bytes 221192 | tf_op jit(solution)/shard_map/ppermute | solution.py:374
  92.4 12.1 %collective-permute-start.23 = (bf16[96,384]{1,0:T(8,128)(2,1)S(1)}, bf16[96,384]{1,0:T(8,128)(2,1)S(1)}, u32[]{:S(2)}, u32[]{:S(2)}) collective-permute-start(bf16[96,384]{1,0:T(8,128)(2,1)S(1)} %get-tuple-element.133), channel_id=1, source_target_pairs={{0,8},{4,12},{8,0},{12,4},{1,9},{5,13},{9,1},{13,5},{2,10},{6,14},... | collective-permute-start | bytes 221192 | tf_op jit(solution)/shard_map/ppermute | solution.py:374
  93.6 11.0 %collective-permute-start.24 = (bf16[96,384]{1,0:T(8,128)(2,1)S(1)}, bf16[96,384]{1,0:T(8,128)(2,1)S(1)}, u32[]{:S(2)}, u32[]{:S(2)}) collective-permute-start(bf16[96,384]{1,0:T(8,128)(2,1)S(1)} %get-tuple-element.134), channel_id=1, source_target_pairs={{0,12},{4,0},{8,4},{12,8},{1,13},{5,1},{9,5},{13,9},{2,14},{6,2},{... | collective-permute-start | bytes 221192 | tf_op jit(solution)/shard_map/ppermute | solution.py:374
  96.2 8.3 %collective-permute-start.18 = (bf16[96,384]{1,0:T(8,128)(2,1)S(1)}, bf16[96,384]{1,0:T(8,128)(2,1)S(1)}, u32[]{:S(2)}, u32[]{:S(2)}) collective-permute-start(bf16[96,384]{1,0:T(8,128)(2,1)S(1)} %get-tuple-element.125), channel_id=1, source_target_pairs={{0,4},{4,8},{8,12},{12,0},{1,5},{5,9},{9,13},{13,1},{2,6},{6,10},{... | collective-permute-start | bytes 221192 | tf_op jit(solution)/shard_map/ppermute | solution.py:374
  96.8 8.2 %collective-permute-start.19 = (bf16[96,384]{1,0:T(8,128)(2,1)S(1)}, bf16[96,384]{1,0:T(8,128)(2,1)S(1)}, u32[]{:S(2)}, u32[]{:S(2)}) collective-permute-start(bf16[96,384]{1,0:T(8,128)(2,1)S(1)} %get-tuple-element.126), channel_id=1, source_target_pairs={{0,8},{4,12},{8,0},{12,4},{1,9},{5,13},{9,1},{13,5},{2,10},{6,14},... | collective-permute-start | bytes 221192 | tf_op jit(solution)/shard_map/ppermute | solution.py:374
  99.4 5.6 %collective-permute-start.20 = (bf16[96,384]{1,0:T(8,128)(2,1)S(1)}, bf16[96,384]{1,0:T(8,128)(2,1)S(1)}, u32[]{:S(2)}, u32[]{:S(2)}) collective-permute-start(bf16[96,384]{1,0:T(8,128)(2,1)S(1)} %get-tuple-element.127), channel_id=1, source_target_pairs={{0,12},{4,0},{8,4},{12,8},{1,13},{5,1},{9,5},{13,9},{2,14},{6,2},{... | collective-permute-start | bytes 221192 | tf_op jit(solution)/shard_map/ppermute | solution.py:374
  105.1 6.1 %collective-permute-start.26 = (bf16[96,768]{1,0:T(8,128)(2,1)S(1)}, bf16[96,768]{1,0:T(8,128)(2,1)S(1)}, u32[]{:S(2)}, u32[]{:S(2)}) collective-permute-start(bf16[96,768]{1,0:T(8,128)(2,1)S(1)} %close.1.own_ref), channel_id=1, source_target_pairs={{0,2},{1,3},{2,0},{3,1},{4,6},{5,7},{6,4},{7,5},{8,10},{9,11},{10,... | collective-permute-start | bytes 442376 | tf_op jit(solution)/shard_map/ppermute | solution.py:369
  108.1 3.1 %collective-permute-start.25 = (bf16[96,768]{1,0:T(8,128)(2,1)S(1)}, bf16[96,768]{1,0:T(8,128)(2,1)S(1)}, u32[]{:S(2)}, u32[]{:S(2)}) collective-permute-start(bf16[96,768]{1,0:T(8,128)(2,1)S(1)} %close.1.own_ref), channel_id=1, source_target_pairs={{0,1},{1,0},{2,3},{3,2},{4,5},{5,4},{6,7},{7,6},{8,9},{9,8},{10,11... | collective-permute-start | bytes 442376 | tf_op jit(solution)/shard_map/ppermute | solution.py:369
  111.2 1.4 %collective-permute-start.27 = (bf16[96,768]{1,0:T(8,128)(2,1)S(1)}, bf16[96,768]{1,0:T(8,128)(2,1)S(1)}, u32[]{:S(2)}, u32[]{:S(2)}) collective-permute-start(bf16[96,768]{1,0:T(8,128)(2,1)S(1)} %collective-permute-done.26.two_ref), channel_id=1, source_target_pairs={{0,1},{1,0},{2,3},{3,2},{4,5},{5,4},{6,7},{7,6},{8,9},{9,8},{10,11... | collective-permute-start | bytes 442376 | tf_op jit(solution)/shard_map/ppermute | solution.py:369
  (9 other events, 16.6 us)

commit v4 on v3

--- a/solution.py
+++ b/solution.py
@@ -42,7 +42,7 @@
         out_specs=specs[0] if single else tuple(specs),
         scratch_shapes=list(scratch),
         compiler_params=pltpu.CompilerParams(vmem_limit_bytes=limit * MIB),
-        cost_estimate=pl.CostEstimate(flops=flops, bytes_accessed=nbytes, transcendentals=0),
+        cost_estimate=pl.CostEstimate(flops=1000, bytes_accessed=1000, transcendentals=0),
         name=name,
     )
 
@@ -78,10 +78,17 @@
 
 
 def project_kernel(
-    cap, padded, src_ref, arr_ref, wqkv_t_ref, normed_ref, enc_ref, u_ref, len_ref, v_ref,
-    place_ref,
+    cap, padded, src_ref, arr_ref, wqkv_hbm, normed_ref, enc_ref, u_ref, len_ref, v_ref,
+    place_ref, wqkv_t_ref, sems,
 ):
     rows, width = normed_ref.shape
+    copies = []
+    for t in range(3):
+        cut = slice(t * width, (t + 1) * width)
+        copies.append(
+            pltpu.make_async_copy(wqkv_hbm.at[cut], wqkv_t_ref.at[cut], sems.at[t])
+        )
+        copies[-1].start()
     heads = len_ref.shape[0] // 2
     size = width // heads
     slots = arr_ref.shape[0]
@@ -98,6 +105,7 @@
     normed = (centred * lax.rsqrt(spread + norm_eps)).astype(bf16)
     normed_ref[...] = normed
     for t in range(2):
+        copies[t].wait()
         raw = mm(wqkv_t_ref[t * width : (t + 1) * width], normed, NT)
         for h in range(heads):
             part = raw[h * size : (h + 1) * size]
@@ -105,16 +113,17 @@
             at = t * width + h * size
             u_ref[at : at + size] = part * inv
             len_ref[t * heads + h : t * heads + h + 1] = inv
+    copies[2].wait()
     v_ref[...] = mm(wqkv_t_ref[2 * width : 3 * width], normed, NT).astype(bf16)
 
 
 def encode_kernel(
     split, win_ref, scale_ref, place_ref, enc_ref, u_ref, len_ref, v_ref, ga_ref, wout_ref,
-    wdec_ref, out_ref, e_ref, *refs,
+    wdec_ref, normed_ref, out_ref, *refs,
 ):
-    left_refs = refs[:-3]
+    peer_refs = refs[:-3]
     p_ref, att_ref, left_ref = refs[-3:]
-    rows, width = e_ref.shape
+    rows, width = enc_ref.shape
     heads = p_ref.shape[0]
     size = width // heads
     slots = out_ref.shape[0]
@@ -130,7 +139,6 @@
         p_ref[h] = weights
         att_ref[lo:hi] = mm(v_ref[lo:hi], weights).astype(bf16)
     attended = jnp.transpose(att_ref[...])
-    e_ref[...] = attended
     enc_out = (enc_ref[...].astype(f32) + mm(attended, wout_ref[...])).astype(bf16)
     dec = mm(enc_out, wdec_ref[...]).astype(bf16)
     places = lax.broadcasted_iota(jnp.int32, (slots, rows), 0).astype(f32)
@@ -154,10 +162,39 @@
         grad_k = (grad_k - k * jnp.sum(k * grad_k, axis=0, keepdims=True)) * len_ref[
             heads + h : heads + h + 1
         ]
-        emit(split, left_ref, lo, grad_q.astype(bf16))
-        emit(split, left_ref, width + lo, grad_k.astype(bf16))
-        emit(split, left_ref, 2 * width + lo, grad_v.astype(bf16))
-    deal(split, left_ref, left_refs)
+        emit_wide(split, left_ref, lo, grad_q.astype(bf16))
+        emit_wide(split, left_ref, width + lo, grad_k.astype(bf16))
+        emit_wide(split, left_ref, 2 * width + lo, grad_v.astype(bf16))
+    if split is None:
+        peer_refs[0][...] = left_ref[...]
+        peer_refs[1][...] = attended
+        return
+    me = lax.axis_index("replica")
+    deep = left_ref.shape[1]
+    for n, ref in enumerate(peer_refs):
+        ref[0:deep] = left_ref[me ^ n]
+        if n == 2:
+            ref[deep : 2 * deep] = left_ref[me ^ 3]
+            ref[2 * deep : 2 * deep + rows] = attended
+        else:
+            ref[deep : deep + rows] = attended
+            ref[deep + rows : deep + 2 * rows] = normed_ref[...]
+
+
+def emit_wide(split, out_ref, start, block):
+    if split is None:
+        out_ref[start : start + block.shape[0]] = block
+        return
+    unit = 32
+    rows = block.shape[1]
+    per_shard, per_part = split[0] // unit, split[1] // unit
+    stack = out_ref.shape[1] // split[1]
+    for j in range(block.shape[0] // unit):
+        shard, rest = divmod(start // unit + j, per_shard)
+        part, place = divmod(rest, per_part)
+        at = (shard % stack) * split[1] + place * unit
+        lane = (shard // stack) * rows
+        out_ref[part, at : at + unit, lane : lane + rows] = block[j * unit : (j + 1) * unit]
 
 
 def deal(split, left_ref, left_refs):
@@ -178,31 +215,46 @@
     for j in range(block.shape[0] // unit):
         shard, rest = divmod(start // unit + j, per_shard)
         part, place = divmod(rest, per_part)
-        out_ref[part, shard, place * unit : (place + 1) * unit] = block[
-            j * unit : (j + 1) * unit
-        ]
-
-
-def term_kernel(columns, *refs):
-    lefts, cots, normed, attended = refs[0:4], refs[4:8], refs[8:12], refs[12:16]
-    keep_ref, send_ref = refs[16:]
-    qkv, part, rows = lefts[0].shape
-    shards = qkv + cots[0].shape[0]
-    half = shards // 2
+        at = shard * split[1] + place * unit
+        out_ref[part, at : at + unit] = block[j * unit : (j + 1) * unit]
+
+
+def term_kernel(columns, rows, *refs):
+    own, near, far, hop, far_normed, hop_normed = refs[0:6]
+    cots = refs[6:10]
+    keep_ref, send_ref = refs[10:]
+    half, part = keep_ref.shape[:2]
+    held, count = cots[0].shape[0] // part, cots[0].shape[1]
+    deep = own.shape[0] - 2 * rows
+    stack = deep // part
     cut = slice(*columns)
     width = columns[1] - columns[0]
-
-    def block(left, lo, hi, right):
+    att = slice(deep, deep + rows)
+    nor = slice(deep + rows, deep + 2 * rows)
+    far_att = slice(2 * deep, 2 * deep + rows)
+    attended = [own[att, cut], near[att, cut], far[far_att, cut], hop[far_att, cut]]
+    normed = [own[nor, cut], near[nor, cut], far_normed[:, cut], hop_normed[:, cut]]
+
+    def left(ref, start, lo, hi):
+        blocks = [
+            ref[start : start + deep, j * count : (j + 1) * count]
+            for j in range(lo // stack, hi // stack)
+        ]
+        return jnp.concatenate(blocks, axis=0) if len(blocks) > 1 else blocks[0]
+
+    def block(lefts, right):
         acc = None
-        for ref, e in zip(left, right):
-            step = mm(ref[lo:hi].reshape((hi - lo) * part, rows), e[:, cut])
+        for value, e in zip(lefts, right):
+            step = mm(value, e)
             acc = step if acc is None else acc + step
-        return acc.reshape(hi - lo, part, width)
-
-    first = [(0, block(lefts, 0, half, normed))]
+        return acc.reshape(acc.shape[0] // part, part, width)
+
+    peers = ((own, 0), (near, 0), (far, 0), (hop, deep))
+    qkv = 2 * half - held
+    first = [(0, block([left(ref, start, 0, half) for ref, start in peers], normed))]
     second = [
-        (0, block(lefts, half, qkv, normed)),
-        (qkv - half, block(cots, 0, shards - qkv, attended)),
+        (0, block([left(ref, start, half, qkv) for ref, start in peers], normed)),
+        (qkv - half, block([ref[...] for ref in cots], attended)),
     ]
     spans = (first, second)
     for mine in range(2):
@@ -426,10 +478,14 @@
     cotangent = enc_cot.reshape(rows, width)
     split = (shard_rows, part_rows) if fast else None
     pieces = replicas if fast else 1
-    cot_part = (width // shard_rows, part_rows, rows) if fast else (width, rows)
-    left_part = (3 * width // shard_rows, part_rows, rows) if fast else (3 * width, rows)
+    cot_part = (width * part_rows // shard_rows, rows) if fast else (width, rows)
+    deep = 3 * width * part_rows // shard_rows * rows // width if fast else 3 * width
     cot_whole = (replicas,) + cot_part if fast else cot_part
-    left_whole = (replicas,) + left_part if fast else left_part
+    left_whole = (replicas, deep, width) if fast else (3 * width, rows)
+    if fast:
+        peer_shapes = [(deep + 2 * rows, width)] * 2 + [(2 * deep + rows, width)]
+    else:
+        peer_shapes = [(3 * width, rows), (rows, width)]
     grad_att, w_qkv_t, *cots = call(
         functools.partial(prep_kernel, split),
         "prep",
@@ -443,7 +499,6 @@
     )(cotangent, w_out, w_qkv)
     if fast:
         cots = [cots[0]] + [flip(cots[k], "replica", k) for k in range(1, 4)]
-        arrived = tie(arrived, cots)
 
     normed, enc_in, units, lengths, values, places = call(
         functools.partial(project_kernel, cap, padded),
@@ -456,20 +511,21 @@
             sds((width, rows), bf16),
             sds((1, rows), f32),
         ],
-        [vmem()] * 3,
+        [vmem(), vmem(), pl.BlockSpec(memory_space=pltpu.HBM)],
+        scratch=[pltpu.VMEM((3 * width, width), bf16), pltpu.SemaphoreType.DMA((3,))],
         flops=2 * rows * width * width * 4,
         nbytes=8 * MIB,
-        limit=10,
+        limit=14,
     )(enc_src.reshape(1, rows), arrived, w_qkv_t)
     if fast:
         normed_y = flip(normed, "replica", 2)
-
-    outbound, attended, *lefts = call(
+        lengths = tie(lengths, cots)
+
+    outbound, *peers = call(
         functools.partial(encode_kernel, split),
         "encode",
-        [sds((slots, dec_width), bf16), sds((rows, width), bf16)]
-        + [sds(left_part, bf16)] * pieces,
-        [vmem(), smem()] + [vmem()] * 8,
+        [sds((slots, dec_width), bf16)] + [sds(shape, bf16) for shape in peer_shapes],
+        [vmem(), smem()] + [vmem()] * 9,
         scratch=[
             pltpu.VMEM((heads, rows, rows), bf16),
             pltpu.VMEM((width, rows), bf16),
@@ -480,22 +536,19 @@
         limit=14,
     )(
         window_id.reshape(1, rows), head_scale, places, enc_in, units, lengths, values, grad_att,
-        w_out, w_dec_in,
+        w_out, w_dec_in, normed,
     )
     returned = lax.all_to_all(
         outbound.reshape(group, padded, dec_width), ("eta", "phi"), split_axis=0, concat_axis=0,
         tiled=True,
     )
     if fast:
-        lefts = [lefts[0]] + [flip(lefts[k], "replica", k) for k in range(1, 4)]
-        attended_y = flip(attended, "replica", 2)
-        normed_y = tie(normed_y, attended)
-        right = [normed, flip(normed, "replica", 1), normed_y, flip(normed_y, "replica", 1)]
-        right += [
-            attended, flip(attended, "replica", 1), attended_y, flip(attended_y, "replica", 1),
-        ]
+        own, near, far = peers[0], flip(peers[1], "replica", 1), flip(peers[2], "replica", 2)
+        normed_y = tie(normed_y, outbound)
+        normed_hop = flip(normed_y, "replica", 1)
+        returned = tie(returned, near, normed_hop)
     else:
-        grad_total = summed_slow(lefts[0], cots[0], normed, attended)
+        grad_total = summed_slow(peers[0], cots[0], normed, peers[1])
 
     span = conv_kernel.shape[0]
     rim = span // 2
@@ -566,20 +619,22 @@
             flat(bottom), flat(low[far:]), flat(high[far:]),
         )
     if fast:
-        lefts, cots, right = tie((lefts, cots, right), filled)
+        far = tie(far, left_halo, right_halo, rims[0])
+        peers = [own, near, far, flip(far, "replica", 1), normed_y, normed_hop]
+        peers, cots = tie((peers, cots), left_halo, right_halo, rims)
         chunk = width // 2
         half = group // 2
         kept, sent = [], []
         for c in range(2):
             keep, send = call(
-                functools.partial(term_kernel, (c * chunk, (c + 1) * chunk)),
+                functools.partial(term_kernel, (c * chunk, (c + 1) * chunk), rows),
                 "terms%d" % c,
                 [sds((half, part_rows, chunk), f32), sds((half, part_rows, chunk), bf16)],
-                [vmem()] * 16,
+                [vmem()] * 10,
                 flops=2 * out_rows * chunk * rows,
                 nbytes=8 * MIB,
                 limit=10,
-            )(*lefts, *cots, *right)
+            )(*peers, *cots)
             kept.append(keep)
             sent.append(turn(send, "eta", 1))
         left, right_halo, rims = tie((left_halo, right_halo, rims), kept)

time: 114 us -> 137 us (1.20)
  waiting for transfers between devices: 30.9 us -> 49.1 us
  local copies, waits for them, and re-layouts: 9.38 us -> 14.7 us
  starting transfers between devices: 40.2 us -> 37.3 us
  Pallas kernels: 32.3 us -> 34.2 us
    ppermute x15 -> x11, waiting for transfers between devices: 22.4 us -> 34.5 us  [flip(): lax.ppermute(value, axis, [(i, i ^ bit) for i in range(lax.axis_size(axis...]
    unnamed x54, local copies, waits for them, and re-layouts: 9.38 us -> 14.7 us
    all_to_all x1, waiting for transfers between devices: 2.86 us -> 7.28 us  [body(): lax.all_to_all(outgoing.reshape(group, padded, width), ('eta', 'phi'), sp...]
    ppermute x15 -> x11, starting transfers between devices: 9.3 us -> 5.48 us  [flip(): lax.ppermute(value, axis, [(i, i ^ bit) for i in range(lax.axis_size(axis...]
    ppermute x3, waiting for transfers between devices: 0.01 us -> 2.95 us  [shifted(): return lax.ppermute(value, plane, pairs)]
    ppermute x10, starting transfers between devices: 13.6 us -> 15.9 us  [turn(): lax.ppermute(value, axis, [(i, (i + k) % count) for i in range(count)])]
    pallas_call x1, Pallas kernels: 2.03 us -> 3.81 us  [body(): call(functools.partial(project_kernel, cap, padded), 'project', [sds((row...]
  transfers between devices with their start and end apart: 30 -> 26, of which waited for: 13 -> 9; matrix products, arithmetic and copies ran while one was open for 0% -> 0% of each run, Pallas kernels for 24% -> 14%
where the time goes in v4:
time: 137 us; the launch traced here: 136 us
  waiting for transfers between devices  49.1 us (36%)
  starting transfers between devices  37.3 us (27%)
  Pallas kernels  34.2 us (25%)
  local copies, waits for them, and re-layouts  14.7 us (11%)
    ppermute x11, waiting for transfers between devices, flip(): lax.ppermute(value, axis, [(i, i ^ bit) for i in range(lax.axis_size(axis...  34.5 us
    ppermute x10, starting transfers between devices, turn(): lax.ppermute(value, axis, [(i, (i + k) % count) for i in range(count)])  15.9 us
    unnamed x54, local copies, waits for them, and re-layouts  14.7 us
    pallas_call x1, Pallas kernels, body(): call(functools.partial(encode_kernel, split), 'encode', [sds((slots, dec_...  9.67 us
    pallas_call x1, Pallas kernels, body(): call(functools.partial(mix_folded if folded else mix_open, (eta_cells, ph...  7.45 us
    all_to_all x1, waiting for transfers between devices, body(): lax.all_to_all(outgoing.reshape(group, padded, width), ('eta', 'phi'), sp...  7.28 us
    all_to_all x1, starting transfers between devices, body(): lax.all_to_all(outgoing.reshape(group, padded, width), ('eta', 'phi'), sp...  7.25 us
    ppermute x11, starting transfers between devices, flip(): lax.ppermute(value, axis, [(i, i ^ bit) for i in range(lax.axis_size(axis...  5.48 us
  transfers between devices with their start and end apart: 26, of which 9 were waited for; matrix products, arithmetic and copies ran while one was open for 0% of the time, Pallas kernels for 14%

profile of v4, /device:TPU:0, one launch (start us, length us, event | category | flops | bytes accessed | tf_op | source)
XLA Modules:
  0.0 136.1 jit_solution(7920708236042221477)
XLA Ops:
  0.6 1.4 %copy-done.4 = bf16[1,32,32,768]{3,2,1,0:T(8,128)(2,1)S(1)} copy-done((bf16[1,32,32,768]{3,2,1,0:T(8,128)(2,1)S(1)}, bf16[1,32,32,768]{3,2,1,0:T(8,128)(2,1)}, u32[]{:S(2)}) %copy-start.4) | copy-done | bytes 1572888
  2.0 0.7 copy-done.20
  2.7 1.7 %pick.1 = bf16[320,768]{1,0:T(8,128)(2,1)} custom-call(s32[8,35]{1,0:T(8,128)S(1)} %bitcast.16, bf16[1024,768]{1,0:T(8,128)(2,1)S(1)} %bitcast.12), custom_call_target="tpu_custom_call" | custom-call | flops 1000 | bytes 1000 | tf_op jit(solution)/shard_map/pick/pallas_call | solution.py:463
  4.4 7.3 %all-to-all-start = ((bf16[8,40,768]{2,1,0:T(8,128)(2,1)}), bf16[8,40,768]{2,1,0:T(8,128)(2,1)S(1)}, u32[]{:S(2)}, u32[]{:S(2)}) async-start(bf16[8,40,768]{2,1,0:T(8,128)(2,1)} %bitcast.4), calls=%async_computation | async-start | bytes 983040 | tf_op jit(solution)/shard_map/all_to_all | solution.py:473
  11.7 2.0 %copy-done.1 = bf16[768,2304]{1,0:T(8,128)(2,1)S(1)} copy-done((bf16[768,2304]{1,0:T(8,128)(2,1)S(1)}, bf16[768,2304]{1,0:T(8,128)(2,1)}, u32[]{:S(2)}) %copy-start.1) | copy-done | bytes 3538968
  13.7 1.1 prep.1
  14.8 1.7 %copy-done.2 = bf16[2304,768]{1,0:T(8,128)(2,1)} copy-done((bf16[2304,768]{1,0:T(8,128)(2,1)}, bf16[2304,768]{1,0:T(8,128)(2,1)S(1)}, u32[]{:S(2)}) %copy-start.2) | copy-done | bytes 3538968
  16.5 0.6 copy-done.9
  17.2 1.5 %collective-permute-start.1 = (bf16[192,256]{1,0:T(8,128)(2,1)S(1)}, bf16[192,256]{1,0:T(8,128)(2,1)S(1)}, u32[]{:S(2)}, u32[]{:S(2)}) collective-permute-start(bf16[192,256]{1,0:T(8,128)(2,1)S(1)} %get-tuple-element.74), channel_id=1, source_target_pairs={{0,2},{1,3},{2,0},{3,1},{4,6},{5,7},{6,4},{7,5},{8,10},{9,11},{10,... | collective-permute-start | bytes 294920 | tf_op jit(solution)/shard_map/ppermute | solution.py:421
  19.1 7.3 %all-to-all-done = bf16[8,40,768]{2,1,0:T(8,128)(2,1)S(1)} async-done(((bf16[8,40,768]{2,1,0:T(8,128)(2,1)}), bf16[8,40,768]{2,1,0:T(8,128)(2,1)S(1)}, u32[]{:S(2)}, u32[]{:S(2)}) %all-to-all-start) | async-done | bytes 491552 | tf_op jit(solution)/shard_map/all_to_all | solution.py:473
  26.3 2.0 %copy-done.3 = bf16[2304,768]{1,0:T(8,128)(2,1)S(1)} copy-done((bf16[2304,768]{1,0:T(8,128)(2,1)S(1)}, bf16[2304,768]{1,0:T(8,128)(2,1)}, u32[]{:S(2)}) %copy-start.3) | copy-done | bytes 3538968
  28.3 3.8 %project.1 = (bf16[256,768]{1,0:T(8,128)(2,1)}, bf16[256,768]{1,0:T(8,128)(2,1)S(1)}, f32[1536,256]{1,0:T(8,128)S(1)}, f32[24,256]{1,0:T(8,128)S(1)}, bf16[768,2...) custom-call(s32[1,256]{1,0:T(1,128)S(1)} %bitcast.18, bf16[320,768]{1,0:T(8,128)(2,1)S(1)} %bitcast.11, ...), custom_call_target="tpu_custom_call" | custom-call | flops 1000 | bytes 1000 | tf_op jit(solution)/shard_map/project/pallas_call | solution.py:503
  32.2 0.6 copy-done.11
  32.8 0.6 copy-done.13
  33.5 0.6 copy-done.15
  34.1 9.7 %encode.1 = (bf16[320,384]{1,0:T(8,128)(2,1)S(1)}, bf16[704,768]{1,0:T(8,128)(2,1)S(1)}, bf16[704,768]{1,0:T(8,128)(2,1)}, bf16[640,768]{1,0:T(8,128)(2,1)}) custom-call(s32[1,256]{1,0:T(1,128)S(1)} %bitcast.19, f32[12]{0:T(128)S(1)} %copy-done.25, f32[1,256]{1,0:T(1,128)S(1)} %get-tuple-element.68.place_ref, ...), custom_call_target="tpu_custom_call" | custom-call | flops 1000 | bytes 1000 | tf_op jit(solution)/shard_map/encode/pallas_call | solution.py:524
  43.8 0.7 copy-done.17
  44.5 1.5 %collective-permute-start.4 = (bf16[640,768]{1,0:T(8,128)(2,1)}, bf16[640,768]{1,0:T(8,128)(2,1)S(1)}, u32[]{:S(2)}, u32[]{:S(2)}) collective-permute-start(bf16[640,768]{1,0:T(8,128)(2,1)} %get-tuple-element.82), channel_id=1, source_target_pairs={{0,2},{1,3},{2,0},{3,1},{4,6},{5,7},{6,4},{7,5},{8,10},{9,11},{10,... | collective-permute-start | bytes 2949128 | tf_op jit(solution)/shard_map/ppermute | solution.py:421
  46.0 0.5 collective-permute-start.5
  46.5 3.4 %all-to-all-start.1 = ((bf16[8,40,384]{2,1,0:T(8,128)(2,1)}), bf16[8,40,384]{2,1,0:T(8,128)(2,1)S(1)}, u32[]{:S(2)}, u32[]{:S(2)}) async-start(bf16[8,40,384]{2,1,0:T(8,128)(2,1)} %bitcast.15), calls=%async_computation.1 | async-start | bytes 491520 | tf_op jit(solution)/shard_map/all_to_all | solution.py:541
  49.9 27.5 %collective-permute-done.5.refs_4_ = bf16[256,768]{1,0:T(8,128)(2,1)} collective-permute-done((bf16[256,768]{1,0:T(8,128)(2,1)}, bf16[256,768]{1,0:T(8,128)(2,1)}, u32[]{:S(2)}, u32[]{:S(2)}) %collective-permute-start.5) | collective-permute-done | bytes 393248 | tf_op jit(solution)/shard_map/ppermute | solution.py:421
  77.4 2.0 %collective-permute-done.6.refs_5_ = bf16[256,768]{1,0:T(8,128)(2,1)} collective-permute-done((bf16[256,768]{1,0:T(8,128)(2,1)}, bf16[256,768]{1,0:T(8,128)(2,1)}, u32[]{:S(2)}, u32[]{:S(2)}) %collective-permute-start.6) | collective-permute-done | bytes 393248 | tf_op jit(solution)/shard_map/ppermute | solution.py:421
  79.5 1.5 %fill.1 = (bf16[1024,384]{1,0:T(8,128)(2,1)S(1)}, bf16[96,384]{1,0:T(8,128)(2,1)S(1)}, bf16[96,384]{1,0:T(8,128)(2,1)S(1)}, bf16[96,384]{1,0:T(8,128)(2,1)S(1)},...) custom-call(s32[8,35]{1,0:T(8,128)S(1)} %bitcast.17, f32[2,1408]{1,0:T(2,128)S(1)} %copy-done.22, ...), custom_call_target="tpu_custom_call" | custom-call | flops 1000 | bytes 1000 | tf_op jit(solution)/shard_map/fill/pallas_call | solution.py:573
  81.0 3.8 %collective-permute-start.8 = (bf16[96,384]{1,0:T(8,128)(2,1)S(1)}, bf16[96,384]{1,0:T(8,128)(2,1)S(1)}, u32[]{:S(2)}, u32[]{:S(2)}) collective-permute-start(bf16[96,384]{1,0:T(8,128)(2,1)S(1)} %get-tuple-element.87), channel_id=1, source_target_pairs={{0,12},{4,0},{8,4},{12,8},{1,13},{5,1},{9,5},{13,9},{2,14},{6,2},{... | collective-permute-start | bytes 221192 | tf_op jit(solution)/shard_map/ppermute | solution.py:426
  84.8 0.6 collective-permute-start.9
  85.4 2.5 %collective-permute-done.7.left = bf16[96,384]{1,0:T(8,128)(2,1)S(1)} collective-permute-done((bf16[96,384]{1,0:T(8,128)(2,1)S(1)}, bf16[96,384]{1,0:T(8,128)(2,1)S(1)}, u32[]{:S(2)}, u32[]{:S(2)}) %collective-permute-start.7) | collective-permute-done | bytes 73760 | tf_op jit(solution)/shard_map/ppermute | solution.py:426
  87.9 1.3 collective-permute-done.9.a
  89.2 4.7 %collective-permute-start.12 = (bf16[16,384]{1,0:T(8,128)(2,1)S(1)}, bf16[16,384]{1,0:T(8,128)(2,1)S(1)}, u32[]{:S(2)}, u32[]{:S(2)}) collective-permute-start(bf16[16,384]{1,0:T(8,128)(2,1)S(1)} %get-tuple-element.91), channel_id=1, source_target_pairs={{0,28},{4,16},{8,20},{12,24},{16,12},{20,0},{24,4},{28,8},{1,29},{... | collective-permute-start | bytes 36872 | tf_op jit(solution)/shard_map/ppermute | solution.py:595
  93.9 1.7 %collective-permute-done.11.b = bf16[16,384]{1,0:T(8,128)(2,1)S(1)} collective-permute-done((bf16[16,384]{1,0:T(8,128)(2,1)S(1)}, bf16[16,384]{1,0:T(8,128)(2,1)S(1)}, u32[]{:S(2)}, u32[]{:S(2)}) %collective-permute-start.11) | collective-permute-done | bytes 12320 | tf_op jit(solution)/shard_map/ppermute | solution.py:595
  95.6 0.9 copy-done.10
  96.5 0.9 copy-done.12
  97.4 0.9 copy-done.14
  98.3 0.9 copy-done.16
  99.2 2.2 %terms0.1 = (f32[4,96,384]{2,1,0:T(8,128)S(1)}, bf16[4,96,384]{2,1,0:T(8,128)(2,1)S(1)}) custom-call(bf16[704,768]{1,0:T(8,128)(2,1)S(1)} %get-tuple-element.92.refs_0_, bf16[704,768]{1,0:T(8,128)(2,1)S(1)} %collective-permute-done.3.refs_1_, bf16[640,768]{1,0:T(8,128)(2,1)S(1)} %collective-permute-done.4.refs_2_, ...), custom_call_target="tpu_custom_call" | custom-call | flops 1000 | bytes 1000 | tf_op jit(solution)/shard_map/terms0/pallas_call | solution.py:629
  101.3 0.6 collective-permute-start.13
  102.0 2.2 %terms1.1 = (f32[4,96,384]{2,1,0:T(8,128)S(1)}, bf16[4,96,384]{2,1,0:T(8,128)(2,1)S(1)}) custom-call(bf16[704,768]{1,0:T(8,128)(2,1)S(1)} %get-tuple-element.92.refs_0_, bf16[704,768]{1,0:T(8,128)(2,1)S(1)} %collective-permute-done.3.refs_1_, bf16[640,768]{1,0:T(8,128)(2,1)S(1)} %collective-permute-done.4.refs_2_, ...), custom_call_target="tpu_custom_call" | custom-call | flops 1000 | bytes 1000 | tf_op jit(solution)/shard_map/terms1/pallas_call | solution.py:629
  104.1 1.5 %collective-permute-start.17 = (bf16[4,96,384]{2,1,0:T(8,128)(2,1)S(1)}, bf16[4,96,384]{2,1,0:T(8,128)(2,1)S(1)}, u32[]{:S(2)}, u32[]{:S(2)}) collective-permute-start(bf16[4,96,384]{2,1,0:T(8,128)(2,1)S(1)} %get-tuple-element.116), channel_id=1, source_target_pairs={{0,16},{16,0},{1,17},{17,1},{2,18},{18,2},{3,19},{19,3},{4,20},{20... | collective-permute-start | bytes 884744 | tf_op jit(solution)/shard_map/ppermute | solution.py:426
  105.7 7.5 %mix.1.normed_ref = bf16[1024,384]{1,0:T(8,128)(2,1)S(1)} custom-call(bf16[1024,384]{1,0:T(8,128)(2,1)S(1)} %get-tuple-element.104.grid.grid_ref, bf16[96,384]{1,0:T(8,128)(2,1)S(1)} %collective-permute-done.7.left, bf16[96,384]{1,0:T(8,128)(2,1)S(1)} %collective-permute-done.8.right, bf16[96,384]{1,0:T(8,128)(2,1)S(1)} %collective-permute-done.9.a, ...), custom_call_target="tpu_custom_call" | custom-call | flops 1000 | bytes 1000 | tf_op jit(solution)/shard_map/mix/pallas_call | solution.py:643
  113.3 4.4 %collective-permute-start.15 = (bf16[96,384]{1,0:T(8,128)(2,1)S(1)}, bf16[96,384]{1,0:T(8,128)(2,1)S(1)}, u32[]{:S(2)}, u32[]{:S(2)}) collective-permute-start(bf16[96,384]{1,0:T(8,128)(2,1)S(1)} %get-tuple-element.114), channel_id=1, source_target_pairs={{0,8},{4,12},{8,0},{12,4},{1,9},{5,13},{9,1},{13,5},{2,10},{6,14},... | collective-permute-start | bytes 221192 | tf_op jit(solution)/shard_map/ppermute | solution.py:426
  117.8 2.1 %collective-permute-start.18 = (bf16[96,384]{1,0:T(8,128)(2,1)S(1)}, bf16[96,384]{1,0:T(8,128)(2,1)S(1)}, u32[]{:S(2)}, u32[]{:S(2)}) collective-permute-start(bf16[96,384]{1,0:T(8,128)(2,1)S(1)} %get-tuple-element.120), channel_id=1, source_target_pairs={{0,4},{4,8},{8,12},{12,0},{1,5},{5,9},{9,13},{13,1},{2,6},{6,10},{... | collective-permute-start | bytes 221192 | tf_op jit(solution)/shard_map/ppermute | solution.py:426
  119.8 0.4 collective-permute-start.19
  120.2 3.0 %collective-permute-start.20 = (bf16[96,384]{1,0:T(8,128)(2,1)S(1)}, bf16[96,384]{1,0:T(8,128)(2,1)S(1)}, u32[]{:S(2)}, u32[]{:S(2)}) collective-permute-start(bf16[96,384]{1,0:T(8,128)(2,1)S(1)} %get-tuple-element.122), channel_id=1, source_target_pairs={{0,12},{4,0},{8,4},{12,8},{1,13},{5,1},{9,5},{13,9},{2,14},{6,2},{... | collective-permute-start | bytes 221192 | tf_op jit(solution)/shard_map/ppermute | solution.py:426
  123.2 3.3 %feed.1 = f32[1024,128]{1,0:T(8,128)} custom-call(bf16[1024,384]{1,0:T(8,128)(2,1)S(1)} %mix.1.normed_ref, bf16[1024,384]{1,0:T(8,128)(2,1)S(1)} %get-tuple-element.104.grid.grid_ref, bf16[384,768]{1,0:T(8,128)(2,1)S(1)} %copy-done.6, bf16[768,384]{1,0:T(8,128)(2,1)S(1)} %copy-done.7, bf16[384,128]{1,0:T(8,128)(2,1)S(1)} %copy-done.18), custom_call_target="tpu_custom_call" | custom-call | flops 1000 | bytes 1000 | tf_op jit(solution)/shard_map/feed/pallas_call | solution.py:671
  126.6 1.8 %collective-permute-done.19.refs_6_ = bf16[96,384]{1,0:T(8,128)(2,1)S(1)} collective-permute-done((bf16[96,384]{1,0:T(8,128)(2,1)S(1)}, bf16[96,384]{1,0:T(8,128)(2,1)S(1)}, u32[]{:S(2)}, u32[]{:S(2)}) %collective-permute-start.19) | collective-permute-done | bytes 73760 | tf_op jit(solution)/shard_map/ppermute | solution.py:426
  128.4 1.6 %collective-permute-start.22 = (bf16[96,768]{1,0:T(8,128)(2,1)S(1)}, bf16[96,768]{1,0:T(8,128)(2,1)S(1)}, u32[]{:S(2)}, u32[]{:S(2)}) collective-permute-start(bf16[96,768]{1,0:T(8,128)(2,1)S(1)} %close.1.own_ref), channel_id=1, source_target_pairs={{0,2},{1,3},{2,0},{3,1},{4,6},{5,7},{6,4},{7,5},{8,10},{9,11},{10,... | collective-permute-start | bytes 442376 | tf_op jit(solution)/shard_map/ppermute | solution.py:421
  130.0 3.6 %collective-permute-done.22.two_ref = bf16[96,768]{1,0:T(8,128)(2,1)S(1)} collective-permute-done((bf16[96,768]{1,0:T(8,128)(2,1)S(1)}, bf16[96,768]{1,0:T(8,128)(2,1)S(1)}, u32[]{:S(2)}, u32[]{:S(2)}) %collective-permute-start.22) | collective-permute-done | bytes 147488 | tf_op jit(solution)/shard_map/ppermute | solution.py:421
  133.6 1.4 %collective-permute-done.23.three_ref = bf16[96,768]{1,0:T(8,128)(2,1)S(1)} collective-permute-done((bf16[96,768]{1,0:T(8,128)(2,1)S(1)}, bf16[96,768]{1,0:T(8,128)(2,1)S(1)}, u32[]{:S(2)}, u32[]{:S(2)}) %collective-permute-start.23) | collective-permute-done | bytes 147488 | tf_op jit(solution)/shard_map/ppermute | solution.py:421
  135.0 1.1 spread.1
  (72 shorter events, 0.8 us)
Async XLA Ops:
  0.6 1.4 %copy-start.4 = (bf16[1,32,32,768]{3,2,1,0:T(8,128)(2,1)S(1)}, bf16[1,32,32,768]{3,2,1,0:T(8,128)(2,1)}, u32[]{:S(2)}) copy-start(bf16[1,32,32,768]{3,2,1,0:T(8,128)(2,1)} %param.15) | copy-start | bytes 4718596
  2.7 8.9 %copy-start = (bf16[768,768]{1,0:T(8,128)(2,1)S(1)}, bf16[768,768]{1,0:T(8,128)(2,1)}, u32[]{:S(2)}) copy-start(bf16[768,768]{1,0:T(8,128)(2,1)} %wout_ref.3) | copy-start | bytes 3538948
  2.7 8.9 %copy-start.8 = (bf16[1,1,1,256,768]{4,3,2,1,0:T(8,128)(2,1)S(1)}, bf16[1,1,1,256,768]{4,3,2,1,0:T(8,128)(2,1)}, u32[]{:S(2)}) copy-start(bf16[1,1,1,256,768]{4,3,2,1,0:T(8,128)(2,1)} %param.19) | copy-start | bytes 1179652
  4.4 21.9 %all-to-all-start = ((bf16[8,40,768]{2,1,0:T(8,128)(2,1)}), bf16[8,40,768]{2,1,0:T(8,128)(2,1)S(1)}, u32[]{:S(2)}, u32[]{:S(2)}) async-start(bf16[8,40,768]{2,1,0:T(8,128)(2,1)} %bitcast.4), calls=%async_computation | async-start | bytes 983040 | tf_op jit(solution)/shard_map/all_to_all | solution.py:473
  11.7 2.0 %copy-start.1 = (bf16[768,2304]{1,0:T(8,128)(2,1)S(1)}, bf16[768,2304]{1,0:T(8,128)(2,1)}, u32[]{:S(2)}) copy-start(bf16[768,2304]{1,0:T(8,128)(2,1)} %wqkv_ref.1) | copy-start | bytes 10616836
  13.7 12.7 %copy-start.23 = (s32[1,1,1,256]{3,2,1,0:T(1,128)S(1)}, s32[1,1,1,256]{3,2,1,0:T(1,128)}, u32[]{:S(2)}) copy-start(s32[1,1,1,256]{3,2,1,0:T(1,128)} %param.17) | copy-start | bytes 3076
  14.8 1.7 %copy-start.2 = (bf16[2304,768]{1,0:T(8,128)(2,1)}, bf16[2304,768]{1,0:T(8,128)(2,1)S(1)}, u32[]{:S(2)}) copy-start(bf16[2304,768]{1,0:T(8,128)(2,1)S(1)} %get-tuple-element.67.wqkv_hbm) | copy-start | bytes 10616836
  17.2 15.0 %collective-permute-start = (bf16[192,256]{1,0:T(8,128)(2,1)S(1)}, bf16[192,256]{1,0:T(8,128)(2,1)S(1)}, u32[]{:S(2)}, u32[]{:S(2)}) collective-permute-start(bf16[192,256]{1,0:T(8,128)(2,1)S(1)} %get-tuple-element.73), channel_id=1, source_target_pairs={{0,1},{1,0},{2,3},{3,2},{4,5},{5,4},{6,7},{7,6},{8,9},{9,8},{10,11... | collective-permute-start | bytes 294920 | tf_op jit(solution)/shard_map/ppermute | solution.py:421
  17.2 15.6 %collective-permute-start.1 = (bf16[192,256]{1,0:T(8,128)(2,1)S(1)}, bf16[192,256]{1,0:T(8,128)(2,1)S(1)}, u32[]{:S(2)}, u32[]{:S(2)}) collective-permute-start(bf16[192,256]{1,0:T(8,128)(2,1)S(1)} %get-tuple-element.74), channel_id=1, source_target_pairs={{0,2},{1,3},{2,0},{3,1},{4,6},{5,7},{6,4},{7,5},{8,10},{9,11},{10,... | collective-permute-start | bytes 294920 | tf_op jit(solution)/shard_map/ppermute | solution.py:421
  18.7 14.7 %collective-permute-start.2 = (bf16[192,256]{1,0:T(8,128)(2,1)S(1)}, bf16[192,256]{1,0:T(8,128)(2,1)S(1)}, u32[]{:S(2)}, u32[]{:S(2)}) collective-permute-start(bf16[192,256]{1,0:T(8,128)(2,1)S(1)} %get-tuple-element.75), channel_id=1, source_target_pairs={{0,3},{1,2},{2,1},{3,0},{4,7},{5,6},{6,5},{7,4},{8,11},{9,10},{10,... | collective-permute-start | bytes 294920 | tf_op jit(solution)/shard_map/ppermute | solution.py:421
  26.3 2.0 %copy-start.3 = (bf16[2304,768]{1,0:T(8,128)(2,1)S(1)}, bf16[2304,768]{1,0:T(8,128)(2,1)}, u32[]{:S(2)}) copy-start(bf16[2304,768]{1,0:T(8,128)(2,1)} %copy-done.2) | copy-start | bytes 10616836
  28.3 5.7 %copy-start.5 = (bf16[768,384]{1,0:T(8,128)(2,1)S(1)}, bf16[768,384]{1,0:T(8,128)(2,1)}, u32[]{:S(2)}) copy-start(bf16[768,384]{1,0:T(8,128)(2,1)} %wdec_ref.1) | copy-start | bytes 1769476
  28.3 5.7 %copy-start.24 = (s32[1,1,1,256]{3,2,1,0:T(1,128)S(1)}, s32[1,1,1,256]{3,2,1,0:T(1,128)}, u32[]{:S(2)}) copy-start(s32[1,1,1,256]{3,2,1,0:T(1,128)} %param.18) | copy-start | bytes 3076
  28.3 5.7 %copy-start.25 = (f32[12]{0:T(128)S(1)}, f32[12]{0:T(128)}, u32[]{:S(2)}) copy-start(f32[12]{0:T(128)} %scale_ref.1) | copy-start | bytes 148
  34.1 43.3 %copy-start.26 = (bf16[384]{0:T(512)(128)(2,1)S(1)}, bf16[384]{0:T(512)(128)(2,1)}, u32[]{:S(2)}) copy-start(bf16[384]{0:T(512)(128)(2,1)} %param.24) | copy-start | bytes 2308
  34.1 45.4 %copy-start.21 = (s32[1,1,1,8,35]{4,3,2,1,0:T(8,128)S(1)}, s32[1,1,1,8,35]{4,3,2,1,0:T(8,128)}, u32[]{:S(2)}) copy-start(s32[1,1,1,8,35]{4,3,2,1,0:T(8,128)} %param.16) | copy-start | bytes 3364
  34.1 45.4 %copy-start.22 = (f32[2,1408]{1,0:T(2,128)S(1)}, f32[2,1408]{1,0:T(2,128)}, u32[]{:S(2)}) copy-start(f32[2,1408]{1,0:T(2,128)} %constant.2.clone.ids_ref) | copy-start | bytes 33796
  43.8 0.7 copy-start.17
  44.5 35.0 %collective-permute-start.3 = (bf16[704,768]{1,0:T(8,128)(2,1)}, bf16[704,768]{1,0:T(8,128)(2,1)S(1)}, u32[]{:S(2)}, u32[]{:S(2)}) collective-permute-start(bf16[704,768]{1,0:T(8,128)(2,1)} %get-tuple-element.81), channel_id=1, source_target_pairs={{0,1},{1,0},{2,3},{3,2},{4,5},{5,4},{6,7},{7,6},{8,9},{9,8},{10,11... | collective-permute-start | bytes 3244040 | tf_op jit(solution)/shard_map/ppermute | solution.py:421
  44.5 40.9 %collective-permute-start.4 = (bf16[640,768]{1,0:T(8,128)(2,1)}, bf16[640,768]{1,0:T(8,128)(2,1)S(1)}, u32[]{:S(2)}, u32[]{:S(2)}) collective-permute-start(bf16[640,768]{1,0:T(8,128)(2,1)} %get-tuple-element.82), channel_id=1, source_target_pairs={{0,2},{1,3},{2,0},{3,1},{4,6},{5,7},{6,4},{7,5},{8,10},{9,11},{10,... | collective-permute-start | bytes 2949128 | tf_op jit(solution)/shard_map/ppermute | solution.py:421
  46.0 31.4 %collective-permute-start.5 = (bf16[256,768]{1,0:T(8,128)(2,1)}, bf16[256,768]{1,0:T(8,128)(2,1)}, u32[]{:S(2)}, u32[]{:S(2)}) collective-permute-start(bf16[256,768]{1,0:T(8,128)(2,1)} %get-tuple-element.79.normed_ref), channel_id=1, source_target_pairs={{0,2},{1,3},{2,0},{3,1},{4,6},{5,7},{6,4},{7,5},{8,10},{9,11},{10,... | collective-permute-start | bytes 1179656 | tf_op jit(solution)/shard_map/ppermute | solution.py:421
  46.5 30.9 %all-to-all-start.1 = ((bf16[8,40,384]{2,1,0:T(8,128)(2,1)}), bf16[8,40,384]{2,1,0:T(8,128)(2,1)S(1)}, u32[]{:S(2)}, u32[]{:S(2)}) async-start(bf16[8,40,384]{2,1,0:T(8,128)(2,1)} %bitcast.15), calls=%async_computation.1 | async-start | bytes 491520 | tf_op jit(solution)/shard_map/all_to_all | solution.py:541
  77.4 2.1 %collective-permute-start.6 = (bf16[256,768]{1,0:T(8,128)(2,1)}, bf16[256,768]{1,0:T(8,128)(2,1)}, u32[]{:S(2)}, u32[]{:S(2)}) collective-permute-start(bf16[256,768]{1,0:T(8,128)(2,1)} %collective-permute-done.5.refs_4_), channel_id=1, source_target_pairs={{0,1},{1,0},{2,3},{3,2},{4,5},{5,4},{6,7},{7,6},{8,9},{9,8},{10,11... | collective-permute-start | bytes 1179656 | tf_op jit(solution)/shard_map/ppermute | solution.py:421
  81.0 6.9 %collective-permute-start.7 = (bf16[96,384]{1,0:T(8,128)(2,1)S(1)}, bf16[96,384]{1,0:T(8,128)(2,1)S(1)}, u32[]{:S(2)}, u32[]{:S(2)}) collective-permute-start(bf16[96,384]{1,0:T(8,128)(2,1)S(1)} %get-tuple-element.86), channel_id=1, source_target_pairs={{0,4},{4,8},{8,12},{12,0},{1,5},{5,9},{9,13},{13,1},{2,6},{6,10},{... | collective-permute-start | bytes 221192 | tf_op jit(solution)/shard_map/ppermute | solution.py:426
  81.0 6.9 %collective-permute-start.8 = (bf16[96,384]{1,0:T(8,128)(2,1)S(1)}, bf16[96,384]{1,0:T(8,128)(2,1)S(1)}, u32[]{:S(2)}, u32[]{:S(2)}) collective-permute-start(bf16[96,384]{1,0:T(8,128)(2,1)S(1)} %get-tuple-element.87), channel_id=1, source_target_pairs={{0,12},{4,0},{8,4},{12,8},{1,13},{5,1},{9,5},{13,9},{2,14},{6,2},{... | collective-permute-start | bytes 221192 | tf_op jit(solution)/shard_map/ppermute | solution.py:426
  84.8 4.4 %collective-permute-start.9 = (bf16[96,384]{1,0:T(8,128)(2,1)S(1)}, bf16[96,384]{1,0:T(8,128)(2,1)S(1)}, u32[]{:S(2)}, u32[]{:S(2)}) collective-permute-start(bf16[96,384]{1,0:T(8,128)(2,1)S(1)} %get-tuple-element.88), channel_id=1, source_target_pairs={{0,16},{4,20},{8,24},{12,28},{16,0},{20,4},{24,8},{28,12},{1,17},{... | collective-permute-start | bytes 221192 | tf_op jit(solution)/shard_map/ppermute | solution.py:595
  89.2 6.4 %collective-permute-start.10 = (bf16[640,768]{1,0:T(8,128)(2,1)S(1)}, bf16[640,768]{1,0:T(8,128)(2,1)S(1)}, u32[]{:S(2)}, u32[]{:S(2)}) collective-permute-start(bf16[640,768]{1,0:T(8,128)(2,1)S(1)} %collective-permute-done.4.refs_2_), channel_id=1, source_target_pairs={{0,1},{1,0},{2,3},{3,2},{4,5},{5,4},{6,7},{7,6},{8,9},{9,8},{10,11... | collective-permute-start | bytes 2949128 | tf_op jit(solution)/shard_map/ppermute | solution.py:421
  89.2 6.4 %collective-permute-start.11 = (bf16[16,384]{1,0:T(8,128)(2,1)S(1)}, bf16[16,384]{1,0:T(8,128)(2,1)S(1)}, u32[]{:S(2)}, u32[]{:S(2)}) collective-permute-start(bf16[16,384]{1,0:T(8,128)(2,1)S(1)} %get-tuple-element.90), channel_id=1, source_target_pairs={{0,20},{4,24},{8,28},{12,16},{16,4},{20,8},{24,12},{28,0},{1,21},{... | collective-permute-start | bytes 36872 | tf_op jit(solution)/shard_map/ppermute | solution.py:595
  89.2 6.4 %collective-permute-start.12 = (bf16[16,384]{1,0:T(8,128)(2,1)S(1)}, bf16[16,384]{1,0:T(8,128)(2,1)S(1)}, u32[]{:S(2)}, u32[]{:S(2)}) collective-permute-start(bf16[16,384]{1,0:T(8,128)(2,1)S(1)} %get-tuple-element.91), channel_id=1, source_target_pairs={{0,28},{4,16},{8,20},{12,24},{16,12},{20,0},{24,4},{28,8},{1,29},{... | collective-permute-start | bytes 36872 | tf_op jit(solution)/shard_map/ppermute | solution.py:595
  95.6 0.9 copy-start.10
  96.5 0.9 copy-start.12
  97.4 0.9 copy-start.14
  98.3 0.9 copy-start.16
  101.3 4.3 %copy-start.19 = (f32[7,7,384]{2,1,0:T(8,128)S(1)}, f32[7,7,384]{2,1,0:T(8,128)}, u32[]{:S(2)}) copy-start(f32[7,7,384]{2,1,0:T(8,128)} %taps.1) | copy-start | bytes 225796
  101.3 11.8 %collective-permute-start.13 = (bf16[4,96,384]{2,1,0:T(8,128)(2,1)S(1)}, bf16[4,96,384]{2,1,0:T(8,128)(2,1)S(1)}, u32[]{:S(2)}, u32[]{:S(2)}) collective-permute-start(bf16[4,96,384]{2,1,0:T(8,128)(2,1)S(1)} %get-tuple-element.103), channel_id=1, source_target_pairs={{0,16},{16,0},{1,17},{17,1},{2,18},{18,2},{3,19},{19,3},{4,20},{20... | collective-permute-start | bytes 884744 | tf_op jit(solution)/shard_map/ppermute | solution.py:426
  104.1 13.6 %collective-permute-start.17 = (bf16[4,96,384]{2,1,0:T(8,128)(2,1)S(1)}, bf16[4,96,384]{2,1,0:T(8,128)(2,1)S(1)}, u32[]{:S(2)}, u32[]{:S(2)}) collective-permute-start(bf16[4,96,384]{2,1,0:T(8,128)(2,1)S(1)} %get-tuple-element.116), channel_id=1, source_target_pairs={{0,16},{16,0},{1,17},{17,1},{2,18},{18,2},{3,19},{19,3},{4,20},{20... | collective-permute-start | bytes 884744 | tf_op jit(solution)/shard_map/ppermute | solution.py:426
  113.1 10.1 %copy-start.6 = (bf16[384,768]{1,0:T(8,128)(2,1)S(1)}, bf16[384,768]{1,0:T(8,128)(2,1)}, u32[]{:S(2)}) copy-start(bf16[384,768]{1,0:T(8,128)(2,1)} %up_ref.1) | copy-start | bytes 1769476
  113.1 10.1 %copy-start.7 = (bf16[768,384]{1,0:T(8,128)(2,1)S(1)}, bf16[768,384]{1,0:T(8,128)(2,1)}, u32[]{:S(2)}) copy-start(bf16[768,384]{1,0:T(8,128)(2,1)} %down_ref.1) | copy-start | bytes 1769476
  113.2 10.0 %copy-start.18 = (bf16[384,128]{1,0:T(8,128)(2,1)S(1)}, bf16[384,128]{1,0:T(8,128)(2,1)}, u32[]{:S(2)}) copy-start(bf16[384,128]{1,0:T(8,128)(2,1)} %head_ref.1) | copy-start | bytes 294916
  113.3 7.0 %collective-permute-start.14 = (bf16[96,384]{1,0:T(8,128)(2,1)S(1)}, bf16[96,384]{1,0:T(8,128)(2,1)S(1)}, u32[]{:S(2)}, u32[]{:S(2)}) collective-permute-start(bf16[96,384]{1,0:T(8,128)(2,1)S(1)} %get-tuple-element.113), channel_id=1, source_target_pairs={{0,4},{4,8},{8,12},{12,0},{1,5},{5,9},{9,13},{13,1},{2,6},{6,10},{... | collective-permute-start | bytes 221192 | tf_op jit(solution)/shard_map/ppermute | solution.py:426
  113.3 13.2 %collective-permute-start.15 = (bf16[96,384]{1,0:T(8,128)(2,1)S(1)}, bf16[96,384]{1,0:T(8,128)(2,1)S(1)}, u32[]{:S(2)}, u32[]{:S(2)}) collective-permute-start(bf16[96,384]{1,0:T(8,128)(2,1)S(1)} %get-tuple-element.114), channel_id=1, source_target_pairs={{0,8},{4,12},{8,0},{12,4},{1,9},{5,13},{9,1},{13,5},{2,10},{6,14},... | collective-permute-start | bytes 221192 | tf_op jit(solution)/shard_map/ppermute | solution.py:426
  117.7 8.9 %collective-permute-start.16 = (bf16[96,384]{1,0:T(8,128)(2,1)S(1)}, bf16[96,384]{1,0:T(8,128)(2,1)S(1)}, u32[]{:S(2)}, u32[]{:S(2)}) collective-permute-start(bf16[96,384]{1,0:T(8,128)(2,1)S(1)} %get-tuple-element.115), channel_id=1, source_target_pairs={{0,12},{4,0},{8,4},{12,8},{1,13},{5,1},{9,5},{13,9},{2,14},{6,2},{... | collective-permute-start | bytes 221192 | tf_op jit(solution)/shard_map/ppermute | solution.py:426
  117.8 8.8 %collective-permute-start.18 = (bf16[96,384]{1,0:T(8,128)(2,1)S(1)}, bf16[96,384]{1,0:T(8,128)(2,1)S(1)}, u32[]{:S(2)}, u32[]{:S(2)}) collective-permute-start(bf16[96,384]{1,0:T(8,128)(2,1)S(1)} %get-tuple-element.120), channel_id=1, source_target_pairs={{0,4},{4,8},{8,12},{12,0},{1,5},{5,9},{9,13},{13,1},{2,6},{6,10},{... | collective-permute-start | bytes 221192 | tf_op jit(solution)/shard_map/ppermute | solution.py:426
  119.8 8.5 %collective-permute-start.19 = (bf16[96,384]{1,0:T(8,128)(2,1)S(1)}, bf16[96,384]{1,0:T(8,128)(2,1)S(1)}, u32[]{:S(2)}, u32[]{:S(2)}) collective-permute-start(bf16[96,384]{1,0:T(8,128)(2,1)S(1)} %get-tuple-element.121), channel_id=1, source_target_pairs={{0,8},{4,12},{8,0},{12,4},{1,9},{5,13},{9,1},{13,5},{2,10},{6,14},... | collective-permute-start | bytes 221192 | tf_op jit(solution)/shard_map/ppermute | solution.py:426
  120.2 8.1 %collective-permute-start.20 = (bf16[96,384]{1,0:T(8,128)(2,1)S(1)}, bf16[96,384]{1,0:T(8,128)(2,1)S(1)}, u32[]{:S(2)}, u32[]{:S(2)}) collective-permute-start(bf16[96,384]{1,0:T(8,128)(2,1)S(1)} %get-tuple-element.122), channel_id=1, source_target_pairs={{0,12},{4,0},{8,4},{12,8},{1,13},{5,1},{9,5},{13,9},{2,14},{6,2},{... | collective-permute-start | bytes 221192 | tf_op jit(solution)/shard_map/ppermute | solution.py:426
  128.4 5.2 %collective-permute-start.22 = (bf16[96,768]{1,0:T(8,128)(2,1)S(1)}, bf16[96,768]{1,0:T(8,128)(2,1)S(1)}, u32[]{:S(2)}, u32[]{:S(2)}) collective-permute-start(bf16[96,768]{1,0:T(8,128)(2,1)S(1)} %close.1.own_ref), channel_id=1, source_target_pairs={{0,2},{1,3},{2,0},{3,1},{4,6},{5,7},{6,4},{7,5},{8,10},{9,11},{10,... | collective-permute-start | bytes 442376 | tf_op jit(solution)/shard_map/ppermute | solution.py:421
  130.0 3.6 %collective-permute-start.21 = (bf16[96,768]{1,0:T(8,128)(2,1)S(1)}, bf16[96,768]{1,0:T(8,128)(2,1)S(1)}, u32[]{:S(2)}, u32[]{:S(2)}) collective-permute-start(bf16[96,768]{1,0:T(8,128)(2,1)S(1)} %close.1.own_ref), channel_id=1, source_target_pairs={{0,1},{1,0},{2,3},{3,2},{4,5},{5,4},{6,7},{7,6},{8,9},{9,8},{10,11... | collective-permute-start | bytes 442376 | tf_op jit(solution)/shard_map/ppermute | solution.py:421
  133.6 1.4 %collective-permute-start.23 = (bf16[96,768]{1,0:T(8,128)(2,1)S(1)}, bf16[96,768]{1,0:T(8,128)(2,1)S(1)}, u32[]{:S(2)}, u32[]{:S(2)}) collective-permute-start(bf16[96,768]{1,0:T(8,128)(2,1)S(1)} %collective-permute-done.22.two_ref), channel_id=1, source_target_pairs={{0,1},{1,0},{2,3},{3,2},{4,5},{5,4},{6,7},{7,6},{8,9},{9,8},{10,11... | collective-permute-start | bytes 442376 | tf_op jit(solution)/shard_map/ppermute | solution.py:421
  (5 other events, 3.2 us)

commit v5 on v4

--- a/solution.py
+++ b/solution.py
@@ -31,7 +31,7 @@
     return pl.BlockSpec(memory_space=pltpu.SMEM)
 
 
-def call(kernel, name, outs, in_specs, scratch=(), flops=0, nbytes=0, limit=20):
+def call(kernel, name, outs, in_specs, scratch=(), flops=0, nbytes=0, limit=20, cost=1000):
     single = not isinstance(outs, (list, tuple))
     out_list = [outs] if single else list(outs)
     specs = [vmem() for _ in out_list]
@@ -42,7 +42,9 @@
         out_specs=specs[0] if single else tuple(specs),
         scratch_shapes=list(scratch),
         compiler_params=pltpu.CompilerParams(vmem_limit_bytes=limit * MIB),
-        cost_estimate=pl.CostEstimate(flops=1000, bytes_accessed=1000, transcendentals=0),
+        cost_estimate=pl.CostEstimate(
+            flops=cost, bytes_accessed=1000 + cost // 300, transcendentals=0
+        ),
         name=name,
     )
 
@@ -78,17 +80,10 @@
 
 
 def project_kernel(
-    cap, padded, src_ref, arr_ref, wqkv_hbm, normed_ref, enc_ref, u_ref, len_ref, v_ref,
-    place_ref, wqkv_t_ref, sems,
+    cap, padded, src_ref, arr_ref, wqkv_t_ref, normed_ref, enc_ref, u_ref, len_ref, v_ref,
+    place_ref,
 ):
     rows, width = normed_ref.shape
-    copies = []
-    for t in range(3):
-        cut = slice(t * width, (t + 1) * width)
-        copies.append(
-            pltpu.make_async_copy(wqkv_hbm.at[cut], wqkv_t_ref.at[cut], sems.at[t])
-        )
-        copies[-1].start()
     heads = len_ref.shape[0] // 2
     size = width // heads
     slots = arr_ref.shape[0]
@@ -105,7 +100,6 @@
     normed = (centred * lax.rsqrt(spread + norm_eps)).astype(bf16)
     normed_ref[...] = normed
     for t in range(2):
-        copies[t].wait()
         raw = mm(wqkv_t_ref[t * width : (t + 1) * width], normed, NT)
         for h in range(heads):
             part = raw[h * size : (h + 1) * size]
@@ -113,15 +107,15 @@
             at = t * width + h * size
             u_ref[at : at + size] = part * inv
             len_ref[t * heads + h : t * heads + h + 1] = inv
-    copies[2].wait()
     v_ref[...] = mm(wqkv_t_ref[2 * width : 3 * width], normed, NT).astype(bf16)
 
 
 def encode_kernel(
     split, win_ref, scale_ref, place_ref, enc_ref, u_ref, len_ref, v_ref, ga_ref, wout_ref,
-    wdec_ref, normed_ref, out_ref, *refs,
+    wdec_ref, normed_ref, *refs,
 ):
-    peer_refs = refs[:-3]
+    cots, refs = (refs[:4], refs[4:]) if split is not None else ((), refs)
+    out_ref, peer_refs = refs[0], refs[1:-3]
     p_ref, att_ref, left_ref = refs[-3:]
     rows, width = enc_ref.shape
     heads = p_ref.shape[0]
@@ -179,6 +173,12 @@
         else:
             ref[deep : deep + rows] = attended
             ref[deep + rows : deep + 2 * rows] = normed_ref[...]
+    at = deep + 2 * rows
+    high = cots[0].shape[0]
+    for n, ref in enumerate(cots):
+        down, lane = divmod(n, width // rows)
+        top = at + down * high
+        peer_refs[0][top : top + high, lane * rows : (lane + 1) * rows] = ref[...]
 
 
 def emit_wide(split, out_ref, start, block):
@@ -221,11 +221,18 @@
 
 def term_kernel(columns, rows, *refs):
     own, near, far, hop, far_normed, hop_normed = refs[0:6]
-    cots = refs[6:10]
-    keep_ref, send_ref = refs[10:]
+    keep_ref, send_ref = refs[6:]
     half, part = keep_ref.shape[:2]
-    held, count = cots[0].shape[0] // part, cots[0].shape[1]
-    deep = own.shape[0] - 2 * rows
+    count = rows
+    deep = near.shape[0] - 2 * rows
+    across = own.shape[1] // count
+    high = (own.shape[0] - near.shape[0]) // -(-4 // across)
+    held = high // part
+    cots = []
+    for n in range(4):
+        down, lane = divmod(n, across)
+        top = near.shape[0] + down * high
+        cots.append(own[top : top + high, lane * count : (lane + 1) * count])
     stack = deep // part
     cut = slice(*columns)
     width = columns[1] - columns[0]
@@ -254,7 +261,7 @@
     first = [(0, block([left(ref, start, 0, half) for ref, start in peers], normed))]
     second = [
         (0, block([left(ref, start, half, qkv) for ref, start in peers], normed)),
-        (qkv - half, block([ref[...] for ref in cots], attended)),
+        (qkv - half, block(cots, attended)),
     ]
     spans = (first, second)
     for mine in range(2):
@@ -483,7 +490,9 @@
     cot_whole = (replicas,) + cot_part if fast else cot_part
     left_whole = (replicas, deep, width) if fast else (3 * width, rows)
     if fast:
-        peer_shapes = [(deep + 2 * rows, width)] * 2 + [(2 * deep + rows, width)]
+        tail = -(-4 // (width // rows)) * (width * part_rows // shard_rows)
+        peer_shapes = [(deep + 2 * rows + tail, width), (deep + 2 * rows, width)]
+        peer_shapes += [(2 * deep + rows, width)]
     else:
         peer_shapes = [(3 * width, rows), (rows, width)]
     grad_att, w_qkv_t, *cots = call(
@@ -511,21 +520,20 @@
             sds((width, rows), bf16),
             sds((1, rows), f32),
         ],
-        [vmem(), vmem(), pl.BlockSpec(memory_space=pltpu.HBM)],
-        scratch=[pltpu.VMEM((3 * width, width), bf16), pltpu.SemaphoreType.DMA((3,))],
+        [vmem()] * 3,
         flops=2 * rows * width * width * 4,
         nbytes=8 * MIB,
         limit=14,
+        cost=2000000000,
     )(enc_src.reshape(1, rows), arrived, w_qkv_t)
     if fast:
         normed_y = flip(normed, "replica", 2)
-        lengths = tie(lengths, cots)
 
     outbound, *peers = call(
         functools.partial(encode_kernel, split),
         "encode",
         [sds((slots, dec_width), bf16)] + [sds(shape, bf16) for shape in peer_shapes],
-        [vmem(), smem()] + [vmem()] * 9,
+        [vmem(), smem()] + [vmem()] * (13 if fast else 9),
         scratch=[
             pltpu.VMEM((heads, rows, rows), bf16),
             pltpu.VMEM((width, rows), bf16),
@@ -534,17 +542,19 @@
         flops=2 * rows * width * width * 10,
         nbytes=8 * MIB,
         limit=14,
+        cost=8000000000,
     )(
         window_id.reshape(1, rows), head_scale, places, enc_in, units, lengths, values, grad_att,
-        w_out, w_dec_in, normed,
-    )
+        w_out, w_dec_in, normed, *(cots if fast else ()),
+    )
+    if fast:
+        peers[1], peers[2], normed_y = lax.optimization_barrier((peers[1], peers[2], normed_y))
     returned = lax.all_to_all(
         outbound.reshape(group, padded, dec_width), ("eta", "phi"), split_axis=0, concat_axis=0,
         tiled=True,
     )
     if fast:
         own, near, far = peers[0], flip(peers[1], "replica", 1), flip(peers[2], "replica", 2)
-        normed_y = tie(normed_y, outbound)
         normed_hop = flip(normed_y, "replica", 1)
         returned = tie(returned, near, normed_hop)
     else:
@@ -619,9 +629,8 @@
             flat(bottom), flat(low[far:]), flat(high[far:]),
         )
     if fast:
-        far = tie(far, left_halo, right_halo, rims[0])
+        far = tie(far, left_halo, right_halo, rims)
         peers = [own, near, far, flip(far, "replica", 1), normed_y, normed_hop]
-        peers, cots = tie((peers, cots), left_halo, right_halo, rims)
         chunk = width // 2
         half = group // 2
         kept, sent = [], []
@@ -630,11 +639,11 @@
                 functools.partial(term_kernel, (c * chunk, (c + 1) * chunk), rows),
                 "terms%d" % c,
                 [sds((half, part_rows, chunk), f32), sds((half, part_rows, chunk), bf16)],
-                [vmem()] * 10,
+                [vmem()] * 6,
                 flops=2 * out_rows * chunk * rows,
                 nbytes=8 * MIB,
                 limit=10,
-            )(*peers, *cots)
+            )(*peers)
             kept.append(keep)
             sent.append(turn(send, "eta", 1))
         left, right_halo, rims = tie((left_halo, right_halo, rims), kept)

time: 137 us -> 112 us (0.82)
  waiting for transfers between devices: 49.1 us -> 31.9 us
  local copies, waits for them, and re-layouts: 14.7 us -> 9.83 us
  starting transfers between devices: 37.3 us -> 35.6 us
    ppermute x11, waiting for transfers between devices: 34.5 us -> 10.6 us  [flip(): lax.ppermute(value, axis, [(i, i ^ bit) for i in range(lax.axis_size(axis...]
    all_to_all x1, waiting for transfers between devices: 0.01 us -> 8.54 us  [body(): lax.all_to_all(outbound.reshape(group, padded, dec_width), ('eta', 'phi')...]
    unnamed x54 -> x38, local copies, waits for them, and re-layouts: 14.7 us -> 8.56 us
    ppermute x3, starting transfers between devices: 5.29 us -> 2.98 us  [shifted(): return lax.ppermute(value, plane, pairs)]
    pallas_call x1, Pallas kernels: 3.81 us -> 2.03 us  [body(): call(functools.partial(project_kernel, cap, padded), 'project', [sds((row...]
  transfers between devices with their start and end apart: 26 -> 26, of which waited for: 9 -> 9; matrix products, arithmetic and copies ran while one was open for 0% -> 1% of each run, Pallas kernels for 14% -> 25%
where the time goes in v5:
time: 112 us
  starting transfers between devices  35.6 us (32%)
  Pallas kernels  33.5 us (30%)
  waiting for transfers between devices  31.9 us (28%)
  local copies, waits for them, and re-layouts  9.83 us (9%)
    ppermute x10, starting transfers between devices, turn(): lax.ppermute(value, axis, [(i, (i + k) % count) for i in range(count)])  15.4 us
    ppermute x11, waiting for transfers between devices, flip(): lax.ppermute(value, axis, [(i, i ^ bit) for i in range(lax.axis_size(axis...  10.6 us
    pallas_call x1, Pallas kernels, body(): call(functools.partial(encode_kernel, split), 'encode', [sds((slots, dec_...  9.27 us
    unnamed x38, local copies, waits for them, and re-layouts  8.56 us
    all_to_all x1, waiting for transfers between devices, body(): lax.all_to_all(outbound.reshape(group, padded, dec_width), ('eta', 'phi')...  8.54 us
    all_to_all x1, waiting for transfers between devices, body(): lax.all_to_all(outgoing.reshape(group, padded, width), ('eta', 'phi'), sp...  7.56 us
    pallas_call x1, Pallas kernels, body(): call(functools.partial(mix_folded if folded else mix_open, (eta_cells, ph...  7.45 us
    all_to_all x1, starting transfers between devices, body(): lax.all_to_all(outgoing.reshape(group, padded, width), ('eta', 'phi'), sp...  7.25 us
  transfers between devices with their start and end apart: 26, of which 9 were waited for; matrix products, arithmetic and copies ran while one was open for 1% of the time, Pallas kernels for 25%

profile of v5, /device:TPU:0, one launch (start us, length us, event | category | flops | bytes accessed | tf_op | source)
XLA Modules:
  0.0 111.7 jit_solution(11701306817260746852)
XLA Ops:
  0.6 1.4 %copy-done.1 = bf16[1,32,32,768]{3,2,1,0:T(8,128)(2,1)S(1)} copy-done((bf16[1,32,32,768]{3,2,1,0:T(8,128)(2,1)S(1)}, bf16[1,32,32,768]{3,2,1,0:T(8,128)(2,1)}, u32[]{:S(2)}) %copy-start.1) | copy-done | bytes 1572888
  2.0 0.7 copy-done.9
  2.7 1.7 %pick.1 = bf16[320,768]{1,0:T(8,128)(2,1)} custom-call(s32[8,35]{1,0:T(8,128)S(1)} %bitcast.14, bf16[1024,768]{1,0:T(8,128)(2,1)S(1)} %bitcast.11), custom_call_target="tpu_custom_call" | custom-call | flops 1000 | bytes 1003 | tf_op jit(solution)/shard_map/pick/pallas_call | solution.py:470
  4.4 7.3 %all-to-all-start = ((bf16[8,40,768]{2,1,0:T(8,128)(2,1)}), bf16[8,40,768]{2,1,0:T(8,128)(2,1)S(1)}, u32[]{:S(2)}, u32[]{:S(2)}) async-start(bf16[8,40,768]{2,1,0:T(8,128)(2,1)} %bitcast.4), calls=%async_computation | async-start | bytes 983040 | tf_op jit(solution)/shard_map/all_to_all | solution.py:480
  11.7 2.0 %copy-done = bf16[768,2304]{1,0:T(8,128)(2,1)S(1)} copy-done((bf16[768,2304]{1,0:T(8,128)(2,1)S(1)}, bf16[768,2304]{1,0:T(8,128)(2,1)}, u32[]{:S(2)}) %copy-start) | copy-done | bytes 3538968
  13.7 1.5 %prep.1 = (bf16[768,256]{1,0:T(8,128)(2,1)S(1)}, bf16[2304,768]{1,0:T(8,128)(2,1)S(1)}, bf16[192,256]{1,0:T(8,128)(2,1)S(1)}, bf16[192,256]{1,0:T(8,128)(2,1)}, ...) custom-call(bf16[256,768]{1,0:T(8,128)(2,1)S(1)} %bitcast.13, bf16[768,768]{1,0:T(8,128)(2,1)S(1)} %copy-done.2, ...), custom_call_target="tpu_custom_call" | custom-call | flops 1000 | bytes 1003 | tf_op jit(solution)/shard_map/prep/pallas_call | solution.py:498
  15.2 1.7 %copy-done.13 = bf16[2304,768]{1,0:T(8,128)(2,1)} copy-done((bf16[2304,768]{1,0:T(8,128)(2,1)}, bf16[2304,768]{1,0:T(8,128)(2,1)S(1)}, u32[]{:S(2)}) %copy-start.13) | copy-done | bytes 3538968
  16.9 1.5 %collective-permute-start.1 = (bf16[192,256]{1,0:T(8,128)(2,1)}, bf16[192,256]{1,0:T(8,128)(2,1)S(1)}, u32[]{:S(2)}, u32[]{:S(2)}) collective-permute-start(bf16[192,256]{1,0:T(8,128)(2,1)} %get-tuple-element.68), channel_id=1, source_target_pairs={{0,2},{1,3},{2,0},{3,1},{4,6},{5,7},{6,4},{7,5},{8,10},{9,11},{10,... | collective-permute-start | bytes 294920 | tf_op jit(solution)/shard_map/ppermute | solution.py:428
  18.4 0.3 collective-permute-start.2
  18.8 7.6 %all-to-all-done = bf16[8,40,768]{2,1,0:T(8,128)(2,1)S(1)} async-done(((bf16[8,40,768]{2,1,0:T(8,128)(2,1)}), bf16[8,40,768]{2,1,0:T(8,128)(2,1)S(1)}, u32[]{:S(2)}, u32[]{:S(2)}) %all-to-all-start) | async-done | bytes 491552 | tf_op jit(solution)/shard_map/all_to_all | solution.py:480
  26.3 2.0 %copy-done.14 = bf16[2304,768]{1,0:T(8,128)(2,1)S(1)} copy-done((bf16[2304,768]{1,0:T(8,128)(2,1)S(1)}, bf16[2304,768]{1,0:T(8,128)(2,1)}, u32[]{:S(2)}) %copy-start.14) | copy-done | bytes 3538968
  28.4 2.0 %project.1 = (bf16[256,768]{1,0:T(8,128)(2,1)S(1)}, bf16[256,768]{1,0:T(8,128)(2,1)S(1)}, f32[1536,256]{1,0:T(8,128)S(1)}, f32[24,256]{1,0:T(8,128)S(1)}, bf16[7...) custom-call(s32[1,256]{1,0:T(1,128)S(1)} %bitcast.16, bf16[320,768]{1,0:T(8,128)(2,1)S(1)} %bitcast.12, ...), custom_call_target="tpu_custom_call" | custom-call | flops 2000000000 | bytes 6667666 | tf_op jit(solution)/shard_map/project/pallas_call | solution.py:512
  30.4 1.6 %collective-permute-start.3 = (bf16[256,768]{1,0:T(8,128)(2,1)S(1)}, bf16[256,768]{1,0:T(8,128)(2,1)S(1)}, u32[]{:S(2)}, u32[]{:S(2)}) collective-permute-start(bf16[256,768]{1,0:T(8,128)(2,1)S(1)} %get-tuple-element.65.normed_ref), channel_id=1, source_target_pairs={{0,2},{1,3},{2,0},{3,1},{4,6},{5,7},{6,4},{7,5},{8,10},{9,11},{10,... | collective-permute-start | bytes 1179656 | tf_op jit(solution)/shard_map/ppermute | solution.py:428
  32.1 9.3 %encode.1 = (bf16[320,384]{1,0:T(8,128)(2,1)}, bf16[1088,768]{1,0:T(8,128)(2,1)S(1)}, bf16[704,768]{1,0:T(8,128)(2,1)}, bf16[640,768]{1,0:T(8,128)(2,1)}) custom-call(s32[1,256]{1,0:T(1,128)S(1)} %bitcast.17, f32[12]{0:T(128)S(1)} %copy-done.18, f32[1,256]{1,0:T(1,128)S(1)} %get-tuple-element.59.place_ref, bf16[256,768]{1,0:T(8,128)(2,1)S(1)} %get-tuple-element.60.enc_ref, ...), custom_call_target="tpu_custom_call" | custom-call | flops 8000000000 | bytes 26667666 | tf_op jit(solution)/shard_map/encode/pallas_call | solution.py:532
  41.3 0.5 collective-permute-start.5
  41.8 4.0 %all-to-all-start.1 = ((bf16[8,40,384]{2,1,0:T(8,128)(2,1)}), bf16[8,40,384]{2,1,0:T(8,128)(2,1)}, u32[]{:S(2)}, u32[]{:S(2)}) async-start(bf16[8,40,384]{2,1,0:T(8,128)(2,1)} %bitcast.7), calls=%async_computation.1 | async-start | bytes 491520 | tf_op jit(solution)/shard_map/all_to_all | solution.py:552
  45.9 0.3 collective-permute-start.6
  46.2 1.3 %reshape.47.mask_ref = bf16[1,384]{1,0:T(2,128)(2,1)} reshape(bf16[384]{0:T(512)(128)(2,1)} %param.24) | data formatting | bytes 1536 | tf_op jit(solution)/shard_map/reshape | solution.py:593
  47.5 8.5 %all-to-all-done.1 = bf16[8,40,384]{2,1,0:T(8,128)(2,1)} async-done(((bf16[8,40,384]{2,1,0:T(8,128)(2,1)}), bf16[8,40,384]{2,1,0:T(8,128)(2,1)}, u32[]{:S(2)}, u32[]{:S(2)}) %all-to-all-start.1) | async-done | bytes 245792 | tf_op jit(solution)/shard_map/all_to_all | solution.py:552
  56.0 0.7 copy-done.12
  56.7 2.4 %fill.1 = (bf16[1024,384]{1,0:T(8,128)(2,1)S(1)}, bf16[96,384]{1,0:T(8,128)(2,1)S(1)}, bf16[96,384]{1,0:T(8,128)(2,1)S(1)}, bf16[96,384]{1,0:T(8,128)(2,1)S(1)},...) custom-call(s32[8,35]{1,0:T(8,128)S(1)} %bitcast.15, f32[2,1408]{1,0:T(2,128)S(1)} %copy-done.11, ...), custom_call_target="tpu_custom_call" | custom-call | flops 1000 | bytes 1003 | tf_op jit(solution)/shard_map/fill/pallas_call | solution.py:583
  59.1 0.1 collective-permute-start.7
  59.2 3.8 %collective-permute-start.8 = (bf16[96,384]{1,0:T(8,128)(2,1)S(1)}, bf16[96,384]{1,0:T(8,128)(2,1)S(1)}, u32[]{:S(2)}, u32[]{:S(2)}) collective-permute-start(bf16[96,384]{1,0:T(8,128)(2,1)S(1)} %get-tuple-element.79), channel_id=1, source_target_pairs={{0,12},{4,0},{8,4},{12,8},{1,13},{5,1},{9,5},{13,9},{2,14},{6,2},{... | collective-permute-start | bytes 221192 | tf_op jit(solution)/shard_map/ppermute | solution.py:433
  63.0 0.5 collective-permute-start.9
  63.5 2.3 %collective-permute-done.5.refs_2_ = bf16[640,768]{1,0:T(8,128)(2,1)} collective-permute-done((bf16[640,768]{1,0:T(8,128)(2,1)}, bf16[640,768]{1,0:T(8,128)(2,1)}, u32[]{:S(2)}, u32[]{:S(2)}) %collective-permute-start.5) | collective-permute-done | bytes 983072 | tf_op jit(solution)/shard_map/ppermute | solution.py:428
  65.8 2.4 %collective-permute-start.11 = (bf16[16,384]{1,0:T(8,128)(2,1)S(1)}, bf16[16,384]{1,0:T(8,128)(2,1)S(1)}, u32[]{:S(2)}, u32[]{:S(2)}) collective-permute-start(bf16[16,384]{1,0:T(8,128)(2,1)S(1)} %get-tuple-element.82), channel_id=1, source_target_pairs={{0,28},{4,16},{8,20},{12,24},{16,12},{20,0},{24,4},{28,8},{1,29},{... | collective-permute-start | bytes 36872 | tf_op jit(solution)/shard_map/ppermute | solution.py:605
  68.3 1.7 %collective-permute-done.10.b = bf16[16,384]{1,0:T(8,128)(2,1)S(1)} collective-permute-done((bf16[16,384]{1,0:T(8,128)(2,1)S(1)}, bf16[16,384]{1,0:T(8,128)(2,1)S(1)}, u32[]{:S(2)}, u32[]{:S(2)}) %collective-permute-start.10) | collective-permute-done | bytes 12320 | tf_op jit(solution)/shard_map/ppermute | solution.py:605
  69.9 0.5 collective-permute-done.11.c
  70.4 0.1 collective-permute-start.12
  70.5 2.8 %collective-permute-done.12.refs_3_ = bf16[640,768]{1,0:T(8,128)(2,1)S(1)} collective-permute-done((bf16[640,768]{1,0:T(8,128)(2,1)}, bf16[640,768]{1,0:T(8,128)(2,1)S(1)}, u32[]{:S(2)}, u32[]{:S(2)}) %collective-permute-start.12) | collective-permute-done | bytes 983072 | tf_op jit(solution)/shard_map/ppermute | solution.py:428
  73.3 2.2 %terms0.1 = (f32[4,96,384]{2,1,0:T(8,128)S(1)}, bf16[4,96,384]{2,1,0:T(8,128)(2,1)S(1)}) custom-call(bf16[1088,768]{1,0:T(8,128)(2,1)S(1)} %get-tuple-element.70.refs_0_, bf16[704,768]{1,0:T(8,128)(2,1)S(1)} %collective-permute-done.4.refs_1_, bf16[640,768]{1,0:T(8,128)(2,1)} %collective-permute-done.5.refs_2_, ...), custom_call_target="tpu_custom_call" | custom-call | flops 1000 | bytes 1003 | tf_op jit(solution)/shard_map/terms0/pallas_call | solution.py:638
  75.5 1.1 collective-permute-start.13
  76.6 2.2 %terms1.1 = (f32[4,96,384]{2,1,0:T(8,128)S(1)}, bf16[4,96,384]{2,1,0:T(8,128)(2,1)S(1)}) custom-call(bf16[1088,768]{1,0:T(8,128)(2,1)S(1)} %get-tuple-element.70.refs_0_, bf16[704,768]{1,0:T(8,128)(2,1)S(1)} %collective-permute-done.4.refs_1_, bf16[640,768]{1,0:T(8,128)(2,1)} %collective-permute-done.5.refs_2_, ...), custom_call_target="tpu_custom_call" | custom-call | flops 1000 | bytes 1003 | tf_op jit(solution)/shard_map/terms1/pallas_call | solution.py:638
  78.9 1.1 collective-permute-start.17
  80.0 7.5 %mix.1.normed_ref = bf16[1024,384]{1,0:T(8,128)(2,1)S(1)} custom-call(bf16[1024,384]{1,0:T(8,128)(2,1)S(1)} %get-tuple-element.86.grid.grid_ref, bf16[96,384]{1,0:T(8,128)(2,1)S(1)} %collective-permute-done.7.left, bf16[96,384]{1,0:T(8,128)(2,1)S(1)} %collective-permute-done.8.right, bf16[96,384]{1,0:T(8,128)(2,1)S(1)} %collective-permute-done.9.a, ...), custom_call_target="tpu_custom_call" | custom-call | flops 1000 | bytes 1003 | tf_op jit(solution)/shard_map/mix/pallas_call | solution.py:652
  87.4 0.1 line0.1
  87.6 4.8 %collective-permute-start.15 = (bf16[96,384]{1,0:T(8,128)(2,1)S(1)}, bf16[96,384]{1,0:T(8,128)(2,1)S(1)}, u32[]{:S(2)}, u32[]{:S(2)}) collective-permute-start(bf16[96,384]{1,0:T(8,128)(2,1)S(1)} %get-tuple-element.96), channel_id=1, source_target_pairs={{0,8},{4,12},{8,0},{12,4},{1,9},{5,13},{9,1},{13,5},{2,10},{6,14},... | collective-permute-start | bytes 221192 | tf_op jit(solution)/shard_map/ppermute | solution.py:433
  92.4 0.1 line1.1
  92.5 2.1 %collective-permute-start.18 = (bf16[96,384]{1,0:T(8,128)(2,1)S(1)}, bf16[96,384]{1,0:T(8,128)(2,1)S(1)}, u32[]{:S(2)}, u32[]{:S(2)}) collective-permute-start(bf16[96,384]{1,0:T(8,128)(2,1)S(1)} %get-tuple-element.102), channel_id=1, source_target_pairs={{0,4},{4,8},{8,12},{12,0},{1,5},{5,9},{9,13},{13,1},{2,6},{6,10},{... | collective-permute-start | bytes 221192 | tf_op jit(solution)/shard_map/ppermute | solution.py:433
  94.5 1.4 %collective-permute-start.19 = (bf16[96,384]{1,0:T(8,128)(2,1)S(1)}, bf16[96,384]{1,0:T(8,128)(2,1)S(1)}, u32[]{:S(2)}, u32[]{:S(2)}) collective-permute-start(bf16[96,384]{1,0:T(8,128)(2,1)S(1)} %get-tuple-element.103), channel_id=1, source_target_pairs={{0,8},{4,12},{8,0},{12,4},{1,9},{5,13},{9,1},{13,5},{2,10},{6,14},... | collective-permute-start | bytes 221192 | tf_op jit(solution)/shard_map/ppermute | solution.py:433
  95.9 1.1 collective-permute-start.20
  97.0 3.4 %feed.1 = f32[1024,128]{1,0:T(8,128)} custom-call(bf16[1024,384]{1,0:T(8,128)(2,1)S(1)} %mix.1.normed_ref, bf16[1024,384]{1,0:T(8,128)(2,1)S(1)} %get-tuple-element.86.grid.grid_ref, bf16[384,768]{1,0:T(8,128)(2,1)S(1)} %copy-done.4, bf16[768,384]{1,0:T(8,128)(2,1)S(1)} %copy-done.5, bf16[384,128]{1,0:T(8,128)(2,1)S(1)} %copy-done.7), custom_call_target="tpu_custom_call" | custom-call | flops 1000 | bytes 1003 | tf_op jit(solution)/shard_map/feed/pallas_call | solution.py:680
  100.4 3.0 %collective-permute-done.19.refs_6_ = bf16[96,384]{1,0:T(8,128)(2,1)S(1)} collective-permute-done((bf16[96,384]{1,0:T(8,128)(2,1)S(1)}, bf16[96,384]{1,0:T(8,128)(2,1)S(1)}, u32[]{:S(2)}, u32[]{:S(2)}) %collective-permute-start.19) | collective-permute-done | bytes 73760 | tf_op jit(solution)/shard_map/ppermute | solution.py:433
  103.4 0.1 close.1.own_ref
  103.5 1.6 %collective-permute-start.22 = (bf16[96,768]{1,0:T(8,128)(2,1)S(1)}, bf16[96,768]{1,0:T(8,128)(2,1)S(1)}, u32[]{:S(2)}, u32[]{:S(2)}) collective-permute-start(bf16[96,768]{1,0:T(8,128)(2,1)S(1)} %close.1.own_ref), channel_id=1, source_target_pairs={{0,2},{1,3},{2,0},{3,1},{4,6},{5,7},{6,4},{7,5},{8,10},{9,11},{10,... | collective-permute-start | bytes 442376 | tf_op jit(solution)/shard_map/ppermute | solution.py:428
  105.1 4.2 %collective-permute-done.22.two_ref = bf16[96,768]{1,0:T(8,128)(2,1)S(1)} collective-permute-done((bf16[96,768]{1,0:T(8,128)(2,1)S(1)}, bf16[96,768]{1,0:T(8,128)(2,1)S(1)}, u32[]{:S(2)}, u32[]{:S(2)}) %collective-permute-start.22) | collective-permute-done | bytes 147488 | tf_op jit(solution)/shard_map/ppermute | solution.py:428
  109.2 1.4 %collective-permute-done.23.three_ref = bf16[96,768]{1,0:T(8,128)(2,1)S(1)} collective-permute-done((bf16[96,768]{1,0:T(8,128)(2,1)S(1)}, bf16[96,768]{1,0:T(8,128)(2,1)S(1)}, u32[]{:S(2)}, u32[]{:S(2)}) %collective-permute-start.23) | collective-permute-done | bytes 147488 | tf_op jit(solution)/shard_map/ppermute | solution.py:428
  110.6 1.1 spread.1
  (56 shorter events, 0.2 us)
Async XLA Ops:
  0.6 1.4 %copy-start.1 = (bf16[1,32,32,768]{3,2,1,0:T(8,128)(2,1)S(1)}, bf16[1,32,32,768]{3,2,1,0:T(8,128)(2,1)}, u32[]{:S(2)}) copy-start(bf16[1,32,32,768]{3,2,1,0:T(8,128)(2,1)} %param.15) | copy-start | bytes 4718596
  2.0 0.7 copy-start.9
  2.7 8.9 %copy-start.2 = (bf16[768,768]{1,0:T(8,128)(2,1)S(1)}, bf16[768,768]{1,0:T(8,128)(2,1)}, u32[]{:S(2)}) copy-start(bf16[768,768]{1,0:T(8,128)(2,1)} %wout_ref.3) | copy-start | bytes 3538948
  2.7 8.9 %copy-start.6 = (bf16[1,1,1,256,768]{4,3,2,1,0:T(8,128)(2,1)S(1)}, bf16[1,1,1,256,768]{4,3,2,1,0:T(8,128)(2,1)}, u32[]{:S(2)}) copy-start(bf16[1,1,1,256,768]{4,3,2,1,0:T(8,128)(2,1)} %param.19) | copy-start | bytes 1179652
  4.4 21.9 %all-to-all-start = ((bf16[8,40,768]{2,1,0:T(8,128)(2,1)}), bf16[8,40,768]{2,1,0:T(8,128)(2,1)S(1)}, u32[]{:S(2)}, u32[]{:S(2)}) async-start(bf16[8,40,768]{2,1,0:T(8,128)(2,1)} %bitcast.4), calls=%async_computation | async-start | bytes 983040 | tf_op jit(solution)/shard_map/all_to_all | solution.py:480
  11.7 2.0 %copy-start = (bf16[768,2304]{1,0:T(8,128)(2,1)S(1)}, bf16[768,2304]{1,0:T(8,128)(2,1)}, u32[]{:S(2)}) copy-start(bf16[768,2304]{1,0:T(8,128)(2,1)} %wqkv_ref.1) | copy-start | bytes 10616836
  13.7 12.7 %copy-start.16 = (s32[1,1,1,256]{3,2,1,0:T(1,128)S(1)}, s32[1,1,1,256]{3,2,1,0:T(1,128)}, u32[]{:S(2)}) copy-start(s32[1,1,1,256]{3,2,1,0:T(1,128)} %param.17) | copy-start | bytes 3076
  15.2 1.8 %copy-start.13 = (bf16[2304,768]{1,0:T(8,128)(2,1)}, bf16[2304,768]{1,0:T(8,128)(2,1)S(1)}, u32[]{:S(2)}) copy-start(bf16[2304,768]{1,0:T(8,128)(2,1)S(1)} %get-tuple-element.58.wqkv_t_ref) | copy-start | bytes 10616836
  16.9 15.1 %collective-permute-start = (bf16[192,256]{1,0:T(8,128)(2,1)}, bf16[192,256]{1,0:T(8,128)(2,1)S(1)}, u32[]{:S(2)}, u32[]{:S(2)}) collective-permute-start(bf16[192,256]{1,0:T(8,128)(2,1)} %get-tuple-element.67), channel_id=1, source_target_pairs={{0,1},{1,0},{2,3},{3,2},{4,5},{5,4},{6,7},{7,6},{8,9},{9,8},{10,11... | collective-permute-start | bytes 294920 | tf_op jit(solution)/shard_map/ppermute | solution.py:428
  16.9 15.1 %collective-permute-start.1 = (bf16[192,256]{1,0:T(8,128)(2,1)}, bf16[192,256]{1,0:T(8,128)(2,1)S(1)}, u32[]{:S(2)}, u32[]{:S(2)}) collective-permute-start(bf16[192,256]{1,0:T(8,128)(2,1)} %get-tuple-element.68), channel_id=1, source_target_pairs={{0,2},{1,3},{2,0},{3,1},{4,6},{5,7},{6,4},{7,5},{8,10},{9,11},{10,... | collective-permute-start | bytes 294920 | tf_op jit(solution)/shard_map/ppermute | solution.py:428
  18.4 13.6 %collective-permute-start.2 = (bf16[192,256]{1,0:T(8,128)(2,1)S(1)}, bf16[192,256]{1,0:T(8,128)(2,1)S(1)}, u32[]{:S(2)}, u32[]{:S(2)}) collective-permute-start(bf16[192,256]{1,0:T(8,128)(2,1)S(1)} %get-tuple-element.69), channel_id=1, source_target_pairs={{0,3},{1,2},{2,1},{3,0},{4,7},{5,6},{6,5},{7,4},{8,11},{9,10},{10,... | collective-permute-start | bytes 294920 | tf_op jit(solution)/shard_map/ppermute | solution.py:428
  26.3 2.0 %copy-start.14 = (bf16[2304,768]{1,0:T(8,128)(2,1)S(1)}, bf16[2304,768]{1,0:T(8,128)(2,1)}, u32[]{:S(2)}) copy-start(bf16[2304,768]{1,0:T(8,128)(2,1)} %copy-done.13) | copy-start | bytes 10616836
  28.3 3.7 %copy-start.3 = (bf16[768,768]{1,0:T(8,128)(2,1)S(1)}, bf16[768,768]{1,0:T(8,128)(2,1)}, u32[]{:S(2)}) copy-start(bf16[768,768]{1,0:T(8,128)(2,1)} %wout_ref.3) | copy-start | bytes 3538948
  28.3 3.7 %copy-start.15 = (bf16[768,384]{1,0:T(8,128)(2,1)S(1)}, bf16[768,384]{1,0:T(8,128)(2,1)}, u32[]{:S(2)}) copy-start(bf16[768,384]{1,0:T(8,128)(2,1)} %wdec_ref.1) | copy-start | bytes 1769476
  28.3 3.7 %copy-start.17 = (s32[1,1,1,256]{3,2,1,0:T(1,128)S(1)}, s32[1,1,1,256]{3,2,1,0:T(1,128)}, u32[]{:S(2)}) copy-start(s32[1,1,1,256]{3,2,1,0:T(1,128)} %param.18) | copy-start | bytes 3076
  28.4 3.7 %copy-start.18 = (f32[12]{0:T(128)S(1)}, f32[12]{0:T(128)}, u32[]{:S(2)}) copy-start(f32[12]{0:T(128)} %scale_ref.1) | copy-start | bytes 148
  30.4 10.9 %collective-permute-start.3 = (bf16[256,768]{1,0:T(8,128)(2,1)S(1)}, bf16[256,768]{1,0:T(8,128)(2,1)S(1)}, u32[]{:S(2)}, u32[]{:S(2)}) collective-permute-start(bf16[256,768]{1,0:T(8,128)(2,1)S(1)} %get-tuple-element.65.normed_ref), channel_id=1, source_target_pairs={{0,2},{1,3},{2,0},{3,1},{4,6},{5,7},{6,4},{7,5},{8,10},{9,11},{10,... | collective-permute-start | bytes 1179656 | tf_op jit(solution)/shard_map/ppermute | solution.py:428
  32.0 24.0 %copy-start.10 = (s32[1,1,1,8,35]{4,3,2,1,0:T(8,128)S(1)}, s32[1,1,1,8,35]{4,3,2,1,0:T(8,128)}, u32[]{:S(2)}) copy-start(s32[1,1,1,8,35]{4,3,2,1,0:T(8,128)} %param.16) | copy-start | bytes 3364
  32.0 24.0 %copy-start.11 = (f32[2,1408]{1,0:T(2,128)S(1)}, f32[2,1408]{1,0:T(2,128)}, u32[]{:S(2)}) copy-start(f32[2,1408]{1,0:T(2,128)} %constant.2.clone.ids_ref) | copy-start | bytes 33796
  41.3 14.7 %collective-permute-start.4 = (bf16[704,768]{1,0:T(8,128)(2,1)}, bf16[704,768]{1,0:T(8,128)(2,1)S(1)}, u32[]{:S(2)}, u32[]{:S(2)}) collective-permute-start(bf16[704,768]{1,0:T(8,128)(2,1)} %get-tuple-element.73), channel_id=1, source_target_pairs={{0,1},{1,0},{2,3},{3,2},{4,5},{5,4},{6,7},{7,6},{8,9},{9,8},{10,11... | collective-permute-start | bytes 3244040 | tf_op jit(solution)/shard_map/ppermute | solution.py:428
  41.3 24.5 %collective-permute-start.5 = (bf16[640,768]{1,0:T(8,128)(2,1)}, bf16[640,768]{1,0:T(8,128)(2,1)}, u32[]{:S(2)}, u32[]{:S(2)}) collective-permute-start(bf16[640,768]{1,0:T(8,128)(2,1)} %get-tuple-element.74), channel_id=1, source_target_pairs={{0,2},{1,3},{2,0},{3,1},{4,6},{5,7},{6,4},{7,5},{8,10},{9,11},{10,... | collective-permute-start | bytes 2949128 | tf_op jit(solution)/shard_map/ppermute | solution.py:428
  41.8 14.2 %all-to-all-start.1 = ((bf16[8,40,384]{2,1,0:T(8,128)(2,1)}), bf16[8,40,384]{2,1,0:T(8,128)(2,1)}, u32[]{:S(2)}, u32[]{:S(2)}) async-start(bf16[8,40,384]{2,1,0:T(8,128)(2,1)} %bitcast.7), calls=%async_computation.1 | async-start | bytes 491520 | tf_op jit(solution)/shard_map/all_to_all | solution.py:552
  45.9 10.1 %collective-permute-start.6 = (bf16[256,768]{1,0:T(8,128)(2,1)S(1)}, bf16[256,768]{1,0:T(8,128)(2,1)S(1)}, u32[]{:S(2)}, u32[]{:S(2)}) collective-permute-start(bf16[256,768]{1,0:T(8,128)(2,1)S(1)} %collective-permute-done.3.refs_4_), channel_id=1, source_target_pairs={{0,1},{1,0},{2,3},{3,2},{4,5},{5,4},{6,7},{7,6},{8,9},{9,8},{10,11... | collective-permute-start | bytes 1179656 | tf_op jit(solution)/shard_map/ppermute | solution.py:428
  56.0 0.7 copy-start.12
  59.1 11.3 %collective-permute-start.7 = (bf16[96,384]{1,0:T(8,128)(2,1)S(1)}, bf16[96,384]{1,0:T(8,128)(2,1)S(1)}, u32[]{:S(2)}, u32[]{:S(2)}) collective-permute-start(bf16[96,384]{1,0:T(8,128)(2,1)S(1)} %get-tuple-element.78), channel_id=1, source_target_pairs={{0,4},{4,8},{8,12},{12,0},{1,5},{5,9},{9,13},{13,1},{2,6},{6,10},{... | collective-permute-start | bytes 221192 | tf_op jit(solution)/shard_map/ppermute | solution.py:433
  59.2 11.2 %collective-permute-start.8 = (bf16[96,384]{1,0:T(8,128)(2,1)S(1)}, bf16[96,384]{1,0:T(8,128)(2,1)S(1)}, u32[]{:S(2)}, u32[]{:S(2)}) collective-permute-start(bf16[96,384]{1,0:T(8,128)(2,1)S(1)} %get-tuple-element.79), channel_id=1, source_target_pairs={{0,12},{4,0},{8,4},{12,8},{1,13},{5,1},{9,5},{13,9},{2,14},{6,2},{... | collective-permute-start | bytes 221192 | tf_op jit(solution)/shard_map/ppermute | solution.py:433
  63.0 7.4 %collective-permute-start.9 = (bf16[96,384]{1,0:T(8,128)(2,1)S(1)}, bf16[96,384]{1,0:T(8,128)(2,1)S(1)}, u32[]{:S(2)}, u32[]{:S(2)}) collective-permute-start(bf16[96,384]{1,0:T(8,128)(2,1)S(1)} %get-tuple-element.80), channel_id=1, source_target_pairs={{0,16},{4,20},{8,24},{12,28},{16,0},{20,4},{24,8},{28,12},{1,17},{... | collective-permute-start | bytes 221192 | tf_op jit(solution)/shard_map/ppermute | solution.py:605
  63.5 6.4 %collective-permute-start.10 = (bf16[16,384]{1,0:T(8,128)(2,1)S(1)}, bf16[16,384]{1,0:T(8,128)(2,1)S(1)}, u32[]{:S(2)}, u32[]{:S(2)}) collective-permute-start(bf16[16,384]{1,0:T(8,128)(2,1)S(1)} %get-tuple-element.81), channel_id=1, source_target_pairs={{0,20},{4,24},{8,28},{12,16},{16,4},{20,8},{24,12},{28,0},{1,21},{... | collective-permute-start | bytes 36872 | tf_op jit(solution)/shard_map/ppermute | solution.py:605
  65.8 4.6 %collective-permute-start.11 = (bf16[16,384]{1,0:T(8,128)(2,1)S(1)}, bf16[16,384]{1,0:T(8,128)(2,1)S(1)}, u32[]{:S(2)}, u32[]{:S(2)}) collective-permute-start(bf16[16,384]{1,0:T(8,128)(2,1)S(1)} %get-tuple-element.82), channel_id=1, source_target_pairs={{0,28},{4,16},{8,20},{12,24},{16,12},{20,0},{24,4},{28,8},{1,29},{... | collective-permute-start | bytes 36872 | tf_op jit(solution)/shard_map/ppermute | solution.py:605
  70.4 2.8 %collective-permute-start.12 = (bf16[640,768]{1,0:T(8,128)(2,1)}, bf16[640,768]{1,0:T(8,128)(2,1)S(1)}, u32[]{:S(2)}, u32[]{:S(2)}) collective-permute-start(bf16[640,768]{1,0:T(8,128)(2,1)} %collective-permute-done.5.refs_2_), channel_id=1, source_target_pairs={{0,1},{1,0},{2,3},{3,2},{4,5},{5,4},{6,7},{7,6},{8,9},{9,8},{10,11... | collective-permute-start | bytes 2949128 | tf_op jit(solution)/shard_map/ppermute | solution.py:428
  75.5 4.4 %copy-start.8 = (f32[7,7,384]{2,1,0:T(8,128)S(1)}, f32[7,7,384]{2,1,0:T(8,128)}, u32[]{:S(2)}) copy-start(f32[7,7,384]{2,1,0:T(8,128)} %taps.1) | copy-start | bytes 225796
  75.5 11.9 %collective-permute-start.13 = (bf16[4,96,384]{2,1,0:T(8,128)(2,1)S(1)}, bf16[4,96,384]{2,1,0:T(8,128)(2,1)S(1)}, u32[]{:S(2)}, u32[]{:S(2)}) collective-permute-start(bf16[4,96,384]{2,1,0:T(8,128)(2,1)S(1)} %get-tuple-element.85), channel_id=1, source_target_pairs={{0,16},{16,0},{1,17},{17,1},{2,18},{18,2},{3,19},{19,3},{4,20},{20... | collective-permute-start | bytes 884744 | tf_op jit(solution)/shard_map/ppermute | solution.py:433
  78.9 13.5 %collective-permute-start.17 = (bf16[4,96,384]{2,1,0:T(8,128)(2,1)S(1)}, bf16[4,96,384]{2,1,0:T(8,128)(2,1)S(1)}, u32[]{:S(2)}, u32[]{:S(2)}) collective-permute-start(bf16[4,96,384]{2,1,0:T(8,128)(2,1)S(1)} %get-tuple-element.98), channel_id=1, source_target_pairs={{0,16},{16,0},{1,17},{17,1},{2,18},{18,2},{3,19},{19,3},{4,20},{20... | collective-permute-start | bytes 884744 | tf_op jit(solution)/shard_map/ppermute | solution.py:433
  79.9 17.0 %copy-start.4 = (bf16[384,768]{1,0:T(8,128)(2,1)S(1)}, bf16[384,768]{1,0:T(8,128)(2,1)}, u32[]{:S(2)}) copy-start(bf16[384,768]{1,0:T(8,128)(2,1)} %up_ref.1) | copy-start | bytes 1769476
  79.9 17.0 %copy-start.5 = (bf16[768,384]{1,0:T(8,128)(2,1)S(1)}, bf16[768,384]{1,0:T(8,128)(2,1)}, u32[]{:S(2)}) copy-start(bf16[768,384]{1,0:T(8,128)(2,1)} %down_ref.1) | copy-start | bytes 1769476
  80.0 17.0 %copy-start.7 = (bf16[384,128]{1,0:T(8,128)(2,1)S(1)}, bf16[384,128]{1,0:T(8,128)(2,1)}, u32[]{:S(2)}) copy-start(bf16[384,128]{1,0:T(8,128)(2,1)} %head_ref.1) | copy-start | bytes 294916
  87.5 8.4 %collective-permute-start.14 = (bf16[96,384]{1,0:T(8,128)(2,1)S(1)}, bf16[96,384]{1,0:T(8,128)(2,1)S(1)}, u32[]{:S(2)}, u32[]{:S(2)}) collective-permute-start(bf16[96,384]{1,0:T(8,128)(2,1)S(1)} %get-tuple-element.95), channel_id=1, source_target_pairs={{0,4},{4,8},{8,12},{12,0},{1,5},{5,9},{9,13},{13,1},{2,6},{6,10},{... | collective-permute-start | bytes 221192 | tf_op jit(solution)/shard_map/ppermute | solution.py:433
  87.6 12.8 %collective-permute-start.15 = (bf16[96,384]{1,0:T(8,128)(2,1)S(1)}, bf16[96,384]{1,0:T(8,128)(2,1)S(1)}, u32[]{:S(2)}, u32[]{:S(2)}) collective-permute-start(bf16[96,384]{1,0:T(8,128)(2,1)S(1)} %get-tuple-element.96), channel_id=1, source_target_pairs={{0,8},{4,12},{8,0},{12,4},{1,9},{5,13},{9,1},{13,5},{2,10},{6,14},... | collective-permute-start | bytes 221192 | tf_op jit(solution)/shard_map/ppermute | solution.py:433
  92.4 8.0 %collective-permute-start.16 = (bf16[96,384]{1,0:T(8,128)(2,1)S(1)}, bf16[96,384]{1,0:T(8,128)(2,1)S(1)}, u32[]{:S(2)}, u32[]{:S(2)}) collective-permute-start(bf16[96,384]{1,0:T(8,128)(2,1)S(1)} %get-tuple-element.97), channel_id=1, source_target_pairs={{0,12},{4,0},{8,4},{12,8},{1,13},{5,1},{9,5},{13,9},{2,14},{6,2},{... | collective-permute-start | bytes 221192 | tf_op jit(solution)/shard_map/ppermute | solution.py:433
  92.5 7.9 %collective-permute-start.18 = (bf16[96,384]{1,0:T(8,128)(2,1)S(1)}, bf16[96,384]{1,0:T(8,128)(2,1)S(1)}, u32[]{:S(2)}, u32[]{:S(2)}) collective-permute-start(bf16[96,384]{1,0:T(8,128)(2,1)S(1)} %get-tuple-element.102), channel_id=1, source_target_pairs={{0,4},{4,8},{8,12},{12,0},{1,5},{5,9},{9,13},{13,1},{2,6},{6,10},{... | collective-permute-start | bytes 221192 | tf_op jit(solution)/shard_map/ppermute | solution.py:433
  94.5 8.9 %collective-permute-start.19 = (bf16[96,384]{1,0:T(8,128)(2,1)S(1)}, bf16[96,384]{1,0:T(8,128)(2,1)S(1)}, u32[]{:S(2)}, u32[]{:S(2)}) collective-permute-start(bf16[96,384]{1,0:T(8,128)(2,1)S(1)} %get-tuple-element.103), channel_id=1, source_target_pairs={{0,8},{4,12},{8,0},{12,4},{1,9},{5,13},{9,1},{13,5},{2,10},{6,14},... | collective-permute-start | bytes 221192 | tf_op jit(solution)/shard_map/ppermute | solution.py:433
  95.9 7.5 %collective-permute-start.20 = (bf16[96,384]{1,0:T(8,128)(2,1)S(1)}, bf16[96,384]{1,0:T(8,128)(2,1)S(1)}, u32[]{:S(2)}, u32[]{:S(2)}) collective-permute-start(bf16[96,384]{1,0:T(8,128)(2,1)S(1)} %get-tuple-element.104), channel_id=1, source_target_pairs={{0,12},{4,0},{8,4},{12,8},{1,13},{5,1},{9,5},{13,9},{2,14},{6,2},{... | collective-permute-start | bytes 221192 | tf_op jit(solution)/shard_map/ppermute | solution.py:433
  103.5 5.7 %collective-permute-start.22 = (bf16[96,768]{1,0:T(8,128)(2,1)S(1)}, bf16[96,768]{1,0:T(8,128)(2,1)S(1)}, u32[]{:S(2)}, u32[]{:S(2)}) collective-permute-start(bf16[96,768]{1,0:T(8,128)(2,1)S(1)} %close.1.own_ref), channel_id=1, source_target_pairs={{0,2},{1,3},{2,0},{3,1},{4,6},{5,7},{6,4},{7,5},{8,10},{9,11},{10,... | collective-permute-start | bytes 442376 | tf_op jit(solution)/shard_map/ppermute | solution.py:428
  105.1 4.2 %collective-permute-start.21 = (bf16[96,768]{1,0:T(8,128)(2,1)S(1)}, bf16[96,768]{1,0:T(8,128)(2,1)S(1)}, u32[]{:S(2)}, u32[]{:S(2)}) collective-permute-start(bf16[96,768]{1,0:T(8,128)(2,1)S(1)} %close.1.own_ref), channel_id=1, source_target_pairs={{0,1},{1,0},{2,3},{3,2},{4,5},{5,4},{6,7},{7,6},{8,9},{9,8},{10,11... | collective-permute-start | bytes 442376 | tf_op jit(solution)/shard_map/ppermute | solution.py:428
  109.2 1.4 %collective-permute-start.23 = (bf16[96,768]{1,0:T(8,128)(2,1)S(1)}, bf16[96,768]{1,0:T(8,128)(2,1)S(1)}, u32[]{:S(2)}, u32[]{:S(2)}) collective-permute-start(bf16[96,768]{1,0:T(8,128)(2,1)S(1)} %collective-permute-done.22.two_ref), channel_id=1, source_target_pairs={{0,1},{1,0},{2,3},{3,2},{4,5},{5,4},{6,7},{7,6},{8,9},{9,8},{10,11... | collective-permute-start | bytes 442376 | tf_op jit(solution)/shard_map/ppermute | solution.py:428

commit v6 on v3

--- a/solution.py
+++ b/solution.py
@@ -31,7 +31,7 @@
     return pl.BlockSpec(memory_space=pltpu.SMEM)
 
 
-def call(kernel, name, outs, in_specs, scratch=(), flops=0, nbytes=0, limit=20):
+def call(kernel, name, outs, in_specs, scratch=(), flops=0, nbytes=0, limit=20, cost=1000):
     single = not isinstance(outs, (list, tuple))
     out_list = [outs] if single else list(outs)
     specs = [vmem() for _ in out_list]
@@ -42,7 +42,9 @@
         out_specs=specs[0] if single else tuple(specs),
         scratch_shapes=list(scratch),
         compiler_params=pltpu.CompilerParams(vmem_limit_bytes=limit * MIB),
-        cost_estimate=pl.CostEstimate(flops=flops, bytes_accessed=nbytes, transcendentals=0),
+        cost_estimate=pl.CostEstimate(
+            flops=cost, bytes_accessed=1000 + cost // 300, transcendentals=0
+        ),
         name=name,
     )
 
@@ -70,20 +72,13 @@
     out_ref[...] = mm(chosen, tok_ref[...]).astype(bf16)
 
 
-def prep_kernel(split, cot_ref, wout_ref, wqkv_ref, ga_ref, wqkv_t_ref, *refs):
+def prep_kernel(cot_ref, wout_ref, wqkv_ref, ga_ref, wqkv_t_ref):
     ga_ref[...] = mm(wout_ref[...], cot_ref[...], NT).astype(bf16)
-    emit(split, refs[-1], 0, jnp.transpose(cot_ref[...]))
-    deal(split, refs[-1], refs[:-1])
     wqkv_t_ref[...] = jnp.transpose(wqkv_ref[...])
 
 
-def project_kernel(
-    cap, padded, src_ref, arr_ref, wqkv_t_ref, normed_ref, enc_ref, u_ref, len_ref, v_ref,
-    place_ref,
-):
-    rows, width = normed_ref.shape
-    heads = len_ref.shape[0] // 2
-    size = width // heads
+def norm_kernel(cap, padded, src_ref, arr_ref, normed_ref, enc_ref, place_ref):
+    rows = normed_ref.shape[0]
     slots = arr_ref.shape[0]
     src = src_ref[...].astype(f32)
     slot_row = src + (padded - cap) * jnp.floor((src + 0.5) * (1.0 / cap))
@@ -95,8 +90,14 @@
     enc_ref[...] = enc_in.astype(bf16)
     centred = enc_in - jnp.mean(enc_in, axis=-1, keepdims=True)
     spread = jnp.mean(centred * centred, axis=-1, keepdims=True)
-    normed = (centred * lax.rsqrt(spread + norm_eps)).astype(bf16)
-    normed_ref[...] = normed
+    normed_ref[...] = (centred * lax.rsqrt(spread + norm_eps)).astype(bf16)
+
+
+def project_kernel(normed_ref, wqkv_t_ref, u_ref, len_ref, v_ref):
+    normed = normed_ref[...]
+    width = normed.shape[1]
+    heads = len_ref.shape[0] // 2
+    size = width // heads
     for t in range(2):
         raw = mm(wqkv_t_ref[t * width : (t + 1) * width], normed, NT)
         for h in range(heads):
@@ -110,11 +111,11 @@
 
 def encode_kernel(
     split, win_ref, scale_ref, place_ref, enc_ref, u_ref, len_ref, v_ref, ga_ref, wout_ref,
-    wdec_ref, out_ref, e_ref, *refs,
+    wdec_ref, out_ref, *refs,
 ):
-    left_refs = refs[:-3]
+    peer_refs = refs[:-3]
     p_ref, att_ref, left_ref = refs[-3:]
-    rows, width = e_ref.shape
+    rows, width = enc_ref.shape
     heads = p_ref.shape[0]
     size = width // heads
     slots = out_ref.shape[0]
@@ -128,9 +129,10 @@
         raised = jnp.where(same, jnp.exp(scores * scale_ref[h]), 0.0)
         weights = (raised * (1.0 / jnp.sum(raised, axis=0, keepdims=True))).astype(bf16)
         p_ref[h] = weights
-        att_ref[lo:hi] = mm(v_ref[lo:hi], weights).astype(bf16)
+        att = mm(v_ref[lo:hi], weights).astype(bf16)
+        att_ref[lo:hi] = att
+        emit(split, left_ref, 3 * width + lo, att)
     attended = jnp.transpose(att_ref[...])
-    e_ref[...] = attended
     enc_out = (enc_ref[...].astype(f32) + mm(attended, wout_ref[...])).astype(bf16)
     dec = mm(enc_out, wdec_ref[...]).astype(bf16)
     places = lax.broadcasted_iota(jnp.int32, (slots, rows), 0).astype(f32)
@@ -157,16 +159,9 @@
         emit(split, left_ref, lo, grad_q.astype(bf16))
         emit(split, left_ref, width + lo, grad_k.astype(bf16))
         emit(split, left_ref, 2 * width + lo, grad_v.astype(bf16))
-    deal(split, left_ref, left_refs)
-
-
-def deal(split, left_ref, left_refs):
-    if split is None:
-        left_refs[0][...] = left_ref[...]
-        return
-    me = lax.axis_index("replica")
-    for n, ref in enumerate(left_refs):
-        ref[...] = left_ref[me ^ n]
+    me = lax.axis_index("replica") if split is not None else 0
+    for n, ref in enumerate(peer_refs):
+        ref[...] = left_ref[me ^ n] if split is not None else left_ref[...]
 
 
 def emit(split, out_ref, start, block):
@@ -174,35 +169,41 @@
         out_ref[start : start + block.shape[0]] = block
         return
     unit = 32
-    per_shard, per_part = split[0] // unit, split[1] // unit
+    shard_rows, part_rows, qkv_rows = split
     for j in range(block.shape[0] // unit):
-        shard, rest = divmod(start // unit + j, per_shard)
-        part, place = divmod(rest, per_part)
-        out_ref[part, shard, place * unit : (place + 1) * unit] = block[
-            j * unit : (j + 1) * unit
-        ]
-
-
-def term_kernel(columns, *refs):
-    lefts, cots, normed, attended = refs[0:4], refs[4:8], refs[8:12], refs[12:16]
-    keep_ref, send_ref = refs[16:]
-    qkv, part, rows = lefts[0].shape
-    shards = qkv + cots[0].shape[0]
-    half = shards // 2
-    cut = slice(*columns)
-    width = columns[1] - columns[0]
-
-    def block(left, lo, hi, right):
+        row = start + j * unit
+        if row < qkv_rows:
+            shard, rest = divmod(row, shard_rows)
+            part, place = divmod(rest, part_rows)
+            at = shard * part_rows + place
+        else:
+            part, place = divmod(row - qkv_rows, qkv_rows // 3 // out_ref.shape[0])
+            at = qkv_rows // out_ref.shape[0] + place
+        out_ref[part, at : at + unit] = block[j * unit : (j + 1) * unit]
+
+
+def term_kernel(c, *refs):
+    lefts, normed, cots = refs[0:4], refs[4:8], refs[8:12]
+    keep_ref, send_ref = refs[12:]
+    half, part, chunk = keep_ref.shape
+    cut = slice(c * chunk, (c + 1) * chunk)
+
+    def block(lo, hi, right, cols):
         acc = None
-        for ref, e in zip(left, right):
-            step = mm(ref[lo:hi].reshape((hi - lo) * part, rows), e[:, cut])
+        for left, e in zip(lefts, right):
+            step = mm(left[lo:hi], e[:, cols])
             acc = step if acc is None else acc + step
-        return acc.reshape(hi - lo, part, width)
-
-    first = [(0, block(lefts, 0, half, normed))]
+        return acc
+
+    rows = half * part
+    first = [(0, block(0, rows, normed, cut).reshape(half, part, chunk))]
+    shared = block(rows, rows + (half - 2) * part, normed, cut).reshape(half - 2, part, chunk)
+    at = rows + (half - 2 + c) * part
+    turned = block(at, at + part, cots, slice(0, 2 * chunk))
     second = [
-        (0, block(lefts, half, qkv, normed)),
-        (qkv - half, block(cots, 0, shards - qkv, attended)),
+        (0, shared),
+        (half - 2, turned[:, 0:chunk].reshape(1, part, chunk)),
+        (half - 1, turned[:, chunk:].reshape(1, part, chunk)),
     ]
     spans = (first, second)
     for mine in range(2):
@@ -233,10 +234,27 @@
         refs[-1][:, n * width : (n + 1) * width] = total.astype(bf16)
 
 
-def spread_kernel(own_ref, one_ref, two_ref, three_ref, out_ref):
+def spread_kernel(own_ref, one_ref, two_ref, three_ref, out_ref, all_ref):
     me = lax.axis_index("replica")
     for n, ref in enumerate((own_ref, one_ref, two_ref, three_ref)):
-        out_ref[me ^ n] = ref[...].astype(f32)
+        all_ref[me ^ n] = ref[...].astype(f32)
+    count, part, width = all_ref.shape
+    chunk = width // 2
+    phis = lax.axis_size("phi")
+    turned = lax.axis_index("eta") * phis + lax.axis_index("phi") >= 2 * phis - 2
+
+    @pl.when(jnp.logical_not(turned))
+    def _():
+        for r in range(count):
+            out_ref[r * part : (r + 1) * part] = all_ref[r]
+
+    @pl.when(turned)
+    def _():
+        pieces = []
+        for r in range(count):
+            for c in range(2):
+                pieces.append(all_ref[r, :, c * chunk : (c + 1) * chunk])
+        out_ref[...] = jnp.transpose(jnp.concatenate(pieces, axis=0))
 
 
 def tie(values, *others):
@@ -374,8 +392,12 @@
     return lax.ppermute(value, axis, [(i, (i + k) % count) for i in range(count)])
 
 
-def summed_slow(left, cot_t, normed, attended):
-    term = jnp.concatenate([mm(left, normed), mm(cot_t, attended)], axis=0)
+def summed_slow(left, normed, cotangent):
+    width = normed.shape[1]
+    term = jnp.concatenate(
+        [mm(left[: 3 * width], normed), mm(cotangent, left[3 * width :], (((0,), (1,)), ((), ())))],
+        axis=0,
+    )
     share = lax.psum_scatter(term, ("eta", "phi", "replica"), scatter_dimension=0, tiled=True)
     return lax.all_gather(share.astype(bf16), "replica", axis=0, tiled=True).astype(f32)
 
@@ -403,8 +425,7 @@
         eta_count == 2
         and replicas == 4
         and part_rows % 32 == 0
-        and width % shard_rows == 0
-        and 3 * width // shard_rows >= group // 2
+        and width == 2 * shard_rows
     )
 
     positions = send_pos.reshape(group, cap)
@@ -424,51 +445,52 @@
     ).reshape(slots, width)
 
     cotangent = enc_cot.reshape(rows, width)
-    split = (shard_rows, part_rows) if fast else None
+    split = (shard_rows, part_rows, 3 * width) if fast else None
     pieces = replicas if fast else 1
-    cot_part = (width // shard_rows, part_rows, rows) if fast else (width, rows)
-    left_part = (3 * width // shard_rows, part_rows, rows) if fast else (3 * width, rows)
-    cot_whole = (replicas,) + cot_part if fast else cot_part
+    left_part = (out_rows // pieces, rows)
     left_whole = (replicas,) + left_part if fast else left_part
-    grad_att, w_qkv_t, *cots = call(
-        functools.partial(prep_kernel, split),
+    if fast:
+        cots = [cotangent, flip(cotangent, "replica", 1), flip(cotangent, "replica", 2)]
+    grad_att, w_qkv_t = call(
+        prep_kernel,
         "prep",
-        [sds((width, rows), bf16), sds((3 * width, width), bf16)]
-        + [sds(cot_part, bf16)] * pieces,
+        [sds((width, rows), bf16), sds((3 * width, width), bf16)],
         [vmem()] * 3,
-        scratch=[pltpu.VMEM(cot_whole, bf16)],
         flops=2 * rows * width * width,
         nbytes=10 * MIB,
         limit=10,
     )(cotangent, w_out, w_qkv)
     if fast:
-        cots = [cots[0]] + [flip(cots[k], "replica", k) for k in range(1, 4)]
-        arrived = tie(arrived, cots)
-
-    normed, enc_in, units, lengths, values, places = call(
-        functools.partial(project_kernel, cap, padded),
+        cots.append(flip(tie(cots[2], w_qkv_t), "replica", 1))
+
+    normed, enc_in, places = call(
+        functools.partial(norm_kernel, cap, padded),
+        "norm",
+        [sds((rows, width), bf16), sds((rows, width), bf16), sds((1, rows), f32)],
+        [vmem()] * 2,
+        flops=2 * rows * width * slots,
+        nbytes=2 * MIB,
+        limit=8,
+        cost=600000000,
+    )(enc_src.reshape(1, rows), arrived)
+    if fast:
+        normed_y = flip(normed, "replica", 2)
+        normed_c = flip(normed, "replica", 1)
+    units, lengths, values = call(
+        project_kernel,
         "project",
-        [
-            sds((rows, width), bf16),
-            sds((rows, width), bf16),
-            sds((2 * width, rows), f32),
-            sds((2 * heads, rows), f32),
-            sds((width, rows), bf16),
-            sds((1, rows), f32),
-        ],
-        [vmem()] * 3,
+        [sds((2 * width, rows), f32), sds((2 * heads, rows), f32), sds((width, rows), bf16)],
+        [vmem()] * 2,
         flops=2 * rows * width * width * 4,
         nbytes=8 * MIB,
         limit=10,
-    )(enc_src.reshape(1, rows), arrived, w_qkv_t)
-    if fast:
-        normed_y = flip(normed, "replica", 2)
-
-    outbound, attended, *lefts = call(
+        cost=2000000000,
+    )(tie(normed, cots) if fast else normed, w_qkv_t)
+
+    outbound, *lefts = call(
         functools.partial(encode_kernel, split),
         "encode",
-        [sds((slots, dec_width), bf16), sds((rows, width), bf16)]
-        + [sds(left_part, bf16)] * pieces,
+        [sds((slots, dec_width), bf16)] + [sds(left_part, bf16)] * pieces,
         [vmem(), smem()] + [vmem()] * 8,
         scratch=[
             pltpu.VMEM((heads, rows, rows), bf16),
@@ -478,24 +500,23 @@
         flops=2 * rows * width * width * 10,
         nbytes=8 * MIB,
         limit=14,
+        cost=8000000000,
     )(
         window_id.reshape(1, rows), head_scale, places, enc_in, units, lengths, values, grad_att,
         w_out, w_dec_in,
     )
+    if fast:
+        *lefts, normed_y, normed_c = lax.optimization_barrier((*lefts, normed_y, normed_c))
     returned = lax.all_to_all(
         outbound.reshape(group, padded, dec_width), ("eta", "phi"), split_axis=0, concat_axis=0,
         tiled=True,
     )
     if fast:
         lefts = [lefts[0]] + [flip(lefts[k], "replica", k) for k in range(1, 4)]
-        attended_y = flip(attended, "replica", 2)
-        normed_y = tie(normed_y, attended)
-        right = [normed, flip(normed, "replica", 1), normed_y, flip(normed_y, "replica", 1)]
-        right += [
-            attended, flip(attended, "replica", 1), attended_y, flip(attended_y, "replica", 1),
-        ]
+        rights = [normed, normed_c, normed_y, flip(normed_y, "replica", 1)]
+        returned = tie(returned, lefts[1], rights[3])
     else:
-        grad_total = summed_slow(lefts[0], cots[0], normed, attended)
+        grad_total = summed_slow(lefts[0], normed, cotangent)
 
     span = conv_kernel.shape[0]
     rim = span // 2
@@ -566,20 +587,20 @@
             flat(bottom), flat(low[far:]), flat(high[far:]),
         )
     if fast:
-        lefts, cots, right = tie((lefts, cots, right), filled)
+        lefts, rights, cots = tie((lefts, rights, cots), left_halo, right_halo, rims)
         chunk = width // 2
         half = group // 2
         kept, sent = [], []
         for c in range(2):
             keep, send = call(
-                functools.partial(term_kernel, (c * chunk, (c + 1) * chunk)),
+                functools.partial(term_kernel, c),
                 "terms%d" % c,
                 [sds((half, part_rows, chunk), f32), sds((half, part_rows, chunk), bf16)],
-                [vmem()] * 16,
+                [vmem()] * 12,
                 flops=2 * out_rows * chunk * rows,
                 nbytes=8 * MIB,
                 limit=10,
-            )(*lefts, *cots, *right)
+            )(*lefts, *rights, *cots)
             kept.append(keep)
             sent.append(turn(send, "eta", 1))
         left, right_halo, rims = tie((left_halo, right_halo, rims), kept)
@@ -637,14 +658,13 @@
         grad_total = call(
             spread_kernel,
             "spread",
-            sds((replicas, part_rows, width), f32),
+            sds((shard_rows, width), f32),
             [vmem()] * 4,
+            scratch=[pltpu.VMEM((replicas, part_rows, width), f32)],
             flops=4 * part_rows * width,
             nbytes=2 * MIB,
-            limit=4,
-        )(
-            mine, flip(mine, "replica", 1), mine_y, flip(mine_y, "replica", 1),
-        ).reshape(shard_rows, width)
+            limit=8,
+        )(mine, flip(mine, "replica", 1), mine_y, flip(mine_y, "replica", 1))
     return (grad_total, reconstruction)
 
 

time: 114 us -> 110 us (0.965)
  waiting for transfers between devices: 30.9 us -> 26 us
  local copies, waits for them, and re-layouts: 9.38 us -> 12.1 us
  starting transfers between devices: 40.2 us -> 38.4 us
    ppermute x15 -> x12, waiting for transfers between devices: 22.4 us -> 12.1 us  [flip(): lax.ppermute(value, axis, [(i, i ^ bit) for i in range(lax.axis_size(axis...]
    all_to_all x1, waiting for transfers between devices: 0.6 us -> 6.64 us  [body(): lax.all_to_all(outbound.reshape(group, padded, dec_width), ('eta', 'phi')...]
    ppermute x10, waiting for transfers between devices: 5.05 us -> 1.88 us  [turn(): lax.ppermute(value, axis, [(i, (i + k) % count) for i in range(count)])]
    ppermute x15 -> x12, starting transfers between devices: 9.3 us -> 6.22 us  [flip(): lax.ppermute(value, axis, [(i, i ^ bit) for i in range(lax.axis_size(axis...]
    ppermute x10, starting transfers between devices: 13.6 us -> 16.2 us  [turn(): lax.ppermute(value, axis, [(i, (i + k) % count) for i in range(count)])]
    unnamed x54 -> x48, local copies, waits for them, and re-layouts: 9.38 us -> 10.8 us
    ppermute x3, starting transfers between devices: 6.03 us -> 4.63 us  [shifted(): return lax.ppermute(value, plane, pairs)]
    ppermute x3, waiting for transfers between devices: 0.01 us -> 1.41 us  [shifted(): return lax.ppermute(value, plane, pairs)]
  transfers between devices with their start and end apart: 30 -> 27, of which waited for: 13 -> 8; matrix products, arithmetic and copies ran while one was open for 0% -> 1% of each run, Pallas kernels for 24% -> 25%
where the time goes in v6:
time: 110 us
  starting transfers between devices  38.4 us (35%)
  Pallas kernels  32.3 us (29%)
  waiting for transfers between devices  26 us (24%)
  local copies, waits for them, and re-layouts  12.1 us (11%)
    ppermute x10, starting transfers between devices, turn(): lax.ppermute(value, axis, [(i, (i + k) % count) for i in range(count)])  16.2 us
    ppermute x12, waiting for transfers between devices, flip(): lax.ppermute(value, axis, [(i, i ^ bit) for i in range(lax.axis_size(axis...  12.1 us
    unnamed x48, local copies, waits for them, and re-layouts  10.8 us
    pallas_call x1, Pallas kernels, body(): call(functools.partial(encode_kernel, split), 'encode', [sds((slots, dec_...  8.52 us
    pallas_call x1, Pallas kernels, body(): call(functools.partial(mix_folded if folded else mix_open, (eta_cells, ph...  7.45 us
    all_to_all x1, starting transfers between devices, body(): lax.all_to_all(outgoing.reshape(group, padded, width), ('eta', 'phi'), sp...  7.25 us
    all_to_all x1, waiting for transfers between devices, body(): lax.all_to_all(outbound.reshape(group, padded, dec_width), ('eta', 'phi')...  6.64 us
    ppermute x12, starting transfers between devices, flip(): lax.ppermute(value, axis, [(i, i ^ bit) for i in range(lax.axis_size(axis...  6.22 us
  transfers between devices with their start and end apart: 27, of which 8 were waited for; matrix products, arithmetic and copies ran while one was open for 1% of the time, Pallas kernels for 25%

profile of v6, /device:TPU:0, one launch (start us, length us, event | category | flops | bytes accessed | tf_op | source)
XLA Modules:
  0.0 109.7 jit_solution(12740141915541633889)
XLA Ops:
  0.6 1.4 %copy-done.2 = bf16[1,32,32,768]{3,2,1,0:T(8,128)(2,1)S(1)} copy-done((bf16[1,32,32,768]{3,2,1,0:T(8,128)(2,1)S(1)}, bf16[1,32,32,768]{3,2,1,0:T(8,128)(2,1)}, u32[]{:S(2)}) %copy-start.2) | copy-done | bytes 1572888
  2.1 0.7 copy-done.9
  2.8 1.7 %pick.1 = bf16[320,768]{1,0:T(8,128)(2,1)} custom-call(s32[8,35]{1,0:T(8,128)S(1)} %bitcast.17, bf16[1024,768]{1,0:T(8,128)(2,1)S(1)} %bitcast.15), custom_call_target="tpu_custom_call" | custom-call | flops 1000 | bytes 1003 | tf_op jit(solution)/shard_map/pick/pallas_call | solution.py:432
  4.5 7.3 %all-to-all-start = ((bf16[8,40,768]{2,1,0:T(8,128)(2,1)}), bf16[8,40,768]{2,1,0:T(8,128)(2,1)S(1)}, u32[]{:S(2)}, u32[]{:S(2)}) async-start(bf16[8,40,768]{2,1,0:T(8,128)(2,1)} %bitcast.4), calls=%async_computation | async-start | bytes 983040 | tf_op jit(solution)/shard_map/all_to_all | solution.py:442
  11.7 1.6 %collective-permute-start.1 = (bf16[256,768]{1,0:T(8,128)(2,1)S(1)}, bf16[256,768]{1,0:T(8,128)(2,1)S(1)}, u32[]{:S(2)}, u32[]{:S(2)}) collective-permute-start(bf16[256,768]{1,0:T(8,128)(2,1)S(1)} %bitcast.10), channel_id=1, source_target_pairs={{0,2},{1,3},{2,0},{3,1},{4,6},{5,7},{6,4},{7,5},{8,10},{9,11},{10,... | collective-permute-start | bytes 1179656 | tf_op jit(solution)/shard_map/ppermute | solution.py:387
  13.3 2.0 %copy-done.1 = bf16[768,2304]{1,0:T(8,128)(2,1)S(1)} copy-done((bf16[768,2304]{1,0:T(8,128)(2,1)S(1)}, bf16[768,2304]{1,0:T(8,128)(2,1)}, u32[]{:S(2)}) %copy-start.1) | copy-done | bytes 3538968
  15.3 1.0 prep.1
  16.3 1.7 %copy-done.13 = bf16[2304,768]{1,0:T(8,128)(2,1)} copy-done((bf16[2304,768]{1,0:T(8,128)(2,1)}, bf16[2304,768]{1,0:T(8,128)(2,1)S(1)}, u32[]{:S(2)}) %copy-start.13) | copy-done | bytes 3538968
  18.1 0.7 copy-done.18
  18.8 3.6 %collective-permute-done.1.refs_10_ = bf16[256,768]{1,0:T(8,128)(2,1)S(1)} collective-permute-done((bf16[256,768]{1,0:T(8,128)(2,1)S(1)}, bf16[256,768]{1,0:T(8,128)(2,1)S(1)}, u32[]{:S(2)}, u32[]{:S(2)}) %collective-permute-start.1) | collective-permute-done | bytes 393248 | tf_op jit(solution)/shard_map/ppermute | solution.py:387
  22.4 4.0 %all-to-all-done = bf16[8,40,768]{2,1,0:T(8,128)(2,1)S(1)} async-done(((bf16[8,40,768]{2,1,0:T(8,128)(2,1)}), bf16[8,40,768]{2,1,0:T(8,128)(2,1)S(1)}, u32[]{:S(2)}, u32[]{:S(2)}) %all-to-all-start) | async-done | bytes 491552 | tf_op jit(solution)/shard_map/all_to_all | solution.py:442
  26.4 0.7 norm.1
  27.2 1.6 %collective-permute-start.3 = (bf16[256,768]{1,0:T(8,128)(2,1)S(1)}, bf16[256,768]{1,0:T(8,128)(2,1)S(1)}, u32[]{:S(2)}, u32[]{:S(2)}) collective-permute-start(bf16[256,768]{1,0:T(8,128)(2,1)S(1)} %get-tuple-element.102.normed_ref.refs_4_), channel_id=1, source_target_pairs={{0,2},{1,3},{2,0},{3,1},{4,6},{5,7},{6,4},{7,5},{8,10},{9,11},{10,... | collective-permute-start | bytes 1179656 | tf_op jit(solution)/shard_map/ppermute | solution.py:387
  28.8 2.0 %copy-done.14 = bf16[2304,768]{1,0:T(8,128)(2,1)S(1)} copy-done((bf16[2304,768]{1,0:T(8,128)(2,1)S(1)}, bf16[2304,768]{1,0:T(8,128)(2,1)}, u32[]{:S(2)}) %copy-start.14) | copy-done | bytes 3538968
  30.8 1.1 %project.1 = (f32[1536,256]{1,0:T(8,128)S(1)}, f32[24,256]{1,0:T(8,128)S(1)}, bf16[768,256]{1,0:T(8,128)(2,1)S(1)}) custom-call(bf16[256,768]{1,0:T(8,128)(2,1)S(1)} %get-tuple-element.102.normed_ref.refs_4_, bf16[2304,768]{1,0:T(8,128)(2,1)S(1)} %copy-done.14), custom_call_target="tpu_custom_call" | custom-call | flops 2000000000 | bytes 6667666 | tf_op jit(solution)/shard_map/project/pallas_call | solution.py:479
  32.0 8.5 %encode.1 = (bf16[320,384]{1,0:T(8,128)(2,1)}, bf16[768,256]{1,0:T(8,128)(2,1)S(1)}, bf16[768,256]{1,0:T(8,128)(2,1)S(1)}, bf16[768,256]{1,0:T(8,128)(2,1)S(1)}, bf16[768,256]{1,0:T(8,128)(2,1)S(1)}) custom-call(s32[1,256]{1,0:T(1,128)S(1)} %bitcast.20, f32[12]{0:T(128)S(1)} %copy-done.23, f32[1,256]{1,0:T(1,128)S(1)} %get-tuple-element.71.place_ref, ...), custom_call_target="tpu_custom_call" | custom-call | flops 8000000000 | bytes 26667666 | tf_op jit(solution)/shard_map/encode/pallas_call | solution.py:490
  40.5 0.7 copy-done.16
  41.3 0.7 copy-done.20
  42.0 4.0 %all-to-all-start.1 = ((bf16[8,40,384]{2,1,0:T(8,128)(2,1)}), bf16[8,40,384]{2,1,0:T(8,128)(2,1)}, u32[]{:S(2)}, u32[]{:S(2)}) async-start(bf16[8,40,384]{2,1,0:T(8,128)(2,1)} %bitcast.7), calls=%async_computation.1 | async-start | bytes 491520 | tf_op jit(solution)/shard_map/all_to_all | solution.py:510
  46.1 0.6 collective-permute-start.5
  46.8 0.5 collective-permute-start.6
  47.3 1.3 %collective-permute-start.7 = (bf16[768,256]{1,0:T(8,128)(2,1)}, bf16[768,256]{1,0:T(8,128)(2,1)}, u32[]{:S(2)}, u32[]{:S(2)}) collective-permute-start(bf16[768,256]{1,0:T(8,128)(2,1)} %copy-done.16), channel_id=1, source_target_pairs={{0,3},{1,2},{2,1},{3,0},{4,7},{5,6},{6,5},{7,4},{8,11},{9,10},{10,... | collective-permute-start | bytes 1179656 | tf_op jit(solution)/shard_map/ppermute | solution.py:387
  48.5 1.3 %reshape.44.mask_ref = bf16[1,384]{1,0:T(2,128)(2,1)} reshape(bf16[384]{0:T(512)(128)(2,1)} %param.24) | data formatting | bytes 1536 | tf_op jit(solution)/shard_map/reshape | solution.py:551
  49.8 6.6 %all-to-all-done.1 = bf16[8,40,384]{2,1,0:T(8,128)(2,1)} async-done(((bf16[8,40,384]{2,1,0:T(8,128)(2,1)}), bf16[8,40,384]{2,1,0:T(8,128)(2,1)}, u32[]{:S(2)}, u32[]{:S(2)}) %all-to-all-start.1) | async-done | bytes 245792 | tf_op jit(solution)/shard_map/all_to_all | solution.py:510
  56.5 0.7 copy-done.12
  57.1 2.4 %fill.1 = (bf16[1024,384]{1,0:T(8,128)(2,1)S(1)}, bf16[96,384]{1,0:T(8,128)(2,1)S(1)}, bf16[96,384]{1,0:T(8,128)(2,1)S(1)}, bf16[96,384]{1,0:T(8,128)(2,1)S(1)},...) custom-call(s32[8,35]{1,0:T(8,128)S(1)} %bitcast.18, f32[2,1408]{1,0:T(2,128)S(1)} %copy-done.11, ...), custom_call_target="tpu_custom_call" | custom-call | flops 1000 | bytes 1003 | tf_op jit(solution)/shard_map/fill/pallas_call | solution.py:541
  59.6 3.8 %collective-permute-start.10 = (bf16[96,384]{1,0:T(8,128)(2,1)S(1)}, bf16[96,384]{1,0:T(8,128)(2,1)S(1)}, u32[]{:S(2)}, u32[]{:S(2)}) collective-permute-start(bf16[96,384]{1,0:T(8,128)(2,1)S(1)} %get-tuple-element.94), channel_id=1, source_target_pairs={{0,12},{4,0},{8,4},{12,8},{1,13},{5,1},{9,5},{13,9},{2,14},{6,2},{... | collective-permute-start | bytes 221192 | tf_op jit(solution)/shard_map/ppermute | solution.py:392
  63.4 0.5 collective-permute-start.11
  64.0 2.5 %collective-permute-done.7.refs_3_ = bf16[768,256]{1,0:T(8,128)(2,1)} collective-permute-done((bf16[768,256]{1,0:T(8,128)(2,1)}, bf16[768,256]{1,0:T(8,128)(2,1)}, u32[]{:S(2)}, u32[]{:S(2)}) %collective-permute-start.7) | collective-permute-done | bytes 393248 | tf_op jit(solution)/shard_map/ppermute | solution.py:387
  66.5 4.1 %collective-permute-start.13 = (bf16[16,384]{1,0:T(8,128)(2,1)S(1)}, bf16[16,384]{1,0:T(8,128)(2,1)S(1)}, u32[]{:S(2)}, u32[]{:S(2)}) collective-permute-start(bf16[16,384]{1,0:T(8,128)(2,1)S(1)} %get-tuple-element.97), channel_id=1, source_target_pairs={{0,28},{4,16},{8,20},{12,24},{16,12},{20,0},{24,4},{28,8},{1,29},{... | collective-permute-start | bytes 36872 | tf_op jit(solution)/shard_map/ppermute | solution.py:563
  70.6 1.4 %collective-permute-done.13.c = bf16[16,384]{1,0:T(8,128)(2,1)S(1)} collective-permute-done((bf16[16,384]{1,0:T(8,128)(2,1)S(1)}, bf16[16,384]{1,0:T(8,128)(2,1)S(1)}, u32[]{:S(2)}, u32[]{:S(2)}) %collective-permute-start.13) | collective-permute-done | bytes 12320 | tf_op jit(solution)/shard_map/ppermute | solution.py:563
  72.0 2.3 %terms0.1 = (f32[4,96,384]{2,1,0:T(8,128)S(1)}, bf16[4,96,384]{2,1,0:T(8,128)(2,1)S(1)}) custom-call(bf16[768,256]{1,0:T(8,128)(2,1)S(1)} %get-tuple-element.98.refs_0_, bf16[768,256]{1,0:T(8,128)(2,1)S(1)} %collective-permute-done.5.refs_1_, bf16[768,256]{1,0:T(8,128)(2,1)} %collective-permute-done.6.refs_2_, ...), custom_call_target="tpu_custom_call" | custom-call | flops 1000 | bytes 1003 | tf_op jit(solution)/shard_map/terms0/pallas_call | solution.py:595
  74.4 0.6 collective-permute-start.14
  74.9 2.3 %terms1.1 = (f32[4,96,384]{2,1,0:T(8,128)S(1)}, bf16[4,96,384]{2,1,0:T(8,128)(2,1)S(1)}) custom-call(bf16[768,256]{1,0:T(8,128)(2,1)S(1)} %get-tuple-element.98.refs_0_, bf16[768,256]{1,0:T(8,128)(2,1)S(1)} %collective-permute-done.5.refs_1_, bf16[768,256]{1,0:T(8,128)(2,1)} %collective-permute-done.6.refs_2_, ...), custom_call_target="tpu_custom_call" | custom-call | flops 1000 | bytes 1003 | tf_op jit(solution)/shard_map/terms1/pallas_call | solution.py:595
  77.3 1.6 %collective-permute-start.18 = (bf16[4,96,384]{2,1,0:T(8,128)(2,1)S(1)}, bf16[4,96,384]{2,1,0:T(8,128)(2,1)S(1)}, u32[]{:S(2)}, u32[]{:S(2)}) collective-permute-start(bf16[4,96,384]{2,1,0:T(8,128)(2,1)S(1)} %get-tuple-element.124), channel_id=1, source_target_pairs={{0,16},{16,0},{1,17},{17,1},{2,18},{18,2},{3,19},{19,3},{4,20},{20... | collective-permute-start | bytes 884744 | tf_op jit(solution)/shard_map/ppermute | solution.py:392
  78.8 7.5 %mix.1.normed_ref = bf16[1024,384]{1,0:T(8,128)(2,1)S(1)} custom-call(bf16[1024,384]{1,0:T(8,128)(2,1)S(1)} %get-tuple-element.112.grid.grid_ref, bf16[96,384]{1,0:T(8,128)(2,1)S(1)} %collective-permute-done.9.left, bf16[96,384]{1,0:T(8,128)(2,1)S(1)} %collective-permute-done.10.right, bf16[96,384]{1,0:T(8,128)(2,1)S(1)} %collective-permute-done.11.a, ...), custom_call_target="tpu_custom_call" | custom-call | flops 1000 | bytes 1003 | tf_op jit(solution)/shard_map/mix/pallas_call | solution.py:609
  86.4 0.5 collective-permute-start.15
  86.9 4.2 %collective-permute-start.16 = (bf16[96,384]{1,0:T(8,128)(2,1)S(1)}, bf16[96,384]{1,0:T(8,128)(2,1)S(1)}, u32[]{:S(2)}, u32[]{:S(2)}) collective-permute-start(bf16[96,384]{1,0:T(8,128)(2,1)S(1)} %get-tuple-element.122), channel_id=1, source_target_pairs={{0,8},{4,12},{8,0},{12,4},{1,9},{5,13},{9,1},{13,5},{2,10},{6,14},... | collective-permute-start | bytes 221192 | tf_op jit(solution)/shard_map/ppermute | solution.py:392
  91.1 2.1 %collective-permute-start.19 = (bf16[96,384]{1,0:T(8,128)(2,1)S(1)}, bf16[96,384]{1,0:T(8,128)(2,1)S(1)}, u32[]{:S(2)}, u32[]{:S(2)}) collective-permute-start(bf16[96,384]{1,0:T(8,128)(2,1)S(1)} %get-tuple-element.128), channel_id=1, source_target_pairs={{0,4},{4,8},{8,12},{12,0},{1,5},{5,9},{9,13},{13,1},{2,6},{6,10},{... | collective-permute-start | bytes 221192 | tf_op jit(solution)/shard_map/ppermute | solution.py:392
  93.2 0.6 collective-permute-start.20
  93.8 2.9 %collective-permute-start.21 = (bf16[96,384]{1,0:T(8,128)(2,1)S(1)}, bf16[96,384]{1,0:T(8,128)(2,1)S(1)}, u32[]{:S(2)}, u32[]{:S(2)}) collective-permute-start(bf16[96,384]{1,0:T(8,128)(2,1)S(1)} %get-tuple-element.130), channel_id=1, source_target_pairs={{0,12},{4,0},{8,4},{12,8},{1,13},{5,1},{9,5},{13,9},{2,14},{6,2},{... | collective-permute-start | bytes 221192 | tf_op jit(solution)/shard_map/ppermute | solution.py:392
  96.7 3.4 %feed.1 = f32[1024,128]{1,0:T(8,128)} custom-call(bf16[1024,384]{1,0:T(8,128)(2,1)S(1)} %mix.1.normed_ref, bf16[1024,384]{1,0:T(8,128)(2,1)S(1)} %get-tuple-element.112.grid.grid_ref, bf16[384,768]{1,0:T(8,128)(2,1)S(1)} %copy-done.5, bf16[768,384]{1,0:T(8,128)(2,1)S(1)} %copy-done.6, bf16[384,128]{1,0:T(8,128)(2,1)S(1)} %copy-done.7), custom_call_target="tpu_custom_call" | custom-call | flops 1000 | bytes 1003 | tf_op jit(solution)/shard_map/feed/pallas_call | solution.py:637
  100.0 1.9 %collective-permute-done.20.refs_6_ = bf16[96,384]{1,0:T(8,128)(2,1)S(1)} collective-permute-done((bf16[96,384]{1,0:T(8,128)(2,1)S(1)}, bf16[96,384]{1,0:T(8,128)(2,1)S(1)}, u32[]{:S(2)}, u32[]{:S(2)}) %collective-permute-start.20) | collective-permute-done | bytes 73760 | tf_op jit(solution)/shard_map/ppermute | solution.py:392
  101.9 0.1 close.1.own_ref
  102.0 0.6 collective-permute-start.23
  102.6 4.6 %collective-permute-done.23.two_ref = bf16[96,768]{1,0:T(8,128)(2,1)S(1)} collective-permute-done((bf16[96,768]{1,0:T(8,128)(2,1)S(1)}, bf16[96,768]{1,0:T(8,128)(2,1)S(1)}, u32[]{:S(2)}, u32[]{:S(2)}) %collective-permute-start.23) | collective-permute-done | bytes 147488 | tf_op jit(solution)/shard_map/ppermute | solution.py:387
  107.2 1.4 %collective-permute-done.24.three_ref = bf16[96,768]{1,0:T(8,128)(2,1)S(1)} collective-permute-done((bf16[96,768]{1,0:T(8,128)(2,1)S(1)}, bf16[96,768]{1,0:T(8,128)(2,1)S(1)}, u32[]{:S(2)}, u32[]{:S(2)}) %collective-permute-start.24) | collective-permute-done | bytes 147488 | tf_op jit(solution)/shard_map/ppermute | solution.py:387
  108.6 1.2 %spread.1 = f32[384,768]{1,0:T(8,128)} custom-call(bf16[96,768]{1,0:T(8,128)(2,1)S(1)} %close.1.own_ref, bf16[96,768]{1,0:T(8,128)(2,1)S(1)} %collective-permute-done.22.one_ref, bf16[96,768]{1,0:T(8,128)(2,1)S(1)} %collective-permute-done.23.two_ref, bf16[96,768]{1,0:T(8,128)(2,1)S(1)} %collective-permute-done.24.three_ref), custom_call_target="tpu_custom_call" | custom-call | flops 1000 | bytes 1003 | tf_op jit(solution)/shard_map/spread/pallas_call | solution.py:658
  (69 shorter events, 0.4 us)
Async XLA Ops:
  0.6 11.1 %copy-start = (bf16[1,1,1,256,768]{4,3,2,1,0:T(8,128)(2,1)S(1)}, bf16[1,1,1,256,768]{4,3,2,1,0:T(8,128)(2,1)}, u32[]{:S(2)}) copy-start(bf16[1,1,1,256,768]{4,3,2,1,0:T(8,128)(2,1)} %param.19) | copy-start | bytes 1179652
  0.6 1.5 %copy-start.2 = (bf16[1,32,32,768]{3,2,1,0:T(8,128)(2,1)S(1)}, bf16[1,32,32,768]{3,2,1,0:T(8,128)(2,1)}, u32[]{:S(2)}) copy-start(bf16[1,32,32,768]{3,2,1,0:T(8,128)(2,1)} %param.15) | copy-start | bytes 4718596
  2.8 10.5 %copy-start.3 = (bf16[768,768]{1,0:T(8,128)(2,1)S(1)}, bf16[768,768]{1,0:T(8,128)(2,1)}, u32[]{:S(2)}) copy-start(bf16[768,768]{1,0:T(8,128)(2,1)} %wout_ref.3) | copy-start | bytes 3538948
  4.5 21.9 %all-to-all-start = ((bf16[8,40,768]{2,1,0:T(8,128)(2,1)}), bf16[8,40,768]{2,1,0:T(8,128)(2,1)S(1)}, u32[]{:S(2)}, u32[]{:S(2)}) async-start(bf16[8,40,768]{2,1,0:T(8,128)(2,1)} %bitcast.4), calls=%async_computation | async-start | bytes 983040 | tf_op jit(solution)/shard_map/all_to_all | solution.py:442
  11.7 14.7 %copy-start.21 = (s32[1,1,1,256]{3,2,1,0:T(1,128)S(1)}, s32[1,1,1,256]{3,2,1,0:T(1,128)}, u32[]{:S(2)}) copy-start(s32[1,1,1,256]{3,2,1,0:T(1,128)} %param.17) | copy-start | bytes 3076
  11.7 10.6 %collective-permute-start.1 = (bf16[256,768]{1,0:T(8,128)(2,1)S(1)}, bf16[256,768]{1,0:T(8,128)(2,1)S(1)}, u32[]{:S(2)}, u32[]{:S(2)}) collective-permute-start(bf16[256,768]{1,0:T(8,128)(2,1)S(1)} %bitcast.10), channel_id=1, source_target_pairs={{0,2},{1,3},{2,0},{3,1},{4,6},{5,7},{6,4},{7,5},{8,10},{9,11},{10,... | collective-permute-start | bytes 1179656 | tf_op jit(solution)/shard_map/ppermute | solution.py:387
  13.3 15.5 %collective-permute-start = (bf16[256,768]{1,0:T(8,128)(2,1)S(1)}, bf16[256,768]{1,0:T(8,128)(2,1)S(1)}, u32[]{:S(2)}, u32[]{:S(2)}) collective-permute-start(bf16[256,768]{1,0:T(8,128)(2,1)S(1)} %bitcast.11), channel_id=1, source_target_pairs={{0,1},{1,0},{2,3},{3,2},{4,5},{5,4},{6,7},{7,6},{8,9},{9,8},{10,11... | collective-permute-start | bytes 1179656 | tf_op jit(solution)/shard_map/ppermute | solution.py:387
  13.3 2.0 %copy-start.1 = (bf16[768,2304]{1,0:T(8,128)(2,1)S(1)}, bf16[768,2304]{1,0:T(8,128)(2,1)}, u32[]{:S(2)}) copy-start(bf16[768,2304]{1,0:T(8,128)(2,1)} %wqkv_ref.1) | copy-start | bytes 10616836
  16.3 1.7 %copy-start.13 = (bf16[2304,768]{1,0:T(8,128)(2,1)}, bf16[2304,768]{1,0:T(8,128)(2,1)S(1)}, u32[]{:S(2)}) copy-start(bf16[2304,768]{1,0:T(8,128)(2,1)S(1)} %get-tuple-element.74.wqkv_t_ref) | copy-start | bytes 10616836
  18.1 0.7 copy-start.18
  22.4 6.4 %collective-permute-start.2 = (bf16[256,768]{1,0:T(8,128)(2,1)S(1)}, bf16[256,768]{1,0:T(8,128)(2,1)S(1)}, u32[]{:S(2)}, u32[]{:S(2)}) collective-permute-start(bf16[256,768]{1,0:T(8,128)(2,1)S(1)} %collective-permute-done.1.refs_10_), channel_id=1, source_target_pairs={{0,1},{1,0},{2,3},{3,2},{4,5},{5,4},{6,7},{7,6},{8,9},{9,8},{10,11... | collective-permute-start | bytes 1179656 | tf_op jit(solution)/shard_map/ppermute | solution.py:387
  26.4 5.5 %copy-start.15 = (bf16[768,384]{1,0:T(8,128)(2,1)S(1)}, bf16[768,384]{1,0:T(8,128)(2,1)}, u32[]{:S(2)}) copy-start(bf16[768,384]{1,0:T(8,128)(2,1)} %wdec_ref.1) | copy-start | bytes 1769476
  26.4 5.5 %copy-start.19 = (bf16[768,256]{1,0:T(8,128)(2,1)S(1)}, bf16[768,256]{1,0:T(8,128)(2,1)}, u32[]{:S(2)}) copy-start(bf16[768,256]{1,0:T(8,128)(2,1)} %copy-done.18) | copy-start | bytes 1179652
  27.2 4.8 %copy-start.22 = (s32[1,1,1,256]{3,2,1,0:T(1,128)S(1)}, s32[1,1,1,256]{3,2,1,0:T(1,128)}, u32[]{:S(2)}) copy-start(s32[1,1,1,256]{3,2,1,0:T(1,128)} %param.18) | copy-start | bytes 3076
  27.2 4.8 %copy-start.23 = (f32[12]{0:T(128)S(1)}, f32[12]{0:T(128)}, u32[]{:S(2)}) copy-start(f32[12]{0:T(128)} %scale_ref.1) | copy-start | bytes 148
  27.2 4.8 %copy-start.4 = (bf16[768,768]{1,0:T(8,128)(2,1)S(1)}, bf16[768,768]{1,0:T(8,128)(2,1)}, u32[]{:S(2)}) copy-start(bf16[768,768]{1,0:T(8,128)(2,1)} %wout_ref.3) | copy-start | bytes 3538948
  27.2 18.9 %collective-permute-start.3 = (bf16[256,768]{1,0:T(8,128)(2,1)S(1)}, bf16[256,768]{1,0:T(8,128)(2,1)S(1)}, u32[]{:S(2)}, u32[]{:S(2)}) collective-permute-start(bf16[256,768]{1,0:T(8,128)(2,1)S(1)} %get-tuple-element.102.normed_ref.refs_4_), channel_id=1, source_target_pairs={{0,2},{1,3},{2,0},{3,1},{4,6},{5,7},{6,4},{7,5},{8,10},{9,11},{10,... | collective-permute-start | bytes 1179656 | tf_op jit(solution)/shard_map/ppermute | solution.py:387
  28.8 17.3 %collective-permute-start.4 = (bf16[256,768]{1,0:T(8,128)(2,1)S(1)}, bf16[256,768]{1,0:T(8,128)(2,1)S(1)}, u32[]{:S(2)}, u32[]{:S(2)}) collective-permute-start(bf16[256,768]{1,0:T(8,128)(2,1)S(1)} %get-tuple-element.102.normed_ref.refs_4_), channel_id=1, source_target_pairs={{0,1},{1,0},{2,3},{3,2},{4,5},{5,4},{6,7},{7,6},{8,9},{9,8},{10,11... | collective-permute-start | bytes 1179656 | tf_op jit(solution)/shard_map/ppermute | solution.py:387
  28.8 2.0 %copy-start.14 = (bf16[2304,768]{1,0:T(8,128)(2,1)S(1)}, bf16[2304,768]{1,0:T(8,128)(2,1)}, u32[]{:S(2)}) copy-start(bf16[2304,768]{1,0:T(8,128)(2,1)} %copy-done.13) | copy-start | bytes 10616836
  32.0 24.5 %copy-start.10 = (s32[1,1,1,8,35]{4,3,2,1,0:T(8,128)S(1)}, s32[1,1,1,8,35]{4,3,2,1,0:T(8,128)}, u32[]{:S(2)}) copy-start(s32[1,1,1,8,35]{4,3,2,1,0:T(8,128)} %param.16) | copy-start | bytes 3364
  32.0 24.5 %copy-start.11 = (f32[2,1408]{1,0:T(2,128)S(1)}, f32[2,1408]{1,0:T(2,128)}, u32[]{:S(2)}) copy-start(f32[2,1408]{1,0:T(2,128)} %constant.2.clone.ids_ref) | copy-start | bytes 33796
  40.5 0.7 copy-start.16
  41.3 4.8 %copy-start.17 = (bf16[768,256]{1,0:T(8,128)(2,1)}, bf16[768,256]{1,0:T(8,128)(2,1)S(1)}, u32[]{:S(2)}) copy-start(bf16[768,256]{1,0:T(8,128)(2,1)S(1)} %get-tuple-element.87) | copy-start | bytes 1179652
  42.0 14.4 %all-to-all-start.1 = ((bf16[8,40,384]{2,1,0:T(8,128)(2,1)}), bf16[8,40,384]{2,1,0:T(8,128)(2,1)}, u32[]{:S(2)}, u32[]{:S(2)}) async-start(bf16[8,40,384]{2,1,0:T(8,128)(2,1)} %bitcast.7), calls=%async_computation.1 | async-start | bytes 491520 | tf_op jit(solution)/shard_map/all_to_all | solution.py:510
  46.1 10.4 %collective-permute-start.5 = (bf16[768,256]{1,0:T(8,128)(2,1)}, bf16[768,256]{1,0:T(8,128)(2,1)S(1)}, u32[]{:S(2)}, u32[]{:S(2)}) collective-permute-start(bf16[768,256]{1,0:T(8,128)(2,1)} %copy-done.20), channel_id=1, source_target_pairs={{0,1},{1,0},{2,3},{3,2},{4,5},{5,4},{6,7},{7,6},{8,9},{9,8},{10,11... | collective-permute-start | bytes 1179656 | tf_op jit(solution)/shard_map/ppermute | solution.py:387
  46.7 9.8 %collective-permute-start.8 = (bf16[256,768]{1,0:T(8,128)(2,1)S(1)}, bf16[256,768]{1,0:T(8,128)(2,1)}, u32[]{:S(2)}, u32[]{:S(2)}) collective-permute-start(bf16[256,768]{1,0:T(8,128)(2,1)S(1)} %collective-permute-done.3.refs_6_), channel_id=1, source_target_pairs={{0,1},{1,0},{2,3},{3,2},{4,5},{5,4},{6,7},{7,6},{8,9},{9,8},{10,11... | collective-permute-start | bytes 1179656 | tf_op jit(solution)/shard_map/ppermute | solution.py:387
  46.8 17.2 %collective-permute-start.6 = (bf16[768,256]{1,0:T(8,128)(2,1)}, bf16[768,256]{1,0:T(8,128)(2,1)}, u32[]{:S(2)}, u32[]{:S(2)}) collective-permute-start(bf16[768,256]{1,0:T(8,128)(2,1)} %copy-done.17), channel_id=1, source_target_pairs={{0,2},{1,3},{2,0},{3,1},{4,6},{5,7},{6,4},{7,5},{8,10},{9,11},{10,... | collective-permute-start | bytes 1179656 | tf_op jit(solution)/shard_map/ppermute | solution.py:387
  47.3 19.2 %collective-permute-start.7 = (bf16[768,256]{1,0:T(8,128)(2,1)}, bf16[768,256]{1,0:T(8,128)(2,1)}, u32[]{:S(2)}, u32[]{:S(2)}) collective-permute-start(bf16[768,256]{1,0:T(8,128)(2,1)} %copy-done.16), channel_id=1, source_target_pairs={{0,3},{1,2},{2,1},{3,0},{4,7},{5,6},{6,5},{7,4},{8,11},{9,10},{10,... | collective-permute-start | bytes 1179656 | tf_op jit(solution)/shard_map/ppermute | solution.py:387
  59.6 12.4 %collective-permute-start.9 = (bf16[96,384]{1,0:T(8,128)(2,1)S(1)}, bf16[96,384]{1,0:T(8,128)(2,1)S(1)}, u32[]{:S(2)}, u32[]{:S(2)}) collective-permute-start(bf16[96,384]{1,0:T(8,128)(2,1)S(1)} %get-tuple-element.93), channel_id=1, source_target_pairs={{0,4},{4,8},{8,12},{12,0},{1,5},{5,9},{9,13},{13,1},{2,6},{6,10},{... | collective-permute-start | bytes 221192 | tf_op jit(solution)/shard_map/ppermute | solution.py:392
  59.6 12.4 %collective-permute-start.10 = (bf16[96,384]{1,0:T(8,128)(2,1)S(1)}, bf16[96,384]{1,0:T(8,128)(2,1)S(1)}, u32[]{:S(2)}, u32[]{:S(2)}) collective-permute-start(bf16[96,384]{1,0:T(8,128)(2,1)S(1)} %get-tuple-element.94), channel_id=1, source_target_pairs={{0,12},{4,0},{8,4},{12,8},{1,13},{5,1},{9,5},{13,9},{2,14},{6,2},{... | collective-permute-start | bytes 221192 | tf_op jit(solution)/shard_map/ppermute | solution.py:392
  63.4 8.6 %collective-permute-start.11 = (bf16[96,384]{1,0:T(8,128)(2,1)S(1)}, bf16[96,384]{1,0:T(8,128)(2,1)S(1)}, u32[]{:S(2)}, u32[]{:S(2)}) collective-permute-start(bf16[96,384]{1,0:T(8,128)(2,1)S(1)} %get-tuple-element.95), channel_id=1, source_target_pairs={{0,16},{4,20},{8,24},{12,28},{16,0},{20,4},{24,8},{28,12},{1,17},{... | collective-permute-start | bytes 221192 | tf_op jit(solution)/shard_map/ppermute | solution.py:563
  64.0 6.6 %collective-permute-start.12 = (bf16[16,384]{1,0:T(8,128)(2,1)S(1)}, bf16[16,384]{1,0:T(8,128)(2,1)S(1)}, u32[]{:S(2)}, u32[]{:S(2)}) collective-permute-start(bf16[16,384]{1,0:T(8,128)(2,1)S(1)} %get-tuple-element.96), channel_id=1, source_target_pairs={{0,20},{4,24},{8,28},{12,16},{16,4},{20,8},{24,12},{28,0},{1,21},{... | collective-permute-start | bytes 36872 | tf_op jit(solution)/shard_map/ppermute | solution.py:563
  66.5 5.5 %collective-permute-start.13 = (bf16[16,384]{1,0:T(8,128)(2,1)S(1)}, bf16[16,384]{1,0:T(8,128)(2,1)S(1)}, u32[]{:S(2)}, u32[]{:S(2)}) collective-permute-start(bf16[16,384]{1,0:T(8,128)(2,1)S(1)} %get-tuple-element.97), channel_id=1, source_target_pairs={{0,28},{4,16},{8,20},{12,24},{16,12},{20,0},{24,4},{28,8},{1,29},{... | collective-permute-start | bytes 36872 | tf_op jit(solution)/shard_map/ppermute | solution.py:563
  74.3 4.5 %copy-start.8 = (f32[7,7,384]{2,1,0:T(8,128)S(1)}, f32[7,7,384]{2,1,0:T(8,128)}, u32[]{:S(2)}) copy-start(f32[7,7,384]{2,1,0:T(8,128)} %taps.1) | copy-start | bytes 225796
  74.4 11.9 %collective-permute-start.14 = (bf16[4,96,384]{2,1,0:T(8,128)(2,1)S(1)}, bf16[4,96,384]{2,1,0:T(8,128)(2,1)S(1)}, u32[]{:S(2)}, u32[]{:S(2)}) collective-permute-start(bf16[4,96,384]{2,1,0:T(8,128)(2,1)S(1)} %get-tuple-element.111), channel_id=1, source_target_pairs={{0,16},{16,0},{1,17},{17,1},{2,18},{18,2},{3,19},{19,3},{4,20},{20... | collective-permute-start | bytes 884744 | tf_op jit(solution)/shard_map/ppermute | solution.py:392
  77.3 13.8 %collective-permute-start.18 = (bf16[4,96,384]{2,1,0:T(8,128)(2,1)S(1)}, bf16[4,96,384]{2,1,0:T(8,128)(2,1)S(1)}, u32[]{:S(2)}, u32[]{:S(2)}) collective-permute-start(bf16[4,96,384]{2,1,0:T(8,128)(2,1)S(1)} %get-tuple-element.124), channel_id=1, source_target_pairs={{0,16},{16,0},{1,17},{17,1},{2,18},{18,2},{3,19},{19,3},{4,20},{20... | collective-permute-start | bytes 884744 | tf_op jit(solution)/shard_map/ppermute | solution.py:392
  78.8 17.8 %copy-start.5 = (bf16[384,768]{1,0:T(8,128)(2,1)S(1)}, bf16[384,768]{1,0:T(8,128)(2,1)}, u32[]{:S(2)}) copy-start(bf16[384,768]{1,0:T(8,128)(2,1)} %up_ref.1) | copy-start | bytes 1769476
  78.8 17.8 %copy-start.6 = (bf16[768,384]{1,0:T(8,128)(2,1)S(1)}, bf16[768,384]{1,0:T(8,128)(2,1)}, u32[]{:S(2)}) copy-start(bf16[768,384]{1,0:T(8,128)(2,1)} %down_ref.1) | copy-start | bytes 1769476
  78.8 17.8 %copy-start.7 = (bf16[384,128]{1,0:T(8,128)(2,1)S(1)}, bf16[384,128]{1,0:T(8,128)(2,1)}, u32[]{:S(2)}) copy-start(bf16[384,128]{1,0:T(8,128)(2,1)} %head_ref.1) | copy-start | bytes 294916
  86.4 7.4 %collective-permute-start.15 = (bf16[96,384]{1,0:T(8,128)(2,1)S(1)}, bf16[96,384]{1,0:T(8,128)(2,1)S(1)}, u32[]{:S(2)}, u32[]{:S(2)}) collective-permute-start(bf16[96,384]{1,0:T(8,128)(2,1)S(1)} %get-tuple-element.121), channel_id=1, source_target_pairs={{0,4},{4,8},{8,12},{12,0},{1,5},{5,9},{9,13},{13,1},{2,6},{6,10},{... | collective-permute-start | bytes 221192 | tf_op jit(solution)/shard_map/ppermute | solution.py:392
  86.9 13.1 %collective-permute-start.16 = (bf16[96,384]{1,0:T(8,128)(2,1)S(1)}, bf16[96,384]{1,0:T(8,128)(2,1)S(1)}, u32[]{:S(2)}, u32[]{:S(2)}) collective-permute-start(bf16[96,384]{1,0:T(8,128)(2,1)S(1)} %get-tuple-element.122), channel_id=1, source_target_pairs={{0,8},{4,12},{8,0},{12,4},{1,9},{5,13},{9,1},{13,5},{2,10},{6,14},... | collective-permute-start | bytes 221192 | tf_op jit(solution)/shard_map/ppermute | solution.py:392
  91.1 9.0 %collective-permute-start.17 = (bf16[96,384]{1,0:T(8,128)(2,1)S(1)}, bf16[96,384]{1,0:T(8,128)(2,1)S(1)}, u32[]{:S(2)}, u32[]{:S(2)}) collective-permute-start(bf16[96,384]{1,0:T(8,128)(2,1)S(1)} %get-tuple-element.123), channel_id=1, source_target_pairs={{0,12},{4,0},{8,4},{12,8},{1,13},{5,1},{9,5},{13,9},{2,14},{6,2},{... | collective-permute-start | bytes 221192 | tf_op jit(solution)/shard_map/ppermute | solution.py:392
  91.1 8.9 %collective-permute-start.19 = (bf16[96,384]{1,0:T(8,128)(2,1)S(1)}, bf16[96,384]{1,0:T(8,128)(2,1)S(1)}, u32[]{:S(2)}, u32[]{:S(2)}) collective-permute-start(bf16[96,384]{1,0:T(8,128)(2,1)S(1)} %get-tuple-element.128), channel_id=1, source_target_pairs={{0,4},{4,8},{8,12},{12,0},{1,5},{5,9},{9,13},{13,1},{2,6},{6,10},{... | collective-permute-start | bytes 221192 | tf_op jit(solution)/shard_map/ppermute | solution.py:392
  93.2 8.7 %collective-permute-start.20 = (bf16[96,384]{1,0:T(8,128)(2,1)S(1)}, bf16[96,384]{1,0:T(8,128)(2,1)S(1)}, u32[]{:S(2)}, u32[]{:S(2)}) collective-permute-start(bf16[96,384]{1,0:T(8,128)(2,1)S(1)} %get-tuple-element.129), channel_id=1, source_target_pairs={{0,8},{4,12},{8,0},{12,4},{1,9},{5,13},{9,1},{13,5},{2,10},{6,14},... | collective-permute-start | bytes 221192 | tf_op jit(solution)/shard_map/ppermute | solution.py:392
  93.8 8.1 %collective-permute-start.21 = (bf16[96,384]{1,0:T(8,128)(2,1)S(1)}, bf16[96,384]{1,0:T(8,128)(2,1)S(1)}, u32[]{:S(2)}, u32[]{:S(2)}) collective-permute-start(bf16[96,384]{1,0:T(8,128)(2,1)S(1)} %get-tuple-element.130), channel_id=1, source_target_pairs={{0,12},{4,0},{8,4},{12,8},{1,13},{5,1},{9,5},{13,9},{2,14},{6,2},{... | collective-permute-start | bytes 221192 | tf_op jit(solution)/shard_map/ppermute | solution.py:392
  102.0 5.2 %collective-permute-start.23 = (bf16[96,768]{1,0:T(8,128)(2,1)S(1)}, bf16[96,768]{1,0:T(8,128)(2,1)S(1)}, u32[]{:S(2)}, u32[]{:S(2)}) collective-permute-start(bf16[96,768]{1,0:T(8,128)(2,1)S(1)} %close.1.own_ref), channel_id=1, source_target_pairs={{0,2},{1,3},{2,0},{3,1},{4,6},{5,7},{6,4},{7,5},{8,10},{9,11},{10,... | collective-permute-start | bytes 442376 | tf_op jit(solution)/shard_map/ppermute | solution.py:387
  102.6 4.6 %collective-permute-start.22 = (bf16[96,768]{1,0:T(8,128)(2,1)S(1)}, bf16[96,768]{1,0:T(8,128)(2,1)S(1)}, u32[]{:S(2)}, u32[]{:S(2)}) collective-permute-start(bf16[96,768]{1,0:T(8,128)(2,1)S(1)} %close.1.own_ref), channel_id=1, source_target_pairs={{0,1},{1,0},{2,3},{3,2},{4,5},{5,4},{6,7},{7,6},{8,9},{9,8},{10,11... | collective-permute-start | bytes 442376 | tf_op jit(solution)/shard_map/ppermute | solution.py:387
  107.2 1.4 %collective-permute-start.24 = (bf16[96,768]{1,0:T(8,128)(2,1)S(1)}, bf16[96,768]{1,0:T(8,128)(2,1)S(1)}, u32[]{:S(2)}, u32[]{:S(2)}) collective-permute-start(bf16[96,768]{1,0:T(8,128)(2,1)S(1)} %collective-permute-done.23.two_ref), channel_id=1, source_target_pairs={{0,1},{1,0},{2,3},{3,2},{4,5},{5,4},{6,7},{7,6},{8,9},{9,8},{10,11... | collective-permute-start | bytes 442376 | tf_op jit(solution)/shard_map/ppermute | solution.py:387
  (3 other events, 2.1 us)

commit v7 on v6

--- a/solution.py
+++ b/solution.py
@@ -124,14 +124,16 @@
     for h in range(heads):
         lo, hi = h * size, (h + 1) * size
         q = u_ref[lo:hi].astype(bf16)
-        k = u_ref[width + lo : width + hi].astype(bf16)
-        scores = mm(k, q, TN)
-        raised = jnp.where(same, jnp.exp(scores * scale_ref[h]), 0.0)
-        weights = (raised * (1.0 / jnp.sum(raised, axis=0, keepdims=True))).astype(bf16)
-        p_ref[h] = weights
-        att = mm(v_ref[lo:hi], weights).astype(bf16)
-        att_ref[lo:hi] = att
-        emit(split, left_ref, 3 * width + lo, att)
+        k = jnp.transpose(u_ref[width + lo : width + hi].astype(bf16))
+        value = v_ref[lo:hi]
+        for at in range(0, rows, 128):
+            cut = slice(at, at + 128)
+            scores = mm(k, q[:, cut])
+            raised = jnp.where(same[:, cut], jnp.exp(scores * scale_ref[h]), 0.0)
+            weights = (raised * (1.0 / jnp.sum(raised, axis=0, keepdims=True))).astype(bf16)
+            p_ref[h, :, cut] = weights
+            att_ref[lo:hi, cut] = mm(value, weights).astype(bf16)
+        emit(split, left_ref, 3 * width + lo, att_ref[lo:hi])
     attended = jnp.transpose(att_ref[...])
     enc_out = (enc_ref[...].astype(f32) + mm(attended, wout_ref[...])).astype(bf16)
     dec = mm(enc_out, wdec_ref[...]).astype(bf16)
@@ -141,17 +143,23 @@
     for h in range(heads):
         lo, hi = h * size, (h + 1) * size
         ga = ga_ref[lo:hi]
-        low = p_ref[h]
-        weights = low.astype(f32)
-        grad_soft = mm(v_ref[lo:hi], ga, TN)
-        part = weights * grad_soft
-        total = jnp.sum(part, axis=0, keepdims=True)
-        grad_scores = ((part - weights * total) * scale_ref[h]).astype(bf16)
         q = u_ref[lo:hi]
         k = u_ref[width + lo : width + hi]
-        grad_v = mm(ga, low, NT)
-        grad_q = mm(k.astype(bf16), grad_scores)
-        grad_k = mm(q.astype(bf16), grad_scores, NT)
+        q_low, k_low = q.astype(bf16), k.astype(bf16)
+        value = jnp.transpose(v_ref[lo:hi])
+        grad_v, grad_k, grad_q = 0.0, 0.0, []
+        for at in range(0, rows, 128):
+            cut = slice(at, at + 128)
+            low = p_ref[h, :, cut]
+            weights = low.astype(f32)
+            grad_soft = mm(value, ga[:, cut])
+            part = weights * grad_soft
+            total = jnp.sum(part, axis=0, keepdims=True)
+            grad_scores = ((part - weights * total) * scale_ref[h]).astype(bf16)
+            grad_v = grad_v + mm(ga[:, cut], low, NT)
+            grad_k = grad_k + mm(q_low[:, cut], grad_scores, NT)
+            grad_q.append(mm(k_low, grad_scores))
+        grad_q = jnp.concatenate(grad_q, axis=1)
         grad_q = (grad_q - q * jnp.sum(q * grad_q, axis=0, keepdims=True)) * len_ref[h : h + 1]
         grad_k = (grad_k - k * jnp.sum(k * grad_k, axis=0, keepdims=True)) * len_ref[
             heads + h : heads + h + 1
@@ -276,6 +284,23 @@
         at += ref.shape[0]
 
 
+def rim_kernel(rim, left_ref, right_ref, edge_ref, out_ref):
+    size = edge_ref.shape[0]
+    out_ref[0:size] = edge_ref[...]
+
+    def corners(at):
+        for start, ref in ((size, left_ref), (size + 16, right_ref)):
+            out_ref[start : start + 16] = ref[at : at + 16]
+
+    @pl.when(lax.axis_index("eta") == 0)
+    def _():
+        corners(left_ref.shape[0] - 16)
+
+    @pl.when(lax.axis_index("eta") != 0)
+    def _():
+        corners(0)
+
+
 def conv_kernel_body(
     shape, span, folded, grid_ref, left_ref, right_ref, rims, taps_ref, out_ref,
     full_ref, wide_ref, mixed_ref,
@@ -293,10 +318,7 @@
         full_ref[rim + x, lead - rim : lead] = left[rim * x : rim * (x + 1)]
         full_ref[rim + x, lead + columns : lead + columns + rim] = right[rim * x : rim * (x + 1)]
 
-    def put(base, edge_ref, first_ref, last_ref):
-        edge = edge_ref[...].astype(f32)
-        first = first_ref[...].astype(f32)
-        last = last_ref[...].astype(f32)
+    def put(base, edge, first, last):
         for i in range(rim):
             full_ref[base + i, lead : lead + columns] = edge[columns * i : columns * (i + 1)]
             full_ref[base + i, lead - rim : lead] = first[rim * i : rim * (i + 1)]
@@ -309,10 +331,19 @@
         base = jnp.where(lax.axis_index("eta") == 0, far, 0)
         for i in range(rim):
             full_ref[far - base + i] = jnp.zeros(full_ref.shape[1:], f32)
-        put(base, *rims)
+        size = rim * columns
+        edge = rims[0][...].astype(f32)
+        low = lax.axis_index("eta") == 0
+        count = rim * rim
+        corners = []
+        for at in (size, size + 16):
+            early, late = edge[at : at + count], edge[at + 16 - count : at + 16]
+            corners.append(jnp.where(low, early, late))
+        put(base, edge[0:size], *corners)
     else:
-        put(0, *rims[:3])
-        put(rim + lines, *rims[3:])
+        pieces = [ref[...].astype(f32) for ref in rims]
+        put(0, *pieces[:3])
+        put(rim + lines, *pieces[3:])
     for t in range(span * span):
         wide_ref[t] = jnp.broadcast_to(taps_ref[t // span, t % span : t % span + 1], (8, width))
     groups = columns // 8
@@ -359,19 +390,12 @@
     out_ref[...] = (centred * lax.rsqrt(spread + norm_eps)).astype(bf16)
 
 
-def mix_folded(shape, span, grid, left, right, a, b, c, taps, out, full, wide, mixed):
-    conv_kernel_body(
-        shape, span, True, grid, left, right, (a, b, c), taps, out, full, wide, mixed
-    )
-
-
-def mix_open(
-    shape, span, grid, left, right, a, b, c, d, e, g, taps, out, full, wide, mixed
-):
-    conv_kernel_body(
-        shape, span, False, grid, left, right, (a, b, c, d, e, g), taps, out, full, wide,
-        mixed,
-    )
+def mix_folded(shape, span, grid, left, right, a, *refs):
+    conv_kernel_body(shape, span, True, grid, left, right, (a,), *refs)
+
+
+def mix_open(shape, span, grid, left, right, a, b, c, d, e, g, *refs):
+    conv_kernel_body(shape, span, False, grid, left, right, (a, b, c, d, e, g), *refs)
 
 
 def feed_kernel(chunk, normed_ref, grid_ref, up_ref, down_ref, head_ref, out_ref):
@@ -528,8 +552,8 @@
     moves = [0]
     if folded:
         edge = cell[eta_cells - rim :]
-        parts += [cell[:, :rim], cell[:, -rim:], edge, edge[:, :rim], edge[:, -rim:]]
-        moves += [0, 0] + [-(eta_cells - rim) * phi_cells] * 3
+        parts += [cell[:, :rim], cell[:, -rim:], edge]
+        moves += [0, 0, -(eta_cells - rim) * phi_cells]
     sizes = [-(-p.size // 16) * 16 for p in parts]
     ids = np.full((2, -(-sum(sizes) // 128) * 128), -7.0, np.float32)
     ids[1] = 0
@@ -552,21 +576,18 @@
         returned.reshape(slots, dec_width),
     )
     dec_grid = filled[0]
-    plane = ("eta", "phi")
-
-    def shifted(value, by):
-        pairs = [
-            (e * phi_count + p, (1 - e) * phi_count + (p + by) % phi_count)
-            for e in range(2)
-            for p in range(phi_count)
-        ]
-        return lax.ppermute(value, plane, pairs)
-
     if folded:
-        _, first, last, edge, edge_first, edge_last = filled
+        _, first, last, edge = filled
         left_halo = turn(last, "phi", 1)
         right_halo = turn(first, "phi", -1)
-        rims = (shifted(edge, 0), shifted(edge_last, 1), shifted(edge_first, -1))
+        rim_out = call(
+            functools.partial(rim_kernel, rim),
+            "rim",
+            sds((edge.shape[0] + 32, dec_width), bf16),
+            [vmem()] * 3,
+            limit=4,
+        )(left_halo, right_halo, edge)
+        rims = (turn(rim_out, "eta", 1),)
     else:
         box = dec_grid.reshape(eta_cells, phi_cells, dec_width)
         down = [(i, i + 1) for i in range(eta_count - 1)]
@@ -587,7 +608,7 @@
             flat(bottom), flat(low[far:]), flat(high[far:]),
         )
     if fast:
-        lefts, rights, cots = tie((lefts, rights, cots), left_halo, right_halo, rims)
+        lefts, rights, cots = tie((lefts, rights, cots), rim_out)
         chunk = width // 2
         half = group // 2
         kept, sent = [], []
@@ -601,6 +622,8 @@
                 nbytes=8 * MIB,
                 limit=10,
             )(*lefts, *rights, *cots)
+            if c == 0:
+                lefts, rights, cots = tie((lefts, rights, cots), rims)
             kept.append(keep)
             sent.append(turn(send, "eta", 1))
         left, right_halo, rims = tie((left_halo, right_halo, rims), kept)

time: 110 us -> 109 us (level)
  starting transfers between devices: 38.4 us -> 33 us
  Pallas kernels: 32.3 us -> 36 us
    ppermute x3 -> x0, starting transfers between devices: 4.63 us -> none  [shifted(): return lax.ppermute(value, plane, pairs)]
    ppermute x10 -> x11, waiting for transfers between devices: 1.88 us -> 5.81 us  [turn(): lax.ppermute(value, axis, [(i, (i + k) % count) for i in range(count)])]
    pallas_call x1, Pallas kernels: 8.52 us -> 12 us  [body(): call(functools.partial(encode_kernel, split), 'encode', [sds((slots, dec_...]
    ppermute x12, waiting for transfers between devices: 12.1 us -> 9.58 us  [flip(): lax.ppermute(value, axis, [(i, i ^ bit) for i in range(lax.axis_size(axis...]
    ppermute x3 -> x0, waiting for transfers between devices: 1.41 us -> none  [shifted(): return lax.ppermute(value, plane, pairs)]
    ppermute x10 -> x11, starting transfers between devices: 16.2 us -> 15.5 us  [turn(): lax.ppermute(value, axis, [(i, (i + k) % count) for i in range(count)])]
  transfers between devices with their start and end apart: 27 -> 25, of which waited for: 8 -> 8; matrix products, arithmetic and copies ran while one was open for 1% -> 1% of each run, Pallas kernels for 25% -> 31%
where the time goes in v7:
time: 109 us; the launch traced here: 108 us
  Pallas kernels  36 us (33%)
  starting transfers between devices  33 us (30%)
  waiting for transfers between devices  26.1 us (24%)
  local copies, waits for them, and re-layouts  12.1 us (11%)
    ppermute x11, starting transfers between devices, turn(): lax.ppermute(value, axis, [(i, (i + k) % count) for i in range(count)])  15.5 us
    pallas_call x1, Pallas kernels, body(): call(functools.partial(encode_kernel, split), 'encode', [sds((slots, dec_...  12 us
    unnamed x48, local copies, waits for them, and re-layouts  10.9 us
    ppermute x12, waiting for transfers between devices, flip(): lax.ppermute(value, axis, [(i, i ^ bit) for i in range(lax.axis_size(axis...  9.58 us
    pallas_call x1, Pallas kernels, body(): call(functools.partial(mix_folded if folded else mix_open, (eta_cells, ph...  7.46 us
    all_to_all x1, starting transfers between devices, body(): lax.all_to_all(outgoing.reshape(group, padded, width), ('eta', 'phi'), sp...  7.25 us
    all_to_all x1, waiting for transfers between devices, body(): lax.all_to_all(outbound.reshape(group, padded, dec_width), ('eta', 'phi')...  6.64 us
    ppermute x12, starting transfers between devices, flip(): lax.ppermute(value, axis, [(i, i ^ bit) for i in range(lax.axis_size(axis...  6.2 us
  transfers between devices with their start and end apart: 25, of which 8 were waited for; matrix products, arithmetic and copies ran while one was open for 1% of the time, Pallas kernels for 31%

profile of v7, /device:TPU:0, one launch (start us, length us, event | category | flops | bytes accessed | tf_op | source)
XLA Modules:
  0.0 108.1 jit_solution(4694395669982149127)
XLA Ops:
  0.6 1.4 %copy-done.2 = bf16[1,32,32,768]{3,2,1,0:T(8,128)(2,1)S(1)} copy-done((bf16[1,32,32,768]{3,2,1,0:T(8,128)(2,1)S(1)}, bf16[1,32,32,768]{3,2,1,0:T(8,128)(2,1)}, u32[]{:S(2)}) %copy-start.2) | copy-done | bytes 1572888
  2.1 0.7 copy-done.9
  2.8 1.7 %pick.1 = bf16[320,768]{1,0:T(8,128)(2,1)} custom-call(s32[8,35]{1,0:T(8,128)S(1)} %bitcast.17, bf16[1024,768]{1,0:T(8,128)(2,1)S(1)} %bitcast.15), custom_call_target="tpu_custom_call" | custom-call | flops 1000 | bytes 1003 | tf_op jit(solution)/shard_map/pick/pallas_call | solution.py:456
  4.5 7.3 %all-to-all-start = ((bf16[8,40,768]{2,1,0:T(8,128)(2,1)}), bf16[8,40,768]{2,1,0:T(8,128)(2,1)S(1)}, u32[]{:S(2)}, u32[]{:S(2)}) async-start(bf16[8,40,768]{2,1,0:T(8,128)(2,1)} %bitcast.4), calls=%async_computation | async-start | bytes 983040 | tf_op jit(solution)/shard_map/all_to_all | solution.py:466
  11.7 1.6 %collective-permute-start.1 = (bf16[256,768]{1,0:T(8,128)(2,1)S(1)}, bf16[256,768]{1,0:T(8,128)(2,1)S(1)}, u32[]{:S(2)}, u32[]{:S(2)}) collective-permute-start(bf16[256,768]{1,0:T(8,128)(2,1)S(1)} %bitcast.10), channel_id=1, source_target_pairs={{0,2},{1,3},{2,0},{3,1},{4,6},{5,7},{6,4},{7,5},{8,10},{9,11},{10,... | collective-permute-start | bytes 1179656 | tf_op jit(solution)/shard_map/ppermute | solution.py:411
  13.3 2.0 %copy-done.1 = bf16[768,2304]{1,0:T(8,128)(2,1)S(1)} copy-done((bf16[768,2304]{1,0:T(8,128)(2,1)S(1)}, bf16[768,2304]{1,0:T(8,128)(2,1)}, u32[]{:S(2)}) %copy-start.1) | copy-done | bytes 3538968
  15.3 1.0 prep.1
  16.3 1.7 %copy-done.13 = bf16[2304,768]{1,0:T(8,128)(2,1)} copy-done((bf16[2304,768]{1,0:T(8,128)(2,1)}, bf16[2304,768]{1,0:T(8,128)(2,1)S(1)}, u32[]{:S(2)}) %copy-start.13) | copy-done | bytes 3538968
  18.1 0.7 copy-done.18
  18.8 3.6 %collective-permute-done.1.refs_10_ = bf16[256,768]{1,0:T(8,128)(2,1)S(1)} collective-permute-done((bf16[256,768]{1,0:T(8,128)(2,1)S(1)}, bf16[256,768]{1,0:T(8,128)(2,1)S(1)}, u32[]{:S(2)}, u32[]{:S(2)}) %collective-permute-start.1) | collective-permute-done | bytes 393248 | tf_op jit(solution)/shard_map/ppermute | solution.py:411
  22.4 4.0 %all-to-all-done = bf16[8,40,768]{2,1,0:T(8,128)(2,1)S(1)} async-done(((bf16[8,40,768]{2,1,0:T(8,128)(2,1)}), bf16[8,40,768]{2,1,0:T(8,128)(2,1)S(1)}, u32[]{:S(2)}, u32[]{:S(2)}) %all-to-all-start) | async-done | bytes 491552 | tf_op jit(solution)/shard_map/all_to_all | solution.py:466
  26.4 0.7 norm.1
  27.2 1.6 %collective-permute-start.3 = (bf16[256,768]{1,0:T(8,128)(2,1)S(1)}, bf16[256,768]{1,0:T(8,128)(2,1)S(1)}, u32[]{:S(2)}, u32[]{:S(2)}) collective-permute-start(bf16[256,768]{1,0:T(8,128)(2,1)S(1)} %get-tuple-element.123.normed_ref.refs_4_), channel_id=1, source_target_pairs={{0,2},{1,3},{2,0},{3,1},{4,6},{5,7},{6,4},{7,5},{8,10},{9,11},{10,... | collective-permute-start | bytes 1179656 | tf_op jit(solution)/shard_map/ppermute | solution.py:411
  28.8 2.0 %copy-done.14 = bf16[2304,768]{1,0:T(8,128)(2,1)S(1)} copy-done((bf16[2304,768]{1,0:T(8,128)(2,1)S(1)}, bf16[2304,768]{1,0:T(8,128)(2,1)}, u32[]{:S(2)}) %copy-start.14) | copy-done | bytes 3538968
  30.8 1.1 %project.1 = (f32[1536,256]{1,0:T(8,128)S(1)}, f32[24,256]{1,0:T(8,128)S(1)}, bf16[768,256]{1,0:T(8,128)(2,1)S(1)}) custom-call(bf16[256,768]{1,0:T(8,128)(2,1)S(1)} %get-tuple-element.123.normed_ref.refs_4_, bf16[2304,768]{1,0:T(8,128)(2,1)S(1)} %copy-done.14), custom_call_target="tpu_custom_call" | custom-call | flops 2000000000 | bytes 6667666 | tf_op jit(solution)/shard_map/project/pallas_call | solution.py:503
  32.0 12.0 %encode.1 = (bf16[320,384]{1,0:T(8,128)(2,1)}, bf16[768,256]{1,0:T(8,128)(2,1)S(1)}, bf16[768,256]{1,0:T(8,128)(2,1)S(1)}, bf16[768,256]{1,0:T(8,128)(2,1)S(1)}, bf16[768,256]{1,0:T(8,128)(2,1)S(1)}) custom-call(s32[1,256]{1,0:T(1,128)S(1)} %bitcast.20, f32[12]{0:T(128)S(1)} %copy-done.23, f32[1,256]{1,0:T(1,128)S(1)} %get-tuple-element.79.place_ref, ...), custom_call_target="tpu_custom_call" | custom-call | flops 8000000000 | bytes 26667666 | tf_op jit(solution)/shard_map/encode/pallas_call | solution.py:514
  44.0 0.8 copy-done.16
  44.8 0.7 copy-done.20
  45.5 4.0 %all-to-all-start.1 = ((bf16[8,40,384]{2,1,0:T(8,128)(2,1)}), bf16[8,40,384]{2,1,0:T(8,128)(2,1)}, u32[]{:S(2)}, u32[]{:S(2)}) async-start(bf16[8,40,384]{2,1,0:T(8,128)(2,1)} %bitcast.7), calls=%async_computation.1 | async-start | bytes 491520 | tf_op jit(solution)/shard_map/all_to_all | solution.py:534
  49.6 0.6 collective-permute-start.5
  50.2 0.5 collective-permute-start.6
  50.7 1.3 %collective-permute-start.7 = (bf16[768,256]{1,0:T(8,128)(2,1)}, bf16[768,256]{1,0:T(8,128)(2,1)}, u32[]{:S(2)}, u32[]{:S(2)}) collective-permute-start(bf16[768,256]{1,0:T(8,128)(2,1)} %copy-done.16), channel_id=1, source_target_pairs={{0,3},{1,2},{2,1},{3,0},{4,7},{5,6},{6,5},{7,4},{8,11},{9,10},{10,... | collective-permute-start | bytes 1179656 | tf_op jit(solution)/shard_map/ppermute | solution.py:411
  52.0 1.3 %reshape.44.mask_ref = bf16[1,384]{1,0:T(2,128)(2,1)} reshape(bf16[384]{0:T(512)(128)(2,1)} %param.24) | data formatting | bytes 1536 | tf_op jit(solution)/shard_map/reshape | solution.py:575
  53.3 6.6 %all-to-all-done.1 = bf16[8,40,384]{2,1,0:T(8,128)(2,1)} async-done(((bf16[8,40,384]{2,1,0:T(8,128)(2,1)}), bf16[8,40,384]{2,1,0:T(8,128)(2,1)}, u32[]{:S(2)}, u32[]{:S(2)}) %all-to-all-start.1) | async-done | bytes 245792 | tf_op jit(solution)/shard_map/all_to_all | solution.py:534
  60.0 0.7 copy-done.12
  60.6 2.4 %fill.1 = (bf16[1024,384]{1,0:T(8,128)(2,1)S(1)}, bf16[96,384]{1,0:T(8,128)(2,1)S(1)}, bf16[96,384]{1,0:T(8,128)(2,1)S(1)}, bf16[96,384]{1,0:T(8,128)(2,1)S(1)}) custom-call(s32[8,35]{1,0:T(8,128)S(1)} %bitcast.18, f32[2,1408]{1,0:T(2,128)S(1)} %copy-done.11, bf16[1,384]{1,0:T(2,128)(2,1)S(1)} %copy-done.12, bf16[320,384]{1,0:T(8,128)(2,1)} %bitcast.8.got_ref), custom_call_target="tpu_custom_call" | custom-call | flops 1000 | bytes 1003 | tf_op jit(solution)/shard_map/fill/pallas_call | solution.py:565
  63.1 3.8 %collective-permute-start.10 = (bf16[96,384]{1,0:T(8,128)(2,1)S(1)}, bf16[96,384]{1,0:T(8,128)(2,1)S(1)}, u32[]{:S(2)}, u32[]{:S(2)}) collective-permute-start(bf16[96,384]{1,0:T(8,128)(2,1)S(1)} %get-tuple-element.102), channel_id=1, source_target_pairs={{0,12},{4,0},{8,4},{12,8},{1,13},{5,1},{9,5},{13,9},{2,14},{6,2},{... | collective-permute-start | bytes 221192 | tf_op jit(solution)/shard_map/ppermute | solution.py:416
  66.9 2.3 %collective-permute-done.9.left_ref.left = bf16[96,384]{1,0:T(8,128)(2,1)S(1)} collective-permute-done((bf16[96,384]{1,0:T(8,128)(2,1)S(1)}, bf16[96,384]{1,0:T(8,128)(2,1)S(1)}, u32[]{:S(2)}, u32[]{:S(2)}) %collective-permute-start.9) | collective-permute-done | bytes 73760 | tf_op jit(solution)/shard_map/ppermute | solution.py:416
  69.2 0.2 rim.1
  69.4 0.6 collective-permute-start.12
  70.1 2.3 %terms0.1 = (f32[4,96,384]{2,1,0:T(8,128)S(1)}, bf16[4,96,384]{2,1,0:T(8,128)(2,1)S(1)}) custom-call(bf16[768,256]{1,0:T(8,128)(2,1)S(1)} %get-tuple-element.119.refs_0_, bf16[768,256]{1,0:T(8,128)(2,1)S(1)} %collective-permute-done.5.refs_1_, bf16[768,256]{1,0:T(8,128)(2,1)} %collective-permute-done.6.refs_2_, ...), custom_call_target="tpu_custom_call" | custom-call | flops 1000 | bytes 1003 | tf_op jit(solution)/shard_map/terms0/pallas_call | solution.py:616
  72.4 1.5 %collective-permute-start.11 = (bf16[4,96,384]{2,1,0:T(8,128)(2,1)S(1)}, bf16[4,96,384]{2,1,0:T(8,128)(2,1)S(1)}, u32[]{:S(2)}, u32[]{:S(2)}) collective-permute-start(bf16[4,96,384]{2,1,0:T(8,128)(2,1)S(1)} %get-tuple-element.117), channel_id=1, source_target_pairs={{0,16},{16,0},{1,17},{17,1},{2,18},{18,2},{3,19},{19,3},{4,20},{20... | collective-permute-start | bytes 884744 | tf_op jit(solution)/shard_map/ppermute | solution.py:416
  73.9 0.2 collective-permute-done.12.a
  74.1 2.3 %terms1.1 = (f32[4,96,384]{2,1,0:T(8,128)S(1)}, bf16[4,96,384]{2,1,0:T(8,128)(2,1)S(1)}) custom-call(bf16[768,256]{1,0:T(8,128)(2,1)S(1)} %get-tuple-element.119.refs_0_, bf16[768,256]{1,0:T(8,128)(2,1)S(1)} %collective-permute-done.5.refs_1_, bf16[768,256]{1,0:T(8,128)(2,1)} %collective-permute-done.6.refs_2_, ...), custom_call_target="tpu_custom_call" | custom-call | flops 1000 | bytes 1003 | tf_op jit(solution)/shard_map/terms1/pallas_call | solution.py:616
  76.5 0.6 collective-permute-start.16
  77.1 7.5 %mix.1.normed_ref = bf16[1024,384]{1,0:T(8,128)(2,1)S(1)} custom-call(bf16[1024,384]{1,0:T(8,128)(2,1)S(1)} %get-tuple-element.118.grid.grid_ref, bf16[96,384]{1,0:T(8,128)(2,1)S(1)} %collective-permute-done.9.left_ref.left, bf16[96,384]{1,0:T(8,128)(2,1)S(1)} %collective-permute-done.10.right_ref.right, bf16[128,384]{1,0:T(8,128)(2,1)S(1)} %collective-permute-done.12.a, ...), custom_call_target="tpu_custom_call" | custom-call | flops 1000 | bytes 1003 | tf_op jit(solution)/shard_map/mix/pallas_call | solution.py:632
  84.6 1.1 %collective-permute-start.13 = (bf16[96,384]{1,0:T(8,128)(2,1)S(1)}, bf16[96,384]{1,0:T(8,128)(2,1)S(1)}, u32[]{:S(2)}, u32[]{:S(2)}) collective-permute-start(bf16[96,384]{1,0:T(8,128)(2,1)S(1)} %get-tuple-element.137), channel_id=1, source_target_pairs={{0,4},{4,8},{8,12},{12,0},{1,5},{5,9},{9,13},{13,1},{2,6},{6,10},{... | collective-permute-start | bytes 221192 | tf_op jit(solution)/shard_map/ppermute | solution.py:416
  85.8 3.3 %collective-permute-start.14 = (bf16[96,384]{1,0:T(8,128)(2,1)S(1)}, bf16[96,384]{1,0:T(8,128)(2,1)S(1)}, u32[]{:S(2)}, u32[]{:S(2)}) collective-permute-start(bf16[96,384]{1,0:T(8,128)(2,1)S(1)} %get-tuple-element.138), channel_id=1, source_target_pairs={{0,8},{4,12},{8,0},{12,4},{1,9},{5,13},{9,1},{13,5},{2,10},{6,14},... | collective-permute-start | bytes 221192 | tf_op jit(solution)/shard_map/ppermute | solution.py:416
  89.0 0.6 collective-permute-start.15
  89.7 1.5 %collective-permute-start.17 = (bf16[96,384]{1,0:T(8,128)(2,1)S(1)}, bf16[96,384]{1,0:T(8,128)(2,1)S(1)}, u32[]{:S(2)}, u32[]{:S(2)}) collective-permute-start(bf16[96,384]{1,0:T(8,128)(2,1)S(1)} %get-tuple-element.144), channel_id=1, source_target_pairs={{0,4},{4,8},{8,12},{12,0},{1,5},{5,9},{9,13},{13,1},{2,6},{6,10},{... | collective-permute-start | bytes 221192 | tf_op jit(solution)/shard_map/ppermute | solution.py:416
  91.2 0.8 collective-permute-start.18
  92.0 1.6 %collective-permute-start.19 = (bf16[96,384]{1,0:T(8,128)(2,1)S(1)}, bf16[96,384]{1,0:T(8,128)(2,1)S(1)}, u32[]{:S(2)}, u32[]{:S(2)}) collective-permute-start(bf16[96,384]{1,0:T(8,128)(2,1)S(1)} %get-tuple-element.146), channel_id=1, source_target_pairs={{0,12},{4,0},{8,4},{12,8},{1,13},{5,1},{9,5},{13,9},{2,14},{6,2},{... | collective-permute-start | bytes 221192 | tf_op jit(solution)/shard_map/ppermute | solution.py:416
  93.6 3.4 %feed.1 = f32[1024,128]{1,0:T(8,128)} custom-call(bf16[1024,384]{1,0:T(8,128)(2,1)S(1)} %mix.1.normed_ref, bf16[1024,384]{1,0:T(8,128)(2,1)S(1)} %get-tuple-element.118.grid.grid_ref, bf16[384,768]{1,0:T(8,128)(2,1)S(1)} %copy-done.5, bf16[768,384]{1,0:T(8,128)(2,1)S(1)} %copy-done.6, bf16[384,128]{1,0:T(8,128)(2,1)S(1)} %copy-done.7), custom_call_target="tpu_custom_call" | custom-call | flops 1000 | bytes 1003 | tf_op jit(solution)/shard_map/feed/pallas_call | solution.py:660
  97.0 3.3 %collective-permute-done.18.refs_6_ = bf16[96,384]{1,0:T(8,128)(2,1)S(1)} collective-permute-done((bf16[96,384]{1,0:T(8,128)(2,1)S(1)}, bf16[96,384]{1,0:T(8,128)(2,1)S(1)}, u32[]{:S(2)}, u32[]{:S(2)}) %collective-permute-start.18) | collective-permute-done | bytes 73760 | tf_op jit(solution)/shard_map/ppermute | solution.py:416
  100.4 0.6 collective-permute-start.21
  100.9 4.6 %collective-permute-done.21.two_ref = bf16[96,768]{1,0:T(8,128)(2,1)S(1)} collective-permute-done((bf16[96,768]{1,0:T(8,128)(2,1)S(1)}, bf16[96,768]{1,0:T(8,128)(2,1)S(1)}, u32[]{:S(2)}, u32[]{:S(2)}) %collective-permute-start.21) | collective-permute-done | bytes 147488 | tf_op jit(solution)/shard_map/ppermute | solution.py:411
  105.6 1.4 %collective-permute-done.22.three_ref = bf16[96,768]{1,0:T(8,128)(2,1)S(1)} collective-permute-done((bf16[96,768]{1,0:T(8,128)(2,1)S(1)}, bf16[96,768]{1,0:T(8,128)(2,1)S(1)}, u32[]{:S(2)}, u32[]{:S(2)}) %collective-permute-start.22) | collective-permute-done | bytes 147488 | tf_op jit(solution)/shard_map/ppermute | solution.py:411
  106.9 1.2 %spread.1 = f32[384,768]{1,0:T(8,128)} custom-call(bf16[96,768]{1,0:T(8,128)(2,1)S(1)} %close.1.own_ref, bf16[96,768]{1,0:T(8,128)(2,1)S(1)} %collective-permute-done.20.one_ref, bf16[96,768]{1,0:T(8,128)(2,1)S(1)} %collective-permute-done.21.two_ref, bf16[96,768]{1,0:T(8,128)(2,1)S(1)} %collective-permute-done.22.three_ref), custom_call_target="tpu_custom_call" | custom-call | flops 1000 | bytes 1003 | tf_op jit(solution)/shard_map/spread/pallas_call | solution.py:681
  (66 shorter events, 0.5 us)
Async XLA Ops:
  0.6 11.1 %copy-start = (bf16[1,1,1,256,768]{4,3,2,1,0:T(8,128)(2,1)S(1)}, bf16[1,1,1,256,768]{4,3,2,1,0:T(8,128)(2,1)}, u32[]{:S(2)}) copy-start(bf16[1,1,1,256,768]{4,3,2,1,0:T(8,128)(2,1)} %param.19) | copy-start | bytes 1179652
  0.6 1.5 %copy-start.2 = (bf16[1,32,32,768]{3,2,1,0:T(8,128)(2,1)S(1)}, bf16[1,32,32,768]{3,2,1,0:T(8,128)(2,1)}, u32[]{:S(2)}) copy-start(bf16[1,32,32,768]{3,2,1,0:T(8,128)(2,1)} %param.15) | copy-start | bytes 4718596
  2.1 0.7 copy-start.9
  2.8 10.5 %copy-start.3 = (bf16[768,768]{1,0:T(8,128)(2,1)S(1)}, bf16[768,768]{1,0:T(8,128)(2,1)}, u32[]{:S(2)}) copy-start(bf16[768,768]{1,0:T(8,128)(2,1)} %wout_ref.3) | copy-start | bytes 3538948
  4.5 21.9 %all-to-all-start = ((bf16[8,40,768]{2,1,0:T(8,128)(2,1)}), bf16[8,40,768]{2,1,0:T(8,128)(2,1)S(1)}, u32[]{:S(2)}, u32[]{:S(2)}) async-start(bf16[8,40,768]{2,1,0:T(8,128)(2,1)} %bitcast.4), calls=%async_computation | async-start | bytes 983040 | tf_op jit(solution)/shard_map/all_to_all | solution.py:466
  11.7 14.7 %copy-start.21 = (s32[1,1,1,256]{3,2,1,0:T(1,128)S(1)}, s32[1,1,1,256]{3,2,1,0:T(1,128)}, u32[]{:S(2)}) copy-start(s32[1,1,1,256]{3,2,1,0:T(1,128)} %param.17) | copy-start | bytes 3076
  11.7 10.6 %collective-permute-start.1 = (bf16[256,768]{1,0:T(8,128)(2,1)S(1)}, bf16[256,768]{1,0:T(8,128)(2,1)S(1)}, u32[]{:S(2)}, u32[]{:S(2)}) collective-permute-start(bf16[256,768]{1,0:T(8,128)(2,1)S(1)} %bitcast.10), channel_id=1, source_target_pairs={{0,2},{1,3},{2,0},{3,1},{4,6},{5,7},{6,4},{7,5},{8,10},{9,11},{10,... | collective-permute-start | bytes 1179656 | tf_op jit(solution)/shard_map/ppermute | solution.py:411
  13.3 15.5 %collective-permute-start = (bf16[256,768]{1,0:T(8,128)(2,1)S(1)}, bf16[256,768]{1,0:T(8,128)(2,1)S(1)}, u32[]{:S(2)}, u32[]{:S(2)}) collective-permute-start(bf16[256,768]{1,0:T(8,128)(2,1)S(1)} %bitcast.11), channel_id=1, source_target_pairs={{0,1},{1,0},{2,3},{3,2},{4,5},{5,4},{6,7},{7,6},{8,9},{9,8},{10,11... | collective-permute-start | bytes 1179656 | tf_op jit(solution)/shard_map/ppermute | solution.py:411
  13.3 2.0 %copy-start.1 = (bf16[768,2304]{1,0:T(8,128)(2,1)S(1)}, bf16[768,2304]{1,0:T(8,128)(2,1)}, u32[]{:S(2)}) copy-start(bf16[768,2304]{1,0:T(8,128)(2,1)} %wqkv_ref.1) | copy-start | bytes 10616836
  16.3 1.8 %copy-start.13 = (bf16[2304,768]{1,0:T(8,128)(2,1)}, bf16[2304,768]{1,0:T(8,128)(2,1)S(1)}, u32[]{:S(2)}) copy-start(bf16[2304,768]{1,0:T(8,128)(2,1)S(1)} %get-tuple-element.82.wqkv_t_ref) | copy-start | bytes 10616836
  18.1 0.7 copy-start.18
  22.4 6.4 %collective-permute-start.2 = (bf16[256,768]{1,0:T(8,128)(2,1)S(1)}, bf16[256,768]{1,0:T(8,128)(2,1)S(1)}, u32[]{:S(2)}, u32[]{:S(2)}) collective-permute-start(bf16[256,768]{1,0:T(8,128)(2,1)S(1)} %collective-permute-done.1.refs_10_), channel_id=1, source_target_pairs={{0,1},{1,0},{2,3},{3,2},{4,5},{5,4},{6,7},{7,6},{8,9},{9,8},{10,11... | collective-permute-start | bytes 1179656 | tf_op jit(solution)/shard_map/ppermute | solution.py:411
  26.4 5.5 %copy-start.15 = (bf16[768,384]{1,0:T(8,128)(2,1)S(1)}, bf16[768,384]{1,0:T(8,128)(2,1)}, u32[]{:S(2)}) copy-start(bf16[768,384]{1,0:T(8,128)(2,1)} %wdec_ref.1) | copy-start | bytes 1769476
  26.4 5.5 %copy-start.19 = (bf16[768,256]{1,0:T(8,128)(2,1)S(1)}, bf16[768,256]{1,0:T(8,128)(2,1)}, u32[]{:S(2)}) copy-start(bf16[768,256]{1,0:T(8,128)(2,1)} %copy-done.18) | copy-start | bytes 1179652
  27.2 4.8 %copy-start.22 = (s32[1,1,1,256]{3,2,1,0:T(1,128)S(1)}, s32[1,1,1,256]{3,2,1,0:T(1,128)}, u32[]{:S(2)}) copy-start(s32[1,1,1,256]{3,2,1,0:T(1,128)} %param.18) | copy-start | bytes 3076
  27.2 4.8 %copy-start.23 = (f32[12]{0:T(128)S(1)}, f32[12]{0:T(128)}, u32[]{:S(2)}) copy-start(f32[12]{0:T(128)} %scale_ref.1) | copy-start | bytes 148
  27.2 4.8 %copy-start.4 = (bf16[768,768]{1,0:T(8,128)(2,1)S(1)}, bf16[768,768]{1,0:T(8,128)(2,1)}, u32[]{:S(2)}) copy-start(bf16[768,768]{1,0:T(8,128)(2,1)} %wout_ref.3) | copy-start | bytes 3538948
  27.2 22.4 %collective-permute-start.3 = (bf16[256,768]{1,0:T(8,128)(2,1)S(1)}, bf16[256,768]{1,0:T(8,128)(2,1)S(1)}, u32[]{:S(2)}, u32[]{:S(2)}) collective-permute-start(bf16[256,768]{1,0:T(8,128)(2,1)S(1)} %get-tuple-element.123.normed_ref.refs_4_), channel_id=1, source_target_pairs={{0,2},{1,3},{2,0},{3,1},{4,6},{5,7},{6,4},{7,5},{8,10},{9,11},{10,... | collective-permute-start | bytes 1179656 | tf_op jit(solution)/shard_map/ppermute | solution.py:411
  28.8 20.8 %collective-permute-start.4 = (bf16[256,768]{1,0:T(8,128)(2,1)S(1)}, bf16[256,768]{1,0:T(8,128)(2,1)S(1)}, u32[]{:S(2)}, u32[]{:S(2)}) collective-permute-start(bf16[256,768]{1,0:T(8,128)(2,1)S(1)} %get-tuple-element.123.normed_ref.refs_4_), channel_id=1, source_target_pairs={{0,1},{1,0},{2,3},{3,2},{4,5},{5,4},{6,7},{7,6},{8,9},{9,8},{10,11... | collective-permute-start | bytes 1179656 | tf_op jit(solution)/shard_map/ppermute | solution.py:411
  28.8 2.0 %copy-start.14 = (bf16[2304,768]{1,0:T(8,128)(2,1)S(1)}, bf16[2304,768]{1,0:T(8,128)(2,1)}, u32[]{:S(2)}) copy-start(bf16[2304,768]{1,0:T(8,128)(2,1)} %copy-done.13) | copy-start | bytes 10616836
  32.0 28.0 %copy-start.10 = (s32[1,1,1,8,35]{4,3,2,1,0:T(8,128)S(1)}, s32[1,1,1,8,35]{4,3,2,1,0:T(8,128)}, u32[]{:S(2)}) copy-start(s32[1,1,1,8,35]{4,3,2,1,0:T(8,128)} %param.16) | copy-start | bytes 3364
  32.0 28.0 %copy-start.11 = (f32[2,1408]{1,0:T(2,128)S(1)}, f32[2,1408]{1,0:T(2,128)}, u32[]{:S(2)}) copy-start(f32[2,1408]{1,0:T(2,128)} %constant.2.clone.ids_ref) | copy-start | bytes 33796
  44.0 0.8 copy-start.16
  44.8 0.7 copy-start.20
  44.8 4.8 %copy-start.17 = (bf16[768,256]{1,0:T(8,128)(2,1)}, bf16[768,256]{1,0:T(8,128)(2,1)S(1)}, u32[]{:S(2)}) copy-start(bf16[768,256]{1,0:T(8,128)(2,1)S(1)} %get-tuple-element.95) | copy-start | bytes 1179652
  45.5 14.4 %all-to-all-start.1 = ((bf16[8,40,384]{2,1,0:T(8,128)(2,1)}), bf16[8,40,384]{2,1,0:T(8,128)(2,1)}, u32[]{:S(2)}, u32[]{:S(2)}) async-start(bf16[8,40,384]{2,1,0:T(8,128)(2,1)} %bitcast.7), calls=%async_computation.1 | async-start | bytes 491520 | tf_op jit(solution)/shard_map/all_to_all | solution.py:534
  49.6 10.4 %collective-permute-start.5 = (bf16[768,256]{1,0:T(8,128)(2,1)}, bf16[768,256]{1,0:T(8,128)(2,1)S(1)}, u32[]{:S(2)}, u32[]{:S(2)}) collective-permute-start(bf16[768,256]{1,0:T(8,128)(2,1)} %copy-done.20), channel_id=1, source_target_pairs={{0,1},{1,0},{2,3},{3,2},{4,5},{5,4},{6,7},{7,6},{8,9},{9,8},{10,11... | collective-permute-start | bytes 1179656 | tf_op jit(solution)/shard_map/ppermute | solution.py:411
  50.2 9.8 %collective-permute-start.8 = (bf16[256,768]{1,0:T(8,128)(2,1)S(1)}, bf16[256,768]{1,0:T(8,128)(2,1)}, u32[]{:S(2)}, u32[]{:S(2)}) collective-permute-start(bf16[256,768]{1,0:T(8,128)(2,1)S(1)} %collective-permute-done.3.refs_6_), channel_id=1, source_target_pairs={{0,1},{1,0},{2,3},{3,2},{4,5},{5,4},{6,7},{7,6},{8,9},{9,8},{10,11... | collective-permute-start | bytes 1179656 | tf_op jit(solution)/shard_map/ppermute | solution.py:411
  50.2 19.8 %collective-permute-start.6 = (bf16[768,256]{1,0:T(8,128)(2,1)}, bf16[768,256]{1,0:T(8,128)(2,1)}, u32[]{:S(2)}, u32[]{:S(2)}) collective-permute-start(bf16[768,256]{1,0:T(8,128)(2,1)} %copy-done.17), channel_id=1, source_target_pairs={{0,2},{1,3},{2,0},{3,1},{4,6},{5,7},{6,4},{7,5},{8,10},{9,11},{10,... | collective-permute-start | bytes 1179656 | tf_op jit(solution)/shard_map/ppermute | solution.py:411
  50.7 19.3 %collective-permute-start.7 = (bf16[768,256]{1,0:T(8,128)(2,1)}, bf16[768,256]{1,0:T(8,128)(2,1)}, u32[]{:S(2)}, u32[]{:S(2)}) collective-permute-start(bf16[768,256]{1,0:T(8,128)(2,1)} %copy-done.16), channel_id=1, source_target_pairs={{0,3},{1,2},{2,1},{3,0},{4,7},{5,6},{6,5},{7,4},{8,11},{9,10},{10,... | collective-permute-start | bytes 1179656 | tf_op jit(solution)/shard_map/ppermute | solution.py:411
  63.0 6.2 %collective-permute-start.9 = (bf16[96,384]{1,0:T(8,128)(2,1)S(1)}, bf16[96,384]{1,0:T(8,128)(2,1)S(1)}, u32[]{:S(2)}, u32[]{:S(2)}) collective-permute-start(bf16[96,384]{1,0:T(8,128)(2,1)S(1)} %get-tuple-element.101), channel_id=1, source_target_pairs={{0,4},{4,8},{8,12},{12,0},{1,5},{5,9},{9,13},{13,1},{2,6},{6,10},{... | collective-permute-start | bytes 221192 | tf_op jit(solution)/shard_map/ppermute | solution.py:416
  63.1 6.1 %collective-permute-start.10 = (bf16[96,384]{1,0:T(8,128)(2,1)S(1)}, bf16[96,384]{1,0:T(8,128)(2,1)S(1)}, u32[]{:S(2)}, u32[]{:S(2)}) collective-permute-start(bf16[96,384]{1,0:T(8,128)(2,1)S(1)} %get-tuple-element.102), channel_id=1, source_target_pairs={{0,12},{4,0},{8,4},{12,8},{1,13},{5,1},{9,5},{13,9},{2,14},{6,2},{... | collective-permute-start | bytes 221192 | tf_op jit(solution)/shard_map/ppermute | solution.py:416
  69.4 4.7 %collective-permute-start.12 = (bf16[128,384]{1,0:T(8,128)(2,1)S(1)}, bf16[128,384]{1,0:T(8,128)(2,1)S(1)}, u32[]{:S(2)}, u32[]{:S(2)}) collective-permute-start(bf16[128,384]{1,0:T(8,128)(2,1)S(1)} %rim.1), channel_id=1, source_target_pairs={{0,16},{16,0},{1,17},{17,1},{2,18},{18,2},{3,19},{19,3},{4,20},{20... | collective-permute-start | bytes 294920 | tf_op jit(solution)/shard_map/ppermute | solution.py:416
  72.4 4.7 %copy-start.8 = (f32[7,7,384]{2,1,0:T(8,128)S(1)}, f32[7,7,384]{2,1,0:T(8,128)}, u32[]{:S(2)}) copy-start(f32[7,7,384]{2,1,0:T(8,128)} %refs_0_.1) | copy-start | bytes 225796
  72.4 12.1 %collective-permute-start.11 = (bf16[4,96,384]{2,1,0:T(8,128)(2,1)S(1)}, bf16[4,96,384]{2,1,0:T(8,128)(2,1)S(1)}, u32[]{:S(2)}, u32[]{:S(2)}) collective-permute-start(bf16[4,96,384]{2,1,0:T(8,128)(2,1)S(1)} %get-tuple-element.117), channel_id=1, source_target_pairs={{0,16},{16,0},{1,17},{17,1},{2,18},{18,2},{3,19},{19,3},{4,20},{20... | collective-permute-start | bytes 884744 | tf_op jit(solution)/shard_map/ppermute | solution.py:416
  76.5 13.1 %collective-permute-start.16 = (bf16[4,96,384]{2,1,0:T(8,128)(2,1)S(1)}, bf16[4,96,384]{2,1,0:T(8,128)(2,1)S(1)}, u32[]{:S(2)}, u32[]{:S(2)}) collective-permute-start(bf16[4,96,384]{2,1,0:T(8,128)(2,1)S(1)} %get-tuple-element.140), channel_id=1, source_target_pairs={{0,16},{16,0},{1,17},{17,1},{2,18},{18,2},{3,19},{19,3},{4,20},{20... | collective-permute-start | bytes 884744 | tf_op jit(solution)/shard_map/ppermute | solution.py:416
  77.1 16.6 %copy-start.5 = (bf16[384,768]{1,0:T(8,128)(2,1)S(1)}, bf16[384,768]{1,0:T(8,128)(2,1)}, u32[]{:S(2)}) copy-start(bf16[384,768]{1,0:T(8,128)(2,1)} %up_ref.1) | copy-start | bytes 1769476
  77.1 16.6 %copy-start.6 = (bf16[768,384]{1,0:T(8,128)(2,1)S(1)}, bf16[768,384]{1,0:T(8,128)(2,1)}, u32[]{:S(2)}) copy-start(bf16[768,384]{1,0:T(8,128)(2,1)} %down_ref.1) | copy-start | bytes 1769476
  77.1 16.6 %copy-start.7 = (bf16[384,128]{1,0:T(8,128)(2,1)S(1)}, bf16[384,128]{1,0:T(8,128)(2,1)}, u32[]{:S(2)}) copy-start(bf16[384,128]{1,0:T(8,128)(2,1)} %head_ref.1) | copy-start | bytes 294916
  84.6 7.4 %collective-permute-start.13 = (bf16[96,384]{1,0:T(8,128)(2,1)S(1)}, bf16[96,384]{1,0:T(8,128)(2,1)S(1)}, u32[]{:S(2)}, u32[]{:S(2)}) collective-permute-start(bf16[96,384]{1,0:T(8,128)(2,1)S(1)} %get-tuple-element.137), channel_id=1, source_target_pairs={{0,4},{4,8},{8,12},{12,0},{1,5},{5,9},{9,13},{13,1},{2,6},{6,10},{... | collective-permute-start | bytes 221192 | tf_op jit(solution)/shard_map/ppermute | solution.py:416
  85.8 11.2 %collective-permute-start.14 = (bf16[96,384]{1,0:T(8,128)(2,1)S(1)}, bf16[96,384]{1,0:T(8,128)(2,1)S(1)}, u32[]{:S(2)}, u32[]{:S(2)}) collective-permute-start(bf16[96,384]{1,0:T(8,128)(2,1)S(1)} %get-tuple-element.138), channel_id=1, source_target_pairs={{0,8},{4,12},{8,0},{12,4},{1,9},{5,13},{9,1},{13,5},{2,10},{6,14},... | collective-permute-start | bytes 221192 | tf_op jit(solution)/shard_map/ppermute | solution.py:416
  89.0 8.0 %collective-permute-start.15 = (bf16[96,384]{1,0:T(8,128)(2,1)S(1)}, bf16[96,384]{1,0:T(8,128)(2,1)S(1)}, u32[]{:S(2)}, u32[]{:S(2)}) collective-permute-start(bf16[96,384]{1,0:T(8,128)(2,1)S(1)} %get-tuple-element.139), channel_id=1, source_target_pairs={{0,12},{4,0},{8,4},{12,8},{1,13},{5,1},{9,5},{13,9},{2,14},{6,2},{... | collective-permute-start | bytes 221192 | tf_op jit(solution)/shard_map/ppermute | solution.py:416
  89.7 7.3 %collective-permute-start.17 = (bf16[96,384]{1,0:T(8,128)(2,1)S(1)}, bf16[96,384]{1,0:T(8,128)(2,1)S(1)}, u32[]{:S(2)}, u32[]{:S(2)}) collective-permute-start(bf16[96,384]{1,0:T(8,128)(2,1)S(1)} %get-tuple-element.144), channel_id=1, source_target_pairs={{0,4},{4,8},{8,12},{12,0},{1,5},{5,9},{9,13},{13,1},{2,6},{6,10},{... | collective-permute-start | bytes 221192 | tf_op jit(solution)/shard_map/ppermute | solution.py:416
  91.2 9.1 %collective-permute-start.18 = (bf16[96,384]{1,0:T(8,128)(2,1)S(1)}, bf16[96,384]{1,0:T(8,128)(2,1)S(1)}, u32[]{:S(2)}, u32[]{:S(2)}) collective-permute-start(bf16[96,384]{1,0:T(8,128)(2,1)S(1)} %get-tuple-element.145), channel_id=1, source_target_pairs={{0,8},{4,12},{8,0},{12,4},{1,9},{5,13},{9,1},{13,5},{2,10},{6,14},... | collective-permute-start | bytes 221192 | tf_op jit(solution)/shard_map/ppermute | solution.py:416
  92.0 8.3 %collective-permute-start.19 = (bf16[96,384]{1,0:T(8,128)(2,1)S(1)}, bf16[96,384]{1,0:T(8,128)(2,1)S(1)}, u32[]{:S(2)}, u32[]{:S(2)}) collective-permute-start(bf16[96,384]{1,0:T(8,128)(2,1)S(1)} %get-tuple-element.146), channel_id=1, source_target_pairs={{0,12},{4,0},{8,4},{12,8},{1,13},{5,1},{9,5},{13,9},{2,14},{6,2},{... | collective-permute-start | bytes 221192 | tf_op jit(solution)/shard_map/ppermute | solution.py:416
  100.4 5.2 %collective-permute-start.21 = (bf16[96,768]{1,0:T(8,128)(2,1)S(1)}, bf16[96,768]{1,0:T(8,128)(2,1)S(1)}, u32[]{:S(2)}, u32[]{:S(2)}) collective-permute-start(bf16[96,768]{1,0:T(8,128)(2,1)S(1)} %close.1.own_ref), channel_id=1, source_target_pairs={{0,2},{1,3},{2,0},{3,1},{4,6},{5,7},{6,4},{7,5},{8,10},{9,11},{10,... | collective-permute-start | bytes 442376 | tf_op jit(solution)/shard_map/ppermute | solution.py:411
  100.9 4.6 %collective-permute-start.20 = (bf16[96,768]{1,0:T(8,128)(2,1)S(1)}, bf16[96,768]{1,0:T(8,128)(2,1)S(1)}, u32[]{:S(2)}, u32[]{:S(2)}) collective-permute-start(bf16[96,768]{1,0:T(8,128)(2,1)S(1)} %close.1.own_ref), channel_id=1, source_target_pairs={{0,1},{1,0},{2,3},{3,2},{4,5},{5,4},{6,7},{7,6},{8,9},{9,8},{10,11... | collective-permute-start | bytes 442376 | tf_op jit(solution)/shard_map/ppermute | solution.py:411
  105.6 1.4 %collective-permute-start.22 = (bf16[96,768]{1,0:T(8,128)(2,1)S(1)}, bf16[96,768]{1,0:T(8,128)(2,1)S(1)}, u32[]{:S(2)}, u32[]{:S(2)}) collective-permute-start(bf16[96,768]{1,0:T(8,128)(2,1)S(1)} %collective-permute-done.21.two_ref), channel_id=1, source_target_pairs={{0,1},{1,0},{2,3},{3,2},{4,5},{5,4},{6,7},{7,6},{8,9},{9,8},{10,11... | collective-permute-start | bytes 442376 | tf_op jit(solution)/shard_map/ppermute | solution.py:411
  (1 other events, 0.7 us)

commit v8 on v7

--- a/solution.py
+++ b/solution.py
@@ -124,16 +124,14 @@
     for h in range(heads):
         lo, hi = h * size, (h + 1) * size
         q = u_ref[lo:hi].astype(bf16)
-        k = jnp.transpose(u_ref[width + lo : width + hi].astype(bf16))
-        value = v_ref[lo:hi]
-        for at in range(0, rows, 128):
-            cut = slice(at, at + 128)
-            scores = mm(k, q[:, cut])
-            raised = jnp.where(same[:, cut], jnp.exp(scores * scale_ref[h]), 0.0)
-            weights = (raised * (1.0 / jnp.sum(raised, axis=0, keepdims=True))).astype(bf16)
-            p_ref[h, :, cut] = weights
-            att_ref[lo:hi, cut] = mm(value, weights).astype(bf16)
-        emit(split, left_ref, 3 * width + lo, att_ref[lo:hi])
+        k = u_ref[width + lo : width + hi].astype(bf16)
+        scores = mm(k, q, TN)
+        raised = jnp.where(same, jnp.exp(scores * scale_ref[h]), 0.0)
+        weights = (raised * (1.0 / jnp.sum(raised, axis=0, keepdims=True))).astype(bf16)
+        p_ref[h] = weights
+        att = mm(v_ref[lo:hi], weights).astype(bf16)
+        att_ref[lo:hi] = att
+        emit(split, left_ref, 3 * width + lo, att)
     attended = jnp.transpose(att_ref[...])
     enc_out = (enc_ref[...].astype(f32) + mm(attended, wout_ref[...])).astype(bf16)
     dec = mm(enc_out, wdec_ref[...]).astype(bf16)
@@ -143,23 +141,17 @@
     for h in range(heads):
         lo, hi = h * size, (h + 1) * size
         ga = ga_ref[lo:hi]
+        low = p_ref[h]
+        weights = low.astype(f32)
+        grad_soft = mm(v_ref[lo:hi], ga, TN)
+        part = weights * grad_soft
+        total = jnp.sum(part, axis=0, keepdims=True)
+        grad_scores = ((part - weights * total) * scale_ref[h]).astype(bf16)
         q = u_ref[lo:hi]
         k = u_ref[width + lo : width + hi]
-        q_low, k_low = q.astype(bf16), k.astype(bf16)
-        value = jnp.transpose(v_ref[lo:hi])
-        grad_v, grad_k, grad_q = 0.0, 0.0, []
-        for at in range(0, rows, 128):
-            cut = slice(at, at + 128)
-            low = p_ref[h, :, cut]
-            weights = low.astype(f32)
-            grad_soft = mm(value, ga[:, cut])
-            part = weights * grad_soft
-            total = jnp.sum(part, axis=0, keepdims=True)
-            grad_scores = ((part - weights * total) * scale_ref[h]).astype(bf16)
-            grad_v = grad_v + mm(ga[:, cut], low, NT)
-            grad_k = grad_k + mm(q_low[:, cut], grad_scores, NT)
-            grad_q.append(mm(k_low, grad_scores))
-        grad_q = jnp.concatenate(grad_q, axis=1)
+        grad_v = mm(ga, low, NT)
+        grad_q = mm(k.astype(bf16), grad_scores)
+        grad_k = mm(q.astype(bf16), grad_scores, NT)
         grad_q = (grad_q - q * jnp.sum(q * grad_q, axis=0, keepdims=True)) * len_ref[h : h + 1]
         grad_k = (grad_k - k * jnp.sum(k * grad_k, axis=0, keepdims=True)) * len_ref[
             heads + h : heads + h + 1
@@ -474,7 +466,7 @@
     left_part = (out_rows // pieces, rows)
     left_whole = (replicas,) + left_part if fast else left_part
     if fast:
-        cots = [cotangent, flip(cotangent, "replica", 1), flip(cotangent, "replica", 2)]
+        cots = [cotangent] + [flip(cotangent, "replica", k) for k in range(1, 4)]
     grad_att, w_qkv_t = call(
         prep_kernel,
         "prep",
@@ -484,8 +476,7 @@
         nbytes=10 * MIB,
         limit=10,
     )(cotangent, w_out, w_qkv)
-    if fast:
-        cots.append(flip(tie(cots[2], w_qkv_t), "replica", 1))
+    arrived = tie(arrived, w_qkv_t)
 
     normed, enc_in, places = call(
         functools.partial(norm_kernel, cap, padded),
@@ -509,7 +500,7 @@
         nbytes=8 * MIB,
         limit=10,
         cost=2000000000,
-    )(tie(normed, cots) if fast else normed, w_qkv_t)
+    )(normed, w_qkv_t)
 
     outbound, *lefts = call(
         functools.partial(encode_kernel, split),
@@ -530,7 +521,9 @@
         w_out, w_dec_in,
     )
     if fast:
-        *lefts, normed_y, normed_c = lax.optimization_barrier((*lefts, normed_y, normed_c))
+        cots, lefts, normed_y, normed_c = lax.optimization_barrier(
+            (cots, lefts, normed_y, normed_c)
+        )
     returned = lax.all_to_all(
         outbound.reshape(group, padded, dec_width), ("eta", "phi"), split_axis=0, concat_axis=0,
         tiled=True,

time: 109 us -> 105 us (0.963)
  Pallas kernels: 36 us -> 32.5 us
  starting transfers between devices: 33 us -> 31.8 us
  waiting for transfers between devices: 26.1 us -> 27.3 us
    ppermute x12, waiting for transfers between devices: 9.58 us -> 6.01 us  [flip(): lax.ppermute(value, axis, [(i, i ^ bit) for i in range(lax.axis_size(axis...]
    pallas_call x1, Pallas kernels: 12 us -> 8.51 us  [body(): call(functools.partial(encode_kernel, split), 'encode', [sds((slots, dec_...]
    all_to_all x1, waiting for transfers between devices: 4.03 us -> 7.23 us  [body(): lax.all_to_all(outgoing.reshape(group, padded, width), ('eta', 'phi'), sp...]
    ppermute x11, waiting for transfers between devices: 5.81 us -> 7.44 us  [turn(): lax.ppermute(value, axis, [(i, (i + k) % count) for i in range(count)])]
    ppermute x11, starting transfers between devices: 15.5 us -> 14 us  [turn(): lax.ppermute(value, axis, [(i, (i + k) % count) for i in range(count)])]
  transfers between devices with their start and end apart: 25 -> 25, of which waited for: 8 -> 7; matrix products, arithmetic and copies ran while one was open for 1% -> 1% of each run, Pallas kernels for 31% -> 28%
where the time goes in v8:
time: 105 us
  Pallas kernels  32.5 us (31%)
  starting transfers between devices  31.8 us (30%)
  waiting for transfers between devices  27.3 us (26%)
  local copies, waits for them, and re-layouts  12.1 us (12%)
    ppermute x11, starting transfers between devices, turn(): lax.ppermute(value, axis, [(i, (i + k) % count) for i in range(count)])  14 us
    unnamed x48, local copies, waits for them, and re-layouts  10.8 us
    pallas_call x1, Pallas kernels, body(): call(functools.partial(encode_kernel, split), 'encode', [sds((slots, dec_...  8.51 us
    pallas_call x1, Pallas kernels, body(): call(functools.partial(mix_folded if folded else mix_open, (eta_cells, ph...  7.45 us
    ppermute x11, waiting for transfers between devices, turn(): lax.ppermute(value, axis, [(i, (i + k) % count) for i in range(count)])  7.44 us
    all_to_all x1, starting transfers between devices, body(): lax.all_to_all(outgoing.reshape(group, padded, width), ('eta', 'phi'), sp...  7.25 us
    all_to_all x1, waiting for transfers between devices, body(): lax.all_to_all(outgoing.reshape(group, padded, width), ('eta', 'phi'), sp...  7.23 us
    all_to_all x1, waiting for transfers between devices, body(): lax.all_to_all(outbound.reshape(group, padded, dec_width), ('eta', 'phi')...  6.61 us
  transfers between devices with their start and end apart: 25, of which 7 were waited for; matrix products, arithmetic and copies ran while one was open for 1% of the time, Pallas kernels for 28%

profile of v8, /device:TPU:0, one launch (start us, length us, event | category | flops | bytes accessed | tf_op | source)
XLA Modules:
  0.0 104.6 jit_solution(13874797302724861866)
XLA Ops:
  0.6 1.4 %copy-done.2 = bf16[1,32,32,768]{3,2,1,0:T(8,128)(2,1)S(1)} copy-done((bf16[1,32,32,768]{3,2,1,0:T(8,128)(2,1)S(1)}, bf16[1,32,32,768]{3,2,1,0:T(8,128)(2,1)}, u32[]{:S(2)}) %copy-start.2) | copy-done | bytes 1572888
  2.1 0.7 copy-done.9
  2.8 1.7 %pick.1 = bf16[320,768]{1,0:T(8,128)(2,1)} custom-call(s32[8,35]{1,0:T(8,128)S(1)} %bitcast.18, bf16[1024,768]{1,0:T(8,128)(2,1)S(1)} %bitcast.16), custom_call_target="tpu_custom_call" | custom-call | flops 1000 | bytes 1003 | tf_op jit(solution)/shard_map/pick/pallas_call | solution.py:448
  4.5 7.3 %all-to-all-start = ((bf16[8,40,768]{2,1,0:T(8,128)(2,1)}), bf16[8,40,768]{2,1,0:T(8,128)(2,1)S(1)}, u32[]{:S(2)}, u32[]{:S(2)}) async-start(bf16[8,40,768]{2,1,0:T(8,128)(2,1)} %bitcast.5), calls=%async_computation | async-start | bytes 983040 | tf_op jit(solution)/shard_map/all_to_all | solution.py:458
  11.8 1.6 %collective-permute-start.1 = (bf16[256,768]{1,0:T(8,128)(2,1)S(1)}, bf16[256,768]{1,0:T(8,128)(2,1)S(1)}, u32[]{:S(2)}, u32[]{:S(2)}) collective-permute-start(bf16[256,768]{1,0:T(8,128)(2,1)S(1)} %bitcast.11), channel_id=1, source_target_pairs={{0,2},{1,3},{2,0},{3,1},{4,6},{5,7},{6,4},{7,5},{8,10},{9,11},{10,... | collective-permute-start | bytes 1179656 | tf_op jit(solution)/shard_map/ppermute | solution.py:403
  13.4 0.3 collective-permute-start.2
  13.7 2.0 %copy-done.1 = bf16[768,2304]{1,0:T(8,128)(2,1)S(1)} copy-done((bf16[768,2304]{1,0:T(8,128)(2,1)S(1)}, bf16[768,2304]{1,0:T(8,128)(2,1)}, u32[]{:S(2)}) %copy-start.1) | copy-done | bytes 3538968
  15.7 1.0 prep.1
  16.7 1.7 %copy-done.13 = bf16[2304,768]{1,0:T(8,128)(2,1)} copy-done((bf16[2304,768]{1,0:T(8,128)(2,1)}, bf16[2304,768]{1,0:T(8,128)(2,1)S(1)}, u32[]{:S(2)}) %copy-start.13) | copy-done | bytes 3538968
  18.4 0.7 copy-done.19
  19.2 7.2 %all-to-all-done = bf16[8,40,768]{2,1,0:T(8,128)(2,1)S(1)} async-done(((bf16[8,40,768]{2,1,0:T(8,128)(2,1)}), bf16[8,40,768]{2,1,0:T(8,128)(2,1)S(1)}, u32[]{:S(2)}, u32[]{:S(2)}) %all-to-all-start) | async-done | bytes 491552 | tf_op jit(solution)/shard_map/all_to_all | solution.py:458
  26.4 0.7 norm.1
  27.2 2.0 %copy-done.14 = bf16[2304,768]{1,0:T(8,128)(2,1)S(1)} copy-done((bf16[2304,768]{1,0:T(8,128)(2,1)S(1)}, bf16[2304,768]{1,0:T(8,128)(2,1)}, u32[]{:S(2)}) %copy-start.14) | copy-done | bytes 3538968
  29.2 1.1 %project.1 = (f32[1536,256]{1,0:T(8,128)S(1)}, f32[24,256]{1,0:T(8,128)S(1)}, bf16[768,256]{1,0:T(8,128)(2,1)S(1)}) custom-call(bf16[256,768]{1,0:T(8,128)(2,1)S(1)} %get-tuple-element.129.normed_ref.refs_4_, bf16[2304,768]{1,0:T(8,128)(2,1)S(1)} %copy-done.14), custom_call_target="tpu_custom_call" | custom-call | flops 2000000000 | bytes 6667666 | tf_op jit(solution)/shard_map/project/pallas_call | solution.py:494
  30.3 1.6 %collective-permute-start.3 = (bf16[256,768]{1,0:T(8,128)(2,1)S(1)}, bf16[256,768]{1,0:T(8,128)(2,1)S(1)}, u32[]{:S(2)}, u32[]{:S(2)}) collective-permute-start(bf16[256,768]{1,0:T(8,128)(2,1)S(1)} %get-tuple-element.129.normed_ref.refs_4_), channel_id=1, source_target_pairs={{0,2},{1,3},{2,0},{3,1},{4,6},{5,7},{6,4},{7,5},{8,10},{9,11},{10,... | collective-permute-start | bytes 1179656 | tf_op jit(solution)/shard_map/ppermute | solution.py:403
  32.0 8.5 %encode.1 = (bf16[320,384]{1,0:T(8,128)(2,1)}, bf16[768,256]{1,0:T(8,128)(2,1)S(1)}, bf16[768,256]{1,0:T(8,128)(2,1)S(1)}, bf16[768,256]{1,0:T(8,128)(2,1)S(1)}, bf16[768,256]{1,0:T(8,128)(2,1)S(1)}) custom-call(s32[1,256]{1,0:T(1,128)S(1)} %bitcast.21, f32[12]{0:T(128)S(1)} %copy-done.23, f32[1,256]{1,0:T(1,128)S(1)} %get-tuple-element.84.place_ref, ...), custom_call_target="tpu_custom_call" | custom-call | flops 8000000000 | bytes 26667666 | tf_op jit(solution)/shard_map/encode/pallas_call | solution.py:505
  40.5 0.8 copy-done.16
  41.2 0.7 copy-done.18
  42.0 4.0 %all-to-all-start.1 = ((bf16[8,40,384]{2,1,0:T(8,128)(2,1)}), bf16[8,40,384]{2,1,0:T(8,128)(2,1)}, u32[]{:S(2)}, u32[]{:S(2)}) async-start(bf16[8,40,384]{2,1,0:T(8,128)(2,1)} %bitcast.7), calls=%async_computation.1 | async-start | bytes 491520 | tf_op jit(solution)/shard_map/all_to_all | solution.py:527
  46.1 0.6 collective-permute-start.5
  46.7 0.5 collective-permute-start.6
  47.2 1.3 %collective-permute-start.7 = (bf16[768,256]{1,0:T(8,128)(2,1)}, bf16[768,256]{1,0:T(8,128)(2,1)}, u32[]{:S(2)}, u32[]{:S(2)}) collective-permute-start(bf16[768,256]{1,0:T(8,128)(2,1)} %copy-done.16), channel_id=1, source_target_pairs={{0,3},{1,2},{2,1},{3,0},{4,7},{5,6},{6,5},{7,4},{8,11},{9,10},{10,... | collective-permute-start | bytes 1179656 | tf_op jit(solution)/shard_map/ppermute | solution.py:403
  48.5 1.3 %reshape.44.mask_ref = bf16[1,384]{1,0:T(2,128)(2,1)} reshape(bf16[384]{0:T(512)(128)(2,1)} %param.24) | data formatting | bytes 1536 | tf_op jit(solution)/shard_map/reshape | solution.py:568
  49.8 6.6 %all-to-all-done.1 = bf16[8,40,384]{2,1,0:T(8,128)(2,1)} async-done(((bf16[8,40,384]{2,1,0:T(8,128)(2,1)}), bf16[8,40,384]{2,1,0:T(8,128)(2,1)}, u32[]{:S(2)}, u32[]{:S(2)}) %all-to-all-start.1) | async-done | bytes 245792 | tf_op jit(solution)/shard_map/all_to_all | solution.py:527
  56.4 0.7 copy-done.12
  57.1 2.4 %fill.1 = (bf16[1024,384]{1,0:T(8,128)(2,1)S(1)}, bf16[96,384]{1,0:T(8,128)(2,1)S(1)}, bf16[96,384]{1,0:T(8,128)(2,1)S(1)}, bf16[96,384]{1,0:T(8,128)(2,1)S(1)}) custom-call(s32[8,35]{1,0:T(8,128)S(1)} %bitcast.19, f32[2,1408]{1,0:T(2,128)S(1)} %copy-done.11, bf16[1,384]{1,0:T(2,128)(2,1)S(1)} %copy-done.12, bf16[320,384]{1,0:T(8,128)(2,1)} %bitcast.8.got_ref), custom_call_target="tpu_custom_call" | custom-call | flops 1000 | bytes 1003 | tf_op jit(solution)/shard_map/fill/pallas_call | solution.py:558
  59.6 2.0 %collective-permute-start.9 = (bf16[96,384]{1,0:T(8,128)(2,1)S(1)}, bf16[96,384]{1,0:T(8,128)(2,1)S(1)}, u32[]{:S(2)}, u32[]{:S(2)}) collective-permute-start(bf16[96,384]{1,0:T(8,128)(2,1)S(1)} %get-tuple-element.107), channel_id=1, source_target_pairs={{0,4},{4,8},{8,12},{12,0},{1,5},{5,9},{9,13},{13,1},{2,6},{6,10},{... | collective-permute-start | bytes 221192 | tf_op jit(solution)/shard_map/ppermute | solution.py:408
  61.6 3.1 %collective-permute-done.10.right_ref.right = bf16[96,384]{1,0:T(8,128)(2,1)S(1)} collective-permute-done((bf16[96,384]{1,0:T(8,128)(2,1)S(1)}, bf16[96,384]{1,0:T(8,128)(2,1)S(1)}, u32[]{:S(2)}, u32[]{:S(2)}) %collective-permute-start.10) | collective-permute-done | bytes 73760 | tf_op jit(solution)/shard_map/ppermute | solution.py:408
  64.7 1.1 %collective-permute-done.9.left_ref.left = bf16[96,384]{1,0:T(8,128)(2,1)S(1)} collective-permute-done((bf16[96,384]{1,0:T(8,128)(2,1)S(1)}, bf16[96,384]{1,0:T(8,128)(2,1)S(1)}, u32[]{:S(2)}, u32[]{:S(2)}) %collective-permute-start.9) | collective-permute-done | bytes 73760 | tf_op jit(solution)/shard_map/ppermute | solution.py:408
  65.8 0.7 collective-permute-start.12
  66.5 2.5 %terms0.1 = (f32[4,96,384]{2,1,0:T(8,128)S(1)}, bf16[4,96,384]{2,1,0:T(8,128)(2,1)S(1)}) custom-call(bf16[768,256]{1,0:T(8,128)(2,1)S(1)} %get-tuple-element.125.refs_0_, bf16[768,256]{1,0:T(8,128)(2,1)S(1)} %collective-permute-done.5.refs_1_, bf16[768,256]{1,0:T(8,128)(2,1)} %collective-permute-done.6.refs_2_, ...), custom_call_target="tpu_custom_call" | custom-call | flops 1000 | bytes 1003 | tf_op jit(solution)/shard_map/terms0/pallas_call | solution.py:609
  69.0 1.4 %collective-permute-start.11 = (bf16[4,96,384]{2,1,0:T(8,128)(2,1)S(1)}, bf16[4,96,384]{2,1,0:T(8,128)(2,1)S(1)}, u32[]{:S(2)}, u32[]{:S(2)}) collective-permute-start(bf16[4,96,384]{2,1,0:T(8,128)(2,1)S(1)} %get-tuple-element.123), channel_id=1, source_target_pairs={{0,16},{16,0},{1,17},{17,1},{2,18},{18,2},{3,19},{19,3},{4,20},{20... | collective-permute-start | bytes 884744 | tf_op jit(solution)/shard_map/ppermute | solution.py:408
  70.5 2.3 %terms1.1 = (f32[4,96,384]{2,1,0:T(8,128)S(1)}, bf16[4,96,384]{2,1,0:T(8,128)(2,1)S(1)}) custom-call(bf16[768,256]{1,0:T(8,128)(2,1)S(1)} %get-tuple-element.125.refs_0_, bf16[768,256]{1,0:T(8,128)(2,1)S(1)} %collective-permute-done.5.refs_1_, bf16[768,256]{1,0:T(8,128)(2,1)} %collective-permute-done.6.refs_2_, ...), custom_call_target="tpu_custom_call" | custom-call | flops 1000 | bytes 1003 | tf_op jit(solution)/shard_map/terms1/pallas_call | solution.py:609
  72.8 0.7 collective-permute-start.16
  73.5 7.5 %mix.1.normed_ref = bf16[1024,384]{1,0:T(8,128)(2,1)S(1)} custom-call(bf16[1024,384]{1,0:T(8,128)(2,1)S(1)} %get-tuple-element.124.grid.grid_ref, bf16[96,384]{1,0:T(8,128)(2,1)S(1)} %collective-permute-done.9.left_ref.left, bf16[96,384]{1,0:T(8,128)(2,1)S(1)} %collective-permute-done.10.right_ref.right, bf16[128,384]{1,0:T(8,128)(2,1)S(1)} %collective-permute-done.12.a, ...), custom_call_target="tpu_custom_call" | custom-call | flops 1000 | bytes 1003 | tf_op jit(solution)/shard_map/mix/pallas_call | solution.py:625
  81.1 1.3 %collective-permute-start.13 = (bf16[96,384]{1,0:T(8,128)(2,1)S(1)}, bf16[96,384]{1,0:T(8,128)(2,1)S(1)}, u32[]{:S(2)}, u32[]{:S(2)}) collective-permute-start(bf16[96,384]{1,0:T(8,128)(2,1)S(1)} %get-tuple-element.143), channel_id=1, source_target_pairs={{0,4},{4,8},{8,12},{12,0},{1,5},{5,9},{9,13},{13,1},{2,6},{6,10},{... | collective-permute-start | bytes 221192 | tf_op jit(solution)/shard_map/ppermute | solution.py:408
  82.4 2.4 %collective-permute-start.14 = (bf16[96,384]{1,0:T(8,128)(2,1)S(1)}, bf16[96,384]{1,0:T(8,128)(2,1)S(1)}, u32[]{:S(2)}, u32[]{:S(2)}) collective-permute-start(bf16[96,384]{1,0:T(8,128)(2,1)S(1)} %get-tuple-element.144), channel_id=1, source_target_pairs={{0,8},{4,12},{8,0},{12,4},{1,9},{5,13},{9,1},{13,5},{2,10},{6,14},... | collective-permute-start | bytes 221192 | tf_op jit(solution)/shard_map/ppermute | solution.py:408
  84.8 1.5 %collective-permute-start.15 = (bf16[96,384]{1,0:T(8,128)(2,1)S(1)}, bf16[96,384]{1,0:T(8,128)(2,1)S(1)}, u32[]{:S(2)}, u32[]{:S(2)}) collective-permute-start(bf16[96,384]{1,0:T(8,128)(2,1)S(1)} %get-tuple-element.145), channel_id=1, source_target_pairs={{0,12},{4,0},{8,4},{12,8},{1,13},{5,1},{9,5},{13,9},{2,14},{6,2},{... | collective-permute-start | bytes 221192 | tf_op jit(solution)/shard_map/ppermute | solution.py:408
  86.3 0.6 collective-permute-start.17
  86.9 1.9 %collective-permute-start.18 = (bf16[96,384]{1,0:T(8,128)(2,1)S(1)}, bf16[96,384]{1,0:T(8,128)(2,1)S(1)}, u32[]{:S(2)}, u32[]{:S(2)}) collective-permute-start(bf16[96,384]{1,0:T(8,128)(2,1)S(1)} %get-tuple-element.151), channel_id=1, source_target_pairs={{0,8},{4,12},{8,0},{12,4},{1,9},{5,13},{9,1},{13,5},{2,10},{6,14},... | collective-permute-start | bytes 221192 | tf_op jit(solution)/shard_map/ppermute | solution.py:408
  88.8 1.4 %collective-permute-start.19 = (bf16[96,384]{1,0:T(8,128)(2,1)S(1)}, bf16[96,384]{1,0:T(8,128)(2,1)S(1)}, u32[]{:S(2)}, u32[]{:S(2)}) collective-permute-start(bf16[96,384]{1,0:T(8,128)(2,1)S(1)} %get-tuple-element.152), channel_id=1, source_target_pairs={{0,12},{4,0},{8,4},{12,8},{1,13},{5,1},{9,5},{13,9},{2,14},{6,2},{... | collective-permute-start | bytes 221192 | tf_op jit(solution)/shard_map/ppermute | solution.py:408
  90.2 3.4 %feed.1 = f32[1024,128]{1,0:T(8,128)} custom-call(bf16[1024,384]{1,0:T(8,128)(2,1)S(1)} %mix.1.normed_ref, bf16[1024,384]{1,0:T(8,128)(2,1)S(1)} %get-tuple-element.124.grid.grid_ref, bf16[384,768]{1,0:T(8,128)(2,1)S(1)} %copy-done.5, bf16[768,384]{1,0:T(8,128)(2,1)S(1)} %copy-done.6, bf16[384,128]{1,0:T(8,128)(2,1)S(1)} %copy-done.7), custom_call_target="tpu_custom_call" | custom-call | flops 1000 | bytes 1003 | tf_op jit(solution)/shard_map/feed/pallas_call | solution.py:653
  93.6 3.2 %collective-permute-done.18.refs_6_ = bf16[96,384]{1,0:T(8,128)(2,1)S(1)} collective-permute-done((bf16[96,384]{1,0:T(8,128)(2,1)S(1)}, bf16[96,384]{1,0:T(8,128)(2,1)S(1)}, u32[]{:S(2)}, u32[]{:S(2)}) %collective-permute-start.18) | collective-permute-done | bytes 73760 | tf_op jit(solution)/shard_map/ppermute | solution.py:408
  96.8 0.1 close.1.own_ref
  96.9 0.6 collective-permute-start.21
  97.5 4.6 %collective-permute-done.21.two_ref = bf16[96,768]{1,0:T(8,128)(2,1)S(1)} collective-permute-done((bf16[96,768]{1,0:T(8,128)(2,1)S(1)}, bf16[96,768]{1,0:T(8,128)(2,1)S(1)}, u32[]{:S(2)}, u32[]{:S(2)}) %collective-permute-start.21) | collective-permute-done | bytes 147488 | tf_op jit(solution)/shard_map/ppermute | solution.py:403
  102.1 1.4 %collective-permute-done.22.three_ref = bf16[96,768]{1,0:T(8,128)(2,1)S(1)} collective-permute-done((bf16[96,768]{1,0:T(8,128)(2,1)S(1)}, bf16[96,768]{1,0:T(8,128)(2,1)S(1)}, u32[]{:S(2)}, u32[]{:S(2)}) %collective-permute-start.22) | collective-permute-done | bytes 147488 | tf_op jit(solution)/shard_map/ppermute | solution.py:403
  103.5 1.2 %spread.1 = f32[384,768]{1,0:T(8,128)} custom-call(bf16[96,768]{1,0:T(8,128)(2,1)S(1)} %close.1.own_ref, bf16[96,768]{1,0:T(8,128)(2,1)S(1)} %collective-permute-done.20.one_ref, bf16[96,768]{1,0:T(8,128)(2,1)S(1)} %collective-permute-done.21.two_ref, bf16[96,768]{1,0:T(8,128)(2,1)S(1)} %collective-permute-done.22.three_ref), custom_call_target="tpu_custom_call" | custom-call | flops 1000 | bytes 1003 | tf_op jit(solution)/shard_map/spread/pallas_call | solution.py:674
  (66 shorter events, 0.5 us)
Async XLA Ops:
  0.6 11.1 %copy-start = (bf16[1,1,1,256,768]{4,3,2,1,0:T(8,128)(2,1)S(1)}, bf16[1,1,1,256,768]{4,3,2,1,0:T(8,128)(2,1)}, u32[]{:S(2)}) copy-start(bf16[1,1,1,256,768]{4,3,2,1,0:T(8,128)(2,1)} %param.19) | copy-start | bytes 1179652
  0.6 1.5 %copy-start.2 = (bf16[1,32,32,768]{3,2,1,0:T(8,128)(2,1)S(1)}, bf16[1,32,32,768]{3,2,1,0:T(8,128)(2,1)}, u32[]{:S(2)}) copy-start(bf16[1,32,32,768]{3,2,1,0:T(8,128)(2,1)} %param.15) | copy-start | bytes 4718596
  2.1 0.7 copy-start.9
  2.8 10.9 %copy-start.3 = (bf16[768,768]{1,0:T(8,128)(2,1)S(1)}, bf16[768,768]{1,0:T(8,128)(2,1)}, u32[]{:S(2)}) copy-start(bf16[768,768]{1,0:T(8,128)(2,1)} %wout_ref.3) | copy-start | bytes 3538948
  4.5 21.9 %all-to-all-start = ((bf16[8,40,768]{2,1,0:T(8,128)(2,1)}), bf16[8,40,768]{2,1,0:T(8,128)(2,1)S(1)}, u32[]{:S(2)}, u32[]{:S(2)}) async-start(bf16[8,40,768]{2,1,0:T(8,128)(2,1)} %bitcast.5), calls=%async_computation | async-start | bytes 983040 | tf_op jit(solution)/shard_map/all_to_all | solution.py:458
  11.7 14.7 %copy-start.21 = (s32[1,1,1,256]{3,2,1,0:T(1,128)S(1)}, s32[1,1,1,256]{3,2,1,0:T(1,128)}, u32[]{:S(2)}) copy-start(s32[1,1,1,256]{3,2,1,0:T(1,128)} %param.17) | copy-start | bytes 3076
  11.7 34.3 %collective-permute-start = (bf16[256,768]{1,0:T(8,128)(2,1)S(1)}, bf16[256,768]{1,0:T(8,128)(2,1)S(1)}, u32[]{:S(2)}, u32[]{:S(2)}) collective-permute-start(bf16[256,768]{1,0:T(8,128)(2,1)S(1)} %bitcast.10), channel_id=1, source_target_pairs={{0,1},{1,0},{2,3},{3,2},{4,5},{5,4},{6,7},{7,6},{8,9},{9,8},{10,11... | collective-permute-start | bytes 1179656 | tf_op jit(solution)/shard_map/ppermute | solution.py:403
  11.8 34.2 %collective-permute-start.1 = (bf16[256,768]{1,0:T(8,128)(2,1)S(1)}, bf16[256,768]{1,0:T(8,128)(2,1)S(1)}, u32[]{:S(2)}, u32[]{:S(2)}) collective-permute-start(bf16[256,768]{1,0:T(8,128)(2,1)S(1)} %bitcast.11), channel_id=1, source_target_pairs={{0,2},{1,3},{2,0},{3,1},{4,6},{5,7},{6,4},{7,5},{8,10},{9,11},{10,... | collective-permute-start | bytes 1179656 | tf_op jit(solution)/shard_map/ppermute | solution.py:403
  13.4 32.7 %collective-permute-start.2 = (bf16[256,768]{1,0:T(8,128)(2,1)S(1)}, bf16[256,768]{1,0:T(8,128)(2,1)S(1)}, u32[]{:S(2)}, u32[]{:S(2)}) collective-permute-start(bf16[256,768]{1,0:T(8,128)(2,1)S(1)} %bitcast.12), channel_id=1, source_target_pairs={{0,3},{1,2},{2,1},{3,0},{4,7},{5,6},{6,5},{7,4},{8,11},{9,10},{10,... | collective-permute-start | bytes 1179656 | tf_op jit(solution)/shard_map/ppermute | solution.py:403
  13.7 2.0 %copy-start.1 = (bf16[768,2304]{1,0:T(8,128)(2,1)S(1)}, bf16[768,2304]{1,0:T(8,128)(2,1)}, u32[]{:S(2)}) copy-start(bf16[768,2304]{1,0:T(8,128)(2,1)} %wqkv_ref.1) | copy-start | bytes 10616836
  16.7 1.8 %copy-start.13 = (bf16[2304,768]{1,0:T(8,128)(2,1)}, bf16[2304,768]{1,0:T(8,128)(2,1)S(1)}, u32[]{:S(2)}) copy-start(bf16[2304,768]{1,0:T(8,128)(2,1)S(1)} %get-tuple-element.82.wqkv_t_ref) | copy-start | bytes 10616836
  18.4 0.7 copy-start.19
  27.2 2.0 %copy-start.14 = (bf16[2304,768]{1,0:T(8,128)(2,1)S(1)}, bf16[2304,768]{1,0:T(8,128)(2,1)}, u32[]{:S(2)}) copy-start(bf16[2304,768]{1,0:T(8,128)(2,1)} %copy-done.13) | copy-start | bytes 10616836
  29.2 2.8 %copy-start.4 = (bf16[768,768]{1,0:T(8,128)(2,1)S(1)}, bf16[768,768]{1,0:T(8,128)(2,1)}, u32[]{:S(2)}) copy-start(bf16[768,768]{1,0:T(8,128)(2,1)} %wout_ref.3) | copy-start | bytes 3538948
  29.2 2.8 %copy-start.15 = (bf16[768,384]{1,0:T(8,128)(2,1)S(1)}, bf16[768,384]{1,0:T(8,128)(2,1)}, u32[]{:S(2)}) copy-start(bf16[768,384]{1,0:T(8,128)(2,1)} %wdec_ref.1) | copy-start | bytes 1769476
  29.2 2.8 %copy-start.20 = (bf16[768,256]{1,0:T(8,128)(2,1)S(1)}, bf16[768,256]{1,0:T(8,128)(2,1)}, u32[]{:S(2)}) copy-start(bf16[768,256]{1,0:T(8,128)(2,1)} %copy-done.19) | copy-start | bytes 1179652
  29.2 2.8 %copy-start.22 = (s32[1,1,1,256]{3,2,1,0:T(1,128)S(1)}, s32[1,1,1,256]{3,2,1,0:T(1,128)}, u32[]{:S(2)}) copy-start(s32[1,1,1,256]{3,2,1,0:T(1,128)} %param.18) | copy-start | bytes 3076
  29.2 2.8 %copy-start.23 = (f32[12]{0:T(128)S(1)}, f32[12]{0:T(128)}, u32[]{:S(2)}) copy-start(f32[12]{0:T(128)} %scale_ref.1) | copy-start | bytes 148
  30.3 15.7 %collective-permute-start.3 = (bf16[256,768]{1,0:T(8,128)(2,1)S(1)}, bf16[256,768]{1,0:T(8,128)(2,1)S(1)}, u32[]{:S(2)}, u32[]{:S(2)}) collective-permute-start(bf16[256,768]{1,0:T(8,128)(2,1)S(1)} %get-tuple-element.129.normed_ref.refs_4_), channel_id=1, source_target_pairs={{0,2},{1,3},{2,0},{3,1},{4,6},{5,7},{6,4},{7,5},{8,10},{9,11},{10,... | collective-permute-start | bytes 1179656 | tf_op jit(solution)/shard_map/ppermute | solution.py:403
  31.9 14.2 %collective-permute-start.4 = (bf16[256,768]{1,0:T(8,128)(2,1)S(1)}, bf16[256,768]{1,0:T(8,128)(2,1)S(1)}, u32[]{:S(2)}, u32[]{:S(2)}) collective-permute-start(bf16[256,768]{1,0:T(8,128)(2,1)S(1)} %get-tuple-element.129.normed_ref.refs_4_), channel_id=1, source_target_pairs={{0,1},{1,0},{2,3},{3,2},{4,5},{5,4},{6,7},{7,6},{8,9},{9,8},{10,11... | collective-permute-start | bytes 1179656 | tf_op jit(solution)/shard_map/ppermute | solution.py:403
  31.9 24.4 %copy-start.10 = (s32[1,1,1,8,35]{4,3,2,1,0:T(8,128)S(1)}, s32[1,1,1,8,35]{4,3,2,1,0:T(8,128)}, u32[]{:S(2)}) copy-start(s32[1,1,1,8,35]{4,3,2,1,0:T(8,128)} %param.16) | copy-start | bytes 3364
  32.0 24.4 %copy-start.11 = (f32[2,1408]{1,0:T(2,128)S(1)}, f32[2,1408]{1,0:T(2,128)}, u32[]{:S(2)}) copy-start(f32[2,1408]{1,0:T(2,128)} %constant.2.clone.ids_ref) | copy-start | bytes 33796
  40.5 0.8 copy-start.16
  41.2 0.7 copy-start.18
  41.2 4.8 %copy-start.17 = (bf16[768,256]{1,0:T(8,128)(2,1)}, bf16[768,256]{1,0:T(8,128)(2,1)S(1)}, u32[]{:S(2)}) copy-start(bf16[768,256]{1,0:T(8,128)(2,1)S(1)} %get-tuple-element.97) | copy-start | bytes 1179652
  42.0 14.4 %all-to-all-start.1 = ((bf16[8,40,384]{2,1,0:T(8,128)(2,1)}), bf16[8,40,384]{2,1,0:T(8,128)(2,1)}, u32[]{:S(2)}, u32[]{:S(2)}) async-start(bf16[8,40,384]{2,1,0:T(8,128)(2,1)} %bitcast.7), calls=%async_computation.1 | async-start | bytes 491520 | tf_op jit(solution)/shard_map/all_to_all | solution.py:527
  46.1 10.3 %collective-permute-start.5 = (bf16[768,256]{1,0:T(8,128)(2,1)}, bf16[768,256]{1,0:T(8,128)(2,1)S(1)}, u32[]{:S(2)}, u32[]{:S(2)}) collective-permute-start(bf16[768,256]{1,0:T(8,128)(2,1)} %copy-done.18), channel_id=1, source_target_pairs={{0,1},{1,0},{2,3},{3,2},{4,5},{5,4},{6,7},{7,6},{8,9},{9,8},{10,11... | collective-permute-start | bytes 1179656 | tf_op jit(solution)/shard_map/ppermute | solution.py:403
  46.6 9.8 %collective-permute-start.8 = (bf16[256,768]{1,0:T(8,128)(2,1)S(1)}, bf16[256,768]{1,0:T(8,128)(2,1)}, u32[]{:S(2)}, u32[]{:S(2)}) collective-permute-start(bf16[256,768]{1,0:T(8,128)(2,1)S(1)} %collective-permute-done.3.refs_6_), channel_id=1, source_target_pairs={{0,1},{1,0},{2,3},{3,2},{4,5},{5,4},{6,7},{7,6},{8,9},{9,8},{10,11... | collective-permute-start | bytes 1179656 | tf_op jit(solution)/shard_map/ppermute | solution.py:403
  46.7 19.8 %collective-permute-start.6 = (bf16[768,256]{1,0:T(8,128)(2,1)}, bf16[768,256]{1,0:T(8,128)(2,1)}, u32[]{:S(2)}, u32[]{:S(2)}) collective-permute-start(bf16[768,256]{1,0:T(8,128)(2,1)} %copy-done.17), channel_id=1, source_target_pairs={{0,2},{1,3},{2,0},{3,1},{4,6},{5,7},{6,4},{7,5},{8,10},{9,11},{10,... | collective-permute-start | bytes 1179656 | tf_op jit(solution)/shard_map/ppermute | solution.py:403
  47.2 19.3 %collective-permute-start.7 = (bf16[768,256]{1,0:T(8,128)(2,1)}, bf16[768,256]{1,0:T(8,128)(2,1)}, u32[]{:S(2)}, u32[]{:S(2)}) collective-permute-start(bf16[768,256]{1,0:T(8,128)(2,1)} %copy-done.16), channel_id=1, source_target_pairs={{0,3},{1,2},{2,1},{3,0},{4,7},{5,6},{6,5},{7,4},{8,11},{9,10},{10,... | collective-permute-start | bytes 1179656 | tf_op jit(solution)/shard_map/ppermute | solution.py:403
  59.5 5.2 %collective-permute-start.10 = (bf16[96,384]{1,0:T(8,128)(2,1)S(1)}, bf16[96,384]{1,0:T(8,128)(2,1)S(1)}, u32[]{:S(2)}, u32[]{:S(2)}) collective-permute-start(bf16[96,384]{1,0:T(8,128)(2,1)S(1)} %get-tuple-element.108), channel_id=1, source_target_pairs={{0,12},{4,0},{8,4},{12,8},{1,13},{5,1},{9,5},{13,9},{2,14},{6,2},{... | collective-permute-start | bytes 221192 | tf_op jit(solution)/shard_map/ppermute | solution.py:408
  59.6 6.2 %collective-permute-start.9 = (bf16[96,384]{1,0:T(8,128)(2,1)S(1)}, bf16[96,384]{1,0:T(8,128)(2,1)S(1)}, u32[]{:S(2)}, u32[]{:S(2)}) collective-permute-start(bf16[96,384]{1,0:T(8,128)(2,1)S(1)} %get-tuple-element.107), channel_id=1, source_target_pairs={{0,4},{4,8},{8,12},{12,0},{1,5},{5,9},{9,13},{13,1},{2,6},{6,10},{... | collective-permute-start | bytes 221192 | tf_op jit(solution)/shard_map/ppermute | solution.py:408
  65.8 4.7 %collective-permute-start.12 = (bf16[128,384]{1,0:T(8,128)(2,1)S(1)}, bf16[128,384]{1,0:T(8,128)(2,1)S(1)}, u32[]{:S(2)}, u32[]{:S(2)}) collective-permute-start(bf16[128,384]{1,0:T(8,128)(2,1)S(1)} %rim.1), channel_id=1, source_target_pairs={{0,16},{16,0},{1,17},{17,1},{2,18},{18,2},{3,19},{19,3},{4,20},{20... | collective-permute-start | bytes 294920 | tf_op jit(solution)/shard_map/ppermute | solution.py:408
  69.0 4.5 %copy-start.8 = (f32[7,7,384]{2,1,0:T(8,128)S(1)}, f32[7,7,384]{2,1,0:T(8,128)}, u32[]{:S(2)}) copy-start(f32[7,7,384]{2,1,0:T(8,128)} %refs_0_.1) | copy-start | bytes 225796
  69.0 12.0 %collective-permute-start.11 = (bf16[4,96,384]{2,1,0:T(8,128)(2,1)S(1)}, bf16[4,96,384]{2,1,0:T(8,128)(2,1)S(1)}, u32[]{:S(2)}, u32[]{:S(2)}) collective-permute-start(bf16[4,96,384]{2,1,0:T(8,128)(2,1)S(1)} %get-tuple-element.123), channel_id=1, source_target_pairs={{0,16},{16,0},{1,17},{17,1},{2,18},{18,2},{3,19},{19,3},{4,20},{20... | collective-permute-start | bytes 884744 | tf_op jit(solution)/shard_map/ppermute | solution.py:408
  72.8 13.5 %collective-permute-start.16 = (bf16[4,96,384]{2,1,0:T(8,128)(2,1)S(1)}, bf16[4,96,384]{2,1,0:T(8,128)(2,1)S(1)}, u32[]{:S(2)}, u32[]{:S(2)}) collective-permute-start(bf16[4,96,384]{2,1,0:T(8,128)(2,1)S(1)} %get-tuple-element.146), channel_id=1, source_target_pairs={{0,16},{16,0},{1,17},{17,1},{2,18},{18,2},{3,19},{19,3},{4,20},{20... | collective-permute-start | bytes 884744 | tf_op jit(solution)/shard_map/ppermute | solution.py:408
  73.5 16.7 %copy-start.5 = (bf16[384,768]{1,0:T(8,128)(2,1)S(1)}, bf16[384,768]{1,0:T(8,128)(2,1)}, u32[]{:S(2)}) copy-start(bf16[384,768]{1,0:T(8,128)(2,1)} %up_ref.1) | copy-start | bytes 1769476
  73.5 16.7 %copy-start.6 = (bf16[768,384]{1,0:T(8,128)(2,1)S(1)}, bf16[768,384]{1,0:T(8,128)(2,1)}, u32[]{:S(2)}) copy-start(bf16[768,384]{1,0:T(8,128)(2,1)} %down_ref.1) | copy-start | bytes 1769476
  73.5 16.7 %copy-start.7 = (bf16[384,128]{1,0:T(8,128)(2,1)S(1)}, bf16[384,128]{1,0:T(8,128)(2,1)}, u32[]{:S(2)}) copy-start(bf16[384,128]{1,0:T(8,128)(2,1)} %head_ref.1) | copy-start | bytes 294916
  81.1 7.8 %collective-permute-start.13 = (bf16[96,384]{1,0:T(8,128)(2,1)S(1)}, bf16[96,384]{1,0:T(8,128)(2,1)S(1)}, u32[]{:S(2)}, u32[]{:S(2)}) collective-permute-start(bf16[96,384]{1,0:T(8,128)(2,1)S(1)} %get-tuple-element.143), channel_id=1, source_target_pairs={{0,4},{4,8},{8,12},{12,0},{1,5},{5,9},{9,13},{13,1},{2,6},{6,10},{... | collective-permute-start | bytes 221192 | tf_op jit(solution)/shard_map/ppermute | solution.py:408
  82.4 11.1 %collective-permute-start.14 = (bf16[96,384]{1,0:T(8,128)(2,1)S(1)}, bf16[96,384]{1,0:T(8,128)(2,1)S(1)}, u32[]{:S(2)}, u32[]{:S(2)}) collective-permute-start(bf16[96,384]{1,0:T(8,128)(2,1)S(1)} %get-tuple-element.144), channel_id=1, source_target_pairs={{0,8},{4,12},{8,0},{12,4},{1,9},{5,13},{9,1},{13,5},{2,10},{6,14},... | collective-permute-start | bytes 221192 | tf_op jit(solution)/shard_map/ppermute | solution.py:408
  84.8 8.8 %collective-permute-start.15 = (bf16[96,384]{1,0:T(8,128)(2,1)S(1)}, bf16[96,384]{1,0:T(8,128)(2,1)S(1)}, u32[]{:S(2)}, u32[]{:S(2)}) collective-permute-start(bf16[96,384]{1,0:T(8,128)(2,1)S(1)} %get-tuple-element.145), channel_id=1, source_target_pairs={{0,12},{4,0},{8,4},{12,8},{1,13},{5,1},{9,5},{13,9},{2,14},{6,2},{... | collective-permute-start | bytes 221192 | tf_op jit(solution)/shard_map/ppermute | solution.py:408
  86.3 7.3 %collective-permute-start.17 = (bf16[96,384]{1,0:T(8,128)(2,1)S(1)}, bf16[96,384]{1,0:T(8,128)(2,1)S(1)}, u32[]{:S(2)}, u32[]{:S(2)}) collective-permute-start(bf16[96,384]{1,0:T(8,128)(2,1)S(1)} %get-tuple-element.150), channel_id=1, source_target_pairs={{0,4},{4,8},{8,12},{12,0},{1,5},{5,9},{9,13},{13,1},{2,6},{6,10},{... | collective-permute-start | bytes 221192 | tf_op jit(solution)/shard_map/ppermute | solution.py:408
  86.9 9.9 %collective-permute-start.18 = (bf16[96,384]{1,0:T(8,128)(2,1)S(1)}, bf16[96,384]{1,0:T(8,128)(2,1)S(1)}, u32[]{:S(2)}, u32[]{:S(2)}) collective-permute-start(bf16[96,384]{1,0:T(8,128)(2,1)S(1)} %get-tuple-element.151), channel_id=1, source_target_pairs={{0,8},{4,12},{8,0},{12,4},{1,9},{5,13},{9,1},{13,5},{2,10},{6,14},... | collective-permute-start | bytes 221192 | tf_op jit(solution)/shard_map/ppermute | solution.py:408
  88.8 7.9 %collective-permute-start.19 = (bf16[96,384]{1,0:T(8,128)(2,1)S(1)}, bf16[96,384]{1,0:T(8,128)(2,1)S(1)}, u32[]{:S(2)}, u32[]{:S(2)}) collective-permute-start(bf16[96,384]{1,0:T(8,128)(2,1)S(1)} %get-tuple-element.152), channel_id=1, source_target_pairs={{0,12},{4,0},{8,4},{12,8},{1,13},{5,1},{9,5},{13,9},{2,14},{6,2},{... | collective-permute-start | bytes 221192 | tf_op jit(solution)/shard_map/ppermute | solution.py:408
  96.9 5.2 %collective-permute-start.21 = (bf16[96,768]{1,0:T(8,128)(2,1)S(1)}, bf16[96,768]{1,0:T(8,128)(2,1)S(1)}, u32[]{:S(2)}, u32[]{:S(2)}) collective-permute-start(bf16[96,768]{1,0:T(8,128)(2,1)S(1)} %close.1.own_ref), channel_id=1, source_target_pairs={{0,2},{1,3},{2,0},{3,1},{4,6},{5,7},{6,4},{7,5},{8,10},{9,11},{10,... | collective-permute-start | bytes 442376 | tf_op jit(solution)/shard_map/ppermute | solution.py:403
  97.5 4.6 %collective-permute-start.20 = (bf16[96,768]{1,0:T(8,128)(2,1)S(1)}, bf16[96,768]{1,0:T(8,128)(2,1)S(1)}, u32[]{:S(2)}, u32[]{:S(2)}) collective-permute-start(bf16[96,768]{1,0:T(8,128)(2,1)S(1)} %close.1.own_ref), channel_id=1, source_target_pairs={{0,1},{1,0},{2,3},{3,2},{4,5},{5,4},{6,7},{7,6},{8,9},{9,8},{10,11... | collective-permute-start | bytes 442376 | tf_op jit(solution)/shard_map/ppermute | solution.py:403
  102.1 1.4 %collective-permute-start.22 = (bf16[96,768]{1,0:T(8,128)(2,1)S(1)}, bf16[96,768]{1,0:T(8,128)(2,1)S(1)}, u32[]{:S(2)}, u32[]{:S(2)}) collective-permute-start(bf16[96,768]{1,0:T(8,128)(2,1)S(1)} %collective-permute-done.21.two_ref), channel_id=1, source_target_pairs={{0,1},{1,0},{2,3},{3,2},{4,5},{5,4},{6,7},{7,6},{8,9},{9,8},{10,11... | collective-permute-start | bytes 442376 | tf_op jit(solution)/shard_map/ppermute | solution.py:403
  (1 other events, 0.7 us)

commit v9 on v8

--- a/solution.py
+++ b/solution.py
@@ -72,9 +72,11 @@
     out_ref[...] = mm(chosen, tok_ref[...]).astype(bf16)
 
 
-def prep_kernel(cot_ref, wout_ref, wqkv_ref, ga_ref, wqkv_t_ref):
+def prep_kernel(cot_ref, wout_ref, wqkv_ref, ga_ref, wqk_t_ref, wval_t_ref):
     ga_ref[...] = mm(wout_ref[...], cot_ref[...], NT).astype(bf16)
-    wqkv_t_ref[...] = jnp.transpose(wqkv_ref[...])
+    cut = wqk_t_ref.shape[0]
+    wqk_t_ref[...] = jnp.transpose(wqkv_ref[:, 0:cut])
+    wval_t_ref[...] = jnp.transpose(wqkv_ref[:, cut:])
 
 
 def norm_kernel(cap, padded, src_ref, arr_ref, normed_ref, enc_ref, place_ref):
@@ -93,7 +95,7 @@
     normed_ref[...] = (centred * lax.rsqrt(spread + norm_eps)).astype(bf16)
 
 
-def project_kernel(normed_ref, wqkv_t_ref, u_ref, len_ref, v_ref):
+def project_kernel(normed_ref, wqkv_t_ref, u_ref, len_ref):
     normed = normed_ref[...]
     width = normed.shape[1]
     heads = len_ref.shape[0] // 2
@@ -106,52 +108,41 @@
             at = t * width + h * size
             u_ref[at : at + size] = part * inv
             len_ref[t * heads + h : t * heads + h + 1] = inv
-    v_ref[...] = mm(wqkv_t_ref[2 * width : 3 * width], normed, NT).astype(bf16)
 
 
 def encode_kernel(
-    split, win_ref, scale_ref, place_ref, enc_ref, u_ref, len_ref, v_ref, ga_ref, wout_ref,
-    wdec_ref, out_ref, *refs,
+    split, win_ref, scale_ref, place_ref, enc_ref, normed_ref, u_ref, len_ref, ga_ref, wval_ref,
+    wout_ref, wdec_ref, out_ref, *refs,
 ):
     peer_refs = refs[:-3]
-    p_ref, att_ref, left_ref = refs[-3:]
+    v_ref, att_ref, left_ref = refs[-3:]
     rows, width = enc_ref.shape
-    heads = p_ref.shape[0]
+    heads = len_ref.shape[0] // 2
     size = width // heads
     slots = out_ref.shape[0]
+    v_ref[...] = mm(wval_ref[...], normed_ref[...], NT).astype(bf16)
     win = win_ref[...].astype(f32)
     same = column_of(win) == win
     for h in range(heads):
         lo, hi = h * size, (h + 1) * size
-        q = u_ref[lo:hi].astype(bf16)
-        k = u_ref[width + lo : width + hi].astype(bf16)
-        scores = mm(k, q, TN)
+        q = u_ref[lo:hi]
+        k = u_ref[width + lo : width + hi]
+        q_low, k_low = q.astype(bf16), k.astype(bf16)
+        value = v_ref[lo:hi]
+        ga = ga_ref[lo:hi]
+        scores = mm(k_low, q_low, TN)
         raised = jnp.where(same, jnp.exp(scores * scale_ref[h]), 0.0)
-        weights = (raised * (1.0 / jnp.sum(raised, axis=0, keepdims=True))).astype(bf16)
-        p_ref[h] = weights
-        att = mm(v_ref[lo:hi], weights).astype(bf16)
+        weights = raised * (1.0 / jnp.sum(raised, axis=0, keepdims=True))
+        low = weights.astype(bf16)
+        att = mm(value, low).astype(bf16)
         att_ref[lo:hi] = att
         emit(split, left_ref, 3 * width + lo, att)
-    attended = jnp.transpose(att_ref[...])
-    enc_out = (enc_ref[...].astype(f32) + mm(attended, wout_ref[...])).astype(bf16)
-    dec = mm(enc_out, wdec_ref[...]).astype(bf16)
-    places = lax.broadcasted_iota(jnp.int32, (slots, rows), 0).astype(f32)
-    put = (places == place_ref[...]).astype(f32).astype(bf16)
-    out_ref[...] = mm(put, dec).astype(bf16)
-    for h in range(heads):
-        lo, hi = h * size, (h + 1) * size
-        ga = ga_ref[lo:hi]
-        low = p_ref[h]
-        weights = low.astype(f32)
-        grad_soft = mm(v_ref[lo:hi], ga, TN)
-        part = weights * grad_soft
+        grad_v = mm(ga, low, NT)
+        part = weights * mm(value, ga, TN)
         total = jnp.sum(part, axis=0, keepdims=True)
         grad_scores = ((part - weights * total) * scale_ref[h]).astype(bf16)
-        q = u_ref[lo:hi]
-        k = u_ref[width + lo : width + hi]
-        grad_v = mm(ga, low, NT)
-        grad_q = mm(k.astype(bf16), grad_scores)
-        grad_k = mm(q.astype(bf16), grad_scores, NT)
+        grad_q = mm(k_low, grad_scores)
+        grad_k = mm(q_low, grad_scores, NT)
         grad_q = (grad_q - q * jnp.sum(q * grad_q, axis=0, keepdims=True)) * len_ref[h : h + 1]
         grad_k = (grad_k - k * jnp.sum(k * grad_k, axis=0, keepdims=True)) * len_ref[
             heads + h : heads + h + 1
@@ -159,6 +150,12 @@
         emit(split, left_ref, lo, grad_q.astype(bf16))
         emit(split, left_ref, width + lo, grad_k.astype(bf16))
         emit(split, left_ref, 2 * width + lo, grad_v.astype(bf16))
+    attended = jnp.transpose(att_ref[...])
+    enc_out = (enc_ref[...].astype(f32) + mm(attended, wout_ref[...])).astype(bf16)
+    dec = mm(enc_out, wdec_ref[...]).astype(bf16)
+    places = lax.broadcasted_iota(jnp.int32, (slots, rows), 0).astype(f32)
+    put = (places == place_ref[...]).astype(f32).astype(bf16)
+    out_ref[...] = mm(put, dec).astype(bf16)
     me = lax.axis_index("replica") if split is not None else 0
     for n, ref in enumerate(peer_refs):
         ref[...] = left_ref[me ^ n] if split is not None else left_ref[...]
@@ -294,48 +291,53 @@
 
 
 def conv_kernel_body(
-    shape, span, folded, grid_ref, left_ref, right_ref, rims, taps_ref, out_ref,
+    shape, span, first_line, folded, grid_ref, left_ref, right_ref, rims, taps_ref, out_ref,
     full_ref, wide_ref, mixed_ref,
 ):
-    lines, columns = shape
+    total, columns = shape
     rim = span // 2
     width = grid_ref.shape[-1]
+    lines = out_ref.shape[0] // columns
     lead = 8
-    full_ref[rim : rim + lines, lead : lead + columns] = (
-        grid_ref[...].astype(f32).reshape(lines, columns, width)
-    )
-    left = left_ref[...].astype(f32)
-    right = right_ref[...].astype(f32)
-    for x in range(lines):
-        full_ref[rim + x, lead - rim : lead] = left[rim * x : rim * (x + 1)]
-        full_ref[rim + x, lead + columns : lead + columns + rim] = right[rim * x : rim * (x + 1)]
-
-    def put(base, edge, first, last):
-        for i in range(rim):
-            full_ref[base + i, lead : lead + columns] = edge[columns * i : columns * (i + 1)]
-            full_ref[base + i, lead - rim : lead] = first[rim * i : rim * (i + 1)]
-            full_ref[base + i, lead + columns : lead + columns + rim] = last[
-                rim * i : rim * (i + 1)
-            ]
-
+    tall = lines + 2 * rim
     if folded:
-        far = rim + lines
-        base = jnp.where(lax.axis_index("eta") == 0, far, 0)
-        for i in range(rim):
-            full_ref[far - base + i] = jnp.zeros(full_ref.shape[1:], f32)
         size = rim * columns
         edge = rims[0][...].astype(f32)
         low = lax.axis_index("eta") == 0
         count = rim * rim
-        corners = []
+        outer = [edge[0:size]]
         for at in (size, size + 16):
             early, late = edge[at : at + count], edge[at + 16 - count : at + 16]
-            corners.append(jnp.where(low, early, late))
-        put(base, edge[0:size], *corners)
+            outer.append(jnp.where(low, early, late))
+        top = [jnp.where(low, 0.0, value) for value in outer]
+        bottom = [jnp.where(low, value, 0.0) for value in outer]
     else:
         pieces = [ref[...].astype(f32) for ref in rims]
-        put(0, *pieces[:3])
-        put(rim + lines, *pieces[3:])
+        top, bottom = pieces[:3], pieces[3:]
+    low_line = max(first_line, rim) - rim
+    high_line = min(first_line + tall, rim + total) - rim
+    base = low_line + rim - first_line
+    cells = slice(low_line * columns, high_line * columns)
+    full_ref[base : base + high_line - low_line, lead : lead + columns] = (
+        grid_ref[cells].astype(f32).reshape(high_line - low_line, columns, width)
+    )
+    left = left_ref[...].astype(f32)
+    right = right_ref[...].astype(f32)
+
+    def put(at, value, col, pieces, high):
+        full_ref[at, col : col + high] = value[pieces : pieces + high]
+
+    for x in range(low_line, high_line):
+        at = x + rim - first_line
+        put(at, left, lead - rim, rim * x, rim)
+        put(at, right, lead + columns, rim * x, rim)
+    for start, group in ((0, top), (rim + total, bottom)):
+        for i in range(rim):
+            at = start + i - first_line
+            if 0 <= at < tall:
+                put(at, group[0], lead, columns * i, columns)
+                put(at, group[1], lead - rim, rim * i, rim)
+                put(at, group[2], lead + columns, rim * i, rim)
     for t in range(span * span):
         wide_ref[t] = jnp.broadcast_to(taps_ref[t // span, t % span : t % span + 1], (8, width))
     groups = columns // 8
@@ -382,18 +384,20 @@
     out_ref[...] = (centred * lax.rsqrt(spread + norm_eps)).astype(bf16)
 
 
-def mix_folded(shape, span, grid, left, right, a, *refs):
-    conv_kernel_body(shape, span, True, grid, left, right, (a,), *refs)
-
-
-def mix_open(shape, span, grid, left, right, a, b, c, d, e, g, *refs):
-    conv_kernel_body(shape, span, False, grid, left, right, (a, b, c, d, e, g), *refs)
-
-
-def feed_kernel(chunk, normed_ref, grid_ref, up_ref, down_ref, head_ref, out_ref):
-    for at in range(0, normed_ref.shape[0], chunk):
+def mix_folded(shape, span, start, grid, left, right, a, *refs):
+    conv_kernel_body(shape, span, start, True, grid, left, right, (a,), *refs)
+
+
+def mix_open(shape, span, start, grid, left, right, a, b, c, d, e, g, *refs):
+    conv_kernel_body(shape, span, start, False, grid, left, right, (a, b, c, d, e, g), *refs)
+
+
+def feed_kernel(chunk, upper_ref, lower_ref, grid_ref, up_ref, down_ref, head_ref, out_ref):
+    half = upper_ref.shape[0]
+    for at in range(0, 2 * half, chunk):
         rows = slice(at, at + chunk)
-        wide = mm(normed_ref[rows], up_ref[...])
+        source = upper_ref if at < half else lower_ref
+        wide = mm(source[at % half : at % half + chunk], up_ref[...])
         hidden = (0.5 * wide * (1.0 + lax.erf(wide * 0.7071067811865476))).astype(bf16)
         decoded = (grid_ref[rows].astype(f32) + mm(hidden, down_ref[...])).astype(bf16)
         out_ref[rows] = mm(decoded, head_ref[...])
@@ -467,16 +471,16 @@
     left_whole = (replicas,) + left_part if fast else left_part
     if fast:
         cots = [cotangent] + [flip(cotangent, "replica", k) for k in range(1, 4)]
-    grad_att, w_qkv_t = call(
+    grad_att, w_qk_t, w_val_t = call(
         prep_kernel,
         "prep",
-        [sds((width, rows), bf16), sds((3 * width, width), bf16)],
+        [sds((width, rows), bf16), sds((2 * width, width), bf16), sds((width, width), bf16)],
         [vmem()] * 3,
         flops=2 * rows * width * width,
         nbytes=10 * MIB,
         limit=10,
     )(cotangent, w_out, w_qkv)
-    arrived = tie(arrived, w_qkv_t)
+    arrived = tie(arrived, w_qk_t)
 
     normed, enc_in, places = call(
         functools.partial(norm_kernel, cap, padded),
@@ -491,24 +495,24 @@
     if fast:
         normed_y = flip(normed, "replica", 2)
         normed_c = flip(normed, "replica", 1)
-    units, lengths, values = call(
+    units, lengths = call(
         project_kernel,
         "project",
-        [sds((2 * width, rows), f32), sds((2 * heads, rows), f32), sds((width, rows), bf16)],
+        [sds((2 * width, rows), f32), sds((2 * heads, rows), f32)],
         [vmem()] * 2,
         flops=2 * rows * width * width * 4,
         nbytes=8 * MIB,
         limit=10,
         cost=2000000000,
-    )(normed, w_qkv_t)
+    )(normed, w_qk_t)
 
     outbound, *lefts = call(
         functools.partial(encode_kernel, split),
         "encode",
         [sds((slots, dec_width), bf16)] + [sds(left_part, bf16)] * pieces,
-        [vmem(), smem()] + [vmem()] * 8,
+        [vmem(), smem()] + [vmem()] * 9,
         scratch=[
-            pltpu.VMEM((heads, rows, rows), bf16),
+            pltpu.VMEM((width, rows), bf16),
             pltpu.VMEM((width, rows), bf16),
             pltpu.VMEM(left_whole, bf16),
         ],
@@ -517,8 +521,8 @@
         limit=14,
         cost=8000000000,
     )(
-        window_id.reshape(1, rows), head_scale, places, enc_in, units, lengths, values, grad_att,
-        w_out, w_dec_in,
+        window_id.reshape(1, rows), head_scale, places, enc_in, normed, units, lengths, grad_att,
+        w_val_t, w_out, w_dec_in,
     )
     if fast:
         cots, lefts, normed_y, normed_c = lax.optimization_barrier(
@@ -622,20 +626,29 @@
         left, right_halo, rims = tie((left_halo, right_halo, rims), kept)
     else:
         left = left_halo
-    normed_cells = call(
-        functools.partial(mix_folded if folded else mix_open, (eta_cells, phi_cells), span),
-        "mix",
-        sds((tile_len, dec_width), bf16),
-        [vmem()] * (4 + len(rims)),
-        scratch=[
-            pltpu.VMEM((eta_cells + 2 * rim, phi_cells + 16, dec_width), f32),
-            pltpu.VMEM((span * span, 8, dec_width), f32),
-            pltpu.VMEM((tile_len, dec_width), f32),
-        ],
-        flops=200 * 2 * span * span * tile_len * dec_width,
-        nbytes=3 * MIB,
-        limit=16,
-    )(dec_grid, left, right_halo, *rims, conv_kernel)
+    rows_half = eta_cells // 2
+
+    def mix(start, *rest):
+        return call(
+            functools.partial(
+                mix_folded if folded else mix_open, (eta_cells, phi_cells), span, start
+            ),
+            "mix%d" % start,
+            sds((tile_len // 2, dec_width), bf16),
+            [vmem()] * (4 + len(rims)),
+            scratch=[
+                pltpu.VMEM((rows_half + 2 * rim, phi_cells + 16, dec_width), f32),
+                pltpu.VMEM((span * span, 8, dec_width), f32),
+                pltpu.VMEM((tile_len // 2, dec_width), f32),
+            ],
+            flops=200 * span * span * tile_len * dec_width,
+            nbytes=3 * MIB,
+            limit=12,
+        )(*rest)
+
+    upper = mix(0, dec_grid, left, right_halo, *rims, conv_kernel)
+    if not fast:
+        lower = mix(rows_half, dec_grid, left, right_halo, *rims, conv_kernel)
     if fast:
         summed = []
         for c in range(2):
@@ -647,18 +660,21 @@
                 flops=half * part_rows * chunk,
                 nbytes=2 * MIB,
                 limit=4,
-            )(kept[c], tie(sent[c], normed_cells))
+            )(kept[c], tie(sent[c], upper if c == 0 else lower))
             summed.append([own] + [turn(outs[k], "phi", k + 1) for k in range(phi_count - 1)])
-            normed_cells = tie(normed_cells, own)
+            if c == 0:
+                lower = mix(rows_half, tie(dec_grid, summed[0][1]), left, right_halo, *rims, conv_kernel)
+            else:
+                upper = tie(upper, own)
     reconstruction = call(
         functools.partial(feed_kernel, 256),
         "feed",
         sds((tile_len, w_head.shape[1]), f32),
-        [vmem()] * 5,
+        [vmem()] * 6,
         flops=2 * tile_len * dec_width * (2 * w_up.shape[1] + w_head.shape[1]),
         nbytes=4 * MIB,
         limit=12,
-    )(normed_cells, dec_grid, w_up, w_down, w_head).reshape(1, eta_cells, phi_cells, -1)
+    )(upper, lower, dec_grid, w_up, w_down, w_head).reshape(1, eta_cells, phi_cells, -1)
     if fast:
         summed = tie(summed, reconstruction)
         mine = call(

time: 105 us -> 107 us (1.019)
  starting transfers between devices: 31.8 us -> 34.5 us
  waiting for transfers between devices: 27.3 us -> 25.8 us
    ppermute x11, starting transfers between devices: 14 us -> 15.5 us  [turn(): lax.ppermute(value, axis, [(i, (i + k) % count) for i in range(count)])]
    ppermute x12, starting transfers between devices: 6.55 us -> 7.69 us  [flip(): lax.ppermute(value, axis, [(i, i ^ bit) for i in range(lax.axis_size(axis...]
    ppermute x12, waiting for transfers between devices: 6.01 us -> 4.86 us  [flip(): lax.ppermute(value, axis, [(i, i ^ bit) for i in range(lax.axis_size(axis...]
    unnamed x48 -> x52, local copies, waits for them, and re-layouts: 10.8 us -> 11.2 us
    pallas_call x2 -> x3, Pallas kernels: 8.43 us -> 8.43 us  [the longest x2 7.44 us: mix(): call(functools.partial(mix_folded if folded else mix_open, (eta_cells, ph...]
  transfers between devices with their start and end apart: 25 -> 25, of which waited for: 7 -> 8; matrix products, arithmetic and copies ran while one was open for 1% -> 1% of each run, Pallas kernels for 28% -> 28%
where the time goes in v9:
time: 107 us
  starting transfers between devices  34.5 us (32%)
  Pallas kernels  32.9 us (31%)
  waiting for transfers between devices  25.8 us (24%)
  local copies, waits for them, and re-layouts  12.4 us (12%)
    ppermute x11, starting transfers between devices, turn(): lax.ppermute(value, axis, [(i, (i + k) % count) for i in range(count)])  15.5 us
    unnamed x52, local copies, waits for them, and re-layouts  11.2 us
    pallas_call x1, Pallas kernels, body(): call(functools.partial(encode_kernel, split), 'encode', [sds((slots, dec_...  9.19 us
    ppermute x11, waiting for transfers between devices, turn(): lax.ppermute(value, axis, [(i, (i + k) % count) for i in range(count)])  7.74 us
    ppermute x12, starting transfers between devices, flip(): lax.ppermute(value, axis, [(i, i ^ bit) for i in range(lax.axis_size(axis...  7.69 us
    pallas_call x2, Pallas kernels, mix(): call(functools.partial(mix_folded if folded else mix_open, (eta_cells, ph...  7.44 us
    all_to_all x1, starting transfers between devices, body(): lax.all_to_all(outgoing.reshape(group, padded, width), ('eta', 'phi'), sp...  7.25 us
    all_to_all x1, waiting for transfers between devices, body(): lax.all_to_all(outbound.reshape(group, padded, dec_width), ('eta', 'phi')...  6.61 us
  transfers between devices with their start and end apart: 25, of which 8 were waited for; matrix products, arithmetic and copies ran while one was open for 1% of the time, Pallas kernels for 28%

profile of v9, /device:TPU:0, one launch (start us, length us, event | category | flops | bytes accessed | tf_op | source)
XLA Modules:
  0.0 106.6 jit_solution(4459804013348595306)
XLA Ops:
  0.6 1.4 %copy-done.2 = bf16[1,32,32,768]{3,2,1,0:T(8,128)(2,1)S(1)} copy-done((bf16[1,32,32,768]{3,2,1,0:T(8,128)(2,1)S(1)}, bf16[1,32,32,768]{3,2,1,0:T(8,128)(2,1)}, u32[]{:S(2)}) %copy-start.2) | copy-done | bytes 1572888
  2.1 0.7 copy-done.9
  2.8 1.7 %pick.1 = bf16[320,768]{1,0:T(8,128)(2,1)} custom-call(s32[8,35]{1,0:T(8,128)S(1)} %bitcast.18, bf16[1024,768]{1,0:T(8,128)(2,1)S(1)} %bitcast.16), custom_call_target="tpu_custom_call" | custom-call | flops 1000 | bytes 1003 | tf_op jit(solution)/shard_map/pick/pallas_call | solution.py:452
  4.5 7.3 %all-to-all-start = ((bf16[8,40,768]{2,1,0:T(8,128)(2,1)}), bf16[8,40,768]{2,1,0:T(8,128)(2,1)S(1)}, u32[]{:S(2)}, u32[]{:S(2)}) async-start(bf16[8,40,768]{2,1,0:T(8,128)(2,1)} %bitcast.5), calls=%async_computation | async-start | bytes 983040 | tf_op jit(solution)/shard_map/all_to_all | solution.py:462
  11.8 1.6 %collective-permute-start.1 = (bf16[256,768]{1,0:T(8,128)(2,1)S(1)}, bf16[256,768]{1,0:T(8,128)(2,1)S(1)}, u32[]{:S(2)}, u32[]{:S(2)}) collective-permute-start(bf16[256,768]{1,0:T(8,128)(2,1)S(1)} %bitcast.11), channel_id=1, source_target_pairs={{0,2},{1,3},{2,0},{3,1},{4,6},{5,7},{6,4},{7,5},{8,10},{9,11},{10,... | collective-permute-start | bytes 1179656 | tf_op jit(solution)/shard_map/ppermute | solution.py:407
  13.7 2.0 %copy-done.1 = bf16[768,2304]{1,0:T(8,128)(2,1)S(1)} copy-done((bf16[768,2304]{1,0:T(8,128)(2,1)S(1)}, bf16[768,2304]{1,0:T(8,128)(2,1)}, u32[]{:S(2)}) %copy-start.1) | copy-done | bytes 3538968
  15.7 1.0 prep.1
  16.7 1.4 %copy-done.13 = bf16[1536,768]{1,0:T(8,128)(2,1)} copy-done((bf16[1536,768]{1,0:T(8,128)(2,1)}, bf16[1536,768]{1,0:T(8,128)(2,1)S(1)}, u32[]{:S(2)}) %copy-start.13) | copy-done | bytes 2359320
  18.1 1.0 copy-done.15
  19.1 0.8 copy-done.21
  19.8 6.6 %all-to-all-done = bf16[8,40,768]{2,1,0:T(8,128)(2,1)S(1)} async-done(((bf16[8,40,768]{2,1,0:T(8,128)(2,1)}), bf16[8,40,768]{2,1,0:T(8,128)(2,1)S(1)}, u32[]{:S(2)}, u32[]{:S(2)}) %all-to-all-start) | async-done | bytes 491552 | tf_op jit(solution)/shard_map/all_to_all | solution.py:462
  26.4 0.7 norm.1
  27.2 1.7 %copy-done.14 = bf16[1536,768]{1,0:T(8,128)(2,1)S(1)} copy-done((bf16[1536,768]{1,0:T(8,128)(2,1)S(1)}, bf16[1536,768]{1,0:T(8,128)(2,1)}, u32[]{:S(2)}) %copy-start.14) | copy-done | bytes 2359320
  28.9 0.9 project.1
  29.7 1.6 %collective-permute-start.3 = (bf16[256,768]{1,0:T(8,128)(2,1)S(1)}, bf16[256,768]{1,0:T(8,128)(2,1)S(1)}, u32[]{:S(2)}, u32[]{:S(2)}) collective-permute-start(bf16[256,768]{1,0:T(8,128)(2,1)S(1)} %get-tuple-element.129.normed_ref.refs_4_), channel_id=1, source_target_pairs={{0,2},{1,3},{2,0},{3,1},{4,6},{5,7},{6,4},{7,5},{8,10},{9,11},{10,... | collective-permute-start | bytes 1179656 | tf_op jit(solution)/shard_map/ppermute | solution.py:407
  31.4 9.2 %encode.1 = (bf16[320,384]{1,0:T(8,128)(2,1)}, bf16[768,256]{1,0:T(8,128)(2,1)S(1)}, bf16[768,256]{1,0:T(8,128)(2,1)S(1)}, bf16[768,256]{1,0:T(8,128)(2,1)S(1)}, bf16[768,256]{1,0:T(8,128)(2,1)S(1)}) custom-call(s32[1,256]{1,0:T(1,128)S(1)} %bitcast.21, f32[12]{0:T(128)S(1)} %copy-done.25, f32[1,256]{1,0:T(1,128)S(1)} %get-tuple-element.84.place_ref, ...), custom_call_target="tpu_custom_call" | custom-call | flops 8000000000 | bytes 26667666 | tf_op jit(solution)/shard_map/encode/pallas_call | solution.py:509
  40.6 0.7 copy-done.18
  41.3 0.7 copy-done.19
  42.1 4.0 %all-to-all-start.1 = ((bf16[8,40,384]{2,1,0:T(8,128)(2,1)}), bf16[8,40,384]{2,1,0:T(8,128)(2,1)}, u32[]{:S(2)}, u32[]{:S(2)}) async-start(bf16[8,40,384]{2,1,0:T(8,128)(2,1)} %bitcast.7), calls=%async_computation.1 | async-start | bytes 491520 | tf_op jit(solution)/shard_map/all_to_all | solution.py:531
  46.8 0.8 collective-permute-start.6
  47.6 1.0 collective-permute-start.7
  48.6 1.3 %reshape.44.mask_ref = bf16[1,384]{1,0:T(2,128)(2,1)} reshape(bf16[384]{0:T(512)(128)(2,1)} %param.24) | data formatting | bytes 1536 | tf_op jit(solution)/shard_map/reshape | solution.py:572
  49.9 6.6 %all-to-all-done.1 = bf16[8,40,384]{2,1,0:T(8,128)(2,1)} async-done(((bf16[8,40,384]{2,1,0:T(8,128)(2,1)}), bf16[8,40,384]{2,1,0:T(8,128)(2,1)}, u32[]{:S(2)}, u32[]{:S(2)}) %all-to-all-start.1) | async-done | bytes 245792 | tf_op jit(solution)/shard_map/all_to_all | solution.py:531
  56.5 0.7 copy-done.12
  57.2 2.4 %fill.1 = (bf16[1024,384]{1,0:T(8,128)(2,1)S(1)}, bf16[96,384]{1,0:T(8,128)(2,1)S(1)}, bf16[96,384]{1,0:T(8,128)(2,1)S(1)}, bf16[96,384]{1,0:T(8,128)(2,1)S(1)}) custom-call(s32[8,35]{1,0:T(8,128)S(1)} %bitcast.19, f32[2,1408]{1,0:T(2,128)S(1)} %copy-done.11, bf16[1,384]{1,0:T(2,128)(2,1)S(1)} %copy-done.12, bf16[320,384]{1,0:T(8,128)(2,1)} %bitcast.8.got_ref), custom_call_target="tpu_custom_call" | custom-call | flops 1000 | bytes 1003 | tf_op jit(solution)/shard_map/fill/pallas_call | solution.py:562
  59.6 2.0 %collective-permute-start.9 = (bf16[96,384]{1,0:T(8,128)(2,1)S(1)}, bf16[96,384]{1,0:T(8,128)(2,1)S(1)}, u32[]{:S(2)}, u32[]{:S(2)}) collective-permute-start(bf16[96,384]{1,0:T(8,128)(2,1)S(1)} %get-tuple-element.107), channel_id=1, source_target_pairs={{0,4},{4,8},{8,12},{12,0},{1,5},{5,9},{9,13},{13,1},{2,6},{6,10},{... | collective-permute-start | bytes 221192 | tf_op jit(solution)/shard_map/ppermute | solution.py:412
  61.7 3.1 %collective-permute-done.10.right_ref.right = bf16[96,384]{1,0:T(8,128)(2,1)S(1)} collective-permute-done((bf16[96,384]{1,0:T(8,128)(2,1)S(1)}, bf16[96,384]{1,0:T(8,128)(2,1)S(1)}, u32[]{:S(2)}, u32[]{:S(2)}) %collective-permute-start.10) | collective-permute-done | bytes 73760 | tf_op jit(solution)/shard_map/ppermute | solution.py:412
  64.8 1.1 %collective-permute-done.9.left_ref.left = bf16[96,384]{1,0:T(8,128)(2,1)S(1)} collective-permute-done((bf16[96,384]{1,0:T(8,128)(2,1)S(1)}, bf16[96,384]{1,0:T(8,128)(2,1)S(1)}, u32[]{:S(2)}, u32[]{:S(2)}) %collective-permute-start.9) | collective-permute-done | bytes 73760 | tf_op jit(solution)/shard_map/ppermute | solution.py:412
  65.9 0.7 collective-permute-start.12
  66.6 2.5 %terms0.1 = (f32[4,96,384]{2,1,0:T(8,128)S(1)}, bf16[4,96,384]{2,1,0:T(8,128)(2,1)S(1)}) custom-call(bf16[768,256]{1,0:T(8,128)(2,1)S(1)} %get-tuple-element.125.refs_0_, bf16[768,256]{1,0:T(8,128)(2,1)S(1)} %collective-permute-done.5.refs_1_, bf16[768,256]{1,0:T(8,128)(2,1)} %collective-permute-done.6.refs_2_, ...), custom_call_target="tpu_custom_call" | custom-call | flops 1000 | bytes 1003 | tf_op jit(solution)/shard_map/terms0/pallas_call | solution.py:613
  69.1 1.4 %collective-permute-start.11 = (bf16[4,96,384]{2,1,0:T(8,128)(2,1)S(1)}, bf16[4,96,384]{2,1,0:T(8,128)(2,1)S(1)}, u32[]{:S(2)}, u32[]{:S(2)}) collective-permute-start(bf16[4,96,384]{2,1,0:T(8,128)(2,1)S(1)} %get-tuple-element.123), channel_id=1, source_target_pairs={{0,16},{16,0},{1,17},{17,1},{2,18},{18,2},{3,19},{19,3},{4,20},{20... | collective-permute-start | bytes 884744 | tf_op jit(solution)/shard_map/ppermute | solution.py:412
  70.6 2.3 %terms1.1 = (f32[4,96,384]{2,1,0:T(8,128)S(1)}, bf16[4,96,384]{2,1,0:T(8,128)(2,1)S(1)}) custom-call(bf16[768,256]{1,0:T(8,128)(2,1)S(1)} %get-tuple-element.125.refs_0_, bf16[768,256]{1,0:T(8,128)(2,1)S(1)} %collective-permute-done.5.refs_1_, bf16[768,256]{1,0:T(8,128)(2,1)} %collective-permute-done.6.refs_2_, ...), custom_call_target="tpu_custom_call" | custom-call | flops 1000 | bytes 1003 | tf_op jit(solution)/shard_map/terms1/pallas_call | solution.py:613
  72.9 0.7 collective-permute-start.16
  73.6 3.7 %mix0.1.upper_ref = bf16[512,384]{1,0:T(8,128)(2,1)S(1)} custom-call(bf16[1024,384]{1,0:T(8,128)(2,1)S(1)} %get-tuple-element.147.grid.grid_ref, bf16[96,384]{1,0:T(8,128)(2,1)S(1)} %collective-permute-done.9.left_ref.left, bf16[96,384]{1,0:T(8,128)(2,1)S(1)} %collective-permute-done.10.right_ref.right, bf16[128,384]{1,0:T(8,128)(2,1)S(1)} %collective-permute-done.12.a, ...), custom_call_target="tpu_custom_call" | custom-call | flops 1000 | bytes 1003 | tf_op jit(solution)/shard_map/mix0/pallas_call | solution.py:632
  77.4 1.7 %collective-permute-done.11.got_ref = bf16[4,96,384]{2,1,0:T(8,128)(2,1)S(1)} collective-permute-done((bf16[4,96,384]{2,1,0:T(8,128)(2,1)S(1)}, bf16[4,96,384]{2,1,0:T(8,128)(2,1)S(1)}, u32[]{:S(2)}, u32[]{:S(2)}) %collective-permute-start.11) | collective-permute-done | bytes 294944 | tf_op jit(solution)/shard_map/ppermute | solution.py:412
  79.1 1.3 %collective-permute-start.13 = (bf16[96,384]{1,0:T(8,128)(2,1)S(1)}, bf16[96,384]{1,0:T(8,128)(2,1)S(1)}, u32[]{:S(2)}, u32[]{:S(2)}) collective-permute-start(bf16[96,384]{1,0:T(8,128)(2,1)S(1)} %get-tuple-element.143), channel_id=1, source_target_pairs={{0,4},{4,8},{8,12},{12,0},{1,5},{5,9},{9,13},{13,1},{2,6},{6,10},{... | collective-permute-start | bytes 221192 | tf_op jit(solution)/shard_map/ppermute | solution.py:412
  80.4 2.5 %collective-permute-start.14 = (bf16[96,384]{1,0:T(8,128)(2,1)S(1)}, bf16[96,384]{1,0:T(8,128)(2,1)S(1)}, u32[]{:S(2)}, u32[]{:S(2)}) collective-permute-start(bf16[96,384]{1,0:T(8,128)(2,1)S(1)} %get-tuple-element.144), channel_id=1, source_target_pairs={{0,8},{4,12},{8,0},{12,4},{1,9},{5,13},{9,1},{13,5},{2,10},{6,14},... | collective-permute-start | bytes 221192 | tf_op jit(solution)/shard_map/ppermute | solution.py:412
  82.9 1.4 %collective-permute-start.15 = (bf16[96,384]{1,0:T(8,128)(2,1)S(1)}, bf16[96,384]{1,0:T(8,128)(2,1)S(1)}, u32[]{:S(2)}, u32[]{:S(2)}) collective-permute-start(bf16[96,384]{1,0:T(8,128)(2,1)S(1)} %get-tuple-element.145), channel_id=1, source_target_pairs={{0,12},{4,0},{8,4},{12,8},{1,13},{5,1},{9,5},{13,9},{2,14},{6,2},{... | collective-permute-start | bytes 221192 | tf_op jit(solution)/shard_map/ppermute | solution.py:412
  84.2 1.9 %collective-permute-done.13.refs_1_ = bf16[96,384]{1,0:T(8,128)(2,1)S(1)} collective-permute-done((bf16[96,384]{1,0:T(8,128)(2,1)S(1)}, bf16[96,384]{1,0:T(8,128)(2,1)S(1)}, u32[]{:S(2)}, u32[]{:S(2)}) %collective-permute-start.13) | collective-permute-done | bytes 73760 | tf_op jit(solution)/shard_map/ppermute | solution.py:412
  86.1 3.7 %mix16.1.lower_ref = bf16[512,384]{1,0:T(8,128)(2,1)S(1)} custom-call(bf16[1024,384]{1,0:T(8,128)(2,1)S(1)} %get-tuple-element.147.grid.grid_ref, bf16[96,384]{1,0:T(8,128)(2,1)S(1)} %collective-permute-done.9.left_ref.left, bf16[96,384]{1,0:T(8,128)(2,1)S(1)} %collective-permute-done.10.right_ref.right, bf16[128,384]{1,0:T(8,128)(2,1)S(1)} %collective-permute-done.12.a, ...), custom_call_target="tpu_custom_call" | custom-call | flops 1000 | bytes 1003 | tf_op jit(solution)/shard_map/mix16/pallas_call | solution.py:632
  89.9 0.6 collective-permute-start.17
  90.5 2.0 %collective-permute-start.18 = (bf16[96,384]{1,0:T(8,128)(2,1)S(1)}, bf16[96,384]{1,0:T(8,128)(2,1)S(1)}, u32[]{:S(2)}, u32[]{:S(2)}) collective-permute-start(bf16[96,384]{1,0:T(8,128)(2,1)S(1)} %get-tuple-element.151), channel_id=1, source_target_pairs={{0,8},{4,12},{8,0},{12,4},{1,9},{5,13},{9,1},{13,5},{2,10},{6,14},... | collective-permute-start | bytes 221192 | tf_op jit(solution)/shard_map/ppermute | solution.py:412
  92.5 2.8 %collective-permute-start.19 = (bf16[96,384]{1,0:T(8,128)(2,1)S(1)}, bf16[96,384]{1,0:T(8,128)(2,1)S(1)}, u32[]{:S(2)}, u32[]{:S(2)}) collective-permute-start(bf16[96,384]{1,0:T(8,128)(2,1)S(1)} %get-tuple-element.152), channel_id=1, source_target_pairs={{0,12},{4,0},{8,4},{12,8},{1,13},{5,1},{9,5},{13,9},{2,14},{6,2},{... | collective-permute-start | bytes 221192 | tf_op jit(solution)/shard_map/ppermute | solution.py:412
  95.3 3.4 %feed.1 = f32[1024,128]{1,0:T(8,128)} custom-call(bf16[512,384]{1,0:T(8,128)(2,1)S(1)} %mix0.1.upper_ref, bf16[512,384]{1,0:T(8,128)(2,1)S(1)} %mix16.1.lower_ref, bf16[1024,384]{1,0:T(8,128)(2,1)S(1)} %get-tuple-element.147.grid.grid_ref, bf16[384,768]{1,0:T(8,128)(2,1)S(1)} %copy-done.5, bf16[768,384]{1,0:T(8,128)(2,1)S(1)} %copy-done.6, ...), custom_call_target="tpu_custom_call" | custom-call | flops 1000 | bytes 1003 | tf_op jit(solution)/shard_map/feed/pallas_call | solution.py:669
  98.8 1.7 %collective-permute-start.21 = (bf16[96,768]{1,0:T(8,128)(2,1)S(1)}, bf16[96,768]{1,0:T(8,128)(2,1)S(1)}, u32[]{:S(2)}, u32[]{:S(2)}) collective-permute-start(bf16[96,768]{1,0:T(8,128)(2,1)S(1)} %close.1.own_ref), channel_id=1, source_target_pairs={{0,2},{1,3},{2,0},{3,1},{4,6},{5,7},{6,4},{7,5},{8,10},{9,11},{10,... | collective-permute-start | bytes 442376 | tf_op jit(solution)/shard_map/ppermute | solution.py:407
  100.6 3.5 %collective-permute-done.21.two_ref = bf16[96,768]{1,0:T(8,128)(2,1)S(1)} collective-permute-done((bf16[96,768]{1,0:T(8,128)(2,1)S(1)}, bf16[96,768]{1,0:T(8,128)(2,1)S(1)}, u32[]{:S(2)}, u32[]{:S(2)}) %collective-permute-start.21) | collective-permute-done | bytes 147488 | tf_op jit(solution)/shard_map/ppermute | solution.py:407
  104.0 1.4 %collective-permute-done.22.three_ref = bf16[96,768]{1,0:T(8,128)(2,1)S(1)} collective-permute-done((bf16[96,768]{1,0:T(8,128)(2,1)S(1)}, bf16[96,768]{1,0:T(8,128)(2,1)S(1)}, u32[]{:S(2)}, u32[]{:S(2)}) %collective-permute-start.22) | collective-permute-done | bytes 147488 | tf_op jit(solution)/shard_map/ppermute | solution.py:407
  105.4 1.2 %spread.1 = f32[384,768]{1,0:T(8,128)} custom-call(bf16[96,768]{1,0:T(8,128)(2,1)S(1)} %close.1.own_ref, bf16[96,768]{1,0:T(8,128)(2,1)S(1)} %collective-permute-done.20.one_ref, bf16[96,768]{1,0:T(8,128)(2,1)S(1)} %collective-permute-done.21.two_ref, bf16[96,768]{1,0:T(8,128)(2,1)S(1)} %collective-permute-done.22.three_ref), custom_call_target="tpu_custom_call" | custom-call | flops 1000 | bytes 1003 | tf_op jit(solution)/shard_map/spread/pallas_call | solution.py:690
  (71 shorter events, 1.4 us)
Async XLA Ops:
  0.6 11.1 %copy-start = (bf16[1,1,1,256,768]{4,3,2,1,0:T(8,128)(2,1)S(1)}, bf16[1,1,1,256,768]{4,3,2,1,0:T(8,128)(2,1)}, u32[]{:S(2)}) copy-start(bf16[1,1,1,256,768]{4,3,2,1,0:T(8,128)(2,1)} %param.19) | copy-start | bytes 1179652
  0.6 1.5 %copy-start.2 = (bf16[1,32,32,768]{3,2,1,0:T(8,128)(2,1)S(1)}, bf16[1,32,32,768]{3,2,1,0:T(8,128)(2,1)}, u32[]{:S(2)}) copy-start(bf16[1,32,32,768]{3,2,1,0:T(8,128)(2,1)} %param.15) | copy-start | bytes 4718596
  2.8 10.9 %copy-start.3 = (bf16[768,768]{1,0:T(8,128)(2,1)S(1)}, bf16[768,768]{1,0:T(8,128)(2,1)}, u32[]{:S(2)}) copy-start(bf16[768,768]{1,0:T(8,128)(2,1)} %wout_ref.3) | copy-start | bytes 3538948
  4.5 21.9 %all-to-all-start = ((bf16[8,40,768]{2,1,0:T(8,128)(2,1)}), bf16[8,40,768]{2,1,0:T(8,128)(2,1)S(1)}, u32[]{:S(2)}, u32[]{:S(2)}) async-start(bf16[8,40,768]{2,1,0:T(8,128)(2,1)} %bitcast.5), calls=%async_computation | async-start | bytes 983040 | tf_op jit(solution)/shard_map/all_to_all | solution.py:462
  11.7 14.7 %copy-start.23 = (s32[1,1,1,256]{3,2,1,0:T(1,128)S(1)}, s32[1,1,1,256]{3,2,1,0:T(1,128)}, u32[]{:S(2)}) copy-start(s32[1,1,1,256]{3,2,1,0:T(1,128)} %param.17) | copy-start | bytes 3076
  11.7 34.4 %collective-permute-start = (bf16[256,768]{1,0:T(8,128)(2,1)S(1)}, bf16[256,768]{1,0:T(8,128)(2,1)S(1)}, u32[]{:S(2)}, u32[]{:S(2)}) collective-permute-start(bf16[256,768]{1,0:T(8,128)(2,1)S(1)} %bitcast.10), channel_id=1, source_target_pairs={{0,1},{1,0},{2,3},{3,2},{4,5},{5,4},{6,7},{7,6},{8,9},{9,8},{10,11... | collective-permute-start | bytes 1179656 | tf_op jit(solution)/shard_map/ppermute | solution.py:407
  11.8 34.3 %collective-permute-start.1 = (bf16[256,768]{1,0:T(8,128)(2,1)S(1)}, bf16[256,768]{1,0:T(8,128)(2,1)S(1)}, u32[]{:S(2)}, u32[]{:S(2)}) collective-permute-start(bf16[256,768]{1,0:T(8,128)(2,1)S(1)} %bitcast.11), channel_id=1, source_target_pairs={{0,2},{1,3},{2,0},{3,1},{4,6},{5,7},{6,4},{7,5},{8,10},{9,11},{10,... | collective-permute-start | bytes 1179656 | tf_op jit(solution)/shard_map/ppermute | solution.py:407
  13.4 32.7 %collective-permute-start.2 = (bf16[256,768]{1,0:T(8,128)(2,1)S(1)}, bf16[256,768]{1,0:T(8,128)(2,1)S(1)}, u32[]{:S(2)}, u32[]{:S(2)}) collective-permute-start(bf16[256,768]{1,0:T(8,128)(2,1)S(1)} %bitcast.12), channel_id=1, source_target_pairs={{0,3},{1,2},{2,1},{3,0},{4,7},{5,6},{6,5},{7,4},{8,11},{9,10},{10,... | collective-permute-start | bytes 1179656 | tf_op jit(solution)/shard_map/ppermute | solution.py:407
  13.7 2.0 %copy-start.1 = (bf16[768,2304]{1,0:T(8,128)(2,1)S(1)}, bf16[768,2304]{1,0:T(8,128)(2,1)}, u32[]{:S(2)}) copy-start(bf16[768,2304]{1,0:T(8,128)(2,1)} %wqkv_ref.1) | copy-start | bytes 10616836
  16.7 1.4 %copy-start.13 = (bf16[1536,768]{1,0:T(8,128)(2,1)}, bf16[1536,768]{1,0:T(8,128)(2,1)S(1)}, u32[]{:S(2)}) copy-start(bf16[1536,768]{1,0:T(8,128)(2,1)S(1)} %get-tuple-element.82.wqkv_t_ref) | copy-start | bytes 7077892
  18.1 1.0 copy-start.15
  19.1 0.8 copy-start.21
  27.2 1.7 %copy-start.14 = (bf16[1536,768]{1,0:T(8,128)(2,1)S(1)}, bf16[1536,768]{1,0:T(8,128)(2,1)}, u32[]{:S(2)}) copy-start(bf16[1536,768]{1,0:T(8,128)(2,1)} %copy-done.13) | copy-start | bytes 7077892
  28.8 2.5 %copy-start.4 = (bf16[768,768]{1,0:T(8,128)(2,1)S(1)}, bf16[768,768]{1,0:T(8,128)(2,1)}, u32[]{:S(2)}) copy-start(bf16[768,768]{1,0:T(8,128)(2,1)} %wout_ref.3) | copy-start | bytes 3538948
  28.8 2.5 %copy-start.16 = (bf16[768,768]{1,0:T(8,128)(2,1)S(1)}, bf16[768,768]{1,0:T(8,128)(2,1)}, u32[]{:S(2)}) copy-start(bf16[768,768]{1,0:T(8,128)(2,1)} %copy-done.15) | copy-start | bytes 3538948
  28.8 2.5 %copy-start.17 = (bf16[768,384]{1,0:T(8,128)(2,1)S(1)}, bf16[768,384]{1,0:T(8,128)(2,1)}, u32[]{:S(2)}) copy-start(bf16[768,384]{1,0:T(8,128)(2,1)} %wdec_ref.1) | copy-start | bytes 1769476
  28.8 2.5 %copy-start.22 = (bf16[768,256]{1,0:T(8,128)(2,1)S(1)}, bf16[768,256]{1,0:T(8,128)(2,1)}, u32[]{:S(2)}) copy-start(bf16[768,256]{1,0:T(8,128)(2,1)} %copy-done.21) | copy-start | bytes 1179652
  28.8 2.5 %copy-start.24 = (s32[1,1,1,256]{3,2,1,0:T(1,128)S(1)}, s32[1,1,1,256]{3,2,1,0:T(1,128)}, u32[]{:S(2)}) copy-start(s32[1,1,1,256]{3,2,1,0:T(1,128)} %param.18) | copy-start | bytes 3076
  28.8 2.5 %copy-start.25 = (f32[12]{0:T(128)S(1)}, f32[12]{0:T(128)}, u32[]{:S(2)}) copy-start(f32[12]{0:T(128)} %scale_ref.1) | copy-start | bytes 148
  29.7 16.4 %collective-permute-start.3 = (bf16[256,768]{1,0:T(8,128)(2,1)S(1)}, bf16[256,768]{1,0:T(8,128)(2,1)S(1)}, u32[]{:S(2)}, u32[]{:S(2)}) collective-permute-start(bf16[256,768]{1,0:T(8,128)(2,1)S(1)} %get-tuple-element.129.normed_ref.refs_4_), channel_id=1, source_target_pairs={{0,2},{1,3},{2,0},{3,1},{4,6},{5,7},{6,4},{7,5},{8,10},{9,11},{10,... | collective-permute-start | bytes 1179656 | tf_op jit(solution)/shard_map/ppermute | solution.py:407
  31.3 14.8 %collective-permute-start.4 = (bf16[256,768]{1,0:T(8,128)(2,1)S(1)}, bf16[256,768]{1,0:T(8,128)(2,1)S(1)}, u32[]{:S(2)}, u32[]{:S(2)}) collective-permute-start(bf16[256,768]{1,0:T(8,128)(2,1)S(1)} %get-tuple-element.129.normed_ref.refs_4_), channel_id=1, source_target_pairs={{0,1},{1,0},{2,3},{3,2},{4,5},{5,4},{6,7},{7,6},{8,9},{9,8},{10,11... | collective-permute-start | bytes 1179656 | tf_op jit(solution)/shard_map/ppermute | solution.py:407
  31.4 25.1 %copy-start.10 = (s32[1,1,1,8,35]{4,3,2,1,0:T(8,128)S(1)}, s32[1,1,1,8,35]{4,3,2,1,0:T(8,128)}, u32[]{:S(2)}) copy-start(s32[1,1,1,8,35]{4,3,2,1,0:T(8,128)} %param.16) | copy-start | bytes 3364
  31.4 25.1 %copy-start.11 = (f32[2,1408]{1,0:T(2,128)S(1)}, f32[2,1408]{1,0:T(2,128)}, u32[]{:S(2)}) copy-start(f32[2,1408]{1,0:T(2,128)} %constant.2.clone.ids_ref) | copy-start | bytes 33796
  40.6 0.7 copy-start.18
  41.3 4.8 %copy-start.20 = (bf16[768,256]{1,0:T(8,128)(2,1)}, bf16[768,256]{1,0:T(8,128)(2,1)S(1)}, u32[]{:S(2)}) copy-start(bf16[768,256]{1,0:T(8,128)(2,1)S(1)} %get-tuple-element.96) | copy-start | bytes 1179652
  42.1 14.4 %all-to-all-start.1 = ((bf16[8,40,384]{2,1,0:T(8,128)(2,1)}), bf16[8,40,384]{2,1,0:T(8,128)(2,1)}, u32[]{:S(2)}, u32[]{:S(2)}) async-start(bf16[8,40,384]{2,1,0:T(8,128)(2,1)} %bitcast.7), calls=%async_computation.1 | async-start | bytes 491520 | tf_op jit(solution)/shard_map/all_to_all | solution.py:531
  46.2 10.3 %collective-permute-start.5 = (bf16[768,256]{1,0:T(8,128)(2,1)}, bf16[768,256]{1,0:T(8,128)(2,1)S(1)}, u32[]{:S(2)}, u32[]{:S(2)}) collective-permute-start(bf16[768,256]{1,0:T(8,128)(2,1)} %copy-done.20), channel_id=1, source_target_pairs={{0,1},{1,0},{2,3},{3,2},{4,5},{5,4},{6,7},{7,6},{8,9},{9,8},{10,11... | collective-permute-start | bytes 1179656 | tf_op jit(solution)/shard_map/ppermute | solution.py:407
  46.7 9.8 %collective-permute-start.8 = (bf16[256,768]{1,0:T(8,128)(2,1)S(1)}, bf16[256,768]{1,0:T(8,128)(2,1)}, u32[]{:S(2)}, u32[]{:S(2)}) collective-permute-start(bf16[256,768]{1,0:T(8,128)(2,1)S(1)} %collective-permute-done.3.refs_6_), channel_id=1, source_target_pairs={{0,1},{1,0},{2,3},{3,2},{4,5},{5,4},{6,7},{7,6},{8,9},{9,8},{10,11... | collective-permute-start | bytes 1179656 | tf_op jit(solution)/shard_map/ppermute | solution.py:407
  46.8 19.8 %collective-permute-start.6 = (bf16[768,256]{1,0:T(8,128)(2,1)}, bf16[768,256]{1,0:T(8,128)(2,1)}, u32[]{:S(2)}, u32[]{:S(2)}) collective-permute-start(bf16[768,256]{1,0:T(8,128)(2,1)} %copy-done.19), channel_id=1, source_target_pairs={{0,2},{1,3},{2,0},{3,1},{4,6},{5,7},{6,4},{7,5},{8,10},{9,11},{10,... | collective-permute-start | bytes 1179656 | tf_op jit(solution)/shard_map/ppermute | solution.py:407
  47.6 19.0 %collective-permute-start.7 = (bf16[768,256]{1,0:T(8,128)(2,1)}, bf16[768,256]{1,0:T(8,128)(2,1)}, u32[]{:S(2)}, u32[]{:S(2)}) collective-permute-start(bf16[768,256]{1,0:T(8,128)(2,1)} %copy-done.18), channel_id=1, source_target_pairs={{0,3},{1,2},{2,1},{3,0},{4,7},{5,6},{6,5},{7,4},{8,11},{9,10},{10,... | collective-permute-start | bytes 1179656 | tf_op jit(solution)/shard_map/ppermute | solution.py:407
  59.6 5.2 %collective-permute-start.10 = (bf16[96,384]{1,0:T(8,128)(2,1)S(1)}, bf16[96,384]{1,0:T(8,128)(2,1)S(1)}, u32[]{:S(2)}, u32[]{:S(2)}) collective-permute-start(bf16[96,384]{1,0:T(8,128)(2,1)S(1)} %get-tuple-element.108), channel_id=1, source_target_pairs={{0,12},{4,0},{8,4},{12,8},{1,13},{5,1},{9,5},{13,9},{2,14},{6,2},{... | collective-permute-start | bytes 221192 | tf_op jit(solution)/shard_map/ppermute | solution.py:412
  59.6 6.2 %collective-permute-start.9 = (bf16[96,384]{1,0:T(8,128)(2,1)S(1)}, bf16[96,384]{1,0:T(8,128)(2,1)S(1)}, u32[]{:S(2)}, u32[]{:S(2)}) collective-permute-start(bf16[96,384]{1,0:T(8,128)(2,1)S(1)} %get-tuple-element.107), channel_id=1, source_target_pairs={{0,4},{4,8},{8,12},{12,0},{1,5},{5,9},{9,13},{13,1},{2,6},{6,10},{... | collective-permute-start | bytes 221192 | tf_op jit(solution)/shard_map/ppermute | solution.py:412
  65.9 4.7 %collective-permute-start.12 = (bf16[128,384]{1,0:T(8,128)(2,1)S(1)}, bf16[128,384]{1,0:T(8,128)(2,1)S(1)}, u32[]{:S(2)}, u32[]{:S(2)}) collective-permute-start(bf16[128,384]{1,0:T(8,128)(2,1)S(1)} %rim.1), channel_id=1, source_target_pairs={{0,16},{16,0},{1,17},{17,1},{2,18},{18,2},{3,19},{19,3},{4,20},{20... | collective-permute-start | bytes 294920 | tf_op jit(solution)/shard_map/ppermute | solution.py:412
  69.1 4.5 %copy-start.7 = (f32[7,7,384]{2,1,0:T(8,128)S(1)}, f32[7,7,384]{2,1,0:T(8,128)}, u32[]{:S(2)}) copy-start(f32[7,7,384]{2,1,0:T(8,128)} %refs_0_.3) | copy-start | bytes 225796
  69.1 9.9 %collective-permute-start.11 = (bf16[4,96,384]{2,1,0:T(8,128)(2,1)S(1)}, bf16[4,96,384]{2,1,0:T(8,128)(2,1)S(1)}, u32[]{:S(2)}, u32[]{:S(2)}) collective-permute-start(bf16[4,96,384]{2,1,0:T(8,128)(2,1)S(1)} %get-tuple-element.123), channel_id=1, source_target_pairs={{0,16},{16,0},{1,17},{17,1},{2,18},{18,2},{3,19},{19,3},{4,20},{20... | collective-permute-start | bytes 884744 | tf_op jit(solution)/shard_map/ppermute | solution.py:412
  72.9 16.9 %collective-permute-start.16 = (bf16[4,96,384]{2,1,0:T(8,128)(2,1)S(1)}, bf16[4,96,384]{2,1,0:T(8,128)(2,1)S(1)}, u32[]{:S(2)}, u32[]{:S(2)}) collective-permute-start(bf16[4,96,384]{2,1,0:T(8,128)(2,1)S(1)} %get-tuple-element.146), channel_id=1, source_target_pairs={{0,16},{16,0},{1,17},{17,1},{2,18},{18,2},{3,19},{19,3},{4,20},{20... | collective-permute-start | bytes 884744 | tf_op jit(solution)/shard_map/ppermute | solution.py:412
  77.3 18.0 %copy-start.5 = (bf16[384,768]{1,0:T(8,128)(2,1)S(1)}, bf16[384,768]{1,0:T(8,128)(2,1)}, u32[]{:S(2)}) copy-start(bf16[384,768]{1,0:T(8,128)(2,1)} %up_ref.1) | copy-start | bytes 1769476
  77.4 18.0 %copy-start.6 = (bf16[768,384]{1,0:T(8,128)(2,1)S(1)}, bf16[768,384]{1,0:T(8,128)(2,1)}, u32[]{:S(2)}) copy-start(bf16[768,384]{1,0:T(8,128)(2,1)} %down_ref.1) | copy-start | bytes 1769476
  77.4 18.0 %copy-start.8 = (bf16[384,128]{1,0:T(8,128)(2,1)S(1)}, bf16[384,128]{1,0:T(8,128)(2,1)}, u32[]{:S(2)}) copy-start(bf16[384,128]{1,0:T(8,128)(2,1)} %head_ref.1) | copy-start | bytes 294916
  79.1 7.0 %collective-permute-start.13 = (bf16[96,384]{1,0:T(8,128)(2,1)S(1)}, bf16[96,384]{1,0:T(8,128)(2,1)S(1)}, u32[]{:S(2)}, u32[]{:S(2)}) collective-permute-start(bf16[96,384]{1,0:T(8,128)(2,1)S(1)} %get-tuple-element.143), channel_id=1, source_target_pairs={{0,4},{4,8},{8,12},{12,0},{1,5},{5,9},{9,13},{13,1},{2,6},{6,10},{... | collective-permute-start | bytes 221192 | tf_op jit(solution)/shard_map/ppermute | solution.py:412
  80.4 18.3 %collective-permute-start.14 = (bf16[96,384]{1,0:T(8,128)(2,1)S(1)}, bf16[96,384]{1,0:T(8,128)(2,1)S(1)}, u32[]{:S(2)}, u32[]{:S(2)}) collective-permute-start(bf16[96,384]{1,0:T(8,128)(2,1)S(1)} %get-tuple-element.144), channel_id=1, source_target_pairs={{0,8},{4,12},{8,0},{12,4},{1,9},{5,13},{9,1},{13,5},{2,10},{6,14},... | collective-permute-start | bytes 221192 | tf_op jit(solution)/shard_map/ppermute | solution.py:412
  82.9 15.9 %collective-permute-start.15 = (bf16[96,384]{1,0:T(8,128)(2,1)S(1)}, bf16[96,384]{1,0:T(8,128)(2,1)S(1)}, u32[]{:S(2)}, u32[]{:S(2)}) collective-permute-start(bf16[96,384]{1,0:T(8,128)(2,1)S(1)} %get-tuple-element.145), channel_id=1, source_target_pairs={{0,12},{4,0},{8,4},{12,8},{1,13},{5,1},{9,5},{13,9},{2,14},{6,2},{... | collective-permute-start | bytes 221192 | tf_op jit(solution)/shard_map/ppermute | solution.py:412
  89.9 8.8 %collective-permute-start.17 = (bf16[96,384]{1,0:T(8,128)(2,1)S(1)}, bf16[96,384]{1,0:T(8,128)(2,1)S(1)}, u32[]{:S(2)}, u32[]{:S(2)}) collective-permute-start(bf16[96,384]{1,0:T(8,128)(2,1)S(1)} %get-tuple-element.150), channel_id=1, source_target_pairs={{0,4},{4,8},{8,12},{12,0},{1,5},{5,9},{9,13},{13,1},{2,6},{6,10},{... | collective-permute-start | bytes 221192 | tf_op jit(solution)/shard_map/ppermute | solution.py:412
  90.5 8.2 %collective-permute-start.18 = (bf16[96,384]{1,0:T(8,128)(2,1)S(1)}, bf16[96,384]{1,0:T(8,128)(2,1)S(1)}, u32[]{:S(2)}, u32[]{:S(2)}) collective-permute-start(bf16[96,384]{1,0:T(8,128)(2,1)S(1)} %get-tuple-element.151), channel_id=1, source_target_pairs={{0,8},{4,12},{8,0},{12,4},{1,9},{5,13},{9,1},{13,5},{2,10},{6,14},... | collective-permute-start | bytes 221192 | tf_op jit(solution)/shard_map/ppermute | solution.py:412
  92.5 6.2 %collective-permute-start.19 = (bf16[96,384]{1,0:T(8,128)(2,1)S(1)}, bf16[96,384]{1,0:T(8,128)(2,1)S(1)}, u32[]{:S(2)}, u32[]{:S(2)}) collective-permute-start(bf16[96,384]{1,0:T(8,128)(2,1)S(1)} %get-tuple-element.152), channel_id=1, source_target_pairs={{0,12},{4,0},{8,4},{12,8},{1,13},{5,1},{9,5},{13,9},{2,14},{6,2},{... | collective-permute-start | bytes 221192 | tf_op jit(solution)/shard_map/ppermute | solution.py:412
  98.8 5.2 %collective-permute-start.21 = (bf16[96,768]{1,0:T(8,128)(2,1)S(1)}, bf16[96,768]{1,0:T(8,128)(2,1)S(1)}, u32[]{:S(2)}, u32[]{:S(2)}) collective-permute-start(bf16[96,768]{1,0:T(8,128)(2,1)S(1)} %close.1.own_ref), channel_id=1, source_target_pairs={{0,2},{1,3},{2,0},{3,1},{4,6},{5,7},{6,4},{7,5},{8,10},{9,11},{10,... | collective-permute-start | bytes 442376 | tf_op jit(solution)/shard_map/ppermute | solution.py:407
  100.6 3.5 %collective-permute-start.20 = (bf16[96,768]{1,0:T(8,128)(2,1)S(1)}, bf16[96,768]{1,0:T(8,128)(2,1)S(1)}, u32[]{:S(2)}, u32[]{:S(2)}) collective-permute-start(bf16[96,768]{1,0:T(8,128)(2,1)S(1)} %close.1.own_ref), channel_id=1, source_target_pairs={{0,1},{1,0},{2,3},{3,2},{4,5},{5,4},{6,7},{7,6},{8,9},{9,8},{10,11... | collective-permute-start | bytes 442376 | tf_op jit(solution)/shard_map/ppermute | solution.py:407
  104.0 1.4 %collective-permute-start.22 = (bf16[96,768]{1,0:T(8,128)(2,1)S(1)}, bf16[96,768]{1,0:T(8,128)(2,1)S(1)}, u32[]{:S(2)}, u32[]{:S(2)}) collective-permute-start(bf16[96,768]{1,0:T(8,128)(2,1)S(1)} %collective-permute-done.21.two_ref), channel_id=1, source_target_pairs={{0,1},{1,0},{2,3},{3,2},{4,5},{5,4},{6,7},{7,6},{8,9},{9,8},{10,11... | collective-permute-start | bytes 442376 | tf_op jit(solution)/shard_map/ppermute | solution.py:407
  (3 other events, 2.1 us)

commit v10 on v8

--- a/solution.py
+++ b/solution.py
@@ -65,11 +65,25 @@
     return jnp.concatenate([turned[0:padded, d : d + 1] for d in range(group)], axis=0)
 
 
-def pick_kernel(padded, pos_ref, tok_ref, out_ref, wide_ref):
+def plane_index():
+    return lax.axis_index("eta") * lax.axis_size("phi") + lax.axis_index("phi")
+
+
+def pick_kernel(padded, pos_ref, tok_ref, *refs):
+    out_refs, (wide_ref, all_ref) = refs[:-2], refs[-2:]
     slots = slot_column(pos_ref, wide_ref, padded)
     cells = lax.broadcasted_iota(jnp.int32, (slots.shape[0], tok_ref.shape[0]), 1).astype(f32)
     chosen = (slots == cells).astype(f32).astype(bf16)
-    out_ref[...] = mm(chosen, tok_ref[...]).astype(bf16)
+    taken = mm(chosen, tok_ref[...])
+    if len(out_refs) == 1:
+        out_refs[0][...] = taken.astype(bf16)
+        return
+    group = len(out_refs)
+    for d in range(group):
+        all_ref[d] = taken[d * padded : (d + 1) * padded].astype(bf16)
+    me = plane_index()
+    for k, ref in enumerate(out_refs):
+        ref[...] = all_ref[lax.rem(me + k, group)]
 
 
 def prep_kernel(cot_ref, wout_ref, wqkv_ref, ga_ref, wqkv_t_ref):
@@ -77,25 +91,35 @@
     wqkv_t_ref[...] = jnp.transpose(wqkv_ref[...])
 
 
-def norm_kernel(cap, padded, src_ref, arr_ref, normed_ref, enc_ref, place_ref):
-    rows = normed_ref.shape[0]
-    slots = arr_ref.shape[0]
+def norm_kernel(cap, padded, src_ref, cot_ref, *refs):
+    arr_refs, (both_ref, enc_ref, place_ref) = refs[:-3], refs[-3:]
+    rows = enc_ref.shape[0]
+    group = len(arr_refs)
     src = src_ref[...].astype(f32)
-    slot_row = src + (padded - cap) * jnp.floor((src + 0.5) * (1.0 / cap))
+    tile = jnp.floor((src + 0.5) * (1.0 / cap))
+    slot_row = src + (padded - cap) * tile
     place_ref[...] = slot_row
+    if group > 1:
+        arrived = jnp.concatenate([ref[...].astype(f32) for ref in arr_refs], axis=0).astype(bf16)
+        turn_by = plane_index().astype(f32) - tile
+        turn_by = jnp.where(turn_by < 0.0, turn_by + group, turn_by)
+        slot_row = slot_row + padded * (turn_by - tile)
+    else:
+        arrived = arr_refs[0][...]
     slot_col = column_of(slot_row)
-    lanes = lax.broadcasted_iota(jnp.int32, (rows, slots), 1).astype(f32)
+    lanes = lax.broadcasted_iota(jnp.int32, (rows, arrived.shape[0]), 1).astype(f32)
     pick = (slot_col == lanes).astype(f32).astype(bf16)
-    enc_in = mm(pick, arr_ref[...])
+    enc_in = mm(pick, arrived)
     enc_ref[...] = enc_in.astype(bf16)
     centred = enc_in - jnp.mean(enc_in, axis=-1, keepdims=True)
     spread = jnp.mean(centred * centred, axis=-1, keepdims=True)
-    normed_ref[...] = (centred * lax.rsqrt(spread + norm_eps)).astype(bf16)
+    both_ref[0:rows] = (centred * lax.rsqrt(spread + norm_eps)).astype(bf16)
+    both_ref[rows : 2 * rows] = cot_ref[...]
 
 
 def project_kernel(normed_ref, wqkv_t_ref, u_ref, len_ref, v_ref):
-    normed = normed_ref[...]
-    width = normed.shape[1]
+    width = v_ref.shape[0]
+    normed = normed_ref[0 : v_ref.shape[1]]
     heads = len_ref.shape[0] // 2
     size = width // heads
     for t in range(2):
@@ -183,15 +207,18 @@
 
 
 def term_kernel(c, *refs):
-    lefts, normed, cots = refs[0:4], refs[4:8], refs[8:12]
-    keep_ref, send_ref = refs[12:]
+    lefts, rights = refs[0:4], refs[4:8]
+    keep_ref, send_ref = refs[8:]
     half, part, chunk = keep_ref.shape
     cut = slice(c * chunk, (c + 1) * chunk)
 
-    def block(lo, hi, right, cols):
+    count = lefts[0].shape[1]
+    normed, cots = slice(0, count), slice(count, 2 * count)
+
+    def block(lo, hi, which, cols):
         acc = None
-        for left, e in zip(lefts, right):
-            step = mm(left[lo:hi], e[:, cols])
+        for left, e in zip(lefts, rights):
+            step = mm(left[lo:hi], e[which, cols])
             acc = step if acc is None else acc + step
         return acc
 
@@ -445,28 +472,35 @@
     )
 
     positions = send_pos.reshape(group, cap)
+    turned = 1 < group <= 8
     outgoing = call(
         functools.partial(pick_kernel, padded),
         "pick",
-        sds((slots, width), bf16),
+        [sds((padded, width), bf16)] * group if turned else [sds((slots, width), bf16)],
         [vmem(), vmem()],
-        scratch=[pltpu.VMEM((group, 128), f32)],
+        scratch=[pltpu.VMEM((group, 128), f32), pltpu.VMEM((group, padded, width), bf16)],
         flops=2 * slots * tile_len * width,
         nbytes=3 * MIB,
         limit=8,
     )(positions, tokens.reshape(tile_len, width))
-    arrived = lax.all_to_all(
-        outgoing.reshape(group, padded, width), ("eta", "phi"), split_axis=0, concat_axis=0,
-        tiled=True,
-    ).reshape(slots, width)
+    if turned:
+        arrived = [outgoing[0]]
+        for k in range(1, group):
+            pairs = [(i, (i + k) % group) for i in range(group)]
+            arrived.append(lax.ppermute(outgoing[k], ("eta", "phi"), pairs))
+    else:
+        arrived = [
+            lax.all_to_all(
+                outgoing[0].reshape(group, padded, width), ("eta", "phi"), split_axis=0,
+                concat_axis=0, tiled=True,
+            ).reshape(slots, width)
+        ]
 
     cotangent = enc_cot.reshape(rows, width)
     split = (shard_rows, part_rows, 3 * width) if fast else None
     pieces = replicas if fast else 1
     left_part = (out_rows // pieces, rows)
     left_whole = (replicas,) + left_part if fast else left_part
-    if fast:
-        cots = [cotangent] + [flip(cotangent, "replica", k) for k in range(1, 4)]
     grad_att, w_qkv_t = call(
         prep_kernel,
         "prep",
@@ -478,19 +512,19 @@
     )(cotangent, w_out, w_qkv)
     arrived = tie(arrived, w_qkv_t)
 
-    normed, enc_in, places = call(
+    both, enc_in, places = call(
         functools.partial(norm_kernel, cap, padded),
         "norm",
-        [sds((rows, width), bf16), sds((rows, width), bf16), sds((1, rows), f32)],
-        [vmem()] * 2,
+        [sds((2 * rows, width), bf16), sds((rows, width), bf16), sds((1, rows), f32)],
+        [vmem()] * (2 + len(arrived)),
         flops=2 * rows * width * slots,
         nbytes=2 * MIB,
         limit=8,
         cost=600000000,
-    )(enc_src.reshape(1, rows), arrived)
+    )(enc_src.reshape(1, rows), cotangent, *arrived)
     if fast:
-        normed_y = flip(normed, "replica", 2)
-        normed_c = flip(normed, "replica", 1)
+        both_y = flip(both, "replica", 2)
+        both_c = flip(both, "replica", 1)
     units, lengths, values = call(
         project_kernel,
         "project",
@@ -500,7 +534,7 @@
         nbytes=8 * MIB,
         limit=10,
         cost=2000000000,
-    )(normed, w_qkv_t)
+    )(both, w_qkv_t)
 
     outbound, *lefts = call(
         functools.partial(encode_kernel, split),
@@ -521,19 +555,17 @@
         w_out, w_dec_in,
     )
     if fast:
-        cots, lefts, normed_y, normed_c = lax.optimization_barrier(
-            (cots, lefts, normed_y, normed_c)
-        )
+        lefts, both_y, both_c = lax.optimization_barrier((lefts, both_y, both_c))
     returned = lax.all_to_all(
         outbound.reshape(group, padded, dec_width), ("eta", "phi"), split_axis=0, concat_axis=0,
         tiled=True,
     )
     if fast:
         lefts = [lefts[0]] + [flip(lefts[k], "replica", k) for k in range(1, 4)]
-        rights = [normed, normed_c, normed_y, flip(normed_y, "replica", 1)]
+        rights = [both, both_c, both_y, flip(both_y, "replica", 1)]
         returned = tie(returned, lefts[1], rights[3])
     else:
-        grad_total = summed_slow(lefts[0], normed, cotangent)
+        grad_total = summed_slow(lefts[0], both[:rows], cotangent)
 
     span = conv_kernel.shape[0]
     rim = span // 2
@@ -601,7 +633,7 @@
             flat(bottom), flat(low[far:]), flat(high[far:]),
         )
     if fast:
-        lefts, rights, cots = tie((lefts, rights, cots), rim_out)
+        lefts, rights = tie((lefts, rights), rim_out)
         chunk = width // 2
         half = group // 2
         kept, sent = [], []
@@ -610,13 +642,13 @@
                 functools.partial(term_kernel, c),
                 "terms%d" % c,
                 [sds((half, part_rows, chunk), f32), sds((half, part_rows, chunk), bf16)],
-                [vmem()] * 12,
+                [vmem()] * 8,
                 flops=2 * out_rows * chunk * rows,
                 nbytes=8 * MIB,
                 limit=10,
-            )(*lefts, *rights, *cots)
+            )(*lefts, *rights)
             if c == 0:
-                lefts, rights, cots = tie((lefts, rights, cots), rims)
+                lefts, rights = tie((lefts, rights), rims)
             kept.append(keep)
             sent.append(turn(send, "eta", 1))
         left, right_halo, rims = tie((left_halo, right_halo, rims), kept)

time: 105 us -> 106 us (level)
  starting transfers between devices: 31.8 us -> 40.4 us
  waiting for transfers between devices: 27.3 us -> 23.9 us
  local copies, waits for them, and re-layouts: 12.1 us -> 8.93 us
  Pallas kernels: 32.5 us -> 31.1 us
    ppermute x0 -> x7, starting transfers between devices: none -> 14.3 us  [body(): arrived.append(lax.ppermute(outgoing[k], ('eta', 'phi'), pairs))]
    all_to_all x1 -> x0, starting transfers between devices: 7.25 us -> none  [body(): lax.all_to_all(outgoing.reshape(group, padded, width), ('eta', 'phi'), sp...]
    all_to_all x1 -> x0, waiting for transfers between devices: 7.23 us -> none  [body(): lax.all_to_all(outgoing.reshape(group, padded, width), ('eta', 'phi'), sp...]
    ppermute x12 -> x9, waiting for transfers between devices: 6.01 us -> 11.3 us  [flip(): lax.ppermute(value, axis, [(i, i ^ bit) for i in range(lax.axis_size(axis...]
    unnamed x48 -> x40, local copies, waits for them, and re-layouts: 10.8 us -> 7.71 us
    ppermute x11, waiting for transfers between devices: 7.44 us -> 5.46 us  [turn(): lax.ppermute(value, axis, [(i, (i + k) % count) for i in range(count)])]
    ppermute x11, starting transfers between devices: 14 us -> 15.9 us  [turn(): lax.ppermute(value, axis, [(i, (i + k) % count) for i in range(count)])]
    ppermute x12 -> x9, starting transfers between devices: 6.55 us -> 5.09 us  [flip(): lax.ppermute(value, axis, [(i, i ^ bit) for i in range(lax.axis_size(axis...]
  transfers between devices with their start and end apart: 25 -> 28, of which waited for: 7 -> 7; matrix products, arithmetic and copies ran while one was open for 1% -> 1% of each run, Pallas kernels for 28% -> 27%
where the time goes in v10:
time: 106 us; the launch traced here: 105 us
  starting transfers between devices  40.4 us (38%)
  Pallas kernels  31.1 us (29%)
  waiting for transfers between devices  23.9 us (23%)
  local copies, waits for them, and re-layouts  8.93 us (8%)
    ppermute x11, starting transfers between devices, turn(): lax.ppermute(value, axis, [(i, (i + k) % count) for i in range(count)])  15.9 us
    ppermute x7, starting transfers between devices, body(): arrived.append(lax.ppermute(outgoing[k], ('eta', 'phi'), pairs))  14.3 us
    ppermute x9, waiting for transfers between devices, flip(): lax.ppermute(value, axis, [(i, i ^ bit) for i in range(lax.axis_size(axis...  11.3 us
    pallas_call x1, Pallas kernels, body(): call(functools.partial(encode_kernel, split), 'encode', [sds((slots, dec_...  7.9 us
    unnamed x40, local copies, waits for them, and re-layouts  7.71 us
    pallas_call x1, Pallas kernels, body(): call(functools.partial(mix_folded if folded else mix_open, (eta_cells, ph...  7.45 us
    all_to_all x1, waiting for transfers between devices, body(): lax.all_to_all(outbound.reshape(group, padded, dec_width), ('eta', 'phi')...  7.11 us
    ppermute x11, waiting for transfers between devices, turn(): lax.ppermute(value, axis, [(i, (i + k) % count) for i in range(count)])  5.46 us
  transfers between devices with their start and end apart: 28, of which 7 were waited for; matrix products, arithmetic and copies ran while one was open for 1% of the time, Pallas kernels for 27%

profile of v10, /device:TPU:0, one launch (start us, length us, event | category | flops | bytes accessed | tf_op | source)
XLA Modules:
  0.0 105.4 jit_solution(8499538387286088367)
XLA Ops:
  0.6 1.4 %copy-done.1 = bf16[1,32,32,768]{3,2,1,0:T(8,128)(2,1)S(1)} copy-done((bf16[1,32,32,768]{3,2,1,0:T(8,128)(2,1)S(1)}, bf16[1,32,32,768]{3,2,1,0:T(8,128)(2,1)}, u32[]{:S(2)}) %copy-start.1) | copy-done | bytes 1572888
  2.0 0.7 copy-done.9
  2.7 0.9 pick.1
  3.7 3.1 %collective-permute-start = (bf16[40,768]{1,0:T(8,128)(2,1)S(1)}, bf16[40,768]{1,0:T(8,128)(2,1)S(1)}, u32[]{:S(2)}, u32[]{:S(2)}) collective-permute-start(bf16[40,768]{1,0:T(8,128)(2,1)S(1)} %get-tuple-element.86), channel_id=1, source_target_pairs={{0,4},{4,8},{8,12},{12,16},{16,20},{20,24},{24,28},{28,0},{1,5},{5... | collective-permute-start | bytes 184328 | tf_op jit(solution)/shard_map/ppermute | solution.py:490
  6.7 2.6 %collective-permute-start.1 = (bf16[40,768]{1,0:T(8,128)(2,1)S(1)}, bf16[40,768]{1,0:T(8,128)(2,1)S(1)}, u32[]{:S(2)}, u32[]{:S(2)}) collective-permute-start(bf16[40,768]{1,0:T(8,128)(2,1)S(1)} %get-tuple-element.87), channel_id=1, source_target_pairs={{0,8},{4,12},{8,16},{12,20},{16,24},{20,28},{24,0},{28,4},{1,9},{5... | collective-permute-start | bytes 184328 | tf_op jit(solution)/shard_map/ppermute | solution.py:490
  9.3 2.3 %collective-permute-start.2 = (bf16[40,768]{1,0:T(8,128)(2,1)S(1)}, bf16[40,768]{1,0:T(8,128)(2,1)S(1)}, u32[]{:S(2)}, u32[]{:S(2)}) collective-permute-start(bf16[40,768]{1,0:T(8,128)(2,1)S(1)} %get-tuple-element.88), channel_id=1, source_target_pairs={{0,12},{4,16},{8,20},{12,24},{16,28},{20,0},{24,4},{28,8},{1,13},{... | collective-permute-start | bytes 184328 | tf_op jit(solution)/shard_map/ppermute | solution.py:490
  11.6 0.5 collective-permute-start.3
  12.1 1.6 %collective-permute-start.4 = (bf16[40,768]{1,0:T(8,128)(2,1)S(1)}, bf16[40,768]{1,0:T(8,128)(2,1)S(1)}, u32[]{:S(2)}, u32[]{:S(2)}) collective-permute-start(bf16[40,768]{1,0:T(8,128)(2,1)S(1)} %get-tuple-element.90), channel_id=1, source_target_pairs={{0,20},{4,24},{8,28},{12,0},{16,4},{20,8},{24,12},{28,16},{1,21},{... | collective-permute-start | bytes 184328 | tf_op jit(solution)/shard_map/ppermute | solution.py:490
  13.7 1.2 %collective-permute-start.5 = (bf16[40,768]{1,0:T(8,128)(2,1)S(1)}, bf16[40,768]{1,0:T(8,128)(2,1)S(1)}, u32[]{:S(2)}, u32[]{:S(2)}) collective-permute-start(bf16[40,768]{1,0:T(8,128)(2,1)S(1)} %get-tuple-element.91), channel_id=1, source_target_pairs={{0,24},{4,28},{8,0},{12,4},{16,8},{20,12},{24,16},{28,20},{1,25},{... | collective-permute-start | bytes 184328 | tf_op jit(solution)/shard_map/ppermute | solution.py:490
  15.0 3.0 %collective-permute-start.6 = (bf16[40,768]{1,0:T(8,128)(2,1)S(1)}, bf16[40,768]{1,0:T(8,128)(2,1)S(1)}, u32[]{:S(2)}, u32[]{:S(2)}) collective-permute-start(bf16[40,768]{1,0:T(8,128)(2,1)S(1)} %get-tuple-element.92), channel_id=1, source_target_pairs={{0,28},{4,0},{8,4},{12,8},{16,12},{20,16},{24,20},{28,24},{1,29},{... | collective-permute-start | bytes 184328 | tf_op jit(solution)/shard_map/ppermute | solution.py:490
  18.0 2.0 %copy-done = bf16[768,2304]{1,0:T(8,128)(2,1)S(1)} copy-done((bf16[768,2304]{1,0:T(8,128)(2,1)S(1)}, bf16[768,2304]{1,0:T(8,128)(2,1)}, u32[]{:S(2)}) %copy-start) | copy-done | bytes 3538968
  20.0 1.0 prep.1
  21.0 0.8 norm.1
  21.9 1.6 %collective-permute-start.7 = (bf16[512,768]{1,0:T(8,128)(2,1)S(1)}, bf16[512,768]{1,0:T(8,128)(2,1)S(1)}, u32[]{:S(2)}, u32[]{:S(2)}) collective-permute-start(bf16[512,768]{1,0:T(8,128)(2,1)S(1)} %get-tuple-element.139.normed_ref.refs_4_), channel_id=1, source_target_pairs={{0,2},{1,3},{2,0},{3,1},{4,6},{5,7},{6,4},{7,5},{8,10},{9,11},{10,... | collective-permute-start | bytes 2359304 | tf_op jit(solution)/shard_map/ppermute | solution.py:430
  23.5 1.1 %project.1 = (f32[1536,256]{1,0:T(8,128)S(1)}, f32[24,256]{1,0:T(8,128)S(1)}, bf16[768,256]{1,0:T(8,128)(2,1)S(1)}) custom-call(bf16[512,768]{1,0:T(8,128)(2,1)S(1)} %get-tuple-element.139.normed_ref.refs_4_, bf16[2304,768]{1,0:T(8,128)(2,1)S(1)} %get-tuple-element.93.wqkv_t_ref), custom_call_target="tpu_custom_call" | custom-call | flops 2000000000 | bytes 6667666 | tf_op jit(solution)/shard_map/project/pallas_call | solution.py:528
  24.7 7.9 %encode.1 = (bf16[320,384]{1,0:T(8,128)(2,1)S(1)}, bf16[768,256]{1,0:T(8,128)(2,1)S(1)}, bf16[768,256]{1,0:T(8,128)(2,1)S(1)}, bf16[768,256]{1,0:T(8,128)(2,1)S(1)}, bf16[768,256]{1,0:T(8,128)(2,1)S(1)}) custom-call(s32[1,256]{1,0:T(1,128)S(1)} %bitcast.15, f32[12]{0:T(128)S(1)} %copy-done.19, f32[1,256]{1,0:T(1,128)S(1)} %get-tuple-element.102.place_ref, ...), custom_call_target="tpu_custom_call" | custom-call | flops 8000000000 | bytes 26667666 | tf_op jit(solution)/shard_map/encode/pallas_call | solution.py:539
  32.6 0.7 copy-done.6
  33.3 0.8 copy-done.14
  34.0 0.7 copy-done.15
  34.8 0.7 copy-done.16
  35.5 6.3 %collective-permute-done.7.refs_6_ = bf16[512,768]{1,0:T(8,128)(2,1)S(1)} collective-permute-done((bf16[512,768]{1,0:T(8,128)(2,1)S(1)}, bf16[512,768]{1,0:T(8,128)(2,1)S(1)}, u32[]{:S(2)}, u32[]{:S(2)}) %collective-permute-start.7) | collective-permute-done | bytes 786464 | tf_op jit(solution)/shard_map/ppermute | solution.py:430
  41.9 5.1 %all-to-all-start = ((bf16[8,40,384]{2,1,0:T(8,128)(2,1)}), bf16[8,40,384]{2,1,0:T(8,128)(2,1)}, u32[]{:S(2)}, u32[]{:S(2)}) async-start(bf16[8,40,384]{2,1,0:T(8,128)(2,1)} %bitcast.11), calls=%async_computation | async-start | bytes 491520 | tf_op jit(solution)/shard_map/all_to_all | solution.py:559
  47.0 0.2 collective-permute-start.9
  47.2 1.5 %collective-permute-start.10 = (bf16[768,256]{1,0:T(8,128)(2,1)}, bf16[768,256]{1,0:T(8,128)(2,1)}, u32[]{:S(2)}, u32[]{:S(2)}) collective-permute-start(bf16[768,256]{1,0:T(8,128)(2,1)} %copy-done.15), channel_id=1, source_target_pairs={{0,2},{1,3},{2,0},{3,1},{4,6},{5,7},{6,4},{7,5},{8,10},{9,11},{10,... | collective-permute-start | bytes 1179656 | tf_op jit(solution)/shard_map/ppermute | solution.py:430
  48.9 1.2 %reshape.36.mask_ref = bf16[1,384]{1,0:T(2,128)(2,1)} reshape(bf16[384]{0:T(512)(128)(2,1)} %param.24) | data formatting | bytes 1536 | tf_op jit(solution)/shard_map/reshape | solution.py:600
  50.1 7.1 %all-to-all-done = bf16[8,40,384]{2,1,0:T(8,128)(2,1)} async-done(((bf16[8,40,384]{2,1,0:T(8,128)(2,1)}), bf16[8,40,384]{2,1,0:T(8,128)(2,1)}, u32[]{:S(2)}, u32[]{:S(2)}) %all-to-all-start) | async-done | bytes 245792 | tf_op jit(solution)/shard_map/all_to_all | solution.py:559
  57.2 0.6 copy-done.12
  57.8 2.4 %fill.1 = (bf16[1024,384]{1,0:T(8,128)(2,1)S(1)}, bf16[96,384]{1,0:T(8,128)(2,1)S(1)}, bf16[96,384]{1,0:T(8,128)(2,1)S(1)}, bf16[96,384]{1,0:T(8,128)(2,1)S(1)}) custom-call(s32[8,35]{1,0:T(8,128)S(1)} %bitcast.13, f32[2,1408]{1,0:T(2,128)S(1)} %copy-done.11, bf16[1,384]{1,0:T(2,128)(2,1)S(1)} %copy-done.12, bf16[320,384]{1,0:T(8,128)(2,1)} %bitcast.6.got_ref), custom_call_target="tpu_custom_call" | custom-call | flops 1000 | bytes 1003 | tf_op jit(solution)/shard_map/fill/pallas_call | solution.py:590
  60.3 3.8 %collective-permute-start.14 = (bf16[96,384]{1,0:T(8,128)(2,1)S(1)}, bf16[96,384]{1,0:T(8,128)(2,1)S(1)}, u32[]{:S(2)}, u32[]{:S(2)}) collective-permute-start(bf16[96,384]{1,0:T(8,128)(2,1)S(1)} %get-tuple-element.122), channel_id=1, source_target_pairs={{0,12},{4,0},{8,4},{12,8},{1,13},{5,1},{9,5},{13,9},{2,14},{6,2},{... | collective-permute-start | bytes 221192 | tf_op jit(solution)/shard_map/ppermute | solution.py:435
  64.1 2.3 %collective-permute-done.13.left_ref.left = bf16[96,384]{1,0:T(8,128)(2,1)S(1)} collective-permute-done((bf16[96,384]{1,0:T(8,128)(2,1)S(1)}, bf16[96,384]{1,0:T(8,128)(2,1)S(1)}, u32[]{:S(2)}, u32[]{:S(2)}) %collective-permute-start.13) | collective-permute-done | bytes 73760 | tf_op jit(solution)/shard_map/ppermute | solution.py:435
  66.7 0.6 collective-permute-start.16
  67.3 2.3 %terms0.1 = (f32[4,96,384]{2,1,0:T(8,128)S(1)}, bf16[4,96,384]{2,1,0:T(8,128)(2,1)S(1)}) custom-call(bf16[768,256]{1,0:T(8,128)(2,1)S(1)} %get-tuple-element.135.refs_0_, bf16[768,256]{1,0:T(8,128)(2,1)} %collective-permute-done.9.refs_1_, bf16[768,256]{1,0:T(8,128)(2,1)} %collective-permute-done.10.refs_2_, ...), custom_call_target="tpu_custom_call" | custom-call | flops 1000 | bytes 1003 | tf_op jit(solution)/shard_map/terms0/pallas_call | solution.py:641
  69.7 1.6 %collective-permute-start.15 = (bf16[4,96,384]{2,1,0:T(8,128)(2,1)S(1)}, bf16[4,96,384]{2,1,0:T(8,128)(2,1)S(1)}, u32[]{:S(2)}, u32[]{:S(2)}) collective-permute-start(bf16[4,96,384]{2,1,0:T(8,128)(2,1)S(1)} %get-tuple-element.133), channel_id=1, source_target_pairs={{0,16},{16,0},{1,17},{17,1},{2,18},{18,2},{3,19},{19,3},{4,20},{20... | collective-permute-start | bytes 884744 | tf_op jit(solution)/shard_map/ppermute | solution.py:435
  71.4 2.3 %terms1.1 = (f32[4,96,384]{2,1,0:T(8,128)S(1)}, bf16[4,96,384]{2,1,0:T(8,128)(2,1)S(1)}) custom-call(bf16[768,256]{1,0:T(8,128)(2,1)S(1)} %get-tuple-element.135.refs_0_, bf16[768,256]{1,0:T(8,128)(2,1)} %collective-permute-done.9.refs_1_, bf16[768,256]{1,0:T(8,128)(2,1)} %collective-permute-done.10.refs_2_, ...), custom_call_target="tpu_custom_call" | custom-call | flops 1000 | bytes 1003 | tf_op jit(solution)/shard_map/terms1/pallas_call | solution.py:641
  73.7 0.6 collective-permute-start.20
  74.3 7.5 %mix.1.normed_ref = bf16[1024,384]{1,0:T(8,128)(2,1)S(1)} custom-call(bf16[1024,384]{1,0:T(8,128)(2,1)S(1)} %get-tuple-element.134.grid.grid_ref, bf16[96,384]{1,0:T(8,128)(2,1)S(1)} %collective-permute-done.13.left_ref.left, bf16[96,384]{1,0:T(8,128)(2,1)S(1)} %collective-permute-done.14.right_ref.right, bf16[128,384]{1,0:T(8,128)(2,1)S(1)} %collective-permute-done.16.a, ...), custom_call_target="tpu_custom_call" | custom-call | flops 1000 | bytes 1003 | tf_op jit(solution)/shard_map/mix/pallas_call | solution.py:657
  81.9 1.5 %collective-permute-start.17 = (bf16[96,384]{1,0:T(8,128)(2,1)S(1)}, bf16[96,384]{1,0:T(8,128)(2,1)S(1)}, u32[]{:S(2)}, u32[]{:S(2)}) collective-permute-start(bf16[96,384]{1,0:T(8,128)(2,1)S(1)} %get-tuple-element.149), channel_id=1, source_target_pairs={{0,4},{4,8},{8,12},{12,0},{1,5},{5,9},{9,13},{13,1},{2,6},{6,10},{... | collective-permute-start | bytes 221192 | tf_op jit(solution)/shard_map/ppermute | solution.py:435
  83.3 3.0 %collective-permute-start.18 = (bf16[96,384]{1,0:T(8,128)(2,1)S(1)}, bf16[96,384]{1,0:T(8,128)(2,1)S(1)}, u32[]{:S(2)}, u32[]{:S(2)}) collective-permute-start(bf16[96,384]{1,0:T(8,128)(2,1)S(1)} %get-tuple-element.150), channel_id=1, source_target_pairs={{0,8},{4,12},{8,0},{12,4},{1,9},{5,13},{9,1},{13,5},{2,10},{6,14},... | collective-permute-start | bytes 221192 | tf_op jit(solution)/shard_map/ppermute | solution.py:435
  86.3 0.9 collective-permute-start.19
  87.2 1.2 %collective-permute-start.21 = (bf16[96,384]{1,0:T(8,128)(2,1)S(1)}, bf16[96,384]{1,0:T(8,128)(2,1)S(1)}, u32[]{:S(2)}, u32[]{:S(2)}) collective-permute-start(bf16[96,384]{1,0:T(8,128)(2,1)S(1)} %get-tuple-element.156), channel_id=1, source_target_pairs={{0,4},{4,8},{8,12},{12,0},{1,5},{5,9},{9,13},{13,1},{2,6},{6,10},{... | collective-permute-start | bytes 221192 | tf_op jit(solution)/shard_map/ppermute | solution.py:435
  88.4 0.8 collective-permute-start.22
  89.2 1.9 %collective-permute-start.23 = (bf16[96,384]{1,0:T(8,128)(2,1)S(1)}, bf16[96,384]{1,0:T(8,128)(2,1)S(1)}, u32[]{:S(2)}, u32[]{:S(2)}) collective-permute-start(bf16[96,384]{1,0:T(8,128)(2,1)S(1)} %get-tuple-element.158), channel_id=1, source_target_pairs={{0,12},{4,0},{8,4},{12,8},{1,13},{5,1},{9,5},{13,9},{2,14},{6,2},{... | collective-permute-start | bytes 221192 | tf_op jit(solution)/shard_map/ppermute | solution.py:435
  91.1 3.3 %feed.1 = f32[1024,128]{1,0:T(8,128)} custom-call(bf16[1024,384]{1,0:T(8,128)(2,1)S(1)} %mix.1.normed_ref, bf16[1024,384]{1,0:T(8,128)(2,1)S(1)} %get-tuple-element.134.grid.grid_ref, bf16[384,768]{1,0:T(8,128)(2,1)S(1)} %copy-done.3, bf16[768,384]{1,0:T(8,128)(2,1)S(1)} %copy-done.4, bf16[384,128]{1,0:T(8,128)(2,1)S(1)} %copy-done.7), custom_call_target="tpu_custom_call" | custom-call | flops 1000 | bytes 1003 | tf_op jit(solution)/shard_map/feed/pallas_call | solution.py:685
  94.5 3.1 %collective-permute-done.22.refs_6_ = bf16[96,384]{1,0:T(8,128)(2,1)S(1)} collective-permute-done((bf16[96,384]{1,0:T(8,128)(2,1)S(1)}, bf16[96,384]{1,0:T(8,128)(2,1)S(1)}, u32[]{:S(2)}, u32[]{:S(2)}) %collective-permute-start.22) | collective-permute-done | bytes 73760 | tf_op jit(solution)/shard_map/ppermute | solution.py:435
  97.6 1.6 %collective-permute-start.25 = (bf16[96,768]{1,0:T(8,128)(2,1)S(1)}, bf16[96,768]{1,0:T(8,128)(2,1)S(1)}, u32[]{:S(2)}, u32[]{:S(2)}) collective-permute-start(bf16[96,768]{1,0:T(8,128)(2,1)S(1)} %close.1.own_ref), channel_id=1, source_target_pairs={{0,2},{1,3},{2,0},{3,1},{4,6},{5,7},{6,4},{7,5},{8,10},{9,11},{10,... | collective-permute-start | bytes 442376 | tf_op jit(solution)/shard_map/ppermute | solution.py:430
  99.2 3.6 %collective-permute-done.25.two_ref = bf16[96,768]{1,0:T(8,128)(2,1)S(1)} collective-permute-done((bf16[96,768]{1,0:T(8,128)(2,1)S(1)}, bf16[96,768]{1,0:T(8,128)(2,1)S(1)}, u32[]{:S(2)}, u32[]{:S(2)}) %collective-permute-start.25) | collective-permute-done | bytes 147488 | tf_op jit(solution)/shard_map/ppermute | solution.py:430
  102.8 1.4 %collective-permute-done.26.three_ref = bf16[96,768]{1,0:T(8,128)(2,1)S(1)} collective-permute-done((bf16[96,768]{1,0:T(8,128)(2,1)S(1)}, bf16[96,768]{1,0:T(8,128)(2,1)S(1)}, u32[]{:S(2)}, u32[]{:S(2)}) %collective-permute-start.26) | collective-permute-done | bytes 147488 | tf_op jit(solution)/shard_map/ppermute | solution.py:430
  104.2 1.2 %spread.1 = f32[384,768]{1,0:T(8,128)} custom-call(bf16[96,768]{1,0:T(8,128)(2,1)S(1)} %close.1.own_ref, bf16[96,768]{1,0:T(8,128)(2,1)S(1)} %collective-permute-done.24.one_ref, bf16[96,768]{1,0:T(8,128)(2,1)S(1)} %collective-permute-done.25.two_ref, bf16[96,768]{1,0:T(8,128)(2,1)S(1)} %collective-permute-done.26.three_ref), custom_call_target="tpu_custom_call" | custom-call | flops 1000 | bytes 1003 | tf_op jit(solution)/shard_map/spread/pallas_call | solution.py:706
  (64 shorter events, 0.9 us)
Async XLA Ops:
  0.6 1.4 %copy-start.1 = (bf16[1,32,32,768]{3,2,1,0:T(8,128)(2,1)S(1)}, bf16[1,32,32,768]{3,2,1,0:T(8,128)(2,1)}, u32[]{:S(2)}) copy-start(bf16[1,32,32,768]{3,2,1,0:T(8,128)(2,1)} %param.15) | copy-start | bytes 4718596
  2.0 0.7 copy-start.9
  2.7 15.2 %copy-start.2 = (bf16[768,768]{1,0:T(8,128)(2,1)S(1)}, bf16[768,768]{1,0:T(8,128)(2,1)}, u32[]{:S(2)}) copy-start(bf16[768,768]{1,0:T(8,128)(2,1)} %wout_ref.3) | copy-start | bytes 3538948
  2.7 15.2 %copy-start.5 = (bf16[1,1,1,256,768]{4,3,2,1,0:T(8,128)(2,1)S(1)}, bf16[1,1,1,256,768]{4,3,2,1,0:T(8,128)(2,1)}, u32[]{:S(2)}) copy-start(bf16[1,1,1,256,768]{4,3,2,1,0:T(8,128)(2,1)} %param.19) | copy-start | bytes 1179652
  3.7 10.1 %collective-permute-start = (bf16[40,768]{1,0:T(8,128)(2,1)S(1)}, bf16[40,768]{1,0:T(8,128)(2,1)S(1)}, u32[]{:S(2)}, u32[]{:S(2)}) collective-permute-start(bf16[40,768]{1,0:T(8,128)(2,1)S(1)} %get-tuple-element.86), channel_id=1, source_target_pairs={{0,4},{4,8},{8,12},{12,16},{16,20},{20,24},{24,28},{28,0},{1,5},{5... | collective-permute-start | bytes 184328 | tf_op jit(solution)/shard_map/ppermute | solution.py:490
  6.7 8.2 %collective-permute-start.1 = (bf16[40,768]{1,0:T(8,128)(2,1)S(1)}, bf16[40,768]{1,0:T(8,128)(2,1)S(1)}, u32[]{:S(2)}, u32[]{:S(2)}) collective-permute-start(bf16[40,768]{1,0:T(8,128)(2,1)S(1)} %get-tuple-element.87), channel_id=1, source_target_pairs={{0,8},{4,12},{8,16},{12,20},{16,24},{20,28},{24,0},{28,4},{1,9},{5... | collective-permute-start | bytes 184328 | tf_op jit(solution)/shard_map/ppermute | solution.py:490
  9.3 11.6 %collective-permute-start.2 = (bf16[40,768]{1,0:T(8,128)(2,1)S(1)}, bf16[40,768]{1,0:T(8,128)(2,1)S(1)}, u32[]{:S(2)}, u32[]{:S(2)}) collective-permute-start(bf16[40,768]{1,0:T(8,128)(2,1)S(1)} %get-tuple-element.88), channel_id=1, source_target_pairs={{0,12},{4,16},{8,20},{12,24},{16,28},{20,0},{24,4},{28,8},{1,13},{... | collective-permute-start | bytes 184328 | tf_op jit(solution)/shard_map/ppermute | solution.py:490
  11.6 9.4 %collective-permute-start.3 = (bf16[40,768]{1,0:T(8,128)(2,1)S(1)}, bf16[40,768]{1,0:T(8,128)(2,1)S(1)}, u32[]{:S(2)}, u32[]{:S(2)}) collective-permute-start(bf16[40,768]{1,0:T(8,128)(2,1)S(1)} %get-tuple-element.89), channel_id=1, source_target_pairs={{0,16},{4,20},{8,24},{12,28},{16,0},{20,4},{24,8},{28,12},{1,17},{... | collective-permute-start | bytes 184328 | tf_op jit(solution)/shard_map/ppermute | solution.py:490
  12.1 8.8 %collective-permute-start.4 = (bf16[40,768]{1,0:T(8,128)(2,1)S(1)}, bf16[40,768]{1,0:T(8,128)(2,1)S(1)}, u32[]{:S(2)}, u32[]{:S(2)}) collective-permute-start(bf16[40,768]{1,0:T(8,128)(2,1)S(1)} %get-tuple-element.90), channel_id=1, source_target_pairs={{0,20},{4,24},{8,28},{12,0},{16,4},{20,8},{24,12},{28,16},{1,21},{... | collective-permute-start | bytes 184328 | tf_op jit(solution)/shard_map/ppermute | solution.py:490
  13.7 7.2 %collective-permute-start.5 = (bf16[40,768]{1,0:T(8,128)(2,1)S(1)}, bf16[40,768]{1,0:T(8,128)(2,1)S(1)}, u32[]{:S(2)}, u32[]{:S(2)}) collective-permute-start(bf16[40,768]{1,0:T(8,128)(2,1)S(1)} %get-tuple-element.91), channel_id=1, source_target_pairs={{0,24},{4,28},{8,0},{12,4},{16,8},{20,12},{24,16},{28,20},{1,25},{... | collective-permute-start | bytes 184328 | tf_op jit(solution)/shard_map/ppermute | solution.py:490
  15.0 6.0 %collective-permute-start.6 = (bf16[40,768]{1,0:T(8,128)(2,1)S(1)}, bf16[40,768]{1,0:T(8,128)(2,1)S(1)}, u32[]{:S(2)}, u32[]{:S(2)}) collective-permute-start(bf16[40,768]{1,0:T(8,128)(2,1)S(1)} %get-tuple-element.92), channel_id=1, source_target_pairs={{0,28},{4,0},{8,4},{12,8},{16,12},{20,16},{24,20},{28,24},{1,29},{... | collective-permute-start | bytes 184328 | tf_op jit(solution)/shard_map/ppermute | solution.py:490
  18.0 2.0 %copy-start = (bf16[768,2304]{1,0:T(8,128)(2,1)S(1)}, bf16[768,2304]{1,0:T(8,128)(2,1)}, u32[]{:S(2)}) copy-start(bf16[768,2304]{1,0:T(8,128)(2,1)} %wqkv_ref.1) | copy-start | bytes 10616836
  20.0 1.0 copy-start.17
  21.8 2.8 %copy-start.13 = (bf16[768,384]{1,0:T(8,128)(2,1)S(1)}, bf16[768,384]{1,0:T(8,128)(2,1)}, u32[]{:S(2)}) copy-start(bf16[768,384]{1,0:T(8,128)(2,1)} %wdec_ref.1) | copy-start | bytes 1769476
  21.8 2.8 %copy-start.18 = (s32[1,1,1,256]{3,2,1,0:T(1,128)S(1)}, s32[1,1,1,256]{3,2,1,0:T(1,128)}, u32[]{:S(2)}) copy-start(s32[1,1,1,256]{3,2,1,0:T(1,128)} %param.18) | copy-start | bytes 3076
  21.8 2.8 %copy-start.19 = (f32[12]{0:T(128)S(1)}, f32[12]{0:T(128)}, u32[]{:S(2)}) copy-start(f32[12]{0:T(128)} %scale_ref.1) | copy-start | bytes 148
  21.8 13.7 %collective-permute-start.8 = (bf16[512,768]{1,0:T(8,128)(2,1)S(1)}, bf16[512,768]{1,0:T(8,128)(2,1)S(1)}, u32[]{:S(2)}, u32[]{:S(2)}) collective-permute-start(bf16[512,768]{1,0:T(8,128)(2,1)S(1)} %get-tuple-element.139.normed_ref.refs_4_), channel_id=1, source_target_pairs={{0,1},{1,0},{2,3},{3,2},{4,5},{5,4},{6,7},{7,6},{8,9},{9,8},{10,11... | collective-permute-start | bytes 2359304 | tf_op jit(solution)/shard_map/ppermute | solution.py:430
  21.9 20.0 %collective-permute-start.7 = (bf16[512,768]{1,0:T(8,128)(2,1)S(1)}, bf16[512,768]{1,0:T(8,128)(2,1)S(1)}, u32[]{:S(2)}, u32[]{:S(2)}) collective-permute-start(bf16[512,768]{1,0:T(8,128)(2,1)S(1)} %get-tuple-element.139.normed_ref.refs_4_), channel_id=1, source_target_pairs={{0,2},{1,3},{2,0},{3,1},{4,6},{5,7},{6,4},{7,5},{8,10},{9,11},{10,... | collective-permute-start | bytes 2359304 | tf_op jit(solution)/shard_map/ppermute | solution.py:430
  24.6 32.5 %copy-start.10 = (s32[1,1,1,8,35]{4,3,2,1,0:T(8,128)S(1)}, s32[1,1,1,8,35]{4,3,2,1,0:T(8,128)}, u32[]{:S(2)}) copy-start(s32[1,1,1,8,35]{4,3,2,1,0:T(8,128)} %param.16) | copy-start | bytes 3364
  24.7 32.5 %copy-start.11 = (f32[2,1408]{1,0:T(2,128)S(1)}, f32[2,1408]{1,0:T(2,128)}, u32[]{:S(2)}) copy-start(f32[2,1408]{1,0:T(2,128)} %constant.2.clone.ids_ref) | copy-start | bytes 33796
  32.6 0.7 copy-start.6
  33.3 0.8 copy-start.14
  34.0 0.7 copy-start.15
  34.8 0.7 copy-start.16
  41.9 15.3 %collective-permute-start.12 = (bf16[512,768]{1,0:T(8,128)(2,1)S(1)}, bf16[512,768]{1,0:T(8,128)(2,1)S(1)}, u32[]{:S(2)}, u32[]{:S(2)}) collective-permute-start(bf16[512,768]{1,0:T(8,128)(2,1)S(1)} %collective-permute-done.7.refs_6_), channel_id=1, source_target_pairs={{0,1},{1,0},{2,3},{3,2},{4,5},{5,4},{6,7},{7,6},{8,9},{9,8},{10,11... | collective-permute-start | bytes 2359304 | tf_op jit(solution)/shard_map/ppermute | solution.py:430
  41.9 15.3 %all-to-all-start = ((bf16[8,40,384]{2,1,0:T(8,128)(2,1)}), bf16[8,40,384]{2,1,0:T(8,128)(2,1)}, u32[]{:S(2)}, u32[]{:S(2)}) async-start(bf16[8,40,384]{2,1,0:T(8,128)(2,1)} %bitcast.11), calls=%async_computation | async-start | bytes 491520 | tf_op jit(solution)/shard_map/all_to_all | solution.py:559
  47.0 10.2 %collective-permute-start.9 = (bf16[768,256]{1,0:T(8,128)(2,1)}, bf16[768,256]{1,0:T(8,128)(2,1)}, u32[]{:S(2)}, u32[]{:S(2)}) collective-permute-start(bf16[768,256]{1,0:T(8,128)(2,1)} %copy-done.16), channel_id=1, source_target_pairs={{0,1},{1,0},{2,3},{3,2},{4,5},{5,4},{6,7},{7,6},{8,9},{9,8},{10,11... | collective-permute-start | bytes 1179656 | tf_op jit(solution)/shard_map/ppermute | solution.py:430
  47.2 20.1 %collective-permute-start.10 = (bf16[768,256]{1,0:T(8,128)(2,1)}, bf16[768,256]{1,0:T(8,128)(2,1)}, u32[]{:S(2)}, u32[]{:S(2)}) collective-permute-start(bf16[768,256]{1,0:T(8,128)(2,1)} %copy-done.15), channel_id=1, source_target_pairs={{0,2},{1,3},{2,0},{3,1},{4,6},{5,7},{6,4},{7,5},{8,10},{9,11},{10,... | collective-permute-start | bytes 1179656 | tf_op jit(solution)/shard_map/ppermute | solution.py:430
  48.7 18.6 %collective-permute-start.11 = (bf16[768,256]{1,0:T(8,128)(2,1)}, bf16[768,256]{1,0:T(8,128)(2,1)}, u32[]{:S(2)}, u32[]{:S(2)}) collective-permute-start(bf16[768,256]{1,0:T(8,128)(2,1)} %copy-done.14), channel_id=1, source_target_pairs={{0,3},{1,2},{2,1},{3,0},{4,7},{5,6},{6,5},{7,4},{8,11},{9,10},{10,... | collective-permute-start | bytes 1179656 | tf_op jit(solution)/shard_map/ppermute | solution.py:430
  57.2 0.6 copy-start.12
  60.3 6.2 %collective-permute-start.13 = (bf16[96,384]{1,0:T(8,128)(2,1)S(1)}, bf16[96,384]{1,0:T(8,128)(2,1)S(1)}, u32[]{:S(2)}, u32[]{:S(2)}) collective-permute-start(bf16[96,384]{1,0:T(8,128)(2,1)S(1)} %get-tuple-element.121), channel_id=1, source_target_pairs={{0,4},{4,8},{8,12},{12,0},{1,5},{5,9},{9,13},{13,1},{2,6},{6,10},{... | collective-permute-start | bytes 221192 | tf_op jit(solution)/shard_map/ppermute | solution.py:435
  60.3 6.1 %collective-permute-start.14 = (bf16[96,384]{1,0:T(8,128)(2,1)S(1)}, bf16[96,384]{1,0:T(8,128)(2,1)S(1)}, u32[]{:S(2)}, u32[]{:S(2)}) collective-permute-start(bf16[96,384]{1,0:T(8,128)(2,1)S(1)} %get-tuple-element.122), channel_id=1, source_target_pairs={{0,12},{4,0},{8,4},{12,8},{1,13},{5,1},{9,5},{13,9},{2,14},{6,2},{... | collective-permute-start | bytes 221192 | tf_op jit(solution)/shard_map/ppermute | solution.py:435
  66.7 4.7 %collective-permute-start.16 = (bf16[128,384]{1,0:T(8,128)(2,1)S(1)}, bf16[128,384]{1,0:T(8,128)(2,1)S(1)}, u32[]{:S(2)}, u32[]{:S(2)}) collective-permute-start(bf16[128,384]{1,0:T(8,128)(2,1)S(1)} %rim.1), channel_id=1, source_target_pairs={{0,16},{16,0},{1,17},{17,1},{2,18},{18,2},{3,19},{19,3},{4,20},{20... | collective-permute-start | bytes 294920 | tf_op jit(solution)/shard_map/ppermute | solution.py:435
  69.6 4.7 %copy-start.8 = (f32[7,7,384]{2,1,0:T(8,128)S(1)}, f32[7,7,384]{2,1,0:T(8,128)}, u32[]{:S(2)}) copy-start(f32[7,7,384]{2,1,0:T(8,128)} %refs_0_.1) | copy-start | bytes 225796
  69.7 12.1 %collective-permute-start.15 = (bf16[4,96,384]{2,1,0:T(8,128)(2,1)S(1)}, bf16[4,96,384]{2,1,0:T(8,128)(2,1)S(1)}, u32[]{:S(2)}, u32[]{:S(2)}) collective-permute-start(bf16[4,96,384]{2,1,0:T(8,128)(2,1)S(1)} %get-tuple-element.133), channel_id=1, source_target_pairs={{0,16},{16,0},{1,17},{17,1},{2,18},{18,2},{3,19},{19,3},{4,20},{20... | collective-permute-start | bytes 884744 | tf_op jit(solution)/shard_map/ppermute | solution.py:435
  73.7 13.5 %collective-permute-start.20 = (bf16[4,96,384]{2,1,0:T(8,128)(2,1)S(1)}, bf16[4,96,384]{2,1,0:T(8,128)(2,1)S(1)}, u32[]{:S(2)}, u32[]{:S(2)}) collective-permute-start(bf16[4,96,384]{2,1,0:T(8,128)(2,1)S(1)} %get-tuple-element.152), channel_id=1, source_target_pairs={{0,16},{16,0},{1,17},{17,1},{2,18},{18,2},{3,19},{19,3},{4,20},{20... | collective-permute-start | bytes 884744 | tf_op jit(solution)/shard_map/ppermute | solution.py:435
  74.3 16.8 %copy-start.3 = (bf16[384,768]{1,0:T(8,128)(2,1)S(1)}, bf16[384,768]{1,0:T(8,128)(2,1)}, u32[]{:S(2)}) copy-start(bf16[384,768]{1,0:T(8,128)(2,1)} %up_ref.1) | copy-start | bytes 1769476
  74.3 16.8 %copy-start.4 = (bf16[768,384]{1,0:T(8,128)(2,1)S(1)}, bf16[768,384]{1,0:T(8,128)(2,1)}, u32[]{:S(2)}) copy-start(bf16[768,384]{1,0:T(8,128)(2,1)} %down_ref.1) | copy-start | bytes 1769476
  74.3 16.8 %copy-start.7 = (bf16[384,128]{1,0:T(8,128)(2,1)S(1)}, bf16[384,128]{1,0:T(8,128)(2,1)}, u32[]{:S(2)}) copy-start(bf16[384,128]{1,0:T(8,128)(2,1)} %head_ref.1) | copy-start | bytes 294916
  81.9 7.4 %collective-permute-start.17 = (bf16[96,384]{1,0:T(8,128)(2,1)S(1)}, bf16[96,384]{1,0:T(8,128)(2,1)S(1)}, u32[]{:S(2)}, u32[]{:S(2)}) collective-permute-start(bf16[96,384]{1,0:T(8,128)(2,1)S(1)} %get-tuple-element.149), channel_id=1, source_target_pairs={{0,4},{4,8},{8,12},{12,0},{1,5},{5,9},{9,13},{13,1},{2,6},{6,10},{... | collective-permute-start | bytes 221192 | tf_op jit(solution)/shard_map/ppermute | solution.py:435
  83.3 11.1 %collective-permute-start.18 = (bf16[96,384]{1,0:T(8,128)(2,1)S(1)}, bf16[96,384]{1,0:T(8,128)(2,1)S(1)}, u32[]{:S(2)}, u32[]{:S(2)}) collective-permute-start(bf16[96,384]{1,0:T(8,128)(2,1)S(1)} %get-tuple-element.150), channel_id=1, source_target_pairs={{0,8},{4,12},{8,0},{12,4},{1,9},{5,13},{9,1},{13,5},{2,10},{6,14},... | collective-permute-start | bytes 221192 | tf_op jit(solution)/shard_map/ppermute | solution.py:435
  86.3 8.2 %collective-permute-start.19 = (bf16[96,384]{1,0:T(8,128)(2,1)S(1)}, bf16[96,384]{1,0:T(8,128)(2,1)S(1)}, u32[]{:S(2)}, u32[]{:S(2)}) collective-permute-start(bf16[96,384]{1,0:T(8,128)(2,1)S(1)} %get-tuple-element.151), channel_id=1, source_target_pairs={{0,12},{4,0},{8,4},{12,8},{1,13},{5,1},{9,5},{13,9},{2,14},{6,2},{... | collective-permute-start | bytes 221192 | tf_op jit(solution)/shard_map/ppermute | solution.py:435
  87.2 7.2 %collective-permute-start.21 = (bf16[96,384]{1,0:T(8,128)(2,1)S(1)}, bf16[96,384]{1,0:T(8,128)(2,1)S(1)}, u32[]{:S(2)}, u32[]{:S(2)}) collective-permute-start(bf16[96,384]{1,0:T(8,128)(2,1)S(1)} %get-tuple-element.156), channel_id=1, source_target_pairs={{0,4},{4,8},{8,12},{12,0},{1,5},{5,9},{9,13},{13,1},{2,6},{6,10},{... | collective-permute-start | bytes 221192 | tf_op jit(solution)/shard_map/ppermute | solution.py:435
  88.4 9.1 %collective-permute-start.22 = (bf16[96,384]{1,0:T(8,128)(2,1)S(1)}, bf16[96,384]{1,0:T(8,128)(2,1)S(1)}, u32[]{:S(2)}, u32[]{:S(2)}) collective-permute-start(bf16[96,384]{1,0:T(8,128)(2,1)S(1)} %get-tuple-element.157), channel_id=1, source_target_pairs={{0,8},{4,12},{8,0},{12,4},{1,9},{5,13},{9,1},{13,5},{2,10},{6,14},... | collective-permute-start | bytes 221192 | tf_op jit(solution)/shard_map/ppermute | solution.py:435
  89.2 8.3 %collective-permute-start.23 = (bf16[96,384]{1,0:T(8,128)(2,1)S(1)}, bf16[96,384]{1,0:T(8,128)(2,1)S(1)}, u32[]{:S(2)}, u32[]{:S(2)}) collective-permute-start(bf16[96,384]{1,0:T(8,128)(2,1)S(1)} %get-tuple-element.158), channel_id=1, source_target_pairs={{0,12},{4,0},{8,4},{12,8},{1,13},{5,1},{9,5},{13,9},{2,14},{6,2},{... | collective-permute-start | bytes 221192 | tf_op jit(solution)/shard_map/ppermute | solution.py:435
  97.6 5.2 %collective-permute-start.25 = (bf16[96,768]{1,0:T(8,128)(2,1)S(1)}, bf16[96,768]{1,0:T(8,128)(2,1)S(1)}, u32[]{:S(2)}, u32[]{:S(2)}) collective-permute-start(bf16[96,768]{1,0:T(8,128)(2,1)S(1)} %close.1.own_ref), channel_id=1, source_target_pairs={{0,2},{1,3},{2,0},{3,1},{4,6},{5,7},{6,4},{7,5},{8,10},{9,11},{10,... | collective-permute-start | bytes 442376 | tf_op jit(solution)/shard_map/ppermute | solution.py:430
  99.2 3.6 %collective-permute-start.24 = (bf16[96,768]{1,0:T(8,128)(2,1)S(1)}, bf16[96,768]{1,0:T(8,128)(2,1)S(1)}, u32[]{:S(2)}, u32[]{:S(2)}) collective-permute-start(bf16[96,768]{1,0:T(8,128)(2,1)S(1)} %close.1.own_ref), channel_id=1, source_target_pairs={{0,1},{1,0},{2,3},{3,2},{4,5},{5,4},{6,7},{7,6},{8,9},{9,8},{10,11... | collective-permute-start | bytes 442376 | tf_op jit(solution)/shard_map/ppermute | solution.py:430
  102.8 1.4 %collective-permute-start.26 = (bf16[96,768]{1,0:T(8,128)(2,1)S(1)}, bf16[96,768]{1,0:T(8,128)(2,1)S(1)}, u32[]{:S(2)}, u32[]{:S(2)}) collective-permute-start(bf16[96,768]{1,0:T(8,128)(2,1)S(1)} %collective-permute-done.25.two_ref), channel_id=1, source_target_pairs={{0,1},{1,0},{2,3},{3,2},{4,5},{5,4},{6,7},{7,6},{8,9},{9,8},{10,11... | collective-permute-start | bytes 442376 | tf_op jit(solution)/shard_map/ppermute | solution.py:430

commit v11 on v10

--- a/solution.py
+++ b/solution.py
@@ -92,7 +92,7 @@
 
 
 def norm_kernel(cap, padded, src_ref, cot_ref, *refs):
-    arr_refs, (both_ref, enc_ref, place_ref) = refs[:-3], refs[-3:]
+    arr_refs, (both_ref, normed_ref, enc_ref, place_ref) = refs[:-4], refs[-4:]
     rows = enc_ref.shape[0]
     group = len(arr_refs)
     src = src_ref[...].astype(f32)
@@ -113,13 +113,15 @@
     enc_ref[...] = enc_in.astype(bf16)
     centred = enc_in - jnp.mean(enc_in, axis=-1, keepdims=True)
     spread = jnp.mean(centred * centred, axis=-1, keepdims=True)
-    both_ref[0:rows] = (centred * lax.rsqrt(spread + norm_eps)).astype(bf16)
+    normed = (centred * lax.rsqrt(spread + norm_eps)).astype(bf16)
+    normed_ref[...] = normed
+    both_ref[0:rows] = normed
     both_ref[rows : 2 * rows] = cot_ref[...]
 
 
 def project_kernel(normed_ref, wqkv_t_ref, u_ref, len_ref, v_ref):
     width = v_ref.shape[0]
-    normed = normed_ref[0 : v_ref.shape[1]]
+    normed = normed_ref[...]
     heads = len_ref.shape[0] // 2
     size = width // heads
     for t in range(2):
@@ -134,15 +136,15 @@
 
 
 def encode_kernel(
-    split, win_ref, scale_ref, place_ref, enc_ref, u_ref, len_ref, v_ref, ga_ref, wout_ref,
-    wdec_ref, out_ref, *refs,
+    split, sends, win_ref, scale_ref, place_ref, enc_ref, u_ref, len_ref, v_ref, ga_ref, wout_ref,
+    wdec_ref, *refs,
 ):
-    peer_refs = refs[:-3]
-    p_ref, att_ref, left_ref = refs[-3:]
+    out_refs, peer_refs = refs[:sends], refs[sends:-4]
+    p_ref, att_ref, left_ref, all_ref = refs[-4:]
     rows, width = enc_ref.shape
     heads = p_ref.shape[0]
     size = width // heads
-    slots = out_ref.shape[0]
+    slots = sends * out_refs[0].shape[0]
     win = win_ref[...].astype(f32)
     same = column_of(win) == win
     for h in range(heads):
@@ -161,7 +163,16 @@
     dec = mm(enc_out, wdec_ref[...]).astype(bf16)
     places = lax.broadcasted_iota(jnp.int32, (slots, rows), 0).astype(f32)
     put = (places == place_ref[...]).astype(f32).astype(bf16)
-    out_ref[...] = mm(put, dec).astype(bf16)
+    placed = mm(put, dec)
+    if sends == 1:
+        out_refs[0][...] = placed.astype(bf16)
+    else:
+        step = slots // sends
+        for d in range(sends):
+            all_ref[d] = placed[d * step : (d + 1) * step].astype(bf16)
+        place = plane_index()
+        for n, ref in enumerate(out_refs):
+            ref[...] = all_ref[lax.rem(place + n, sends)]
     for h in range(heads):
         lo, hi = h * size, (h + 1) * size
         ga = ga_ref[lo:hi]
@@ -207,18 +218,21 @@
 
 
 def term_kernel(c, *refs):
-    lefts, rights = refs[0:4], refs[4:8]
-    keep_ref, send_ref = refs[8:]
+    lefts, rights = refs[0:4], refs[4:10]
+    keep_ref, send_ref = refs[10:]
     half, part, chunk = keep_ref.shape
     cut = slice(c * chunk, (c + 1) * chunk)
 
     count = lefts[0].shape[1]
-    normed, cots = slice(0, count), slice(count, 2 * count)
-
-    def block(lo, hi, which, cols):
+    whole = slice(0, count)
+    below = slice(count, 2 * count)
+    normed = [(ref, whole) for ref in rights[0:4]]
+    cots = [(ref, below) for ref in rights[0:2]] + [(ref, whole) for ref in rights[4:6]]
+
+    def block(lo, hi, right, cols):
         acc = None
-        for left, e in zip(lefts, rights):
-            step = mm(left[lo:hi], e[which, cols])
+        for left, (ref, which) in zip(lefts, right):
+            step = mm(left[lo:hi], ref[which, cols])
             acc = step if acc is None else acc + step
         return acc
 
@@ -288,17 +302,24 @@
     return lax.optimization_barrier((values, others))[0]
 
 
-def fill_kernel(padded, pos_ref, ids_ref, mask_ref, got_ref, *refs):
-    wide_ref = refs[-1]
+def fill_kernel(padded, parts, pos_ref, ids_ref, mask_ref, *refs):
+    got_refs, (wide_ref, all_ref) = refs[:parts], refs[-2:]
+    refs = refs[parts:-2]
     slots = slot_column(pos_ref, wide_ref, padded)
     ids = ids_ref[0:1] + lax.axis_index("eta").astype(f32) * ids_ref[1:2]
     chosen = (slots == ids).astype(f32).astype(bf16)
-    got = got_ref[...]
+    if parts == 1:
+        got = got_refs[0][...]
+    else:
+        me = plane_index()
+        for k, ref in enumerate(got_refs):
+            all_ref[lax.rem(me + parts - k, parts)] = ref[...].astype(f32)
+        got = all_ref[...].reshape(parts * padded, got_refs[0].shape[1]).astype(bf16)
     values = mm(chosen, got, TN)
     hits = mm(chosen, jnp.ones((got.shape[0], 128), bf16), TN)[:, 0:1]
     values = jnp.where(hits > 0.5, values, mask_ref[...].astype(f32)).astype(bf16)
     at = 0
-    for ref in refs[:-1]:
+    for ref in refs:
         ref[...] = values[at : at + ref.shape[0]]
         at += ref.shape[0]
 
@@ -510,12 +531,14 @@
         nbytes=10 * MIB,
         limit=10,
     )(cotangent, w_out, w_qkv)
+    if fast:
+        cot_y = flip(cotangent, "replica", 2)
     arrived = tie(arrived, w_qkv_t)
 
-    both, enc_in, places = call(
+    both, normed, enc_in, places = call(
         functools.partial(norm_kernel, cap, padded),
         "norm",
-        [sds((2 * rows, width), bf16), sds((rows, width), bf16), sds((1, rows), f32)],
+        [sds((2 * rows, width), bf16)] + [sds((rows, width), bf16)] * 2 + [sds((1, rows), f32)],
         [vmem()] * (2 + len(arrived)),
         flops=2 * rows * width * slots,
         nbytes=2 * MIB,
@@ -523,7 +546,7 @@
         cost=600000000,
     )(enc_src.reshape(1, rows), cotangent, *arrived)
     if fast:
-        both_y = flip(both, "replica", 2)
+        normed_y = flip(normed, "replica", 2)
         both_c = flip(both, "replica", 1)
     units, lengths, values = call(
         project_kernel,
@@ -534,17 +557,19 @@
         nbytes=8 * MIB,
         limit=10,
         cost=2000000000,
-    )(both, w_qkv_t)
-
-    outbound, *lefts = call(
-        functools.partial(encode_kernel, split),
+    )(normed, w_qkv_t)
+
+    sends = group if turned else 1
+    outs = call(
+        functools.partial(encode_kernel, split, sends),
         "encode",
-        [sds((slots, dec_width), bf16)] + [sds(left_part, bf16)] * pieces,
+        [sds((slots // sends, dec_width), bf16)] * sends + [sds(left_part, bf16)] * pieces,
         [vmem(), smem()] + [vmem()] * 8,
         scratch=[
             pltpu.VMEM((heads, rows, rows), bf16),
             pltpu.VMEM((width, rows), bf16),
             pltpu.VMEM(left_whole, bf16),
+            pltpu.VMEM((group, padded, dec_width), bf16),
         ],
         flops=2 * rows * width * width * 10,
         nbytes=8 * MIB,
@@ -554,18 +579,31 @@
         window_id.reshape(1, rows), head_scale, places, enc_in, units, lengths, values, grad_att,
         w_out, w_dec_in,
     )
+    outbound, lefts = list(outs[:sends]), list(outs[sends:])
     if fast:
-        lefts, both_y, both_c = lax.optimization_barrier((lefts, both_y, both_c))
-    returned = lax.all_to_all(
-        outbound.reshape(group, padded, dec_width), ("eta", "phi"), split_axis=0, concat_axis=0,
-        tiled=True,
-    )
+        lefts, normed_y, cot_y, both_c = lax.optimization_barrier(
+            (lefts, normed_y, cot_y, both_c)
+        )
     if fast:
         lefts = [lefts[0]] + [flip(lefts[k], "replica", k) for k in range(1, 4)]
-        rights = [both, both_c, both_y, flip(both_y, "replica", 1)]
-        returned = tie(returned, lefts[1], rights[3])
-    else:
-        grad_total = summed_slow(lefts[0], both[:rows], cotangent)
+        rights = [both, both_c, normed_y, flip(normed_y, "replica", 1)]
+        rights += [cot_y, flip(cot_y, "replica", 1)]
+        outbound = tie(outbound, lefts[1], rights[3], rights[5])
+    else:
+        grad_total = summed_slow(lefts[0], normed, cotangent)
+
+    if turned:
+        returned = [outbound[0]]
+        for k in range(1, group):
+            pairs = [(i, (i + k) % group) for i in range(group)]
+            returned.append(lax.ppermute(outbound[k], ("eta", "phi"), pairs))
+    else:
+        returned = [
+            lax.all_to_all(
+                outbound[0].reshape(group, padded, dec_width), ("eta", "phi"), split_axis=0,
+                concat_axis=0, tiled=True,
+            ).reshape(slots, dec_width)
+        ]
 
     span = conv_kernel.shape[0]
     rim = span // 2
@@ -588,17 +626,17 @@
         ids[1, at : at + p.size] = move
         at += size
     filled = call(
-        functools.partial(fill_kernel, padded),
+        functools.partial(fill_kernel, padded, len(returned)),
         "fill",
         [sds((size, dec_width), bf16) for size in sizes],
-        [vmem()] * 4,
-        scratch=[pltpu.VMEM((group, 128), f32)],
+        [vmem()] * (3 + len(returned)),
+        scratch=[pltpu.VMEM((group, 128), f32), pltpu.VMEM((group, padded, dec_width), f32)],
         flops=2 * slots * ids.shape[1] * (dec_width + 128),
         nbytes=3 * MIB,
         limit=12,
     )(
         positions, jnp.asarray(ids), mask_token.reshape(1, dec_width),
-        returned.reshape(slots, dec_width),
+        *returned,
     )
     dec_grid = filled[0]
     if folded:
@@ -642,7 +680,7 @@
                 functools.partial(term_kernel, c),
                 "terms%d" % c,
                 [sds((half, part_rows, chunk), f32), sds((half, part_rows, chunk), bf16)],
-                [vmem()] * 8,
+                [vmem()] * 10,
                 flops=2 * out_rows * chunk * rows,
                 nbytes=8 * MIB,
                 limit=10,

time: 106 us -> 100 us (0.943)
  starting transfers between devices: 40.4 us -> 46.4 us
  local copies, waits for them, and re-layouts: 8.93 us -> 4.16 us
  Pallas kernels: 31.1 us -> 27.6 us
  waiting for transfers between devices: 23.9 us -> 20.7 us
    ppermute x0 -> x7, starting transfers between devices: none -> 9.83 us  [body(): returned.append(lax.ppermute(outbound[k], ('eta', 'phi'), pairs))]
    all_to_all x1 -> x0, waiting for transfers between devices: 7.11 us -> none  [body(): lax.all_to_all(outbound.reshape(group, padded, dec_width), ('eta', 'phi')...]
    all_to_all x1 -> x0, starting transfers between devices: 5.13 us -> none  [body(): lax.all_to_all(outbound.reshape(group, padded, dec_width), ('eta', 'phi')...]
    ppermute x0 -> x7, waiting for transfers between devices: none -> 4.85 us  [body(): returned.append(lax.ppermute(outbound[k], ('eta', 'phi'), pairs))]
    unnamed x40 -> x32, local copies, waits for them, and re-layouts: 7.71 us -> 4.15 us
    pallas_call x2, Pallas kernels: 4.65 us -> 2.15 us  [body(): call(functools.partial(term_kernel, c), 'terms%d' % c, [sds((half, part_r...]
    ppermute x9 -> x11, waiting for transfers between devices: 11.3 us -> 9.86 us  [flip(): lax.ppermute(value, axis, [(i, i ^ bit) for i in range(lax.axis_size(axis...]
    reshape x1, local copies, waits for them, and re-layouts: 1.22 us -> 0.01 us  [body(): mask_token.reshape(1, dec_width)]
  transfers between devices with their start and end apart: 28 -> 36, of which waited for: 7 -> 13; matrix products, arithmetic and copies ran while one was open for 1% -> 0% of each run, Pallas kernels for 27% -> 26%
where the time goes in v11:
time: 100 us; the launch traced here: 99.8 us
  starting transfers between devices  46.4 us (46%)
  Pallas kernels  27.6 us (28%)
  waiting for transfers between devices  20.7 us (21%)
  local copies, waits for them, and re-layouts  4.16 us (4%)
    ppermute x11, starting transfers between devices, turn(): lax.ppermute(value, axis, [(i, (i + k) % count) for i in range(count)])  16 us
    ppermute x7, starting transfers between devices, body(): arrived.append(lax.ppermute(outgoing[k], ('eta', 'phi'), pairs))  14.3 us
    ppermute x11, waiting for transfers between devices, flip(): lax.ppermute(value, axis, [(i, i ^ bit) for i in range(lax.axis_size(axis...  9.86 us
    ppermute x7, starting transfers between devices, body(): returned.append(lax.ppermute(outbound[k], ('eta', 'phi'), pairs))  9.83 us
    pallas_call x1, Pallas kernels, body(): call(functools.partial(encode_kernel, split, sends), 'encode', [sds((slot...  7.97 us
    pallas_call x1, Pallas kernels, body(): call(functools.partial(mix_folded if folded else mix_open, (eta_cells, ph...  7.46 us
    ppermute x11, starting transfers between devices, flip(): lax.ppermute(value, axis, [(i, i ^ bit) for i in range(lax.axis_size(axis...  6.2 us
    ppermute x11, waiting for transfers between devices, turn(): lax.ppermute(value, axis, [(i, (i + k) % count) for i in range(count)])  5.98 us
  transfers between devices with their start and end apart: 36, of which 13 were waited for; matrix products, arithmetic and copies ran while one was open for 0% of the time, Pallas kernels for 26%

profile of v11, /device:TPU:0, one launch (start us, length us, event | category | flops | bytes accessed | tf_op | source)
XLA Modules:
  0.0 99.8 jit_solution(11364370619997207036)
XLA Ops:
  0.6 1.4 %copy-done.1 = bf16[1,32,32,768]{3,2,1,0:T(8,128)(2,1)S(1)} copy-done((bf16[1,32,32,768]{3,2,1,0:T(8,128)(2,1)S(1)}, bf16[1,32,32,768]{3,2,1,0:T(8,128)(2,1)}, u32[]{:S(2)}) %copy-start.1) | copy-done | bytes 1572888
  2.0 0.7 copy-done.8
  2.7 0.9 pick.1
  3.7 3.1 %collective-permute-start = (bf16[40,768]{1,0:T(8,128)(2,1)S(1)}, bf16[40,768]{1,0:T(8,128)(2,1)S(1)}, u32[]{:S(2)}, u32[]{:S(2)}) collective-permute-start(bf16[40,768]{1,0:T(8,128)(2,1)S(1)} %get-tuple-element.106), channel_id=1, source_target_pairs={{0,4},{4,8},{8,12},{12,16},{16,20},{20,24},{24,28},{28,0},{1,5},{5... | collective-permute-start | bytes 184328 | tf_op jit(solution)/shard_map/ppermute | solution.py:511
  6.7 2.6 %collective-permute-start.1 = (bf16[40,768]{1,0:T(8,128)(2,1)S(1)}, bf16[40,768]{1,0:T(8,128)(2,1)S(1)}, u32[]{:S(2)}, u32[]{:S(2)}) collective-permute-start(bf16[40,768]{1,0:T(8,128)(2,1)S(1)} %get-tuple-element.107), channel_id=1, source_target_pairs={{0,8},{4,12},{8,16},{12,20},{16,24},{20,28},{24,0},{28,4},{1,9},{5... | collective-permute-start | bytes 184328 | tf_op jit(solution)/shard_map/ppermute | solution.py:511
  9.3 2.3 %collective-permute-start.2 = (bf16[40,768]{1,0:T(8,128)(2,1)S(1)}, bf16[40,768]{1,0:T(8,128)(2,1)S(1)}, u32[]{:S(2)}, u32[]{:S(2)}) collective-permute-start(bf16[40,768]{1,0:T(8,128)(2,1)S(1)} %get-tuple-element.108), channel_id=1, source_target_pairs={{0,12},{4,16},{8,20},{12,24},{16,28},{20,0},{24,4},{28,8},{1,13},{... | collective-permute-start | bytes 184328 | tf_op jit(solution)/shard_map/ppermute | solution.py:511
  12.1 1.6 %collective-permute-start.4 = (bf16[40,768]{1,0:T(8,128)(2,1)S(1)}, bf16[40,768]{1,0:T(8,128)(2,1)S(1)}, u32[]{:S(2)}, u32[]{:S(2)}) collective-permute-start(bf16[40,768]{1,0:T(8,128)(2,1)S(1)} %get-tuple-element.110), channel_id=1, source_target_pairs={{0,20},{4,24},{8,28},{12,0},{16,4},{20,8},{24,12},{28,16},{1,21},{... | collective-permute-start | bytes 184328 | tf_op jit(solution)/shard_map/ppermute | solution.py:511
  13.7 1.2 %collective-permute-start.5 = (bf16[40,768]{1,0:T(8,128)(2,1)S(1)}, bf16[40,768]{1,0:T(8,128)(2,1)S(1)}, u32[]{:S(2)}, u32[]{:S(2)}) collective-permute-start(bf16[40,768]{1,0:T(8,128)(2,1)S(1)} %get-tuple-element.111), channel_id=1, source_target_pairs={{0,24},{4,28},{8,0},{12,4},{16,8},{20,12},{24,16},{28,20},{1,25},{... | collective-permute-start | bytes 184328 | tf_op jit(solution)/shard_map/ppermute | solution.py:511
  15.0 3.0 %collective-permute-start.6 = (bf16[40,768]{1,0:T(8,128)(2,1)S(1)}, bf16[40,768]{1,0:T(8,128)(2,1)S(1)}, u32[]{:S(2)}, u32[]{:S(2)}) collective-permute-start(bf16[40,768]{1,0:T(8,128)(2,1)S(1)} %get-tuple-element.112), channel_id=1, source_target_pairs={{0,28},{4,0},{8,4},{12,8},{16,12},{20,16},{24,20},{28,24},{1,29},{... | collective-permute-start | bytes 184328 | tf_op jit(solution)/shard_map/ppermute | solution.py:511
  18.0 2.0 %copy-done = bf16[768,2304]{1,0:T(8,128)(2,1)S(1)} copy-done((bf16[768,2304]{1,0:T(8,128)(2,1)S(1)}, bf16[768,2304]{1,0:T(8,128)(2,1)}, u32[]{:S(2)}) %copy-start) | copy-done | bytes 3538968
  20.0 1.0 %prep.1 = (bf16[768,256]{1,0:T(8,128)(2,1)S(1)}, bf16[2304,768]{1,0:T(8,128)(2,1)S(1)}) custom-call(bf16[256,768]{1,0:T(8,128)(2,1)S(1)} %bitcast.7, bf16[768,768]{1,0:T(8,128)(2,1)S(1)} %copy-done.2, bf16[768,2304]{1,0:T(8,128)(2,1)S(1)} %copy-done), custom_call_target="tpu_custom_call" | custom-call | flops 1000 | bytes 1003 | tf_op jit(solution)/shard_map/prep/pallas_call | solution.py:525
  21.0 1.6 %collective-permute-start.8 = (bf16[256,768]{1,0:T(8,128)(2,1)S(1)}, bf16[256,768]{1,0:T(8,128)(2,1)S(1)}, u32[]{:S(2)}, u32[]{:S(2)}) collective-permute-start(bf16[256,768]{1,0:T(8,128)(2,1)S(1)} %bitcast.8), channel_id=1, source_target_pairs={{0,2},{1,3},{2,0},{3,1},{4,6},{5,7},{6,4},{7,5},{8,10},{9,11},{10,... | collective-permute-start | bytes 1179656 | tf_op jit(solution)/shard_map/ppermute | solution.py:451
  22.6 0.8 norm.1
  23.5 1.1 %project.1 = (f32[1536,256]{1,0:T(8,128)S(1)}, f32[24,256]{1,0:T(8,128)S(1)}, bf16[768,256]{1,0:T(8,128)(2,1)S(1)}) custom-call(bf16[256,768]{1,0:T(8,128)(2,1)S(1)} %get-tuple-element.124.normed_ref, bf16[2304,768]{1,0:T(8,128)(2,1)S(1)} %get-tuple-element.113.wqkv_t_ref), custom_call_target="tpu_custom_call" | custom-call | flops 2000000000 | bytes 6667666 | tf_op jit(solution)/shard_map/project/pallas_call | solution.py:551
  25.3 8.0 %encode.1 = (bf16[40,384]{1,0:T(8,128)(2,1)S(1)}, bf16[40,384]{1,0:T(8,128)(2,1)S(1)}, bf16[40,384]{1,0:T(8,128)(2,1)S(1)}, bf16[40,384]{1,0:T(8,128)(2,1)S(1)},...) custom-call(s32[1,256]{1,0:T(1,128)S(1)} %bitcast.13, ...), custom_call_target="tpu_custom_call" | custom-call | flops 8000000000 | bytes 26667666 | tf_op jit(solution)/shard_map/encode/pallas_call | solution.py:563
  33.3 4.4 %collective-permute-done.7.refs_6_ = bf16[256,768]{1,0:T(8,128)(2,1)S(1)} collective-permute-done((bf16[256,768]{1,0:T(8,128)(2,1)S(1)}, bf16[256,768]{1,0:T(8,128)(2,1)S(1)}, u32[]{:S(2)}, u32[]{:S(2)}) %collective-permute-start.7) | collective-permute-done | bytes 393248 | tf_op jit(solution)/shard_map/ppermute | solution.py:451
  38.2 1.5 %collective-permute-start.11 = (bf16[768,256]{1,0:T(8,128)(2,1)S(1)}, bf16[768,256]{1,0:T(8,128)(2,1)S(1)}, u32[]{:S(2)}, u32[]{:S(2)}) collective-permute-start(bf16[768,256]{1,0:T(8,128)(2,1)S(1)} %get-tuple-element.136), channel_id=1, source_target_pairs={{0,2},{1,3},{2,0},{3,1},{4,6},{5,7},{6,4},{7,5},{8,10},{9,11},{10,... | collective-permute-start | bytes 1179656 | tf_op jit(solution)/shard_map/ppermute | solution.py:451
  41.1 1.1 %collective-permute-start.16 = (bf16[40,384]{1,0:T(8,128)(2,1)S(1)}, bf16[40,384]{1,0:T(8,128)(2,1)S(1)}, u32[]{:S(2)}, u32[]{:S(2)}) collective-permute-start(bf16[40,384]{1,0:T(8,128)(2,1)S(1)} %get-tuple-element.151), channel_id=1, source_target_pairs={{0,8},{4,12},{8,16},{12,20},{16,24},{20,28},{24,0},{28,4},{1,9},{5... | collective-permute-start | bytes 92168 | tf_op jit(solution)/shard_map/ppermute | solution.py:599
  42.2 2.9 %collective-permute-start.17 = (bf16[40,384]{1,0:T(8,128)(2,1)S(1)}, bf16[40,384]{1,0:T(8,128)(2,1)S(1)}, u32[]{:S(2)}, u32[]{:S(2)}) collective-permute-start(bf16[40,384]{1,0:T(8,128)(2,1)S(1)} %get-tuple-element.152), channel_id=1, source_target_pairs={{0,12},{4,16},{8,20},{12,24},{16,28},{20,0},{24,4},{28,8},{1,13},{... | collective-permute-start | bytes 92168 | tf_op jit(solution)/shard_map/ppermute | solution.py:599
  45.1 2.3 %collective-permute-done.15.refs_1_ = bf16[40,384]{1,0:T(8,128)(2,1)S(1)} collective-permute-done((bf16[40,384]{1,0:T(8,128)(2,1)S(1)}, bf16[40,384]{1,0:T(8,128)(2,1)S(1)}, u32[]{:S(2)}, u32[]{:S(2)}) %collective-permute-start.15) | collective-permute-done | bytes 30752 | tf_op jit(solution)/shard_map/ppermute | solution.py:599
  47.8 0.8 collective-permute-start.19
  48.6 2.4 %collective-permute-start.20 = (bf16[40,384]{1,0:T(8,128)(2,1)S(1)}, bf16[40,384]{1,0:T(8,128)(2,1)S(1)}, u32[]{:S(2)}, u32[]{:S(2)}) collective-permute-start(bf16[40,384]{1,0:T(8,128)(2,1)S(1)} %get-tuple-element.155), channel_id=1, source_target_pairs={{0,24},{4,28},{8,0},{12,4},{16,8},{20,12},{24,16},{28,20},{1,25},{... | collective-permute-start | bytes 92168 | tf_op jit(solution)/shard_map/ppermute | solution.py:599
  51.3 1.6 %collective-permute-start.21 = (bf16[40,384]{1,0:T(8,128)(2,1)S(1)}, bf16[40,384]{1,0:T(8,128)(2,1)S(1)}, u32[]{:S(2)}, u32[]{:S(2)}) collective-permute-start(bf16[40,384]{1,0:T(8,128)(2,1)S(1)} %get-tuple-element.156), channel_id=1, source_target_pairs={{0,28},{4,0},{8,4},{12,8},{16,12},{20,16},{24,20},{28,24},{1,29},{... | collective-permute-start | bytes 92168 | tf_op jit(solution)/shard_map/ppermute | solution.py:599
  53.0 0.6 collective-permute-done.19.refs_5_
  53.6 0.8 collective-permute-done.20.refs_6_
  54.4 0.8 collective-permute-done.21.refs_7_
  55.2 1.5 %fill.1 = (bf16[1024,384]{1,0:T(8,128)(2,1)S(1)}, bf16[96,384]{1,0:T(8,128)(2,1)S(1)}, bf16[96,384]{1,0:T(8,128)(2,1)S(1)}, bf16[96,384]{1,0:T(8,128)(2,1)S(1)}) custom-call(s32[8,35]{1,0:T(8,128)S(1)} %bitcast.11, f32[2,1408]{1,0:T(2,128)S(1)} %copy-done.10, bf16[1,384]{1,0:T(2,128)(2,1)S(1)} %reshape.30.mask_ref, ...), custom_call_target="tpu_custom_call" | custom-call | flops 1000 | bytes 1003 | tf_op jit(solution)/shard_map/fill/pallas_call | solution.py:628
  56.7 2.0 %collective-permute-start.22 = (bf16[96,384]{1,0:T(8,128)(2,1)S(1)}, bf16[96,384]{1,0:T(8,128)(2,1)S(1)}, u32[]{:S(2)}, u32[]{:S(2)}) collective-permute-start(bf16[96,384]{1,0:T(8,128)(2,1)S(1)} %get-tuple-element.157), channel_id=1, source_target_pairs={{0,4},{4,8},{8,12},{12,0},{1,5},{5,9},{9,13},{13,1},{2,6},{6,10},{... | collective-permute-start | bytes 221192 | tf_op jit(solution)/shard_map/ppermute | solution.py:456
  58.7 1.9 %collective-permute-start.23 = (bf16[96,384]{1,0:T(8,128)(2,1)S(1)}, bf16[96,384]{1,0:T(8,128)(2,1)S(1)}, u32[]{:S(2)}, u32[]{:S(2)}) collective-permute-start(bf16[96,384]{1,0:T(8,128)(2,1)S(1)} %get-tuple-element.158), channel_id=1, source_target_pairs={{0,12},{4,0},{8,4},{12,8},{1,13},{5,1},{9,5},{13,9},{2,14},{6,2},{... | collective-permute-start | bytes 221192 | tf_op jit(solution)/shard_map/ppermute | solution.py:456
  60.6 2.4 %collective-permute-done.22.left_ref.left = bf16[96,384]{1,0:T(8,128)(2,1)S(1)} collective-permute-done((bf16[96,384]{1,0:T(8,128)(2,1)S(1)}, bf16[96,384]{1,0:T(8,128)(2,1)S(1)}, u32[]{:S(2)}, u32[]{:S(2)}) %collective-permute-start.22) | collective-permute-done | bytes 73760 | tf_op jit(solution)/shard_map/ppermute | solution.py:456
  63.0 0.7 collective-permute-done.23.right_ref.right
  63.7 0.6 collective-permute-start.25
  64.3 1.1 %terms0.1 = (f32[4,96,384]{2,1,0:T(8,128)S(1)}, bf16[4,96,384]{2,1,0:T(8,128)(2,1)S(1)}) custom-call(bf16[768,256]{1,0:T(8,128)(2,1)S(1)} %get-tuple-element.173.refs_0_, bf16[768,256]{1,0:T(8,128)(2,1)S(1)} %collective-permute-done.10.refs_1_, bf16[768,256]{1,0:T(8,128)(2,1)S(1)} %collective-permute-done.11.refs_2_, ...), custom_call_target="tpu_custom_call" | custom-call | flops 1000 | bytes 1003 | tf_op jit(solution)/shard_map/terms0/pallas_call | solution.py:679
  65.4 1.6 %collective-permute-start.24 = (bf16[4,96,384]{2,1,0:T(8,128)(2,1)S(1)}, bf16[4,96,384]{2,1,0:T(8,128)(2,1)S(1)}, u32[]{:S(2)}, u32[]{:S(2)}) collective-permute-start(bf16[4,96,384]{2,1,0:T(8,128)(2,1)S(1)} %get-tuple-element.171), channel_id=1, source_target_pairs={{0,16},{16,0},{1,17},{17,1},{2,18},{18,2},{3,19},{19,3},{4,20},{20... | collective-permute-start | bytes 884744 | tf_op jit(solution)/shard_map/ppermute | solution.py:456
  67.0 2.3 %collective-permute-done.25.a = bf16[128,384]{1,0:T(8,128)(2,1)S(1)} collective-permute-done((bf16[128,384]{1,0:T(8,128)(2,1)S(1)}, bf16[128,384]{1,0:T(8,128)(2,1)S(1)}, u32[]{:S(2)}, u32[]{:S(2)}) %collective-permute-start.25) | collective-permute-done | bytes 98336 | tf_op jit(solution)/shard_map/ppermute | solution.py:456
  69.3 1.1 %terms1.1 = (f32[4,96,384]{2,1,0:T(8,128)S(1)}, bf16[4,96,384]{2,1,0:T(8,128)(2,1)S(1)}) custom-call(bf16[768,256]{1,0:T(8,128)(2,1)S(1)} %get-tuple-element.173.refs_0_, bf16[768,256]{1,0:T(8,128)(2,1)S(1)} %collective-permute-done.10.refs_1_, bf16[768,256]{1,0:T(8,128)(2,1)S(1)} %collective-permute-done.11.refs_2_, ...), custom_call_target="tpu_custom_call" | custom-call | flops 1000 | bytes 1003 | tf_op jit(solution)/shard_map/terms1/pallas_call | solution.py:679
  70.4 0.8 collective-permute-start.29
  71.2 7.5 %mix.1.normed_ref = bf16[1024,384]{1,0:T(8,128)(2,1)S(1)} custom-call(bf16[1024,384]{1,0:T(8,128)(2,1)S(1)} %get-tuple-element.172.grid.grid_ref, bf16[96,384]{1,0:T(8,128)(2,1)S(1)} %collective-permute-done.22.left_ref.left, bf16[96,384]{1,0:T(8,128)(2,1)S(1)} %collective-permute-done.23.right_ref.right, bf16[128,384]{1,0:T(8,128)(2,1)S(1)} %collective-permute-done.25.a, ...), custom_call_target="tpu_custom_call" | custom-call | flops 1000 | bytes 1003 | tf_op jit(solution)/shard_map/mix/pallas_call | solution.py:695
  78.7 1.2 %collective-permute-start.26 = (bf16[96,384]{1,0:T(8,128)(2,1)S(1)}, bf16[96,384]{1,0:T(8,128)(2,1)S(1)}, u32[]{:S(2)}, u32[]{:S(2)}) collective-permute-start(bf16[96,384]{1,0:T(8,128)(2,1)S(1)} %get-tuple-element.189), channel_id=1, source_target_pairs={{0,4},{4,8},{8,12},{12,0},{1,5},{5,9},{9,13},{13,1},{2,6},{6,10},{... | collective-permute-start | bytes 221192 | tf_op jit(solution)/shard_map/ppermute | solution.py:456
  79.9 3.3 %collective-permute-start.27 = (bf16[96,384]{1,0:T(8,128)(2,1)S(1)}, bf16[96,384]{1,0:T(8,128)(2,1)S(1)}, u32[]{:S(2)}, u32[]{:S(2)}) collective-permute-start(bf16[96,384]{1,0:T(8,128)(2,1)S(1)} %get-tuple-element.190), channel_id=1, source_target_pairs={{0,8},{4,12},{8,0},{12,4},{1,9},{5,13},{9,1},{13,5},{2,10},{6,14},... | collective-permute-start | bytes 221192 | tf_op jit(solution)/shard_map/ppermute | solution.py:456
  83.2 0.9 collective-permute-start.28
  84.1 1.2 %collective-permute-start.30 = (bf16[96,384]{1,0:T(8,128)(2,1)S(1)}, bf16[96,384]{1,0:T(8,128)(2,1)S(1)}, u32[]{:S(2)}, u32[]{:S(2)}) collective-permute-start(bf16[96,384]{1,0:T(8,128)(2,1)S(1)} %get-tuple-element.196), channel_id=1, source_target_pairs={{0,4},{4,8},{8,12},{12,0},{1,5},{5,9},{9,13},{13,1},{2,6},{6,10},{... | collective-permute-start | bytes 221192 | tf_op jit(solution)/shard_map/ppermute | solution.py:456
  85.3 2.7 %collective-permute-start.32 = (bf16[96,384]{1,0:T(8,128)(2,1)S(1)}, bf16[96,384]{1,0:T(8,128)(2,1)S(1)}, u32[]{:S(2)}, u32[]{:S(2)}) collective-permute-start(bf16[96,384]{1,0:T(8,128)(2,1)S(1)} %get-tuple-element.198), channel_id=1, source_target_pairs={{0,12},{4,0},{8,4},{12,8},{1,13},{5,1},{9,5},{13,9},{2,14},{6,2},{... | collective-permute-start | bytes 221192 | tf_op jit(solution)/shard_map/ppermute | solution.py:456
  88.0 3.4 %feed.1 = f32[1024,128]{1,0:T(8,128)} custom-call(bf16[1024,384]{1,0:T(8,128)(2,1)S(1)} %mix.1.normed_ref, bf16[1024,384]{1,0:T(8,128)(2,1)S(1)} %get-tuple-element.172.grid.grid_ref, bf16[384,768]{1,0:T(8,128)(2,1)S(1)} %copy-done.3, bf16[768,384]{1,0:T(8,128)(2,1)S(1)} %copy-done.4, bf16[384,128]{1,0:T(8,128)(2,1)S(1)} %copy-done.6), custom_call_target="tpu_custom_call" | custom-call | flops 1000 | bytes 1003 | tf_op jit(solution)/shard_map/feed/pallas_call | solution.py:723
  92.0 1.6 %collective-permute-start.34 = (bf16[96,768]{1,0:T(8,128)(2,1)S(1)}, bf16[96,768]{1,0:T(8,128)(2,1)S(1)}, u32[]{:S(2)}, u32[]{:S(2)}) collective-permute-start(bf16[96,768]{1,0:T(8,128)(2,1)S(1)} %close.1.own_ref), channel_id=1, source_target_pairs={{0,2},{1,3},{2,0},{3,1},{4,6},{5,7},{6,4},{7,5},{8,10},{9,11},{10,... | collective-permute-start | bytes 442376 | tf_op jit(solution)/shard_map/ppermute | solution.py:451
  93.6 3.6 %collective-permute-done.34.two_ref = bf16[96,768]{1,0:T(8,128)(2,1)S(1)} collective-permute-done((bf16[96,768]{1,0:T(8,128)(2,1)S(1)}, bf16[96,768]{1,0:T(8,128)(2,1)S(1)}, u32[]{:S(2)}, u32[]{:S(2)}) %collective-permute-start.34) | collective-permute-done | bytes 147488 | tf_op jit(solution)/shard_map/ppermute | solution.py:451
  97.2 1.4 %collective-permute-done.35.three_ref = bf16[96,768]{1,0:T(8,128)(2,1)S(1)} collective-permute-done((bf16[96,768]{1,0:T(8,128)(2,1)S(1)}, bf16[96,768]{1,0:T(8,128)(2,1)S(1)}, u32[]{:S(2)}, u32[]{:S(2)}) %collective-permute-start.35) | collective-permute-done | bytes 147488 | tf_op jit(solution)/shard_map/ppermute | solution.py:451
  98.6 1.2 %spread.1 = f32[384,768]{1,0:T(8,128)} custom-call(bf16[96,768]{1,0:T(8,128)(2,1)S(1)} %close.1.own_ref, bf16[96,768]{1,0:T(8,128)(2,1)S(1)} %collective-permute-done.33.one_ref, bf16[96,768]{1,0:T(8,128)(2,1)S(1)} %collective-permute-done.34.two_ref, bf16[96,768]{1,0:T(8,128)(2,1)S(1)} %collective-permute-done.35.three_ref), custom_call_target="tpu_custom_call" | custom-call | flops 1000 | bytes 1003 | tf_op jit(solution)/shard_map/spread/pallas_call | solution.py:744
  (72 shorter events, 4.6 us)
Async XLA Ops:
  2.7 15.2 %copy-start.2 = (bf16[768,768]{1,0:T(8,128)(2,1)S(1)}, bf16[768,768]{1,0:T(8,128)(2,1)}, u32[]{:S(2)}) copy-start(bf16[768,768]{1,0:T(8,128)(2,1)} %wout_ref.3) | copy-start | bytes 3538948
  2.7 15.2 %copy-start.5 = (bf16[1,1,1,256,768]{4,3,2,1,0:T(8,128)(2,1)S(1)}, bf16[1,1,1,256,768]{4,3,2,1,0:T(8,128)(2,1)}, u32[]{:S(2)}) copy-start(bf16[1,1,1,256,768]{4,3,2,1,0:T(8,128)(2,1)} %param.19) | copy-start | bytes 1179652
  3.7 10.1 %collective-permute-start = (bf16[40,768]{1,0:T(8,128)(2,1)S(1)}, bf16[40,768]{1,0:T(8,128)(2,1)S(1)}, u32[]{:S(2)}, u32[]{:S(2)}) collective-permute-start(bf16[40,768]{1,0:T(8,128)(2,1)S(1)} %get-tuple-element.106), channel_id=1, source_target_pairs={{0,4},{4,8},{8,12},{12,16},{16,20},{20,24},{24,28},{28,0},{1,5},{5... | collective-permute-start | bytes 184328 | tf_op jit(solution)/shard_map/ppermute | solution.py:511
  6.7 8.2 %collective-permute-start.1 = (bf16[40,768]{1,0:T(8,128)(2,1)S(1)}, bf16[40,768]{1,0:T(8,128)(2,1)S(1)}, u32[]{:S(2)}, u32[]{:S(2)}) collective-permute-start(bf16[40,768]{1,0:T(8,128)(2,1)S(1)} %get-tuple-element.107), channel_id=1, source_target_pairs={{0,8},{4,12},{8,16},{12,20},{16,24},{20,28},{24,0},{28,4},{1,9},{5... | collective-permute-start | bytes 184328 | tf_op jit(solution)/shard_map/ppermute | solution.py:511
  9.3 11.6 %collective-permute-start.2 = (bf16[40,768]{1,0:T(8,128)(2,1)S(1)}, bf16[40,768]{1,0:T(8,128)(2,1)S(1)}, u32[]{:S(2)}, u32[]{:S(2)}) collective-permute-start(bf16[40,768]{1,0:T(8,128)(2,1)S(1)} %get-tuple-element.108), channel_id=1, source_target_pairs={{0,12},{4,16},{8,20},{12,24},{16,28},{20,0},{24,4},{28,8},{1,13},{... | collective-permute-start | bytes 184328 | tf_op jit(solution)/shard_map/ppermute | solution.py:511
  11.6 11.0 %collective-permute-start.3 = (bf16[40,768]{1,0:T(8,128)(2,1)S(1)}, bf16[40,768]{1,0:T(8,128)(2,1)S(1)}, u32[]{:S(2)}, u32[]{:S(2)}) collective-permute-start(bf16[40,768]{1,0:T(8,128)(2,1)S(1)} %get-tuple-element.109), channel_id=1, source_target_pairs={{0,16},{4,20},{8,24},{12,28},{16,0},{20,4},{24,8},{28,12},{1,17},{... | collective-permute-start | bytes 184328 | tf_op jit(solution)/shard_map/ppermute | solution.py:511
  12.1 10.4 %collective-permute-start.4 = (bf16[40,768]{1,0:T(8,128)(2,1)S(1)}, bf16[40,768]{1,0:T(8,128)(2,1)S(1)}, u32[]{:S(2)}, u32[]{:S(2)}) collective-permute-start(bf16[40,768]{1,0:T(8,128)(2,1)S(1)} %get-tuple-element.110), channel_id=1, source_target_pairs={{0,20},{4,24},{8,28},{12,0},{16,4},{20,8},{24,12},{28,16},{1,21},{... | collective-permute-start | bytes 184328 | tf_op jit(solution)/shard_map/ppermute | solution.py:511
  13.7 8.8 %collective-permute-start.5 = (bf16[40,768]{1,0:T(8,128)(2,1)S(1)}, bf16[40,768]{1,0:T(8,128)(2,1)S(1)}, u32[]{:S(2)}, u32[]{:S(2)}) collective-permute-start(bf16[40,768]{1,0:T(8,128)(2,1)S(1)} %get-tuple-element.111), channel_id=1, source_target_pairs={{0,24},{4,28},{8,0},{12,4},{16,8},{20,12},{24,16},{28,20},{1,25},{... | collective-permute-start | bytes 184328 | tf_op jit(solution)/shard_map/ppermute | solution.py:511
  15.0 7.6 %collective-permute-start.6 = (bf16[40,768]{1,0:T(8,128)(2,1)S(1)}, bf16[40,768]{1,0:T(8,128)(2,1)S(1)}, u32[]{:S(2)}, u32[]{:S(2)}) collective-permute-start(bf16[40,768]{1,0:T(8,128)(2,1)S(1)} %get-tuple-element.112), channel_id=1, source_target_pairs={{0,28},{4,0},{8,4},{12,8},{16,12},{20,16},{24,20},{28,24},{1,29},{... | collective-permute-start | bytes 184328 | tf_op jit(solution)/shard_map/ppermute | solution.py:511
  18.0 2.0 %copy-start = (bf16[768,2304]{1,0:T(8,128)(2,1)S(1)}, bf16[768,2304]{1,0:T(8,128)(2,1)}, u32[]{:S(2)}) copy-start(bf16[768,2304]{1,0:T(8,128)(2,1)} %wqkv_ref.1) | copy-start | bytes 10616836
  20.0 2.6 %copy-start.12 = (s32[1,1,1,256]{3,2,1,0:T(1,128)S(1)}, s32[1,1,1,256]{3,2,1,0:T(1,128)}, u32[]{:S(2)}) copy-start(s32[1,1,1,256]{3,2,1,0:T(1,128)} %param.17) | copy-start | bytes 3076
  21.0 12.3 %collective-permute-start.8 = (bf16[256,768]{1,0:T(8,128)(2,1)S(1)}, bf16[256,768]{1,0:T(8,128)(2,1)S(1)}, u32[]{:S(2)}, u32[]{:S(2)}) collective-permute-start(bf16[256,768]{1,0:T(8,128)(2,1)S(1)} %bitcast.8), channel_id=1, source_target_pairs={{0,2},{1,3},{2,0},{3,1},{4,6},{5,7},{6,4},{7,5},{8,10},{9,11},{10,... | collective-permute-start | bytes 1179656 | tf_op jit(solution)/shard_map/ppermute | solution.py:451
  23.4 14.3 %collective-permute-start.9 = (bf16[512,768]{1,0:T(8,128)(2,1)S(1)}, bf16[512,768]{1,0:T(8,128)(2,1)S(1)}, u32[]{:S(2)}, u32[]{:S(2)}) collective-permute-start(bf16[512,768]{1,0:T(8,128)(2,1)S(1)} %get-tuple-element.177.refs_4_), channel_id=1, source_target_pairs={{0,1},{1,0},{2,3},{3,2},{4,5},{5,4},{6,7},{7,6},{8,9},{9,8},{10,11... | collective-permute-start | bytes 2359304 | tf_op jit(solution)/shard_map/ppermute | solution.py:451
  23.4 1.8 %copy-start.11 = (bf16[768,384]{1,0:T(8,128)(2,1)S(1)}, bf16[768,384]{1,0:T(8,128)(2,1)}, u32[]{:S(2)}) copy-start(bf16[768,384]{1,0:T(8,128)(2,1)} %wdec_ref.1) | copy-start | bytes 1769476
  24.6 13.0 %collective-permute-start.7 = (bf16[256,768]{1,0:T(8,128)(2,1)S(1)}, bf16[256,768]{1,0:T(8,128)(2,1)S(1)}, u32[]{:S(2)}, u32[]{:S(2)}) collective-permute-start(bf16[256,768]{1,0:T(8,128)(2,1)S(1)} %get-tuple-element.124.normed_ref), channel_id=1, source_target_pairs={{0,2},{1,3},{2,0},{3,1},{4,6},{5,7},{6,4},{7,5},{8,10},{9,11},{10,... | collective-permute-start | bytes 1179656 | tf_op jit(solution)/shard_map/ppermute | solution.py:451
  25.2 27.7 %copy-start.15 = (bf16[384]{0:T(512)(128)(2,1)S(1)}, bf16[384]{0:T(512)(128)(2,1)}, u32[]{:S(2)}) copy-start(bf16[384]{0:T(512)(128)(2,1)} %param.24) | copy-start | bytes 2308
  25.2 30.0 %copy-start.9 = (s32[1,1,1,8,35]{4,3,2,1,0:T(8,128)S(1)}, s32[1,1,1,8,35]{4,3,2,1,0:T(8,128)}, u32[]{:S(2)}) copy-start(s32[1,1,1,8,35]{4,3,2,1,0:T(8,128)} %param.16) | copy-start | bytes 3364
  25.3 30.0 %copy-start.10 = (f32[2,1408]{1,0:T(2,128)S(1)}, f32[2,1408]{1,0:T(2,128)}, u32[]{:S(2)}) copy-start(f32[2,1408]{1,0:T(2,128)} %constant.2.clone.ids_ref) | copy-start | bytes 33796
  37.7 2.4 %collective-permute-start.10 = (bf16[768,256]{1,0:T(8,128)(2,1)S(1)}, bf16[768,256]{1,0:T(8,128)(2,1)S(1)}, u32[]{:S(2)}, u32[]{:S(2)}) collective-permute-start(bf16[768,256]{1,0:T(8,128)(2,1)S(1)} %get-tuple-element.135), channel_id=1, source_target_pairs={{0,1},{1,0},{2,3},{3,2},{4,5},{5,4},{6,7},{7,6},{8,9},{9,8},{10,11... | collective-permute-start | bytes 1179656 | tf_op jit(solution)/shard_map/ppermute | solution.py:451
  37.7 2.4 %collective-permute-start.13 = (bf16[256,768]{1,0:T(8,128)(2,1)S(1)}, bf16[256,768]{1,0:T(8,128)(2,1)S(1)}, u32[]{:S(2)}, u32[]{:S(2)}) collective-permute-start(bf16[256,768]{1,0:T(8,128)(2,1)S(1)} %collective-permute-done.7.refs_6_), channel_id=1, source_target_pairs={{0,1},{1,0},{2,3},{3,2},{4,5},{5,4},{6,7},{7,6},{8,9},{9,8},{10,11... | collective-permute-start | bytes 1179656 | tf_op jit(solution)/shard_map/ppermute | solution.py:451
  38.2 2.3 %collective-permute-start.14 = (bf16[256,768]{1,0:T(8,128)(2,1)S(1)}, bf16[256,768]{1,0:T(8,128)(2,1)S(1)}, u32[]{:S(2)}, u32[]{:S(2)}) collective-permute-start(bf16[256,768]{1,0:T(8,128)(2,1)S(1)} %collective-permute-done.8.refs_8_), channel_id=1, source_target_pairs={{0,1},{1,0},{2,3},{3,2},{4,5},{5,4},{6,7},{7,6},{8,9},{9,8},{10,11... | collective-permute-start | bytes 1179656 | tf_op jit(solution)/shard_map/ppermute | solution.py:451
  38.2 26.1 %collective-permute-start.11 = (bf16[768,256]{1,0:T(8,128)(2,1)S(1)}, bf16[768,256]{1,0:T(8,128)(2,1)S(1)}, u32[]{:S(2)}, u32[]{:S(2)}) collective-permute-start(bf16[768,256]{1,0:T(8,128)(2,1)S(1)} %get-tuple-element.136), channel_id=1, source_target_pairs={{0,2},{1,3},{2,0},{3,1},{4,6},{5,7},{6,4},{7,5},{8,10},{9,11},{10,... | collective-permute-start | bytes 1179656 | tf_op jit(solution)/shard_map/ppermute | solution.py:451
  39.7 24.6 %collective-permute-start.12 = (bf16[768,256]{1,0:T(8,128)(2,1)S(1)}, bf16[768,256]{1,0:T(8,128)(2,1)S(1)}, u32[]{:S(2)}, u32[]{:S(2)}) collective-permute-start(bf16[768,256]{1,0:T(8,128)(2,1)S(1)} %get-tuple-element.137), channel_id=1, source_target_pairs={{0,3},{1,2},{2,1},{3,0},{4,7},{5,6},{6,5},{7,4},{8,11},{9,10},{10,... | collective-permute-start | bytes 1179656 | tf_op jit(solution)/shard_map/ppermute | solution.py:451
  40.5 6.9 %collective-permute-start.15 = (bf16[40,384]{1,0:T(8,128)(2,1)S(1)}, bf16[40,384]{1,0:T(8,128)(2,1)S(1)}, u32[]{:S(2)}, u32[]{:S(2)}) collective-permute-start(bf16[40,384]{1,0:T(8,128)(2,1)S(1)} %get-tuple-element.150), channel_id=1, source_target_pairs={{0,4},{4,8},{8,12},{12,16},{16,20},{20,24},{24,28},{28,0},{1,5},{5... | collective-permute-start | bytes 92168 | tf_op jit(solution)/shard_map/ppermute | solution.py:599
  41.1 6.7 %collective-permute-start.16 = (bf16[40,384]{1,0:T(8,128)(2,1)S(1)}, bf16[40,384]{1,0:T(8,128)(2,1)S(1)}, u32[]{:S(2)}, u32[]{:S(2)}) collective-permute-start(bf16[40,384]{1,0:T(8,128)(2,1)S(1)} %get-tuple-element.151), channel_id=1, source_target_pairs={{0,8},{4,12},{8,16},{12,20},{16,24},{20,28},{24,0},{28,4},{1,9},{5... | collective-permute-start | bytes 92168 | tf_op jit(solution)/shard_map/ppermute | solution.py:599
  42.2 6.4 %collective-permute-start.17 = (bf16[40,384]{1,0:T(8,128)(2,1)S(1)}, bf16[40,384]{1,0:T(8,128)(2,1)S(1)}, u32[]{:S(2)}, u32[]{:S(2)}) collective-permute-start(bf16[40,384]{1,0:T(8,128)(2,1)S(1)} %get-tuple-element.152), channel_id=1, source_target_pairs={{0,12},{4,16},{8,20},{12,24},{16,28},{20,0},{24,4},{28,8},{1,13},{... | collective-permute-start | bytes 92168 | tf_op jit(solution)/shard_map/ppermute | solution.py:599
  47.4 3.9 %collective-permute-start.18 = (bf16[40,384]{1,0:T(8,128)(2,1)S(1)}, bf16[40,384]{1,0:T(8,128)(2,1)S(1)}, u32[]{:S(2)}, u32[]{:S(2)}) collective-permute-start(bf16[40,384]{1,0:T(8,128)(2,1)S(1)} %get-tuple-element.153), channel_id=1, source_target_pairs={{0,16},{4,20},{8,24},{12,28},{16,0},{20,4},{24,8},{28,12},{1,17},{... | collective-permute-start | bytes 92168 | tf_op jit(solution)/shard_map/ppermute | solution.py:599
  47.8 5.8 %collective-permute-start.19 = (bf16[40,384]{1,0:T(8,128)(2,1)S(1)}, bf16[40,384]{1,0:T(8,128)(2,1)S(1)}, u32[]{:S(2)}, u32[]{:S(2)}) collective-permute-start(bf16[40,384]{1,0:T(8,128)(2,1)S(1)} %get-tuple-element.154), channel_id=1, source_target_pairs={{0,20},{4,24},{8,28},{12,0},{16,4},{20,8},{24,12},{28,16},{1,21},{... | collective-permute-start | bytes 92168 | tf_op jit(solution)/shard_map/ppermute | solution.py:599
  48.6 5.7 %collective-permute-start.20 = (bf16[40,384]{1,0:T(8,128)(2,1)S(1)}, bf16[40,384]{1,0:T(8,128)(2,1)S(1)}, u32[]{:S(2)}, u32[]{:S(2)}) collective-permute-start(bf16[40,384]{1,0:T(8,128)(2,1)S(1)} %get-tuple-element.155), channel_id=1, source_target_pairs={{0,24},{4,28},{8,0},{12,4},{16,8},{20,12},{24,16},{28,20},{1,25},{... | collective-permute-start | bytes 92168 | tf_op jit(solution)/shard_map/ppermute | solution.py:599
  51.3 3.9 %collective-permute-start.21 = (bf16[40,384]{1,0:T(8,128)(2,1)S(1)}, bf16[40,384]{1,0:T(8,128)(2,1)S(1)}, u32[]{:S(2)}, u32[]{:S(2)}) collective-permute-start(bf16[40,384]{1,0:T(8,128)(2,1)S(1)} %get-tuple-element.156), channel_id=1, source_target_pairs={{0,28},{4,0},{8,4},{12,8},{16,12},{20,16},{24,20},{28,24},{1,29},{... | collective-permute-start | bytes 92168 | tf_op jit(solution)/shard_map/ppermute | solution.py:599
  56.7 6.3 %collective-permute-start.22 = (bf16[96,384]{1,0:T(8,128)(2,1)S(1)}, bf16[96,384]{1,0:T(8,128)(2,1)S(1)}, u32[]{:S(2)}, u32[]{:S(2)}) collective-permute-start(bf16[96,384]{1,0:T(8,128)(2,1)S(1)} %get-tuple-element.157), channel_id=1, source_target_pairs={{0,4},{4,8},{8,12},{12,0},{1,5},{5,9},{9,13},{13,1},{2,6},{6,10},{... | collective-permute-start | bytes 221192 | tf_op jit(solution)/shard_map/ppermute | solution.py:456
  58.7 5.0 %collective-permute-start.23 = (bf16[96,384]{1,0:T(8,128)(2,1)S(1)}, bf16[96,384]{1,0:T(8,128)(2,1)S(1)}, u32[]{:S(2)}, u32[]{:S(2)}) collective-permute-start(bf16[96,384]{1,0:T(8,128)(2,1)S(1)} %get-tuple-element.158), channel_id=1, source_target_pairs={{0,12},{4,0},{8,4},{12,8},{1,13},{5,1},{9,5},{13,9},{2,14},{6,2},{... | collective-permute-start | bytes 221192 | tf_op jit(solution)/shard_map/ppermute | solution.py:456
  63.7 5.6 %collective-permute-start.25 = (bf16[128,384]{1,0:T(8,128)(2,1)S(1)}, bf16[128,384]{1,0:T(8,128)(2,1)S(1)}, u32[]{:S(2)}, u32[]{:S(2)}) collective-permute-start(bf16[128,384]{1,0:T(8,128)(2,1)S(1)} %rim.1), channel_id=1, source_target_pairs={{0,16},{16,0},{1,17},{17,1},{2,18},{18,2},{3,19},{19,3},{4,20},{20... | collective-permute-start | bytes 294920 | tf_op jit(solution)/shard_map/ppermute | solution.py:456
  65.4 5.8 %copy-start.7 = (f32[7,7,384]{2,1,0:T(8,128)S(1)}, f32[7,7,384]{2,1,0:T(8,128)}, u32[]{:S(2)}) copy-start(f32[7,7,384]{2,1,0:T(8,128)} %refs_0_.1) | copy-start | bytes 225796
  65.4 13.3 %collective-permute-start.24 = (bf16[4,96,384]{2,1,0:T(8,128)(2,1)S(1)}, bf16[4,96,384]{2,1,0:T(8,128)(2,1)S(1)}, u32[]{:S(2)}, u32[]{:S(2)}) collective-permute-start(bf16[4,96,384]{2,1,0:T(8,128)(2,1)S(1)} %get-tuple-element.171), channel_id=1, source_target_pairs={{0,16},{16,0},{1,17},{17,1},{2,18},{18,2},{3,19},{19,3},{4,20},{20... | collective-permute-start | bytes 884744 | tf_op jit(solution)/shard_map/ppermute | solution.py:456
  70.4 13.7 %collective-permute-start.29 = (bf16[4,96,384]{2,1,0:T(8,128)(2,1)S(1)}, bf16[4,96,384]{2,1,0:T(8,128)(2,1)S(1)}, u32[]{:S(2)}, u32[]{:S(2)}) collective-permute-start(bf16[4,96,384]{2,1,0:T(8,128)(2,1)S(1)} %get-tuple-element.192), channel_id=1, source_target_pairs={{0,16},{16,0},{1,17},{17,1},{2,18},{18,2},{3,19},{19,3},{4,20},{20... | collective-permute-start | bytes 884744 | tf_op jit(solution)/shard_map/ppermute | solution.py:456
  71.2 16.8 %copy-start.3 = (bf16[384,768]{1,0:T(8,128)(2,1)S(1)}, bf16[384,768]{1,0:T(8,128)(2,1)}, u32[]{:S(2)}) copy-start(bf16[384,768]{1,0:T(8,128)(2,1)} %up_ref.1) | copy-start | bytes 1769476
  71.2 16.8 %copy-start.4 = (bf16[768,384]{1,0:T(8,128)(2,1)S(1)}, bf16[768,384]{1,0:T(8,128)(2,1)}, u32[]{:S(2)}) copy-start(bf16[768,384]{1,0:T(8,128)(2,1)} %down_ref.1) | copy-start | bytes 1769476
  71.2 16.8 %copy-start.6 = (bf16[384,128]{1,0:T(8,128)(2,1)S(1)}, bf16[384,128]{1,0:T(8,128)(2,1)}, u32[]{:S(2)}) copy-start(bf16[384,128]{1,0:T(8,128)(2,1)} %head_ref.1) | copy-start | bytes 294916
  78.7 6.6 %collective-permute-start.26 = (bf16[96,384]{1,0:T(8,128)(2,1)S(1)}, bf16[96,384]{1,0:T(8,128)(2,1)S(1)}, u32[]{:S(2)}, u32[]{:S(2)}) collective-permute-start(bf16[96,384]{1,0:T(8,128)(2,1)S(1)} %get-tuple-element.189), channel_id=1, source_target_pairs={{0,4},{4,8},{8,12},{12,0},{1,5},{5,9},{9,13},{13,1},{2,6},{6,10},{... | collective-permute-start | bytes 221192 | tf_op jit(solution)/shard_map/ppermute | solution.py:456
  79.9 11.5 %collective-permute-start.27 = (bf16[96,384]{1,0:T(8,128)(2,1)S(1)}, bf16[96,384]{1,0:T(8,128)(2,1)S(1)}, u32[]{:S(2)}, u32[]{:S(2)}) collective-permute-start(bf16[96,384]{1,0:T(8,128)(2,1)S(1)} %get-tuple-element.190), channel_id=1, source_target_pairs={{0,8},{4,12},{8,0},{12,4},{1,9},{5,13},{9,1},{13,5},{2,10},{6,14},... | collective-permute-start | bytes 221192 | tf_op jit(solution)/shard_map/ppermute | solution.py:456
  83.2 8.2 %collective-permute-start.28 = (bf16[96,384]{1,0:T(8,128)(2,1)S(1)}, bf16[96,384]{1,0:T(8,128)(2,1)S(1)}, u32[]{:S(2)}, u32[]{:S(2)}) collective-permute-start(bf16[96,384]{1,0:T(8,128)(2,1)S(1)} %get-tuple-element.191), channel_id=1, source_target_pairs={{0,12},{4,0},{8,4},{12,8},{1,13},{5,1},{9,5},{13,9},{2,14},{6,2},{... | collective-permute-start | bytes 221192 | tf_op jit(solution)/shard_map/ppermute | solution.py:456
  84.1 7.3 %collective-permute-start.30 = (bf16[96,384]{1,0:T(8,128)(2,1)S(1)}, bf16[96,384]{1,0:T(8,128)(2,1)S(1)}, u32[]{:S(2)}, u32[]{:S(2)}) collective-permute-start(bf16[96,384]{1,0:T(8,128)(2,1)S(1)} %get-tuple-element.196), channel_id=1, source_target_pairs={{0,4},{4,8},{8,12},{12,0},{1,5},{5,9},{9,13},{13,1},{2,6},{6,10},{... | collective-permute-start | bytes 221192 | tf_op jit(solution)/shard_map/ppermute | solution.py:456
  85.3 6.6 %collective-permute-start.31 = (bf16[96,384]{1,0:T(8,128)(2,1)S(1)}, bf16[96,384]{1,0:T(8,128)(2,1)S(1)}, u32[]{:S(2)}, u32[]{:S(2)}) collective-permute-start(bf16[96,384]{1,0:T(8,128)(2,1)S(1)} %get-tuple-element.197), channel_id=1, source_target_pairs={{0,8},{4,12},{8,0},{12,4},{1,9},{5,13},{9,1},{13,5},{2,10},{6,14},... | collective-permute-start | bytes 221192 | tf_op jit(solution)/shard_map/ppermute | solution.py:456
  85.3 6.6 %collective-permute-start.32 = (bf16[96,384]{1,0:T(8,128)(2,1)S(1)}, bf16[96,384]{1,0:T(8,128)(2,1)S(1)}, u32[]{:S(2)}, u32[]{:S(2)}) collective-permute-start(bf16[96,384]{1,0:T(8,128)(2,1)S(1)} %get-tuple-element.198), channel_id=1, source_target_pairs={{0,12},{4,0},{8,4},{12,8},{1,13},{5,1},{9,5},{13,9},{2,14},{6,2},{... | collective-permute-start | bytes 221192 | tf_op jit(solution)/shard_map/ppermute | solution.py:456
  92.0 5.2 %collective-permute-start.34 = (bf16[96,768]{1,0:T(8,128)(2,1)S(1)}, bf16[96,768]{1,0:T(8,128)(2,1)S(1)}, u32[]{:S(2)}, u32[]{:S(2)}) collective-permute-start(bf16[96,768]{1,0:T(8,128)(2,1)S(1)} %close.1.own_ref), channel_id=1, source_target_pairs={{0,2},{1,3},{2,0},{3,1},{4,6},{5,7},{6,4},{7,5},{8,10},{9,11},{10,... | collective-permute-start | bytes 442376 | tf_op jit(solution)/shard_map/ppermute | solution.py:451
  93.6 3.6 %collective-permute-start.33 = (bf16[96,768]{1,0:T(8,128)(2,1)S(1)}, bf16[96,768]{1,0:T(8,128)(2,1)S(1)}, u32[]{:S(2)}, u32[]{:S(2)}) collective-permute-start(bf16[96,768]{1,0:T(8,128)(2,1)S(1)} %close.1.own_ref), channel_id=1, source_target_pairs={{0,1},{1,0},{2,3},{3,2},{4,5},{5,4},{6,7},{7,6},{8,9},{9,8},{10,11... | collective-permute-start | bytes 442376 | tf_op jit(solution)/shard_map/ppermute | solution.py:451
  97.2 1.4 %collective-permute-start.35 = (bf16[96,768]{1,0:T(8,128)(2,1)S(1)}, bf16[96,768]{1,0:T(8,128)(2,1)S(1)}, u32[]{:S(2)}, u32[]{:S(2)}) collective-permute-start(bf16[96,768]{1,0:T(8,128)(2,1)S(1)} %collective-permute-done.34.two_ref), channel_id=1, source_target_pairs={{0,1},{1,0},{2,3},{3,2},{4,5},{5,4},{6,7},{7,6},{8,9},{9,8},{10,11... | collective-permute-start | bytes 442376 | tf_op jit(solution)/shard_map/ppermute | solution.py:451
  (4 other events, 5.6 us)

commit v12 on v11

--- a/solution.py
+++ b/solution.py
@@ -504,6 +504,11 @@
         nbytes=3 * MIB,
         limit=8,
     )(positions, tokens.reshape(tile_len, width))
+    cotangent = enc_cot.reshape(rows, width)
+    if fast:
+        cot_y = flip(cotangent, "replica", 2)
+        outgoing = list(outgoing)
+        outgoing[-2:] = tie(outgoing[-2:], cot_y)
     if turned:
         arrived = [outgoing[0]]
         for k in range(1, group):
@@ -531,8 +536,6 @@
         nbytes=10 * MIB,
         limit=10,
     )(cotangent, w_out, w_qkv)
-    if fast:
-        cot_y = flip(cotangent, "replica", 2)
     arrived = tie(arrived, w_qkv_t)
 
     both, normed, enc_in, places = call(

time: 100 us -> 99.3 us (level)
  waiting for transfers between devices: 20.7 us -> 17 us
  starting transfers between devices: 46.4 us -> 49.4 us
    ppermute x11, starting transfers between devices: 6.2 us -> 8.65 us  [flip(): lax.ppermute(value, axis, [(i, i ^ bit) for i in range(lax.axis_size(axis...]
    ppermute x11, waiting for transfers between devices: 9.86 us -> 7.42 us  [flip(): lax.ppermute(value, axis, [(i, i ^ bit) for i in range(lax.axis_size(axis...]
    ppermute x7, starting transfers between devices: 14.3 us -> 12.9 us  [body(): arrived.append(lax.ppermute(outgoing[k], ('eta', 'phi'), pairs))]
    ppermute x11, starting transfers between devices: 16 us -> 17.2 us  [turn(): lax.ppermute(value, axis, [(i, (i + k) % count) for i in range(count)])]
  transfers between devices with their start and end apart: 36 -> 36, of which waited for: 13 -> 12; matrix products, arithmetic and copies ran while one was open for 0% -> 0% of each run, Pallas kernels for 26% -> 26%
where the time goes in v12:
time: 99.3 us; the launch traced here: 99.1 us
  starting transfers between devices  49.4 us (50%)
  Pallas kernels  27.6 us (28%)
  waiting for transfers between devices  17 us (17%)
  local copies, waits for them, and re-layouts  4.16 us (4%)
    ppermute x11, starting transfers between devices, turn(): lax.ppermute(value, axis, [(i, (i + k) % count) for i in range(count)])  17.2 us
    ppermute x7, starting transfers between devices, body(): arrived.append(lax.ppermute(outgoing[k], ('eta', 'phi'), pairs))  12.9 us
    ppermute x7, starting transfers between devices, body(): returned.append(lax.ppermute(outbound[k], ('eta', 'phi'), pairs))  10.7 us
    ppermute x11, starting transfers between devices, flip(): lax.ppermute(value, axis, [(i, i ^ bit) for i in range(lax.axis_size(axis...  8.65 us
    pallas_call x1, Pallas kernels, body(): call(functools.partial(encode_kernel, split, sends), 'encode', [sds((slot...  7.97 us
    pallas_call x1, Pallas kernels, body(): call(functools.partial(mix_folded if folded else mix_open, (eta_cells, ph...  7.46 us
    ppermute x11, waiting for transfers between devices, flip(): lax.ppermute(value, axis, [(i, i ^ bit) for i in range(lax.axis_size(axis...  7.42 us
    ppermute x11, waiting for transfers between devices, turn(): lax.ppermute(value, axis, [(i, (i + k) % count) for i in range(count)])  5.26 us
  transfers between devices with their start and end apart: 36, of which 12 were waited for; matrix products, arithmetic and copies ran while one was open for 0% of the time, Pallas kernels for 26%

profile of v12, /device:TPU:0, one launch (start us, length us, event | category | flops | bytes accessed | tf_op | source)
XLA Modules:
  0.0 99.1 jit_solution(5648888075389107481)
XLA Ops:
  0.6 3.0 %collective-permute-start.5 = (bf16[256,768]{1,0:T(8,128)(2,1)}, bf16[256,768]{1,0:T(8,128)(2,1)S(1)}, u32[]{:S(2)}, u32[]{:S(2)}) collective-permute-start(bf16[256,768]{1,0:T(8,128)(2,1)} %bitcast.7), channel_id=1, source_target_pairs={{0,2},{1,3},{2,0},{3,1},{4,6},{5,7},{6,4},{7,5},{8,10},{9,11},{10,... | collective-permute-start | bytes 1179656 | tf_op jit(solution)/shard_map/ppermute | solution.py:451
  3.7 1.4 %copy-done.1 = bf16[1,32,32,768]{3,2,1,0:T(8,128)(2,1)S(1)} copy-done((bf16[1,32,32,768]{3,2,1,0:T(8,128)(2,1)S(1)}, bf16[1,32,32,768]{3,2,1,0:T(8,128)(2,1)}, u32[]{:S(2)}) %copy-start.1) | copy-done | bytes 1572888
  5.1 0.7 copy-done.8
  5.8 0.9 pick.1
  6.7 1.6 %collective-permute-start = (bf16[40,768]{1,0:T(8,128)(2,1)S(1)}, bf16[40,768]{1,0:T(8,128)(2,1)S(1)}, u32[]{:S(2)}, u32[]{:S(2)}) collective-permute-start(bf16[40,768]{1,0:T(8,128)(2,1)S(1)} %get-tuple-element.108), channel_id=1, source_target_pairs={{0,4},{4,8},{8,12},{12,16},{16,20},{20,24},{24,28},{28,0},{1,5},{5... | collective-permute-start | bytes 184328 | tf_op jit(solution)/shard_map/ppermute | solution.py:516
  8.3 2.6 %collective-permute-start.1 = (bf16[40,768]{1,0:T(8,128)(2,1)S(1)}, bf16[40,768]{1,0:T(8,128)(2,1)S(1)}, u32[]{:S(2)}, u32[]{:S(2)}) collective-permute-start(bf16[40,768]{1,0:T(8,128)(2,1)S(1)} %get-tuple-element.109), channel_id=1, source_target_pairs={{0,8},{4,12},{8,16},{12,20},{16,24},{20,28},{24,0},{28,4},{1,9},{5... | collective-permute-start | bytes 184328 | tf_op jit(solution)/shard_map/ppermute | solution.py:516
  10.9 2.3 %collective-permute-start.2 = (bf16[40,768]{1,0:T(8,128)(2,1)S(1)}, bf16[40,768]{1,0:T(8,128)(2,1)S(1)}, u32[]{:S(2)}, u32[]{:S(2)}) collective-permute-start(bf16[40,768]{1,0:T(8,128)(2,1)S(1)} %get-tuple-element.110), channel_id=1, source_target_pairs={{0,12},{4,16},{8,20},{12,24},{16,28},{20,0},{24,4},{28,8},{1,13},{... | collective-permute-start | bytes 184328 | tf_op jit(solution)/shard_map/ppermute | solution.py:516
  13.2 0.5 collective-permute-start.3
  13.7 2.0 %collective-permute-start.4 = (bf16[40,768]{1,0:T(8,128)(2,1)S(1)}, bf16[40,768]{1,0:T(8,128)(2,1)S(1)}, u32[]{:S(2)}, u32[]{:S(2)}) collective-permute-start(bf16[40,768]{1,0:T(8,128)(2,1)S(1)} %get-tuple-element.112), channel_id=1, source_target_pairs={{0,20},{4,24},{8,28},{12,0},{16,4},{20,8},{24,12},{28,16},{1,21},{... | collective-permute-start | bytes 184328 | tf_op jit(solution)/shard_map/ppermute | solution.py:516
  15.7 2.6 %collective-permute-start.6 = (bf16[40,768]{1,0:T(8,128)(2,1)S(1)}, bf16[40,768]{1,0:T(8,128)(2,1)S(1)}, u32[]{:S(2)}, u32[]{:S(2)}) collective-permute-start(bf16[40,768]{1,0:T(8,128)(2,1)S(1)} %get-tuple-element.115), channel_id=1, source_target_pairs={{0,24},{4,28},{8,0},{12,4},{16,8},{20,12},{24,16},{28,20},{1,25},{... | collective-permute-start | bytes 184328 | tf_op jit(solution)/shard_map/ppermute | solution.py:516
  18.3 1.3 %collective-permute-start.7 = (bf16[40,768]{1,0:T(8,128)(2,1)S(1)}, bf16[40,768]{1,0:T(8,128)(2,1)S(1)}, u32[]{:S(2)}, u32[]{:S(2)}) collective-permute-start(bf16[40,768]{1,0:T(8,128)(2,1)S(1)} %get-tuple-element.116), channel_id=1, source_target_pairs={{0,28},{4,0},{8,4},{12,8},{16,12},{20,16},{24,20},{28,24},{1,29},{... | collective-permute-start | bytes 184328 | tf_op jit(solution)/shard_map/ppermute | solution.py:516
  19.6 2.0 %copy-done = bf16[768,2304]{1,0:T(8,128)(2,1)S(1)} copy-done((bf16[768,2304]{1,0:T(8,128)(2,1)S(1)}, bf16[768,2304]{1,0:T(8,128)(2,1)}, u32[]{:S(2)}) %copy-start) | copy-done | bytes 3538968
  21.6 1.0 %prep.1 = (bf16[768,256]{1,0:T(8,128)(2,1)S(1)}, bf16[2304,768]{1,0:T(8,128)(2,1)S(1)}) custom-call(bf16[256,768]{1,0:T(8,128)(2,1)S(1)} %bitcast.8, bf16[768,768]{1,0:T(8,128)(2,1)S(1)} %copy-done.2, bf16[768,2304]{1,0:T(8,128)(2,1)S(1)} %copy-done), custom_call_target="tpu_custom_call" | custom-call | flops 1000 | bytes 1003 | tf_op jit(solution)/shard_map/prep/pallas_call | solution.py:530
  22.7 0.8 norm.1
  23.6 1.1 %project.1 = (f32[1536,256]{1,0:T(8,128)S(1)}, f32[24,256]{1,0:T(8,128)S(1)}, bf16[768,256]{1,0:T(8,128)(2,1)S(1)}) custom-call(bf16[256,768]{1,0:T(8,128)(2,1)S(1)} %get-tuple-element.128.normed_ref, bf16[2304,768]{1,0:T(8,128)(2,1)S(1)} %get-tuple-element.117.wqkv_t_ref), custom_call_target="tpu_custom_call" | custom-call | flops 2000000000 | bytes 6667666 | tf_op jit(solution)/shard_map/project/pallas_call | solution.py:554
  24.8 1.6 %collective-permute-start.8 = (bf16[256,768]{1,0:T(8,128)(2,1)S(1)}, bf16[256,768]{1,0:T(8,128)(2,1)S(1)}, u32[]{:S(2)}, u32[]{:S(2)}) collective-permute-start(bf16[256,768]{1,0:T(8,128)(2,1)S(1)} %get-tuple-element.128.normed_ref), channel_id=1, source_target_pairs={{0,2},{1,3},{2,0},{3,1},{4,6},{5,7},{6,4},{7,5},{8,10},{9,11},{10,... | collective-permute-start | bytes 1179656 | tf_op jit(solution)/shard_map/ppermute | solution.py:451
  26.4 8.0 %encode.1 = (bf16[40,384]{1,0:T(8,128)(2,1)S(1)}, bf16[40,384]{1,0:T(8,128)(2,1)S(1)}, bf16[40,384]{1,0:T(8,128)(2,1)S(1)}, bf16[40,384]{1,0:T(8,128)(2,1)S(1)},...) custom-call(s32[1,256]{1,0:T(1,128)S(1)} %bitcast.13, ...), custom_call_target="tpu_custom_call" | custom-call | flops 8000000000 | bytes 26667666 | tf_op jit(solution)/shard_map/encode/pallas_call | solution.py:566
  34.4 1.9 %collective-permute-done.8.refs_6_ = bf16[256,768]{1,0:T(8,128)(2,1)S(1)} collective-permute-done((bf16[256,768]{1,0:T(8,128)(2,1)S(1)}, bf16[256,768]{1,0:T(8,128)(2,1)S(1)}, u32[]{:S(2)}, u32[]{:S(2)}) %collective-permute-start.8) | collective-permute-done | bytes 393248 | tf_op jit(solution)/shard_map/ppermute | solution.py:451
  36.3 0.5 collective-permute-start.13
  36.8 1.5 %collective-permute-start.11 = (bf16[768,256]{1,0:T(8,128)(2,1)S(1)}, bf16[768,256]{1,0:T(8,128)(2,1)S(1)}, u32[]{:S(2)}, u32[]{:S(2)}) collective-permute-start(bf16[768,256]{1,0:T(8,128)(2,1)S(1)} %get-tuple-element.140), channel_id=1, source_target_pairs={{0,2},{1,3},{2,0},{3,1},{4,6},{5,7},{6,4},{7,5},{8,10},{9,11},{10,... | collective-permute-start | bytes 1179656 | tf_op jit(solution)/shard_map/ppermute | solution.py:451
  39.2 0.7 collective-permute-start.15
  39.9 3.7 %collective-permute-start.16 = (bf16[40,384]{1,0:T(8,128)(2,1)S(1)}, bf16[40,384]{1,0:T(8,128)(2,1)S(1)}, u32[]{:S(2)}, u32[]{:S(2)}) collective-permute-start(bf16[40,384]{1,0:T(8,128)(2,1)S(1)} %get-tuple-element.155), channel_id=1, source_target_pairs={{0,8},{4,12},{8,16},{12,20},{16,24},{20,28},{24,0},{28,4},{1,9},{5... | collective-permute-start | bytes 92168 | tf_op jit(solution)/shard_map/ppermute | solution.py:602
  43.9 1.9 %collective-permute-done.15.refs_1_ = bf16[40,384]{1,0:T(8,128)(2,1)S(1)} collective-permute-done((bf16[40,384]{1,0:T(8,128)(2,1)S(1)}, bf16[40,384]{1,0:T(8,128)(2,1)S(1)}, u32[]{:S(2)}, u32[]{:S(2)}) %collective-permute-start.15) | collective-permute-done | bytes 30752 | tf_op jit(solution)/shard_map/ppermute | solution.py:602
  45.8 1.8 %collective-permute-start.18 = (bf16[40,384]{1,0:T(8,128)(2,1)S(1)}, bf16[40,384]{1,0:T(8,128)(2,1)S(1)}, u32[]{:S(2)}, u32[]{:S(2)}) collective-permute-start(bf16[40,384]{1,0:T(8,128)(2,1)S(1)} %get-tuple-element.157), channel_id=1, source_target_pairs={{0,16},{4,20},{8,24},{12,28},{16,0},{20,4},{24,8},{28,12},{1,17},{... | collective-permute-start | bytes 92168 | tf_op jit(solution)/shard_map/ppermute | solution.py:602
  48.4 1.9 %collective-permute-start.20 = (bf16[40,384]{1,0:T(8,128)(2,1)S(1)}, bf16[40,384]{1,0:T(8,128)(2,1)S(1)}, u32[]{:S(2)}, u32[]{:S(2)}) collective-permute-start(bf16[40,384]{1,0:T(8,128)(2,1)S(1)} %get-tuple-element.159), channel_id=1, source_target_pairs={{0,24},{4,28},{8,0},{12,4},{16,8},{20,12},{24,16},{28,20},{1,25},{... | collective-permute-start | bytes 92168 | tf_op jit(solution)/shard_map/ppermute | solution.py:602
  50.3 1.9 %collective-permute-start.21 = (bf16[40,384]{1,0:T(8,128)(2,1)S(1)}, bf16[40,384]{1,0:T(8,128)(2,1)S(1)}, u32[]{:S(2)}, u32[]{:S(2)}) collective-permute-start(bf16[40,384]{1,0:T(8,128)(2,1)S(1)} %get-tuple-element.160), channel_id=1, source_target_pairs={{0,28},{4,0},{8,4},{12,8},{16,12},{20,16},{24,20},{28,24},{1,29},{... | collective-permute-start | bytes 92168 | tf_op jit(solution)/shard_map/ppermute | solution.py:602
  52.2 1.1 %collective-permute-done.19.refs_5_ = bf16[40,384]{1,0:T(8,128)(2,1)S(1)} collective-permute-done((bf16[40,384]{1,0:T(8,128)(2,1)S(1)}, bf16[40,384]{1,0:T(8,128)(2,1)S(1)}, u32[]{:S(2)}, u32[]{:S(2)}) %collective-permute-start.19) | collective-permute-done | bytes 30752 | tf_op jit(solution)/shard_map/ppermute | solution.py:602
  54.2 1.5 %fill.1 = (bf16[1024,384]{1,0:T(8,128)(2,1)S(1)}, bf16[96,384]{1,0:T(8,128)(2,1)S(1)}, bf16[96,384]{1,0:T(8,128)(2,1)S(1)}, bf16[96,384]{1,0:T(8,128)(2,1)S(1)}) custom-call(s32[8,35]{1,0:T(8,128)S(1)} %bitcast.11, f32[2,1408]{1,0:T(2,128)S(1)} %copy-done.10, bf16[1,384]{1,0:T(2,128)(2,1)S(1)} %reshape.31.mask_ref, ...), custom_call_target="tpu_custom_call" | custom-call | flops 1000 | bytes 1003 | tf_op jit(solution)/shard_map/fill/pallas_call | solution.py:631
  55.7 1.4 %collective-permute-start.22 = (bf16[96,384]{1,0:T(8,128)(2,1)S(1)}, bf16[96,384]{1,0:T(8,128)(2,1)S(1)}, u32[]{:S(2)}, u32[]{:S(2)}) collective-permute-start(bf16[96,384]{1,0:T(8,128)(2,1)S(1)} %get-tuple-element.161), channel_id=1, source_target_pairs={{0,4},{4,8},{8,12},{12,0},{1,5},{5,9},{9,13},{13,1},{2,6},{6,10},{... | collective-permute-start | bytes 221192 | tf_op jit(solution)/shard_map/ppermute | solution.py:456
  57.1 3.0 %collective-permute-start.23 = (bf16[96,384]{1,0:T(8,128)(2,1)S(1)}, bf16[96,384]{1,0:T(8,128)(2,1)S(1)}, u32[]{:S(2)}, u32[]{:S(2)}) collective-permute-start(bf16[96,384]{1,0:T(8,128)(2,1)S(1)} %get-tuple-element.162), channel_id=1, source_target_pairs={{0,12},{4,0},{8,4},{12,8},{1,13},{5,1},{9,5},{13,9},{2,14},{6,2},{... | collective-permute-start | bytes 221192 | tf_op jit(solution)/shard_map/ppermute | solution.py:456
  60.0 2.2 %collective-permute-done.22.left_ref.left = bf16[96,384]{1,0:T(8,128)(2,1)S(1)} collective-permute-done((bf16[96,384]{1,0:T(8,128)(2,1)S(1)}, bf16[96,384]{1,0:T(8,128)(2,1)S(1)}, u32[]{:S(2)}, u32[]{:S(2)}) %collective-permute-start.22) | collective-permute-done | bytes 73760 | tf_op jit(solution)/shard_map/ppermute | solution.py:456
  62.2 1.9 %collective-permute-start.25 = (bf16[128,384]{1,0:T(8,128)(2,1)S(1)}, bf16[128,384]{1,0:T(8,128)(2,1)S(1)}, u32[]{:S(2)}, u32[]{:S(2)}) collective-permute-start(bf16[128,384]{1,0:T(8,128)(2,1)S(1)} %rim.1), channel_id=1, source_target_pairs={{0,16},{16,0},{1,17},{17,1},{2,18},{18,2},{3,19},{19,3},{4,20},{20... | collective-permute-start | bytes 294920 | tf_op jit(solution)/shard_map/ppermute | solution.py:456
  64.1 1.1 %terms0.1 = (f32[4,96,384]{2,1,0:T(8,128)S(1)}, bf16[4,96,384]{2,1,0:T(8,128)(2,1)S(1)}) custom-call(bf16[768,256]{1,0:T(8,128)(2,1)S(1)} %get-tuple-element.177.refs_0_, bf16[768,256]{1,0:T(8,128)(2,1)S(1)} %collective-permute-done.10.refs_1_, bf16[768,256]{1,0:T(8,128)(2,1)S(1)} %collective-permute-done.11.refs_2_, ...), custom_call_target="tpu_custom_call" | custom-call | flops 1000 | bytes 1003 | tf_op jit(solution)/shard_map/terms0/pallas_call | solution.py:682
  65.5 2.5 %collective-permute-done.25.a = bf16[128,384]{1,0:T(8,128)(2,1)S(1)} collective-permute-done((bf16[128,384]{1,0:T(8,128)(2,1)S(1)}, bf16[128,384]{1,0:T(8,128)(2,1)S(1)}, u32[]{:S(2)}, u32[]{:S(2)}) %collective-permute-start.25) | collective-permute-done | bytes 98336 | tf_op jit(solution)/shard_map/ppermute | solution.py:456
  68.0 1.1 %terms1.1 = (f32[4,96,384]{2,1,0:T(8,128)S(1)}, bf16[4,96,384]{2,1,0:T(8,128)(2,1)S(1)}) custom-call(bf16[768,256]{1,0:T(8,128)(2,1)S(1)} %get-tuple-element.177.refs_0_, bf16[768,256]{1,0:T(8,128)(2,1)S(1)} %collective-permute-done.10.refs_1_, bf16[768,256]{1,0:T(8,128)(2,1)S(1)} %collective-permute-done.11.refs_2_, ...), custom_call_target="tpu_custom_call" | custom-call | flops 1000 | bytes 1003 | tf_op jit(solution)/shard_map/terms1/pallas_call | solution.py:682
  69.1 1.8 %collective-permute-start.29 = (bf16[4,96,384]{2,1,0:T(8,128)(2,1)S(1)}, bf16[4,96,384]{2,1,0:T(8,128)(2,1)S(1)}, u32[]{:S(2)}, u32[]{:S(2)}) collective-permute-start(bf16[4,96,384]{2,1,0:T(8,128)(2,1)S(1)} %get-tuple-element.196), channel_id=1, source_target_pairs={{0,16},{16,0},{1,17},{17,1},{2,18},{18,2},{3,19},{19,3},{4,20},{20... | collective-permute-start | bytes 884744 | tf_op jit(solution)/shard_map/ppermute | solution.py:456
  70.9 7.5 %mix.1.normed_ref = bf16[1024,384]{1,0:T(8,128)(2,1)S(1)} custom-call(bf16[1024,384]{1,0:T(8,128)(2,1)S(1)} %get-tuple-element.176.grid.grid_ref, bf16[96,384]{1,0:T(8,128)(2,1)S(1)} %collective-permute-done.22.left_ref.left, bf16[96,384]{1,0:T(8,128)(2,1)S(1)} %collective-permute-done.23.right_ref.right, bf16[128,384]{1,0:T(8,128)(2,1)S(1)} %collective-permute-done.25.a, ...), custom_call_target="tpu_custom_call" | custom-call | flops 1000 | bytes 1003 | tf_op jit(solution)/shard_map/mix/pallas_call | solution.py:698
  78.5 0.8 collective-permute-start.26
  79.3 3.3 %collective-permute-start.27 = (bf16[96,384]{1,0:T(8,128)(2,1)S(1)}, bf16[96,384]{1,0:T(8,128)(2,1)S(1)}, u32[]{:S(2)}, u32[]{:S(2)}) collective-permute-start(bf16[96,384]{1,0:T(8,128)(2,1)S(1)} %get-tuple-element.194), channel_id=1, source_target_pairs={{0,8},{4,12},{8,0},{12,4},{1,9},{5,13},{9,1},{13,5},{2,10},{6,14},... | collective-permute-start | bytes 221192 | tf_op jit(solution)/shard_map/ppermute | solution.py:456
  82.6 0.9 collective-permute-start.28
  83.5 1.2 %collective-permute-start.30 = (bf16[96,384]{1,0:T(8,128)(2,1)S(1)}, bf16[96,384]{1,0:T(8,128)(2,1)S(1)}, u32[]{:S(2)}, u32[]{:S(2)}) collective-permute-start(bf16[96,384]{1,0:T(8,128)(2,1)S(1)} %get-tuple-element.200), channel_id=1, source_target_pairs={{0,4},{4,8},{8,12},{12,0},{1,5},{5,9},{9,13},{13,1},{2,6},{6,10},{... | collective-permute-start | bytes 221192 | tf_op jit(solution)/shard_map/ppermute | solution.py:456
  84.7 2.7 %collective-permute-start.32 = (bf16[96,384]{1,0:T(8,128)(2,1)S(1)}, bf16[96,384]{1,0:T(8,128)(2,1)S(1)}, u32[]{:S(2)}, u32[]{:S(2)}) collective-permute-start(bf16[96,384]{1,0:T(8,128)(2,1)S(1)} %get-tuple-element.202), channel_id=1, source_target_pairs={{0,12},{4,0},{8,4},{12,8},{1,13},{5,1},{9,5},{13,9},{2,14},{6,2},{... | collective-permute-start | bytes 221192 | tf_op jit(solution)/shard_map/ppermute | solution.py:456
  87.4 3.4 %feed.1 = f32[1024,128]{1,0:T(8,128)} custom-call(bf16[1024,384]{1,0:T(8,128)(2,1)S(1)} %mix.1.normed_ref, bf16[1024,384]{1,0:T(8,128)(2,1)S(1)} %get-tuple-element.176.grid.grid_ref, bf16[384,768]{1,0:T(8,128)(2,1)S(1)} %copy-done.3, bf16[768,384]{1,0:T(8,128)(2,1)S(1)} %copy-done.4, bf16[384,128]{1,0:T(8,128)(2,1)S(1)} %copy-done.6), custom_call_target="tpu_custom_call" | custom-call | flops 1000 | bytes 1003 | tf_op jit(solution)/shard_map/feed/pallas_call | solution.py:726
  90.8 0.5 collective-permute-done.31.refs_6_
  91.4 1.6 %collective-permute-start.34 = (bf16[96,768]{1,0:T(8,128)(2,1)S(1)}, bf16[96,768]{1,0:T(8,128)(2,1)S(1)}, u32[]{:S(2)}, u32[]{:S(2)}) collective-permute-start(bf16[96,768]{1,0:T(8,128)(2,1)S(1)} %close.1.own_ref), channel_id=1, source_target_pairs={{0,2},{1,3},{2,0},{3,1},{4,6},{5,7},{6,4},{7,5},{8,10},{9,11},{10,... | collective-permute-start | bytes 442376 | tf_op jit(solution)/shard_map/ppermute | solution.py:451
  93.0 3.6 %collective-permute-done.34.two_ref = bf16[96,768]{1,0:T(8,128)(2,1)S(1)} collective-permute-done((bf16[96,768]{1,0:T(8,128)(2,1)S(1)}, bf16[96,768]{1,0:T(8,128)(2,1)S(1)}, u32[]{:S(2)}, u32[]{:S(2)}) %collective-permute-start.34) | collective-permute-done | bytes 147488 | tf_op jit(solution)/shard_map/ppermute | solution.py:451
  96.6 1.4 %collective-permute-done.35.three_ref = bf16[96,768]{1,0:T(8,128)(2,1)S(1)} collective-permute-done((bf16[96,768]{1,0:T(8,128)(2,1)S(1)}, bf16[96,768]{1,0:T(8,128)(2,1)S(1)}, u32[]{:S(2)}, u32[]{:S(2)}) %collective-permute-start.35) | collective-permute-done | bytes 147488 | tf_op jit(solution)/shard_map/ppermute | solution.py:451
  98.0 1.2 %spread.1 = f32[384,768]{1,0:T(8,128)} custom-call(bf16[96,768]{1,0:T(8,128)(2,1)S(1)} %close.1.own_ref, bf16[96,768]{1,0:T(8,128)(2,1)S(1)} %collective-permute-done.33.one_ref, bf16[96,768]{1,0:T(8,128)(2,1)S(1)} %collective-permute-done.34.two_ref, bf16[96,768]{1,0:T(8,128)(2,1)S(1)} %collective-permute-done.35.three_ref), custom_call_target="tpu_custom_call" | custom-call | flops 1000 | bytes 1003 | tf_op jit(solution)/shard_map/spread/pallas_call | solution.py:747
  (72 shorter events, 3.5 us)
Async XLA Ops:
  0.6 13.1 %collective-permute-start.5 = (bf16[256,768]{1,0:T(8,128)(2,1)}, bf16[256,768]{1,0:T(8,128)(2,1)S(1)}, u32[]{:S(2)}, u32[]{:S(2)}) collective-permute-start(bf16[256,768]{1,0:T(8,128)(2,1)} %bitcast.7), channel_id=1, source_target_pairs={{0,2},{1,3},{2,0},{3,1},{4,6},{5,7},{6,4},{7,5},{8,10},{9,11},{10,... | collective-permute-start | bytes 1179656 | tf_op jit(solution)/shard_map/ppermute | solution.py:451
  5.8 13.9 %copy-start.2 = (bf16[768,768]{1,0:T(8,128)(2,1)S(1)}, bf16[768,768]{1,0:T(8,128)(2,1)}, u32[]{:S(2)}) copy-start(bf16[768,768]{1,0:T(8,128)(2,1)} %wout_ref.3) | copy-start | bytes 3538948
  5.8 13.9 %copy-start.5 = (bf16[1,1,1,256,768]{4,3,2,1,0:T(8,128)(2,1)S(1)}, bf16[1,1,1,256,768]{4,3,2,1,0:T(8,128)(2,1)}, u32[]{:S(2)}) copy-start(bf16[1,1,1,256,768]{4,3,2,1,0:T(8,128)(2,1)} %param.19) | copy-start | bytes 1179652
  6.7 9.0 %collective-permute-start = (bf16[40,768]{1,0:T(8,128)(2,1)S(1)}, bf16[40,768]{1,0:T(8,128)(2,1)S(1)}, u32[]{:S(2)}, u32[]{:S(2)}) collective-permute-start(bf16[40,768]{1,0:T(8,128)(2,1)S(1)} %get-tuple-element.108), channel_id=1, source_target_pairs={{0,4},{4,8},{8,12},{12,16},{16,20},{20,24},{24,28},{28,0},{1,5},{5... | collective-permute-start | bytes 184328 | tf_op jit(solution)/shard_map/ppermute | solution.py:516
  8.3 10.0 %collective-permute-start.1 = (bf16[40,768]{1,0:T(8,128)(2,1)S(1)}, bf16[40,768]{1,0:T(8,128)(2,1)S(1)}, u32[]{:S(2)}, u32[]{:S(2)}) collective-permute-start(bf16[40,768]{1,0:T(8,128)(2,1)S(1)} %get-tuple-element.109), channel_id=1, source_target_pairs={{0,8},{4,12},{8,16},{12,20},{16,24},{20,28},{24,0},{28,4},{1,9},{5... | collective-permute-start | bytes 184328 | tf_op jit(solution)/shard_map/ppermute | solution.py:516
  10.9 11.7 %collective-permute-start.2 = (bf16[40,768]{1,0:T(8,128)(2,1)S(1)}, bf16[40,768]{1,0:T(8,128)(2,1)S(1)}, u32[]{:S(2)}, u32[]{:S(2)}) collective-permute-start(bf16[40,768]{1,0:T(8,128)(2,1)S(1)} %get-tuple-element.110), channel_id=1, source_target_pairs={{0,12},{4,16},{8,20},{12,24},{16,28},{20,0},{24,4},{28,8},{1,13},{... | collective-permute-start | bytes 184328 | tf_op jit(solution)/shard_map/ppermute | solution.py:516
  13.2 9.5 %collective-permute-start.3 = (bf16[40,768]{1,0:T(8,128)(2,1)S(1)}, bf16[40,768]{1,0:T(8,128)(2,1)S(1)}, u32[]{:S(2)}, u32[]{:S(2)}) collective-permute-start(bf16[40,768]{1,0:T(8,128)(2,1)S(1)} %get-tuple-element.111), channel_id=1, source_target_pairs={{0,16},{4,20},{8,24},{12,28},{16,0},{20,4},{24,8},{28,12},{1,17},{... | collective-permute-start | bytes 184328 | tf_op jit(solution)/shard_map/ppermute | solution.py:516
  13.7 8.9 %collective-permute-start.4 = (bf16[40,768]{1,0:T(8,128)(2,1)S(1)}, bf16[40,768]{1,0:T(8,128)(2,1)S(1)}, u32[]{:S(2)}, u32[]{:S(2)}) collective-permute-start(bf16[40,768]{1,0:T(8,128)(2,1)S(1)} %get-tuple-element.112), channel_id=1, source_target_pairs={{0,20},{4,24},{8,28},{12,0},{16,4},{20,8},{24,12},{28,16},{1,21},{... | collective-permute-start | bytes 184328 | tf_op jit(solution)/shard_map/ppermute | solution.py:516
  15.7 7.0 %copy-start.12 = (s32[1,1,1,256]{3,2,1,0:T(1,128)S(1)}, s32[1,1,1,256]{3,2,1,0:T(1,128)}, u32[]{:S(2)}) copy-start(s32[1,1,1,256]{3,2,1,0:T(1,128)} %param.17) | copy-start | bytes 3076
  15.7 7.0 %collective-permute-start.6 = (bf16[40,768]{1,0:T(8,128)(2,1)S(1)}, bf16[40,768]{1,0:T(8,128)(2,1)S(1)}, u32[]{:S(2)}, u32[]{:S(2)}) collective-permute-start(bf16[40,768]{1,0:T(8,128)(2,1)S(1)} %get-tuple-element.115), channel_id=1, source_target_pairs={{0,24},{4,28},{8,0},{12,4},{16,8},{20,12},{24,16},{28,20},{1,25},{... | collective-permute-start | bytes 184328 | tf_op jit(solution)/shard_map/ppermute | solution.py:516
  18.3 4.4 %collective-permute-start.7 = (bf16[40,768]{1,0:T(8,128)(2,1)S(1)}, bf16[40,768]{1,0:T(8,128)(2,1)S(1)}, u32[]{:S(2)}, u32[]{:S(2)}) collective-permute-start(bf16[40,768]{1,0:T(8,128)(2,1)S(1)} %get-tuple-element.116), channel_id=1, source_target_pairs={{0,28},{4,0},{8,4},{12,8},{16,12},{20,16},{24,20},{28,24},{1,29},{... | collective-permute-start | bytes 184328 | tf_op jit(solution)/shard_map/ppermute | solution.py:516
  23.5 12.8 %collective-permute-start.9 = (bf16[512,768]{1,0:T(8,128)(2,1)S(1)}, bf16[512,768]{1,0:T(8,128)(2,1)S(1)}, u32[]{:S(2)}, u32[]{:S(2)}) collective-permute-start(bf16[512,768]{1,0:T(8,128)(2,1)S(1)} %get-tuple-element.181.refs_4_), channel_id=1, source_target_pairs={{0,1},{1,0},{2,3},{3,2},{4,5},{5,4},{6,7},{7,6},{8,9},{9,8},{10,11... | collective-permute-start | bytes 2359304 | tf_op jit(solution)/shard_map/ppermute | solution.py:451
  23.6 2.8 %copy-start.11 = (bf16[768,384]{1,0:T(8,128)(2,1)S(1)}, bf16[768,384]{1,0:T(8,128)(2,1)}, u32[]{:S(2)}) copy-start(bf16[768,384]{1,0:T(8,128)(2,1)} %wdec_ref.1) | copy-start | bytes 1769476
  23.6 2.8 %copy-start.13 = (s32[1,1,1,256]{3,2,1,0:T(1,128)S(1)}, s32[1,1,1,256]{3,2,1,0:T(1,128)}, u32[]{:S(2)}) copy-start(s32[1,1,1,256]{3,2,1,0:T(1,128)} %param.18) | copy-start | bytes 3076
  24.8 11.5 %collective-permute-start.8 = (bf16[256,768]{1,0:T(8,128)(2,1)S(1)}, bf16[256,768]{1,0:T(8,128)(2,1)S(1)}, u32[]{:S(2)}, u32[]{:S(2)}) collective-permute-start(bf16[256,768]{1,0:T(8,128)(2,1)S(1)} %get-tuple-element.128.normed_ref), channel_id=1, source_target_pairs={{0,2},{1,3},{2,0},{3,1},{4,6},{5,7},{6,4},{7,5},{8,10},{9,11},{10,... | collective-permute-start | bytes 1179656 | tf_op jit(solution)/shard_map/ppermute | solution.py:451
  26.4 25.9 %copy-start.15 = (bf16[384]{0:T(512)(128)(2,1)S(1)}, bf16[384]{0:T(512)(128)(2,1)}, u32[]{:S(2)}) copy-start(bf16[384]{0:T(512)(128)(2,1)} %param.24) | copy-start | bytes 2308
  26.4 27.8 %copy-start.9 = (s32[1,1,1,8,35]{4,3,2,1,0:T(8,128)S(1)}, s32[1,1,1,8,35]{4,3,2,1,0:T(8,128)}, u32[]{:S(2)}) copy-start(s32[1,1,1,8,35]{4,3,2,1,0:T(8,128)} %param.16) | copy-start | bytes 3364
  26.4 27.8 %copy-start.10 = (f32[2,1408]{1,0:T(2,128)S(1)}, f32[2,1408]{1,0:T(2,128)}, u32[]{:S(2)}) copy-start(f32[2,1408]{1,0:T(2,128)} %constant.2.clone.ids_ref) | copy-start | bytes 33796
  36.3 2.4 %collective-permute-start.10 = (bf16[768,256]{1,0:T(8,128)(2,1)S(1)}, bf16[768,256]{1,0:T(8,128)(2,1)S(1)}, u32[]{:S(2)}, u32[]{:S(2)}) collective-permute-start(bf16[768,256]{1,0:T(8,128)(2,1)S(1)} %get-tuple-element.139), channel_id=1, source_target_pairs={{0,1},{1,0},{2,3},{3,2},{4,5},{5,4},{6,7},{7,6},{8,9},{9,8},{10,11... | collective-permute-start | bytes 1179656 | tf_op jit(solution)/shard_map/ppermute | solution.py:451
  36.3 2.4 %collective-permute-start.13 = (bf16[256,768]{1,0:T(8,128)(2,1)S(1)}, bf16[256,768]{1,0:T(8,128)(2,1)S(1)}, u32[]{:S(2)}, u32[]{:S(2)}) collective-permute-start(bf16[256,768]{1,0:T(8,128)(2,1)S(1)} %collective-permute-done.8.refs_6_), channel_id=1, source_target_pairs={{0,1},{1,0},{2,3},{3,2},{4,5},{5,4},{6,7},{7,6},{8,9},{9,8},{10,11... | collective-permute-start | bytes 1179656 | tf_op jit(solution)/shard_map/ppermute | solution.py:451
  36.8 2.3 %collective-permute-start.14 = (bf16[256,768]{1,0:T(8,128)(2,1)S(1)}, bf16[256,768]{1,0:T(8,128)(2,1)S(1)}, u32[]{:S(2)}, u32[]{:S(2)}) collective-permute-start(bf16[256,768]{1,0:T(8,128)(2,1)S(1)} %collective-permute-done.5.refs_8_), channel_id=1, source_target_pairs={{0,1},{1,0},{2,3},{3,2},{4,5},{5,4},{6,7},{7,6},{8,9},{9,8},{10,11... | collective-permute-start | bytes 1179656 | tf_op jit(solution)/shard_map/ppermute | solution.py:451
  36.8 27.3 %collective-permute-start.11 = (bf16[768,256]{1,0:T(8,128)(2,1)S(1)}, bf16[768,256]{1,0:T(8,128)(2,1)S(1)}, u32[]{:S(2)}, u32[]{:S(2)}) collective-permute-start(bf16[768,256]{1,0:T(8,128)(2,1)S(1)} %get-tuple-element.140), channel_id=1, source_target_pairs={{0,2},{1,3},{2,0},{3,1},{4,6},{5,7},{6,4},{7,5},{8,10},{9,11},{10,... | collective-permute-start | bytes 1179656 | tf_op jit(solution)/shard_map/ppermute | solution.py:451
  38.4 25.7 %collective-permute-start.12 = (bf16[768,256]{1,0:T(8,128)(2,1)S(1)}, bf16[768,256]{1,0:T(8,128)(2,1)S(1)}, u32[]{:S(2)}, u32[]{:S(2)}) collective-permute-start(bf16[768,256]{1,0:T(8,128)(2,1)S(1)} %get-tuple-element.141), channel_id=1, source_target_pairs={{0,3},{1,2},{2,1},{3,0},{4,7},{5,6},{6,5},{7,4},{8,11},{9,10},{10,... | collective-permute-start | bytes 1179656 | tf_op jit(solution)/shard_map/ppermute | solution.py:451
  39.2 6.6 %collective-permute-start.15 = (bf16[40,384]{1,0:T(8,128)(2,1)S(1)}, bf16[40,384]{1,0:T(8,128)(2,1)S(1)}, u32[]{:S(2)}, u32[]{:S(2)}) collective-permute-start(bf16[40,384]{1,0:T(8,128)(2,1)S(1)} %get-tuple-element.154), channel_id=1, source_target_pairs={{0,4},{4,8},{8,12},{12,16},{16,20},{20,24},{24,28},{28,0},{1,5},{5... | collective-permute-start | bytes 92168 | tf_op jit(solution)/shard_map/ppermute | solution.py:602
  39.9 7.7 %collective-permute-start.16 = (bf16[40,384]{1,0:T(8,128)(2,1)S(1)}, bf16[40,384]{1,0:T(8,128)(2,1)S(1)}, u32[]{:S(2)}, u32[]{:S(2)}) collective-permute-start(bf16[40,384]{1,0:T(8,128)(2,1)S(1)} %get-tuple-element.155), channel_id=1, source_target_pairs={{0,8},{4,12},{8,16},{12,20},{16,24},{20,28},{24,0},{28,4},{1,9},{5... | collective-permute-start | bytes 92168 | tf_op jit(solution)/shard_map/ppermute | solution.py:602
  43.6 4.8 %collective-permute-start.17 = (bf16[40,384]{1,0:T(8,128)(2,1)S(1)}, bf16[40,384]{1,0:T(8,128)(2,1)S(1)}, u32[]{:S(2)}, u32[]{:S(2)}) collective-permute-start(bf16[40,384]{1,0:T(8,128)(2,1)S(1)} %get-tuple-element.156), channel_id=1, source_target_pairs={{0,12},{4,16},{8,20},{12,24},{16,28},{20,0},{24,4},{28,8},{1,13},{... | collective-permute-start | bytes 92168 | tf_op jit(solution)/shard_map/ppermute | solution.py:602
  45.8 4.5 %collective-permute-start.18 = (bf16[40,384]{1,0:T(8,128)(2,1)S(1)}, bf16[40,384]{1,0:T(8,128)(2,1)S(1)}, u32[]{:S(2)}, u32[]{:S(2)}) collective-permute-start(bf16[40,384]{1,0:T(8,128)(2,1)S(1)} %get-tuple-element.157), channel_id=1, source_target_pairs={{0,16},{4,20},{8,24},{12,28},{16,0},{20,4},{24,8},{28,12},{1,17},{... | collective-permute-start | bytes 92168 | tf_op jit(solution)/shard_map/ppermute | solution.py:602
  47.6 5.8 %collective-permute-start.19 = (bf16[40,384]{1,0:T(8,128)(2,1)S(1)}, bf16[40,384]{1,0:T(8,128)(2,1)S(1)}, u32[]{:S(2)}, u32[]{:S(2)}) collective-permute-start(bf16[40,384]{1,0:T(8,128)(2,1)S(1)} %get-tuple-element.158), channel_id=1, source_target_pairs={{0,20},{4,24},{8,28},{12,0},{16,4},{20,8},{24,12},{28,16},{1,21},{... | collective-permute-start | bytes 92168 | tf_op jit(solution)/shard_map/ppermute | solution.py:602
  48.4 5.5 %collective-permute-start.20 = (bf16[40,384]{1,0:T(8,128)(2,1)S(1)}, bf16[40,384]{1,0:T(8,128)(2,1)S(1)}, u32[]{:S(2)}, u32[]{:S(2)}) collective-permute-start(bf16[40,384]{1,0:T(8,128)(2,1)S(1)} %get-tuple-element.159), channel_id=1, source_target_pairs={{0,24},{4,28},{8,0},{12,4},{16,8},{20,12},{24,16},{28,20},{1,25},{... | collective-permute-start | bytes 92168 | tf_op jit(solution)/shard_map/ppermute | solution.py:602
  50.3 3.9 %collective-permute-start.21 = (bf16[40,384]{1,0:T(8,128)(2,1)S(1)}, bf16[40,384]{1,0:T(8,128)(2,1)S(1)}, u32[]{:S(2)}, u32[]{:S(2)}) collective-permute-start(bf16[40,384]{1,0:T(8,128)(2,1)S(1)} %get-tuple-element.160), channel_id=1, source_target_pairs={{0,28},{4,0},{8,4},{12,8},{16,12},{20,16},{24,20},{28,24},{1,29},{... | collective-permute-start | bytes 92168 | tf_op jit(solution)/shard_map/ppermute | solution.py:602
  55.7 6.5 %collective-permute-start.22 = (bf16[96,384]{1,0:T(8,128)(2,1)S(1)}, bf16[96,384]{1,0:T(8,128)(2,1)S(1)}, u32[]{:S(2)}, u32[]{:S(2)}) collective-permute-start(bf16[96,384]{1,0:T(8,128)(2,1)S(1)} %get-tuple-element.161), channel_id=1, source_target_pairs={{0,4},{4,8},{8,12},{12,0},{1,5},{5,9},{9,13},{13,1},{2,6},{6,10},{... | collective-permute-start | bytes 221192 | tf_op jit(solution)/shard_map/ppermute | solution.py:456
  57.1 5.1 %collective-permute-start.23 = (bf16[96,384]{1,0:T(8,128)(2,1)S(1)}, bf16[96,384]{1,0:T(8,128)(2,1)S(1)}, u32[]{:S(2)}, u32[]{:S(2)}) collective-permute-start(bf16[96,384]{1,0:T(8,128)(2,1)S(1)} %get-tuple-element.162), channel_id=1, source_target_pairs={{0,12},{4,0},{8,4},{12,8},{1,13},{5,1},{9,5},{13,9},{2,14},{6,2},{... | collective-permute-start | bytes 221192 | tf_op jit(solution)/shard_map/ppermute | solution.py:456
  62.2 5.8 %collective-permute-start.25 = (bf16[128,384]{1,0:T(8,128)(2,1)S(1)}, bf16[128,384]{1,0:T(8,128)(2,1)S(1)}, u32[]{:S(2)}, u32[]{:S(2)}) collective-permute-start(bf16[128,384]{1,0:T(8,128)(2,1)S(1)} %rim.1), channel_id=1, source_target_pairs={{0,16},{16,0},{1,17},{17,1},{2,18},{18,2},{3,19},{19,3},{4,20},{20... | collective-permute-start | bytes 294920 | tf_op jit(solution)/shard_map/ppermute | solution.py:456
  65.2 5.7 %copy-start.7 = (f32[7,7,384]{2,1,0:T(8,128)S(1)}, f32[7,7,384]{2,1,0:T(8,128)}, u32[]{:S(2)}) copy-start(f32[7,7,384]{2,1,0:T(8,128)} %refs_0_.1) | copy-start | bytes 225796
  65.2 13.2 %collective-permute-start.24 = (bf16[4,96,384]{2,1,0:T(8,128)(2,1)S(1)}, bf16[4,96,384]{2,1,0:T(8,128)(2,1)S(1)}, u32[]{:S(2)}, u32[]{:S(2)}) collective-permute-start(bf16[4,96,384]{2,1,0:T(8,128)(2,1)S(1)} %get-tuple-element.175), channel_id=1, source_target_pairs={{0,16},{16,0},{1,17},{17,1},{2,18},{18,2},{3,19},{19,3},{4,20},{20... | collective-permute-start | bytes 884744 | tf_op jit(solution)/shard_map/ppermute | solution.py:456
  69.1 14.3 %collective-permute-start.29 = (bf16[4,96,384]{2,1,0:T(8,128)(2,1)S(1)}, bf16[4,96,384]{2,1,0:T(8,128)(2,1)S(1)}, u32[]{:S(2)}, u32[]{:S(2)}) collective-permute-start(bf16[4,96,384]{2,1,0:T(8,128)(2,1)S(1)} %get-tuple-element.196), channel_id=1, source_target_pairs={{0,16},{16,0},{1,17},{17,1},{2,18},{18,2},{3,19},{19,3},{4,20},{20... | collective-permute-start | bytes 884744 | tf_op jit(solution)/shard_map/ppermute | solution.py:456
  70.9 16.5 %copy-start.3 = (bf16[384,768]{1,0:T(8,128)(2,1)S(1)}, bf16[384,768]{1,0:T(8,128)(2,1)}, u32[]{:S(2)}) copy-start(bf16[384,768]{1,0:T(8,128)(2,1)} %up_ref.1) | copy-start | bytes 1769476
  70.9 16.5 %copy-start.4 = (bf16[768,384]{1,0:T(8,128)(2,1)S(1)}, bf16[768,384]{1,0:T(8,128)(2,1)}, u32[]{:S(2)}) copy-start(bf16[768,384]{1,0:T(8,128)(2,1)} %down_ref.1) | copy-start | bytes 1769476
  70.9 16.5 %copy-start.6 = (bf16[384,128]{1,0:T(8,128)(2,1)S(1)}, bf16[384,128]{1,0:T(8,128)(2,1)}, u32[]{:S(2)}) copy-start(bf16[384,128]{1,0:T(8,128)(2,1)} %head_ref.1) | copy-start | bytes 294916
  78.5 6.3 %collective-permute-start.26 = (bf16[96,384]{1,0:T(8,128)(2,1)S(1)}, bf16[96,384]{1,0:T(8,128)(2,1)S(1)}, u32[]{:S(2)}, u32[]{:S(2)}) collective-permute-start(bf16[96,384]{1,0:T(8,128)(2,1)S(1)} %get-tuple-element.193), channel_id=1, source_target_pairs={{0,4},{4,8},{8,12},{12,0},{1,5},{5,9},{9,13},{13,1},{2,6},{6,10},{... | collective-permute-start | bytes 221192 | tf_op jit(solution)/shard_map/ppermute | solution.py:456
  79.3 11.5 %collective-permute-start.27 = (bf16[96,384]{1,0:T(8,128)(2,1)S(1)}, bf16[96,384]{1,0:T(8,128)(2,1)S(1)}, u32[]{:S(2)}, u32[]{:S(2)}) collective-permute-start(bf16[96,384]{1,0:T(8,128)(2,1)S(1)} %get-tuple-element.194), channel_id=1, source_target_pairs={{0,8},{4,12},{8,0},{12,4},{1,9},{5,13},{9,1},{13,5},{2,10},{6,14},... | collective-permute-start | bytes 221192 | tf_op jit(solution)/shard_map/ppermute | solution.py:456
  82.6 8.2 %collective-permute-start.28 = (bf16[96,384]{1,0:T(8,128)(2,1)S(1)}, bf16[96,384]{1,0:T(8,128)(2,1)S(1)}, u32[]{:S(2)}, u32[]{:S(2)}) collective-permute-start(bf16[96,384]{1,0:T(8,128)(2,1)S(1)} %get-tuple-element.195), channel_id=1, source_target_pairs={{0,12},{4,0},{8,4},{12,8},{1,13},{5,1},{9,5},{13,9},{2,14},{6,2},{... | collective-permute-start | bytes 221192 | tf_op jit(solution)/shard_map/ppermute | solution.py:456
  83.5 7.3 %collective-permute-start.30 = (bf16[96,384]{1,0:T(8,128)(2,1)S(1)}, bf16[96,384]{1,0:T(8,128)(2,1)S(1)}, u32[]{:S(2)}, u32[]{:S(2)}) collective-permute-start(bf16[96,384]{1,0:T(8,128)(2,1)S(1)} %get-tuple-element.200), channel_id=1, source_target_pairs={{0,4},{4,8},{8,12},{12,0},{1,5},{5,9},{9,13},{13,1},{2,6},{6,10},{... | collective-permute-start | bytes 221192 | tf_op jit(solution)/shard_map/ppermute | solution.py:456
  84.7 6.6 %collective-permute-start.31 = (bf16[96,384]{1,0:T(8,128)(2,1)S(1)}, bf16[96,384]{1,0:T(8,128)(2,1)S(1)}, u32[]{:S(2)}, u32[]{:S(2)}) collective-permute-start(bf16[96,384]{1,0:T(8,128)(2,1)S(1)} %get-tuple-element.201), channel_id=1, source_target_pairs={{0,8},{4,12},{8,0},{12,4},{1,9},{5,13},{9,1},{13,5},{2,10},{6,14},... | collective-permute-start | bytes 221192 | tf_op jit(solution)/shard_map/ppermute | solution.py:456
  84.7 6.6 %collective-permute-start.32 = (bf16[96,384]{1,0:T(8,128)(2,1)S(1)}, bf16[96,384]{1,0:T(8,128)(2,1)S(1)}, u32[]{:S(2)}, u32[]{:S(2)}) collective-permute-start(bf16[96,384]{1,0:T(8,128)(2,1)S(1)} %get-tuple-element.202), channel_id=1, source_target_pairs={{0,12},{4,0},{8,4},{12,8},{1,13},{5,1},{9,5},{13,9},{2,14},{6,2},{... | collective-permute-start | bytes 221192 | tf_op jit(solution)/shard_map/ppermute | solution.py:456
  91.4 5.2 %collective-permute-start.34 = (bf16[96,768]{1,0:T(8,128)(2,1)S(1)}, bf16[96,768]{1,0:T(8,128)(2,1)S(1)}, u32[]{:S(2)}, u32[]{:S(2)}) collective-permute-start(bf16[96,768]{1,0:T(8,128)(2,1)S(1)} %close.1.own_ref), channel_id=1, source_target_pairs={{0,2},{1,3},{2,0},{3,1},{4,6},{5,7},{6,4},{7,5},{8,10},{9,11},{10,... | collective-permute-start | bytes 442376 | tf_op jit(solution)/shard_map/ppermute | solution.py:451
  93.0 3.6 %collective-permute-start.33 = (bf16[96,768]{1,0:T(8,128)(2,1)S(1)}, bf16[96,768]{1,0:T(8,128)(2,1)S(1)}, u32[]{:S(2)}, u32[]{:S(2)}) collective-permute-start(bf16[96,768]{1,0:T(8,128)(2,1)S(1)} %close.1.own_ref), channel_id=1, source_target_pairs={{0,1},{1,0},{2,3},{3,2},{4,5},{5,4},{6,7},{7,6},{8,9},{9,8},{10,11... | collective-permute-start | bytes 442376 | tf_op jit(solution)/shard_map/ppermute | solution.py:451
  96.6 1.4 %collective-permute-start.35 = (bf16[96,768]{1,0:T(8,128)(2,1)S(1)}, bf16[96,768]{1,0:T(8,128)(2,1)S(1)}, u32[]{:S(2)}, u32[]{:S(2)}) collective-permute-start(bf16[96,768]{1,0:T(8,128)(2,1)S(1)} %collective-permute-done.34.two_ref), channel_id=1, source_target_pairs={{0,1},{1,0},{2,3},{3,2},{4,5},{5,4},{6,7},{7,6},{8,9},{9,8},{10,11... | collective-permute-start | bytes 442376 | tf_op jit(solution)/shard_map/ppermute | solution.py:451
  (4 other events, 6.9 us)

commit v13 on v12

--- a/solution.py
+++ b/solution.py
@@ -688,9 +688,9 @@
                 nbytes=8 * MIB,
                 limit=10,
             )(*lefts, *rights)
-            if c == 0:
-                lefts, rights = tie((lefts, rights), rims)
             kept.append(keep)
+            if c == 1:
+                send = tie(send, rims)
             sent.append(turn(send, "eta", 1))
         left, right_halo, rims = tie((left_halo, right_halo, rims), kept)
     else:

time: 99.3 us -> 98.2 us (0.989)
  waiting for transfers between devices: 17 us -> 15.9 us
    ppermute x11, waiting for transfers between devices: 5.26 us -> 4.19 us  [turn(): lax.ppermute(value, axis, [(i, (i + k) % count) for i in range(count)])]
  transfers between devices with their start and end apart: 36 -> 36, of which waited for: 12 -> 13; matrix products, arithmetic and copies ran while one was open for 0% -> 0% of each run, Pallas kernels for 26% -> 26%
where the time goes in v13:
time: 98.2 us; the launch traced here: 98 us
  starting transfers between devices  49.4 us (50%)
  Pallas kernels  27.6 us (28%)
  waiting for transfers between devices  15.9 us (16%)
  local copies, waits for them, and re-layouts  4.16 us (4%)
    ppermute x11, starting transfers between devices, turn(): lax.ppermute(value, axis, [(i, (i + k) % count) for i in range(count)])  17.1 us
    ppermute x7, starting transfers between devices, body(): arrived.append(lax.ppermute(outgoing[k], ('eta', 'phi'), pairs))  12.9 us
    ppermute x7, starting transfers between devices, body(): returned.append(lax.ppermute(outbound[k], ('eta', 'phi'), pairs))  10.7 us
    ppermute x11, starting transfers between devices, flip(): lax.ppermute(value, axis, [(i, i ^ bit) for i in range(lax.axis_size(axis...  8.65 us
    pallas_call x1, Pallas kernels, body(): call(functools.partial(encode_kernel, split, sends), 'encode', [sds((slot...  7.97 us
    pallas_call x1, Pallas kernels, body(): call(functools.partial(mix_folded if folded else mix_open, (eta_cells, ph...  7.46 us
    ppermute x11, waiting for transfers between devices, flip(): lax.ppermute(value, axis, [(i, i ^ bit) for i in range(lax.axis_size(axis...  7.42 us
    ppermute x7, waiting for transfers between devices, body(): returned.append(lax.ppermute(outbound[k], ('eta', 'phi'), pairs))  4.31 us
  transfers between devices with their start and end apart: 36, of which 13 were waited for; matrix products, arithmetic and copies ran while one was open for 0% of the time, Pallas kernels for 26%

profile of v13, /device:TPU:0, one launch (start us, length us, event | category | flops | bytes accessed | tf_op | source)
XLA Modules:
  0.0 98.0 jit_solution(12047638920929917928)
XLA Ops:
  0.6 3.0 %collective-permute-start.5 = (bf16[256,768]{1,0:T(8,128)(2,1)}, bf16[256,768]{1,0:T(8,128)(2,1)S(1)}, u32[]{:S(2)}, u32[]{:S(2)}) collective-permute-start(bf16[256,768]{1,0:T(8,128)(2,1)} %bitcast.7), channel_id=1, source_target_pairs={{0,2},{1,3},{2,0},{3,1},{4,6},{5,7},{6,4},{7,5},{8,10},{9,11},{10,... | collective-permute-start | bytes 1179656 | tf_op jit(solution)/shard_map/ppermute | solution.py:451
  3.7 1.4 %copy-done.1 = bf16[1,32,32,768]{3,2,1,0:T(8,128)(2,1)S(1)} copy-done((bf16[1,32,32,768]{3,2,1,0:T(8,128)(2,1)S(1)}, bf16[1,32,32,768]{3,2,1,0:T(8,128)(2,1)}, u32[]{:S(2)}) %copy-start.1) | copy-done | bytes 1572888
  5.1 0.7 copy-done.8
  5.8 0.9 pick.1
  6.7 1.6 %collective-permute-start = (bf16[40,768]{1,0:T(8,128)(2,1)S(1)}, bf16[40,768]{1,0:T(8,128)(2,1)S(1)}, u32[]{:S(2)}, u32[]{:S(2)}) collective-permute-start(bf16[40,768]{1,0:T(8,128)(2,1)S(1)} %get-tuple-element.99), channel_id=1, source_target_pairs={{0,4},{4,8},{8,12},{12,16},{16,20},{20,24},{24,28},{28,0},{1,5},{5... | collective-permute-start | bytes 184328 | tf_op jit(solution)/shard_map/ppermute | solution.py:516
  8.3 2.6 %collective-permute-start.1 = (bf16[40,768]{1,0:T(8,128)(2,1)S(1)}, bf16[40,768]{1,0:T(8,128)(2,1)S(1)}, u32[]{:S(2)}, u32[]{:S(2)}) collective-permute-start(bf16[40,768]{1,0:T(8,128)(2,1)S(1)} %get-tuple-element.100), channel_id=1, source_target_pairs={{0,8},{4,12},{8,16},{12,20},{16,24},{20,28},{24,0},{28,4},{1,9},{5... | collective-permute-start | bytes 184328 | tf_op jit(solution)/shard_map/ppermute | solution.py:516
  10.9 2.3 %collective-permute-start.2 = (bf16[40,768]{1,0:T(8,128)(2,1)S(1)}, bf16[40,768]{1,0:T(8,128)(2,1)S(1)}, u32[]{:S(2)}, u32[]{:S(2)}) collective-permute-start(bf16[40,768]{1,0:T(8,128)(2,1)S(1)} %get-tuple-element.101), channel_id=1, source_target_pairs={{0,12},{4,16},{8,20},{12,24},{16,28},{20,0},{24,4},{28,8},{1,13},{... | collective-permute-start | bytes 184328 | tf_op jit(solution)/shard_map/ppermute | solution.py:516
  13.2 0.5 collective-permute-start.3
  13.7 2.0 %collective-permute-start.4 = (bf16[40,768]{1,0:T(8,128)(2,1)S(1)}, bf16[40,768]{1,0:T(8,128)(2,1)S(1)}, u32[]{:S(2)}, u32[]{:S(2)}) collective-permute-start(bf16[40,768]{1,0:T(8,128)(2,1)S(1)} %get-tuple-element.103), channel_id=1, source_target_pairs={{0,20},{4,24},{8,28},{12,0},{16,4},{20,8},{24,12},{28,16},{1,21},{... | collective-permute-start | bytes 184328 | tf_op jit(solution)/shard_map/ppermute | solution.py:516
  15.7 2.6 %collective-permute-start.6 = (bf16[40,768]{1,0:T(8,128)(2,1)S(1)}, bf16[40,768]{1,0:T(8,128)(2,1)S(1)}, u32[]{:S(2)}, u32[]{:S(2)}) collective-permute-start(bf16[40,768]{1,0:T(8,128)(2,1)S(1)} %get-tuple-element.106), channel_id=1, source_target_pairs={{0,24},{4,28},{8,0},{12,4},{16,8},{20,12},{24,16},{28,20},{1,25},{... | collective-permute-start | bytes 184328 | tf_op jit(solution)/shard_map/ppermute | solution.py:516
  18.3 1.3 %collective-permute-start.7 = (bf16[40,768]{1,0:T(8,128)(2,1)S(1)}, bf16[40,768]{1,0:T(8,128)(2,1)S(1)}, u32[]{:S(2)}, u32[]{:S(2)}) collective-permute-start(bf16[40,768]{1,0:T(8,128)(2,1)S(1)} %get-tuple-element.107), channel_id=1, source_target_pairs={{0,28},{4,0},{8,4},{12,8},{16,12},{20,16},{24,20},{28,24},{1,29},{... | collective-permute-start | bytes 184328 | tf_op jit(solution)/shard_map/ppermute | solution.py:516
  19.6 2.0 %copy-done = bf16[768,2304]{1,0:T(8,128)(2,1)S(1)} copy-done((bf16[768,2304]{1,0:T(8,128)(2,1)S(1)}, bf16[768,2304]{1,0:T(8,128)(2,1)}, u32[]{:S(2)}) %copy-start) | copy-done | bytes 3538968
  21.6 1.0 %prep.1 = (bf16[768,256]{1,0:T(8,128)(2,1)S(1)}, bf16[2304,768]{1,0:T(8,128)(2,1)S(1)}) custom-call(bf16[256,768]{1,0:T(8,128)(2,1)S(1)} %bitcast.8, bf16[768,768]{1,0:T(8,128)(2,1)S(1)} %copy-done.2, bf16[768,2304]{1,0:T(8,128)(2,1)S(1)} %copy-done), custom_call_target="tpu_custom_call" | custom-call | flops 1000 | bytes 1003 | tf_op jit(solution)/shard_map/prep/pallas_call | solution.py:530
  22.7 0.8 norm.1
  23.6 1.1 %project.1 = (f32[1536,256]{1,0:T(8,128)S(1)}, f32[24,256]{1,0:T(8,128)S(1)}, bf16[768,256]{1,0:T(8,128)(2,1)S(1)}) custom-call(bf16[256,768]{1,0:T(8,128)(2,1)S(1)} %get-tuple-element.119.normed_ref, bf16[2304,768]{1,0:T(8,128)(2,1)S(1)} %get-tuple-element.108.wqkv_t_ref), custom_call_target="tpu_custom_call" | custom-call | flops 2000000000 | bytes 6667666 | tf_op jit(solution)/shard_map/project/pallas_call | solution.py:554
  24.8 1.6 %collective-permute-start.8 = (bf16[256,768]{1,0:T(8,128)(2,1)S(1)}, bf16[256,768]{1,0:T(8,128)(2,1)S(1)}, u32[]{:S(2)}, u32[]{:S(2)}) collective-permute-start(bf16[256,768]{1,0:T(8,128)(2,1)S(1)} %get-tuple-element.119.normed_ref), channel_id=1, source_target_pairs={{0,2},{1,3},{2,0},{3,1},{4,6},{5,7},{6,4},{7,5},{8,10},{9,11},{10,... | collective-permute-start | bytes 1179656 | tf_op jit(solution)/shard_map/ppermute | solution.py:451
  26.4 8.0 %encode.1 = (bf16[40,384]{1,0:T(8,128)(2,1)S(1)}, bf16[40,384]{1,0:T(8,128)(2,1)S(1)}, bf16[40,384]{1,0:T(8,128)(2,1)S(1)}, bf16[40,384]{1,0:T(8,128)(2,1)S(1)},...) custom-call(s32[1,256]{1,0:T(1,128)S(1)} %bitcast.13, ...), custom_call_target="tpu_custom_call" | custom-call | flops 8000000000 | bytes 26667666 | tf_op jit(solution)/shard_map/encode/pallas_call | solution.py:566
  34.4 1.9 %collective-permute-done.8.refs_6_ = bf16[256,768]{1,0:T(8,128)(2,1)S(1)} collective-permute-done((bf16[256,768]{1,0:T(8,128)(2,1)S(1)}, bf16[256,768]{1,0:T(8,128)(2,1)S(1)}, u32[]{:S(2)}, u32[]{:S(2)}) %collective-permute-start.8) | collective-permute-done | bytes 393248 | tf_op jit(solution)/shard_map/ppermute | solution.py:451
  36.3 0.5 collective-permute-start.13
  36.8 1.5 %collective-permute-start.11 = (bf16[768,256]{1,0:T(8,128)(2,1)S(1)}, bf16[768,256]{1,0:T(8,128)(2,1)S(1)}, u32[]{:S(2)}, u32[]{:S(2)}) collective-permute-start(bf16[768,256]{1,0:T(8,128)(2,1)S(1)} %get-tuple-element.131), channel_id=1, source_target_pairs={{0,2},{1,3},{2,0},{3,1},{4,6},{5,7},{6,4},{7,5},{8,10},{9,11},{10,... | collective-permute-start | bytes 1179656 | tf_op jit(solution)/shard_map/ppermute | solution.py:451
  39.2 0.7 collective-permute-start.15
  39.9 3.7 %collective-permute-start.16 = (bf16[40,384]{1,0:T(8,128)(2,1)S(1)}, bf16[40,384]{1,0:T(8,128)(2,1)S(1)}, u32[]{:S(2)}, u32[]{:S(2)}) collective-permute-start(bf16[40,384]{1,0:T(8,128)(2,1)S(1)} %get-tuple-element.146), channel_id=1, source_target_pairs={{0,8},{4,12},{8,16},{12,20},{16,24},{20,28},{24,0},{28,4},{1,9},{5... | collective-permute-start | bytes 92168 | tf_op jit(solution)/shard_map/ppermute | solution.py:602
  43.9 1.9 %collective-permute-done.15.refs_1_ = bf16[40,384]{1,0:T(8,128)(2,1)S(1)} collective-permute-done((bf16[40,384]{1,0:T(8,128)(2,1)S(1)}, bf16[40,384]{1,0:T(8,128)(2,1)S(1)}, u32[]{:S(2)}, u32[]{:S(2)}) %collective-permute-start.15) | collective-permute-done | bytes 30752 | tf_op jit(solution)/shard_map/ppermute | solution.py:602
  45.8 1.8 %collective-permute-start.18 = (bf16[40,384]{1,0:T(8,128)(2,1)S(1)}, bf16[40,384]{1,0:T(8,128)(2,1)S(1)}, u32[]{:S(2)}, u32[]{:S(2)}) collective-permute-start(bf16[40,384]{1,0:T(8,128)(2,1)S(1)} %get-tuple-element.148), channel_id=1, source_target_pairs={{0,16},{4,20},{8,24},{12,28},{16,0},{20,4},{24,8},{28,12},{1,17},{... | collective-permute-start | bytes 92168 | tf_op jit(solution)/shard_map/ppermute | solution.py:602
  47.9 0.5 collective-permute-done.17.refs_3_
  48.4 1.9 %collective-permute-start.20 = (bf16[40,384]{1,0:T(8,128)(2,1)S(1)}, bf16[40,384]{1,0:T(8,128)(2,1)S(1)}, u32[]{:S(2)}, u32[]{:S(2)}) collective-permute-start(bf16[40,384]{1,0:T(8,128)(2,1)S(1)} %get-tuple-element.150), channel_id=1, source_target_pairs={{0,24},{4,28},{8,0},{12,4},{16,8},{20,12},{24,16},{28,20},{1,25},{... | collective-permute-start | bytes 92168 | tf_op jit(solution)/shard_map/ppermute | solution.py:602
  50.3 1.9 %collective-permute-start.21 = (bf16[40,384]{1,0:T(8,128)(2,1)S(1)}, bf16[40,384]{1,0:T(8,128)(2,1)S(1)}, u32[]{:S(2)}, u32[]{:S(2)}) collective-permute-start(bf16[40,384]{1,0:T(8,128)(2,1)S(1)} %get-tuple-element.151), channel_id=1, source_target_pairs={{0,28},{4,0},{8,4},{12,8},{16,12},{20,16},{24,20},{28,24},{1,29},{... | collective-permute-start | bytes 92168 | tf_op jit(solution)/shard_map/ppermute | solution.py:602
  52.2 1.1 %collective-permute-done.19.refs_5_ = bf16[40,384]{1,0:T(8,128)(2,1)S(1)} collective-permute-done((bf16[40,384]{1,0:T(8,128)(2,1)S(1)}, bf16[40,384]{1,0:T(8,128)(2,1)S(1)}, u32[]{:S(2)}, u32[]{:S(2)}) %collective-permute-start.19) | collective-permute-done | bytes 30752 | tf_op jit(solution)/shard_map/ppermute | solution.py:602
  54.2 1.5 %fill.1 = (bf16[1024,384]{1,0:T(8,128)(2,1)S(1)}, bf16[96,384]{1,0:T(8,128)(2,1)S(1)}, bf16[96,384]{1,0:T(8,128)(2,1)S(1)}, bf16[96,384]{1,0:T(8,128)(2,1)S(1)}) custom-call(s32[8,35]{1,0:T(8,128)S(1)} %bitcast.11, f32[2,1408]{1,0:T(2,128)S(1)} %copy-done.10, bf16[1,384]{1,0:T(2,128)(2,1)S(1)} %reshape.31.mask_ref, ...), custom_call_target="tpu_custom_call" | custom-call | flops 1000 | bytes 1003 | tf_op jit(solution)/shard_map/fill/pallas_call | solution.py:631
  55.7 1.4 %collective-permute-start.22 = (bf16[96,384]{1,0:T(8,128)(2,1)S(1)}, bf16[96,384]{1,0:T(8,128)(2,1)S(1)}, u32[]{:S(2)}, u32[]{:S(2)}) collective-permute-start(bf16[96,384]{1,0:T(8,128)(2,1)S(1)} %get-tuple-element.152), channel_id=1, source_target_pairs={{0,4},{4,8},{8,12},{12,0},{1,5},{5,9},{9,13},{13,1},{2,6},{6,10},{... | collective-permute-start | bytes 221192 | tf_op jit(solution)/shard_map/ppermute | solution.py:456
  57.1 3.0 %collective-permute-start.23 = (bf16[96,384]{1,0:T(8,128)(2,1)S(1)}, bf16[96,384]{1,0:T(8,128)(2,1)S(1)}, u32[]{:S(2)}, u32[]{:S(2)}) collective-permute-start(bf16[96,384]{1,0:T(8,128)(2,1)S(1)} %get-tuple-element.153), channel_id=1, source_target_pairs={{0,12},{4,0},{8,4},{12,8},{1,13},{5,1},{9,5},{13,9},{2,14},{6,2},{... | collective-permute-start | bytes 221192 | tf_op jit(solution)/shard_map/ppermute | solution.py:456
  60.0 2.2 %collective-permute-done.22.left_ref.left = bf16[96,384]{1,0:T(8,128)(2,1)S(1)} collective-permute-done((bf16[96,384]{1,0:T(8,128)(2,1)S(1)}, bf16[96,384]{1,0:T(8,128)(2,1)S(1)}, u32[]{:S(2)}, u32[]{:S(2)}) %collective-permute-start.22) | collective-permute-done | bytes 73760 | tf_op jit(solution)/shard_map/ppermute | solution.py:456
  62.2 1.9 %collective-permute-start.25 = (bf16[128,384]{1,0:T(8,128)(2,1)S(1)}, bf16[128,384]{1,0:T(8,128)(2,1)S(1)}, u32[]{:S(2)}, u32[]{:S(2)}) collective-permute-start(bf16[128,384]{1,0:T(8,128)(2,1)S(1)} %rim.1), channel_id=1, source_target_pairs={{0,16},{16,0},{1,17},{17,1},{2,18},{18,2},{3,19},{19,3},{4,20},{20... | collective-permute-start | bytes 294920 | tf_op jit(solution)/shard_map/ppermute | solution.py:456
  64.1 1.1 %terms0.1 = (f32[4,96,384]{2,1,0:T(8,128)S(1)}, bf16[4,96,384]{2,1,0:T(8,128)(2,1)S(1)}) custom-call(bf16[768,256]{1,0:T(8,128)(2,1)S(1)} %get-tuple-element.155.refs_0_, bf16[768,256]{1,0:T(8,128)(2,1)S(1)} %collective-permute-done.10.refs_1_, bf16[768,256]{1,0:T(8,128)(2,1)S(1)} %collective-permute-done.11.refs_2_, ...), custom_call_target="tpu_custom_call" | custom-call | flops 1000 | bytes 1003 | tf_op jit(solution)/shard_map/terms0/pallas_call | solution.py:682
  65.5 1.1 %terms1.1 = (f32[4,96,384]{2,1,0:T(8,128)S(1)}, bf16[4,96,384]{2,1,0:T(8,128)(2,1)S(1)}) custom-call(bf16[768,256]{1,0:T(8,128)(2,1)S(1)} %get-tuple-element.155.refs_0_, bf16[768,256]{1,0:T(8,128)(2,1)S(1)} %collective-permute-done.10.refs_1_, bf16[768,256]{1,0:T(8,128)(2,1)S(1)} %collective-permute-done.11.refs_2_, ...), custom_call_target="tpu_custom_call" | custom-call | flops 1000 | bytes 1003 | tf_op jit(solution)/shard_map/terms1/pallas_call | solution.py:682
  66.6 1.5 %collective-permute-done.25.a = bf16[128,384]{1,0:T(8,128)(2,1)S(1)} collective-permute-done((bf16[128,384]{1,0:T(8,128)(2,1)S(1)}, bf16[128,384]{1,0:T(8,128)(2,1)S(1)}, u32[]{:S(2)}, u32[]{:S(2)}) %collective-permute-start.25) | collective-permute-done | bytes 98336 | tf_op jit(solution)/shard_map/ppermute | solution.py:456
  68.0 1.8 %collective-permute-start.29 = (bf16[4,96,384]{2,1,0:T(8,128)(2,1)S(1)}, bf16[4,96,384]{2,1,0:T(8,128)(2,1)S(1)}, u32[]{:S(2)}, u32[]{:S(2)}) collective-permute-start(bf16[4,96,384]{2,1,0:T(8,128)(2,1)S(1)} %get-tuple-element.178), channel_id=1, source_target_pairs={{0,16},{16,0},{1,17},{17,1},{2,18},{18,2},{3,19},{19,3},{4,20},{20... | collective-permute-start | bytes 884744 | tf_op jit(solution)/shard_map/ppermute | solution.py:456
  69.8 7.5 %mix.1.normed_ref = bf16[1024,384]{1,0:T(8,128)(2,1)S(1)} custom-call(bf16[1024,384]{1,0:T(8,128)(2,1)S(1)} %get-tuple-element.167.grid.grid_ref, bf16[96,384]{1,0:T(8,128)(2,1)S(1)} %collective-permute-done.22.left_ref.left, bf16[96,384]{1,0:T(8,128)(2,1)S(1)} %collective-permute-done.23.right_ref.right, bf16[128,384]{1,0:T(8,128)(2,1)S(1)} %collective-permute-done.25.a, ...), custom_call_target="tpu_custom_call" | custom-call | flops 1000 | bytes 1003 | tf_op jit(solution)/shard_map/mix/pallas_call | solution.py:698
  77.4 0.7 collective-permute-start.26
  78.1 3.3 %collective-permute-start.27 = (bf16[96,384]{1,0:T(8,128)(2,1)S(1)}, bf16[96,384]{1,0:T(8,128)(2,1)S(1)}, u32[]{:S(2)}, u32[]{:S(2)}) collective-permute-start(bf16[96,384]{1,0:T(8,128)(2,1)S(1)} %get-tuple-element.175), channel_id=1, source_target_pairs={{0,8},{4,12},{8,0},{12,4},{1,9},{5,13},{9,1},{13,5},{2,10},{6,14},... | collective-permute-start | bytes 221192 | tf_op jit(solution)/shard_map/ppermute | solution.py:456
  81.4 0.9 collective-permute-start.28
  82.4 1.2 %collective-permute-start.30 = (bf16[96,384]{1,0:T(8,128)(2,1)S(1)}, bf16[96,384]{1,0:T(8,128)(2,1)S(1)}, u32[]{:S(2)}, u32[]{:S(2)}) collective-permute-start(bf16[96,384]{1,0:T(8,128)(2,1)S(1)} %get-tuple-element.182), channel_id=1, source_target_pairs={{0,4},{4,8},{8,12},{12,0},{1,5},{5,9},{9,13},{13,1},{2,6},{6,10},{... | collective-permute-start | bytes 221192 | tf_op jit(solution)/shard_map/ppermute | solution.py:456
  83.7 2.7 %collective-permute-start.32 = (bf16[96,384]{1,0:T(8,128)(2,1)S(1)}, bf16[96,384]{1,0:T(8,128)(2,1)S(1)}, u32[]{:S(2)}, u32[]{:S(2)}) collective-permute-start(bf16[96,384]{1,0:T(8,128)(2,1)S(1)} %get-tuple-element.184), channel_id=1, source_target_pairs={{0,12},{4,0},{8,4},{12,8},{1,13},{5,1},{9,5},{13,9},{2,14},{6,2},{... | collective-permute-start | bytes 221192 | tf_op jit(solution)/shard_map/ppermute | solution.py:456
  86.4 3.4 %feed.1 = f32[1024,128]{1,0:T(8,128)} custom-call(bf16[1024,384]{1,0:T(8,128)(2,1)S(1)} %mix.1.normed_ref, bf16[1024,384]{1,0:T(8,128)(2,1)S(1)} %get-tuple-element.167.grid.grid_ref, bf16[384,768]{1,0:T(8,128)(2,1)S(1)} %copy-done.3, bf16[768,384]{1,0:T(8,128)(2,1)S(1)} %copy-done.4, bf16[384,128]{1,0:T(8,128)(2,1)S(1)} %copy-done.6), custom_call_target="tpu_custom_call" | custom-call | flops 1000 | bytes 1003 | tf_op jit(solution)/shard_map/feed/pallas_call | solution.py:726
  90.2 1.6 %collective-permute-start.34 = (bf16[96,768]{1,0:T(8,128)(2,1)S(1)}, bf16[96,768]{1,0:T(8,128)(2,1)S(1)}, u32[]{:S(2)}, u32[]{:S(2)}) collective-permute-start(bf16[96,768]{1,0:T(8,128)(2,1)S(1)} %close.1.own_ref), channel_id=1, source_target_pairs={{0,2},{1,3},{2,0},{3,1},{4,6},{5,7},{6,4},{7,5},{8,10},{9,11},{10,... | collective-permute-start | bytes 442376 | tf_op jit(solution)/shard_map/ppermute | solution.py:451
  91.8 3.6 %collective-permute-done.34.two_ref = bf16[96,768]{1,0:T(8,128)(2,1)S(1)} collective-permute-done((bf16[96,768]{1,0:T(8,128)(2,1)S(1)}, bf16[96,768]{1,0:T(8,128)(2,1)S(1)}, u32[]{:S(2)}, u32[]{:S(2)}) %collective-permute-start.34) | collective-permute-done | bytes 147488 | tf_op jit(solution)/shard_map/ppermute | solution.py:451
  95.4 1.4 %collective-permute-done.35.three_ref = bf16[96,768]{1,0:T(8,128)(2,1)S(1)} collective-permute-done((bf16[96,768]{1,0:T(8,128)(2,1)S(1)}, bf16[96,768]{1,0:T(8,128)(2,1)S(1)}, u32[]{:S(2)}, u32[]{:S(2)}) %collective-permute-start.35) | collective-permute-done | bytes 147488 | tf_op jit(solution)/shard_map/ppermute | solution.py:451
  96.8 1.2 %spread.1 = f32[384,768]{1,0:T(8,128)} custom-call(bf16[96,768]{1,0:T(8,128)(2,1)S(1)} %close.1.own_ref, bf16[96,768]{1,0:T(8,128)(2,1)S(1)} %collective-permute-done.33.one_ref, bf16[96,768]{1,0:T(8,128)(2,1)S(1)} %collective-permute-done.34.two_ref, bf16[96,768]{1,0:T(8,128)(2,1)S(1)} %collective-permute-done.35.three_ref), custom_call_target="tpu_custom_call" | custom-call | flops 1000 | bytes 1003 | tf_op jit(solution)/shard_map/spread/pallas_call | solution.py:747
  (72 shorter events, 3.5 us)
Async XLA Ops:
  0.6 13.1 %collective-permute-start.5 = (bf16[256,768]{1,0:T(8,128)(2,1)}, bf16[256,768]{1,0:T(8,128)(2,1)S(1)}, u32[]{:S(2)}, u32[]{:S(2)}) collective-permute-start(bf16[256,768]{1,0:T(8,128)(2,1)} %bitcast.7), channel_id=1, source_target_pairs={{0,2},{1,3},{2,0},{3,1},{4,6},{5,7},{6,4},{7,5},{8,10},{9,11},{10,... | collective-permute-start | bytes 1179656 | tf_op jit(solution)/shard_map/ppermute | solution.py:451
  5.8 13.9 %copy-start.2 = (bf16[768,768]{1,0:T(8,128)(2,1)S(1)}, bf16[768,768]{1,0:T(8,128)(2,1)}, u32[]{:S(2)}) copy-start(bf16[768,768]{1,0:T(8,128)(2,1)} %wout_ref.3) | copy-start | bytes 3538948
  5.8 13.9 %copy-start.5 = (bf16[1,1,1,256,768]{4,3,2,1,0:T(8,128)(2,1)S(1)}, bf16[1,1,1,256,768]{4,3,2,1,0:T(8,128)(2,1)}, u32[]{:S(2)}) copy-start(bf16[1,1,1,256,768]{4,3,2,1,0:T(8,128)(2,1)} %param.19) | copy-start | bytes 1179652
  6.7 9.0 %collective-permute-start = (bf16[40,768]{1,0:T(8,128)(2,1)S(1)}, bf16[40,768]{1,0:T(8,128)(2,1)S(1)}, u32[]{:S(2)}, u32[]{:S(2)}) collective-permute-start(bf16[40,768]{1,0:T(8,128)(2,1)S(1)} %get-tuple-element.99), channel_id=1, source_target_pairs={{0,4},{4,8},{8,12},{12,16},{16,20},{20,24},{24,28},{28,0},{1,5},{5... | collective-permute-start | bytes 184328 | tf_op jit(solution)/shard_map/ppermute | solution.py:516
  8.3 10.0 %collective-permute-start.1 = (bf16[40,768]{1,0:T(8,128)(2,1)S(1)}, bf16[40,768]{1,0:T(8,128)(2,1)S(1)}, u32[]{:S(2)}, u32[]{:S(2)}) collective-permute-start(bf16[40,768]{1,0:T(8,128)(2,1)S(1)} %get-tuple-element.100), channel_id=1, source_target_pairs={{0,8},{4,12},{8,16},{12,20},{16,24},{20,28},{24,0},{28,4},{1,9},{5... | collective-permute-start | bytes 184328 | tf_op jit(solution)/shard_map/ppermute | solution.py:516
  10.9 11.7 %collective-permute-start.2 = (bf16[40,768]{1,0:T(8,128)(2,1)S(1)}, bf16[40,768]{1,0:T(8,128)(2,1)S(1)}, u32[]{:S(2)}, u32[]{:S(2)}) collective-permute-start(bf16[40,768]{1,0:T(8,128)(2,1)S(1)} %get-tuple-element.101), channel_id=1, source_target_pairs={{0,12},{4,16},{8,20},{12,24},{16,28},{20,0},{24,4},{28,8},{1,13},{... | collective-permute-start | bytes 184328 | tf_op jit(solution)/shard_map/ppermute | solution.py:516
  13.2 9.5 %collective-permute-start.3 = (bf16[40,768]{1,0:T(8,128)(2,1)S(1)}, bf16[40,768]{1,0:T(8,128)(2,1)S(1)}, u32[]{:S(2)}, u32[]{:S(2)}) collective-permute-start(bf16[40,768]{1,0:T(8,128)(2,1)S(1)} %get-tuple-element.102), channel_id=1, source_target_pairs={{0,16},{4,20},{8,24},{12,28},{16,0},{20,4},{24,8},{28,12},{1,17},{... | collective-permute-start | bytes 184328 | tf_op jit(solution)/shard_map/ppermute | solution.py:516
  13.7 8.9 %collective-permute-start.4 = (bf16[40,768]{1,0:T(8,128)(2,1)S(1)}, bf16[40,768]{1,0:T(8,128)(2,1)S(1)}, u32[]{:S(2)}, u32[]{:S(2)}) collective-permute-start(bf16[40,768]{1,0:T(8,128)(2,1)S(1)} %get-tuple-element.103), channel_id=1, source_target_pairs={{0,20},{4,24},{8,28},{12,0},{16,4},{20,8},{24,12},{28,16},{1,21},{... | collective-permute-start | bytes 184328 | tf_op jit(solution)/shard_map/ppermute | solution.py:516
  15.7 7.0 %copy-start.12 = (s32[1,1,1,256]{3,2,1,0:T(1,128)S(1)}, s32[1,1,1,256]{3,2,1,0:T(1,128)}, u32[]{:S(2)}) copy-start(s32[1,1,1,256]{3,2,1,0:T(1,128)} %param.17) | copy-start | bytes 3076
  15.7 7.0 %collective-permute-start.6 = (bf16[40,768]{1,0:T(8,128)(2,1)S(1)}, bf16[40,768]{1,0:T(8,128)(2,1)S(1)}, u32[]{:S(2)}, u32[]{:S(2)}) collective-permute-start(bf16[40,768]{1,0:T(8,128)(2,1)S(1)} %get-tuple-element.106), channel_id=1, source_target_pairs={{0,24},{4,28},{8,0},{12,4},{16,8},{20,12},{24,16},{28,20},{1,25},{... | collective-permute-start | bytes 184328 | tf_op jit(solution)/shard_map/ppermute | solution.py:516
  18.3 4.4 %collective-permute-start.7 = (bf16[40,768]{1,0:T(8,128)(2,1)S(1)}, bf16[40,768]{1,0:T(8,128)(2,1)S(1)}, u32[]{:S(2)}, u32[]{:S(2)}) collective-permute-start(bf16[40,768]{1,0:T(8,128)(2,1)S(1)} %get-tuple-element.107), channel_id=1, source_target_pairs={{0,28},{4,0},{8,4},{12,8},{16,12},{20,16},{24,20},{28,24},{1,29},{... | collective-permute-start | bytes 184328 | tf_op jit(solution)/shard_map/ppermute | solution.py:516
  23.5 12.8 %collective-permute-start.9 = (bf16[512,768]{1,0:T(8,128)(2,1)S(1)}, bf16[512,768]{1,0:T(8,128)(2,1)S(1)}, u32[]{:S(2)}, u32[]{:S(2)}) collective-permute-start(bf16[512,768]{1,0:T(8,128)(2,1)S(1)} %get-tuple-element.159.refs_4_), channel_id=1, source_target_pairs={{0,1},{1,0},{2,3},{3,2},{4,5},{5,4},{6,7},{7,6},{8,9},{9,8},{10,11... | collective-permute-start | bytes 2359304 | tf_op jit(solution)/shard_map/ppermute | solution.py:451
  23.6 2.8 %copy-start.11 = (bf16[768,384]{1,0:T(8,128)(2,1)S(1)}, bf16[768,384]{1,0:T(8,128)(2,1)}, u32[]{:S(2)}) copy-start(bf16[768,384]{1,0:T(8,128)(2,1)} %wdec_ref.1) | copy-start | bytes 1769476
  23.6 2.8 %copy-start.13 = (s32[1,1,1,256]{3,2,1,0:T(1,128)S(1)}, s32[1,1,1,256]{3,2,1,0:T(1,128)}, u32[]{:S(2)}) copy-start(s32[1,1,1,256]{3,2,1,0:T(1,128)} %param.18) | copy-start | bytes 3076
  24.8 11.5 %collective-permute-start.8 = (bf16[256,768]{1,0:T(8,128)(2,1)S(1)}, bf16[256,768]{1,0:T(8,128)(2,1)S(1)}, u32[]{:S(2)}, u32[]{:S(2)}) collective-permute-start(bf16[256,768]{1,0:T(8,128)(2,1)S(1)} %get-tuple-element.119.normed_ref), channel_id=1, source_target_pairs={{0,2},{1,3},{2,0},{3,1},{4,6},{5,7},{6,4},{7,5},{8,10},{9,11},{10,... | collective-permute-start | bytes 1179656 | tf_op jit(solution)/shard_map/ppermute | solution.py:451
  26.4 25.9 %copy-start.15 = (bf16[384]{0:T(512)(128)(2,1)S(1)}, bf16[384]{0:T(512)(128)(2,1)}, u32[]{:S(2)}) copy-start(bf16[384]{0:T(512)(128)(2,1)} %param.24) | copy-start | bytes 2308
  26.4 27.8 %copy-start.9 = (s32[1,1,1,8,35]{4,3,2,1,0:T(8,128)S(1)}, s32[1,1,1,8,35]{4,3,2,1,0:T(8,128)}, u32[]{:S(2)}) copy-start(s32[1,1,1,8,35]{4,3,2,1,0:T(8,128)} %param.16) | copy-start | bytes 3364
  26.4 27.8 %copy-start.10 = (f32[2,1408]{1,0:T(2,128)S(1)}, f32[2,1408]{1,0:T(2,128)}, u32[]{:S(2)}) copy-start(f32[2,1408]{1,0:T(2,128)} %constant.2.clone.ids_ref) | copy-start | bytes 33796
  36.3 2.4 %collective-permute-start.10 = (bf16[768,256]{1,0:T(8,128)(2,1)S(1)}, bf16[768,256]{1,0:T(8,128)(2,1)S(1)}, u32[]{:S(2)}, u32[]{:S(2)}) collective-permute-start(bf16[768,256]{1,0:T(8,128)(2,1)S(1)} %get-tuple-element.130), channel_id=1, source_target_pairs={{0,1},{1,0},{2,3},{3,2},{4,5},{5,4},{6,7},{7,6},{8,9},{9,8},{10,11... | collective-permute-start | bytes 1179656 | tf_op jit(solution)/shard_map/ppermute | solution.py:451
  36.3 2.4 %collective-permute-start.13 = (bf16[256,768]{1,0:T(8,128)(2,1)S(1)}, bf16[256,768]{1,0:T(8,128)(2,1)S(1)}, u32[]{:S(2)}, u32[]{:S(2)}) collective-permute-start(bf16[256,768]{1,0:T(8,128)(2,1)S(1)} %collective-permute-done.8.refs_6_), channel_id=1, source_target_pairs={{0,1},{1,0},{2,3},{3,2},{4,5},{5,4},{6,7},{7,6},{8,9},{9,8},{10,11... | collective-permute-start | bytes 1179656 | tf_op jit(solution)/shard_map/ppermute | solution.py:451
  36.8 2.3 %collective-permute-start.14 = (bf16[256,768]{1,0:T(8,128)(2,1)S(1)}, bf16[256,768]{1,0:T(8,128)(2,1)S(1)}, u32[]{:S(2)}, u32[]{:S(2)}) collective-permute-start(bf16[256,768]{1,0:T(8,128)(2,1)S(1)} %collective-permute-done.5.refs_8_), channel_id=1, source_target_pairs={{0,1},{1,0},{2,3},{3,2},{4,5},{5,4},{6,7},{7,6},{8,9},{9,8},{10,11... | collective-permute-start | bytes 1179656 | tf_op jit(solution)/shard_map/ppermute | solution.py:451
  36.8 27.3 %collective-permute-start.11 = (bf16[768,256]{1,0:T(8,128)(2,1)S(1)}, bf16[768,256]{1,0:T(8,128)(2,1)S(1)}, u32[]{:S(2)}, u32[]{:S(2)}) collective-permute-start(bf16[768,256]{1,0:T(8,128)(2,1)S(1)} %get-tuple-element.131), channel_id=1, source_target_pairs={{0,2},{1,3},{2,0},{3,1},{4,6},{5,7},{6,4},{7,5},{8,10},{9,11},{10,... | collective-permute-start | bytes 1179656 | tf_op jit(solution)/shard_map/ppermute | solution.py:451
  38.4 25.7 %collective-permute-start.12 = (bf16[768,256]{1,0:T(8,128)(2,1)S(1)}, bf16[768,256]{1,0:T(8,128)(2,1)S(1)}, u32[]{:S(2)}, u32[]{:S(2)}) collective-permute-start(bf16[768,256]{1,0:T(8,128)(2,1)S(1)} %get-tuple-element.132), channel_id=1, source_target_pairs={{0,3},{1,2},{2,1},{3,0},{4,7},{5,6},{6,5},{7,4},{8,11},{9,10},{10,... | collective-permute-start | bytes 1179656 | tf_op jit(solution)/shard_map/ppermute | solution.py:451
  39.2 6.6 %collective-permute-start.15 = (bf16[40,384]{1,0:T(8,128)(2,1)S(1)}, bf16[40,384]{1,0:T(8,128)(2,1)S(1)}, u32[]{:S(2)}, u32[]{:S(2)}) collective-permute-start(bf16[40,384]{1,0:T(8,128)(2,1)S(1)} %get-tuple-element.145), channel_id=1, source_target_pairs={{0,4},{4,8},{8,12},{12,16},{16,20},{20,24},{24,28},{28,0},{1,5},{5... | collective-permute-start | bytes 92168 | tf_op jit(solution)/shard_map/ppermute | solution.py:602
  39.9 7.7 %collective-permute-start.16 = (bf16[40,384]{1,0:T(8,128)(2,1)S(1)}, bf16[40,384]{1,0:T(8,128)(2,1)S(1)}, u32[]{:S(2)}, u32[]{:S(2)}) collective-permute-start(bf16[40,384]{1,0:T(8,128)(2,1)S(1)} %get-tuple-element.146), channel_id=1, source_target_pairs={{0,8},{4,12},{8,16},{12,20},{16,24},{20,28},{24,0},{28,4},{1,9},{5... | collective-permute-start | bytes 92168 | tf_op jit(solution)/shard_map/ppermute | solution.py:602
  43.6 4.8 %collective-permute-start.17 = (bf16[40,384]{1,0:T(8,128)(2,1)S(1)}, bf16[40,384]{1,0:T(8,128)(2,1)S(1)}, u32[]{:S(2)}, u32[]{:S(2)}) collective-permute-start(bf16[40,384]{1,0:T(8,128)(2,1)S(1)} %get-tuple-element.147), channel_id=1, source_target_pairs={{0,12},{4,16},{8,20},{12,24},{16,28},{20,0},{24,4},{28,8},{1,13},{... | collective-permute-start | bytes 92168 | tf_op jit(solution)/shard_map/ppermute | solution.py:602
  45.8 4.5 %collective-permute-start.18 = (bf16[40,384]{1,0:T(8,128)(2,1)S(1)}, bf16[40,384]{1,0:T(8,128)(2,1)S(1)}, u32[]{:S(2)}, u32[]{:S(2)}) collective-permute-start(bf16[40,384]{1,0:T(8,128)(2,1)S(1)} %get-tuple-element.148), channel_id=1, source_target_pairs={{0,16},{4,20},{8,24},{12,28},{16,0},{20,4},{24,8},{28,12},{1,17},{... | collective-permute-start | bytes 92168 | tf_op jit(solution)/shard_map/ppermute | solution.py:602
  47.6 5.8 %collective-permute-start.19 = (bf16[40,384]{1,0:T(8,128)(2,1)S(1)}, bf16[40,384]{1,0:T(8,128)(2,1)S(1)}, u32[]{:S(2)}, u32[]{:S(2)}) collective-permute-start(bf16[40,384]{1,0:T(8,128)(2,1)S(1)} %get-tuple-element.149), channel_id=1, source_target_pairs={{0,20},{4,24},{8,28},{12,0},{16,4},{20,8},{24,12},{28,16},{1,21},{... | collective-permute-start | bytes 92168 | tf_op jit(solution)/shard_map/ppermute | solution.py:602
  48.4 5.5 %collective-permute-start.20 = (bf16[40,384]{1,0:T(8,128)(2,1)S(1)}, bf16[40,384]{1,0:T(8,128)(2,1)S(1)}, u32[]{:S(2)}, u32[]{:S(2)}) collective-permute-start(bf16[40,384]{1,0:T(8,128)(2,1)S(1)} %get-tuple-element.150), channel_id=1, source_target_pairs={{0,24},{4,28},{8,0},{12,4},{16,8},{20,12},{24,16},{28,20},{1,25},{... | collective-permute-start | bytes 92168 | tf_op jit(solution)/shard_map/ppermute | solution.py:602
  50.3 3.9 %collective-permute-start.21 = (bf16[40,384]{1,0:T(8,128)(2,1)S(1)}, bf16[40,384]{1,0:T(8,128)(2,1)S(1)}, u32[]{:S(2)}, u32[]{:S(2)}) collective-permute-start(bf16[40,384]{1,0:T(8,128)(2,1)S(1)} %get-tuple-element.151), channel_id=1, source_target_pairs={{0,28},{4,0},{8,4},{12,8},{16,12},{20,16},{24,20},{28,24},{1,29},{... | collective-permute-start | bytes 92168 | tf_op jit(solution)/shard_map/ppermute | solution.py:602
  55.7 6.5 %collective-permute-start.22 = (bf16[96,384]{1,0:T(8,128)(2,1)S(1)}, bf16[96,384]{1,0:T(8,128)(2,1)S(1)}, u32[]{:S(2)}, u32[]{:S(2)}) collective-permute-start(bf16[96,384]{1,0:T(8,128)(2,1)S(1)} %get-tuple-element.152), channel_id=1, source_target_pairs={{0,4},{4,8},{8,12},{12,0},{1,5},{5,9},{9,13},{13,1},{2,6},{6,10},{... | collective-permute-start | bytes 221192 | tf_op jit(solution)/shard_map/ppermute | solution.py:456
  57.1 5.1 %collective-permute-start.23 = (bf16[96,384]{1,0:T(8,128)(2,1)S(1)}, bf16[96,384]{1,0:T(8,128)(2,1)S(1)}, u32[]{:S(2)}, u32[]{:S(2)}) collective-permute-start(bf16[96,384]{1,0:T(8,128)(2,1)S(1)} %get-tuple-element.153), channel_id=1, source_target_pairs={{0,12},{4,0},{8,4},{12,8},{1,13},{5,1},{9,5},{13,9},{2,14},{6,2},{... | collective-permute-start | bytes 221192 | tf_op jit(solution)/shard_map/ppermute | solution.py:456
  62.2 5.8 %collective-permute-start.25 = (bf16[128,384]{1,0:T(8,128)(2,1)S(1)}, bf16[128,384]{1,0:T(8,128)(2,1)S(1)}, u32[]{:S(2)}, u32[]{:S(2)}) collective-permute-start(bf16[128,384]{1,0:T(8,128)(2,1)S(1)} %rim.1), channel_id=1, source_target_pairs={{0,16},{16,0},{1,17},{17,1},{2,18},{18,2},{3,19},{19,3},{4,20},{20... | collective-permute-start | bytes 294920 | tf_op jit(solution)/shard_map/ppermute | solution.py:456
  65.2 4.7 %copy-start.7 = (f32[7,7,384]{2,1,0:T(8,128)S(1)}, f32[7,7,384]{2,1,0:T(8,128)}, u32[]{:S(2)}) copy-start(f32[7,7,384]{2,1,0:T(8,128)} %refs_0_.1) | copy-start | bytes 225796
  65.2 12.1 %collective-permute-start.24 = (bf16[4,96,384]{2,1,0:T(8,128)(2,1)S(1)}, bf16[4,96,384]{2,1,0:T(8,128)(2,1)S(1)}, u32[]{:S(2)}, u32[]{:S(2)}) collective-permute-start(bf16[4,96,384]{2,1,0:T(8,128)(2,1)S(1)} %get-tuple-element.166), channel_id=1, source_target_pairs={{0,16},{16,0},{1,17},{17,1},{2,18},{18,2},{3,19},{19,3},{4,20},{20... | collective-permute-start | bytes 884744 | tf_op jit(solution)/shard_map/ppermute | solution.py:456
  68.0 14.3 %collective-permute-start.29 = (bf16[4,96,384]{2,1,0:T(8,128)(2,1)S(1)}, bf16[4,96,384]{2,1,0:T(8,128)(2,1)S(1)}, u32[]{:S(2)}, u32[]{:S(2)}) collective-permute-start(bf16[4,96,384]{2,1,0:T(8,128)(2,1)S(1)} %get-tuple-element.178), channel_id=1, source_target_pairs={{0,16},{16,0},{1,17},{17,1},{2,18},{18,2},{3,19},{19,3},{4,20},{20... | collective-permute-start | bytes 884744 | tf_op jit(solution)/shard_map/ppermute | solution.py:456
  69.8 16.5 %copy-start.3 = (bf16[384,768]{1,0:T(8,128)(2,1)S(1)}, bf16[384,768]{1,0:T(8,128)(2,1)}, u32[]{:S(2)}) copy-start(bf16[384,768]{1,0:T(8,128)(2,1)} %up_ref.1) | copy-start | bytes 1769476
  69.8 16.5 %copy-start.4 = (bf16[768,384]{1,0:T(8,128)(2,1)S(1)}, bf16[768,384]{1,0:T(8,128)(2,1)}, u32[]{:S(2)}) copy-start(bf16[768,384]{1,0:T(8,128)(2,1)} %down_ref.1) | copy-start | bytes 1769476
  69.8 16.5 %copy-start.6 = (bf16[384,128]{1,0:T(8,128)(2,1)S(1)}, bf16[384,128]{1,0:T(8,128)(2,1)}, u32[]{:S(2)}) copy-start(bf16[384,128]{1,0:T(8,128)(2,1)} %head_ref.1) | copy-start | bytes 294916
  77.4 6.3 %collective-permute-start.26 = (bf16[96,384]{1,0:T(8,128)(2,1)S(1)}, bf16[96,384]{1,0:T(8,128)(2,1)S(1)}, u32[]{:S(2)}, u32[]{:S(2)}) collective-permute-start(bf16[96,384]{1,0:T(8,128)(2,1)S(1)} %get-tuple-element.174), channel_id=1, source_target_pairs={{0,4},{4,8},{8,12},{12,0},{1,5},{5,9},{9,13},{13,1},{2,6},{6,10},{... | collective-permute-start | bytes 221192 | tf_op jit(solution)/shard_map/ppermute | solution.py:456
  78.1 11.6 %collective-permute-start.27 = (bf16[96,384]{1,0:T(8,128)(2,1)S(1)}, bf16[96,384]{1,0:T(8,128)(2,1)S(1)}, u32[]{:S(2)}, u32[]{:S(2)}) collective-permute-start(bf16[96,384]{1,0:T(8,128)(2,1)S(1)} %get-tuple-element.175), channel_id=1, source_target_pairs={{0,8},{4,12},{8,0},{12,4},{1,9},{5,13},{9,1},{13,5},{2,10},{6,14},... | collective-permute-start | bytes 221192 | tf_op jit(solution)/shard_map/ppermute | solution.py:456
  81.4 8.3 %collective-permute-start.28 = (bf16[96,384]{1,0:T(8,128)(2,1)S(1)}, bf16[96,384]{1,0:T(8,128)(2,1)S(1)}, u32[]{:S(2)}, u32[]{:S(2)}) collective-permute-start(bf16[96,384]{1,0:T(8,128)(2,1)S(1)} %get-tuple-element.176), channel_id=1, source_target_pairs={{0,12},{4,0},{8,4},{12,8},{1,13},{5,1},{9,5},{13,9},{2,14},{6,2},{... | collective-permute-start | bytes 221192 | tf_op jit(solution)/shard_map/ppermute | solution.py:456
  82.4 7.4 %collective-permute-start.30 = (bf16[96,384]{1,0:T(8,128)(2,1)S(1)}, bf16[96,384]{1,0:T(8,128)(2,1)S(1)}, u32[]{:S(2)}, u32[]{:S(2)}) collective-permute-start(bf16[96,384]{1,0:T(8,128)(2,1)S(1)} %get-tuple-element.182), channel_id=1, source_target_pairs={{0,4},{4,8},{8,12},{12,0},{1,5},{5,9},{9,13},{13,1},{2,6},{6,10},{... | collective-permute-start | bytes 221192 | tf_op jit(solution)/shard_map/ppermute | solution.py:456
  83.6 6.6 %collective-permute-start.31 = (bf16[96,384]{1,0:T(8,128)(2,1)S(1)}, bf16[96,384]{1,0:T(8,128)(2,1)S(1)}, u32[]{:S(2)}, u32[]{:S(2)}) collective-permute-start(bf16[96,384]{1,0:T(8,128)(2,1)S(1)} %get-tuple-element.183), channel_id=1, source_target_pairs={{0,8},{4,12},{8,0},{12,4},{1,9},{5,13},{9,1},{13,5},{2,10},{6,14},... | collective-permute-start | bytes 221192 | tf_op jit(solution)/shard_map/ppermute | solution.py:456
  83.7 6.5 %collective-permute-start.32 = (bf16[96,384]{1,0:T(8,128)(2,1)S(1)}, bf16[96,384]{1,0:T(8,128)(2,1)S(1)}, u32[]{:S(2)}, u32[]{:S(2)}) collective-permute-start(bf16[96,384]{1,0:T(8,128)(2,1)S(1)} %get-tuple-element.184), channel_id=1, source_target_pairs={{0,12},{4,0},{8,4},{12,8},{1,13},{5,1},{9,5},{13,9},{2,14},{6,2},{... | collective-permute-start | bytes 221192 | tf_op jit(solution)/shard_map/ppermute | solution.py:456
  90.2 5.2 %collective-permute-start.34 = (bf16[96,768]{1,0:T(8,128)(2,1)S(1)}, bf16[96,768]{1,0:T(8,128)(2,1)S(1)}, u32[]{:S(2)}, u32[]{:S(2)}) collective-permute-start(bf16[96,768]{1,0:T(8,128)(2,1)S(1)} %close.1.own_ref), channel_id=1, source_target_pairs={{0,2},{1,3},{2,0},{3,1},{4,6},{5,7},{6,4},{7,5},{8,10},{9,11},{10,... | collective-permute-start | bytes 442376 | tf_op jit(solution)/shard_map/ppermute | solution.py:451
  91.8 3.6 %collective-permute-start.33 = (bf16[96,768]{1,0:T(8,128)(2,1)S(1)}, bf16[96,768]{1,0:T(8,128)(2,1)S(1)}, u32[]{:S(2)}, u32[]{:S(2)}) collective-permute-start(bf16[96,768]{1,0:T(8,128)(2,1)S(1)} %close.1.own_ref), channel_id=1, source_target_pairs={{0,1},{1,0},{2,3},{3,2},{4,5},{5,4},{6,7},{7,6},{8,9},{9,8},{10,11... | collective-permute-start | bytes 442376 | tf_op jit(solution)/shard_map/ppermute | solution.py:451
  95.4 1.4 %collective-permute-start.35 = (bf16[96,768]{1,0:T(8,128)(2,1)S(1)}, bf16[96,768]{1,0:T(8,128)(2,1)S(1)}, u32[]{:S(2)}, u32[]{:S(2)}) collective-permute-start(bf16[96,768]{1,0:T(8,128)(2,1)S(1)} %collective-permute-done.34.two_ref), channel_id=1, source_target_pairs={{0,1},{1,0},{2,3},{3,2},{4,5},{5,4},{6,7},{7,6},{8,9},{9,8},{10,11... | collective-permute-start | bytes 442376 | tf_op jit(solution)/shard_map/ppermute | solution.py:451
  (4 other events, 6.9 us)

commit v14 on v13

--- a/solution.py
+++ b/solution.py
@@ -550,7 +550,6 @@
     )(enc_src.reshape(1, rows), cotangent, *arrived)
     if fast:
         normed_y = flip(normed, "replica", 2)
-        both_c = flip(both, "replica", 1)
     units, lengths, values = call(
         project_kernel,
         "project",
@@ -562,6 +561,8 @@
         cost=2000000000,
     )(normed, w_qkv_t)
 
+    if fast:
+        both_c = flip(tie(both, lengths), "replica", 1)
     sends = group if turned else 1
     outs = call(
         functools.partial(encode_kernel, split, sends),

time: 98.2 us -> 98.2 us (level)
  transfers between devices with their start and end apart: 36 -> 36, of which waited for: 13 -> 13; matrix products, arithmetic and copies ran while one was open for 0% -> 0% of each run, Pallas kernels for 26% -> 25%
where the time goes in v14:
time: 98.2 us; the launch traced here: 98 us
  starting transfers between devices  49.4 us (50%)
  Pallas kernels  27.6 us (28%)
  waiting for transfers between devices  15.9 us (16%)
  local copies, waits for them, and re-layouts  4.16 us (4%)
    ppermute x11, starting transfers between devices, turn(): lax.ppermute(value, axis, [(i, (i + k) % count) for i in range(count)])  17.1 us
    ppermute x7, starting transfers between devices, body(): arrived.append(lax.ppermute(outgoing[k], ('eta', 'phi'), pairs))  12.9 us
    ppermute x7, starting transfers between devices, body(): returned.append(lax.ppermute(outbound[k], ('eta', 'phi'), pairs))  10.7 us
    ppermute x11, starting transfers between devices, flip(): lax.ppermute(value, axis, [(i, i ^ bit) for i in range(lax.axis_size(axis...  8.66 us
    pallas_call x1, Pallas kernels, body(): call(functools.partial(encode_kernel, split, sends), 'encode', [sds((slot...  7.97 us
    pallas_call x1, Pallas kernels, body(): call(functools.partial(mix_folded if folded else mix_open, (eta_cells, ph...  7.46 us
    ppermute x11, waiting for transfers between devices, flip(): lax.ppermute(value, axis, [(i, i ^ bit) for i in range(lax.axis_size(axis...  7.39 us
    ppermute x7, waiting for transfers between devices, body(): returned.append(lax.ppermute(outbound[k], ('eta', 'phi'), pairs))  4.31 us
  transfers between devices with their start and end apart: 36, of which 13 were waited for; matrix products, arithmetic and copies ran while one was open for 0% of the time, Pallas kernels for 25%

profile of v14, /device:TPU:0, one launch (start us, length us, event | category | flops | bytes accessed | tf_op | source)
XLA Modules:
  0.0 98.0 jit_solution(9856278931711479078)
XLA Ops:
  0.6 3.0 %collective-permute-start.5 = (bf16[256,768]{1,0:T(8,128)(2,1)}, bf16[256,768]{1,0:T(8,128)(2,1)S(1)}, u32[]{:S(2)}, u32[]{:S(2)}) collective-permute-start(bf16[256,768]{1,0:T(8,128)(2,1)} %bitcast.7), channel_id=1, source_target_pairs={{0,2},{1,3},{2,0},{3,1},{4,6},{5,7},{6,4},{7,5},{8,10},{9,11},{10,... | collective-permute-start | bytes 1179656 | tf_op jit(solution)/shard_map/ppermute | solution.py:451
  3.7 1.4 %copy-done.1 = bf16[1,32,32,768]{3,2,1,0:T(8,128)(2,1)S(1)} copy-done((bf16[1,32,32,768]{3,2,1,0:T(8,128)(2,1)S(1)}, bf16[1,32,32,768]{3,2,1,0:T(8,128)(2,1)}, u32[]{:S(2)}) %copy-start.1) | copy-done | bytes 1572888
  5.1 0.7 copy-done.8
  5.8 0.9 pick.1
  6.7 1.6 %collective-permute-start = (bf16[40,768]{1,0:T(8,128)(2,1)S(1)}, bf16[40,768]{1,0:T(8,128)(2,1)S(1)}, u32[]{:S(2)}, u32[]{:S(2)}) collective-permute-start(bf16[40,768]{1,0:T(8,128)(2,1)S(1)} %get-tuple-element.100), channel_id=1, source_target_pairs={{0,4},{4,8},{8,12},{12,16},{16,20},{20,24},{24,28},{28,0},{1,5},{5... | collective-permute-start | bytes 184328 | tf_op jit(solution)/shard_map/ppermute | solution.py:516
  8.3 2.6 %collective-permute-start.1 = (bf16[40,768]{1,0:T(8,128)(2,1)S(1)}, bf16[40,768]{1,0:T(8,128)(2,1)S(1)}, u32[]{:S(2)}, u32[]{:S(2)}) collective-permute-start(bf16[40,768]{1,0:T(8,128)(2,1)S(1)} %get-tuple-element.101), channel_id=1, source_target_pairs={{0,8},{4,12},{8,16},{12,20},{16,24},{20,28},{24,0},{28,4},{1,9},{5... | collective-permute-start | bytes 184328 | tf_op jit(solution)/shard_map/ppermute | solution.py:516
  10.9 2.3 %collective-permute-start.2 = (bf16[40,768]{1,0:T(8,128)(2,1)S(1)}, bf16[40,768]{1,0:T(8,128)(2,1)S(1)}, u32[]{:S(2)}, u32[]{:S(2)}) collective-permute-start(bf16[40,768]{1,0:T(8,128)(2,1)S(1)} %get-tuple-element.102), channel_id=1, source_target_pairs={{0,12},{4,16},{8,20},{12,24},{16,28},{20,0},{24,4},{28,8},{1,13},{... | collective-permute-start | bytes 184328 | tf_op jit(solution)/shard_map/ppermute | solution.py:516
  13.2 0.5 collective-permute-start.3
  13.7 2.0 %collective-permute-start.4 = (bf16[40,768]{1,0:T(8,128)(2,1)S(1)}, bf16[40,768]{1,0:T(8,128)(2,1)S(1)}, u32[]{:S(2)}, u32[]{:S(2)}) collective-permute-start(bf16[40,768]{1,0:T(8,128)(2,1)S(1)} %get-tuple-element.104), channel_id=1, source_target_pairs={{0,20},{4,24},{8,28},{12,0},{16,4},{20,8},{24,12},{28,16},{1,21},{... | collective-permute-start | bytes 184328 | tf_op jit(solution)/shard_map/ppermute | solution.py:516
  15.7 2.6 %collective-permute-start.6 = (bf16[40,768]{1,0:T(8,128)(2,1)S(1)}, bf16[40,768]{1,0:T(8,128)(2,1)S(1)}, u32[]{:S(2)}, u32[]{:S(2)}) collective-permute-start(bf16[40,768]{1,0:T(8,128)(2,1)S(1)} %get-tuple-element.107), channel_id=1, source_target_pairs={{0,24},{4,28},{8,0},{12,4},{16,8},{20,12},{24,16},{28,20},{1,25},{... | collective-permute-start | bytes 184328 | tf_op jit(solution)/shard_map/ppermute | solution.py:516
  18.3 1.3 %collective-permute-start.7 = (bf16[40,768]{1,0:T(8,128)(2,1)S(1)}, bf16[40,768]{1,0:T(8,128)(2,1)S(1)}, u32[]{:S(2)}, u32[]{:S(2)}) collective-permute-start(bf16[40,768]{1,0:T(8,128)(2,1)S(1)} %get-tuple-element.108), channel_id=1, source_target_pairs={{0,28},{4,0},{8,4},{12,8},{16,12},{20,16},{24,20},{28,24},{1,29},{... | collective-permute-start | bytes 184328 | tf_op jit(solution)/shard_map/ppermute | solution.py:516
  19.6 2.0 %copy-done = bf16[768,2304]{1,0:T(8,128)(2,1)S(1)} copy-done((bf16[768,2304]{1,0:T(8,128)(2,1)S(1)}, bf16[768,2304]{1,0:T(8,128)(2,1)}, u32[]{:S(2)}) %copy-start) | copy-done | bytes 3538968
  21.6 1.0 %prep.1 = (bf16[768,256]{1,0:T(8,128)(2,1)S(1)}, bf16[2304,768]{1,0:T(8,128)(2,1)S(1)}) custom-call(bf16[256,768]{1,0:T(8,128)(2,1)S(1)} %bitcast.8, bf16[768,768]{1,0:T(8,128)(2,1)S(1)} %copy-done.2, bf16[768,2304]{1,0:T(8,128)(2,1)S(1)} %copy-done), custom_call_target="tpu_custom_call" | custom-call | flops 1000 | bytes 1003 | tf_op jit(solution)/shard_map/prep/pallas_call | solution.py:530
  22.7 0.8 norm.1
  23.5 1.1 %project.1 = (f32[1536,256]{1,0:T(8,128)S(1)}, f32[24,256]{1,0:T(8,128)S(1)}, bf16[768,256]{1,0:T(8,128)(2,1)S(1)}) custom-call(bf16[256,768]{1,0:T(8,128)(2,1)S(1)} %get-tuple-element.120.normed_ref, bf16[2304,768]{1,0:T(8,128)(2,1)S(1)} %get-tuple-element.109.wqkv_t_ref), custom_call_target="tpu_custom_call" | custom-call | flops 2000000000 | bytes 6667666 | tf_op jit(solution)/shard_map/project/pallas_call | solution.py:553
  24.8 1.6 %collective-permute-start.8 = (bf16[256,768]{1,0:T(8,128)(2,1)S(1)}, bf16[256,768]{1,0:T(8,128)(2,1)S(1)}, u32[]{:S(2)}, u32[]{:S(2)}) collective-permute-start(bf16[256,768]{1,0:T(8,128)(2,1)S(1)} %get-tuple-element.120.normed_ref), channel_id=1, source_target_pairs={{0,2},{1,3},{2,0},{3,1},{4,6},{5,7},{6,4},{7,5},{8,10},{9,11},{10,... | collective-permute-start | bytes 1179656 | tf_op jit(solution)/shard_map/ppermute | solution.py:451
  26.4 8.0 %encode.1 = (bf16[40,384]{1,0:T(8,128)(2,1)S(1)}, bf16[40,384]{1,0:T(8,128)(2,1)S(1)}, bf16[40,384]{1,0:T(8,128)(2,1)S(1)}, bf16[40,384]{1,0:T(8,128)(2,1)S(1)},...) custom-call(s32[1,256]{1,0:T(1,128)S(1)} %bitcast.13, ...), custom_call_target="tpu_custom_call" | custom-call | flops 8000000000 | bytes 26667666 | tf_op jit(solution)/shard_map/encode/pallas_call | solution.py:567
  34.4 1.9 %collective-permute-done.8.refs_6_ = bf16[256,768]{1,0:T(8,128)(2,1)S(1)} collective-permute-done((bf16[256,768]{1,0:T(8,128)(2,1)S(1)}, bf16[256,768]{1,0:T(8,128)(2,1)S(1)}, u32[]{:S(2)}, u32[]{:S(2)}) %collective-permute-start.8) | collective-permute-done | bytes 393248 | tf_op jit(solution)/shard_map/ppermute | solution.py:451
  36.3 0.5 collective-permute-start.13
  36.8 1.5 %collective-permute-start.11 = (bf16[768,256]{1,0:T(8,128)(2,1)S(1)}, bf16[768,256]{1,0:T(8,128)(2,1)S(1)}, u32[]{:S(2)}, u32[]{:S(2)}) collective-permute-start(bf16[768,256]{1,0:T(8,128)(2,1)S(1)} %get-tuple-element.133), channel_id=1, source_target_pairs={{0,2},{1,3},{2,0},{3,1},{4,6},{5,7},{6,4},{7,5},{8,10},{9,11},{10,... | collective-permute-start | bytes 1179656 | tf_op jit(solution)/shard_map/ppermute | solution.py:451
  39.1 0.7 collective-permute-start.15
  39.9 3.7 %collective-permute-start.16 = (bf16[40,384]{1,0:T(8,128)(2,1)S(1)}, bf16[40,384]{1,0:T(8,128)(2,1)S(1)}, u32[]{:S(2)}, u32[]{:S(2)}) collective-permute-start(bf16[40,384]{1,0:T(8,128)(2,1)S(1)} %get-tuple-element.148), channel_id=1, source_target_pairs={{0,8},{4,12},{8,16},{12,20},{16,24},{20,28},{24,0},{28,4},{1,9},{5... | collective-permute-start | bytes 92168 | tf_op jit(solution)/shard_map/ppermute | solution.py:603
  43.9 1.9 %collective-permute-done.15.refs_1_ = bf16[40,384]{1,0:T(8,128)(2,1)S(1)} collective-permute-done((bf16[40,384]{1,0:T(8,128)(2,1)S(1)}, bf16[40,384]{1,0:T(8,128)(2,1)S(1)}, u32[]{:S(2)}, u32[]{:S(2)}) %collective-permute-start.15) | collective-permute-done | bytes 30752 | tf_op jit(solution)/shard_map/ppermute | solution.py:603
  45.8 1.8 %collective-permute-start.18 = (bf16[40,384]{1,0:T(8,128)(2,1)S(1)}, bf16[40,384]{1,0:T(8,128)(2,1)S(1)}, u32[]{:S(2)}, u32[]{:S(2)}) collective-permute-start(bf16[40,384]{1,0:T(8,128)(2,1)S(1)} %get-tuple-element.150), channel_id=1, source_target_pairs={{0,16},{4,20},{8,24},{12,28},{16,0},{20,4},{24,8},{28,12},{1,17},{... | collective-permute-start | bytes 92168 | tf_op jit(solution)/shard_map/ppermute | solution.py:603
  47.9 0.5 collective-permute-done.17.refs_3_
  48.4 1.9 %collective-permute-start.20 = (bf16[40,384]{1,0:T(8,128)(2,1)S(1)}, bf16[40,384]{1,0:T(8,128)(2,1)S(1)}, u32[]{:S(2)}, u32[]{:S(2)}) collective-permute-start(bf16[40,384]{1,0:T(8,128)(2,1)S(1)} %get-tuple-element.152), channel_id=1, source_target_pairs={{0,24},{4,28},{8,0},{12,4},{16,8},{20,12},{24,16},{28,20},{1,25},{... | collective-permute-start | bytes 92168 | tf_op jit(solution)/shard_map/ppermute | solution.py:603
  50.3 1.9 %collective-permute-start.21 = (bf16[40,384]{1,0:T(8,128)(2,1)S(1)}, bf16[40,384]{1,0:T(8,128)(2,1)S(1)}, u32[]{:S(2)}, u32[]{:S(2)}) collective-permute-start(bf16[40,384]{1,0:T(8,128)(2,1)S(1)} %get-tuple-element.153), channel_id=1, source_target_pairs={{0,28},{4,0},{8,4},{12,8},{16,12},{20,16},{24,20},{28,24},{1,29},{... | collective-permute-start | bytes 92168 | tf_op jit(solution)/shard_map/ppermute | solution.py:603
  52.2 1.1 %collective-permute-done.19.refs_5_ = bf16[40,384]{1,0:T(8,128)(2,1)S(1)} collective-permute-done((bf16[40,384]{1,0:T(8,128)(2,1)S(1)}, bf16[40,384]{1,0:T(8,128)(2,1)S(1)}, u32[]{:S(2)}, u32[]{:S(2)}) %collective-permute-start.19) | collective-permute-done | bytes 30752 | tf_op jit(solution)/shard_map/ppermute | solution.py:603
  54.2 1.5 %fill.1 = (bf16[1024,384]{1,0:T(8,128)(2,1)S(1)}, bf16[96,384]{1,0:T(8,128)(2,1)S(1)}, bf16[96,384]{1,0:T(8,128)(2,1)S(1)}, bf16[96,384]{1,0:T(8,128)(2,1)S(1)}) custom-call(s32[8,35]{1,0:T(8,128)S(1)} %bitcast.11, f32[2,1408]{1,0:T(2,128)S(1)} %copy-done.10, bf16[1,384]{1,0:T(2,128)(2,1)S(1)} %reshape.31.mask_ref, ...), custom_call_target="tpu_custom_call" | custom-call | flops 1000 | bytes 1003 | tf_op jit(solution)/shard_map/fill/pallas_call | solution.py:632
  55.7 1.4 %collective-permute-start.22 = (bf16[96,384]{1,0:T(8,128)(2,1)S(1)}, bf16[96,384]{1,0:T(8,128)(2,1)S(1)}, u32[]{:S(2)}, u32[]{:S(2)}) collective-permute-start(bf16[96,384]{1,0:T(8,128)(2,1)S(1)} %get-tuple-element.154), channel_id=1, source_target_pairs={{0,4},{4,8},{8,12},{12,0},{1,5},{5,9},{9,13},{13,1},{2,6},{6,10},{... | collective-permute-start | bytes 221192 | tf_op jit(solution)/shard_map/ppermute | solution.py:456
  57.0 3.0 %collective-permute-start.23 = (bf16[96,384]{1,0:T(8,128)(2,1)S(1)}, bf16[96,384]{1,0:T(8,128)(2,1)S(1)}, u32[]{:S(2)}, u32[]{:S(2)}) collective-permute-start(bf16[96,384]{1,0:T(8,128)(2,1)S(1)} %get-tuple-element.155), channel_id=1, source_target_pairs={{0,12},{4,0},{8,4},{12,8},{1,13},{5,1},{9,5},{13,9},{2,14},{6,2},{... | collective-permute-start | bytes 221192 | tf_op jit(solution)/shard_map/ppermute | solution.py:456
  60.0 2.2 %collective-permute-done.22.left_ref.left = bf16[96,384]{1,0:T(8,128)(2,1)S(1)} collective-permute-done((bf16[96,384]{1,0:T(8,128)(2,1)S(1)}, bf16[96,384]{1,0:T(8,128)(2,1)S(1)}, u32[]{:S(2)}, u32[]{:S(2)}) %collective-permute-start.22) | collective-permute-done | bytes 73760 | tf_op jit(solution)/shard_map/ppermute | solution.py:456
  62.2 1.9 %collective-permute-start.25 = (bf16[128,384]{1,0:T(8,128)(2,1)S(1)}, bf16[128,384]{1,0:T(8,128)(2,1)S(1)}, u32[]{:S(2)}, u32[]{:S(2)}) collective-permute-start(bf16[128,384]{1,0:T(8,128)(2,1)S(1)} %rim.1), channel_id=1, source_target_pairs={{0,16},{16,0},{1,17},{17,1},{2,18},{18,2},{3,19},{19,3},{4,20},{20... | collective-permute-start | bytes 294920 | tf_op jit(solution)/shard_map/ppermute | solution.py:456
  64.1 1.1 %terms0.1 = (f32[4,96,384]{2,1,0:T(8,128)S(1)}, bf16[4,96,384]{2,1,0:T(8,128)(2,1)S(1)}) custom-call(bf16[768,256]{1,0:T(8,128)(2,1)S(1)} %get-tuple-element.157.refs_0_, bf16[768,256]{1,0:T(8,128)(2,1)S(1)} %collective-permute-done.10.refs_1_, bf16[768,256]{1,0:T(8,128)(2,1)S(1)} %collective-permute-done.11.refs_2_, ...), custom_call_target="tpu_custom_call" | custom-call | flops 1000 | bytes 1003 | tf_op jit(solution)/shard_map/terms0/pallas_call | solution.py:683
  65.5 1.1 %terms1.1 = (f32[4,96,384]{2,1,0:T(8,128)S(1)}, bf16[4,96,384]{2,1,0:T(8,128)(2,1)S(1)}) custom-call(bf16[768,256]{1,0:T(8,128)(2,1)S(1)} %get-tuple-element.157.refs_0_, bf16[768,256]{1,0:T(8,128)(2,1)S(1)} %collective-permute-done.10.refs_1_, bf16[768,256]{1,0:T(8,128)(2,1)S(1)} %collective-permute-done.11.refs_2_, ...), custom_call_target="tpu_custom_call" | custom-call | flops 1000 | bytes 1003 | tf_op jit(solution)/shard_map/terms1/pallas_call | solution.py:683
  66.6 1.5 %collective-permute-done.25.a = bf16[128,384]{1,0:T(8,128)(2,1)S(1)} collective-permute-done((bf16[128,384]{1,0:T(8,128)(2,1)S(1)}, bf16[128,384]{1,0:T(8,128)(2,1)S(1)}, u32[]{:S(2)}, u32[]{:S(2)}) %collective-permute-start.25) | collective-permute-done | bytes 98336 | tf_op jit(solution)/shard_map/ppermute | solution.py:456
  68.0 1.8 %collective-permute-start.29 = (bf16[4,96,384]{2,1,0:T(8,128)(2,1)S(1)}, bf16[4,96,384]{2,1,0:T(8,128)(2,1)S(1)}, u32[]{:S(2)}, u32[]{:S(2)}) collective-permute-start(bf16[4,96,384]{2,1,0:T(8,128)(2,1)S(1)} %get-tuple-element.180), channel_id=1, source_target_pairs={{0,16},{16,0},{1,17},{17,1},{2,18},{18,2},{3,19},{19,3},{4,20},{20... | collective-permute-start | bytes 884744 | tf_op jit(solution)/shard_map/ppermute | solution.py:456
  69.8 7.5 %mix.1.normed_ref = bf16[1024,384]{1,0:T(8,128)(2,1)S(1)} custom-call(bf16[1024,384]{1,0:T(8,128)(2,1)S(1)} %get-tuple-element.169.grid.grid_ref, bf16[96,384]{1,0:T(8,128)(2,1)S(1)} %collective-permute-done.22.left_ref.left, bf16[96,384]{1,0:T(8,128)(2,1)S(1)} %collective-permute-done.23.right_ref.right, bf16[128,384]{1,0:T(8,128)(2,1)S(1)} %collective-permute-done.25.a, ...), custom_call_target="tpu_custom_call" | custom-call | flops 1000 | bytes 1003 | tf_op jit(solution)/shard_map/mix/pallas_call | solution.py:699
  77.4 0.7 collective-permute-start.26
  78.1 3.3 %collective-permute-start.27 = (bf16[96,384]{1,0:T(8,128)(2,1)S(1)}, bf16[96,384]{1,0:T(8,128)(2,1)S(1)}, u32[]{:S(2)}, u32[]{:S(2)}) collective-permute-start(bf16[96,384]{1,0:T(8,128)(2,1)S(1)} %get-tuple-element.177), channel_id=1, source_target_pairs={{0,8},{4,12},{8,0},{12,4},{1,9},{5,13},{9,1},{13,5},{2,10},{6,14},... | collective-permute-start | bytes 221192 | tf_op jit(solution)/shard_map/ppermute | solution.py:456
  81.4 0.9 collective-permute-start.28
  82.3 1.2 %collective-permute-start.30 = (bf16[96,384]{1,0:T(8,128)(2,1)S(1)}, bf16[96,384]{1,0:T(8,128)(2,1)S(1)}, u32[]{:S(2)}, u32[]{:S(2)}) collective-permute-start(bf16[96,384]{1,0:T(8,128)(2,1)S(1)} %get-tuple-element.184), channel_id=1, source_target_pairs={{0,4},{4,8},{8,12},{12,0},{1,5},{5,9},{9,13},{13,1},{2,6},{6,10},{... | collective-permute-start | bytes 221192 | tf_op jit(solution)/shard_map/ppermute | solution.py:456
  83.6 2.7 %collective-permute-start.32 = (bf16[96,384]{1,0:T(8,128)(2,1)S(1)}, bf16[96,384]{1,0:T(8,128)(2,1)S(1)}, u32[]{:S(2)}, u32[]{:S(2)}) collective-permute-start(bf16[96,384]{1,0:T(8,128)(2,1)S(1)} %get-tuple-element.186), channel_id=1, source_target_pairs={{0,12},{4,0},{8,4},{12,8},{1,13},{5,1},{9,5},{13,9},{2,14},{6,2},{... | collective-permute-start | bytes 221192 | tf_op jit(solution)/shard_map/ppermute | solution.py:456
  86.3 3.4 %feed.1 = f32[1024,128]{1,0:T(8,128)} custom-call(bf16[1024,384]{1,0:T(8,128)(2,1)S(1)} %mix.1.normed_ref, bf16[1024,384]{1,0:T(8,128)(2,1)S(1)} %get-tuple-element.169.grid.grid_ref, bf16[384,768]{1,0:T(8,128)(2,1)S(1)} %copy-done.3, bf16[768,384]{1,0:T(8,128)(2,1)S(1)} %copy-done.4, bf16[384,128]{1,0:T(8,128)(2,1)S(1)} %copy-done.6), custom_call_target="tpu_custom_call" | custom-call | flops 1000 | bytes 1003 | tf_op jit(solution)/shard_map/feed/pallas_call | solution.py:727
  90.2 1.6 %collective-permute-start.34 = (bf16[96,768]{1,0:T(8,128)(2,1)S(1)}, bf16[96,768]{1,0:T(8,128)(2,1)S(1)}, u32[]{:S(2)}, u32[]{:S(2)}) collective-permute-start(bf16[96,768]{1,0:T(8,128)(2,1)S(1)} %close.1.own_ref), channel_id=1, source_target_pairs={{0,2},{1,3},{2,0},{3,1},{4,6},{5,7},{6,4},{7,5},{8,10},{9,11},{10,... | collective-permute-start | bytes 442376 | tf_op jit(solution)/shard_map/ppermute | solution.py:451
  91.8 3.6 %collective-permute-done.34.two_ref = bf16[96,768]{1,0:T(8,128)(2,1)S(1)} collective-permute-done((bf16[96,768]{1,0:T(8,128)(2,1)S(1)}, bf16[96,768]{1,0:T(8,128)(2,1)S(1)}, u32[]{:S(2)}, u32[]{:S(2)}) %collective-permute-start.34) | collective-permute-done | bytes 147488 | tf_op jit(solution)/shard_map/ppermute | solution.py:451
  95.4 1.4 %collective-permute-done.35.three_ref = bf16[96,768]{1,0:T(8,128)(2,1)S(1)} collective-permute-done((bf16[96,768]{1,0:T(8,128)(2,1)S(1)}, bf16[96,768]{1,0:T(8,128)(2,1)S(1)}, u32[]{:S(2)}, u32[]{:S(2)}) %collective-permute-start.35) | collective-permute-done | bytes 147488 | tf_op jit(solution)/shard_map/ppermute | solution.py:451
  96.8 1.2 %spread.1 = f32[384,768]{1,0:T(8,128)} custom-call(bf16[96,768]{1,0:T(8,128)(2,1)S(1)} %close.1.own_ref, bf16[96,768]{1,0:T(8,128)(2,1)S(1)} %collective-permute-done.33.one_ref, bf16[96,768]{1,0:T(8,128)(2,1)S(1)} %collective-permute-done.34.two_ref, bf16[96,768]{1,0:T(8,128)(2,1)S(1)} %collective-permute-done.35.three_ref), custom_call_target="tpu_custom_call" | custom-call | flops 1000 | bytes 1003 | tf_op jit(solution)/shard_map/spread/pallas_call | solution.py:748
  (72 shorter events, 3.5 us)
Async XLA Ops:
  0.6 13.1 %collective-permute-start.5 = (bf16[256,768]{1,0:T(8,128)(2,1)}, bf16[256,768]{1,0:T(8,128)(2,1)S(1)}, u32[]{:S(2)}, u32[]{:S(2)}) collective-permute-start(bf16[256,768]{1,0:T(8,128)(2,1)} %bitcast.7), channel_id=1, source_target_pairs={{0,2},{1,3},{2,0},{3,1},{4,6},{5,7},{6,4},{7,5},{8,10},{9,11},{10,... | collective-permute-start | bytes 1179656 | tf_op jit(solution)/shard_map/ppermute | solution.py:451
  5.8 13.9 %copy-start.2 = (bf16[768,768]{1,0:T(8,128)(2,1)S(1)}, bf16[768,768]{1,0:T(8,128)(2,1)}, u32[]{:S(2)}) copy-start(bf16[768,768]{1,0:T(8,128)(2,1)} %wout_ref.3) | copy-start | bytes 3538948
  5.8 13.9 %copy-start.5 = (bf16[1,1,1,256,768]{4,3,2,1,0:T(8,128)(2,1)S(1)}, bf16[1,1,1,256,768]{4,3,2,1,0:T(8,128)(2,1)}, u32[]{:S(2)}) copy-start(bf16[1,1,1,256,768]{4,3,2,1,0:T(8,128)(2,1)} %param.19) | copy-start | bytes 1179652
  6.7 9.0 %collective-permute-start = (bf16[40,768]{1,0:T(8,128)(2,1)S(1)}, bf16[40,768]{1,0:T(8,128)(2,1)S(1)}, u32[]{:S(2)}, u32[]{:S(2)}) collective-permute-start(bf16[40,768]{1,0:T(8,128)(2,1)S(1)} %get-tuple-element.100), channel_id=1, source_target_pairs={{0,4},{4,8},{8,12},{12,16},{16,20},{20,24},{24,28},{28,0},{1,5},{5... | collective-permute-start | bytes 184328 | tf_op jit(solution)/shard_map/ppermute | solution.py:516
  8.3 10.0 %collective-permute-start.1 = (bf16[40,768]{1,0:T(8,128)(2,1)S(1)}, bf16[40,768]{1,0:T(8,128)(2,1)S(1)}, u32[]{:S(2)}, u32[]{:S(2)}) collective-permute-start(bf16[40,768]{1,0:T(8,128)(2,1)S(1)} %get-tuple-element.101), channel_id=1, source_target_pairs={{0,8},{4,12},{8,16},{12,20},{16,24},{20,28},{24,0},{28,4},{1,9},{5... | collective-permute-start | bytes 184328 | tf_op jit(solution)/shard_map/ppermute | solution.py:516
  10.9 11.7 %collective-permute-start.2 = (bf16[40,768]{1,0:T(8,128)(2,1)S(1)}, bf16[40,768]{1,0:T(8,128)(2,1)S(1)}, u32[]{:S(2)}, u32[]{:S(2)}) collective-permute-start(bf16[40,768]{1,0:T(8,128)(2,1)S(1)} %get-tuple-element.102), channel_id=1, source_target_pairs={{0,12},{4,16},{8,20},{12,24},{16,28},{20,0},{24,4},{28,8},{1,13},{... | collective-permute-start | bytes 184328 | tf_op jit(solution)/shard_map/ppermute | solution.py:516
  13.2 9.5 %collective-permute-start.3 = (bf16[40,768]{1,0:T(8,128)(2,1)S(1)}, bf16[40,768]{1,0:T(8,128)(2,1)S(1)}, u32[]{:S(2)}, u32[]{:S(2)}) collective-permute-start(bf16[40,768]{1,0:T(8,128)(2,1)S(1)} %get-tuple-element.103), channel_id=1, source_target_pairs={{0,16},{4,20},{8,24},{12,28},{16,0},{20,4},{24,8},{28,12},{1,17},{... | collective-permute-start | bytes 184328 | tf_op jit(solution)/shard_map/ppermute | solution.py:516
  13.7 8.9 %collective-permute-start.4 = (bf16[40,768]{1,0:T(8,128)(2,1)S(1)}, bf16[40,768]{1,0:T(8,128)(2,1)S(1)}, u32[]{:S(2)}, u32[]{:S(2)}) collective-permute-start(bf16[40,768]{1,0:T(8,128)(2,1)S(1)} %get-tuple-element.104), channel_id=1, source_target_pairs={{0,20},{4,24},{8,28},{12,0},{16,4},{20,8},{24,12},{28,16},{1,21},{... | collective-permute-start | bytes 184328 | tf_op jit(solution)/shard_map/ppermute | solution.py:516
  15.7 7.0 %copy-start.12 = (s32[1,1,1,256]{3,2,1,0:T(1,128)S(1)}, s32[1,1,1,256]{3,2,1,0:T(1,128)}, u32[]{:S(2)}) copy-start(s32[1,1,1,256]{3,2,1,0:T(1,128)} %param.17) | copy-start | bytes 3076
  15.7 7.0 %collective-permute-start.6 = (bf16[40,768]{1,0:T(8,128)(2,1)S(1)}, bf16[40,768]{1,0:T(8,128)(2,1)S(1)}, u32[]{:S(2)}, u32[]{:S(2)}) collective-permute-start(bf16[40,768]{1,0:T(8,128)(2,1)S(1)} %get-tuple-element.107), channel_id=1, source_target_pairs={{0,24},{4,28},{8,0},{12,4},{16,8},{20,12},{24,16},{28,20},{1,25},{... | collective-permute-start | bytes 184328 | tf_op jit(solution)/shard_map/ppermute | solution.py:516
  18.3 4.4 %collective-permute-start.7 = (bf16[40,768]{1,0:T(8,128)(2,1)S(1)}, bf16[40,768]{1,0:T(8,128)(2,1)S(1)}, u32[]{:S(2)}, u32[]{:S(2)}) collective-permute-start(bf16[40,768]{1,0:T(8,128)(2,1)S(1)} %get-tuple-element.108), channel_id=1, source_target_pairs={{0,28},{4,0},{8,4},{12,8},{16,12},{20,16},{24,20},{28,24},{1,29},{... | collective-permute-start | bytes 184328 | tf_op jit(solution)/shard_map/ppermute | solution.py:516
  23.5 2.9 %copy-start.11 = (bf16[768,384]{1,0:T(8,128)(2,1)S(1)}, bf16[768,384]{1,0:T(8,128)(2,1)}, u32[]{:S(2)}) copy-start(bf16[768,384]{1,0:T(8,128)(2,1)} %wdec_ref.1) | copy-start | bytes 1769476
  23.5 2.9 %copy-start.13 = (s32[1,1,1,256]{3,2,1,0:T(1,128)S(1)}, s32[1,1,1,256]{3,2,1,0:T(1,128)}, u32[]{:S(2)}) copy-start(s32[1,1,1,256]{3,2,1,0:T(1,128)} %param.18) | copy-start | bytes 3076
  24.7 11.6 %collective-permute-start.9 = (bf16[512,768]{1,0:T(8,128)(2,1)S(1)}, bf16[512,768]{1,0:T(8,128)(2,1)S(1)}, u32[]{:S(2)}, u32[]{:S(2)}) collective-permute-start(bf16[512,768]{1,0:T(8,128)(2,1)S(1)} %get-tuple-element.161.refs_4_), channel_id=1, source_target_pairs={{0,1},{1,0},{2,3},{3,2},{4,5},{5,4},{6,7},{7,6},{8,9},{9,8},{10,11... | collective-permute-start | bytes 2359304 | tf_op jit(solution)/shard_map/ppermute | solution.py:451
  24.8 11.5 %collective-permute-start.8 = (bf16[256,768]{1,0:T(8,128)(2,1)S(1)}, bf16[256,768]{1,0:T(8,128)(2,1)S(1)}, u32[]{:S(2)}, u32[]{:S(2)}) collective-permute-start(bf16[256,768]{1,0:T(8,128)(2,1)S(1)} %get-tuple-element.120.normed_ref), channel_id=1, source_target_pairs={{0,2},{1,3},{2,0},{3,1},{4,6},{5,7},{6,4},{7,5},{8,10},{9,11},{10,... | collective-permute-start | bytes 1179656 | tf_op jit(solution)/shard_map/ppermute | solution.py:451
  26.4 25.8 %copy-start.15 = (bf16[384]{0:T(512)(128)(2,1)S(1)}, bf16[384]{0:T(512)(128)(2,1)}, u32[]{:S(2)}) copy-start(bf16[384]{0:T(512)(128)(2,1)} %param.24) | copy-start | bytes 2308
  26.4 27.8 %copy-start.9 = (s32[1,1,1,8,35]{4,3,2,1,0:T(8,128)S(1)}, s32[1,1,1,8,35]{4,3,2,1,0:T(8,128)}, u32[]{:S(2)}) copy-start(s32[1,1,1,8,35]{4,3,2,1,0:T(8,128)} %param.16) | copy-start | bytes 3364
  26.4 27.8 %copy-start.10 = (f32[2,1408]{1,0:T(2,128)S(1)}, f32[2,1408]{1,0:T(2,128)}, u32[]{:S(2)}) copy-start(f32[2,1408]{1,0:T(2,128)} %constant.2.clone.ids_ref) | copy-start | bytes 33796
  36.3 2.4 %collective-permute-start.10 = (bf16[768,256]{1,0:T(8,128)(2,1)S(1)}, bf16[768,256]{1,0:T(8,128)(2,1)S(1)}, u32[]{:S(2)}, u32[]{:S(2)}) collective-permute-start(bf16[768,256]{1,0:T(8,128)(2,1)S(1)} %get-tuple-element.132), channel_id=1, source_target_pairs={{0,1},{1,0},{2,3},{3,2},{4,5},{5,4},{6,7},{7,6},{8,9},{9,8},{10,11... | collective-permute-start | bytes 1179656 | tf_op jit(solution)/shard_map/ppermute | solution.py:451
  36.3 2.4 %collective-permute-start.13 = (bf16[256,768]{1,0:T(8,128)(2,1)S(1)}, bf16[256,768]{1,0:T(8,128)(2,1)S(1)}, u32[]{:S(2)}, u32[]{:S(2)}) collective-permute-start(bf16[256,768]{1,0:T(8,128)(2,1)S(1)} %collective-permute-done.8.refs_6_), channel_id=1, source_target_pairs={{0,1},{1,0},{2,3},{3,2},{4,5},{5,4},{6,7},{7,6},{8,9},{9,8},{10,11... | collective-permute-start | bytes 1179656 | tf_op jit(solution)/shard_map/ppermute | solution.py:451
  36.8 2.3 %collective-permute-start.14 = (bf16[256,768]{1,0:T(8,128)(2,1)S(1)}, bf16[256,768]{1,0:T(8,128)(2,1)S(1)}, u32[]{:S(2)}, u32[]{:S(2)}) collective-permute-start(bf16[256,768]{1,0:T(8,128)(2,1)S(1)} %collective-permute-done.5.refs_8_), channel_id=1, source_target_pairs={{0,1},{1,0},{2,3},{3,2},{4,5},{5,4},{6,7},{7,6},{8,9},{9,8},{10,11... | collective-permute-start | bytes 1179656 | tf_op jit(solution)/shard_map/ppermute | solution.py:451
  36.8 27.3 %collective-permute-start.11 = (bf16[768,256]{1,0:T(8,128)(2,1)S(1)}, bf16[768,256]{1,0:T(8,128)(2,1)S(1)}, u32[]{:S(2)}, u32[]{:S(2)}) collective-permute-start(bf16[768,256]{1,0:T(8,128)(2,1)S(1)} %get-tuple-element.133), channel_id=1, source_target_pairs={{0,2},{1,3},{2,0},{3,1},{4,6},{5,7},{6,4},{7,5},{8,10},{9,11},{10,... | collective-permute-start | bytes 1179656 | tf_op jit(solution)/shard_map/ppermute | solution.py:451
  38.3 25.7 %collective-permute-start.12 = (bf16[768,256]{1,0:T(8,128)(2,1)S(1)}, bf16[768,256]{1,0:T(8,128)(2,1)S(1)}, u32[]{:S(2)}, u32[]{:S(2)}) collective-permute-start(bf16[768,256]{1,0:T(8,128)(2,1)S(1)} %get-tuple-element.134), channel_id=1, source_target_pairs={{0,3},{1,2},{2,1},{3,0},{4,7},{5,6},{6,5},{7,4},{8,11},{9,10},{10,... | collective-permute-start | bytes 1179656 | tf_op jit(solution)/shard_map/ppermute | solution.py:451
  39.1 6.6 %collective-permute-start.15 = (bf16[40,384]{1,0:T(8,128)(2,1)S(1)}, bf16[40,384]{1,0:T(8,128)(2,1)S(1)}, u32[]{:S(2)}, u32[]{:S(2)}) collective-permute-start(bf16[40,384]{1,0:T(8,128)(2,1)S(1)} %get-tuple-element.147), channel_id=1, source_target_pairs={{0,4},{4,8},{8,12},{12,16},{16,20},{20,24},{24,28},{28,0},{1,5},{5... | collective-permute-start | bytes 92168 | tf_op jit(solution)/shard_map/ppermute | solution.py:603
  39.9 7.7 %collective-permute-start.16 = (bf16[40,384]{1,0:T(8,128)(2,1)S(1)}, bf16[40,384]{1,0:T(8,128)(2,1)S(1)}, u32[]{:S(2)}, u32[]{:S(2)}) collective-permute-start(bf16[40,384]{1,0:T(8,128)(2,1)S(1)} %get-tuple-element.148), channel_id=1, source_target_pairs={{0,8},{4,12},{8,16},{12,20},{16,24},{20,28},{24,0},{28,4},{1,9},{5... | collective-permute-start | bytes 92168 | tf_op jit(solution)/shard_map/ppermute | solution.py:603
  43.6 4.8 %collective-permute-start.17 = (bf16[40,384]{1,0:T(8,128)(2,1)S(1)}, bf16[40,384]{1,0:T(8,128)(2,1)S(1)}, u32[]{:S(2)}, u32[]{:S(2)}) collective-permute-start(bf16[40,384]{1,0:T(8,128)(2,1)S(1)} %get-tuple-element.149), channel_id=1, source_target_pairs={{0,12},{4,16},{8,20},{12,24},{16,28},{20,0},{24,4},{28,8},{1,13},{... | collective-permute-start | bytes 92168 | tf_op jit(solution)/shard_map/ppermute | solution.py:603
  45.8 4.5 %collective-permute-start.18 = (bf16[40,384]{1,0:T(8,128)(2,1)S(1)}, bf16[40,384]{1,0:T(8,128)(2,1)S(1)}, u32[]{:S(2)}, u32[]{:S(2)}) collective-permute-start(bf16[40,384]{1,0:T(8,128)(2,1)S(1)} %get-tuple-element.150), channel_id=1, source_target_pairs={{0,16},{4,20},{8,24},{12,28},{16,0},{20,4},{24,8},{28,12},{1,17},{... | collective-permute-start | bytes 92168 | tf_op jit(solution)/shard_map/ppermute | solution.py:603
  47.6 5.8 %collective-permute-start.19 = (bf16[40,384]{1,0:T(8,128)(2,1)S(1)}, bf16[40,384]{1,0:T(8,128)(2,1)S(1)}, u32[]{:S(2)}, u32[]{:S(2)}) collective-permute-start(bf16[40,384]{1,0:T(8,128)(2,1)S(1)} %get-tuple-element.151), channel_id=1, source_target_pairs={{0,20},{4,24},{8,28},{12,0},{16,4},{20,8},{24,12},{28,16},{1,21},{... | collective-permute-start | bytes 92168 | tf_op jit(solution)/shard_map/ppermute | solution.py:603
  48.4 5.5 %collective-permute-start.20 = (bf16[40,384]{1,0:T(8,128)(2,1)S(1)}, bf16[40,384]{1,0:T(8,128)(2,1)S(1)}, u32[]{:S(2)}, u32[]{:S(2)}) collective-permute-start(bf16[40,384]{1,0:T(8,128)(2,1)S(1)} %get-tuple-element.152), channel_id=1, source_target_pairs={{0,24},{4,28},{8,0},{12,4},{16,8},{20,12},{24,16},{28,20},{1,25},{... | collective-permute-start | bytes 92168 | tf_op jit(solution)/shard_map/ppermute | solution.py:603
  50.3 3.9 %collective-permute-start.21 = (bf16[40,384]{1,0:T(8,128)(2,1)S(1)}, bf16[40,384]{1,0:T(8,128)(2,1)S(1)}, u32[]{:S(2)}, u32[]{:S(2)}) collective-permute-start(bf16[40,384]{1,0:T(8,128)(2,1)S(1)} %get-tuple-element.153), channel_id=1, source_target_pairs={{0,28},{4,0},{8,4},{12,8},{16,12},{20,16},{24,20},{28,24},{1,29},{... | collective-permute-start | bytes 92168 | tf_op jit(solution)/shard_map/ppermute | solution.py:603
  55.7 6.5 %collective-permute-start.22 = (bf16[96,384]{1,0:T(8,128)(2,1)S(1)}, bf16[96,384]{1,0:T(8,128)(2,1)S(1)}, u32[]{:S(2)}, u32[]{:S(2)}) collective-permute-start(bf16[96,384]{1,0:T(8,128)(2,1)S(1)} %get-tuple-element.154), channel_id=1, source_target_pairs={{0,4},{4,8},{8,12},{12,0},{1,5},{5,9},{9,13},{13,1},{2,6},{6,10},{... | collective-permute-start | bytes 221192 | tf_op jit(solution)/shard_map/ppermute | solution.py:456
  57.0 5.1 %collective-permute-start.23 = (bf16[96,384]{1,0:T(8,128)(2,1)S(1)}, bf16[96,384]{1,0:T(8,128)(2,1)S(1)}, u32[]{:S(2)}, u32[]{:S(2)}) collective-permute-start(bf16[96,384]{1,0:T(8,128)(2,1)S(1)} %get-tuple-element.155), channel_id=1, source_target_pairs={{0,12},{4,0},{8,4},{12,8},{1,13},{5,1},{9,5},{13,9},{2,14},{6,2},{... | collective-permute-start | bytes 221192 | tf_op jit(solution)/shard_map/ppermute | solution.py:456
  62.2 5.8 %collective-permute-start.25 = (bf16[128,384]{1,0:T(8,128)(2,1)S(1)}, bf16[128,384]{1,0:T(8,128)(2,1)S(1)}, u32[]{:S(2)}, u32[]{:S(2)}) collective-permute-start(bf16[128,384]{1,0:T(8,128)(2,1)S(1)} %rim.1), channel_id=1, source_target_pairs={{0,16},{16,0},{1,17},{17,1},{2,18},{18,2},{3,19},{19,3},{4,20},{20... | collective-permute-start | bytes 294920 | tf_op jit(solution)/shard_map/ppermute | solution.py:456
  65.2 4.7 %copy-start.7 = (f32[7,7,384]{2,1,0:T(8,128)S(1)}, f32[7,7,384]{2,1,0:T(8,128)}, u32[]{:S(2)}) copy-start(f32[7,7,384]{2,1,0:T(8,128)} %refs_0_.1) | copy-start | bytes 225796
  65.2 12.1 %collective-permute-start.24 = (bf16[4,96,384]{2,1,0:T(8,128)(2,1)S(1)}, bf16[4,96,384]{2,1,0:T(8,128)(2,1)S(1)}, u32[]{:S(2)}, u32[]{:S(2)}) collective-permute-start(bf16[4,96,384]{2,1,0:T(8,128)(2,1)S(1)} %get-tuple-element.168), channel_id=1, source_target_pairs={{0,16},{16,0},{1,17},{17,1},{2,18},{18,2},{3,19},{19,3},{4,20},{20... | collective-permute-start | bytes 884744 | tf_op jit(solution)/shard_map/ppermute | solution.py:456
  68.0 14.3 %collective-permute-start.29 = (bf16[4,96,384]{2,1,0:T(8,128)(2,1)S(1)}, bf16[4,96,384]{2,1,0:T(8,128)(2,1)S(1)}, u32[]{:S(2)}, u32[]{:S(2)}) collective-permute-start(bf16[4,96,384]{2,1,0:T(8,128)(2,1)S(1)} %get-tuple-element.180), channel_id=1, source_target_pairs={{0,16},{16,0},{1,17},{17,1},{2,18},{18,2},{3,19},{19,3},{4,20},{20... | collective-permute-start | bytes 884744 | tf_op jit(solution)/shard_map/ppermute | solution.py:456
  69.8 16.5 %copy-start.3 = (bf16[384,768]{1,0:T(8,128)(2,1)S(1)}, bf16[384,768]{1,0:T(8,128)(2,1)}, u32[]{:S(2)}) copy-start(bf16[384,768]{1,0:T(8,128)(2,1)} %up_ref.1) | copy-start | bytes 1769476
  69.8 16.5 %copy-start.4 = (bf16[768,384]{1,0:T(8,128)(2,1)S(1)}, bf16[768,384]{1,0:T(8,128)(2,1)}, u32[]{:S(2)}) copy-start(bf16[768,384]{1,0:T(8,128)(2,1)} %down_ref.1) | copy-start | bytes 1769476
  69.8 16.5 %copy-start.6 = (bf16[384,128]{1,0:T(8,128)(2,1)S(1)}, bf16[384,128]{1,0:T(8,128)(2,1)}, u32[]{:S(2)}) copy-start(bf16[384,128]{1,0:T(8,128)(2,1)} %head_ref.1) | copy-start | bytes 294916
  77.4 6.3 %collective-permute-start.26 = (bf16[96,384]{1,0:T(8,128)(2,1)S(1)}, bf16[96,384]{1,0:T(8,128)(2,1)S(1)}, u32[]{:S(2)}, u32[]{:S(2)}) collective-permute-start(bf16[96,384]{1,0:T(8,128)(2,1)S(1)} %get-tuple-element.176), channel_id=1, source_target_pairs={{0,4},{4,8},{8,12},{12,0},{1,5},{5,9},{9,13},{13,1},{2,6},{6,10},{... | collective-permute-start | bytes 221192 | tf_op jit(solution)/shard_map/ppermute | solution.py:456
  78.1 11.6 %collective-permute-start.27 = (bf16[96,384]{1,0:T(8,128)(2,1)S(1)}, bf16[96,384]{1,0:T(8,128)(2,1)S(1)}, u32[]{:S(2)}, u32[]{:S(2)}) collective-permute-start(bf16[96,384]{1,0:T(8,128)(2,1)S(1)} %get-tuple-element.177), channel_id=1, source_target_pairs={{0,8},{4,12},{8,0},{12,4},{1,9},{5,13},{9,1},{13,5},{2,10},{6,14},... | collective-permute-start | bytes 221192 | tf_op jit(solution)/shard_map/ppermute | solution.py:456
  81.4 8.3 %collective-permute-start.28 = (bf16[96,384]{1,0:T(8,128)(2,1)S(1)}, bf16[96,384]{1,0:T(8,128)(2,1)S(1)}, u32[]{:S(2)}, u32[]{:S(2)}) collective-permute-start(bf16[96,384]{1,0:T(8,128)(2,1)S(1)} %get-tuple-element.178), channel_id=1, source_target_pairs={{0,12},{4,0},{8,4},{12,8},{1,13},{5,1},{9,5},{13,9},{2,14},{6,2},{... | collective-permute-start | bytes 221192 | tf_op jit(solution)/shard_map/ppermute | solution.py:456
  82.3 7.4 %collective-permute-start.30 = (bf16[96,384]{1,0:T(8,128)(2,1)S(1)}, bf16[96,384]{1,0:T(8,128)(2,1)S(1)}, u32[]{:S(2)}, u32[]{:S(2)}) collective-permute-start(bf16[96,384]{1,0:T(8,128)(2,1)S(1)} %get-tuple-element.184), channel_id=1, source_target_pairs={{0,4},{4,8},{8,12},{12,0},{1,5},{5,9},{9,13},{13,1},{2,6},{6,10},{... | collective-permute-start | bytes 221192 | tf_op jit(solution)/shard_map/ppermute | solution.py:456
  83.5 6.6 %collective-permute-start.31 = (bf16[96,384]{1,0:T(8,128)(2,1)S(1)}, bf16[96,384]{1,0:T(8,128)(2,1)S(1)}, u32[]{:S(2)}, u32[]{:S(2)}) collective-permute-start(bf16[96,384]{1,0:T(8,128)(2,1)S(1)} %get-tuple-element.185), channel_id=1, source_target_pairs={{0,8},{4,12},{8,0},{12,4},{1,9},{5,13},{9,1},{13,5},{2,10},{6,14},... | collective-permute-start | bytes 221192 | tf_op jit(solution)/shard_map/ppermute | solution.py:456
  83.6 6.5 %collective-permute-start.32 = (bf16[96,384]{1,0:T(8,128)(2,1)S(1)}, bf16[96,384]{1,0:T(8,128)(2,1)S(1)}, u32[]{:S(2)}, u32[]{:S(2)}) collective-permute-start(bf16[96,384]{1,0:T(8,128)(2,1)S(1)} %get-tuple-element.186), channel_id=1, source_target_pairs={{0,12},{4,0},{8,4},{12,8},{1,13},{5,1},{9,5},{13,9},{2,14},{6,2},{... | collective-permute-start | bytes 221192 | tf_op jit(solution)/shard_map/ppermute | solution.py:456
  90.2 5.2 %collective-permute-start.34 = (bf16[96,768]{1,0:T(8,128)(2,1)S(1)}, bf16[96,768]{1,0:T(8,128)(2,1)S(1)}, u32[]{:S(2)}, u32[]{:S(2)}) collective-permute-start(bf16[96,768]{1,0:T(8,128)(2,1)S(1)} %close.1.own_ref), channel_id=1, source_target_pairs={{0,2},{1,3},{2,0},{3,1},{4,6},{5,7},{6,4},{7,5},{8,10},{9,11},{10,... | collective-permute-start | bytes 442376 | tf_op jit(solution)/shard_map/ppermute | solution.py:451
  91.8 3.6 %collective-permute-start.33 = (bf16[96,768]{1,0:T(8,128)(2,1)S(1)}, bf16[96,768]{1,0:T(8,128)(2,1)S(1)}, u32[]{:S(2)}, u32[]{:S(2)}) collective-permute-start(bf16[96,768]{1,0:T(8,128)(2,1)S(1)} %close.1.own_ref), channel_id=1, source_target_pairs={{0,1},{1,0},{2,3},{3,2},{4,5},{5,4},{6,7},{7,6},{8,9},{9,8},{10,11... | collective-permute-start | bytes 442376 | tf_op jit(solution)/shard_map/ppermute | solution.py:451
  95.4 1.4 %collective-permute-start.35 = (bf16[96,768]{1,0:T(8,128)(2,1)S(1)}, bf16[96,768]{1,0:T(8,128)(2,1)S(1)}, u32[]{:S(2)}, u32[]{:S(2)}) collective-permute-start(bf16[96,768]{1,0:T(8,128)(2,1)S(1)} %collective-permute-done.34.two_ref), channel_id=1, source_target_pairs={{0,1},{1,0},{2,3},{3,2},{4,5},{5,4},{6,7},{7,6},{8,9},{9,8},{10,11... | collective-permute-start | bytes 442376 | tf_op jit(solution)/shard_map/ppermute | solution.py:451
  (4 other events, 6.9 us)
